TPU v7x, 32 devices: a whole 2x2x4 slice. The times are simulated.
32 devices in a mesh: fsdp: 2 (over x), context: 4 (over z), tensor: 4 (over y, core).
Axes of the slice: x: 2, y: 2, z: 4, core: 2. Of those that a mesh axis runs over, the one named last changes fastest.
Arguments:
- inputs: bfloat16 [4096, 1536], P(('fsdp', 'context')), may hold values from -6 to 6
- cotangent: bfloat16 [4096, 1536], P(('fsdp', 'context')), may hold values from -6 to 6
- blocks: int32 [2, 8], P('fsdp'), may hold values from 0 to 7, each once within a row
- attn_gain: bfloat16 [1536], P('fsdp'), may hold values from 0.25 to 1.75
- w_query: bfloat16 [1536, 1536], P('fsdp', 'tensor'), may hold values from -0.21875 to 0.21875
- b_query: bfloat16 [12, 128], P('tensor', 'fsdp'), may hold values from -3 to 3
- w_key: bfloat16 [1536, 256], P('fsdp'), may hold values from -0.21875 to 0.21875
- b_key: bfloat16 [2, 128], P(None, 'fsdp'), may hold values from -3 to 3
- w_value: bfloat16 [1536, 256], P('fsdp'), may hold values from -0.15625 to 0.15625
- b_value: bfloat16 [2, 128], P(None, 'fsdp'), may hold values from -3 to 3
- w_out: bfloat16 [1536, 1536], P('tensor', 'fsdp'), may hold values from -1 to 1
- ffn_gain: bfloat16 [1536], P('fsdp'), may hold values from 0.25 to 1.75
- w_gate: bfloat16 [1536, 8960], P('fsdp', 'tensor'), may hold values from -0.15625 to 0.15625
- w_up: bfloat16 [1536, 8960], P('fsdp', 'tensor'), may hold values from -0.15625 to 0.15625
- w_down: bfloat16 [8960, 1536], P('tensor', 'fsdp'), may hold values from -0.09375 to 0.09375
Outputs:
- outputs: bfloat16 [4096, 1536], P(('fsdp', 'context'))
- input_grad: bfloat16 [4096, 1536], P(('fsdp', 'context'))
- attn_gain_grad: float32 [1536], P('fsdp')
- w_query_grad: float32 [1536, 1536], P('fsdp', 'tensor')
- b_query_grad: float32 [12, 128], P('tensor', 'fsdp')
- w_key_grad: float32 [1536, 256], P('fsdp')
- b_key_grad: float32 [2, 128], P(None, 'fsdp')
- w_value_grad: float32 [1536, 256], P('fsdp')
- b_value_grad: float32 [2, 128], P(None, 'fsdp')
- w_out_grad: float32 [1536, 1536], P('tensor', 'fsdp')
- ffn_gain_grad: float32 [1536], P('fsdp')
- w_gate_grad: float32 [1536, 8960], P('fsdp', 'tensor')
- w_up_grad: float32 [1536, 8960], P('fsdp', 'tensor')
- w_down_grad: float32 [8960, 1536], P('tensor', 'fsdp')
Inputs may be any that keep to these rules, and one draw needn't show every extreme that they name: `blocks`: each row lists every block number of 0 to 7 once.
All inputs are finite; a program needn't handle non-finite values.
Results may differ from a plain program's by a relative error of at most 0.02.
Values may be sent and summed in bfloat16 or wider, within the bound.
A program may use at most 192 MiB of HBM per device.

v0:
```python
import jax
import jax.numpy as jnp
from jax import lax
from jax.sharding import PartitionSpec as P

H = 12
KV = 2
HD = 128
BLOCK = 256


EPSILON = 1e-06
ROPE_BASE = 1000000.0
MASKED = -1e30


def rope_tables(positions):
    halfway = HD // 2
    frequency = ROPE_BASE ** (-(jnp.arange(halfway, dtype=jnp.float32) * 2.0 / HD))
    angles = positions.astype(jnp.float32)[:, None] * frequency[None, :]
    cosine = jnp.concatenate([jnp.cos(angles), jnp.cos(angles)], axis=1)
    sine = jnp.concatenate([jnp.sin(angles), jnp.sin(angles)], axis=1)
    return (cosine, sine)


def rotate(field, cosine, sine):
    halfway = HD // 2
    turned = jnp.concatenate([-field[..., halfway:], field[..., :halfway]], axis=-1)
    return field * cosine[:, None, :] + turned * sine[:, None, :]


def rotate_back(grad_field, cosine, sine):
    halfway = HD // 2
    moved = grad_field * sine[:, None, :]
    turned = jnp.concatenate([moved[..., halfway:], -moved[..., :halfway]], axis=-1)
    return grad_field * cosine[:, None, :] + turned


def rms_scale(values):
    return lax.rsqrt(jnp.mean(values * values, axis=-1, keepdims=True) + EPSILON)


def norm_back(values, factor, gain, grad_normed):
    gained = gain * grad_normed
    inner = jnp.mean(gained * values, axis=-1, keepdims=True)
    grad_values = factor * gained - values * (factor * factor * factor) * inner
    return (grad_values, jnp.sum(grad_normed * values * factor, axis=0))


def contract_rows(left, right):
    return lax.dot_general(
        left, right, (((0,), (0,)), ((), ())), preferred_element_type=jnp.float32
    )


def contract_cols(left, right):
    return lax.dot_general(
        left, right, (((1,), (1,)), ((), ())), preferred_element_type=jnp.float32
    )


def local(
    inputs,
    cotangent,
    blocks,
    attn_gain,
    w_query,
    b_query,
    w_key,
    b_key,
    w_value,
    b_value,
    w_out,
    ffn_gain,
    w_gate,
    w_up,
    w_down,
):
    rows_here = inputs.shape[0]
    context_index = lax.axis_index("context")
    tensor_index = lax.axis_index("tensor")
    gain_first, wq_all, bq_all, wk_all, bk_all, wv_all, bv_all, wo_all = (
        lax.all_gather(attn_gain, "fsdp", axis=0, tiled=True),
        lax.all_gather(w_query, "fsdp", axis=0, tiled=True),
        lax.all_gather(b_query, "fsdp", axis=1, tiled=True),
        lax.all_gather(w_key, "fsdp", axis=0, tiled=True),
        lax.all_gather(b_key, "fsdp", axis=1, tiled=True),
        lax.all_gather(w_value, "fsdp", axis=0, tiled=True),
        lax.all_gather(b_value, "fsdp", axis=1, tiled=True),
        lax.all_gather(w_out, "fsdp", axis=1, tiled=True),
    )
    seq_blocks = blocks[0]
    seq_length = seq_blocks.shape[0] * BLOCK
    block_of_row = jnp.repeat(seq_blocks, BLOCK, total_repeat_length=seq_length)
    key_positions = block_of_row * BLOCK + jnp.arange(seq_length, dtype=jnp.int32) % BLOCK
    my_blocks = lax.dynamic_slice_in_dim(block_of_row, context_index * rows_here, rows_here)
    my_positions = lax.dynamic_slice_in_dim(key_positions, context_index * rows_here, rows_here)
    cosine, sine = rope_tables(my_positions)
    allowed = block_of_row[None, :] <= my_blocks[:, None]
    inputs_f = inputs.astype(jnp.float32)
    factor_first = rms_scale(inputs_f)
    gain_first_f = gain_first.astype(jnp.float32)
    normed = (inputs_f * factor_first * gain_first_f).astype(jnp.bfloat16)
    query_pre = jnp.dot(normed, wq_all, preferred_element_type=jnp.float32).reshape(
        rows_here, -1, HD
    ) + bq_all.astype(jnp.float32)
    key_pre = jnp.dot(normed, wk_all, preferred_element_type=jnp.float32).reshape(
        rows_here, KV, HD
    ) + bk_all.astype(jnp.float32)
    value_pre = jnp.dot(normed, wv_all, preferred_element_type=jnp.float32).reshape(
        rows_here, KV, HD
    ) + bv_all.astype(jnp.float32)
    queries = rotate(query_pre, cosine, sine).astype(jnp.bfloat16)
    keys = rotate(key_pre, cosine, sine).astype(jnp.bfloat16)
    values = value_pre.astype(jnp.bfloat16)
    key_whole, value_whole = (
        lax.all_gather(keys, "context", axis=0, tiled=True),
        lax.all_gather(values, "context", axis=0, tiled=True),
    )
    heads_here = queries.shape[1]
    group_size = H // KV
    scaling = HD ** (-0.5)
    attended_list = []
    log_totals = []
    for head_slot in range(heads_here):
        key_group = (tensor_index * heads_here + head_slot) // group_size
        key_head = lax.dynamic_index_in_dim(key_whole, key_group, 1, keepdims=False)
        value_head = lax.dynamic_index_in_dim(value_whole, key_group, 1, keepdims=False)
        raw_scores = (
            jnp.einsum(
                "qd,kd->qk", queries[:, head_slot], key_head, preferred_element_type=jnp.float32
            )
            * scaling
        )
        scores = jnp.where(allowed, raw_scores, MASKED)
        row_max = jnp.max(scores, axis=1, keepdims=True)
        expo = jnp.exp(scores - row_max)
        total = jnp.sum(expo, axis=1, keepdims=True)
        probability = (expo / total).astype(jnp.bfloat16)
        attended_list.append(jnp.dot(probability, value_head, preferred_element_type=jnp.float32))
        log_totals.append(row_max + jnp.log(total))
    attended = jnp.concatenate(attended_list, axis=1).astype(jnp.bfloat16)
    attn_part = jnp.dot(attended, wo_all, preferred_element_type=jnp.float32)
    middle = inputs_f + lax.psum(attn_part, "tensor")
    gain_second, wg_all, wu_all, wd_all = (
        lax.all_gather(ffn_gain, "fsdp", axis=0, tiled=True),
        lax.all_gather(w_gate, "fsdp", axis=0, tiled=True),
        lax.all_gather(w_up, "fsdp", axis=0, tiled=True),
        lax.all_gather(w_down, "fsdp", axis=1, tiled=True),
    )
    factor_second = rms_scale(middle)
    gain_second_f = gain_second.astype(jnp.float32)
    normed2 = (middle * factor_second * gain_second_f).astype(jnp.bfloat16)
    gate_pre = jnp.dot(normed2, wg_all, preferred_element_type=jnp.float32)
    up_pre = jnp.dot(normed2, wu_all, preferred_element_type=jnp.float32)
    sigma = jax.nn.sigmoid(gate_pre)
    hidden = (gate_pre * sigma * up_pre).astype(jnp.bfloat16)
    ffn_part = jnp.dot(hidden, wd_all, preferred_element_type=jnp.float32)
    final = middle + lax.psum(ffn_part.astype(jnp.bfloat16), "tensor").astype(jnp.float32)
    outputs = final.astype(jnp.bfloat16)
    grad_out = cotangent.astype(jnp.float32)
    wd_grad = contract_rows(hidden, cotangent)
    grad_hidden = contract_cols(cotangent, wd_all)
    grad_gate = (grad_hidden * up_pre * (sigma + gate_pre * sigma * (1.0 - sigma))).astype(
        jnp.bfloat16
    )
    grad_upper = (grad_hidden * gate_pre * sigma).astype(jnp.bfloat16)
    wg_grad = contract_rows(normed2, grad_gate)
    wu_grad = contract_rows(normed2, grad_upper)
    normed2_part = contract_cols(grad_gate, wg_all) + contract_cols(grad_upper, wu_all)
    grad_normed2 = lax.psum(normed2_part, "tensor")
    grad_mid_norm, ffn_gain_grad = norm_back(middle, factor_second, gain_second_f, grad_normed2)
    grad_middle = grad_out + grad_mid_norm
    grad_middle_low = grad_middle.astype(jnp.bfloat16)
    wo_grad = contract_rows(attended, grad_middle_low)
    grad_attended = contract_cols(grad_middle_low, wo_all).astype(jnp.bfloat16)
    key_grad = jnp.zeros((seq_length, KV, HD), jnp.float32)
    value_grad = jnp.zeros((seq_length, KV, HD), jnp.float32)
    query_grads = []
    for head_slot in range(heads_here):
        key_group = (tensor_index * heads_here + head_slot) // group_size
        key_head = lax.dynamic_index_in_dim(key_whole, key_group, 1, keepdims=False)
        value_head = lax.dynamic_index_in_dim(value_whole, key_group, 1, keepdims=False)
        query_head = queries[:, head_slot]
        raw_scores = (
            jnp.einsum("qd,kd->qk", query_head, key_head, preferred_element_type=jnp.float32)
            * scaling
        )
        scores = jnp.where(allowed, raw_scores, MASKED)
        probability = jnp.exp(scores - log_totals[head_slot])
        prob_low = probability.astype(jnp.bfloat16)
        grad_head = grad_attended[:, head_slot * HD : (head_slot + 1) * HD]
        grad_probs = jnp.einsum(
            "qd,kd->qk", grad_head, value_head, preferred_element_type=jnp.float32
        )
        inner = jnp.sum(probability * grad_probs, axis=1, keepdims=True)
        grad_scores = (probability * (grad_probs - inner)).astype(jnp.bfloat16)
        query_grads.append(
            jnp.dot(grad_scores, key_head, preferred_element_type=jnp.float32) * scaling
        )
        key_piece = contract_rows(grad_scores, query_head) * scaling
        value_piece = contract_rows(prob_low, grad_head)
        select = (jnp.arange(KV, dtype=jnp.int32) == key_group)[None, :, None]
        key_grad = key_grad + jnp.where(select, key_piece[:, None, :], 0.0)
        value_grad = value_grad + jnp.where(select, value_piece[:, None, :], 0.0)
    key_share, value_share = (
        lax.psum_scatter(key_grad, "context", scatter_dimension=0, tiled=True),
        lax.psum_scatter(value_grad, "context", scatter_dimension=0, tiled=True),
    )
    query_grad = jnp.stack(query_grads, axis=1)
    query_low = rotate_back(query_grad, cosine, sine).astype(jnp.bfloat16)
    flat_query = query_low.reshape(rows_here, -1)
    normed_part = contract_cols(flat_query, wq_all)
    grad_normed_query, key_total, value_total = lax.psum(
        (normed_part, key_share, value_share), "tensor"
    )
    key_low = rotate_back(key_total, cosine, sine).astype(jnp.bfloat16)
    value_low = value_total.astype(jnp.bfloat16)
    flat_key = key_low.reshape(rows_here, -1)
    flat_value = value_low.reshape(rows_here, -1)
    grad_normed = (
        grad_normed_query + contract_cols(flat_key, wk_all) + contract_cols(flat_value, wv_all)
    )
    grad_in_norm, attn_gain_grad = norm_back(inputs_f, factor_first, gain_first_f, grad_normed)
    input_grad = (grad_middle + grad_in_norm).astype(jnp.bfloat16)
    wq_grad = contract_rows(normed, flat_query)
    bq_grad = jnp.sum(query_low.astype(jnp.float32), axis=0)
    wk_grad = contract_rows(normed, flat_key)
    bk_grad = jnp.sum(key_low.astype(jnp.float32), axis=0)
    wv_grad = contract_rows(normed, flat_value)
    bv_grad = jnp.sum(value_low.astype(jnp.float32), axis=0)
    pieces = (
        lax.psum_scatter(
            attn_gain_grad.astype(jnp.bfloat16),
            ("fsdp", "context"),
            scatter_dimension=0,
            tiled=True,
        ).astype(jnp.float32),
        lax.psum_scatter(
            wq_grad.astype(jnp.bfloat16), ("fsdp", "context"), scatter_dimension=0, tiled=True
        ).astype(jnp.float32),
        lax.psum_scatter(
            bq_grad.astype(jnp.bfloat16), ("fsdp", "context"), scatter_dimension=1, tiled=True
        ).astype(jnp.float32),
        lax.psum_scatter(
            wk_grad.astype(jnp.bfloat16), ("fsdp", "context"), scatter_dimension=0, tiled=True
        ).astype(jnp.float32),
        lax.psum_scatter(
            bk_grad.astype(jnp.bfloat16), ("fsdp", "context"), scatter_dimension=1, tiled=True
        ).astype(jnp.float32),
        lax.psum_scatter(
            wv_grad.astype(jnp.bfloat16), ("fsdp", "context"), scatter_dimension=0, tiled=True
        ).astype(jnp.float32),
        lax.psum_scatter(
            bv_grad.astype(jnp.bfloat16), ("fsdp", "context"), scatter_dimension=1, tiled=True
        ).astype(jnp.float32),
        lax.psum_scatter(
            wo_grad.astype(jnp.bfloat16), ("fsdp", "context"), scatter_dimension=1, tiled=True
        ).astype(jnp.float32),
        lax.psum_scatter(
            ffn_gain_grad.astype(jnp.bfloat16), ("fsdp", "context"), scatter_dimension=0, tiled=True
        ).astype(jnp.float32),
        lax.psum_scatter(
            wg_grad.astype(jnp.bfloat16), ("fsdp", "context"), scatter_dimension=0, tiled=True
        ).astype(jnp.float32),
        lax.psum_scatter(
            wu_grad.astype(jnp.bfloat16), ("fsdp", "context"), scatter_dimension=0, tiled=True
        ).astype(jnp.float32),
        lax.psum_scatter(
            wd_grad.astype(jnp.bfloat16), ("fsdp", "context"), scatter_dimension=1, tiled=True
        ).astype(jnp.float32),
    )
    shards = (
        lax.all_gather(pieces[0].astype(jnp.bfloat16), "context", axis=0, tiled=True).astype(
            jnp.float32
        ),
        lax.all_gather(pieces[1].astype(jnp.bfloat16), "context", axis=0, tiled=True).astype(
            jnp.float32
        ),
        lax.all_gather(pieces[2].astype(jnp.bfloat16), "context", axis=1, tiled=True).astype(
            jnp.float32
        ),
        lax.all_gather(pieces[3].astype(jnp.bfloat16), "context", axis=0, tiled=True).astype(
            jnp.float32
        ),
        lax.all_gather(pieces[4].astype(jnp.bfloat16), "context", axis=1, tiled=True).astype(
            jnp.float32
        ),
        lax.all_gather(pieces[5].astype(jnp.bfloat16), "context", axis=0, tiled=True).astype(
            jnp.float32
        ),
        lax.all_gather(pieces[6].astype(jnp.bfloat16), "context", axis=1, tiled=True).astype(
            jnp.float32
        ),
        lax.all_gather(pieces[7].astype(jnp.bfloat16), "context", axis=1, tiled=True).astype(
            jnp.float32
        ),
        lax.all_gather(pieces[8].astype(jnp.bfloat16), "context", axis=0, tiled=True).astype(
            jnp.float32
        ),
        lax.all_gather(pieces[9].astype(jnp.bfloat16), "context", axis=0, tiled=True).astype(
            jnp.float32
        ),
        lax.all_gather(pieces[10].astype(jnp.bfloat16), "context", axis=0, tiled=True).astype(
            jnp.float32
        ),
        lax.all_gather(pieces[11].astype(jnp.bfloat16), "context", axis=1, tiled=True).astype(
            jnp.float32
        ),
    )
    return (
        outputs,
        input_grad,
        shards[0],
        shards[1],
        shards[2],
        shards[3],
        shards[4],
        shards[5],
        shards[6],
        shards[7],
        shards[8],
        shards[9],
        shards[10],
        shards[11],
    )


def solution(mesh):
    in_specs = (
        P(("fsdp", "context"), None),
        P(("fsdp", "context"), None),
        P("fsdp", None),
        P("fsdp"),
        P("fsdp", "tensor"),
        P("tensor", "fsdp"),
        P("fsdp", None),
        P(None, "fsdp"),
        P("fsdp", None),
        P(None, "fsdp"),
        P("tensor", "fsdp"),
        P("fsdp"),
        P("fsdp", "tensor"),
        P("fsdp", "tensor"),
        P("tensor", "fsdp"),
    )
    out_specs = (
        P(("fsdp", "context"), None),
        P(("fsdp", "context"), None),
        P("fsdp"),
        P("fsdp", "tensor"),
        P("tensor", "fsdp"),
        P("fsdp", None),
        P(None, "fsdp"),
        P("fsdp", None),
        P(None, "fsdp"),
        P("tensor", "fsdp"),
        P("fsdp"),
        P("fsdp", "tensor"),
        P("fsdp", "tensor"),
        P("tensor", "fsdp"),
    )
    return jax.shard_map(local, mesh=mesh, in_specs=in_specs, out_specs=out_specs, check_vma=False)
```

profile of v0, /device:TPU:0, one launch (start us, length us, event | category | flops | bytes accessed | tf_op | source)
XLA Modules:
  0.0 1892.6 jit_solution(14799244396280470210)
XLA Ops:
  17.9 19.9 %all_gather.81 = bf16[1536,256]{1,0:T(8,128)(2,1)S(1)} all-gather(bf16[768,256]{1,0:T(8,128)(2,1)} %param.23), channel_id=1, replica_groups=mesh['fsdp'=2,'context'=4,'tensor'=4] {'fsdp'}, dimensions={0}, use_global_device_ids=true | all-gather | bytes 1179648 | tf_op jit(solution)/shard_map/all_gather | solution.py:86
  92.5 17.4 all-gather.23.cloned.1.call-done
  117.1 16.5 all-gather.25.cloned.1.call-done
  144.2 61.9 %all-reduce.13.cloned.1.call-done = f32[512,1536]{1,0:T(8,128)} async-done(((f32[512,1536]{1,0:T(8,128)}), f32[512,1536]{1,0:T(8,128)}) %all-reduce.13.cloned.1.call-update) | async-done | bytes 3145744 | tf_op jit(solution)/shard_map/psum | solution.py:144
  212.0 82.6 %all-gather.29.cloned.1.call-done = bf16[1536,2240]{0,1:T(8,128)(2,1)} async-done(((bf16[768,2240]{0,1:T(8,128)(2,1)}), bf16[1536,2240]{0,1:T(8,128)(2,1)}) %all-gather.29.cloned.1.call-update) | async-done | bytes 6881296 | tf_op jit(solution)/shard_map/all_gather | solution.py:148
  304.2 79.1 %all-gather.27.cloned.1.call-done = bf16[1536,2240]{0,1:T(8,128)(2,1)} async-done(((bf16[768,2240]{0,1:T(8,128)(2,1)}), bf16[1536,2240]{0,1:T(8,128)(2,1)}) %all-gather.27.cloned.1.call-update) | async-done | bytes 6881296 | tf_op jit(solution)/shard_map/all_gather | solution.py:147
  392.8 79.1 %all-gather.31.cloned.1.call-done = bf16[2240,1536]{1,0:T(8,128)(2,1)} async-done(((bf16[2240,768]{1,0:T(8,128)(2,1)}), bf16[2240,1536]{1,0:T(8,128)(2,1)}) %all-gather.31.cloned.1.call-update) | async-done | bytes 6881296 | tf_op jit(solution)/shard_map/all_gather | solution.py:149
  471.9 13.3 multiply_convert_fusion
  510.5 56.0 %all-reduce.17.cloned.1.call-done = f32[512,1536]{1,0:T(8,128)} async-done(((f32[512,1536]{1,0:T(8,128)}), f32[512,1536]{1,0:T(8,128)}) %all-reduce.17.cloned.1.call-update) | async-done | bytes 3145744 | tf_op jit(solution)/shard_map/psum | solution.py:171
  570.3 41.9 %all-reduce.15.cloned.1.call-done = bf16[512,1536]{1,0:T(8,128)(2,1)} async-done(((bf16[512,1536]{1,0:T(8,128)(2,1)}), bf16[512,1536]{1,0:T(8,128)(2,1)}) %all-reduce.15.cloned.1.call-update) | async-done | bytes 1572880 | tf_op jit(solution)/shard_map/psum | solution.py:159
  674.8 34.0 %reduce-scatter.19.cloned.1.call-done = f32[512,2,128]{0,2,1:T(8,128)} async-done(((f32[2048,2,128]{0,2,1:T(8,128)}), f32[512,2,128]{0,2,1:T(8,128)}) %reduce-scatter.19.cloned.1.call-update) | async-done | bytes 524304 | tf_op jit(solution)/shard_map/reduce_scatter | solution.py:207
  743.7 10.4 reduce-scatter.21.cloned.1.call-done
  754.1 24.1 %all-reduce.20 = bf16[512,2,128]{0,2,1:T(8,128)(2,1)} all-reduce(f32[512,2,128]{0,2,1:T(8,128)} %reduce-scatter.21.cloned.1.call-done), channel_id=1, replica_groups=mesh['fsdp'=2,'context'=4,'tensor'=4] {'tensor'}, use_global_device_ids=true, to_apply=%region_19.20 | all-reduce | flops 131072 | bytes 786432 | tf_op jit(solution)/shard_map/psum | solution.py:214
  783.3 54.8 %all-reduce.19.cloned.1.call-done = (f32[512,1536]{1,0:T(8,128)}, f32[512,2,128]{0,2,1:T(8,128)}) async-done(((f32[512,1536]{1,0:T(8,128)}, f32[512,2,128]{0,2,1:T(8,128)}), (f32[512,1536]{1,0:T(8,128)}, f32[512,2,128]{0,2,1:T(8,128)})) %all-reduce.19.cloned.1.call-update) | async-done | bytes 3670032 | tf_op jit(solution)/shard_map/psum | solution.py:214
  844.7 126.0 %reduce-scatter.35.cloned.1.call-done = bf16[2240,192]{0,1:T(8,128)(2,1)} async-done(((bf16[2240,1536]{0,1:T(8,128)(2,1)}), bf16[2240,192]{0,1:T(8,128)(2,1)}) %reduce-scatter.35.cloned.1.call-update) | async-done | bytes 860176 | tf_op jit(solution)/shard_map/reduce_scatter | solution.py:269
  970.8 132.0 %reduce-scatter.31.cloned.1.call-done = bf16[192,2240]{1,0:T(8,128)(2,1)} async-done(((bf16[1536,2240]{1,0:T(8,128)(2,1)}), bf16[192,2240]{1,0:T(8,128)(2,1)}) %reduce-scatter.31.cloned.1.call-update) | async-done | bytes 860176 | tf_op jit(solution)/shard_map/reduce_scatter | solution.py:263
  1102.9 131.6 %reduce-scatter.33.cloned.1.call-done = bf16[192,2240]{1,0:T(8,128)(2,1)} async-done(((bf16[1536,2240]{1,0:T(8,128)(2,1)}), bf16[192,2240]{1,0:T(8,128)(2,1)}) %reduce-scatter.33.cloned.1.call-update) | async-done | bytes 860176 | tf_op jit(solution)/shard_map/reduce_scatter | solution.py:266
  1237.0 53.9 %reduce-scatter.37.cloned.1.call-done = bf16[16,3]{1,0:T(8,128)(2,1)} async-done(((bf16[128,3]{1,0:T(8,128)(2,1)}), bf16[16,3]{1,0:T(8,128)(2,1)}) %reduce-scatter.37.cloned.1.call-update) | async-done | bytes 112
  1291.7 9.9 all-gather.5
  1302.3 55.9 %reduce-scatter.29.cloned.1.call-done = bf16[384,192]{0,1:T(8,128)(2,1)} async-done(((bf16[384,1536]{0,1:T(8,128)(2,1)}), bf16[384,192]{0,1:T(8,128)(2,1)}) %reduce-scatter.29.cloned.1.call-update) | async-done | bytes 147472 | tf_op jit(solution)/shard_map/reduce_scatter | solution.py:257
  1358.1 17.9 all_gather.99
  1378.4 47.0 %reduce-scatter.23.cloned.1.call-done = bf16[192,384]{1,0:T(8,128)(2,1)} async-done(((bf16[1536,384]{1,0:T(8,128)(2,1)}), bf16[192,384]{1,0:T(8,128)(2,1)}) %reduce-scatter.23.cloned.1.call-update) | async-done | bytes 147472 | tf_op jit(solution)/shard_map/reduce_scatter | solution.py:239
  1425.4 16.6 all_gather.93
  1443.1 38.1 %reduce-scatter.41.cloned.1.call-done = bf16[16,2]{1,0:T(8,128)(2,1)} async-done(((bf16[128,2]{1,0:T(8,128)(2,1)}), bf16[16,2]{1,0:T(8,128)(2,1)}) %reduce-scatter.41.cloned.1.call-update) | async-done | bytes 80
  1492.5 54.5 %reduce-scatter.27.cloned.1.call-done = bf16[192,256]{1,0:T(8,128)(2,1)} async-done(((bf16[1536,256]{1,0:T(8,128)(2,1)}), bf16[192,256]{1,0:T(8,128)(2,1)}) %reduce-scatter.27.cloned.1.call-update) | async-done | bytes 98320 | tf_op jit(solution)/shard_map/reduce_scatter | solution.py:251
  1547.0 15.3 all_gather.97
  1569.1 20.1 %all-reduce.5 = (bf16[1536]{0:T(1024)(128)(2,1)S(1)}, bf16[1536]{0:T(1024)(128)(2,1)S(1)}) all-reduce(bf16[1536]{0:T(1024)(128)(2,1)S(1)} %get-tuple-element.84, bf16[1536]{0:T(1024)(128)(2,1)S(1)} %copy-done.40), channel_id=4, replica_groups=mesh['fsdp'=2,'context'=4,'tensor'=4] {'fsdp','context'}, use_global_device_ids=true, to_apply=%region_22.23.clone | all-reduce | flops 3072 | bytes 12288
  1614.6 53.4 %reduce-scatter.25.cloned.1.call-done = bf16[192,256]{1,0:T(8,128)(2,1)} async-done(((bf16[1536,256]{1,0:T(8,128)(2,1)}), bf16[192,256]{1,0:T(8,128)(2,1)}) %reduce-scatter.25.cloned.1.call-update) | async-done | bytes 98320 | tf_op jit(solution)/shard_map/reduce_scatter | solution.py:245
  1668.0 16.2 all_gather.95
  1685.1 54.4 %all-gather.37.cloned.1.call-done = bf16[2240,768]{0,1:T(8,128)(2,1)} async-done(((bf16[2240,192]{0,1:T(8,128)(2,1)}), bf16[2240,768]{0,1:T(8,128)(2,1)}) %all-gather.37.cloned.1.call-update) | async-done | bytes 3440656 | tf_op jit(solution)/shard_map/all_gather | solution.py:307
  1745.4 64.4 %all-gather.33.cloned.1.call-done = bf16[768,2240]{1,0:T(8,128)(2,1)} async-done(((bf16[192,2240]{1,0:T(8,128)(2,1)}), bf16[768,2240]{1,0:T(8,128)(2,1)}) %all-gather.33.cloned.1.call-update) | async-done | bytes 3440656 | tf_op jit(solution)/shard_map/all_gather | solution.py:301
  1815.7 64.3 %all-gather.35.cloned.1.call-done = bf16[768,2240]{1,0:T(8,128)(2,1)} async-done(((bf16[192,2240]{1,0:T(8,128)(2,1)}), bf16[768,2240]{1,0:T(8,128)(2,1)}) %all-gather.35.cloned.1.call-update) | async-done | bytes 3440656 | tf_op jit(solution)/shard_map/all_gather | solution.py:304
  (320 shorter events, 313.4 us)
Async XLA Ops:
  7.3 41.2 %copy-start.11 = (bf16[512,1536]{1,0:T(8,128)(2,1)S(1)}, bf16[512,1536]{1,0:T(8,128)(2,1)}, u32[]{:S(2)}) copy-start(bf16[512,1536]{1,0:T(8,128)(2,1)} %param.17) | copy-start | bytes 4718596
  7.3 36.5 %copy-start.61 = (bf16[2,64]{1,0:T(2,128)(2,1)S(1)}, bf16[2,64]{1,0:T(2,128)(2,1)}, u32[]{:S(2)}) copy-start(bf16[2,64]{1,0:T(2,128)(2,1)} %param.24) | copy-start | bytes 772
  7.3 63.3 %all-gather.19.cloned.1.call-start = ((), (), s32[]{:S(2)}) async-start(), calls=%async_computation.12 | async-start | bytes 1769472 | tf_op jit(solution)/shard_map/all_gather | solution.py:84
  8.0 72.2 %all-gather.21.cloned.1.call-start = ((), (), s32[]{:S(2)}) async-start(), calls=%async_computation.13 | async-start | bytes 1310720 | tf_op jit(solution)/shard_map/all_gather | solution.py:117
  10.5 60.2 %copy-start.38 = (f32[512]{0:T(512)}, f32[512]{0:T(512)S(1)}, u32[]{:S(2)}) copy-start(f32[512]{0:T(512)S(1)} %get-tuple-element.116) | copy-start | bytes 6148
  50.3 59.5 %all-gather.23.cloned.1.call-start = ((), (), s32[]{:S(2)}) async-start(), calls=%async_computation.14 | async-start | bytes 1310720 | tf_op jit(solution)/shard_map/all_gather | solution.py:118
  65.1 68.5 %all-gather.25.cloned.1.call-start = ((), (), s32[]{:S(2)}) async-start(), calls=%async_computation.15 | async-start | bytes 1769472 | tf_op jit(solution)/shard_map/all_gather | solution.py:90
  65.7 140.5 %all-reduce.13.cloned.1.call-start = ((), (), s32[]{:S(2)}) async-start(), calls=%async_computation.16 | async-start | bytes 6291456 | tf_op jit(solution)/shard_map/psum | solution.py:144
  137.5 157.2 %all-gather.29.cloned.1.call-start = ((), (), s32[]{:S(2)}) async-start(), calls=%async_computation.18 | async-start | bytes 10321920 | tf_op jit(solution)/shard_map/all_gather | solution.py:148
  138.1 245.2 %all-gather.27.cloned.1.call-start = ((), (), s32[]{:S(2)}) async-start(), calls=%async_computation.17 | async-start | bytes 10321920 | tf_op jit(solution)/shard_map/all_gather | solution.py:147
  138.9 333.0 %all-gather.31.cloned.1.call-start = ((), (), s32[]{:S(2)}) async-start(), calls=%async_computation.19 | async-start | bytes 10321920 | tf_op jit(solution)/shard_map/all_gather | solution.py:149
  139.6 426.9 %all-reduce.17.cloned.1.call-start = ((), (), s32[]{:S(2)}) async-start(), calls=%async_computation.21 | async-start | bytes 6291456 | tf_op jit(solution)/shard_map/psum | solution.py:171
  209.0 357.5 %copy-start.10 = (f32[512,1536]{1,0:T(8,128)}, f32[512,1536]{1,0:T(8,128)S(1)}, u32[]{:S(2)}) copy-start(f32[512,1536]{1,0:T(8,128)S(1)} %get-tuple-element.97) | copy-start | bytes 9437188
  497.9 114.4 %all-reduce.15.cloned.1.call-start = ((), (), s32[]{:S(2)}) async-start(), calls=%async_computation.20 | async-start | bytes 3145728 | tf_op jit(solution)/shard_map/psum | solution.py:159
  509.4 199.5 %reduce-scatter.19.cloned.1.call-start = ((), (), s32[]{:S(2)}) async-start(), calls=%async_computation.22 | async-start | bytes 2621440 | tf_op jit(solution)/shard_map/reduce_scatter | solution.py:207
  664.7 89.4 %reduce-scatter.21.cloned.1.call-start = ((), (), s32[]{:S(2)}) async-start(), calls=%async_computation.23 | async-start | bytes 2621440 | tf_op jit(solution)/shard_map/reduce_scatter | solution.py:208
  665.3 172.8 %all-reduce.19.cloned.1.call-start = ((), (), s32[]{:S(2)}) async-start(), calls=%async_computation.37 | async-start | bytes 7340032 | tf_op jit(solution)/shard_map/psum | solution.py:214
  708.9 261.9 %reduce-scatter.35.cloned.1.call-start = ((), (), s32[]{:S(2)}) async-start(), calls=%async_computation.32 | async-start | bytes 7962624 | tf_op jit(solution)/shard_map/reduce_scatter | solution.py:269
  717.7 385.1 %reduce-scatter.31.cloned.1.call-start = ((), (), s32[]{:S(2)}) async-start(), calls=%async_computation.28 | async-start | bytes 7962624 | tf_op jit(solution)/shard_map/reduce_scatter | solution.py:263
  727.0 507.5 %reduce-scatter.33.cloned.1.call-start = ((), (), s32[]{:S(2)}) async-start(), calls=%async_computation.30 | async-start | bytes 7962624 | tf_op jit(solution)/shard_map/reduce_scatter | solution.py:266
  736.0 555.0 %reduce-scatter.37.cloned.1.call-start = ((), (), s32[]{:S(2)}) async-start(), calls=%async_computation.34 | async-start | bytes 36864
  736.8 621.4 %reduce-scatter.29.cloned.1.call-start = ((), (), s32[]{:S(2)}) async-start(), calls=%async_computation.27 | async-start | bytes 1327104 | tf_op jit(solution)/shard_map/reduce_scatter | solution.py:257
  739.9 685.5 %reduce-scatter.23.cloned.1.call-start = ((), (), s32[]{:S(2)}) async-start(), calls=%async_computation.24 | async-start | bytes 1327104 | tf_op jit(solution)/shard_map/reduce_scatter | solution.py:239
  743.6 737.6 %reduce-scatter.41.cloned.1.call-start = ((), (), s32[]{:S(2)}) async-start(), calls=%async_computation.36 | async-start | bytes 36864
  780.0 767.0 %reduce-scatter.27.cloned.1.call-start = ((), (), s32[]{:S(2)}) async-start(), calls=%async_computation.26 | async-start | bytes 884736 | tf_op jit(solution)/shard_map/reduce_scatter | solution.py:251
  783.2 820.4 %reduce-scatter.39.cloned.1.call-start = ((), (), s32[]{:S(2)}) async-start(), calls=%async_computation.35 | async-start | bytes 36864
  841.3 826.8 %reduce-scatter.25.cloned.1.call-start = ((), (), s32[]{:S(2)}) async-start(), calls=%async_computation.25 | async-start | bytes 884736 | tf_op jit(solution)/shard_map/reduce_scatter | solution.py:245
  841.6 393.0 %copy-start.64 = (u32[32]{0:T(128)S(1)}, u32[32]{0:T(128)}, u32[]{:S(2)}) copy-start(u32[32]{0:T(128)} %constant.248) | copy-start | bytes 388
  841.6 394.2 %copy-start.63 = (u32[32]{0:T(128)S(1)}, u32[32]{0:T(128)}, u32[]{:S(2)}) copy-start(u32[32]{0:T(128)} %constant.236) | copy-start | bytes 388
  844.7 894.9 %all-gather.37.cloned.1.call-start = ((), (), s32[]{:S(2)}) async-start(), calls=%async_computation.33 | async-start | bytes 4423680 | tf_op jit(solution)/shard_map/all_gather | solution.py:307
  970.8 839.0 %all-gather.33.cloned.1.call-start = ((), (), s32[]{:S(2)}) async-start(), calls=%async_computation.29 | async-start | bytes 4423680 | tf_op jit(solution)/shard_map/all_gather | solution.py:301
  1102.9 777.1 %all-gather.35.cloned.1.call-start = ((), (), s32[]{:S(2)}) async-start(), calls=%async_computation.31 | async-start | bytes 4423680 | tf_op jit(solution)/shard_map/all_gather | solution.py:304
  (60 other events, 601.7 us)
Sparse Core Ops, SparseCore 0:
  9.7 32.0 all-gather.18
  50.4 29.7 all-gather.20
  82.4 27.4 all-gather.22
  111.2 22.2 all-gather.24
  137.6 68.4 all-reduce.12
  207.5 87.1 all-gather.28
  296.2 87.0 all-gather.26
  384.8 87.0 all-gather.30
  498.0 68.4 all-reduce.16
  569.3 42.9 all-reduce.14
  664.8 43.9 reduce-scatter.18
  711.1 42.9 reduce-scatter.20
  757.2 80.8 all-reduce.18
  841.6 129.0 reduce-scatter.34
  974.7 128.0 reduce-scatter.30
  1106.4 128.0 reduce-scatter.32
  1238.3 52.5 reduce-scatter.36
  1295.1 62.9 reduce-scatter.28
  1362.5 62.8 reduce-scatter.22
  1428.7 52.4 reduce-scatter.40
  1485.4 61.4 reduce-scatter.26
  1550.1 52.5 reduce-scatter.38
  1606.5 61.4 reduce-scatter.24
  1669.5 69.9 all-gather.36
  1741.2 68.5 all-gather.32
  1811.3 68.5 all-gather.34
where the time goes:
time: 1900 us; the launch traced here: 1890 us
  waiting for transfers between devices  1420 us (75%)
  blocking collectives  200 us (11%)
  matrix products  148 us (8%)
  local copies, waits for them, and re-layouts  54.8 us (3%)
  other arithmetic  51.8 us (3%)
    reduce_scatter x1, waiting for transfers between devices, local(): lax.psum_scatter(wg_grad.astype(jnp.bfloat16), ('fsdp', 'context'), scatt...  132 us
    reduce_scatter x1, waiting for transfers between devices, local(): lax.psum_scatter(wu_grad.astype(jnp.bfloat16), ('fsdp', 'context'), scatt...  132 us
    reduce_scatter x1, waiting for transfers between devices, local(): lax.psum_scatter(wd_grad.astype(jnp.bfloat16), ('fsdp', 'context'), scatt...  126 us
    unnamed x29, waiting for transfers between devices  96 us
    all_gather x1, waiting for transfers between devices, local(): lax.all_gather(w_up, 'fsdp', axis=0, tiled=True)  82.6 us
    all_gather x1, waiting for transfers between devices, local(): lax.all_gather(w_gate, 'fsdp', axis=0, tiled=True)  79.1 us
    all_gather x1, waiting for transfers between devices, local(): lax.all_gather(w_down, 'fsdp', axis=1, tiled=True)  79.1 us
    all_gather x1, waiting for transfers between devices, local(): lax.all_gather(pieces[9].astype(jnp.bfloat16), 'context', axis=0, tiled=T...  64.4 us
  transfers between devices with their start and end apart: 26, of which 24 were waited for; matrix products, arithmetic and copies ran while one was open for 8% of the time, Pallas kernels for 0%

commit v1 on v0

v1 whole, which is shorter than its diff:
```python
import functools

import jax
import jax.numpy as jnp
from jax import lax
from jax.experimental import pallas as pl
from jax.experimental.pallas import tpu as pltpu
from jax.sharding import PartitionSpec as P

H = 12
KV = 2
HD = 128
BLOCK = 256

EPSILON = 1e-06
ROPE_BASE = 1000000.0
MASKED = -1e30
SCALING = HD ** (-0.5)
LANES = 128
VMEM_LIMIT = 60 << 20

f32 = jnp.float32
bf16 = jnp.bfloat16


def rope_tables(positions):
    halfway = HD // 2
    frequency = ROPE_BASE ** (-(jnp.arange(halfway, dtype=f32) * 2.0 / HD))
    angles = positions.astype(f32)[:, None] * frequency[None, :]
    cosine, sine = jnp.cos(angles), jnp.sin(angles)
    return (jnp.concatenate([cosine, cosine], axis=1), jnp.concatenate([sine, sine], axis=1))


def rotate(field, cosine, sine):
    halfway = HD // 2
    turned = jnp.concatenate([-field[..., halfway:], field[..., :halfway]], axis=-1)
    return field * cosine + turned * sine


def rotate_back(grad_field, cosine, sine):
    halfway = HD // 2
    moved = grad_field * sine
    turned = jnp.concatenate([moved[..., halfway:], -moved[..., :halfway]], axis=-1)
    return grad_field * cosine + turned


def rms_scale(values):
    return lax.rsqrt(jnp.mean(values * values, axis=-1, keepdims=True) + EPSILON)


def norm_back(values, factor, gain, grad_normed):
    gained = gain * grad_normed
    inner = jnp.mean(gained * values, axis=-1, keepdims=True)
    grad_values = factor * gained - values * (factor * factor * factor) * inner
    return (grad_values, jnp.sum(grad_normed * values * factor, axis=0))


def dot(left, right):
    return jnp.dot(left, right, preferred_element_type=f32)


def dot_rows(left, right):
    return lax.dot_general(left, right, (((0,), (0,)), ((), ())), preferred_element_type=f32)


def dot_cols(left, right):
    return lax.dot_general(left, right, (((1,), (1,)), ((), ())), preferred_element_type=f32)


def mask_row(kb_ref, own_block, key_blocks):
    return jnp.concatenate(
        [
            jnp.full((1, BLOCK), jnp.where(kb_ref[j] <= own_block, 0.0, MASKED), f32)
            for j in range(key_blocks)
        ],
        axis=1,
    )


def attention_kernel(key_blocks, kb_ref, q_ref, k_ref, v_ref, o_ref, lse_ref):
    bias = mask_row(kb_ref, kb_ref[pl.program_id(1)], key_blocks)
    scores = dot_cols(q_ref[...], k_ref[...]) * SCALING + bias
    row_max = jnp.max(scores, axis=1, keepdims=True)
    expo = jnp.exp(scores - row_max)
    total = jnp.sum(expo, axis=1, keepdims=True)
    probability = (expo * (1.0 / total)).astype(bf16)
    o_ref[...] = dot(probability, v_ref[...]).astype(bf16)
    lse_ref[0] = row_max + jnp.log(total)


def attention(key_blocks, queries, keys, values):
    rows, width = queries.shape
    heads = width // HD
    whole = pl.BlockSpec(keys.shape, lambda h, i, kb: (0, 0))
    tile = pl.BlockSpec((BLOCK, HD), lambda h, i, kb: (i, h))
    return pl.pallas_call(
        functools.partial(attention_kernel, keys.shape[0] // BLOCK),
        name="attention",
        grid_spec=pltpu.PrefetchScalarGridSpec(
            num_scalar_prefetch=1,
            grid=(heads, rows // BLOCK),
            in_specs=[tile, whole, whole],
            out_specs=[tile, pl.BlockSpec((1, BLOCK, 1), lambda h, i, kb: (h, i, 0))],
        ),
        out_shape=[
            jax.ShapeDtypeStruct((rows, width), bf16),
            jax.ShapeDtypeStruct((heads, rows, 1), f32),
        ],
        compiler_params=pltpu.CompilerParams(vmem_limit_bytes=VMEM_LIMIT),
        cost_estimate=pl.CostEstimate(
            flops=4 * rows * keys.shape[0] * width,
            bytes_accessed=4 * rows * width + 4 * keys.size,
            transcendentals=rows * keys.shape[0] * heads,
        ),
    )(key_blocks, queries, keys, values)


def attention_back_kernel(
    key_blocks,
    kb_ref,
    q_ref,
    do_ref,
    lse_ref,
    cos_ref,
    sin_ref,
    k_ref,
    v_ref,
    dq_ref,
    dk_ref,
    dv_ref,
):
    head, i = pl.program_id(0), pl.program_id(1)

    @pl.when((head == 0) & (i == 0))
    def _():
        dk_ref[...] = jnp.zeros_like(dk_ref)
        dv_ref[...] = jnp.zeros_like(dv_ref)

    bias = mask_row(kb_ref, kb_ref[i], key_blocks)
    scores = dot_cols(q_ref[...], k_ref[...]) * SCALING + bias
    probability = jnp.exp(scores - lse_ref[0])
    grad_probs = dot_cols(do_ref[...], v_ref[...])
    inner = jnp.sum(probability * grad_probs, axis=1, keepdims=True)
    grad_scores = (probability * (grad_probs - inner)).astype(bf16)
    grad_query = dot(grad_scores, k_ref[...]) * SCALING
    moved = grad_query * sin_ref[...]
    sign = jnp.where(lax.broadcasted_iota(jnp.int32, moved.shape, 1) < HD // 2, 1.0, -1.0)
    dq_ref[...] = (
        grad_query * cos_ref[...] + pltpu.roll(moved, HD // 2, 1) * sign
    ).astype(bf16)
    dk_ref[...] += dot_rows(grad_scores, q_ref[...]) * SCALING
    dv_ref[...] += dot_rows(probability.astype(bf16), do_ref[...])


def attention_back(key_blocks, queries, grad_out, lse, cosine, sine, keys, values):
    rows, width = queries.shape
    heads = width // HD
    whole = pl.BlockSpec(keys.shape, lambda h, i, kb: (0, 0))
    tile = pl.BlockSpec((BLOCK, HD), lambda h, i, kb: (i, h))
    table = pl.BlockSpec((BLOCK, HD), lambda h, i, kb: (i, 0))
    return pl.pallas_call(
        functools.partial(attention_back_kernel, keys.shape[0] // BLOCK),
        name="attention_back",
        grid_spec=pltpu.PrefetchScalarGridSpec(
            num_scalar_prefetch=1,
            grid=(heads, rows // BLOCK),
            in_specs=[
                tile,
                tile,
                pl.BlockSpec((1, BLOCK, 1), lambda h, i, kb: (h, i, 0)),
                table,
                table,
                whole,
                whole,
            ],
            out_specs=[tile, whole, whole],
        ),
        out_shape=[
            jax.ShapeDtypeStruct((rows, width), bf16),
            jax.ShapeDtypeStruct(keys.shape, f32),
            jax.ShapeDtypeStruct(keys.shape, f32),
        ],
        compiler_params=pltpu.CompilerParams(vmem_limit_bytes=VMEM_LIMIT),
        cost_estimate=pl.CostEstimate(
            flops=10 * rows * keys.shape[0] * width,
            bytes_accessed=6 * rows * width + 12 * keys.size,
            transcendentals=rows * keys.shape[0] * heads,
        ),
    )(key_blocks, queries, grad_out, lse, cosine, sine, keys, values)


def ffn_kernel(with_dx, base_ref, x_ref, dy_ref, wg_ref, wu_ref, wd_ref, *refs):
    hid_ref, dg_ref, du_ref = refs[-4:-1] if with_dx else refs[-3:]
    gate = dot(x_ref[...], wg_ref[...])
    up = dot(x_ref[...], wu_ref[...])
    grad_hidden = dot_cols(dy_ref[...], wd_ref[...])
    sigma = 1.0 / (1.0 + jnp.exp(-gate))
    gated = gate * sigma
    hid_ref[...] = (gated * up).astype(bf16)
    grad_gate = (grad_hidden * up * (sigma + gated * (1.0 - sigma))).astype(bf16)
    grad_up = (grad_hidden * gated).astype(bf16)
    dg_ref[...] = grad_gate
    du_ref[...] = grad_up
    if with_dx:
        refs[-1][...] = (dot_cols(grad_gate, wg_ref[...]) + dot_cols(grad_up, wu_ref[...])).astype(
            bf16
        )


def ffn(base, normed, grad_out, wg, wu, wd, filled=None):
    rows, width = normed.shape
    units = wg.shape[1]
    tile = 512
    steps = rows // tile
    with_dx = filled is None
    row = lambda n: pl.BlockSpec((tile, n), lambda i, b: (i, 0))
    weight = lambda w: pl.BlockSpec(
        w.shape, lambda i, b: (0, 0), pipeline_mode=pl.Buffered(1)
    )
    out_row = pl.BlockSpec((tile, units), lambda i, b: (i + b[0] * steps, 0))
    out_specs = [out_row] * 3
    out_shape = [jax.ShapeDtypeStruct((2 * rows, units), bf16)] * 3
    in_specs = [row(width), row(width), weight(wg), weight(wu), weight(wd)]
    args = [base, normed, grad_out, wg, wu, wd]
    aliases = {}
    if with_dx:
        out_specs = out_specs + [row(width)]
        out_shape = out_shape + [jax.ShapeDtypeStruct((rows, width), bf16)]
    else:
        in_specs = in_specs + [pl.BlockSpec(memory_space=pl.ANY)] * 3
        args = args + list(filled)
        aliases = {6: 0, 7: 1, 8: 2}
    return pl.pallas_call(
        functools.partial(ffn_kernel, with_dx),
        name="ffn_pair" if with_dx else "ffn_far",
        grid_spec=pltpu.PrefetchScalarGridSpec(
            num_scalar_prefetch=1, grid=(steps,), in_specs=in_specs, out_specs=out_specs
        ),
        out_shape=out_shape,
        input_output_aliases=aliases,
        compiler_params=pltpu.CompilerParams(vmem_limit_bytes=VMEM_LIMIT),
        cost_estimate=pl.CostEstimate(
            flops=2 * rows * width * units * (5 if with_dx else 3),
            bytes_accessed=2 * (3 * width * units + 3 * rows * units + 3 * rows * width),
            transcendentals=rows * units,
        ),
    )(*args)


def build(n_f, n_c, n_t):
    def flip(x, axis, bit):
        size = {"fsdp": n_f, "context": n_c, "tensor": n_t}[axis]
        return lax.ppermute(x, axis, [(i, i ^ bit) for i in range(size)])

    def by_bit(bit, x, other, axis):
        return jnp.where(
            bit == 0,
            jnp.concatenate([x, other], axis=axis),
            jnp.concatenate([other, x], axis=axis),
        )

    def local(
        inputs,
        cotangent,
        blocks,
        attn_gain,
        w_query,
        b_query,
        w_key,
        b_key,
        w_value,
        b_value,
        w_out,
        ffn_gain,
        w_gate,
        w_up,
        w_down,
    ):
        rows, width = inputs.shape
        f = lax.axis_index("fsdp")
        c = lax.axis_index("context")
        t = lax.axis_index("tensor")
        core, parity, pair = t % 2, c % 2, c // 2
        heads = w_query.shape[1] // HD
        group = (t * heads) // (H // KV)
        part = rows // n_t
        units_all = w_gate.shape[1]
        units = -(-units_all // (2 * LANES)) * LANES

        def gather_f(x, axis):
            if n_f == 2:
                return by_bit(f, x, flip(x, "fsdp", 1), axis)
            return lax.all_gather(x, "fsdp", axis=axis, tiled=True)

        def grad_f(left, right, side):
            if n_f == 2:
                half = width // 2
                source = (left, right)[side]
                own = lax.dynamic_slice_in_dim(source, f * half, half, 1)
                far = lax.dynamic_slice_in_dim(source, (1 - f) * half, half, 1)
                pick = lambda x: dot_rows(x, right) if side == 0 else dot_rows(left, x)
                got = flip(pick(far).astype(bf16), "fsdp", 1)
                return pick(own) + got.astype(f32)
            return lax.psum_scatter(
                dot_rows(left, right).astype(bf16), "fsdp", scatter_dimension=side, tiled=True
            ).astype(f32)

        def sum_c(x):
            for bit in (1, 2):
                low = x.astype(bf16)
                x = low.astype(f32) + flip(low, "context", bit).astype(f32)
            return x

        order = (0, 2, 1, 3)

        def mixed(x):
            return jnp.concatenate(
                [lax.dynamic_slice_in_dim(x, (t ^ j) * part, part, 0) for j in order], axis=0
            )

        def natural(x):
            blocks_of = [x[i * part : (i + 1) * part] for i in range(n_t)]
            place = [blocks_of[order.index(j)] for j in range(n_t)]
            out = jnp.stack(place)
            return jnp.concatenate(
                [lax.dynamic_index_in_dim(out, n ^ t, 0, keepdims=False) for n in range(n_t)],
                axis=0,
            )

        def add_half(x, axis, bit):
            half = x.shape[0] // 2
            got = flip(x[half:].astype(bf16), axis, bit)
            return x[:half].astype(f32) + got.astype(f32)

        def scatter_t(x):
            return add_half(add_half(x, "tensor", 1), "tensor", 2)

        def scatter_pair(x):
            return add_half(add_half(add_half(x, "tensor", 1), "context", 1), "tensor", 2)

        def grow(x, axis, bit):
            return jnp.concatenate([x, flip(x, axis, bit)], axis=0)

        def gather_t(x):
            return grow(grow(x, "tensor", 2), "tensor", 1)

        def gather_pair(x):
            return grow(grow(grow(x, "tensor", 2), "context", 1), "tensor", 1)

        small = jnp.concatenate(
            [v.reshape(1, -1) for v in (attn_gain, ffn_gain, b_query, b_key, b_value)], axis=1
        )
        column = lambda w: lax.dynamic_slice_in_dim(w, group * HD, HD, 1)
        w_kv_own = jnp.where(core == 0, column(w_key), column(w_value))
        w_qkv = gather_f(jnp.concatenate([w_query, w_kv_own], axis=1), 0)
        small = gather_f(small, 0)
        w_out_all = gather_f(w_out, 1)
        piece = attn_gain.shape[0]
        gain_first = small[:, :piece].reshape(1, width).astype(f32)
        gain_second = small[:, piece : 2 * piece].reshape(1, width).astype(f32)
        bias_of = lambda lo, n: (
            small[:, lo : lo + n * (HD // n_f)]
            .reshape(n_f, n, HD // n_f)
            .transpose(1, 0, 2)
            .reshape(n, HD)
            .astype(f32)
        )
        at = 2 * piece
        bq = bias_of(at, heads)
        bk = bias_of(at + heads * (HD // n_f), KV)
        bv = bias_of(at + (heads + KV) * (HD // n_f), KV)
        b_kv = lax.dynamic_index_in_dim(jnp.where(core == 0, bk, bv), group, 0)

        def unit_slice(w, axis):
            low = lax.slice_in_dim(w, 0, units, axis=axis)
            high = lax.slice_in_dim(w, units, units_all, axis=axis)
            pad = [(0, 0), (0, 0)]
            pad[axis] = (0, 2 * units - units_all)
            return jnp.where(parity == 0, low, jnp.pad(high, pad))

        wg = gather_f(unit_slice(w_gate, 1), 0)
        wu = gather_f(unit_slice(w_up, 1), 0)
        wd = gather_f(unit_slice(w_down, 0), 1)

        dy_own = mixed(cotangent)[: 2 * part]
        dy_near = jnp.concatenate([dy_own, flip(dy_own, "context", 1)], axis=0)
        dy_pair = grow(dy_near, "tensor", 1)
        dy_far = grow(grow(flip(dy_own, "context", 2), "context", 1), "tensor", 1)

        seq_blocks = blocks[0].reshape(n_c, -1)
        own_blocks = seq_blocks.shape[1]
        key_blocks = jnp.concatenate(
            [lax.dynamic_index_in_dim(seq_blocks, c ^ j, 0, keepdims=False) for j in range(n_c)]
        )
        positions = (
            key_blocks[:own_blocks, None] * BLOCK + jnp.arange(BLOCK, dtype=jnp.int32)[None, :]
        ).reshape(-1)
        cosine, sine = rope_tables(positions)
        inputs_f = inputs.astype(f32)
        factor_first = rms_scale(inputs_f)
        normed = (inputs_f * factor_first * gain_first).astype(bf16)
        qkv_pre = dot(normed, w_qkv)
        query_pre = qkv_pre[:, : heads * HD].reshape(rows, heads, HD) + bq
        queries = (
            rotate(query_pre, cosine[:, None, :], sine[:, None, :])
            .astype(bf16)
            .reshape(rows, heads * HD)
        )
        kv_pre = qkv_pre[:, heads * HD :] + b_kv
        kv_own = jnp.where(core == 0, rotate(kv_pre, cosine, sine), kv_pre).astype(bf16)
        kv_whole = grow(grow(kv_own, "context", 1), "context", 2)
        kv_other = flip(kv_whole, "tensor", 1)
        keys = jnp.where(core == 0, kv_whole, kv_other)
        values = jnp.where(core == 0, kv_other, kv_whole)
        attended, lse = attention(key_blocks, queries, keys, values)

        attended_mixed = mixed(attended)
        attn_sum = scatter_t(dot(attended_mixed, w_out_all))
        middle = lax.dynamic_slice_in_dim(inputs, t * part, part, 0).astype(f32) + attn_sum

        factor_second = rms_scale(middle)
        normed2 = (middle * factor_second * gain_second).astype(bf16)
        normed2_pair = gather_pair(normed2)
        normed2_far = gather_pair(flip(normed2, "context", 2))
        base = pair.reshape(1)
        *half_filled, dx_part = ffn(base, normed2_pair, dy_pair, wg, wu, wd)
        grad_normed2 = scatter_pair(dx_part)
        hidden, grad_gate, grad_up = ffn(
            1 - base, normed2_far, dy_far, wg, wu, wd, filled=half_filled
        )
        hidden_pair = lax.dynamic_slice_in_dim(hidden, pair * 2 * rows, 2 * rows, 0)
        final = middle + scatter_pair(dot(hidden_pair, wd))
        outputs = natural(gather_t(final.astype(bf16)))

        normed2_all = by_bit(pair, normed2_pair, normed2_far, 0)
        dy_all = by_bit(pair, dy_pair, dy_far, 0)

        def unit_grad(left, right, side):
            own = grad_f(left, right, side).astype(bf16)
            other = flip(own, "context", 1)
            whole = by_bit(parity, own, other, 1 - side)
            return lax.slice_in_dim(whole, 0, units_all, axis=1 - side).astype(f32)

        wd_grad = unit_grad(hidden, dy_all, 1)
        wg_grad = unit_grad(normed2_all, grad_gate, 0)
        wu_grad = unit_grad(normed2_all, grad_up, 0)

        grad_mid_norm, ffn_gain_grad = norm_back(middle, factor_second, gain_second, grad_normed2)
        dy_part = lax.dynamic_slice_in_dim(cotangent, t * part, part, 0).astype(f32)
        grad_middle = dy_part + grad_mid_norm
        grad_middle_low = gather_t(grad_middle.astype(bf16))
        wo_grad = sum_c(grad_f(attended_mixed, grad_middle_low, 1))
        grad_attended = natural(dot_cols(grad_middle_low, w_out_all).astype(bf16))

        dq_low, dk, dv = attention_back(
            key_blocks, queries, grad_attended, lse, cosine, sine, keys, values
        )
        dkv_keep = jnp.where(core == 0, dk, dv)
        dkv_send = jnp.where(core == 0, dv, dk).astype(bf16)
        dkv = dkv_keep + flip(dkv_send, "tensor", 1).astype(f32)
        dkv = add_half(add_half(dkv, "context", 2), "context", 1)
        dkv_low = jnp.where(core == 0, rotate_back(dkv, cosine, sine), dkv).astype(bf16)
        wq_grad = sum_c(grad_f(normed, dq_low, 0))
        wkv_own = sum_c(grad_f(normed, dkv_low, 0)).astype(bf16)
        wkv_stack = gather_t(wkv_own)
        depth = wkv_own.shape[0]
        wkv_of = [wkv_stack[order.index(j) * depth : (order.index(j) + 1) * depth] for j in range(n_t)]
        wkv_stack = jnp.stack(wkv_of)
        wkv_rank = [
            lax.dynamic_index_in_dim(wkv_stack, n ^ t, 0, keepdims=False).astype(f32)
            for n in range(n_t)
        ]
        wk_grad = jnp.concatenate(wkv_rank[0::2], axis=1)
        wv_grad = jnp.concatenate(wkv_rank[1::2], axis=1)

        d_qkv = mixed(jnp.concatenate([dq_low, dkv_low], axis=1))
        grad_normed = scatter_t(dot_cols(d_qkv, w_qkv))
        inputs_part = lax.dynamic_slice_in_dim(inputs, t * part, part, 0).astype(f32)
        factor_part = lax.dynamic_slice_in_dim(factor_first, t * part, part, 0)
        grad_in_norm, attn_gain_grad = norm_back(inputs_part, factor_part, gain_first, grad_normed)
        input_grad = natural(gather_t((grad_middle + grad_in_norm).astype(bf16)))

        bq_grad = jnp.sum(dq_low.astype(f32), axis=0)
        bkv_grad = jnp.sum(dkv_low.astype(f32), axis=0)
        slots = jnp.zeros((n_t, (heads + 1) * HD), f32)
        slots = lax.dynamic_update_slice(
            slots, jnp.concatenate([bq_grad, bkv_grad])[None], (t, 0)
        )
        packed = lax.psum(
            jnp.concatenate([attn_gain_grad, ffn_gain_grad, slots.reshape(-1)]),
            ("fsdp", "context", "tensor"),
        )
        attn_gain_grad = lax.dynamic_slice_in_dim(packed, f * piece, piece, 0)
        ffn_gain_grad = lax.dynamic_slice_in_dim(packed, width + f * piece, piece, 0)
        slots = packed[2 * width :].reshape(n_t, heads + 1, HD)
        slots = lax.dynamic_slice_in_dim(slots, f * (HD // n_f), HD // n_f, 2)
        bq_out = lax.dynamic_index_in_dim(slots, t, 0, keepdims=False)[:heads]
        bk_out = slots[0::2, heads]
        bv_out = slots[1::2, heads]

        return (
            outputs,
            input_grad,
            attn_gain_grad,
            wq_grad,
            bq_out,
            wk_grad,
            bk_out,
            wv_grad,
            bv_out,
            wo_grad,
            ffn_gain_grad,
            wg_grad,
            wu_grad,
            wd_grad,
        )

    return local


def solution(mesh):
    in_specs = (
        P(("fsdp", "context"), None),
        P(("fsdp", "context"), None),
        P("fsdp", None),
        P("fsdp"),
        P("fsdp", "tensor"),
        P("tensor", "fsdp"),
        P("fsdp", None),
        P(None, "fsdp"),
        P("fsdp", None),
        P(None, "fsdp"),
        P("tensor", "fsdp"),
        P("fsdp"),
        P("fsdp", "tensor"),
        P("fsdp", "tensor"),
        P("tensor", "fsdp"),
    )
    out_specs = (
        P(("fsdp", "context"), None),
        P(("fsdp", "context"), None),
        P("fsdp"),
        P("fsdp", "tensor"),
        P("tensor", "fsdp"),
        P("fsdp", None),
        P(None, "fsdp"),
        P("fsdp", None),
        P(None, "fsdp"),
        P("tensor", "fsdp"),
        P("fsdp"),
        P("fsdp", "tensor"),
        P("fsdp", "tensor"),
        P("tensor", "fsdp"),
    )
    local = build(mesh.shape["fsdp"], mesh.shape["context"], mesh.shape["tensor"])
    return jax.shard_map(local, mesh=mesh, in_specs=in_specs, out_specs=out_specs, check_vma=False)
```

time: 1900 us -> 746 us (0.39)
  waiting for transfers between devices: 1420 us -> 301 us
  blocking collectives: 200 us -> 41.2 us
  matrix products: 148 us -> 63.4 us
  Pallas kernels: 0 us -> 76.7 us
  other arithmetic: 51.8 us -> 108 us
  local copies, waits for them, and re-layouts: 54.8 us -> 101 us
  starting transfers between devices: 1.92 us -> 40.9 us
    reduce_scatter x9 -> x0, waiting for transfers between devices: 645 us -> none  [the longest x1 132 us: local(): lax.psum_scatter(wg_grad.astype(jnp.bfloat16), ('fsdp', 'context'), scatt...]
    all_gather x10 -> x0, waiting for transfers between devices: 465 us -> none  [the longest x1 82.6 us: local(): lax.all_gather(w_up, 'fsdp', axis=0, tiled=True)]
    ppermute x0 -> x57, waiting for transfers between devices: none -> 301 us  [flip(): return lax.ppermute(x, axis, [(i, i ^ bit) for i in range(size)])]
    psum x4 -> x0, waiting for transfers between devices: 215 us -> none  [the longest x1 61.9 us: local(): middle = inputs_f + lax.psum(attn_part, 'tensor')]
    all_gather x14 -> x0, blocking collectives: 147 us -> none  [the longest x1 19.9 us: local(): lax.all_gather(w_key, 'fsdp', axis=0, tiled=True)]
    unnamed x29 -> x0, waiting for transfers between devices: 96 us -> none
    dot_general x39 -> x17, matrix products: 148 us -> 63.4 us  [the longest x12 46.2 us: dot_rows(): lax.dot_general(left, right, (((0,), (0,)), ((), ())), preferred_element_...]
    pallas_call x0 -> x4, Pallas kernels: none -> 76.7 us  [the longest x2 51 us: ffn(): pl.pallas_call(functools.partial(ffn_kernel, with_dx), name='ffn_pair' if...]
  transfers between devices with their start and end apart: 26 -> 57, of which waited for: 24 -> 25; matrix products, arithmetic and copies ran while one was open for 8% -> 35% of each run, Pallas kernels for 0% -> 10%
where the time goes in v1:
time: 746 us; the launch traced here: 734 us
  waiting for transfers between devices  301 us (40%)
  other arithmetic  108 us (14%)
  local copies, waits for them, and re-layouts  101 us (14%)
  Pallas kernels  76.7 us (10%)
  matrix products  63.4 us (8%)
  blocking collectives  41.2 us (6%)
  starting transfers between devices  40.9 us (5%)
    ppermute x57, waiting for transfers between devices, flip(): return lax.ppermute(x, axis, [(i, i ^ bit) for i in range(size)])  301 us
    unnamed x181, local copies, waits for them, and re-layouts  59.9 us
    pallas_call x2, Pallas kernels, ffn(): pl.pallas_call(functools.partial(ffn_kernel, with_dx), name='ffn_pair' if...  51 us
    dot_general x12, matrix products, dot_rows(): lax.dot_general(left, right, (((0,), (0,)), ((), ())), preferred_element_...  46.2 us
    psum x1, blocking collectives, local(): lax.psum(jnp.concatenate([attn_gain_grad, ffn_gain_grad, slots.reshape(-1...  41.2 us
    ppermute x57, starting transfers between devices, flip(): return lax.ppermute(x, axis, [(i, i ^ bit) for i in range(size)])  40.9 us
    select_n x6, other arithmetic, by_bit(): jnp.where(bit == 0, jnp.concatenate([x, other], axis=axis), jnp.concatena...  28 us
    convert_element_type x3, other arithmetic, unit_grad(): return lax.slice_in_dim(whole, 0, units_all, axis=1 - side).astype(f32)  17.3 us
  transfers between devices with their start and end apart: 57, of which 25 were waited for; matrix products, arithmetic and copies ran while one was open for 35% of the time, Pallas kernels for 10%

profile of v1, /device:TPU:0, one launch (start us, length us, event | category | flops | bytes accessed | tf_op | source)
XLA Modules:
  0.0 734.0 jit_solution(3668864341605845027)
XLA Ops:
  86.0 16.4 %collective-permute-done.3 = bf16[1024,128]{1,0:T(8,128)(2,1)S(1)} collective-permute-done((bf16[1024,128]{1,0:T(8,128)(2,1)S(1)}, bf16[1024,128]{1,0:T(8,128)(2,1)S(1)}, u32[]{:S(2)}, u32[]{:S(2)}) %collective-permute-start.3) | collective-permute-done | bytes 262176 | tf_op jit(solution)/shard_map/ppermute | solution.py:253
  107.2 10.3 %attention.1 = (bf16[512,384]{1,0:T(8,128)(2,1)}, f32[3,512,1]{2,1,0:T(8,128)}) custom-call(s32[8]{0:T(128)} %pad_add_fusion.kb_ref, bf16[512,384]{1,0:T(8,128)(2,1)} %add_convert_fusion.2.q_ref, bf16[2048,128]{1,0:T(8,128)(2,1)} %get-tuple-element.113.k_ref, bf16[2048,128]{1,0:T(8,128)(2,1)} %get-tuple-element.112.v_ref), custom_call_target="tpu_custom_call" | custom-call | flops 1610612736 | bytes 1835008 | tf_op jit(solution)/shard_map/attention/pallas_call | solution.py:96
  127.0 7.5 %collective-permute-done.15 = bf16[768,1152]{1,0:T(8,128)(2,1)} collective-permute-done((bf16[768,1152]{1,0:T(8,128)(2,1)}, bf16[768,1152]{1,0:T(8,128)(2,1)}, u32[]{:S(2)}, u32[]{:S(2)}) %collective-permute-start.15) | collective-permute-done | bytes 1769504 | tf_op jit(solution)/shard_map/ppermute | solution.py:253
  141.3 28.4 %collective-permute-done.17 = bf16[1152,768]{1,0:T(8,128)(2,1)} collective-permute-done((bf16[1152,768]{1,0:T(8,128)(2,1)}, bf16[1152,768]{1,0:T(8,128)(2,1)}, u32[]{:S(2)}, u32[]{:S(2)}) %collective-permute-start.17) | collective-permute-done | bytes 1769504 | tf_op jit(solution)/shard_map/ppermute | solution.py:253
  200.5 6.1 broadcast_select_fusion
  206.6 10.2 %collective-permute-done.19 = bf16[256,1536]{1,0:T(8,128)(2,1)S(1)} collective-permute-done((bf16[256,1536]{1,0:T(8,128)(2,1)}, bf16[256,1536]{1,0:T(8,128)(2,1)S(1)}, u32[]{:S(2)}, u32[]{:S(2)}) %collective-permute-start.19) | collective-permute-done | bytes 786464 | tf_op jit(solution)/shard_map/ppermute | solution.py:253
  221.8 16.5 %collective-permute-done.10 = bf16[256,1536]{1,0:T(8,128)(2,1)S(1)} collective-permute-done((bf16[256,1536]{1,0:T(8,128)(2,1)S(1)}, bf16[256,1536]{1,0:T(8,128)(2,1)S(1)}, u32[]{:S(2)}, u32[]{:S(2)}) %collective-permute-start.10) | collective-permute-done | bytes 786464 | tf_op jit(solution)/shard_map/ppermute | solution.py:253
  243.4 31.2 %ffn_pair.1 = (bf16[2048,1152]{1,0:T(8,128)(2,1)}, bf16[2048,1152]{1,0:T(8,128)(2,1)}, bf16[2048,1152]{1,0:T(8,128)(2,1)}, bf16[1024,1536]{1,0:T(8,128)(2,1)}) custom-call(s32[1]{0:T(128)} %bitcast.10.base_ref, bf16[1024,1536]{1,0:T(8,128)(2,1)} %pad_maximum_fusion.8.x_ref, bf16[1024,1536]{1,0:T(8,128)(2,1)} %pad_maximum_fusion.9.dy_ref, ...), custom_call_target="tpu_custom_call" | custom-call | flops 18119393280 | bytes 27131904 | tf_op jit(solution)/shard_map/ffn_pair/pallas_call | solution.py:233
  281.6 19.8 %ffn_far.1 = (bf16[2048,1152]{1,0:T(8,128)(2,1)}, bf16[2048,1152]{1,0:T(8,128)(2,1)}, bf16[2048,1152]{1,0:T(8,128)(2,1)}) custom-call(s32[1]{0:T(128)S(6)} %sub.26.base_ref, bf16[1024,1536]{1,0:T(8,128)(2,1)} %pad_maximum_fusion.6.x_ref, bf16[1024,1536]{1,0:T(8,128)(2,1)} %pad_maximum_fusion.7.dy_ref, ...), custom_call_target="tpu_custom_call", output_to_operand_aliasing={{0}: (6, {}), {1}: (7, {}), {2}: (8, {})} | custom-call | flops 10871635968 | bytes 27131904 | tf_op jit(solution)/shard_map/ffn_far/pallas_call | solution.py:233
  301.4 6.9 fusion.18
  317.8 6.1 broadcast_select_fusion.1
  323.9 8.9 %convolution_convert_fusion.2 = bf16[768,1152]{1,0:T(8,128)(2,1)} fusion(bf16[2048,1152]{1,0:T(8,128)(2,1)} %get-tuple-element.36, bf16[2048,1536]{1,0:T(8,128)(2,1)} %broadcast_select_fusion.1, s32[]{:T(128)S(6)} %select_n.330), kind=kOutput, calls=%fused_computation.27 | convolution fusion | flops 3624763392 | bytes 9633796 | tf_op jit(solution)/shard_map/dot_general | solution.py:63
  332.9 8.2 %convolution_convert_fusion.1 = bf16[768,1152]{1,0:T(8,128)(2,1)} fusion(bf16[2048,1152]{1,0:T(8,128)(2,1)} %get-tuple-element.37, bf16[2048,1536]{1,0:T(8,128)(2,1)S(1)} %copy-done.21, s32[]{:T(128)S(6)} %select_n.330), kind=kOutput, calls=%fused_computation.26 | convolution fusion | flops 3624763392 | bytes 9633796 | tf_op jit(solution)/shard_map/dot_general | solution.py:63
  353.9 29.0 %collective-permute-done.53 = bf16[768,1152]{1,0:T(8,128)(2,1)} collective-permute-done((bf16[768,1152]{1,0:T(8,128)(2,1)}, bf16[768,1152]{1,0:T(8,128)(2,1)}, u32[]{:S(2)}, u32[]{:S(2)}) %collective-permute-start.53) | collective-permute-done | bytes 1769504 | tf_op jit(solution)/shard_map/ppermute | solution.py:253
  382.9 8.1 %fusion.7 = bf16[768,1152]{1,0:T(8,128)(2,1)} fusion(bf16[768,1152]{1,0:T(8,128)(2,1)} %collective-permute-done.53, bf16[2048,1152]{1,0:T(8,128)(2,1)} %get-tuple-element.37, bf16[2048,1536]{1,0:T(8,128)(2,1)S(1)} %copy-done.21, s32[]{:T(128)S(6)} %select_n.329), kind=kOutput, calls=%fused_computation.23 | convolution fusion | flops 3626532864 | bytes 11403268 | tf_op jit(solution)/shard_map/dot_general | solution.py:63
  391.2 66.5 %collective-permute-done.51 = bf16[768,1152]{1,0:T(8,128)(2,1)} collective-permute-done((bf16[768,1152]{1,0:T(8,128)(2,1)}, bf16[768,1152]{1,0:T(8,128)(2,1)}, u32[]{:S(2)}, u32[]{:S(2)}) %collective-permute-start.51) | collective-permute-done | bytes 1769504 | tf_op jit(solution)/shard_map/ppermute | solution.py:253
  457.8 7.0 fusion.6
  467.8 9.7 %collective-permute-done.30 = bf16[128,1536]{1,0:T(8,128)(2,1)S(1)} collective-permute-done((bf16[128,1536]{1,0:T(8,128)(2,1)S(1)}, bf16[128,1536]{1,0:T(8,128)(2,1)S(1)}, u32[]{:S(2)}, u32[]{:S(2)}) %collective-permute-start.30) | collective-permute-done | bytes 393248 | tf_op jit(solution)/shard_map/ppermute | solution.py:253
  477.8 6.0 collective-permute-done.25
  506.7 6.4 fusion.3
  513.1 6.2 fusion.1
  519.3 7.9 %copy.78 = f32[768,2240]{0,1:T(8,128)} copy(f32[768,2240]{1,0:T(8,128)} %fusion.3) | data formatting | bytes 13762560
  527.2 7.9 %copy.79 = f32[768,2240]{0,1:T(8,128)} copy(f32[768,2240]{1,0:T(8,128)} %fusion.1) | data formatting | bytes 13762560
  535.1 7.6 %collective-permute-done.56 = bf16[1152,768]{1,0:T(8,128)(2,1)} collective-permute-done((bf16[1152,768]{1,0:T(8,128)(2,1)S(1)}, bf16[1152,768]{1,0:T(8,128)(2,1)}, u32[]{:S(2)}, u32[]{:S(2)}) %collective-permute-start.56) | collective-permute-done | bytes 1769504 | tf_op jit(solution)/shard_map/ppermute | solution.py:253
  550.9 15.4 %attention_back.1 = (bf16[512,384]{1,0:T(8,128)(2,1)}, f32[2048,128]{1,0:T(8,128)}, f32[2048,128]{1,0:T(8,128)}) custom-call(s32[8]{0:T(128)} %pad_add_fusion.kb_ref, bf16[512,384]{1,0:T(8,128)(2,1)} %add_convert_fusion.2.q_ref, bf16[512,384]{1,0:T(8,128)(2,1)} %pad_maximum_fusion.30.do_ref, f32[3,512,1]{2,1,0:T(8,128)} %get-tuple-element.32.lse_ref, ...), custom_call_target="tpu_custom_call" | custom-call | flops 4026531840 | bytes 4325376 | tf_op jit(solution)/shard_map/attention_back/pallas_call | solution.py:161
  575.8 10.2 %collective-permute-done.48 = bf16[384,768]{1,0:T(8,128)(2,1)S(1)} collective-permute-done((bf16[384,768]{1,0:T(8,128)(2,1)S(1)}, bf16[384,768]{1,0:T(8,128)(2,1)S(1)}, u32[]{:S(2)}, u32[]{:S(2)}) %collective-permute-start.48) | collective-permute-done | bytes 589856 | tf_op jit(solution)/shard_map/ppermute | solution.py:253
  590.1 7.9 %collective-permute-done.40 = bf16[768,384]{1,0:T(8,128)(2,1)S(1)} collective-permute-done((bf16[768,384]{1,0:T(8,128)(2,1)S(1)}, bf16[768,384]{1,0:T(8,128)(2,1)S(1)}, u32[]{:S(2)}, u32[]{:S(2)}) %collective-permute-start.40) | collective-permute-done | bytes 589856 | tf_op jit(solution)/shard_map/ppermute | solution.py:253
  599.8 6.8 collective-permute-done.35
  626.7 18.5 %collective-permute-done.45 = bf16[768,128]{0,1:T(8,128)(2,1)S(1)} collective-permute-done((bf16[768,128]{0,1:T(8,128)(2,1)S(1)}, bf16[768,128]{0,1:T(8,128)(2,1)S(1)}, u32[]{:S(2)}, u32[]{:S(2)}) %collective-permute-start.45) | collective-permute-done | bytes 196640 | tf_op jit(solution)/shard_map/ppermute | solution.py:253
  653.1 17.4 %collective-permute-done.50 = bf16[384,768]{1,0:T(8,128)(2,1)S(1)} collective-permute-done((bf16[384,768]{1,0:T(8,128)(2,1)S(1)}, bf16[384,768]{1,0:T(8,128)(2,1)S(1)}, u32[]{:S(2)}, u32[]{:S(2)}) %collective-permute-start.50) | collective-permute-done | bytes 589856 | tf_op jit(solution)/shard_map/ppermute | solution.py:253
  671.6 11.4 %collective-permute-done.42 = bf16[768,384]{1,0:T(8,128)(2,1)S(1)} collective-permute-done((bf16[768,384]{1,0:T(8,128)(2,1)S(1)}, bf16[768,384]{1,0:T(8,128)(2,1)S(1)}, u32[]{:S(2)}, u32[]{:S(2)}) %collective-permute-start.42) | collective-permute-done | bytes 589856 | tf_op jit(solution)/shard_map/ppermute | solution.py:253
  686.4 41.2 %psum.7 = f32[5120]{0:T(1024)S(1)} all-reduce(f32[5120]{0:T(1024)S(1)} %pad_maximum_fusion.35), channel_id=1, replica_groups=mesh['fsdp'=2,'context'=4,'tensor'=4] {'fsdp','context','tensor'}, use_global_device_ids=true, to_apply=%region_8.9 | all-reduce | flops 5120 | bytes 40960 | tf_op jit(solution)/shard_map/psum | solution.py:489
  (448 shorter events, 264.1 us)
Async XLA Ops:
  5.4 76.8 %collective-permute-start.21 = (bf16[256,1536]{1,0:T(8,128)(2,1)}, bf16[256,1536]{1,0:T(8,128)(2,1)}, u32[]{:S(2)}, u32[]{:S(2)}) collective-permute-start(bf16[256,1536]{1,0:T(8,128)(2,1)} %pad_maximum_fusion.21), channel_id=1, source_target_pairs={{0,4},{4,0},{8,12},{12,8},{1,5},{5,1},{9,13},{13,9},{2,6},{6,2},{1... | collective-permute-start | bytes 2359304 | tf_op jit(solution)/shard_map/ppermute | solution.py:253
  8.5 70.7 %collective-permute-start.12 = (bf16[256,1536]{1,0:T(8,128)(2,1)}, bf16[256,1536]{1,0:T(8,128)(2,1)S(1)}, u32[]{:S(2)}, u32[]{:S(2)}) collective-permute-start(bf16[256,1536]{1,0:T(8,128)(2,1)} %pad_maximum_fusion.21), channel_id=1, source_target_pairs={{0,8},{4,12},{8,0},{12,4},{1,9},{5,13},{9,1},{13,5},{2,10},{6,14},... | collective-permute-start | bytes 2359304 | tf_op jit(solution)/shard_map/ppermute | solution.py:253
  11.4 43.2 %collective-permute-start = (bf16[1,1984]{1,0:T(2,128)(2,1)S(1)}, bf16[1,1984]{1,0:T(2,128)(2,1)S(1)}, u32[]{:S(2)}, u32[]{:S(2)}) collective-permute-start(bf16[1,1984]{1,0:T(2,128)(2,1)S(1)} %concatenate.194), channel_id=1, source_target_pairs={{0,16},{16,0},{1,17},{17,1},{2,18},{18,2},{3,19},{19,3},{4,20},{20... | collective-permute-start | bytes 11912 | tf_op jit(solution)/shard_map/ppermute | solution.py:253
  13.0 105.7 %collective-permute-start.5 = (bf16[384,768]{1,0:T(8,128)(2,1)}, bf16[384,768]{1,0:T(8,128)(2,1)}, u32[]{:S(2)}, u32[]{:S(2)}) collective-permute-start(bf16[384,768]{1,0:T(8,128)(2,1)} %param.25), channel_id=1, source_target_pairs={{0,16},{16,0},{1,17},{17,1},{2,18},{18,2},{3,19},{19,3},{4,20},{20... | collective-permute-start | bytes 1769480 | tf_op jit(solution)/shard_map/ppermute | solution.py:253
  14.5 41.7 %collective-permute-start.1 = (bf16[768,512]{1,0:T(8,128)(2,1)}, bf16[768,512]{1,0:T(8,128)(2,1)}, u32[]{:S(2)}, u32[]{:S(2)}) collective-permute-start(bf16[768,512]{1,0:T(8,128)(2,1)} %pad_maximum_fusion.19), channel_id=1, source_target_pairs={{0,16},{16,0},{1,17},{17,1},{2,18},{18,2},{3,19},{19,3},{4,20},{20... | collective-permute-start | bytes 2359304 | tf_op jit(solution)/shard_map/ppermute | solution.py:253
  54.6 66.6 %collective-permute-start.16 = (bf16[768,1152]{1,0:T(8,128)(2,1)}, bf16[768,1152]{1,0:T(8,128)(2,1)}, u32[]{:S(2)}, u32[]{:S(2)}) collective-permute-start(bf16[768,1152]{1,0:T(8,128)(2,1)} %pad_select_fusion.1), channel_id=1, source_target_pairs={{0,16},{16,0},{1,17},{17,1},{2,18},{18,2},{3,19},{19,3},{4,20},{20... | collective-permute-start | bytes 5308424 | tf_op jit(solution)/shard_map/ppermute | solution.py:253
  79.2 55.2 %collective-permute-start.15 = (bf16[768,1152]{1,0:T(8,128)(2,1)}, bf16[768,1152]{1,0:T(8,128)(2,1)}, u32[]{:S(2)}, u32[]{:S(2)}) collective-permute-start(bf16[768,1152]{1,0:T(8,128)(2,1)} %pad_select_fusion.2), channel_id=1, source_target_pairs={{0,16},{16,0},{1,17},{17,1},{2,18},{18,2},{3,19},{19,3},{4,20},{20... | collective-permute-start | bytes 5308424 | tf_op jit(solution)/shard_map/ppermute | solution.py:253
  102.4 67.3 %collective-permute-start.17 = (bf16[1152,768]{1,0:T(8,128)(2,1)}, bf16[1152,768]{1,0:T(8,128)(2,1)}, u32[]{:S(2)}, u32[]{:S(2)}) collective-permute-start(bf16[1152,768]{1,0:T(8,128)(2,1)} %pad_select_fusion), channel_id=1, source_target_pairs={{0,16},{16,0},{1,17},{17,1},{2,18},{18,2},{3,19},{19,3},{4,20},{20... | collective-permute-start | bytes 5308424 | tf_op jit(solution)/shard_map/ppermute | solution.py:253
  105.5 69.8 %collective-permute-start.22 = (bf16[512,1536]{1,0:T(8,128)(2,1)}, bf16[512,1536]{1,0:T(8,128)(2,1)}, u32[]{:S(2)}, u32[]{:S(2)}) collective-permute-start(bf16[512,1536]{1,0:T(8,128)(2,1)} %pad_maximum_fusion.13), channel_id=1, source_target_pairs={{0,1},{1,0},{2,3},{3,2},{4,5},{5,4},{6,7},{7,6},{8,9},{9,8},{10,11... | collective-permute-start | bytes 4718600 | tf_op jit(solution)/shard_map/ppermute | solution.py:253
  118.6 64.2 %collective-permute-start.14 = (bf16[512,1536]{1,0:T(8,128)(2,1)}, bf16[512,1536]{1,0:T(8,128)(2,1)S(1)}, u32[]{:S(2)}, u32[]{:S(2)}) collective-permute-start(bf16[512,1536]{1,0:T(8,128)(2,1)} %pad_maximum_fusion.11), channel_id=1, source_target_pairs={{0,1},{1,0},{2,3},{3,2},{4,5},{5,4},{6,7},{7,6},{8,9},{9,8},{10,11... | collective-permute-start | bytes 4718600 | tf_op jit(solution)/shard_map/ppermute | solution.py:253
  139.8 39.0 %collective-permute-start.7 = (bf16[128,1536]{1,0:T(8,128)(2,1)S(1)}, bf16[128,1536]{1,0:T(8,128)(2,1)S(1)}, u32[]{:S(2)}, u32[]{:S(2)}) collective-permute-start(bf16[128,1536]{1,0:T(8,128)(2,1)S(1)} %slice.387), channel_id=1, source_target_pairs={{0,2},{1,3},{2,0},{3,1},{4,6},{5,7},{6,4},{7,5},{8,10},{9,11},{10,... | collective-permute-start | bytes 1179656 | tf_op jit(solution)/shard_map/ppermute | solution.py:253
  239.5 38.3 %collective-permute-start.11 = (bf16[512,1536]{1,0:T(8,128)(2,1)}, bf16[512,1536]{1,0:T(8,128)(2,1)S(1)}, u32[]{:S(2)}, u32[]{:S(2)}) collective-permute-start(bf16[512,1536]{1,0:T(8,128)(2,1)} %pad_maximum_fusion.10), channel_id=1, source_target_pairs={{0,1},{1,0},{2,3},{3,2},{4,5},{5,4},{6,7},{7,6},{8,9},{9,8},{10,11... | collective-permute-start | bytes 4718600 | tf_op jit(solution)/shard_map/ppermute | solution.py:253
  277.3 70.4 %collective-permute-start.28 = (bf16[512,1536]{1,0:T(8,128)(2,1)}, bf16[512,1536]{1,0:T(8,128)(2,1)}, u32[]{:S(2)}, u32[]{:S(2)}) collective-permute-start(bf16[512,1536]{1,0:T(8,128)(2,1)} %slice.234), channel_id=1, source_target_pairs={{0,1},{1,0},{2,3},{3,2},{4,5},{5,4},{6,7},{7,6},{8,9},{9,8},{10,11... | collective-permute-start | bytes 4718600 | tf_op jit(solution)/shard_map/ppermute | solution.py:253
  308.6 41.4 %collective-permute-start.23 = (bf16[512,1536]{1,0:T(8,128)(2,1)S(1)}, bf16[512,1536]{1,0:T(8,128)(2,1)}, u32[]{:S(2)}, u32[]{:S(2)}) collective-permute-start(bf16[512,1536]{1,0:T(8,128)(2,1)S(1)} %slice.379), channel_id=1, source_target_pairs={{0,1},{1,0},{2,3},{3,2},{4,5},{5,4},{6,7},{7,6},{8,9},{9,8},{10,11... | collective-permute-start | bytes 4718600 | tf_op jit(solution)/shard_map/ppermute | solution.py:253
  341.0 41.9 %collective-permute-start.53 = (bf16[768,1152]{1,0:T(8,128)(2,1)}, bf16[768,1152]{1,0:T(8,128)(2,1)}, u32[]{:S(2)}, u32[]{:S(2)}) collective-permute-start(bf16[768,1152]{1,0:T(8,128)(2,1)} %convolution_convert_fusion.1), channel_id=1, source_target_pairs={{0,16},{16,0},{1,17},{17,1},{2,18},{18,2},{3,19},{19,3},{4,20},{20... | collective-permute-start | bytes 5308424 | tf_op jit(solution)/shard_map/ppermute | solution.py:253
  345.6 141.5 %collective-permute-start.55 = (bf16[1152,768]{1,0:T(8,128)(2,1)S(1)}, bf16[1152,768]{1,0:T(8,128)(2,1)S(1)}, u32[]{:S(2)}, u32[]{:S(2)}) collective-permute-start(bf16[1152,768]{1,0:T(8,128)(2,1)S(1)} %convolution_convert_fusion), channel_id=1, source_target_pairs={{0,16},{16,0},{1,17},{17,1},{2,18},{18,2},{3,19},{19,3},{4,20},{20... | collective-permute-start | bytes 5308424 | tf_op jit(solution)/shard_map/ppermute | solution.py:253
  347.2 110.6 %collective-permute-start.51 = (bf16[768,1152]{1,0:T(8,128)(2,1)}, bf16[768,1152]{1,0:T(8,128)(2,1)}, u32[]{:S(2)}, u32[]{:S(2)}) collective-permute-start(bf16[768,1152]{1,0:T(8,128)(2,1)} %convolution_convert_fusion.2), channel_id=1, source_target_pairs={{0,16},{16,0},{1,17},{17,1},{2,18},{18,2},{3,19},{19,3},{4,20},{20... | collective-permute-start | bytes 5308424 | tf_op jit(solution)/shard_map/ppermute | solution.py:253
  349.7 115.5 %collective-permute-start.29 = (bf16[256,1536]{1,0:T(8,128)(2,1)S(1)}, bf16[256,1536]{1,0:T(8,128)(2,1)S(1)}, u32[]{:S(2)}, u32[]{:S(2)}) collective-permute-start(bf16[256,1536]{1,0:T(8,128)(2,1)S(1)} %slice.381), channel_id=1, source_target_pairs={{0,4},{4,0},{8,12},{12,8},{1,5},{5,1},{9,13},{13,9},{2,6},{6,2},{1... | collective-permute-start | bytes 2359304 | tf_op jit(solution)/shard_map/ppermute | solution.py:253
  352.1 113.9 %collective-permute-start.24 = (bf16[256,1536]{1,0:T(8,128)(2,1)S(1)}, bf16[256,1536]{1,0:T(8,128)(2,1)S(1)}, u32[]{:S(2)}, u32[]{:S(2)}) collective-permute-start(bf16[256,1536]{1,0:T(8,128)(2,1)S(1)} %slice.382), channel_id=1, source_target_pairs={{0,4},{4,0},{8,12},{12,8},{1,5},{5,1},{9,13},{13,9},{2,6},{6,2},{1... | collective-permute-start | bytes 2359304 | tf_op jit(solution)/shard_map/ppermute | solution.py:253
  391.0 122.1 %collective-permute-start.54 = (bf16[768,1152]{1,0:T(8,128)(2,1)}, bf16[768,1152]{1,0:T(8,128)(2,1)}, u32[]{:S(2)}, u32[]{:S(2)}) collective-permute-start(bf16[768,1152]{1,0:T(8,128)(2,1)} %fusion.7), channel_id=1, source_target_pairs={{0,4},{4,0},{8,12},{12,8},{1,5},{5,1},{9,13},{13,9},{2,6},{6,2},{1... | collective-permute-start | bytes 5308424 | tf_op jit(solution)/shard_map/ppermute | solution.py:253
  464.8 41.9 %collective-permute-start.52 = (bf16[768,1152]{1,0:T(8,128)(2,1)}, bf16[768,1152]{1,0:T(8,128)(2,1)}, u32[]{:S(2)}, u32[]{:S(2)}) collective-permute-start(bf16[768,1152]{1,0:T(8,128)(2,1)} %fusion.6), channel_id=1, source_target_pairs={{0,4},{4,0},{8,12},{12,8},{1,5},{5,1},{9,13},{13,9},{2,6},{6,2},{1... | collective-permute-start | bytes 5308424 | tf_op jit(solution)/shard_map/ppermute | solution.py:253
  491.2 51.5 %collective-permute-start.56 = (bf16[1152,768]{1,0:T(8,128)(2,1)S(1)}, bf16[1152,768]{1,0:T(8,128)(2,1)}, u32[]{:S(2)}, u32[]{:S(2)}) collective-permute-start(bf16[1152,768]{1,0:T(8,128)(2,1)S(1)} %fusion.8), channel_id=1, source_target_pairs={{0,4},{4,0},{8,12},{12,8},{1,5},{5,1},{9,13},{13,9},{2,6},{6,2},{1... | collective-permute-start | bytes 5308424 | tf_op jit(solution)/shard_map/ppermute | solution.py:253
  498.1 74.5 %collective-permute-start.27 = (bf16[256,1536]{1,0:T(8,128)(2,1)}, bf16[256,1536]{1,0:T(8,128)(2,1)}, u32[]{:S(2)}, u32[]{:S(2)}) collective-permute-start(bf16[256,1536]{1,0:T(8,128)(2,1)} %pad_maximum_fusion.23), channel_id=1, source_target_pairs={{0,1},{1,0},{2,3},{3,2},{4,5},{5,4},{6,7},{7,6},{8,9},{9,8},{10,11... | collective-permute-start | bytes 2359304 | tf_op jit(solution)/shard_map/ppermute | solution.py:253
  503.5 43.9 %collective-permute-start.32 = (bf16[256,1536]{1,0:T(8,128)(2,1)}, bf16[256,1536]{1,0:T(8,128)(2,1)}, u32[]{:S(2)}, u32[]{:S(2)}) collective-permute-start(bf16[256,1536]{1,0:T(8,128)(2,1)} %pad_maximum_fusion.24), channel_id=1, source_target_pairs={{0,1},{1,0},{2,3},{3,2},{4,5},{5,4},{6,7},{7,6},{8,9},{9,8},{10,11... | collective-permute-start | bytes 2359304 | tf_op jit(solution)/shard_map/ppermute | solution.py:253
  587.3 35.0 %collective-permute-start.49 = (bf16[384,768]{1,0:T(8,128)(2,1)}, bf16[384,768]{1,0:T(8,128)(2,1)}, u32[]{:S(2)}, u32[]{:S(2)}) collective-permute-start(bf16[384,768]{1,0:T(8,128)(2,1)} %fusion.21), channel_id=1, source_target_pairs={{0,4},{4,0},{8,12},{12,8},{1,5},{5,1},{9,13},{13,9},{2,6},{6,2},{1... | collective-permute-start | bytes 1769480 | tf_op jit(solution)/shard_map/ppermute | solution.py:253
  599.5 46.3 %collective-permute-start.41 = (bf16[768,384]{1,0:T(8,128)(2,1)}, bf16[768,384]{1,0:T(8,128)(2,1)}, u32[]{:S(2)}, u32[]{:S(2)}) collective-permute-start(bf16[768,384]{1,0:T(8,128)(2,1)} %fusion.20), channel_id=1, source_target_pairs={{0,4},{4,0},{8,12},{12,8},{1,5},{5,1},{9,13},{13,9},{2,6},{6,2},{1... | collective-permute-start | bytes 1769480 | tf_op jit(solution)/shard_map/ppermute | solution.py:253
  618.7 33.5 %collective-permute-start.36 = (bf16[256,1536]{1,0:T(8,128)(2,1)S(1)}, bf16[256,1536]{1,0:T(8,128)(2,1)S(1)}, u32[]{:S(2)}, u32[]{:S(2)}) collective-permute-start(bf16[256,1536]{1,0:T(8,128)(2,1)S(1)} %slice.380), channel_id=1, source_target_pairs={{0,1},{1,0},{2,3},{3,2},{4,5},{5,4},{6,7},{7,6},{8,9},{9,8},{10,11... | collective-permute-start | bytes 2359304 | tf_op jit(solution)/shard_map/ppermute | solution.py:253
  623.7 46.8 %collective-permute-start.50 = (bf16[384,768]{1,0:T(8,128)(2,1)S(1)}, bf16[384,768]{1,0:T(8,128)(2,1)S(1)}, u32[]{:S(2)}, u32[]{:S(2)}) collective-permute-start(bf16[384,768]{1,0:T(8,128)(2,1)S(1)} %add_convert_fusion), channel_id=1, source_target_pairs={{0,8},{4,12},{8,0},{12,4},{1,9},{5,13},{9,1},{13,5},{2,10},{6,14},... | collective-permute-start | bytes 1769480 | tf_op jit(solution)/shard_map/ppermute | solution.py:253
  647.2 35.8 %collective-permute-start.42 = (bf16[768,384]{1,0:T(8,128)(2,1)S(1)}, bf16[768,384]{1,0:T(8,128)(2,1)S(1)}, u32[]{:S(2)}, u32[]{:S(2)}) collective-permute-start(bf16[768,384]{1,0:T(8,128)(2,1)S(1)} %add_convert_fusion.1), channel_id=1, source_target_pairs={{0,8},{4,12},{8,0},{12,4},{1,9},{5,13},{9,1},{13,5},{2,10},{6,14},... | collective-permute-start | bytes 1769480 | tf_op jit(solution)/shard_map/ppermute | solution.py:253
  652.1 33.4 %collective-permute-start.47 = (bf16[1536,128]{0,1:T(8,128)(2,1)S(1)}, bf16[1536,128]{0,1:T(8,128)(2,1)S(1)}, u32[]{:S(2)}, u32[]{:S(2)}) collective-permute-start(bf16[1536,128]{0,1:T(8,128)(2,1)S(1)} %pad_maximum_fusion.31), channel_id=1, source_target_pairs={{0,1},{1,0},{2,3},{3,2},{4,5},{5,4},{6,7},{7,6},{8,9},{9,8},{10,11... | collective-permute-start | bytes 1179656 | tf_op jit(solution)/shard_map/ppermute | solution.py:253
  652.5 31.7 %collective-permute-start.37 = (bf16[128,1536]{1,0:T(8,128)(2,1)S(1)}, bf16[128,1536]{1,0:T(8,128)(2,1)S(1)}, u32[]{:S(2)}, u32[]{:S(2)}) collective-permute-start(bf16[128,1536]{1,0:T(8,128)(2,1)S(1)} %slice.384), channel_id=1, source_target_pairs={{0,2},{1,3},{2,0},{3,1},{4,6},{5,7},{6,4},{7,5},{8,10},{9,11},{10,... | collective-permute-start | bytes 1179656 | tf_op jit(solution)/shard_map/ppermute | solution.py:253
  684.9 42.8 %collective-permute-start.38 = (bf16[128,1536]{1,0:T(8,128)(2,1)S(1)}, bf16[128,1536]{1,0:T(8,128)(2,1)S(1)}, u32[]{:S(2)}, u32[]{:S(2)}) collective-permute-start(bf16[128,1536]{1,0:T(8,128)(2,1)S(1)} %fusion.26), channel_id=1, source_target_pairs={{0,2},{1,3},{2,0},{3,1},{4,6},{5,7},{6,4},{7,5},{8,10},{9,11},{10,... | collective-permute-start | bytes 1179656 | tf_op jit(solution)/shard_map/ppermute | solution.py:253
  (101 other events, 1484.1 us)

commit v2 on v1

--- a/solution.py
+++ b/solution.py
@@ -189,11 +189,73 @@
     )(key_blocks, queries, grad_out, lse, cosine, sine, keys, values)
 
 
-def ffn_kernel(with_dx, base_ref, x_ref, dy_ref, wg_ref, wu_ref, wd_ref, *refs):
-    hid_ref, dg_ref, du_ref = refs[-4:-1] if with_dx else refs[-3:]
-    gate = dot(x_ref[...], wg_ref[...])
-    up = dot(x_ref[...], wu_ref[...])
-    grad_hidden = dot_cols(dy_ref[...], wd_ref[...])
+def qkv_kernel(pieces, meta_ref, x_ref, gain_ref, bias_ref, cos_ref, sin_ref, *refs):
+    weights, (xn_ref, factor_ref, q_ref, kv_ref) = refs[:pieces], refs[pieces:]
+    values = x_ref[...].astype(f32)
+    factor = lax.rsqrt(jnp.mean(values * values, axis=-1, keepdims=True) + EPSILON)
+    factor_ref[...] = factor
+    xn_ref[...] = (values * factor * gain_ref[...]).astype(bf16)
+    total = bias_ref[...]
+    for j, weight in enumerate(weights):
+        depth = weight.shape[0]
+        total = total + dot(xn_ref[:, columns_of(meta_ref, j, depth, pieces)], weight[...])
+    cosine, sine = cos_ref[...], sin_ref[...]
+    sign = jnp.where(lax.broadcasted_iota(jnp.int32, cosine.shape, 1) < HD // 2, -1.0, 1.0)
+    heads = q_ref.shape[1] // HD
+    for h in range(heads + 1):
+        own = total[:, h * HD : (h + 1) * HD]
+        turned = own * cosine + pltpu.roll(own, HD // 2, 1) * sign * sine
+        if h < heads:
+            q_ref[:, h * HD : (h + 1) * HD] = turned.astype(bf16)
+        else:
+            kv_ref[...] = jnp.where(meta_ref[2] == 0, turned, own).astype(bf16)
+
+
+def columns_of(meta_ref, j, depth, pieces):
+    if pieces == 1:
+        return slice(None)
+    return pl.ds(pl.multiple_of(meta_ref[j] * depth, LANES), depth)
+
+
+def qkv(meta, inputs, gain, bias, cosine, sine, weights):
+    rows, width = inputs.shape
+    out = weights[0].shape[1]
+    tile = 256
+    row = lambda n: pl.BlockSpec((tile, n), lambda i, m: (i, 0))
+    fixed = lambda w: pl.BlockSpec(w.shape, lambda i, m: (0, 0))
+    return pl.pallas_call(
+        functools.partial(qkv_kernel, len(weights)),
+        name="qkv",
+        grid_spec=pltpu.PrefetchScalarGridSpec(
+            num_scalar_prefetch=1,
+            grid=(rows // tile,),
+            in_specs=[row(width), fixed(gain), fixed(bias), row(HD), row(HD)]
+            + [fixed(w) for w in weights],
+            out_specs=[row(width), row(1), row(out - HD), row(HD)],
+        ),
+        out_shape=[
+            jax.ShapeDtypeStruct((rows, width), bf16),
+            jax.ShapeDtypeStruct((rows, 1), f32),
+            jax.ShapeDtypeStruct((rows, out - HD), bf16),
+            jax.ShapeDtypeStruct((rows, HD), bf16),
+        ],
+        compiler_params=pltpu.CompilerParams(vmem_limit_bytes=VMEM_LIMIT),
+        cost_estimate=pl.CostEstimate(
+            flops=2 * rows * width * out,
+            bytes_accessed=4 * rows * width + 2 * width * out,
+            transcendentals=0,
+        ),
+    )(meta, inputs, gain, bias, cosine, sine, *weights)
+
+
+def ffn_kernel(with_dx, pieces, meta_ref, x_ref, dy_ref, *refs):
+    wg, wu, wd = (refs[m * pieces : (m + 1) * pieces] for m in range(3))
+    outs = refs[-4:] if with_dx else refs[-3:]
+    hid_ref, dg_ref, du_ref = outs[:3]
+    columns = [columns_of(meta_ref, j, wg[j].shape[1], pieces) for j in range(pieces)]
+    gate = sum(dot_cols(x_ref[:, at], w[...]) for at, w in zip(columns, wg))
+    up = sum(dot_cols(x_ref[:, at], w[...]) for at, w in zip(columns, wu))
+    grad_hidden = sum(dot_cols(dy_ref[:, at], w[...]) for at, w in zip(columns, wd))
     sigma = 1.0 / (1.0 + jnp.exp(-gate))
     gated = gate * sigma
     hid_ref[...] = (gated * up).astype(bf16)
@@ -202,49 +264,92 @@
     dg_ref[...] = grad_gate
     du_ref[...] = grad_up
     if with_dx:
-        refs[-1][...] = (dot_cols(grad_gate, wg_ref[...]) + dot_cols(grad_up, wu_ref[...])).astype(
-            bf16
-        )
-
-
-def ffn(base, normed, grad_out, wg, wu, wd, filled=None):
+        for at, g, u in zip(columns, wg, wu):
+            outs[3][:, at] = (dot(grad_gate, g[...]) + dot(grad_up, u[...])).astype(bf16)
+
+
+def ffn(meta, normed, grad_out, wg, wu, wd, with_dx):
     rows, width = normed.shape
-    units = wg.shape[1]
+    units = wg[0].shape[0]
     tile = 512
-    steps = rows // tile
-    with_dx = filled is None
-    row = lambda n: pl.BlockSpec((tile, n), lambda i, b: (i, 0))
-    weight = lambda w: pl.BlockSpec(
-        w.shape, lambda i, b: (0, 0), pipeline_mode=pl.Buffered(1)
-    )
-    out_row = pl.BlockSpec((tile, units), lambda i, b: (i + b[0] * steps, 0))
-    out_specs = [out_row] * 3
-    out_shape = [jax.ShapeDtypeStruct((2 * rows, units), bf16)] * 3
-    in_specs = [row(width), row(width), weight(wg), weight(wu), weight(wd)]
-    args = [base, normed, grad_out, wg, wu, wd]
-    aliases = {}
-    if with_dx:
-        out_specs = out_specs + [row(width)]
-        out_shape = out_shape + [jax.ShapeDtypeStruct((rows, width), bf16)]
-    else:
-        in_specs = in_specs + [pl.BlockSpec(memory_space=pl.ANY)] * 3
-        args = args + list(filled)
-        aliases = {6: 0, 7: 1, 8: 2}
+    row = lambda n: pl.BlockSpec((tile, n), lambda i, m: (i, 0))
+    weight = lambda w: pl.BlockSpec(w.shape, lambda i, m: (0, 0), pipeline_mode=pl.Buffered(1))
+    weights = list(wg) + list(wu) + list(wd)
+    widths = [units] * 3 + [width] * with_dx
     return pl.pallas_call(
-        functools.partial(ffn_kernel, with_dx),
+        functools.partial(ffn_kernel, with_dx, len(wg)),
         name="ffn_pair" if with_dx else "ffn_far",
         grid_spec=pltpu.PrefetchScalarGridSpec(
-            num_scalar_prefetch=1, grid=(steps,), in_specs=in_specs, out_specs=out_specs
-        ),
-        out_shape=out_shape,
-        input_output_aliases=aliases,
+            num_scalar_prefetch=1,
+            grid=(rows // tile,),
+            in_specs=[row(width), row(width)] + [weight(w) for w in weights],
+            out_specs=[row(n) for n in widths],
+        ),
+        out_shape=[jax.ShapeDtypeStruct((rows, n), bf16) for n in widths],
         compiler_params=pltpu.CompilerParams(vmem_limit_bytes=VMEM_LIMIT),
         cost_estimate=pl.CostEstimate(
             flops=2 * rows * width * units * (5 if with_dx else 3),
             bytes_accessed=2 * (3 * width * units + 3 * rows * units + 3 * rows * width),
             transcendentals=rows * units,
         ),
-    )(*args)
+    )(meta, normed, grad_out, *weights)
+
+
+def unit_grads_kernel(meta_ref, xp, xf, yp, yf, hp, hf, gp, gf, up, uf, og, ou, od, ag, au, ad):
+    step = pl.program_id(0)
+
+    @pl.when(step == 0)
+    def _():
+        for acc in (ag, au, ad):
+            acc[...] = jnp.zeros_like(acc)
+
+    for use, x, y, h, g, u in ((True, xp, yp, hp, gp, up), (False, xf, yf, hf, gf, uf)):
+
+        @pl.when((step // (pl.num_programs(0) // 2) == meta_ref[3]) == use)
+        def _():
+            ag[...] += dot_rows(g[...], x[...])
+            au[...] += dot_rows(u[...], x[...])
+            ad[...] += dot_rows(h[...], y[...])
+
+    @pl.when(step == pl.num_programs(0) - 1)
+    def _():
+        og[...] = ag[...].astype(bf16)
+        ou[...] = au[...].astype(bf16)
+        od[...] = ad[...].astype(bf16)
+
+
+def unit_grads(meta, which, pieces, x, y, hid, dg, du):
+    rows, width = x[0].shape
+    units = dg[0].shape[1]
+    depth = width // pieces
+    tile = 512
+    steps = rows // tile
+    shard = (lambda m: m[which]) if pieces > 1 else (lambda m: 0)
+    near = lambda i, m: jnp.clip(i - steps * m[3], 0, steps - 1)
+    far = lambda i, m: jnp.clip(i - steps * (1 - m[3]), 0, steps - 1)
+    feature = lambda at: pl.BlockSpec((tile, depth), lambda i, m: (at(i, m), shard(m)))
+    unit = lambda at: pl.BlockSpec((tile, units), lambda i, m: (at(i, m), 0))
+    return pl.pallas_call(
+        unit_grads_kernel,
+        name=f"unit_grads_{which}",
+        grid_spec=pltpu.PrefetchScalarGridSpec(
+            num_scalar_prefetch=1,
+            grid=(2 * steps,),
+            in_specs=[feature(near), feature(far)] * 2 + [unit(near), unit(far)] * 3,
+            out_specs=[
+                pl.BlockSpec((units, depth), lambda i, m: (0, 0), pipeline_mode=pl.Buffered(1))
+            ]
+            * 3,
+            scratch_shapes=[pltpu.VMEM((units, depth), f32)] * 3,
+        ),
+        out_shape=[jax.ShapeDtypeStruct((units, depth), bf16)] * 3,
+        compiler_params=pltpu.CompilerParams(vmem_limit_bytes=VMEM_LIMIT),
+        cost_estimate=pl.CostEstimate(
+            flops=12 * rows * depth * units,
+            bytes_accessed=2 * (6 * rows * units + 4 * rows * depth + 3 * units * depth),
+            transcendentals=0,
+        ),
+    )(meta, *x, *y, *hid, *dg, *du)
 
 
 def build(n_f, n_c, n_t):
@@ -285,12 +390,16 @@
         group = (t * heads) // (H // KV)
         part = rows // n_t
         units_all = w_gate.shape[1]
-        units = -(-units_all // (2 * LANES)) * LANES
+        units = units_all // 2
 
         def gather_f(x, axis):
             if n_f == 2:
                 return by_bit(f, x, flip(x, "fsdp", 1), axis)
             return lax.all_gather(x, "fsdp", axis=axis, tiled=True)
+
+        def columns_f(parts):
+            parts = [x.astype(bf16) for x in parts]
+            return by_bit(f, parts[0], parts[1], 1) if n_f == 2 else parts[0]
 
         def grad_f(left, right, side):
             if n_f == 2:
@@ -352,7 +461,13 @@
         )
         column = lambda w: lax.dynamic_slice_in_dim(w, group * HD, HD, 1)
         w_kv_own = jnp.where(core == 0, column(w_key), column(w_value))
-        w_qkv = gather_f(jnp.concatenate([w_query, w_kv_own], axis=1), 0)
+        pieces_f = lambda x, axis: (
+            [x, flip(x, "fsdp", 1)]
+            if n_f == 2
+            else [lax.all_gather(x, "fsdp", axis=axis, tiled=True)]
+        )
+        meta = jnp.stack([f, 1 - f, core, pair]).astype(jnp.int32)
+        w_qkv = pieces_f(jnp.concatenate([w_query, w_kv_own], axis=1), 0)
         small = gather_f(small, 0)
         w_out_all = gather_f(w_out, 1)
         piece = attn_gain.shape[0]
@@ -371,16 +486,10 @@
         bv = bias_of(at + (heads + KV) * (HD // n_f), KV)
         b_kv = lax.dynamic_index_in_dim(jnp.where(core == 0, bk, bv), group, 0)
 
-        def unit_slice(w, axis):
-            low = lax.slice_in_dim(w, 0, units, axis=axis)
-            high = lax.slice_in_dim(w, units, units_all, axis=axis)
-            pad = [(0, 0), (0, 0)]
-            pad[axis] = (0, 2 * units - units_all)
-            return jnp.where(parity == 0, low, jnp.pad(high, pad))
-
-        wg = gather_f(unit_slice(w_gate, 1), 0)
-        wu = gather_f(unit_slice(w_up, 1), 0)
-        wd = gather_f(unit_slice(w_down, 0), 1)
+        unit_slice = lambda w: lax.dynamic_slice_in_dim(w, parity * units, units, 0)
+        wg = pieces_f(unit_slice(w_gate.T), 1)
+        wu = pieces_f(unit_slice(w_up.T), 1)
+        wd = pieces_f(unit_slice(w_down), 1)
 
         dy_own = mixed(cotangent)[: 2 * part]
         dy_near = jnp.concatenate([dy_own, flip(dy_own, "context", 1)], axis=0)
@@ -396,18 +505,10 @@
             key_blocks[:own_blocks, None] * BLOCK + jnp.arange(BLOCK, dtype=jnp.int32)[None, :]
         ).reshape(-1)
         cosine, sine = rope_tables(positions)
-        inputs_f = inputs.astype(f32)
-        factor_first = rms_scale(inputs_f)
-        normed = (inputs_f * factor_first * gain_first).astype(bf16)
-        qkv_pre = dot(normed, w_qkv)
-        query_pre = qkv_pre[:, : heads * HD].reshape(rows, heads, HD) + bq
-        queries = (
-            rotate(query_pre, cosine[:, None, :], sine[:, None, :])
-            .astype(bf16)
-            .reshape(rows, heads * HD)
-        )
-        kv_pre = qkv_pre[:, heads * HD :] + b_kv
-        kv_own = jnp.where(core == 0, rotate(kv_pre, cosine, sine), kv_pre).astype(bf16)
+        bias = jnp.concatenate([bq.reshape(1, -1), b_kv], axis=1)
+        normed, factor_first, queries, kv_own = qkv(
+            meta, inputs, gain_first, bias, cosine, sine, w_qkv
+        )
         kv_whole = grow(grow(kv_own, "context", 1), "context", 2)
         kv_other = flip(kv_whole, "tensor", 1)
         keys = jnp.where(core == 0, kv_whole, kv_other)
@@ -422,28 +523,33 @@
         normed2 = (middle * factor_second * gain_second).astype(bf16)
         normed2_pair = gather_pair(normed2)
         normed2_far = gather_pair(flip(normed2, "context", 2))
-        base = pair.reshape(1)
-        *half_filled, dx_part = ffn(base, normed2_pair, dy_pair, wg, wu, wd)
+        hid_pair, dg_pair, du_pair, dx_part = ffn(meta, normed2_pair, dy_pair, wg, wu, wd, True)
         grad_normed2 = scatter_pair(dx_part)
-        hidden, grad_gate, grad_up = ffn(
-            1 - base, normed2_far, dy_far, wg, wu, wd, filled=half_filled
-        )
-        hidden_pair = lax.dynamic_slice_in_dim(hidden, pair * 2 * rows, 2 * rows, 0)
-        final = middle + scatter_pair(dot(hidden_pair, wd))
+        hid_far, dg_far, du_far = ffn(meta, normed2_far, dy_far, wg, wu, wd, False)
+        final = middle + scatter_pair(columns_f([dot(hid_pair, w) for w in wd]))
         outputs = natural(gather_t(final.astype(bf16)))
 
-        normed2_all = by_bit(pair, normed2_pair, normed2_far, 0)
-        dy_all = by_bit(pair, dy_pair, dy_far, 0)
-
-        def unit_grad(left, right, side):
-            own = grad_f(left, right, side).astype(bf16)
-            other = flip(own, "context", 1)
-            whole = by_bit(parity, own, other, 1 - side)
-            return lax.slice_in_dim(whole, 0, units_all, axis=1 - side).astype(f32)
-
-        wd_grad = unit_grad(hidden, dy_all, 1)
-        wg_grad = unit_grad(normed2_all, grad_gate, 0)
-        wu_grad = unit_grad(normed2_all, grad_up, 0)
+        grad_args = (
+            (normed2_pair, normed2_far),
+            (dy_pair, dy_far),
+            (hid_pair, hid_far),
+            (dg_pair, dg_far),
+            (du_pair, du_far),
+        )
+        if n_f == 2:
+            unit_sent = unit_grads(meta, 1, 2, *grad_args)
+            unit_got = [flip(x, "fsdp", 1) for x in unit_sent]
+            unit_own = unit_grads(meta, 0, 2, *grad_args)
+        else:
+            unit_own = [
+                lax.psum_scatter(x, "fsdp", scatter_dimension=1, tiled=True)
+                for x in unit_grads(meta, 0, 1, *grad_args)
+            ]
+            unit_got = [jnp.zeros_like(x) for x in unit_own]
+
+        def unit_done(own, got):
+            low = (own.astype(f32) + got.astype(f32)).astype(bf16)
+            return by_bit(parity, low, flip(low, "context", 1), 0).astype(f32)
 
         grad_mid_norm, ffn_gain_grad = norm_back(middle, factor_second, gain_second, grad_normed2)
         dy_part = lax.dynamic_slice_in_dim(cotangent, t * part, part, 0).astype(f32)
@@ -455,6 +561,9 @@
         dq_low, dk, dv = attention_back(
             key_blocks, queries, grad_attended, lse, cosine, sine, keys, values
         )
+        unit_own, unit_got, dq_low = lax.optimization_barrier((unit_own, unit_got, dq_low))
+        wg_grad, wu_grad, wd_grad = (unit_done(a, b) for a, b in zip(unit_own, unit_got))
+        wg_grad, wu_grad = wg_grad.T, wu_grad.T
         dkv_keep = jnp.where(core == 0, dk, dv)
         dkv_send = jnp.where(core == 0, dv, dk).astype(bf16)
         dkv = dkv_keep + flip(dkv_send, "tensor", 1).astype(f32)
@@ -474,7 +583,7 @@
         wv_grad = jnp.concatenate(wkv_rank[1::2], axis=1)
 
         d_qkv = mixed(jnp.concatenate([dq_low, dkv_low], axis=1))
-        grad_normed = scatter_t(dot_cols(d_qkv, w_qkv))
+        grad_normed = scatter_t(columns_f([dot_cols(d_qkv, w) for w in w_qkv]))
         inputs_part = lax.dynamic_slice_in_dim(inputs, t * part, part, 0).astype(f32)
         factor_part = lax.dynamic_slice_in_dim(factor_first, t * part, part, 0)
         grad_in_norm, attn_gain_grad = norm_back(inputs_part, factor_part, gain_first, grad_normed)

time: 746 us -> 752 us (level)
  waiting for transfers between devices: 301 us -> 379 us
  local copies, waits for them, and re-layouts: 101 us -> 37.2 us
  Pallas kernels: 76.7 us -> 121 us
  matrix products: 63.4 us -> 22.6 us
  other arithmetic: 108 us -> 78.7 us
  starting transfers between devices: 40.9 us -> 63.1 us
    ppermute x57, waiting for transfers between devices: 301 us -> 379 us  [flip(): return lax.ppermute(x, axis, [(i, i ^ bit) for i in range(size)])]
    unnamed x181 -> x131, local copies, waits for them, and re-layouts: 59.9 us -> 14.6 us
    pallas_call x2 -> x5, Pallas kernels: 51 us -> 95.1 us  [the longest x2 48.2 us: ffn(): pl.pallas_call(functools.partial(ffn_kernel, with_dx, len(wg)), name='ffn...]
    dot_general x12 -> x6, matrix products: 46.2 us -> 6.11 us  [dot_rows(): lax.dot_general(left, right, (((0,), (0,)), ((), ())), preferred_element_...]
    select_n x6 -> x3, other arithmetic: 28 us -> 1.41 us  [by_bit(): jnp.where(bit == 0, jnp.concatenate([x, other], axis=axis), jnp.concatena...]
    ppermute x57, starting transfers between devices: 40.9 us -> 63.1 us  [flip(): return lax.ppermute(x, axis, [(i, i ^ bit) for i in range(size)])]
    slice x7 -> x0, local copies, waits for them, and re-layouts: 14.3 us -> none  [the longest x3 6.94 us: unit_slice(): high = lax.slice_in_dim(w, units, units_all, axis=axis)]
    convert_element_type x7 -> x6, other arithmetic: 21.1 us -> 12.4 us  [the longest x3 6.15 us: unit_done(): low = (own.astype(f32) + got.astype(f32)).astype(bf16)]
  transfers between devices with their start and end apart: 57 -> 57, of which waited for: 25 -> 27; matrix products, arithmetic and copies ran while one was open for 35% -> 16% of each run, Pallas kernels for 10% -> 15%
where the time goes in v2:
time: 752 us; the launch traced here: 744 us
  waiting for transfers between devices  379 us (50%)
  Pallas kernels  121 us (16%)
  other arithmetic  78.7 us (10%)
  starting transfers between devices  63.1 us (8%)
  blocking collectives  40.9 us (5%)
  local copies, waits for them, and re-layouts  37.2 us (5%)
  matrix products  22.6 us (3%)
    ppermute x57, waiting for transfers between devices, flip(): return lax.ppermute(x, axis, [(i, i ^ bit) for i in range(size)])  379 us
    ppermute x57, starting transfers between devices, flip(): return lax.ppermute(x, axis, [(i, i ^ bit) for i in range(size)])  63.1 us
    pallas_call x2, Pallas kernels, ffn(): pl.pallas_call(functools.partial(ffn_kernel, with_dx, len(wg)), name='ffn...  48.2 us
    pallas_call x2, Pallas kernels, unit_grads(): pl.pallas_call(unit_grads_kernel, name=f'unit_grads_{which}', grid_spec=p...  41.3 us
    psum x1, blocking collectives, local(): lax.psum(jnp.concatenate([attn_gain_grad, ffn_gain_grad, slots.reshape(-1...  40.9 us
    concatenate x13, other arithmetic, grow(): return jnp.concatenate([x, flip(x, axis, bit)], axis=0)  19.3 us
    pallas_call x1, Pallas kernels, attention_back(): pl.pallas_call(functools.partial(attention_back_kernel, keys.shape[0] //...  15.4 us
  transfers between devices with their start and end apart: 57, of which 27 were waited for; matrix products, arithmetic and copies ran while one was open for 16% of the time, Pallas kernels for 15%

profile of v2, /device:TPU:0, one launch (start us, length us, event | category | flops | bytes accessed | tf_op | source)
XLA Modules:
  0.0 743.9 jit_solution(2214061460612185827)
XLA Ops:
  17.9 12.9 %collective-permute-done.1.refs_1_ = bf16[768,512]{1,0:T(8,128)(2,1)} collective-permute-done((bf16[768,512]{1,0:T(8,128)(2,1)}, bf16[768,512]{1,0:T(8,128)(2,1)}, u32[]{:S(2)}, u32[]{:S(2)}) %collective-permute-start.1) | collective-permute-done | bytes 786464 | tf_op jit(solution)/shard_map/ppermute | solution.py:358
  30.8 5.6 qkv.1
  47.4 7.4 collective-permute-done.3
  60.0 10.2 %attention.1 = (bf16[512,384]{1,0:T(8,128)(2,1)}, f32[3,512,1]{2,1,0:T(8,128)}) custom-call(s32[8]{0:T(128)} %pad_add_fusion.kb_ref, bf16[512,384]{1,0:T(8,128)(2,1)} %get-tuple-element.43.q_ref, bf16[2048,128]{1,0:T(8,128)(2,1)} %get-tuple-element.97.k_ref, bf16[2048,128]{1,0:T(8,128)(2,1)} %get-tuple-element.96.v_ref), custom_call_target="tpu_custom_call" | custom-call | flops 1610612736 | bytes 1835008 | tf_op jit(solution)/shard_map/attention/pallas_call | solution.py:96
  81.8 7.5 %collective-permute-done.7 = bf16[128,1536]{1,0:T(8,128)(2,1)} collective-permute-done((bf16[128,1536]{1,0:T(8,128)(2,1)}, bf16[128,1536]{1,0:T(8,128)(2,1)}, u32[]{:S(2)}, u32[]{:S(2)}) %collective-permute-start.7) | collective-permute-done | bytes 393248 | tf_op jit(solution)/shard_map/ppermute | solution.py:358
  94.2 9.0 %collective-permute-done.8 = bf16[128,1536]{1,0:T(8,128)(2,1)S(1)} collective-permute-done((bf16[128,1536]{1,0:T(8,128)(2,1)}, bf16[128,1536]{1,0:T(8,128)(2,1)S(1)}, u32[]{:S(2)}, u32[]{:S(2)}) %collective-permute-start.8) | collective-permute-done | bytes 393248 | tf_op jit(solution)/shard_map/ppermute | solution.py:358
  114.3 18.5 %collective-permute-done.28 = bf16[256,1536]{1,0:T(8,128)(2,1)} collective-permute-done((bf16[256,1536]{1,0:T(8,128)(2,1)}, bf16[256,1536]{1,0:T(8,128)(2,1)}, u32[]{:S(2)}, u32[]{:S(2)}) %collective-permute-start.28) | collective-permute-done | bytes 786464 | tf_op jit(solution)/shard_map/ppermute | solution.py:358
  134.6 13.1 %collective-permute-done.24 = bf16[128,1536]{1,0:T(8,128)(2,1)S(1)} collective-permute-done((bf16[128,1536]{1,0:T(8,128)(2,1)}, bf16[128,1536]{1,0:T(8,128)(2,1)S(1)}, u32[]{:S(2)}, u32[]{:S(2)}) %collective-permute-start.24) | collective-permute-done | bytes 393248 | tf_op jit(solution)/shard_map/ppermute | solution.py:358
  152.1 8.6 %collective-permute-done.29 = bf16[256,1536]{1,0:T(8,128)(2,1)S(1)} collective-permute-done((bf16[256,1536]{1,0:T(8,128)(2,1)}, bf16[256,1536]{1,0:T(8,128)(2,1)S(1)}, u32[]{:S(2)}, u32[]{:S(2)}) %collective-permute-start.29) | collective-permute-done | bytes 786464 | tf_op jit(solution)/shard_map/ppermute | solution.py:358
  169.2 11.1 %collective-permute-done.26 = bf16[256,1536]{1,0:T(8,128)(2,1)S(1)} collective-permute-done((bf16[256,1536]{1,0:T(8,128)(2,1)}, bf16[256,1536]{1,0:T(8,128)(2,1)S(1)}, u32[]{:S(2)}, u32[]{:S(2)}) %collective-permute-start.26) | collective-permute-done | bytes 786464 | tf_op jit(solution)/shard_map/ppermute | solution.py:358
  185.2 16.3 %collective-permute-done.14.refs_3_ = bf16[1120,768]{1,0:T(8,128)(2,1)} collective-permute-done((bf16[1120,768]{1,0:T(8,128)(2,1)}, bf16[1120,768]{1,0:T(8,128)(2,1)}, u32[]{:S(2)}, u32[]{:S(2)}) %collective-permute-start.14) | collective-permute-done | bytes 1720352 | tf_op jit(solution)/shard_map/ppermute | solution.py:358
  201.5 33.4 %collective-permute-done.15.refs_5_ = bf16[1120,768]{1,0:T(8,128)(2,1)} collective-permute-done((bf16[1120,768]{1,0:T(8,128)(2,1)}, bf16[1120,768]{1,0:T(8,128)(2,1)}, u32[]{:S(2)}, u32[]{:S(2)}) %collective-permute-start.15) | collective-permute-done | bytes 1720352 | tf_op jit(solution)/shard_map/ppermute | solution.py:358
  234.9 28.3 %ffn_pair.1 = (bf16[1024,1120]{1,0:T(8,128)(2,1)}, bf16[1024,1120]{1,0:T(8,128)(2,1)}, bf16[1024,1120]{1,0:T(8,128)(2,1)}, bf16[1024,1536]{1,0:T(8,128)(2,1)}) custom-call(s32[4]{0:T(128)} %pad_add_fusion.1.meta_ref, bf16[1024,1536]{1,0:T(8,128)(2,1)} %pad_maximum_fusion.x_ref.xp, bf16[1024,1536]{1,0:T(8,128)(2,1)} %pad_maximum_fusion.1.dy_ref.yp, ...), custom_call_target="tpu_custom_call" | custom-call | flops 17616076800 | bytes 26640384 | tf_op jit(solution)/shard_map/ffn_pair/pallas_call | solution.py:279
  290.2 19.9 %ffn_far.1 = (bf16[1024,1120]{1,0:T(8,128)(2,1)}, bf16[1024,1120]{1,0:T(8,128)(2,1)}, bf16[1024,1120]{1,0:T(8,128)(2,1)}) custom-call(s32[4]{0:T(128)} %pad_add_fusion.1.meta_ref, bf16[1024,1536]{1,0:T(8,128)(2,1)} %copy-done.52, bf16[1024,1536]{1,0:T(8,128)(2,1)} %copy-done.39, bf16[1120,768]{1,0:T(8,128)(2,1)} %dynamic-slice_bitcast_fusion.1.refs_0_, ...), custom_call_target="tpu_custom_call" | custom-call | flops 10569646080 | bytes 26640384 | tf_op jit(solution)/shard_map/ffn_far/pallas_call | solution.py:279
  310.1 10.2 %collective-permute-done.22 = bf16[256,1536]{1,0:T(8,128)(2,1)} collective-permute-done((bf16[256,1536]{1,0:T(8,128)(2,1)}, bf16[256,1536]{1,0:T(8,128)(2,1)}, u32[]{:S(2)}, u32[]{:S(2)}) %collective-permute-start.22) | collective-permute-done | bytes 786464 | tf_op jit(solution)/shard_map/ppermute | solution.py:358
  325.7 8.6 %collective-permute-done.23 = bf16[128,1536]{1,0:T(8,128)(2,1)S(1)} collective-permute-done((bf16[128,1536]{1,0:T(8,128)(2,1)S(1)}, bf16[128,1536]{1,0:T(8,128)(2,1)S(1)}, u32[]{:S(2)}, u32[]{:S(2)}) %collective-permute-start.23) | collective-permute-done | bytes 393248 | tf_op jit(solution)/shard_map/ppermute | solution.py:358
  334.6 6.3 collective-permute-done.18
  343.7 20.8 %unit_grads_1.1 = (bf16[1120,768]{1,0:T(8,128)(2,1)}, bf16[1120,768]{1,0:T(8,128)(2,1)}, bf16[1120,768]{1,0:T(8,128)(2,1)}) custom-call(s32[4]{0:T(128)} %pad_add_fusion.1.meta_ref, bf16[1024,1536]{1,0:T(8,128)(2,1)} %pad_maximum_fusion.x_ref.xp, bf16[1024,1536]{1,0:T(8,128)(2,1)} %copy-done.52, bf16[1024,1536]{1,0:T(8,128)(2,1)} %pad_maximum_fusion.1.dy_ref.yp, ...), custom_call_target="tpu_custom_call" | custom-call | flops 10569646080 | bytes 25214976 | tf_op jit(solution)/shard_map/unit_grads_1/pallas_call | solution.py:332
  368.8 20.5 %unit_grads_0.1 = (bf16[1120,768]{1,0:T(8,128)(2,1)}, bf16[1120,768]{1,0:T(8,128)(2,1)}, bf16[1120,768]{1,0:T(8,128)(2,1)}) custom-call(s32[4]{0:T(128)} %pad_add_fusion.1.meta_ref, bf16[1024,1536]{1,0:T(8,128)(2,1)} %pad_maximum_fusion.x_ref.xp, bf16[1024,1536]{1,0:T(8,128)(2,1)} %copy-done.52, bf16[1024,1536]{1,0:T(8,128)(2,1)} %pad_maximum_fusion.1.dy_ref.yp, ...), custom_call_target="tpu_custom_call" | custom-call | flops 10569646080 | bytes 25214976 | tf_op jit(solution)/shard_map/unit_grads_0/pallas_call | solution.py:332
  394.6 15.4 %attention_back.1 = (bf16[512,384]{1,0:T(8,128)(2,1)}, f32[2048,128]{1,0:T(8,128)}, f32[2048,128]{1,0:T(8,128)}) custom-call(s32[8]{0:T(128)} %pad_add_fusion.kb_ref, bf16[512,384]{1,0:T(8,128)(2,1)} %get-tuple-element.43.q_ref, bf16[512,384]{1,0:T(8,128)(2,1)} %pad_maximum_fusion.22.do_ref, f32[3,512,1]{2,1,0:T(8,128)} %get-tuple-element.60.lse_ref, ...), custom_call_target="tpu_custom_call" | custom-call | flops 4026531840 | bytes 4325376 | tf_op jit(solution)/shard_map/attention_back/pallas_call | solution.py:161
  410.0 32.1 %collective-permute-done.32 = bf16[1120,768]{1,0:T(8,128)(2,1)} collective-permute-done((bf16[1120,768]{1,0:T(8,128)(2,1)}, bf16[1120,768]{1,0:T(8,128)(2,1)}, u32[]{:S(2)}, u32[]{:S(2)}) %collective-permute-start.32) | collective-permute-done | bytes 1720352 | tf_op jit(solution)/shard_map/ppermute | solution.py:358
  442.1 33.8 %collective-permute-done.33 = bf16[1120,768]{1,0:T(8,128)(2,1)} collective-permute-done((bf16[1120,768]{1,0:T(8,128)(2,1)}, bf16[1120,768]{1,0:T(8,128)(2,1)}, u32[]{:S(2)}, u32[]{:S(2)}) %collective-permute-start.33) | collective-permute-done | bytes 1720352 | tf_op jit(solution)/shard_map/ppermute | solution.py:358
  493.2 5.9 collective-permute-start.37
  502.6 20.2 %collective-permute-done.37 = bf16[1024,128]{1,0:T(8,128)(2,1)S(1)} collective-permute-done((bf16[1024,128]{1,0:T(8,128)(2,1)S(1)}, bf16[1024,128]{1,0:T(8,128)(2,1)S(1)}, u32[]{:S(2)}, u32[]{:S(2)}) %collective-permute-start.37) | collective-permute-done | bytes 262176 | tf_op jit(solution)/shard_map/ppermute | solution.py:358
  522.9 7.5 %collective-permute-start.38 = (bf16[512,128]{1,0:T(8,128)(2,1)S(1)}, bf16[512,128]{1,0:T(8,128)(2,1)S(1)}, u32[]{:S(2)}, u32[]{:S(2)}) collective-permute-start(bf16[512,128]{1,0:T(8,128)(2,1)S(1)} %slice.314), channel_id=1, source_target_pairs={{0,4},{4,0},{8,12},{12,8},{1,5},{5,1},{9,13},{13,9},{2,6},{6,2},{1... | collective-permute-start | bytes 393224 | tf_op jit(solution)/shard_map/ppermute | solution.py:358
  531.9 45.0 %collective-permute-done.38 = bf16[512,128]{1,0:T(8,128)(2,1)S(1)} collective-permute-done((bf16[512,128]{1,0:T(8,128)(2,1)S(1)}, bf16[512,128]{1,0:T(8,128)(2,1)S(1)}, u32[]{:S(2)}, u32[]{:S(2)}) %collective-permute-start.38) | collective-permute-done | bytes 131104 | tf_op jit(solution)/shard_map/ppermute | solution.py:358
  594.6 6.1 collective-permute-start.48
  602.1 33.3 %collective-permute-done.48 = bf16[768,128]{0,1:T(8,128)(2,1)S(1)} collective-permute-done((bf16[768,128]{0,1:T(8,128)(2,1)S(1)}, bf16[768,128]{0,1:T(8,128)(2,1)S(1)}, u32[]{:S(2)}, u32[]{:S(2)}) %collective-permute-start.48) | collective-permute-done | bytes 196640 | tf_op jit(solution)/shard_map/ppermute | solution.py:358
  644.8 5.4 fusion
  658.9 21.5 %collective-permute-done.53 = bf16[384,768]{1,0:T(8,128)(2,1)S(1)} collective-permute-done((bf16[384,768]{1,0:T(8,128)(2,1)S(1)}, bf16[384,768]{1,0:T(8,128)(2,1)S(1)}, u32[]{:S(2)}, u32[]{:S(2)}) %collective-permute-start.53) | collective-permute-done | bytes 589856 | tf_op jit(solution)/shard_map/ppermute | solution.py:358
  681.6 10.9 %collective-permute-done.45 = bf16[768,384]{1,0:T(8,128)(2,1)S(1)} collective-permute-done((bf16[768,384]{1,0:T(8,128)(2,1)S(1)}, bf16[768,384]{1,0:T(8,128)(2,1)S(1)}, u32[]{:S(2)}, u32[]{:S(2)}) %collective-permute-start.45) | collective-permute-done | bytes 589856 | tf_op jit(solution)/shard_map/ppermute | solution.py:358
  696.0 40.9 %psum.7 = f32[5120]{0:T(1024)S(1)} all-reduce(f32[5120]{0:T(1024)S(1)} %pad_maximum_fusion.29), channel_id=1, replica_groups=mesh['fsdp'=2,'context'=4,'tensor'=4] {'fsdp','context','tensor'}, use_global_device_ids=true, to_apply=%region_7.8 | all-reduce | flops 5120 | bytes 40960 | tf_op jit(solution)/shard_map/psum | solution.py:598
  (370 shorter events, 195.4 us)
Async XLA Ops:
  94.2 38.7 %collective-permute-start.28 = (bf16[256,1536]{1,0:T(8,128)(2,1)}, bf16[256,1536]{1,0:T(8,128)(2,1)}, u32[]{:S(2)}, u32[]{:S(2)}) collective-permute-start(bf16[256,1536]{1,0:T(8,128)(2,1)} %pad_maximum_fusion.13), channel_id=1, source_target_pairs={{0,8},{4,12},{8,0},{12,4},{1,9},{5,13},{9,1},{13,5},{2,10},{6,14},... | collective-permute-start | bytes 2359304 | tf_op jit(solution)/shard_map/ppermute | solution.py:358
  105.9 42.3 %collective-permute-start.9 = (bf16[256,1536]{1,0:T(8,128)(2,1)}, bf16[256,1536]{1,0:T(8,128)(2,1)}, u32[]{:S(2)}, u32[]{:S(2)}) collective-permute-start(bf16[256,1536]{1,0:T(8,128)(2,1)} %pad_maximum_fusion.12), channel_id=1, source_target_pairs={{0,4},{4,0},{8,12},{12,8},{1,5},{5,1},{9,13},{13,9},{2,6},{6,2},{1... | collective-permute-start | bytes 2359304 | tf_op jit(solution)/shard_map/ppermute | solution.py:358
  109.0 54.7 %collective-permute-start.12 = (bf16[512,1536]{1,0:T(8,128)(2,1)}, bf16[512,1536]{1,0:T(8,128)(2,1)}, u32[]{:S(2)}, u32[]{:S(2)}) collective-permute-start(bf16[512,1536]{1,0:T(8,128)(2,1)} %pad_maximum_fusion.3), channel_id=1, source_target_pairs={{0,1},{1,0},{2,3},{3,2},{4,5},{5,4},{6,7},{7,6},{8,9},{9,8},{10,11... | collective-permute-start | bytes 4718600 | tf_op jit(solution)/shard_map/ppermute | solution.py:358
  109.0 38.7 %collective-permute-start.24 = (bf16[128,1536]{1,0:T(8,128)(2,1)}, bf16[128,1536]{1,0:T(8,128)(2,1)S(1)}, u32[]{:S(2)}, u32[]{:S(2)}) collective-permute-start(bf16[128,1536]{1,0:T(8,128)(2,1)} %multiply_convert_fusion), channel_id=1, source_target_pairs={{0,8},{4,12},{8,0},{12,4},{1,9},{5,13},{9,1},{13,5},{2,10},{6,14},... | collective-permute-start | bytes 1179656 | tf_op jit(solution)/shard_map/ppermute | solution.py:358
  113.8 71.4 %collective-permute-start.13 = (bf16[1120,768]{1,0:T(8,128)(2,1)}, bf16[1120,768]{1,0:T(8,128)(2,1)}, u32[]{:S(2)}, u32[]{:S(2)}) collective-permute-start(bf16[1120,768]{1,0:T(8,128)(2,1)} %dynamic-slice_bitcast_fusion.1.refs_0_), channel_id=1, source_target_pairs={{0,16},{16,0},{1,17},{17,1},{2,18},{18,2},{3,19},{19,3},{4,20},{20... | collective-permute-start | bytes 5160968 | tf_op jit(solution)/shard_map/ppermute | solution.py:358
  132.8 27.8 %collective-permute-start.29 = (bf16[256,1536]{1,0:T(8,128)(2,1)}, bf16[256,1536]{1,0:T(8,128)(2,1)S(1)}, u32[]{:S(2)}, u32[]{:S(2)}) collective-permute-start(bf16[256,1536]{1,0:T(8,128)(2,1)} %collective-permute-done.28), channel_id=1, source_target_pairs={{0,4},{4,0},{8,12},{12,8},{1,5},{5,1},{9,13},{13,9},{2,6},{6,2},{1... | collective-permute-start | bytes 2359304 | tf_op jit(solution)/shard_map/ppermute | solution.py:358
  150.7 30.9 %collective-permute-start.10 = (bf16[512,1536]{1,0:T(8,128)(2,1)}, bf16[512,1536]{1,0:T(8,128)(2,1)}, u32[]{:S(2)}, u32[]{:S(2)}) collective-permute-start(bf16[512,1536]{1,0:T(8,128)(2,1)} %pad_maximum_fusion.2), channel_id=1, source_target_pairs={{0,1},{1,0},{2,3},{3,2},{4,5},{5,4},{6,7},{7,6},{8,9},{9,8},{10,11... | collective-permute-start | bytes 4718600 | tf_op jit(solution)/shard_map/ppermute | solution.py:358
  160.7 40.8 %collective-permute-start.14 = (bf16[1120,768]{1,0:T(8,128)(2,1)}, bf16[1120,768]{1,0:T(8,128)(2,1)}, u32[]{:S(2)}, u32[]{:S(2)}) collective-permute-start(bf16[1120,768]{1,0:T(8,128)(2,1)} %dynamic-slice_bitcast_fusion.refs_2_), channel_id=1, source_target_pairs={{0,16},{16,0},{1,17},{17,1},{2,18},{18,2},{3,19},{19,3},{4,20},{20... | collective-permute-start | bytes 5160968 | tf_op jit(solution)/shard_map/ppermute | solution.py:358
  161.3 73.6 %collective-permute-start.15 = (bf16[1120,768]{1,0:T(8,128)(2,1)}, bf16[1120,768]{1,0:T(8,128)(2,1)}, u32[]{:S(2)}, u32[]{:S(2)}) collective-permute-start(bf16[1120,768]{1,0:T(8,128)(2,1)} %constant_dynamic-slice_fusion.6.refs_4_), channel_id=1, source_target_pairs={{0,16},{16,0},{1,17},{17,1},{2,18},{18,2},{3,19},{19,3},{4,20},{20... | collective-permute-start | bytes 5160968 | tf_op jit(solution)/shard_map/ppermute | solution.py:358
  180.3 95.0 %collective-permute-start.30 = (bf16[512,1536]{1,0:T(8,128)(2,1)}, bf16[512,1536]{1,0:T(8,128)(2,1)}, u32[]{:S(2)}, u32[]{:S(2)}) collective-permute-start(bf16[512,1536]{1,0:T(8,128)(2,1)} %pad_maximum_fusion.7), channel_id=1, source_target_pairs={{0,1},{1,0},{2,3},{3,2},{4,5},{5,4},{6,7},{7,6},{8,9},{9,8},{10,11... | collective-permute-start | bytes 4718600 | tf_op jit(solution)/shard_map/ppermute | solution.py:358
  181.6 97.9 %collective-permute-start.27 = (bf16[512,1536]{1,0:T(8,128)(2,1)}, bf16[512,1536]{1,0:T(8,128)(2,1)}, u32[]{:S(2)}, u32[]{:S(2)}) collective-permute-start(bf16[512,1536]{1,0:T(8,128)(2,1)} %pad_maximum_fusion.6), channel_id=1, source_target_pairs={{0,1},{1,0},{2,3},{3,2},{4,5},{5,4},{6,7},{7,6},{8,9},{9,8},{10,11... | collective-permute-start | bytes 4718600 | tf_op jit(solution)/shard_map/ppermute | solution.py:358
  283.7 40.1 %collective-permute-start.17 = (bf16[256,1536]{1,0:T(8,128)(2,1)}, bf16[256,1536]{1,0:T(8,128)(2,1)}, u32[]{:S(2)}, u32[]{:S(2)}) collective-permute-start(bf16[256,1536]{1,0:T(8,128)(2,1)} %slice.307), channel_id=1, source_target_pairs={{0,4},{4,0},{8,12},{12,8},{1,5},{5,1},{9,13},{13,9},{2,6},{6,2},{1... | collective-permute-start | bytes 2359304 | tf_op jit(solution)/shard_map/ppermute | solution.py:358
  289.2 31.1 %collective-permute-start.22 = (bf16[256,1536]{1,0:T(8,128)(2,1)}, bf16[256,1536]{1,0:T(8,128)(2,1)}, u32[]{:S(2)}, u32[]{:S(2)}) collective-permute-start(bf16[256,1536]{1,0:T(8,128)(2,1)} %slice.306), channel_id=1, source_target_pairs={{0,4},{4,0},{8,12},{12,8},{1,5},{5,1},{9,13},{13,9},{2,6},{6,2},{1... | collective-permute-start | bytes 2359304 | tf_op jit(solution)/shard_map/ppermute | solution.py:358
  364.5 45.5 %collective-permute-start.31 = (bf16[1120,768]{1,0:T(8,128)(2,1)}, bf16[1120,768]{1,0:T(8,128)(2,1)S(1)}, u32[]{:S(2)}, u32[]{:S(2)}) collective-permute-start(bf16[1120,768]{1,0:T(8,128)(2,1)} %get-tuple-element.57), channel_id=1, source_target_pairs={{0,16},{16,0},{1,17},{17,1},{2,18},{18,2},{3,19},{19,3},{4,20},{20... | collective-permute-start | bytes 5160968 | tf_op jit(solution)/shard_map/ppermute | solution.py:358
  365.3 76.8 %collective-permute-start.32 = (bf16[1120,768]{1,0:T(8,128)(2,1)}, bf16[1120,768]{1,0:T(8,128)(2,1)}, u32[]{:S(2)}, u32[]{:S(2)}) collective-permute-start(bf16[1120,768]{1,0:T(8,128)(2,1)} %get-tuple-element.58), channel_id=1, source_target_pairs={{0,16},{16,0},{1,17},{17,1},{2,18},{18,2},{3,19},{19,3},{4,20},{20... | collective-permute-start | bytes 5160968 | tf_op jit(solution)/shard_map/ppermute | solution.py:358
  366.5 109.5 %collective-permute-start.33 = (bf16[1120,768]{1,0:T(8,128)(2,1)}, bf16[1120,768]{1,0:T(8,128)(2,1)}, u32[]{:S(2)}, u32[]{:S(2)}) collective-permute-start(bf16[1120,768]{1,0:T(8,128)(2,1)} %get-tuple-element.59), channel_id=1, source_target_pairs={{0,16},{16,0},{1,17},{17,1},{2,18},{18,2},{3,19},{19,3},{4,20},{20... | collective-permute-start | bytes 5160968 | tf_op jit(solution)/shard_map/ppermute | solution.py:358
  390.2 94.2 %collective-permute-start.20 = (bf16[256,1536]{1,0:T(8,128)(2,1)}, bf16[256,1536]{1,0:T(8,128)(2,1)}, u32[]{:S(2)}, u32[]{:S(2)}) collective-permute-start(bf16[256,1536]{1,0:T(8,128)(2,1)} %pad_maximum_fusion.14), channel_id=1, source_target_pairs={{0,1},{1,0},{2,3},{3,2},{4,5},{5,4},{6,7},{7,6},{8,9},{9,8},{10,11... | collective-permute-start | bytes 2359304 | tf_op jit(solution)/shard_map/ppermute | solution.py:358
  478.4 171.8 %collective-permute-start.55 = (bf16[1120,768]{1,0:T(8,128)(2,1)S(1)}, bf16[1120,768]{1,0:T(8,128)(2,1)}, u32[]{:S(2)}, u32[]{:S(2)}) collective-permute-start(bf16[1120,768]{1,0:T(8,128)(2,1)S(1)} %add_convert_fusion.1), channel_id=1, source_target_pairs={{0,4},{4,0},{8,12},{12,8},{1,5},{5,1},{9,13},{13,9},{2,6},{6,2},{1... | collective-permute-start | bytes 5160968 | tf_op jit(solution)/shard_map/ppermute | solution.py:358
  483.3 47.1 %collective-permute-start.43 = (bf16[768,384]{1,0:T(8,128)(2,1)S(1)}, bf16[768,384]{1,0:T(8,128)(2,1)S(1)}, u32[]{:S(2)}, u32[]{:S(2)}) collective-permute-start(bf16[768,384]{1,0:T(8,128)(2,1)S(1)} %convolution_convert_fusion.5), channel_id=1, source_target_pairs={{0,16},{16,0},{1,17},{17,1},{2,18},{18,2},{3,19},{19,3},{4,20},{20... | collective-permute-start | bytes 1769480 | tf_op jit(solution)/shard_map/ppermute | solution.py:358
  493.2 29.6 %collective-permute-start.37 = (bf16[1024,128]{1,0:T(8,128)(2,1)S(1)}, bf16[1024,128]{1,0:T(8,128)(2,1)S(1)}, u32[]{:S(2)}, u32[]{:S(2)}) collective-permute-start(bf16[1024,128]{1,0:T(8,128)(2,1)S(1)} %slice.313), channel_id=1, source_target_pairs={{0,8},{4,12},{8,0},{12,4},{1,9},{5,13},{9,1},{13,5},{2,10},{6,14},... | collective-permute-start | bytes 786440 | tf_op jit(solution)/shard_map/ppermute | solution.py:358
  499.2 145.5 %collective-permute-start.56 = (bf16[1120,768]{1,0:T(8,128)(2,1)}, bf16[1120,768]{1,0:T(8,128)(2,1)}, u32[]{:S(2)}, u32[]{:S(2)}) collective-permute-start(bf16[1120,768]{1,0:T(8,128)(2,1)} %add_convert_fusion), channel_id=1, source_target_pairs={{0,4},{4,0},{8,12},{12,8},{1,5},{5,1},{9,13},{13,9},{2,6},{6,2},{1... | collective-permute-start | bytes 5160968 | tf_op jit(solution)/shard_map/ppermute | solution.py:358
  501.5 84.9 %collective-permute-start.52 = (bf16[384,768]{1,0:T(8,128)(2,1)}, bf16[384,768]{1,0:T(8,128)(2,1)}, u32[]{:S(2)}, u32[]{:S(2)}) collective-permute-start(bf16[384,768]{1,0:T(8,128)(2,1)} %fusion.2), channel_id=1, source_target_pairs={{0,4},{4,0},{8,12},{12,8},{1,5},{5,1},{9,13},{13,9},{2,6},{6,2},{1... | collective-permute-start | bytes 1769480 | tf_op jit(solution)/shard_map/ppermute | solution.py:358
  522.9 54.0 %collective-permute-start.38 = (bf16[512,128]{1,0:T(8,128)(2,1)S(1)}, bf16[512,128]{1,0:T(8,128)(2,1)S(1)}, u32[]{:S(2)}, u32[]{:S(2)}) collective-permute-start(bf16[512,128]{1,0:T(8,128)(2,1)S(1)} %slice.314), channel_id=1, source_target_pairs={{0,4},{4,0},{8,12},{12,8},{1,5},{5,1},{9,13},{13,9},{2,6},{6,2},{1... | collective-permute-start | bytes 393224 | tf_op jit(solution)/shard_map/ppermute | solution.py:358
  531.9 62.8 %collective-permute-start.44 = (bf16[768,384]{1,0:T(8,128)(2,1)}, bf16[768,384]{1,0:T(8,128)(2,1)}, u32[]{:S(2)}, u32[]{:S(2)}) collective-permute-start(bf16[768,384]{1,0:T(8,128)(2,1)} %fusion.1), channel_id=1, source_target_pairs={{0,4},{4,0},{8,12},{12,8},{1,5},{5,1},{9,13},{13,9},{2,6},{6,2},{1... | collective-permute-start | bytes 1769480 | tf_op jit(solution)/shard_map/ppermute | solution.py:358
  585.2 53.7 %collective-permute-start.39 = (bf16[256,1536]{1,0:T(8,128)(2,1)S(1)}, bf16[256,1536]{1,0:T(8,128)(2,1)S(1)}, u32[]{:S(2)}, u32[]{:S(2)}) collective-permute-start(bf16[256,1536]{1,0:T(8,128)(2,1)S(1)} %slice.236), channel_id=1, source_target_pairs={{0,1},{1,0},{2,3},{3,2},{4,5},{5,4},{6,7},{7,6},{8,9},{9,8},{10,11... | collective-permute-start | bytes 2359304 | tf_op jit(solution)/shard_map/ppermute | solution.py:358
  593.8 61.9 %collective-permute-start.54 = (bf16[1120,768]{1,0:T(8,128)(2,1)S(1)}, bf16[1120,768]{1,0:T(8,128)(2,1)S(1)}, u32[]{:S(2)}, u32[]{:S(2)}) collective-permute-start(bf16[1120,768]{1,0:T(8,128)(2,1)S(1)} %add_convert_fusion.2), channel_id=1, source_target_pairs={{0,4},{4,0},{8,12},{12,8},{1,5},{5,1},{9,13},{13,9},{2,6},{6,2},{1... | collective-permute-start | bytes 5160968 | tf_op jit(solution)/shard_map/ppermute | solution.py:358
  594.6 40.8 %collective-permute-start.48 = (bf16[768,128]{0,1:T(8,128)(2,1)S(1)}, bf16[768,128]{0,1:T(8,128)(2,1)S(1)}, u32[]{:S(2)}, u32[]{:S(2)}) collective-permute-start(bf16[768,128]{0,1:T(8,128)(2,1)S(1)} %add_convert_fusion.6), channel_id=1, source_target_pairs={{0,8},{4,12},{8,0},{12,4},{1,9},{5,13},{9,1},{13,5},{2,10},{6,14},... | collective-permute-start | bytes 589832 | tf_op jit(solution)/shard_map/ppermute | solution.py:358
  635.5 45.0 %collective-permute-start.53 = (bf16[384,768]{1,0:T(8,128)(2,1)S(1)}, bf16[384,768]{1,0:T(8,128)(2,1)S(1)}, u32[]{:S(2)}, u32[]{:S(2)}) collective-permute-start(bf16[384,768]{1,0:T(8,128)(2,1)S(1)} %add_convert_fusion.3), channel_id=1, source_target_pairs={{0,8},{4,12},{8,0},{12,4},{1,9},{5,13},{9,1},{13,5},{2,10},{6,14},... | collective-permute-start | bytes 1769480 | tf_op jit(solution)/shard_map/ppermute | solution.py:358
  644.6 47.8 %collective-permute-start.45 = (bf16[768,384]{1,0:T(8,128)(2,1)S(1)}, bf16[768,384]{1,0:T(8,128)(2,1)S(1)}, u32[]{:S(2)}, u32[]{:S(2)}) collective-permute-start(bf16[768,384]{1,0:T(8,128)(2,1)S(1)} %add_convert_fusion.4), channel_id=1, source_target_pairs={{0,8},{4,12},{8,0},{12,4},{1,9},{5,13},{9,1},{13,5},{2,10},{6,14},... | collective-permute-start | bytes 1769480 | tf_op jit(solution)/shard_map/ppermute | solution.py:358
  644.7 50.4 %collective-permute-start.50 = (bf16[1536,128]{0,1:T(8,128)(2,1)S(1)}, bf16[1536,128]{0,1:T(8,128)(2,1)S(1)}, u32[]{:S(2)}, u32[]{:S(2)}) collective-permute-start(bf16[1536,128]{0,1:T(8,128)(2,1)S(1)} %pad_maximum_fusion.23), channel_id=1, source_target_pairs={{0,1},{1,0},{2,3},{3,2},{4,5},{5,4},{6,7},{7,6},{8,9},{9,8},{10,11... | collective-permute-start | bytes 1179656 | tf_op jit(solution)/shard_map/ppermute | solution.py:358
  650.2 43.4 %collective-permute-start.40 = (bf16[128,1536]{1,0:T(8,128)(2,1)S(1)}, bf16[128,1536]{1,0:T(8,128)(2,1)S(1)}, u32[]{:S(2)}, u32[]{:S(2)}) collective-permute-start(bf16[128,1536]{1,0:T(8,128)(2,1)S(1)} %slice.309), channel_id=1, source_target_pairs={{0,2},{1,3},{2,0},{3,1},{4,6},{5,7},{6,4},{7,5},{8,10},{9,11},{10,... | collective-permute-start | bytes 1179656 | tf_op jit(solution)/shard_map/ppermute | solution.py:358
  694.3 43.3 %collective-permute-start.41 = (bf16[128,1536]{1,0:T(8,128)(2,1)S(1)}, bf16[128,1536]{1,0:T(8,128)(2,1)S(1)}, u32[]{:S(2)}, u32[]{:S(2)}) collective-permute-start(bf16[128,1536]{1,0:T(8,128)(2,1)S(1)} %fusion.7), channel_id=1, source_target_pairs={{0,2},{1,3},{2,0},{3,1},{4,6},{5,7},{6,4},{7,5},{8,10},{9,11},{10,... | collective-permute-start | bytes 1179656 | tf_op jit(solution)/shard_map/ppermute | solution.py:358
  (85 other events, 940.3 us)

commit v3 on v2

--- a/solution.py
+++ b/solution.py
@@ -42,17 +42,6 @@
     moved = grad_field * sine
     turned = jnp.concatenate([moved[..., halfway:], -moved[..., :halfway]], axis=-1)
     return grad_field * cosine + turned
-
-
-def rms_scale(values):
-    return lax.rsqrt(jnp.mean(values * values, axis=-1, keepdims=True) + EPSILON)
-
-
-def norm_back(values, factor, gain, grad_normed):
-    gained = gain * grad_normed
-    inner = jnp.mean(gained * values, axis=-1, keepdims=True)
-    grad_values = factor * gained - values * (factor * factor * factor) * inner
-    return (grad_values, jnp.sum(grad_normed * values * factor, axis=0))
 
 
 def dot(left, right):
@@ -88,18 +77,18 @@
     lse_ref[0] = row_max + jnp.log(total)
 
 
-def attention(key_blocks, queries, keys, values):
+def attention(key_blocks, queries, kv):
     rows, width = queries.shape
     heads = width // HD
-    whole = pl.BlockSpec(keys.shape, lambda h, i, kb: (0, 0))
+    whole = lambda kind: pl.BlockSpec((None,) + kv.shape[1:], lambda h, i, kb: (kind, 0, 0))
     tile = pl.BlockSpec((BLOCK, HD), lambda h, i, kb: (i, h))
     return pl.pallas_call(
-        functools.partial(attention_kernel, keys.shape[0] // BLOCK),
+        functools.partial(attention_kernel, kv.shape[1] // BLOCK),
         name="attention",
         grid_spec=pltpu.PrefetchScalarGridSpec(
             num_scalar_prefetch=1,
             grid=(heads, rows // BLOCK),
-            in_specs=[tile, whole, whole],
+            in_specs=[tile, whole(0), whole(1)],
             out_specs=[tile, pl.BlockSpec((1, BLOCK, 1), lambda h, i, kb: (h, i, 0))],
         ),
         out_shape=[
@@ -107,12 +96,7 @@
             jax.ShapeDtypeStruct((heads, rows, 1), f32),
         ],
         compiler_params=pltpu.CompilerParams(vmem_limit_bytes=VMEM_LIMIT),
-        cost_estimate=pl.CostEstimate(
-            flops=4 * rows * keys.shape[0] * width,
-            bytes_accessed=4 * rows * width + 4 * keys.size,
-            transcendentals=rows * keys.shape[0] * heads,
-        ),
-    )(key_blocks, queries, keys, values)
+    )(key_blocks, queries, kv, kv)
 
 
 def attention_back_kernel(
@@ -126,6 +110,7 @@
     k_ref,
     v_ref,
     dq_ref,
+    dkv_ref,
     dk_ref,
     dv_ref,
 ):
@@ -151,15 +136,20 @@
     dk_ref[...] += dot_rows(grad_scores, q_ref[...]) * SCALING
     dv_ref[...] += dot_rows(probability.astype(bf16), do_ref[...])
 
-
-def attention_back(key_blocks, queries, grad_out, lse, cosine, sine, keys, values):
+    @pl.when((head == pl.num_programs(0) - 1) & (i == pl.num_programs(1) - 1))
+    def _():
+        dkv_ref[0] = dk_ref[...].astype(bf16)
+        dkv_ref[1] = dv_ref[...].astype(bf16)
+
+
+def attention_back(key_blocks, queries, grad_out, lse, cosine, sine, kv):
     rows, width = queries.shape
     heads = width // HD
-    whole = pl.BlockSpec(keys.shape, lambda h, i, kb: (0, 0))
+    whole = lambda kind: pl.BlockSpec((None,) + kv.shape[1:], lambda h, i, kb: (kind, 0, 0))
     tile = pl.BlockSpec((BLOCK, HD), lambda h, i, kb: (i, h))
     table = pl.BlockSpec((BLOCK, HD), lambda h, i, kb: (i, 0))
     return pl.pallas_call(
-        functools.partial(attention_back_kernel, keys.shape[0] // BLOCK),
+        functools.partial(attention_back_kernel, kv.shape[1] // BLOCK),
         name="attention_back",
         grid_spec=pltpu.PrefetchScalarGridSpec(
             num_scalar_prefetch=1,
@@ -170,23 +160,18 @@
                 pl.BlockSpec((1, BLOCK, 1), lambda h, i, kb: (h, i, 0)),
                 table,
                 table,
-                whole,
-                whole,
+                whole(0),
+                whole(1),
             ],
-            out_specs=[tile, whole, whole],
+            out_specs=[tile, pl.BlockSpec(kv.shape, lambda h, i, kb: (0, 0, 0))],
+            scratch_shapes=[pltpu.VMEM(kv.shape[1:], f32)] * 2,
         ),
         out_shape=[
             jax.ShapeDtypeStruct((rows, width), bf16),
-            jax.ShapeDtypeStruct(keys.shape, f32),
-            jax.ShapeDtypeStruct(keys.shape, f32),
+            jax.ShapeDtypeStruct(kv.shape, bf16),
         ],
         compiler_params=pltpu.CompilerParams(vmem_limit_bytes=VMEM_LIMIT),
-        cost_estimate=pl.CostEstimate(
-            flops=10 * rows * keys.shape[0] * width,
-            bytes_accessed=6 * rows * width + 12 * keys.size,
-            transcendentals=rows * keys.shape[0] * heads,
-        ),
-    )(key_blocks, queries, grad_out, lse, cosine, sine, keys, values)
+    )(key_blocks, queries, grad_out, lse, cosine, sine, kv, kv)
 
 
 def qkv_kernel(pieces, meta_ref, x_ref, gain_ref, bias_ref, cos_ref, sin_ref, *refs):
@@ -240,11 +225,6 @@
             jax.ShapeDtypeStruct((rows, HD), bf16),
         ],
         compiler_params=pltpu.CompilerParams(vmem_limit_bytes=VMEM_LIMIT),
-        cost_estimate=pl.CostEstimate(
-            flops=2 * rows * width * out,
-            bytes_accessed=4 * rows * width + 2 * width * out,
-            transcendentals=0,
-        ),
     )(meta, inputs, gain, bias, cosine, sine, *weights)
 
 
@@ -268,34 +248,35 @@
             outs[3][:, at] = (dot(grad_gate, g[...]) + dot(grad_up, u[...])).astype(bf16)
 
 
-def ffn(meta, normed, grad_out, wg, wu, wd, with_dx):
-    rows, width = normed.shape
-    units = wg[0].shape[0]
+def ffn(meta, normed, grad_out, weights, with_dx):
+    width = normed.shape[-1]
+    half = 0 if with_dx else 1
+    rows = normed.shape[1] * normed.shape[2]
+    units = weights[0].shape[0] // 3
     tile = 512
+    steps = rows // tile
+    flat = lambda x: x.reshape(-1, width)
     row = lambda n: pl.BlockSpec((tile, n), lambda i, m: (i, 0))
-    weight = lambda w: pl.BlockSpec(w.shape, lambda i, m: (0, 0), pipeline_mode=pl.Buffered(1))
-    weights = list(wg) + list(wu) + list(wd)
+    read = pl.BlockSpec((tile, width), lambda i, m: (i + half * steps, 0))
+    weight = lambda w, k: pl.BlockSpec(
+        (units, w.shape[1]), lambda i, m: (k, 0), pipeline_mode=pl.Buffered(1)
+    )
     widths = [units] * 3 + [width] * with_dx
     return pl.pallas_call(
-        functools.partial(ffn_kernel, with_dx, len(wg)),
+        functools.partial(ffn_kernel, with_dx, len(weights)),
         name="ffn_pair" if with_dx else "ffn_far",
         grid_spec=pltpu.PrefetchScalarGridSpec(
             num_scalar_prefetch=1,
-            grid=(rows // tile,),
-            in_specs=[row(width), row(width)] + [weight(w) for w in weights],
+            grid=(steps,),
+            in_specs=[read, read] + [weight(w, k) for k in range(3) for w in weights],
             out_specs=[row(n) for n in widths],
         ),
         out_shape=[jax.ShapeDtypeStruct((rows, n), bf16) for n in widths],
         compiler_params=pltpu.CompilerParams(vmem_limit_bytes=VMEM_LIMIT),
-        cost_estimate=pl.CostEstimate(
-            flops=2 * rows * width * units * (5 if with_dx else 3),
-            bytes_accessed=2 * (3 * width * units + 3 * rows * units + 3 * rows * width),
-            transcendentals=rows * units,
-        ),
-    )(meta, normed, grad_out, *weights)
-
-
-def unit_grads_kernel(meta_ref, xp, xf, yp, yf, hp, hf, gp, gf, up, uf, og, ou, od, ag, au, ad):
+    )(meta, flat(normed), flat(grad_out), *(list(weights) * 3))
+
+
+def unit_grads_kernel(meta_ref, x, y, hp, hf, gp, gf, up, uf, og, ou, od, ag, au, ad):
     step = pl.program_id(0)
 
     @pl.when(step == 0)
@@ -303,7 +284,7 @@
         for acc in (ag, au, ad):
             acc[...] = jnp.zeros_like(acc)
 
-    for use, x, y, h, g, u in ((True, xp, yp, hp, gp, up), (False, xf, yf, hf, gf, uf)):
+    for use, h, g, u in ((True, hp, gp, up), (False, hf, gf, uf)):
 
         @pl.when((step // (pl.num_programs(0) // 2) == meta_ref[3]) == use)
         def _():
@@ -319,15 +300,17 @@
 
 
 def unit_grads(meta, which, pieces, x, y, hid, dg, du):
-    rows, width = x[0].shape
-    units = dg[0].shape[1]
+    width = x.shape[-1]
+    rows, units = dg[0].shape
     depth = width // pieces
     tile = 512
     steps = rows // tile
     shard = (lambda m: m[which]) if pieces > 1 else (lambda m: 0)
     near = lambda i, m: jnp.clip(i - steps * m[3], 0, steps - 1)
     far = lambda i, m: jnp.clip(i - steps * (1 - m[3]), 0, steps - 1)
-    feature = lambda at: pl.BlockSpec((tile, depth), lambda i, m: (at(i, m), shard(m)))
+    feature = pl.BlockSpec(
+        (tile, depth), lambda i, m: (lax.rem(i + steps * m[3], 2 * steps), shard(m))
+    )
     unit = lambda at: pl.BlockSpec((tile, units), lambda i, m: (at(i, m), 0))
     return pl.pallas_call(
         unit_grads_kernel,
@@ -335,7 +318,7 @@
         grid_spec=pltpu.PrefetchScalarGridSpec(
             num_scalar_prefetch=1,
             grid=(2 * steps,),
-            in_specs=[feature(near), feature(far)] * 2 + [unit(near), unit(far)] * 3,
+            in_specs=[feature] * 2 + [unit(near), unit(far)] * 3,
             out_specs=[
                 pl.BlockSpec((units, depth), lambda i, m: (0, 0), pipeline_mode=pl.Buffered(1))
             ]
@@ -344,12 +327,406 @@
         ),
         out_shape=[jax.ShapeDtypeStruct((units, depth), bf16)] * 3,
         compiler_params=pltpu.CompilerParams(vmem_limit_bytes=VMEM_LIMIT),
-        cost_estimate=pl.CostEstimate(
-            flops=12 * rows * depth * units,
-            bytes_accessed=2 * (6 * rows * units + 4 * rows * depth + 3 * units * depth),
-            transcendentals=0,
+    )(meta, x.reshape(-1, width), y.reshape(-1, width), *hid, *dg, *du)
+
+
+class Wires:
+    def __init__(self, sends, receives, locals_):
+        self.sends, self.receives, self.locals = sends, receives, locals_
+        self.used = self.used_local = 0
+        self.started = []
+
+    def copy(self, source, target, device):
+        k = self.used
+        self.used += 1
+        one = pltpu.make_async_remote_copy(
+            source,
+            target,
+            self.sends.at[k],
+            self.receives.at[k],
+            device_id=device,
+            device_id_type=pl.DeviceIdType.MESH,
+        )
+        one.start()
+        self.started.append(one)
+        return one
+
+    def here(self, source, target):
+        k = self.used_local
+        self.used_local += 1
+        one = pltpu.make_async_copy(source, target, self.locals.at[k])
+        one.start()
+        return one
+
+    def finish(self):
+        for one in self.started:
+            one.wait_send()
+
+
+def meet(devices):
+    barrier = pltpu.get_barrier_semaphore()
+    for device in devices:
+        pl.semaphore_signal(barrier, inc=1, device_id=device, device_id_type=pl.DeviceIdType.MESH)
+    pl.semaphore_wait(barrier, len(devices))
+
+
+def partners():
+    c, t = lax.axis_index("context"), lax.axis_index("tensor")
+    flip = lambda x, bit: x + bit * (1 - 2 * lax.rem(x // bit, 2))
+    return {
+        "core": {"tensor": flip(t, 1)},
+        "y": {"tensor": flip(t, 2)},
+        "z": {"context": flip(c, 1)},
+        "far": {"context": flip(c, 2)},
+        "last": {"context": flip(flip(c, 1), 2)},
+    }
+
+
+def wide(x):
+    return x.astype(f32)
+
+
+def scatter_rank(wires, to, part, own, got_core, sent, got_y):
+    size = part.shape[1] // 2
+    halves = [pl.ds(0, size), pl.ds(size, size)]
+    from_core = {}
+    for block in (1, 0):
+        for k, at in enumerate(halves):
+            from_core[block, k] = wires.copy(
+                part.at[2 + block, at], got_core.at[block, at], to["core"]
+            )
+    mine = wires.here(part.at[pl.ds(0, 2)], own)
+    mine.wait()
+    from_y = []
+    for k, at in enumerate(halves):
+        from_core[1, k].wait_recv()
+        sent[at] = (wide(own[1, at]) + wide(got_core[1, at])).astype(bf16)
+        from_y.append(wires.copy(sent.at[at], got_y.at[at], to["y"]))
+    for k in range(2):
+        from_core[0, k].wait_recv()
+    total = wide(own[0]) + wide(got_core[0])
+    for one in from_y:
+        one.wait_recv()
+    return total + wide(got_y[...])
+
+
+def scatter_pair(wires, to, part, own, got_core, sent, got_y, got_z, diag_y, diag_z):
+    size = part.shape[1] // 2
+    low, high = pl.ds(0, size), pl.ds(size, size)
+    from_core = {j: wires.copy(part.at[4 + j], got_core.at[j], to["core"]) for j in (3, 1, 2, 0)}
+    mine = wires.here(part.at[pl.ds(0, 4)], own)
+    mine.wait()
+    both = lambda j, at: wide(own[j, at]) + wide(got_core[j, at])
+    from_core[3].wait_recv()
+    sent[2] = (wide(own[3]) + wide(got_core[3])).astype(bf16)
+    via_z = wires.copy(sent.at[2, low], diag_z, to["z"])
+    via_y = wires.copy(sent.at[2, high], diag_y, to["y"])
+    from_core[1].wait_recv()
+    sent[0, high] = both(1, high).astype(bf16)
+    y_high = wires.copy(sent.at[0, high], got_y.at[high], to["y"])
+    from_core[2].wait_recv()
+    sent[1, low] = both(2, low).astype(bf16)
+    z_low = wires.copy(sent.at[1, low], got_z.at[low], to["z"])
+    via_z.wait_recv()
+    sent[0, low] = (both(1, low) + wide(diag_z[...])).astype(bf16)
+    y_low = wires.copy(sent.at[0, low], got_y.at[low], to["y"])
+    via_y.wait_recv()
+    sent[1, high] = (both(2, high) + wide(diag_y[...])).astype(bf16)
+    z_high = wires.copy(sent.at[1, high], got_z.at[high], to["z"])
+    from_core[0].wait_recv()
+    total = wide(own[0]) + wide(got_core[0])
+    for one in (y_high, z_low, y_low, z_high):
+        one.wait_recv()
+    return total + wide(got_y[...]) + wide(got_z[...])
+
+
+def gather_rank(wires, to, block, out, at):
+    size = block.shape[0] // 2
+    halves = [pl.ds(0, size), pl.ds(size, size)]
+    mine = wires.here(block, out.at[at(0, 0)])
+    from_y = [wires.copy(block.at[h], out.at[at(0, 2), h], to["y"]) for h in halves]
+    from_core = [wires.copy(block, out.at[at(0, 1)], to["core"])]
+    for h, one in zip(halves, from_y):
+        one.wait_recv()
+        from_core.append(wires.copy(out.at[at(2, 0), h], out.at[at(2, 1), h], to["core"]))
+    for one in from_core:
+        one.wait_recv()
+    mine.wait()
+
+
+def gather_pair(wires, to, block, out, base):
+    size = block.shape[0] // 2
+    low, high = pl.ds(0, size), pl.ds(size, size)
+    at = lambda j: out.at[base + j]
+    from_y = wires.copy(block, at(1), to["y"])
+    from_z = wires.copy(block, at(2), to["z"])
+    from_core = [wires.copy(block, at(4), to["core"])]
+    from_y.wait_recv()
+    via_z = wires.copy(out.at[base + 1, low], out.at[base + 3, low], to["z"])
+    from_core.append(wires.copy(at(1), at(5), to["core"]))
+    from_z.wait_recv()
+    via_y = wires.copy(out.at[base + 2, high], out.at[base + 3, high], to["y"])
+    from_core.append(wires.copy(at(2), at(6), to["core"]))
+    via_z.wait_recv()
+    via_y.wait_recv()
+    from_core.append(wires.copy(at(3), at(7), to["core"]))
+    return from_core
+
+
+def remote_call(kernel, name, key, args, outs, scratch, copies, in_vmem):
+    ins, out_in = in_vmem
+    spec = lambda inside: pl.BlockSpec(memory_space=pltpu.VMEM if inside else pl.ANY)
+    return pl.pallas_call(
+        kernel,
+        name=name,
+        out_shape=outs,
+        in_specs=[spec(x) for x in ins],
+        out_specs=[spec(x) for x in out_in],
+        scratch_shapes=list(scratch)
+        + [
+            pltpu.SemaphoreType.DMA((copies,)),
+            pltpu.SemaphoreType.DMA((copies,)),
+            pltpu.SemaphoreType.DMA((4,)),
+        ],
+        compiler_params=pltpu.CompilerParams(
+            collective_id=key, has_side_effects=True, vmem_limit_bytes=VMEM_LIMIT
         ),
-    )(meta, *x, *y, *hid, *dg, *du)
+    )(*args)
+
+
+def kv_gather_kernel(own_ref, out_ref, *sems):
+    wires, to = Wires(*sems), partners()
+    kind = lax.rem(lax.axis_index("tensor"), 2)
+    rows = own_ref.shape[0]
+    block = lambda j: out_ref.at[kind, pl.ds(j * rows, rows)]
+    meet([to[k] for k in ("core", "z", "far", "last")])
+    mine = wires.here(own_ref, block(0))
+    arrive = [wires.copy(own_ref, block(j), to[k]) for j, k in ((3, "last"), (2, "far"), (1, "z"))]
+    from_core = [wires.copy(own_ref, block(0), to["core"])]
+    for j, one in ((1, arrive[2]), (2, arrive[1]), (3, arrive[0])):
+        one.wait_recv()
+        from_core.append(wires.copy(block(j), block(j), to["core"]))
+    for one in from_core:
+        one.wait_recv()
+    mine.wait()
+    wires.finish()
+
+
+def kv_gather(own):
+    rows, width = own.shape
+    n_c = lax.axis_size("context")
+    return remote_call(
+        kv_gather_kernel,
+        "kv_gather",
+        0,
+        [own],
+        [jax.ShapeDtypeStruct((2, n_c * rows, width), bf16)],
+        [],
+        8,
+        ([False], [False]),
+    )[0]
+
+
+def kv_scatter_kernel(part_ref, out_ref, own, got_core, sent, got, *sems):
+    wires, to = Wires(*sems), partners()
+    kind = lax.rem(lax.axis_index("tensor"), 2)
+    rows = out_ref.shape[0]
+    block = lambda j: pl.ds(j * rows, rows)
+    meet([to[k] for k in ("core", "z", "far", "last")])
+    steps = ((3, "last"), (2, "far"), (1, "z"), (0, None))
+    from_core = {
+        j: wires.copy(part_ref.at[1 - kind, block(j)], got_core.at[block(j)], to["core"])
+        for j, _ in steps
+    }
+    mine = wires.here(part_ref.at[kind], own)
+    mine.wait()
+    arrive = []
+    for j, k in steps[:3]:
+        from_core[j].wait_recv()
+        sent[block(j)] = (wide(own[block(j)]) + wide(got_core[block(j)])).astype(bf16)
+        arrive.append(wires.copy(sent.at[block(j)], got.at[block(j)], to[k]))
+    from_core[0].wait_recv()
+    total = wide(own[block(0)]) + wide(got_core[block(0)])
+    for one in arrive:
+        one.wait_recv()
+    for j in (1, 2, 3):
+        total = total + wide(got[block(j)])
+    out_ref[...] = total
+    wires.finish()
+
+
+def kv_scatter(part):
+    _, rows, width = part.shape
+    n_c = lax.axis_size("context")
+    return remote_call(
+        kv_scatter_kernel,
+        "kv_scatter",
+        1,
+        [part],
+        [jax.ShapeDtypeStruct((rows // n_c, width), f32)],
+        [pltpu.VMEM((rows, width), bf16)] * 4,
+        7,
+        ([False], [True]),
+    )[0]
+
+
+def middle_kernel(part, x_ref, gain_ref, mid_ref, factor_ref, out, own, core, sent, got, xn, *sems):
+    wires, to = Wires(*sems), partners()
+    meet([to[k] for k in ("core", "y", "z", "far")])
+    middle = wide(x_ref[...]) + scatter_rank(wires, to, part, own, core, sent, got)
+    mid_ref[...] = middle
+    factor = lax.rsqrt(jnp.mean(middle * middle, axis=-1, keepdims=True) + EPSILON)
+    factor_ref[...] = factor
+    xn[...] = (middle * factor * gain_ref[...]).astype(bf16)
+    blocks = out.shape[0] // 2
+    mine = wires.here(xn, out.at[0])
+    from_far = wires.copy(xn, out.at[blocks], to["far"])
+    last = gather_pair(wires, to, xn, out, 0)
+    from_far.wait_recv()
+    last += gather_pair(wires, to, out.at[blocks], out, blocks)
+    for one in last:
+        one.wait_recv()
+    mine.wait()
+    wires.finish()
+
+
+def middle_norm(part, inputs_part, gain):
+    rows, width = inputs_part.shape
+    return remote_call(
+        middle_kernel,
+        "middle_norm",
+        2,
+        [part.reshape(4, rows, width), inputs_part, gain],
+        [
+            jax.ShapeDtypeStruct((rows, width), f32),
+            jax.ShapeDtypeStruct((rows, 1), f32),
+            jax.ShapeDtypeStruct((16, rows, width), bf16),
+        ],
+        [
+            pltpu.VMEM((2, rows, width), bf16),
+            pltpu.VMEM((2, rows, width), bf16),
+            pltpu.VMEM((rows, width), bf16),
+            pltpu.VMEM((rows, width), bf16),
+            pltpu.VMEM((rows, width), bf16),
+        ],
+        32,
+        ([False, True, True], [True, True, False]),
+    )
+
+
+def norm_back_rows(values, factor, gain, grad_normed):
+    gained = gain * grad_normed
+    inner = jnp.mean(gained * values, axis=-1, keepdims=True)
+    grad_values = factor * gained - values * (factor * factor * factor) * inner
+    return grad_values, jnp.sum(grad_normed * values * factor, axis=0, keepdims=True)
+
+
+MIXED = (0, 2, 1, 3)
+
+
+def middle_back_kernel(part, mid_ref, factor_ref, gain_ref, dy_ref, dmid_ref, dgain_ref, out, *rest):
+    low, rest = rest[0], rest[1:]
+    wires, to = Wires(*rest[-3:]), partners()
+    meet([to[k] for k in ("core", "y", "z")])
+    grad_normed = scatter_pair(wires, to, part, *rest[:-3])
+    du, dgain = norm_back_rows(mid_ref[...], factor_ref[...], gain_ref[...], grad_normed)
+    dgain_ref[...] = dgain
+    dmid = wide(dy_ref[...]) + du
+    dmid_ref[...] = dmid
+    low[...] = dmid.astype(bf16)
+    gather_rank(wires, to, low, out, lambda j, flip: MIXED.index(j ^ flip))
+    wires.finish()
+
+
+def pair_scratch(rows, width):
+    return [
+        pltpu.VMEM((4, rows, width), bf16),
+        pltpu.VMEM((4, rows, width), bf16),
+        pltpu.VMEM((3, rows, width), bf16),
+        pltpu.VMEM((rows, width), bf16),
+        pltpu.VMEM((rows, width), bf16),
+        pltpu.VMEM((rows // 2, width), bf16),
+        pltpu.VMEM((rows // 2, width), bf16),
+    ]
+
+
+def middle_back(part, middle, factor, gain, dy_part):
+    rows, width = middle.shape
+    return remote_call(
+        middle_back_kernel,
+        "middle_back",
+        3,
+        [part.reshape(8, rows, width), middle, factor, gain, dy_part],
+        [
+            jax.ShapeDtypeStruct((rows, width), f32),
+            jax.ShapeDtypeStruct((1, width), f32),
+            jax.ShapeDtypeStruct((4, rows, width), bf16),
+        ],
+        [pltpu.VMEM((rows, width), bf16)] + pair_scratch(rows, width),
+        16,
+        ([False, True, True, True, True], [True, True, False]),
+    )
+
+
+def outputs_kernel(part, mid_ref, out, low, *rest):
+    wires, to = Wires(*rest[-3:]), partners()
+    t = lax.axis_index("tensor")
+    flip = lambda x, bit: x + bit * (1 - 2 * lax.rem(x // bit, 2))
+    meet([to[k] for k in ("core", "y", "z")])
+    low[...] = (mid_ref[...] + scatter_pair(wires, to, part, *rest[:-3])).astype(bf16)
+    gather_rank(wires, to, low, out, lambda j, _: t if j == 0 else flip(t, j))
+    wires.finish()
+
+
+def final_outputs(part, middle):
+    rows, width = middle.shape
+    return remote_call(
+        outputs_kernel,
+        "final_outputs",
+        4,
+        [part.reshape(8, rows, width), middle],
+        [jax.ShapeDtypeStruct((4, rows, width), bf16)],
+        [pltpu.VMEM((rows, width), bf16)] + pair_scratch(rows, width),
+        16,
+        ([False, True], [False]),
+    )[0].reshape(4 * rows, width)
+
+
+def input_back_kernel(part, x_ref, factor_ref, gain_ref, dmid_ref, dgain_ref, out, *rest):
+    low, own, core, sent, got = rest[:-3]
+    wires, to = Wires(*rest[-3:]), partners()
+    t = lax.axis_index("tensor")
+    flip = lambda x, bit: x + bit * (1 - 2 * lax.rem(x // bit, 2))
+    meet([to[k] for k in ("core", "y")])
+    grad_normed = scatter_rank(wires, to, part, own, core, sent, got)
+    du, dgain = norm_back_rows(wide(x_ref[...]), factor_ref[...], gain_ref[...], grad_normed)
+    dgain_ref[...] = dgain
+    low[...] = (dmid_ref[...] + du).astype(bf16)
+    gather_rank(wires, to, low, out, lambda j, _: t if j == 0 else flip(t, j))
+    wires.finish()
+
+
+def input_back(part, inputs_part, factor, gain, grad_middle):
+    rows, width = inputs_part.shape
+    return remote_call(
+        input_back_kernel,
+        "input_back",
+        5,
+        [part.reshape(4, rows, width), inputs_part, factor, gain, grad_middle],
+        [
+            jax.ShapeDtypeStruct((1, width), f32),
+            jax.ShapeDtypeStruct((4, rows, width), bf16),
+        ],
+        [
+            pltpu.VMEM((rows, width), bf16),
+            pltpu.VMEM((2, rows, width), bf16),
+            pltpu.VMEM((2, rows, width), bf16),
+            pltpu.VMEM((rows, width), bf16),
+            pltpu.VMEM((rows, width), bf16),
+        ],
+        16,
+        ([False, True, True, True, True], [True, False]),
+    )
 
 
 def build(n_f, n_c, n_t):
@@ -420,7 +797,7 @@
                 x = low.astype(f32) + flip(low, "context", bit).astype(f32)
             return x
 
-        order = (0, 2, 1, 3)
+        order = MIXED
 
         def mixed(x):
             return jnp.concatenate(
@@ -436,25 +813,11 @@
                 axis=0,
             )
 
-        def add_half(x, axis, bit):
-            half = x.shape[0] // 2
-            got = flip(x[half:].astype(bf16), axis, bit)
-            return x[:half].astype(f32) + got.astype(f32)
-
-        def scatter_t(x):
-            return add_half(add_half(x, "tensor", 1), "tensor", 2)
-
-        def scatter_pair(x):
-            return add_half(add_half(add_half(x, "tensor", 1), "context", 1), "tensor", 2)
-
         def grow(x, axis, bit):
             return jnp.concatenate([x, flip(x, axis, bit)], axis=0)
 
         def gather_t(x):
             return grow(grow(x, "tensor", 2), "tensor", 1)
-
-        def gather_pair(x):
-            return grow(grow(grow(x, "tensor", 2), "context", 1), "tensor", 1)
 
         small = jnp.concatenate(
             [v.reshape(1, -1) for v in (attn_gain, ffn_gain, b_query, b_key, b_value)], axis=1
@@ -487,14 +850,15 @@
         b_kv = lax.dynamic_index_in_dim(jnp.where(core == 0, bk, bv), group, 0)
 
         unit_slice = lambda w: lax.dynamic_slice_in_dim(w, parity * units, units, 0)
-        wg = pieces_f(unit_slice(w_gate.T), 1)
-        wu = pieces_f(unit_slice(w_up.T), 1)
-        wd = pieces_f(unit_slice(w_down), 1)
+        w_units = pieces_f(
+            jnp.concatenate([unit_slice(w) for w in (w_gate.T, w_up.T, w_down)], axis=0), 1
+        )
 
         dy_own = mixed(cotangent)[: 2 * part]
         dy_near = jnp.concatenate([dy_own, flip(dy_own, "context", 1)], axis=0)
         dy_pair = grow(dy_near, "tensor", 1)
         dy_far = grow(grow(flip(dy_own, "context", 2), "context", 1), "tensor", 1)
+        dy_all = jnp.concatenate([dy_pair, dy_far], axis=0).reshape(2, -1, part, width)
 
         seq_blocks = blocks[0].reshape(n_c, -1)
         own_blocks = seq_blocks.shape[1]
@@ -509,37 +873,22 @@
         normed, factor_first, queries, kv_own = qkv(
             meta, inputs, gain_first, bias, cosine, sine, w_qkv
         )
-        kv_whole = grow(grow(kv_own, "context", 1), "context", 2)
-        kv_other = flip(kv_whole, "tensor", 1)
-        keys = jnp.where(core == 0, kv_whole, kv_other)
-        values = jnp.where(core == 0, kv_other, kv_whole)
-        attended, lse = attention(key_blocks, queries, keys, values)
-
+        kv = kv_gather(kv_own)
+        attended, lse = attention(key_blocks, queries, kv)
         attended_mixed = mixed(attended)
-        attn_sum = scatter_t(dot(attended_mixed, w_out_all))
-        middle = lax.dynamic_slice_in_dim(inputs, t * part, part, 0).astype(f32) + attn_sum
-
-        factor_second = rms_scale(middle)
-        normed2 = (middle * factor_second * gain_second).astype(bf16)
-        normed2_pair = gather_pair(normed2)
-        normed2_far = gather_pair(flip(normed2, "context", 2))
-        hid_pair, dg_pair, du_pair, dx_part = ffn(meta, normed2_pair, dy_pair, wg, wu, wd, True)
-        grad_normed2 = scatter_pair(dx_part)
-        hid_far, dg_far, du_far = ffn(meta, normed2_far, dy_far, wg, wu, wd, False)
-        final = middle + scatter_pair(columns_f([dot(hid_pair, w) for w in wd]))
-        outputs = natural(gather_t(final.astype(bf16)))
-
-        grad_args = (
-            (normed2_pair, normed2_far),
-            (dy_pair, dy_far),
-            (hid_pair, hid_far),
-            (dg_pair, dg_far),
-            (du_pair, du_far),
-        )
+        inputs_part = lax.dynamic_slice_in_dim(inputs, t * part, part, 0)
+        middle, factor_second, normed2 = middle_norm(
+            dot(attended_mixed, w_out_all).astype(bf16), inputs_part, gain_second
+        )
+
+        normed2 = normed2.reshape(2, -1, part, width)
+        hid_pair, dg_pair, du_pair, dx_part = ffn(meta, normed2, dy_all, w_units, True)
+        hid_far, dg_far, du_far = ffn(meta, normed2, dy_all, w_units, False)
+        grad_args = (normed2, dy_all, (hid_pair, hid_far), (dg_pair, dg_far), (du_pair, du_far))
         if n_f == 2:
             unit_sent = unit_grads(meta, 1, 2, *grad_args)
             unit_got = [flip(x, "fsdp", 1) for x in unit_sent]
-            unit_own = unit_grads(meta, 0, 2, *grad_args)
+            dx_part, _ = lax.optimization_barrier((dx_part, unit_sent))
         else:
             unit_own = [
                 lax.psum_scatter(x, "fsdp", scatter_dimension=1, tiled=True)
@@ -551,23 +900,20 @@
             low = (own.astype(f32) + got.astype(f32)).astype(bf16)
             return by_bit(parity, low, flip(low, "context", 1), 0).astype(f32)
 
-        grad_mid_norm, ffn_gain_grad = norm_back(middle, factor_second, gain_second, grad_normed2)
-        dy_part = lax.dynamic_slice_in_dim(cotangent, t * part, part, 0).astype(f32)
-        grad_middle = dy_part + grad_mid_norm
-        grad_middle_low = gather_t(grad_middle.astype(bf16))
+        dy_part = lax.dynamic_slice_in_dim(cotangent, t * part, part, 0)
+        grad_middle, ffn_gain_grad, grad_middle_low = middle_back(
+            dx_part, middle, factor_second, gain_second, dy_part
+        )
+        grad_middle_low = grad_middle_low.reshape(rows, width)
         wo_grad = sum_c(grad_f(attended_mixed, grad_middle_low, 1))
         grad_attended = natural(dot_cols(grad_middle_low, w_out_all).astype(bf16))
 
-        dq_low, dk, dv = attention_back(
-            key_blocks, queries, grad_attended, lse, cosine, sine, keys, values
-        )
-        unit_own, unit_got, dq_low = lax.optimization_barrier((unit_own, unit_got, dq_low))
-        wg_grad, wu_grad, wd_grad = (unit_done(a, b) for a, b in zip(unit_own, unit_got))
-        wg_grad, wu_grad = wg_grad.T, wu_grad.T
-        dkv_keep = jnp.where(core == 0, dk, dv)
-        dkv_send = jnp.where(core == 0, dv, dk).astype(bf16)
-        dkv = dkv_keep + flip(dkv_send, "tensor", 1).astype(f32)
-        dkv = add_half(add_half(dkv, "context", 2), "context", 1)
+        dq_low, dkv = attention_back(key_blocks, queries, grad_attended, lse, cosine, sine, kv)
+        dkv = kv_scatter(dkv)
+        if n_f == 2:
+            late_args, _ = lax.optimization_barrier((grad_args, dkv))
+            unit_own = unit_grads(meta, 0, 2, *late_args)
+            unit_got, _ = lax.optimization_barrier((unit_got, dkv))
         dkv_low = jnp.where(core == 0, rotate_back(dkv, cosine, sine), dkv).astype(bf16)
         wq_grad = sum_c(grad_f(normed, dq_low, 0))
         wkv_own = sum_c(grad_f(normed, dkv_low, 0)).astype(bf16)
@@ -583,11 +929,20 @@
         wv_grad = jnp.concatenate(wkv_rank[1::2], axis=1)
 
         d_qkv = mixed(jnp.concatenate([dq_low, dkv_low], axis=1))
-        grad_normed = scatter_t(columns_f([dot_cols(d_qkv, w) for w in w_qkv]))
-        inputs_part = lax.dynamic_slice_in_dim(inputs, t * part, part, 0).astype(f32)
         factor_part = lax.dynamic_slice_in_dim(factor_first, t * part, part, 0)
-        grad_in_norm, attn_gain_grad = norm_back(inputs_part, factor_part, gain_first, grad_normed)
-        input_grad = natural(gather_t((grad_middle + grad_in_norm).astype(bf16)))
+        attn_gain_grad, input_grad = input_back(
+            columns_f([dot_cols(d_qkv, w) for w in w_qkv]),
+            inputs_part,
+            factor_part,
+            gain_first,
+            grad_middle,
+        )
+        input_grad = input_grad.reshape(rows, width)
+        outputs = final_outputs(
+            columns_f([dot(hid_pair, w[2 * units :]) for w in w_units]), middle
+        )
+        wg_grad, wu_grad, wd_grad = (unit_done(a, b) for a, b in zip(unit_own, unit_got))
+        wg_grad, wu_grad = wg_grad.T, wu_grad.T
 
         bq_grad = jnp.sum(dq_low.astype(f32), axis=0)
         bkv_grad = jnp.sum(dkv_low.astype(f32), axis=0)
@@ -596,7 +951,7 @@
             slots, jnp.concatenate([bq_grad, bkv_grad])[None], (t, 0)
         )
         packed = lax.psum(
-            jnp.concatenate([attn_gain_grad, ffn_gain_grad, slots.reshape(-1)]),
+            jnp.concatenate([attn_gain_grad[0], ffn_gain_grad[0], slots.reshape(-1)]),
             ("fsdp", "context", "tensor"),
         )
         attn_gain_grad = lax.dynamic_slice_in_dim(packed, f * piece, piece, 0)

time: 752 us -> 784 us (1.043)
  Pallas kernels: 121 us -> 304 us
  waiting for transfers between devices: 379 us -> 261 us
  blocking collectives: 40.9 us -> 76.9 us
  starting transfers between devices: 63.1 us -> 28 us
  other arithmetic: 78.7 us -> 45.2 us
    pallas_call x4 -> x10, Pallas kernels: 73.8 us -> 258 us  [the longest x6 184 us: remote_call(): pl.pallas_call(kernel, name=name, out_shape=outs, in_specs=[spec(x) for x...]
    ppermute x57 -> x26, waiting for transfers between devices: 379 us -> 261 us  [flip(): return lax.ppermute(x, axis, [(i, i ^ bit) for i in range(size)])]
    psum x1, blocking collectives: 40.9 us -> 76.9 us  [local(): lax.psum(jnp.concatenate([attn_gain_grad[0], ffn_gain_grad[0], slots.resh...]
    ppermute x57 -> x26, starting transfers between devices: 63.1 us -> 28 us  [flip(): return lax.ppermute(x, axis, [(i, i ^ bit) for i in range(size)])]
    concatenate x13 -> x2, other arithmetic: 19.3 us -> 2.42 us  [grow(): return jnp.concatenate([x, flip(x, axis, bit)], axis=0)]
    unnamed x131 -> x113, local copies, waits for them, and re-layouts: 14.6 us -> 20.3 us
  transfers between devices with their start and end apart: 57 -> 26, of which waited for: 27 -> 14; matrix products, arithmetic and copies ran while one was open for 16% -> 9% of each run, Pallas kernels for 15% -> 22%
where the time goes in v3:
time: 784 us; the launch traced here: 776 us
  Pallas kernels  304 us (39%)
  waiting for transfers between devices  261 us (33%)
  blocking collectives  76.9 us (10%)
  other arithmetic  45.2 us (6%)
  local copies, waits for them, and re-layouts  36.1 us (5%)
  starting transfers between devices  28 us (4%)
  matrix products  23.5 us (3%)
    ppermute x26, waiting for transfers between devices, flip(): return lax.ppermute(x, axis, [(i, i ^ bit) for i in range(size)])  261 us
    pallas_call x6, Pallas kernels, remote_call(): pl.pallas_call(kernel, name=name, out_shape=outs, in_specs=[spec(x) for x...  184 us
    psum x1, blocking collectives, local(): lax.psum(jnp.concatenate([attn_gain_grad[0], ffn_gain_grad[0], slots.resh...  76.9 us
    pallas_call x2, Pallas kernels, ffn(): pl.pallas_call(functools.partial(ffn_kernel, with_dx, len(weights)), name...  48.9 us
    pallas_call x2, Pallas kernels, unit_grads(): pl.pallas_call(unit_grads_kernel, name=f'unit_grads_{which}', grid_spec=p...  40.1 us
    ppermute x26, starting transfers between devices, flip(): return lax.ppermute(x, axis, [(i, i ^ bit) for i in range(size)])  28 us
    unnamed x113, local copies, waits for them, and re-layouts  20.3 us
  transfers between devices with their start and end apart: 26, of which 14 were waited for; matrix products, arithmetic and copies ran while one was open for 9% of the time, Pallas kernels for 22%

profile of v3, /device:TPU:0, one launch (start us, length us, event | category | flops | bytes accessed | tf_op | source)
XLA Modules:
  0.0 775.7 jit_solution(1257682827521352323)
XLA Ops:
  32.4 92.5 %collective-permute-done = bf16[1,1984]{1,0:T(2,128)(2,1)S(1)} collective-permute-done((bf16[1,1984]{1,0:T(2,128)(2,1)S(1)}, bf16[1,1984]{1,0:T(2,128)(2,1)S(1)}, u32[]{:S(2)}, u32[]{:S(2)}) %collective-permute-start) | collective-permute-done | bytes 4000 | tf_op jit(solution)/shard_map/ppermute | solution.py:735
  131.6 12.7 %collective-permute-done.6 = bf16[256,1536]{1,0:T(8,128)(2,1)} collective-permute-done((bf16[256,1536]{1,0:T(8,128)(2,1)S(1)}, bf16[256,1536]{1,0:T(8,128)(2,1)}, u32[]{:S(2)}, u32[]{:S(2)}) %collective-permute-start.6) | collective-permute-done | bytes 786464 | tf_op jit(solution)/shard_map/ppermute | solution.py:735
  147.3 6.4 collective-permute-done.1.refs_1_
  153.8 5.6 qkv.1
  159.3 17.5 %kv_gather.1.k_ref.v_ref = bf16[2,2048,128]{2,1,0:T(8,128)(2,1)} custom-call(bf16[512,128]{1,0:T(8,128)(2,1)} %get-tuple-element.56.own_ref), custom_call_target="tpu_custom_call" | custom-call | tf_op jit(solution)/shard_map/kv_gather/pallas_call | solution.py:479
  176.8 10.3 %attention.1 = (bf16[512,384]{1,0:T(8,128)(2,1)}, f32[3,512,1]{2,1,0:T(8,128)}) custom-call(s32[8]{0:T(128)} %pad_add_fusion.1.kb_ref, bf16[512,384]{1,0:T(8,128)(2,1)} %get-tuple-element.55.q_ref, bf16[2,2048,128]{2,1,0:T(8,128)(2,1)} %kv_gather.1.k_ref.v_ref, bf16[2,2048,128]{2,1,0:T(8,128)(2,1)} %kv_gather.1.k_ref.v_ref), custom_call_target="tpu_custom_call" | custom-call | tf_op jit(solution)/shard_map/attention/pallas_call | solution.py:85
  188.2 3.5 convolution_convert_fusion
  191.7 58.2 %middle_norm.1 = (f32[128,1536]{1,0:T(8,128)}, f32[128,1]{1,0:T(8,128)}, bf16[16,128,1536]{2,1,0:T(8,128)(2,1)}) custom-call(bf16[4,128,1536]{2,1,0:T(8,128)(2,1)} %bitcast.101, bf16[128,1536]{1,0:T(8,128)(2,1)} %constant_dynamic-slice_fusion.10.x_ref, f32[1,1536]{1,0:T(1,128)} %bitcast.111), custom_call_target="tpu_custom_call" | custom-call | tf_op jit(solution)/shard_map/middle_norm/pallas_call | solution.py:479
  260.6 28.8 %ffn_pair.1 = (bf16[1024,1120]{1,0:T(8,128)(2,1)}, bf16[1024,1120]{1,0:T(8,128)(2,1)}, bf16[1024,1120]{1,0:T(8,128)(2,1)}, bf16[1024,1536]{1,0:T(8,128)(2,1)}) custom-call(s32[4]{0:T(128)} %pad_add_fusion.meta_ref, bf16[2048,1536]{1,0:T(8,128)(2,1)} %bitcast.93, bf16[2048,1536]{1,0:T(8,128)(2,1)} %constant_dynamic-update-slice_fusion.dy_ref.y, ...), custom_call_target="tpu_custom_call" | custom-call | tf_op jit(solution)/shard_map/ffn_pair/pallas_call | solution.py:265
  289.5 5.0 convolution_convert_fusion.1
  294.5 20.1 %ffn_far.1 = (bf16[1024,1120]{1,0:T(8,128)(2,1)}, bf16[1024,1120]{1,0:T(8,128)(2,1)}, bf16[1024,1120]{1,0:T(8,128)(2,1)}) custom-call(s32[4]{0:T(128)} %pad_add_fusion.meta_ref, bf16[2048,1536]{1,0:T(8,128)(2,1)} %bitcast.94, bf16[2048,1536]{1,0:T(8,128)(2,1)} %constant_dynamic-update-slice_fusion.dy_ref.y, ...), custom_call_target="tpu_custom_call" | custom-call | tf_op jit(solution)/shard_map/ffn_far/pallas_call | solution.py:265
  314.6 20.0 %unit_grads_1.1 = (bf16[1120,768]{1,0:T(8,128)(2,1)}, bf16[1120,768]{1,0:T(8,128)(2,1)}, bf16[1120,768]{1,0:T(8,128)(2,1)}) custom-call(s32[4]{0:T(128)} %pad_add_fusion.meta_ref, bf16[2048,1536]{1,0:T(8,128)(2,1)} %bitcast.95, bf16[2048,1536]{1,0:T(8,128)(2,1)} %constant_dynamic-update-slice_fusion.dy_ref.y, bf16[1024,1120]{1,0:T(8,128)(2,1)} %get-tuple-element.84.hp, ...), custom_call_target="tpu_custom_call" | custom-call | tf_op jit(solution)/shard_map/unit_grads_1/pallas_call | solution.py:315
  334.5 31.8 %middle_back.1 = (f32[128,1536]{1,0:T(8,128)}, f32[1,1536]{1,0:T(1,128)}, bf16[4,128,1536]{2,1,0:T(8,128)(2,1)}) custom-call(bf16[8,128,1536]{2,1,0:T(8,128)(2,1)} %bitcast.98, f32[128,1536]{1,0:T(8,128)} %get-tuple-element.60.mid_ref, f32[128,1]{1,0:T(8,128)} %get-tuple-element.71.factor_ref, f32[1,1536]{1,0:T(1,128)} %bitcast.112, bf16[128,1536]{1,0:T(8,128)(2,1)} %copy-done.5), custom_call_target="tpu_custom_call" | custom-call | tf_op jit(solution)/shard_map/middle_back/pallas_call | solution.py:479
  370.1 15.0 %attention_back.1 = (bf16[512,384]{1,0:T(8,128)(2,1)}, bf16[2,2048,128]{2,1,0:T(8,128)(2,1)}) custom-call(s32[8]{0:T(128)} %pad_add_fusion.1.kb_ref, bf16[512,384]{1,0:T(8,128)(2,1)} %get-tuple-element.55.q_ref, bf16[512,384]{1,0:T(8,128)(2,1)} %pad_maximum_fusion.9.do_ref, f32[3,512,1]{2,1,0:T(8,128)} %get-tuple-element.73.lse_ref, ...), custom_call_target="tpu_custom_call" | custom-call | tf_op jit(solution)/shard_map/attention_back/pallas_call | solution.py:151
  385.1 17.6 %kv_scatter.1 = f32[512,128]{1,0:T(8,128)} custom-call(bf16[2,2048,128]{2,1,0:T(8,128)(2,1)} %get-tuple-element.75.part_ref), custom_call_target="tpu_custom_call" | custom-call | tf_op jit(solution)/shard_map/kv_scatter/pallas_call | solution.py:479
  413.1 3.7 fusion.3
  418.9 31.6 %final_outputs.1 = bf16[4,128,1536]{2,1,0:T(8,128)(2,1)} custom-call(bf16[8,128,1536]{2,1,0:T(8,128)(2,1)} %maximum_select_fusion.3.part, f32[128,1536]{1,0:T(8,128)} %get-tuple-element.60.mid_ref), custom_call_target="tpu_custom_call" | custom-call | tf_op jit(solution)/shard_map/final_outputs/pallas_call | solution.py:479
  455.1 27.2 %input_back.1 = (f32[1,1536]{1,0:T(1,128)}, bf16[4,128,1536]{2,1,0:T(8,128)(2,1)}) custom-call(bf16[4,128,1536]{2,1,0:T(8,128)(2,1)} %maximum_select_fusion.4.part, bf16[128,1536]{1,0:T(8,128)(2,1)} %constant_dynamic-slice_fusion.10.x_ref, f32[128,1]{1,0:T(8,128)} %constant_dynamic-slice_fusion.6.factor_ref, f32[1,1536]{1,0:T(1,128)} %bitcast.114, ...), custom_call_target="tpu_custom_call" | custom-call | tf_op jit(solution)/shard_map/input_back/pallas_call | solution.py:479
  483.1 76.9 %psum.7 = f32[5120]{0:T(1024)S(1)} all-reduce(f32[5120]{0:T(1024)S(1)} %pad_maximum_fusion.15), channel_id=1, replica_groups=mesh['fsdp'=2,'context'=4,'tensor'=4] {'fsdp','context','tensor'}, use_global_device_ids=true, to_apply=%region_2.3 | all-reduce | flops 5120 | bytes 40960 | tf_op jit(solution)/shard_map/psum | solution.py:953
  562.4 20.2 %unit_grads_0.1 = (bf16[1120,768]{1,0:T(8,128)(2,1)}, bf16[1120,768]{1,0:T(8,128)(2,1)}, bf16[1120,768]{1,0:T(8,128)(2,1)}) custom-call(s32[4]{0:T(128)} %pad_add_fusion.meta_ref, bf16[2048,1536]{1,0:T(8,128)(2,1)} %bitcast.96, bf16[2048,1536]{1,0:T(8,128)(2,1)} %bitcast.46.y, bf16[1024,1120]{1,0:T(8,128)(2,1)} %get-tuple-element.84.hp, ...), custom_call_target="tpu_custom_call" | custom-call | tf_op jit(solution)/shard_map/unit_grads_0/pallas_call | solution.py:315
  584.2 5.1 collective-permute-done.13
  591.4 6.8 collective-permute-done.14
  609.1 5.3 collective-permute-done.18
  615.4 9.2 %collective-permute-done.10 = bf16[768,384]{1,0:T(8,128)(2,1)S(1)} collective-permute-done((bf16[768,384]{1,0:T(8,128)(2,1)S(1)}, bf16[768,384]{1,0:T(8,128)(2,1)S(1)}, u32[]{:S(2)}, u32[]{:S(2)}) %collective-permute-start.10) | collective-permute-done | bytes 589856 | tf_op jit(solution)/shard_map/ppermute | solution.py:735
  641.2 22.9 %collective-permute-done.19 = bf16[384,768]{1,0:T(8,128)(2,1)} collective-permute-done((bf16[384,768]{1,0:T(8,128)(2,1)}, bf16[384,768]{1,0:T(8,128)(2,1)}, u32[]{:S(2)}, u32[]{:S(2)}) %collective-permute-start.19) | collective-permute-done | bytes 589856 | tf_op jit(solution)/shard_map/ppermute | solution.py:735
  666.5 10.2 %collective-permute-done.11 = bf16[768,384]{1,0:T(8,128)(2,1)} collective-permute-done((bf16[768,384]{1,0:T(8,128)(2,1)}, bf16[768,384]{1,0:T(8,128)(2,1)}, u32[]{:S(2)}, u32[]{:S(2)}) %collective-permute-start.11) | collective-permute-done | bytes 589856 | tf_op jit(solution)/shard_map/ppermute | solution.py:735
  679.0 20.4 %collective-permute-done.25 = bf16[1120,768]{1,0:T(8,128)(2,1)S(1)} collective-permute-done((bf16[1120,768]{1,0:T(8,128)(2,1)S(1)}, bf16[1120,768]{1,0:T(8,128)(2,1)S(1)}, u32[]{:S(2)}, u32[]{:S(2)}) %collective-permute-start.25) | collective-permute-done | bytes 1720352 | tf_op jit(solution)/shard_map/ppermute | solution.py:735
  699.4 3.2 fusion
  702.6 33.6 %collective-permute-done.23 = bf16[1120,768]{1,0:T(8,128)(2,1)S(1)} collective-permute-done((bf16[1120,768]{1,0:T(8,128)(2,1)S(1)}, bf16[1120,768]{1,0:T(8,128)(2,1)S(1)}, u32[]{:S(2)}, u32[]{:S(2)}) %collective-permute-start.23) | collective-permute-done | bytes 1720352 | tf_op jit(solution)/shard_map/ppermute | solution.py:735
  736.2 3.2 convert_bitcast_fusion.1
  739.5 29.6 %collective-permute-done.24 = bf16[1120,768]{1,0:T(8,128)(2,1)S(1)} collective-permute-done((bf16[1120,768]{1,0:T(8,128)(2,1)S(1)}, bf16[1120,768]{1,0:T(8,128)(2,1)S(1)}, u32[]{:S(2)}, u32[]{:S(2)}) %collective-permute-start.24) | collective-permute-done | bytes 1720352 | tf_op jit(solution)/shard_map/ppermute | solution.py:735
  769.1 3.2 convert_bitcast_fusion
  (244 shorter events, 116.9 us)
Async XLA Ops:
  9.5 251.1 %collective-permute-start.8 = (bf16[3360,768]{1,0:T(8,128)(2,1)}, bf16[3360,768]{1,0:T(8,128)(2,1)}, u32[]{:S(2)}, u32[]{:S(2)}) collective-permute-start(bf16[3360,768]{1,0:T(8,128)(2,1)} %pad_maximum_fusion.refs_0_.refs_2_.refs_4_), channel_id=1, source_target_pairs={{0,16},{16,0},{1,17},{17,1},{2,18},{18,2},{3,19},{19,3},{4,20},{20... | collective-permute-start | bytes 15482888 | tf_op jit(solution)/shard_map/ppermute | solution.py:735
  14.4 114.4 %copy-start.5 = (bf16[128,1536]{1,0:T(8,128)(2,1)}, bf16[128,1536]{1,0:T(8,128)(2,1)S(1)}, u32[]{:S(2)}) copy-start(bf16[128,1536]{1,0:T(8,128)(2,1)S(1)} %get-tuple-element.101.dy_ref) | copy-start | bytes 1179652
  17.3 109.8 %collective-permute-start.5 = (bf16[256,1536]{1,0:T(8,128)(2,1)}, bf16[256,1536]{1,0:T(8,128)(2,1)S(1)}, u32[]{:S(2)}, u32[]{:S(2)}) collective-permute-start(bf16[256,1536]{1,0:T(8,128)(2,1)} %pad_maximum_fusion.4), channel_id=1, source_target_pairs={{0,8},{4,12},{8,0},{12,4},{1,9},{5,13},{9,1},{13,5},{2,10},{6,14},... | collective-permute-start | bytes 2359304 | tf_op jit(solution)/shard_map/ppermute | solution.py:735
  19.9 108.9 %collective-permute-start.3 = (bf16[256,1536]{1,0:T(8,128)(2,1)}, bf16[256,1536]{1,0:T(8,128)(2,1)S(1)}, u32[]{:S(2)}, u32[]{:S(2)}) collective-permute-start(bf16[256,1536]{1,0:T(8,128)(2,1)} %pad_maximum_fusion.4), channel_id=1, source_target_pairs={{0,4},{4,0},{8,12},{12,8},{1,5},{5,1},{9,13},{13,9},{2,6},{6,2},{1... | collective-permute-start | bytes 2359304 | tf_op jit(solution)/shard_map/ppermute | solution.py:735
  21.8 103.2 %collective-permute-start = (bf16[1,1984]{1,0:T(2,128)(2,1)S(1)}, bf16[1,1984]{1,0:T(2,128)(2,1)S(1)}, u32[]{:S(2)}, u32[]{:S(2)}) collective-permute-start(bf16[1,1984]{1,0:T(2,128)(2,1)S(1)} %concatenate.126), channel_id=1, source_target_pairs={{0,16},{16,0},{1,17},{17,1},{2,18},{18,2},{3,19},{19,3},{4,20},{20... | collective-permute-start | bytes 11912 | tf_op jit(solution)/shard_map/ppermute | solution.py:735
  22.4 165.8 %collective-permute-start.2 = (bf16[384,768]{1,0:T(8,128)(2,1)}, bf16[384,768]{1,0:T(8,128)(2,1)}, u32[]{:S(2)}, u32[]{:S(2)}) collective-permute-start(bf16[384,768]{1,0:T(8,128)(2,1)} %param.25), channel_id=1, source_target_pairs={{0,16},{16,0},{1,17},{17,1},{2,18},{18,2},{3,19},{19,3},{4,20},{20... | collective-permute-start | bytes 1769480 | tf_op jit(solution)/shard_map/ppermute | solution.py:735
  29.8 100.2 %copy-start.7 = (bf16[768,512]{1,0:T(8,128)(2,1)}, bf16[768,512]{1,0:T(8,128)(2,1)S(1)}, u32[]{:S(2)}) copy-start(bf16[768,512]{1,0:T(8,128)(2,1)S(1)} %pad_maximum_fusion.3.refs_0_) | copy-start | bytes 2359300
  125.0 28.8 %collective-permute-start.1 = (bf16[768,512]{1,0:T(8,128)(2,1)S(1)}, bf16[768,512]{1,0:T(8,128)(2,1)}, u32[]{:S(2)}, u32[]{:S(2)}) collective-permute-start(bf16[768,512]{1,0:T(8,128)(2,1)S(1)} %pad_maximum_fusion.3.refs_0_), channel_id=1, source_target_pairs={{0,16},{16,0},{1,17},{17,1},{2,18},{18,2},{3,19},{19,3},{4,20},{20... | collective-permute-start | bytes 2359304 | tf_op jit(solution)/shard_map/ppermute | solution.py:735
  127.1 17.3 %collective-permute-start.6 = (bf16[256,1536]{1,0:T(8,128)(2,1)S(1)}, bf16[256,1536]{1,0:T(8,128)(2,1)}, u32[]{:S(2)}, u32[]{:S(2)}) collective-permute-start(bf16[256,1536]{1,0:T(8,128)(2,1)S(1)} %collective-permute-done.5), channel_id=1, source_target_pairs={{0,4},{4,0},{8,12},{12,8},{1,5},{5,1},{9,13},{13,9},{2,6},{6,2},{1... | collective-permute-start | bytes 2359304 | tf_op jit(solution)/shard_map/ppermute | solution.py:735
  130.0 122.3 %collective-permute-start.4 = (bf16[512,1536]{1,0:T(8,128)(2,1)}, bf16[512,1536]{1,0:T(8,128)(2,1)}, u32[]{:S(2)}, u32[]{:S(2)}) collective-permute-start(bf16[512,1536]{1,0:T(8,128)(2,1)} %pad_maximum_fusion.1), channel_id=1, source_target_pairs={{0,1},{1,0},{2,3},{3,2},{4,5},{5,4},{6,7},{7,6},{8,9},{9,8},{10,11... | collective-permute-start | bytes 4718600 | tf_op jit(solution)/shard_map/ppermute | solution.py:735
  146.8 111.2 %collective-permute-start.7 = (bf16[512,1536]{1,0:T(8,128)(2,1)}, bf16[512,1536]{1,0:T(8,128)(2,1)}, u32[]{:S(2)}, u32[]{:S(2)}) collective-permute-start(bf16[512,1536]{1,0:T(8,128)(2,1)} %pad_maximum_fusion.2), channel_id=1, source_target_pairs={{0,1},{1,0},{2,3},{3,2},{4,5},{5,4},{6,7},{7,6},{8,9},{9,8},{10,11... | collective-permute-start | bytes 4718600 | tf_op jit(solution)/shard_map/ppermute | solution.py:735
  188.2 219.7 %copy-start.31 = (bf16[128,384]{1,0:T(8,128)(2,1)}, bf16[128,384]{1,0:T(8,128)(2,1)S(1)}, u32[]{:S(2)}) copy-start(bf16[128,384]{1,0:T(8,128)(2,1)S(1)} %get-tuple-element.123) | copy-start | bytes 294916
  188.2 219.7 %copy-start.33 = (bf16[128,384]{1,0:T(8,128)(2,1)}, bf16[128,384]{1,0:T(8,128)(2,1)S(1)}, u32[]{:S(2)}) copy-start(bf16[128,384]{1,0:T(8,128)(2,1)S(1)} %get-tuple-element.124) | copy-start | bytes 294916
  188.2 219.7 %copy-start.35 = (bf16[128,384]{1,0:T(8,128)(2,1)}, bf16[128,384]{1,0:T(8,128)(2,1)S(1)}, u32[]{:S(2)}) copy-start(bf16[128,384]{1,0:T(8,128)(2,1)S(1)} %get-tuple-element.125) | copy-start | bytes 294916
  409.2 222.3 %collective-permute-start.20 = (bf16[1120,768]{1,0:T(8,128)(2,1)}, bf16[1120,768]{1,0:T(8,128)(2,1)}, u32[]{:S(2)}, u32[]{:S(2)}) collective-permute-start(bf16[1120,768]{1,0:T(8,128)(2,1)} %get-tuple-element.67), channel_id=1, source_target_pairs={{0,16},{16,0},{1,17},{17,1},{2,18},{18,2},{3,19},{19,3},{4,20},{20... | collective-permute-start | bytes 5160968 | tf_op jit(solution)/shard_map/ppermute | solution.py:735
  411.1 220.5 %collective-permute-start.21 = (bf16[1120,768]{1,0:T(8,128)(2,1)}, bf16[1120,768]{1,0:T(8,128)(2,1)}, u32[]{:S(2)}, u32[]{:S(2)}) collective-permute-start(bf16[1120,768]{1,0:T(8,128)(2,1)} %get-tuple-element.68), channel_id=1, source_target_pairs={{0,16},{16,0},{1,17},{17,1},{2,18},{18,2},{3,19},{19,3},{4,20},{20... | collective-permute-start | bytes 5160968 | tf_op jit(solution)/shard_map/ppermute | solution.py:735
  411.3 220.3 %collective-permute-start.22 = (bf16[1120,768]{1,0:T(8,128)(2,1)}, bf16[1120,768]{1,0:T(8,128)(2,1)}, u32[]{:S(2)}, u32[]{:S(2)}) collective-permute-start(bf16[1120,768]{1,0:T(8,128)(2,1)} %get-tuple-element.69), channel_id=1, source_target_pairs={{0,16},{16,0},{1,17},{17,1},{2,18},{18,2},{3,19},{19,3},{4,20},{20... | collective-permute-start | bytes 5160968 | tf_op jit(solution)/shard_map/ppermute | solution.py:735
  451.0 132.2 %collective-permute-start.12 = (bf16[768,128]{0,1:T(8,128)(2,1)S(1)}, bf16[768,128]{0,1:T(8,128)(2,1)S(1)}, u32[]{:S(2)}, u32[]{:S(2)}) collective-permute-start(bf16[768,128]{0,1:T(8,128)(2,1)S(1)} %copy-done.26), channel_id=1, source_target_pairs={{0,16},{16,0},{1,17},{17,1},{2,18},{18,2},{3,19},{19,3},{4,20},{20... | collective-permute-start | bytes 589832 | tf_op jit(solution)/shard_map/ppermute | solution.py:735
  560.0 29.3 %collective-permute-start.17 = (bf16[384,768]{1,0:T(8,128)(2,1)}, bf16[384,768]{1,0:T(8,128)(2,1)}, u32[]{:S(2)}, u32[]{:S(2)}) collective-permute-start(bf16[384,768]{1,0:T(8,128)(2,1)} %convolution_convert_fusion.4), channel_id=1, source_target_pairs={{0,16},{16,0},{1,17},{17,1},{2,18},{18,2},{3,19},{19,3},{4,20},{20... | collective-permute-start | bytes 1769480 | tf_op jit(solution)/shard_map/ppermute | solution.py:735
  583.5 5.7 collective-permute-start.13
  589.3 11.8 %collective-permute-start.9 = (bf16[768,384]{1,0:T(8,128)(2,1)}, bf16[768,384]{1,0:T(8,128)(2,1)S(1)}, u32[]{:S(2)}, u32[]{:S(2)}) collective-permute-start(bf16[768,384]{1,0:T(8,128)(2,1)} %convolution_convert_fusion.5), channel_id=1, source_target_pairs={{0,16},{16,0},{1,17},{17,1},{2,18},{18,2},{3,19},{19,3},{4,20},{20... | collective-permute-start | bytes 1769480 | tf_op jit(solution)/shard_map/ppermute | solution.py:735
  589.4 8.8 %collective-permute-start.14 = (bf16[768,128]{0,1:T(8,128)(2,1)S(1)}, bf16[768,128]{0,1:T(8,128)(2,1)S(1)}, u32[]{:S(2)}, u32[]{:S(2)}) collective-permute-start(bf16[768,128]{0,1:T(8,128)(2,1)S(1)} %add_convert_fusion.7), channel_id=1, source_target_pairs={{0,8},{4,12},{8,0},{12,4},{1,9},{5,13},{9,1},{13,5},{2,10},{6,14},... | collective-permute-start | bytes 589832 | tf_op jit(solution)/shard_map/ppermute | solution.py:735
  598.2 16.3 %collective-permute-start.18 = (bf16[384,768]{1,0:T(8,128)(2,1)S(1)}, bf16[384,768]{1,0:T(8,128)(2,1)S(1)}, u32[]{:S(2)}, u32[]{:S(2)}) collective-permute-start(bf16[384,768]{1,0:T(8,128)(2,1)S(1)} %add_convert_fusion.4), channel_id=1, source_target_pairs={{0,4},{4,0},{8,12},{12,8},{1,5},{5,1},{9,13},{13,9},{2,6},{6,2},{1... | collective-permute-start | bytes 1769480 | tf_op jit(solution)/shard_map/ppermute | solution.py:735
  601.1 6.0 collective-permute-start.15
  607.1 17.5 %collective-permute-start.10 = (bf16[768,384]{1,0:T(8,128)(2,1)S(1)}, bf16[768,384]{1,0:T(8,128)(2,1)S(1)}, u32[]{:S(2)}, u32[]{:S(2)}) collective-permute-start(bf16[768,384]{1,0:T(8,128)(2,1)S(1)} %fusion.6), channel_id=1, source_target_pairs={{0,4},{4,0},{8,12},{12,8},{1,5},{5,1},{9,13},{13,9},{2,6},{6,2},{1... | collective-permute-start | bytes 1769480 | tf_op jit(solution)/shard_map/ppermute | solution.py:735
  614.5 11.6 %collective-permute-start.16 = (bf16[1536,128]{0,1:T(8,128)(2,1)S(1)}, bf16[1536,128]{0,1:T(8,128)(2,1)S(1)}, u32[]{:S(2)}, u32[]{:S(2)}) collective-permute-start(bf16[1536,128]{0,1:T(8,128)(2,1)S(1)} %pad_maximum_fusion.10), channel_id=1, source_target_pairs={{0,1},{1,0},{2,3},{3,2},{4,5},{5,4},{6,7},{7,6},{8,9},{9,8},{10,11... | collective-permute-start | bytes 1179656 | tf_op jit(solution)/shard_map/ppermute | solution.py:735
  624.6 39.5 %collective-permute-start.19 = (bf16[384,768]{1,0:T(8,128)(2,1)}, bf16[384,768]{1,0:T(8,128)(2,1)}, u32[]{:S(2)}, u32[]{:S(2)}) collective-permute-start(bf16[384,768]{1,0:T(8,128)(2,1)} %add_convert_fusion.3), channel_id=1, source_target_pairs={{0,8},{4,12},{8,0},{12,4},{1,9},{5,13},{9,1},{13,5},{2,10},{6,14},... | collective-permute-start | bytes 1769480 | tf_op jit(solution)/shard_map/ppermute | solution.py:735
  626.1 50.6 %collective-permute-start.11 = (bf16[768,384]{1,0:T(8,128)(2,1)}, bf16[768,384]{1,0:T(8,128)(2,1)}, u32[]{:S(2)}, u32[]{:S(2)}) collective-permute-start(bf16[768,384]{1,0:T(8,128)(2,1)} %add_convert_fusion.5), channel_id=1, source_target_pairs={{0,8},{4,12},{8,0},{12,4},{1,9},{5,13},{9,1},{13,5},{2,10},{6,14},... | collective-permute-start | bytes 1769480 | tf_op jit(solution)/shard_map/ppermute | solution.py:735
  633.6 65.7 %collective-permute-start.25 = (bf16[1120,768]{1,0:T(8,128)(2,1)S(1)}, bf16[1120,768]{1,0:T(8,128)(2,1)S(1)}, u32[]{:S(2)}, u32[]{:S(2)}) collective-permute-start(bf16[1120,768]{1,0:T(8,128)(2,1)S(1)} %add_convert_fusion), channel_id=1, source_target_pairs={{0,4},{4,0},{8,12},{12,8},{1,5},{5,1},{9,13},{13,9},{2,6},{6,2},{1... | collective-permute-start | bytes 5160968 | tf_op jit(solution)/shard_map/ppermute | solution.py:735
  636.1 100.1 %collective-permute-start.23 = (bf16[1120,768]{1,0:T(8,128)(2,1)S(1)}, bf16[1120,768]{1,0:T(8,128)(2,1)S(1)}, u32[]{:S(2)}, u32[]{:S(2)}) collective-permute-start(bf16[1120,768]{1,0:T(8,128)(2,1)S(1)} %add_convert_fusion.2), channel_id=1, source_target_pairs={{0,4},{4,0},{8,12},{12,8},{1,5},{5,1},{9,13},{13,9},{2,6},{6,2},{1... | collective-permute-start | bytes 5160968 | tf_op jit(solution)/shard_map/ppermute | solution.py:735
  639.9 129.2 %collective-permute-start.24 = (bf16[1120,768]{1,0:T(8,128)(2,1)S(1)}, bf16[1120,768]{1,0:T(8,128)(2,1)S(1)}, u32[]{:S(2)}, u32[]{:S(2)}) collective-permute-start(bf16[1120,768]{1,0:T(8,128)(2,1)S(1)} %add_convert_fusion.1), channel_id=1, source_target_pairs={{0,4},{4,0},{8,12},{12,8},{1,5},{5,1},{9,13},{13,9},{2,6},{6,2},{1... | collective-permute-start | bytes 5160968 | tf_op jit(solution)/shard_map/ppermute | solution.py:735
  739.5 32.9 %copy-start.6 = (bf16[4,128,1536]{2,1,0:T(8,128)(2,1)S(1)}, bf16[4,128,1536]{2,1,0:T(8,128)(2,1)}, u32[]{:S(2)}) copy-start(bf16[4,128,1536]{2,1,0:T(8,128)(2,1)} %final_outputs.1) | copy-start | bytes 4718596
  (44 other events, 546.6 us)

commit v4 on v3

--- a/solution.py
+++ b/solution.py
@@ -230,7 +230,7 @@
 
 def ffn_kernel(with_dx, pieces, meta_ref, x_ref, dy_ref, *refs):
     wg, wu, wd = (refs[m * pieces : (m + 1) * pieces] for m in range(3))
-    outs = refs[-4:] if with_dx else refs[-3:]
+    outs = refs[-5:] if with_dx else refs[-3:]
     hid_ref, dg_ref, du_ref = outs[:3]
     columns = [columns_of(meta_ref, j, wg[j].shape[1], pieces) for j in range(pieces)]
     gate = sum(dot_cols(x_ref[:, at], w[...]) for at, w in zip(columns, wg))
@@ -238,7 +238,8 @@
     grad_hidden = sum(dot_cols(dy_ref[:, at], w[...]) for at, w in zip(columns, wd))
     sigma = 1.0 / (1.0 + jnp.exp(-gate))
     gated = gate * sigma
-    hid_ref[...] = (gated * up).astype(bf16)
+    hidden = (gated * up).astype(bf16)
+    hid_ref[...] = hidden
     grad_gate = (grad_hidden * up * (sigma + gated * (1.0 - sigma))).astype(bf16)
     grad_up = (grad_hidden * gated).astype(bf16)
     dg_ref[...] = grad_gate
@@ -246,6 +247,8 @@
     if with_dx:
         for at, g, u in zip(columns, wg, wu):
             outs[3][:, at] = (dot(grad_gate, g[...]) + dot(grad_up, u[...])).astype(bf16)
+        for at, d in zip(columns, wd):
+            outs[4][:, at] = dot(hidden, d[...]).astype(bf16)
 
 
 def ffn(meta, normed, grad_out, weights, with_dx):
@@ -261,7 +264,7 @@
     weight = lambda w, k: pl.BlockSpec(
         (units, w.shape[1]), lambda i, m: (k, 0), pipeline_mode=pl.Buffered(1)
     )
-    widths = [units] * 3 + [width] * with_dx
+    widths = [units] * 3 + [width] * (2 * with_dx)
     return pl.pallas_call(
         functools.partial(ffn_kernel, with_dx, len(weights)),
         name="ffn_pair" if with_dx else "ffn_far",
@@ -276,7 +279,7 @@
     )(meta, flat(normed), flat(grad_out), *(list(weights) * 3))
 
 
-def unit_grads_kernel(meta_ref, x, y, hp, hf, gp, gf, up, uf, og, ou, od, ag, au, ad):
+def unit_grads_kernel(meta_ref, x, y, hp, hf, gp, gf, up, uf, og, oud, ag, au, ad):
     step = pl.program_id(0)
 
     @pl.when(step == 0)
@@ -294,9 +297,10 @@
 
     @pl.when(step == pl.num_programs(0) - 1)
     def _():
+        units = og.shape[0]
         og[...] = ag[...].astype(bf16)
-        ou[...] = au[...].astype(bf16)
-        od[...] = ad[...].astype(bf16)
+        oud[:units] = au[...].astype(bf16)
+        oud[units:] = ad[...].astype(bf16)
 
 
 def unit_grads(meta, which, pieces, x, y, hid, dg, du):
@@ -320,12 +324,12 @@
             grid=(2 * steps,),
             in_specs=[feature] * 2 + [unit(near), unit(far)] * 3,
             out_specs=[
-                pl.BlockSpec((units, depth), lambda i, m: (0, 0), pipeline_mode=pl.Buffered(1))
-            ]
-            * 3,
+                pl.BlockSpec((k * units, depth), lambda i, m: (0, 0), pipeline_mode=pl.Buffered(1))
+                for k in (1, 2)
+            ],
             scratch_shapes=[pltpu.VMEM((units, depth), f32)] * 3,
         ),
-        out_shape=[jax.ShapeDtypeStruct((units, depth), bf16)] * 3,
+        out_shape=[jax.ShapeDtypeStruct((k * units, depth), bf16) for k in (1, 2)],
         compiler_params=pltpu.CompilerParams(vmem_limit_bytes=VMEM_LIMIT),
     )(meta, x.reshape(-1, width), y.reshape(-1, width), *hid, *dg, *du)
 
@@ -415,6 +419,7 @@
     low, high = pl.ds(0, size), pl.ds(size, size)
     from_core = {j: wires.copy(part.at[4 + j], got_core.at[j], to["core"]) for j in (3, 1, 2, 0)}
     mine = wires.here(part.at[pl.ds(0, 4)], own)
+    yield
     mine.wait()
     both = lambda j, at: wide(own[j, at]) + wide(got_core[j, at])
     from_core[3].wait_recv()
@@ -427,17 +432,27 @@
     from_core[2].wait_recv()
     sent[1, low] = both(2, low).astype(bf16)
     z_low = wires.copy(sent.at[1, low], got_z.at[low], to["z"])
+    yield
     via_z.wait_recv()
     sent[0, low] = (both(1, low) + wide(diag_z[...])).astype(bf16)
     y_low = wires.copy(sent.at[0, low], got_y.at[low], to["y"])
     via_y.wait_recv()
     sent[1, high] = (both(2, high) + wide(diag_y[...])).astype(bf16)
     z_high = wires.copy(sent.at[1, high], got_z.at[high], to["z"])
+    yield
     from_core[0].wait_recv()
     total = wide(own[0]) + wide(got_core[0])
     for one in (y_high, z_low, y_low, z_high):
         one.wait_recv()
     return total + wide(got_y[...]) + wide(got_z[...])
+
+
+def result_of(steps):
+    while True:
+        try:
+            next(steps)
+        except StopIteration as done:
+            return done.value
 
 
 def gather_rank(wires, to, block, out, at):
@@ -446,6 +461,7 @@
     mine = wires.here(block, out.at[at(0, 0)])
     from_y = [wires.copy(block.at[h], out.at[at(0, 2), h], to["y"]) for h in halves]
     from_core = [wires.copy(block, out.at[at(0, 1)], to["core"])]
+    yield
     for h, one in zip(halves, from_y):
         one.wait_recv()
         from_core.append(wires.copy(out.at[at(2, 0), h], out.at[at(2, 1), h], to["core"]))
@@ -624,17 +640,39 @@
 MIXED = (0, 2, 1, 3)
 
 
-def middle_back_kernel(part, mid_ref, factor_ref, gain_ref, dy_ref, dmid_ref, dgain_ref, out, *rest):
-    low, rest = rest[0], rest[1:]
-    wires, to = Wires(*rest[-3:]), partners()
+def natural_place(t):
+    flip = lambda x, bit: x + bit * (1 - 2 * lax.rem(x // bit, 2))
+    return lambda j, _: t if j == 0 else flip(t, j)
+
+
+def middle_back_kernel(
+    part, out_part, mid_ref, factor_ref, gain_ref, dy_ref, dmid_ref, dgain_ref, out, outputs, *rest
+):
+    low, out_low, first, second, wires = rest[0], rest[1], rest[2:9], rest[9:16], Wires(*rest[16:])
+    to = partners()
     meet([to[k] for k in ("core", "y", "z")])
-    grad_normed = scatter_pair(wires, to, part, *rest[:-3])
+    back = scatter_pair(wires, to, part, *first)
+    ahead = scatter_pair(wires, to, out_part, *second)
+    next(back)
+    next(ahead)
+    next(back)
+    next(back)
+    next(ahead)
+    grad_normed = result_of(back)
     du, dgain = norm_back_rows(mid_ref[...], factor_ref[...], gain_ref[...], grad_normed)
     dgain_ref[...] = dgain
     dmid = wide(dy_ref[...]) + du
     dmid_ref[...] = dmid
     low[...] = dmid.astype(bf16)
-    gather_rank(wires, to, low, out, lambda j, flip: MIXED.index(j ^ flip))
+    share = gather_rank(wires, to, low, out, lambda j, flip: MIXED.index(j ^ flip))
+    next(share)
+    next(ahead)
+    out_low[...] = (mid_ref[...] + result_of(ahead)).astype(bf16)
+    place = natural_place(lax.axis_index("tensor"))
+    out_share = gather_rank(wires, to, out_low, outputs, place)
+    next(out_share)
+    result_of(share)
+    result_of(out_share)
     wires.finish()
 
 
@@ -650,71 +688,62 @@
     ]
 
 
-def middle_back(part, middle, factor, gain, dy_part):
+def middle_back(part, out_part, middle, factor, gain, dy_part):
     rows, width = middle.shape
     return remote_call(
         middle_back_kernel,
         "middle_back",
         3,
-        [part.reshape(8, rows, width), middle, factor, gain, dy_part],
+        [part.reshape(8, rows, width), out_part.reshape(8, rows, width)]
+        + [middle, factor, gain, dy_part],
         [
             jax.ShapeDtypeStruct((rows, width), f32),
             jax.ShapeDtypeStruct((1, width), f32),
             jax.ShapeDtypeStruct((4, rows, width), bf16),
+            jax.ShapeDtypeStruct((4, rows, width), bf16),
         ],
-        [pltpu.VMEM((rows, width), bf16)] + pair_scratch(rows, width),
-        16,
-        ([False, True, True, True, True], [True, True, False]),
+        [pltpu.VMEM((rows, width), bf16)] * 2 + pair_scratch(rows, width) * 2,
+        32,
+        ([False, False, True, True, True, True], [True, True, False, False]),
     )
 
 
-def outputs_kernel(part, mid_ref, out, low, *rest):
+def add_all(wires, ways, value, slots):
+    for k, device in enumerate(ways):
+        one = wires.copy(value, slots.at[k], device)
+        one.wait()
+        wires.started = [x for x in wires.started if x is not one]
+        value[...] = value[...] + slots[k]
+
+
+def input_back_kernel(
+    part, x_ref, factor_ref, gain_ref, dmid_ref, small_ref, sum_ref, out, *rest
+):
+    low, own, core, sent, got, slots = rest[:-3]
     wires, to = Wires(*rest[-3:]), partners()
-    t = lax.axis_index("tensor")
-    flip = lambda x, bit: x + bit * (1 - 2 * lax.rem(x // bit, 2))
-    meet([to[k] for k in ("core", "y", "z")])
-    low[...] = (mid_ref[...] + scatter_pair(wires, to, part, *rest[:-3])).astype(bf16)
-    gather_rank(wires, to, low, out, lambda j, _: t if j == 0 else flip(t, j))
-    wires.finish()
-
-
-def final_outputs(part, middle):
-    rows, width = middle.shape
-    return remote_call(
-        outputs_kernel,
-        "final_outputs",
-        4,
-        [part.reshape(8, rows, width), middle],
-        [jax.ShapeDtypeStruct((4, rows, width), bf16)],
-        [pltpu.VMEM((rows, width), bf16)] + pair_scratch(rows, width),
-        16,
-        ([False, True], [False]),
-    )[0].reshape(4 * rows, width)
-
-
-def input_back_kernel(part, x_ref, factor_ref, gain_ref, dmid_ref, dgain_ref, out, *rest):
-    low, own, core, sent, got = rest[:-3]
-    wires, to = Wires(*rest[-3:]), partners()
-    t = lax.axis_index("tensor")
-    flip = lambda x, bit: x + bit * (1 - 2 * lax.rem(x // bit, 2))
     meet([to[k] for k in ("core", "y")])
     grad_normed = scatter_rank(wires, to, part, own, core, sent, got)
     du, dgain = norm_back_rows(wide(x_ref[...]), factor_ref[...], gain_ref[...], grad_normed)
-    dgain_ref[...] = dgain
     low[...] = (dmid_ref[...] + du).astype(bf16)
-    gather_rank(wires, to, low, out, lambda j, _: t if j == 0 else flip(t, j))
+    share = gather_rank(wires, to, low, out, natural_place(lax.axis_index("tensor")))
+    next(share)
+    width = dgain.shape[1]
+    sum_ref[:, width:] = small_ref[:, width:]
+    sum_ref[:, :width] = dgain
+    add_all(wires, [to["core"], to["y"]], sum_ref, slots)
+    result_of(share)
     wires.finish()
 
 
-def input_back(part, inputs_part, factor, gain, grad_middle):
+def input_back(part, inputs_part, factor, gain, grad_middle, small):
     rows, width = inputs_part.shape
     return remote_call(
         input_back_kernel,
         "input_back",
         5,
-        [part.reshape(4, rows, width), inputs_part, factor, gain, grad_middle],
+        [part.reshape(4, rows, width), inputs_part, factor, gain, grad_middle, small],
         [
-            jax.ShapeDtypeStruct((1, width), f32),
+            jax.ShapeDtypeStruct(small.shape, f32),
             jax.ShapeDtypeStruct((4, rows, width), bf16),
         ],
         [
@@ -723,9 +752,74 @@
             pltpu.VMEM((2, rows, width), bf16),
             pltpu.VMEM((rows, width), bf16),
             pltpu.VMEM((rows, width), bf16),
+            pltpu.VMEM((2,) + small.shape, f32),
         ],
         16,
-        ([False, True, True, True, True], [True, False]),
+        ([False, True, True, True, True, True], [True, False]),
+    )
+
+
+def context_sum_kernel(over_f, *refs):
+    (parts, refs), (small_ref, refs) = (refs[:3], refs[3:]), (refs[3], refs[4:])
+    (outs, refs), (sum_ref, shared, refs) = (refs[:3], refs[3:]), (refs[3], refs[4], refs[5:])
+    gots, slots, wires = refs[:3], refs[3], Wires(*refs[4:])
+    to, c = partners(), lax.axis_index("context")
+    ways = ((1, "z"), (2, "far"), (3, "last"))
+    greet = ["core", "y", "z", "far", "last"]
+    flip = lambda x, bit: x + bit * (1 - 2 * lax.rem(x // bit, 2))
+    if over_f:
+        to["f"] = {"fsdp": 1 - lax.axis_index("fsdp")}
+        greet.append("f")
+    meet([to[k] for k in greet])
+    rank = {1: flip(c, 1), 2: flip(c, 2), 3: flip(flip(c, 1), 2)}
+    arrive = []
+    order = (2, 0, 1)
+    quarter = lambda ref, k: pl.ds(
+        pl.multiple_of(k * (ref.shape[0] // 4), ref.shape[0] // 4), ref.shape[0] // 4
+    )
+    for i in order:
+        part, got = parts[i], gots[i]
+        arrive.append(
+            [
+                wires.copy(part.at[quarter(part, rank[j])], got.at[j - 1], to[way])
+                for j, way in ways
+            ]
+        )
+    sum_ref[...] = small_ref[...]
+    sent = []
+    for i, copies in zip(order, arrive):
+        part, got, out = parts[i], gots[i], outs[i]
+        for one in copies:
+            one.wait_recv()
+        at = quarter(part, c)
+        out[at] = (
+            wide(part[at]) + wide(got[0]) + wide(got[1]) + wide(got[2])
+        ).astype(bf16)
+        sent.append([wires.copy(out.at[at], out.at[at], to[way]) for _, way in ways])
+    add_all(wires, [to[k] for k in (("f",) if over_f else ()) + ("z", "far")], sum_ref, slots)
+    for one in sent[0]:
+        one.wait_recv()
+    share = gather_rank(wires, to, outs[2], shared, natural_place(lax.axis_index("tensor")))
+    next(share)
+    for one in sent[1] + sent[2]:
+        one.wait_recv()
+    result_of(share)
+    wires.finish()
+
+
+def context_sum(over_f, parts, small):
+    shape = lambda x: jax.ShapeDtypeStruct(x.shape, x.dtype)
+    return remote_call(
+        functools.partial(context_sum_kernel, over_f),
+        "context_sum",
+        6,
+        [*parts, small],
+        [shape(x) for x in parts]
+        + [shape(small), jax.ShapeDtypeStruct((4,) + parts[2].shape, bf16)],
+        [pltpu.VMEM((3, x.shape[0] // 4, x.shape[1]), bf16) for x in parts]
+        + [pltpu.VMEM((3,) + small.shape, f32)],
+        32,
+        ([True] * 4, [True] * 4 + [False]),
     )
 
 
@@ -740,6 +834,9 @@
             jnp.concatenate([x, other], axis=axis),
             jnp.concatenate([other, x], axis=axis),
         )
+
+    def after(x, *others):
+        return lax.optimization_barrier((x, others))[0]
 
     def local(
         inputs,
@@ -791,12 +888,6 @@
                 dot_rows(left, right).astype(bf16), "fsdp", scatter_dimension=side, tiled=True
             ).astype(f32)
 
-        def sum_c(x):
-            for bit in (1, 2):
-                low = x.astype(bf16)
-                x = low.astype(f32) + flip(low, "context", bit).astype(f32)
-            return x
-
         order = MIXED
 
         def mixed(x):
@@ -815,9 +906,6 @@
 
         def grow(x, axis, bit):
             return jnp.concatenate([x, flip(x, axis, bit)], axis=0)
-
-        def gather_t(x):
-            return grow(grow(x, "tensor", 2), "tensor", 1)
 
         small = jnp.concatenate(
             [v.reshape(1, -1) for v in (attn_gain, ffn_gain, b_query, b_key, b_value)], axis=1
@@ -850,9 +938,8 @@
         b_kv = lax.dynamic_index_in_dim(jnp.where(core == 0, bk, bv), group, 0)
 
         unit_slice = lambda w: lax.dynamic_slice_in_dim(w, parity * units, units, 0)
-        w_units = pieces_f(
-            jnp.concatenate([unit_slice(w) for w in (w_gate.T, w_up.T, w_down)], axis=0), 1
-        )
+        own_units = jnp.concatenate([unit_slice(w) for w in (w_gate.T, w_up.T, w_down)], axis=0)
+        w_units = pieces_f(after(own_units, w_qkv, small), 1)
 
         dy_own = mixed(cotangent)[: 2 * part]
         dy_near = jnp.concatenate([dy_own, flip(dy_own, "context", 1)], axis=0)
@@ -882,13 +969,14 @@
         )
 
         normed2 = normed2.reshape(2, -1, part, width)
-        hid_pair, dg_pair, du_pair, dx_part = ffn(meta, normed2, dy_all, w_units, True)
-        hid_far, dg_far, du_far = ffn(meta, normed2, dy_all, w_units, False)
+        hid_pair, dg_pair, du_pair, dx_part, out_part = ffn(meta, normed2, dy_all, w_units, True)
+        hid_far, dg_far, du_far = ffn(meta, after(normed2, dx_part), dy_all, w_units, False)
         grad_args = (normed2, dy_all, (hid_pair, hid_far), (dg_pair, dg_far), (du_pair, du_far))
         if n_f == 2:
             unit_sent = unit_grads(meta, 1, 2, *grad_args)
             unit_got = [flip(x, "fsdp", 1) for x in unit_sent]
-            dx_part, _ = lax.optimization_barrier((dx_part, unit_sent))
+            unit_own = unit_grads(meta, 0, 2, *after(grad_args, unit_sent))
+            dx_part = after(dx_part, unit_own)
         else:
             unit_own = [
                 lax.psum_scatter(x, "fsdp", scatter_dimension=1, tiled=True)
@@ -896,64 +984,58 @@
             ]
             unit_got = [jnp.zeros_like(x) for x in unit_own]
 
-        def unit_done(own, got):
-            low = (own.astype(f32) + got.astype(f32)).astype(bf16)
-            return by_bit(parity, low, flip(low, "context", 1), 0).astype(f32)
+        unit_sum = lambda own, got: (own.astype(f32) + got.astype(f32)).astype(bf16)
+        unit_whole = lambda low, other: by_bit(parity, low, other, 0).astype(f32)
 
         dy_part = lax.dynamic_slice_in_dim(cotangent, t * part, part, 0)
-        grad_middle, ffn_gain_grad, grad_middle_low = middle_back(
-            dx_part, middle, factor_second, gain_second, dy_part
-        )
+        grad_middle, ffn_gain_grad, grad_middle_low, outputs = middle_back(
+            dx_part, out_part, middle, factor_second, gain_second, dy_part
+        )
+        outputs = outputs.reshape(rows, width)
         grad_middle_low = grad_middle_low.reshape(rows, width)
-        wo_grad = sum_c(grad_f(attended_mixed, grad_middle_low, 1))
-        grad_attended = natural(dot_cols(grad_middle_low, w_out_all).astype(bf16))
+        unit_low = [unit_sum(unit_own[0], after(unit_got[0], grad_middle_low))]
+        unit_other = [flip(unit_low[0], "context", 1)]
+        grad_attended = natural(
+            dot_cols(after(grad_middle_low, unit_low), w_out_all).astype(bf16)
+        )
 
         dq_low, dkv = attention_back(key_blocks, queries, grad_attended, lse, cosine, sine, kv)
         dkv = kv_scatter(dkv)
-        if n_f == 2:
-            late_args, _ = lax.optimization_barrier((grad_args, dkv))
-            unit_own = unit_grads(meta, 0, 2, *late_args)
-            unit_got, _ = lax.optimization_barrier((unit_got, dkv))
+        unit_low.append(unit_sum(unit_own[1], after(unit_got[1], dkv)))
+        unit_other.append(flip(unit_low[1], "context", 1))
+        wo_part = grad_f(attended_mixed, after(grad_middle_low, dkv), 1).astype(bf16)
         dkv_low = jnp.where(core == 0, rotate_back(dkv, cosine, sine), dkv).astype(bf16)
-        wq_grad = sum_c(grad_f(normed, dq_low, 0))
-        wkv_own = sum_c(grad_f(normed, dkv_low, 0)).astype(bf16)
-        wkv_stack = gather_t(wkv_own)
-        depth = wkv_own.shape[0]
-        wkv_of = [wkv_stack[order.index(j) * depth : (order.index(j) + 1) * depth] for j in range(n_t)]
-        wkv_stack = jnp.stack(wkv_of)
-        wkv_rank = [
-            lax.dynamic_index_in_dim(wkv_stack, n ^ t, 0, keepdims=False).astype(f32)
-            for n in range(n_t)
-        ]
-        wk_grad = jnp.concatenate(wkv_rank[0::2], axis=1)
-        wv_grad = jnp.concatenate(wkv_rank[1::2], axis=1)
-
+        wq_part = grad_f(normed, dq_low, 0).astype(bf16)
+        wkv_part = grad_f(normed, dkv_low, 0).astype(bf16)
         d_qkv = mixed(jnp.concatenate([dq_low, dkv_low], axis=1))
         factor_part = lax.dynamic_slice_in_dim(factor_first, t * part, part, 0)
-        attn_gain_grad, input_grad = input_back(
+        own_biases = jnp.sum(
+            jnp.concatenate([dq_low, dkv_low], axis=1).astype(f32), axis=0, keepdims=True
+        )
+        slots = lax.dynamic_update_slice(
+            jnp.zeros((n_t, (heads + 1) * HD), f32), own_biases, (t, 0)
+        )
+        small_grads = jnp.concatenate(
+            [jnp.zeros((1, width), f32), ffn_gain_grad, slots.reshape(1, -1)], axis=1
+        )
+        small_grads, input_grad = input_back(
             columns_f([dot_cols(d_qkv, w) for w in w_qkv]),
             inputs_part,
             factor_part,
             gain_first,
             grad_middle,
+            small_grads,
         )
         input_grad = input_grad.reshape(rows, width)
-        outputs = final_outputs(
-            columns_f([dot(hid_pair, w[2 * units :]) for w in w_units]), middle
-        )
-        wg_grad, wu_grad, wd_grad = (unit_done(a, b) for a, b in zip(unit_own, unit_got))
-        wg_grad, wu_grad = wg_grad.T, wu_grad.T
-
-        bq_grad = jnp.sum(dq_low.astype(f32), axis=0)
-        bkv_grad = jnp.sum(dkv_low.astype(f32), axis=0)
-        slots = jnp.zeros((n_t, (heads + 1) * HD), f32)
-        slots = lax.dynamic_update_slice(
-            slots, jnp.concatenate([bq_grad, bkv_grad])[None], (t, 0)
-        )
-        packed = lax.psum(
-            jnp.concatenate([attn_gain_grad[0], ffn_gain_grad[0], slots.reshape(-1)]),
-            ("fsdp", "context", "tensor"),
-        )
+        if n_f > 2:
+            small_grads = lax.psum(small_grads, "fsdp")
+        wo_grad, wq_grad, _, packed, wkv_all = context_sum(
+            n_f == 2, (wo_part, wq_part, wkv_part), small_grads
+        )
+        wo_grad, wq_grad, wkv_all = (x.astype(f32) for x in (wo_grad, wq_grad, wkv_all))
+        wk_grad = jnp.concatenate([wkv_all[0], wkv_all[2]], axis=1)
+        wv_grad = jnp.concatenate([wkv_all[1], wkv_all[3]], axis=1)
+        packed = packed[0]
         attn_gain_grad = lax.dynamic_slice_in_dim(packed, f * piece, piece, 0)
         ffn_gain_grad = lax.dynamic_slice_in_dim(packed, width + f * piece, piece, 0)
         slots = packed[2 * width :].reshape(n_t, heads + 1, HD)
@@ -961,6 +1043,14 @@
         bq_out = lax.dynamic_index_in_dim(slots, t, 0, keepdims=False)[:heads]
         bk_out = slots[0::2, heads]
         bv_out = slots[1::2, heads]
+
+        shares = [
+            (low[k : k + units], other[k : k + units])
+            for low, other in zip(unit_low, unit_other)
+            for k in range(0, low.shape[0], units)
+        ]
+        wg_grad, wu_grad, wd_grad = (unit_whole(*share) for share in shares)
+        wg_grad, wu_grad = wg_grad.T, wu_grad.T
 
         return (
             outputs,

time: 784 us -> 612 us (0.78)
  waiting for transfers between devices: 261 us -> 79.5 us
  Pallas kernels: 304 us -> 406 us
  blocking collectives: 76.9 us -> 0 us
  starting transfers between devices: 28 us -> 18.3 us
    ppermute x26 -> x16, waiting for transfers between devices: 261 us -> 79.5 us  [flip(): return lax.ppermute(x, axis, [(i, i ^ bit) for i in range(size)])]
    pallas_call x6, Pallas kernels: 184 us -> 281 us  [remote_call(): pl.pallas_call(kernel, name=name, out_shape=outs, in_specs=[spec(x) for x...]
    psum x1 -> x0, blocking collectives: 76.9 us -> none  [local(): lax.psum(jnp.concatenate([attn_gain_grad[0], ffn_gain_grad[0], slots.resh...]
    ppermute x26 -> x16, starting transfers between devices: 28 us -> 18.3 us  [flip(): return lax.ppermute(x, axis, [(i, i ^ bit) for i in range(size)])]
    dot_general x3 -> x1, matrix products: 12.1 us -> 3.82 us  [dot(): return jnp.dot(left, right, preferred_element_type=f32)]
    unnamed x113 -> x71, local copies, waits for them, and re-layouts: 20.3 us -> 16.7 us
  transfers between devices with their start and end apart: 26 -> 16, of which waited for: 14 -> 4; matrix products, arithmetic and copies ran while one was open for 9% -> 13% of each run, Pallas kernels for 22% -> 55%
where the time goes in v4:
time: 612 us; the launch traced here: 605 us
  Pallas kernels  406 us (66%)
  waiting for transfers between devices  79.5 us (13%)
  other arithmetic  43.7 us (7%)
  local copies, waits for them, and re-layouts  36 us (6%)
  matrix products  19.8 us (3%)
  starting transfers between devices  18.3 us (3%)
    pallas_call x6, Pallas kernels, remote_call(): pl.pallas_call(kernel, name=name, out_shape=outs, in_specs=[spec(x) for x...  281 us
    ppermute x16, waiting for transfers between devices, flip(): return lax.ppermute(x, axis, [(i, i ^ bit) for i in range(size)])  79.5 us
    pallas_call x2, Pallas kernels, ffn(): pl.pallas_call(functools.partial(ffn_kernel, with_dx, len(weights)), name...  54.3 us
    pallas_call x2, Pallas kernels, unit_grads(): pl.pallas_call(unit_grads_kernel, name=f'unit_grads_{which}', grid_spec=p...  39.9 us
    ppermute x16, starting transfers between devices, flip(): return lax.ppermute(x, axis, [(i, i ^ bit) for i in range(size)])  18.3 us
    unnamed x71, local copies, waits for them, and re-layouts  16.7 us
    pallas_call x1, Pallas kernels, attention_back(): pl.pallas_call(functools.partial(attention_back_kernel, kv.shape[1] // BL...  15.2 us
  transfers between devices with their start and end apart: 16, of which 4 were waited for; matrix products, arithmetic and copies ran while one was open for 13% of the time, Pallas kernels for 55%

profile of v4, /device:TPU:0, one launch (start us, length us, event | category | flops | bytes accessed | tf_op | source)
XLA Modules:
  0.0 604.5 jit_solution(12221559895616439224)
XLA Ops:
  4.7 3.0 collective-permute-start
  15.1 2.6 pad_maximum_fusion.refs_0_.refs_2_.refs_4_
  17.8 12.9 %collective-permute-done.1.refs_1_ = bf16[768,512]{1,0:T(8,128)(2,1)} collective-permute-done((bf16[768,512]{1,0:T(8,128)(2,1)}, bf16[768,512]{1,0:T(8,128)(2,1)}, u32[]{:S(2)}, u32[]{:S(2)}) %collective-permute-start.1) | collective-permute-done | bytes 786464 | tf_op jit(solution)/shard_map/ppermute | solution.py:829
  35.7 2.8 collective-permute-start.5
  47.3 24.6 %collective-permute-done.5 = bf16[256,1536]{1,0:T(8,128)(2,1)S(1)} collective-permute-done((bf16[256,1536]{1,0:T(8,128)(2,1)}, bf16[256,1536]{1,0:T(8,128)(2,1)S(1)}, u32[]{:S(2)}, u32[]{:S(2)}) %collective-permute-start.5) | collective-permute-done | bytes 786464 | tf_op jit(solution)/shard_map/ppermute | solution.py:829
  74.3 16.0 %collective-permute-done.6 = bf16[256,1536]{1,0:T(8,128)(2,1)S(1)} collective-permute-done((bf16[256,1536]{1,0:T(8,128)(2,1)S(1)}, bf16[256,1536]{1,0:T(8,128)(2,1)S(1)}, u32[]{:S(2)}, u32[]{:S(2)}) %collective-permute-start.6) | collective-permute-done | bytes 786464 | tf_op jit(solution)/shard_map/ppermute | solution.py:829
  93.8 5.6 qkv.1
  99.4 18.9 %kv_gather.1.k_ref.v_ref = bf16[2,2048,128]{2,1,0:T(8,128)(2,1)} custom-call(bf16[512,128]{1,0:T(8,128)(2,1)} %get-tuple-element.63.own_ref), custom_call_target="tpu_custom_call" | custom-call | tf_op jit(solution)/shard_map/kv_gather/pallas_call | solution.py:495
  118.4 10.2 %attention.1 = (bf16[512,384]{1,0:T(8,128)(2,1)}, f32[3,512,1]{2,1,0:T(8,128)}) custom-call(s32[8]{0:T(128)} %pad_add_fusion.1.kb_ref, bf16[512,384]{1,0:T(8,128)(2,1)} %get-tuple-element.62.q_ref, bf16[2,2048,128]{2,1,0:T(8,128)(2,1)} %kv_gather.1.k_ref.v_ref, bf16[2,2048,128]{2,1,0:T(8,128)(2,1)} %kv_gather.1.k_ref.v_ref), custom_call_target="tpu_custom_call" | custom-call | tf_op jit(solution)/shard_map/attention/pallas_call | solution.py:85
  129.6 25.9 %collective-permute-done.2 = bf16[384,768]{1,0:T(8,128)(2,1)} collective-permute-done((bf16[384,768]{1,0:T(8,128)(2,1)}, bf16[384,768]{1,0:T(8,128)(2,1)}, u32[]{:S(2)}, u32[]{:S(2)}) %collective-permute-start.2) | collective-permute-done | bytes 589856 | tf_op jit(solution)/shard_map/ppermute | solution.py:829
  155.5 3.8 convolution_convert_fusion
  159.3 59.7 %middle_norm.1 = (f32[128,1536]{1,0:T(8,128)}, f32[128,1]{1,0:T(8,128)}, bf16[16,128,1536]{2,1,0:T(8,128)(2,1)}) custom-call(bf16[4,128,1536]{2,1,0:T(8,128)(2,1)} %bitcast.98, bf16[128,1536]{1,0:T(8,128)(2,1)} %constant_dynamic-slice_fusion.8.x_ref, f32[1,1536]{1,0:T(1,128)} %bitcast.104), custom_call_target="tpu_custom_call" | custom-call | tf_op jit(solution)/shard_map/middle_norm/pallas_call | solution.py:495
  220.0 2.7 constant_dynamic-update-slice_fusion.3
  224.6 2.7 constant_dynamic-update-slice_fusion.dy_ref.y
  227.2 34.1 %ffn_pair.1 = (bf16[1024,1120]{1,0:T(8,128)(2,1)}, bf16[1024,1120]{1,0:T(8,128)(2,1)}, bf16[1024,1120]{1,0:T(8,128)(2,1)}, bf16[1024,1536]{1,0:T(8,128)(2,1)}, bf16[1024,1536]{1,0:T(8,128)(2,1)}) custom-call(s32[4]{0:T(128)} %pad_add_fusion.meta_ref, bf16[2048,1536]{1,0:T(8,128)(2,1)} %bitcast.90, ...), custom_call_target="tpu_custom_call" | custom-call | tf_op jit(solution)/shard_map/ffn_pair/pallas_call | solution.py:268
  261.4 20.1 %ffn_far.1 = (bf16[1024,1120]{1,0:T(8,128)(2,1)}, bf16[1024,1120]{1,0:T(8,128)(2,1)}, bf16[1024,1120]{1,0:T(8,128)(2,1)}) custom-call(s32[4]{0:T(128)} %pad_add_fusion.meta_ref, bf16[2048,1536]{1,0:T(8,128)(2,1)} %bitcast.91, bf16[2048,1536]{1,0:T(8,128)(2,1)} %constant_dynamic-update-slice_fusion.dy_ref.y, ...), custom_call_target="tpu_custom_call" | custom-call | tf_op jit(solution)/shard_map/ffn_far/pallas_call | solution.py:268
  281.5 19.9 %unit_grads_1.1 = (bf16[1120,768]{1,0:T(8,128)(2,1)}, bf16[2240,768]{1,0:T(8,128)(2,1)}) custom-call(s32[4]{0:T(128)} %pad_add_fusion.meta_ref, bf16[2048,1536]{1,0:T(8,128)(2,1)} %bitcast.92, bf16[2048,1536]{1,0:T(8,128)(2,1)} %constant_dynamic-update-slice_fusion.dy_ref.y, bf16[1024,1120]{1,0:T(8,128)(2,1)} %get-tuple-element.79.hp, ...), custom_call_target="tpu_custom_call" | custom-call | tf_op jit(solution)/shard_map/unit_grads_1/pallas_call | solution.py:319
  304.8 20.0 %unit_grads_0.1 = (bf16[1120,768]{1,0:T(8,128)(2,1)}, bf16[2240,768]{1,0:T(8,128)(2,1)}) custom-call(s32[4]{0:T(128)} %pad_add_fusion.meta_ref, bf16[2048,1536]{1,0:T(8,128)(2,1)} %bitcast.93, bf16[2048,1536]{1,0:T(8,128)(2,1)} %bitcast.18.y, bf16[1024,1120]{1,0:T(8,128)(2,1)} %get-tuple-element.79.hp, bf16[1024,1120]{1,0:T(8,128)(2,1)} %get-tuple-element.80.hf, ...), custom_call_target="tpu_custom_call" | custom-call | tf_op jit(solution)/shard_map/unit_grads_0/pallas_call | solution.py:319
  324.8 52.6 %middle_back.1 = (f32[128,1536]{1,0:T(8,128)}, f32[1,1536]{1,0:T(1,128)}, bf16[4,128,1536]{2,1,0:T(8,128)(2,1)}, bf16[4,128,1536]{2,1,0:T(8,128)(2,1)}) custom-call(bf16[8,128,1536]{2,1,0:T(8,128)(2,1)} %bitcast.94, bf16[8,128,1536]{2,1,0:T(8,128)(2,1)} %bitcast.95, f32[128,1536]{1,0:T(8,128)} %get-tuple-element.89.mid_ref, ...), custom_call_target="tpu_custom_call" | custom-call | tf_op jit(solution)/shard_map/middle_back/pallas_call | solution.py:495
  377.5 3.2 add_convert_fusion.1
  382.5 2.7 convolution_convert_fusion.5
  386.2 15.2 %attention_back.1 = (bf16[512,384]{1,0:T(8,128)(2,1)}, bf16[2,2048,128]{2,1,0:T(8,128)(2,1)}) custom-call(s32[8]{0:T(128)} %pad_add_fusion.1.kb_ref, bf16[512,384]{1,0:T(8,128)(2,1)} %get-tuple-element.62.q_ref, bf16[512,384]{1,0:T(8,128)(2,1)} %pad_maximum_fusion.11.do_ref, f32[3,512,1]{2,1,0:T(8,128)} %get-tuple-element.95.lse_ref, ...), custom_call_target="tpu_custom_call" | custom-call | tf_op jit(solution)/shard_map/attention_back/pallas_call | solution.py:151
  401.4 28.8 %kv_scatter.1 = f32[512,128]{1,0:T(8,128)} custom-call(bf16[2,2048,128]{2,1,0:T(8,128)(2,1)} %get-tuple-element.97.part_ref), custom_call_target="tpu_custom_call" | custom-call | tf_op jit(solution)/shard_map/kv_scatter/pallas_call | solution.py:495
  442.2 3.0 add_convert_fusion
  448.6 27.2 %input_back.1 = (f32[1,5120]{1,0:T(1,128)}, bf16[4,128,1536]{2,1,0:T(8,128)(2,1)}) custom-call(bf16[4,128,1536]{2,1,0:T(8,128)(2,1)} %maximum_select_fusion.3.part, bf16[128,1536]{1,0:T(8,128)(2,1)} %constant_dynamic-slice_fusion.8.x_ref, f32[128,1]{1,0:T(8,128)} %constant_dynamic-slice_fusion.4.factor_ref, f32[1,1536]{1,0:T(1,128)} %bitcast.103, ...), custom_call_target="tpu_custom_call" | custom-call | tf_op jit(solution)/shard_map/input_back/pallas_call | solution.py:495
  475.9 2.4 fusion.2.refs_2_
  478.2 2.8 add_convert_fusion.2.refs_0_
  481.0 2.5 fusion.1.refs_1_
  483.5 93.3 %context_sum.1 = (bf16[384,768]{1,0:T(8,128)(2,1)}, bf16[768,384]{1,0:T(8,128)(2,1)}, bf16[768,128]{1,0:T(8,128)(2,1)}, f32[1,5120]{1,0:T(1,128)}, bf16[4,768,128]{2,1,0:T(8,128)(2,1)}) custom-call(bf16[384,768]{1,0:T(8,128)(2,1)} %add_convert_fusion.2.refs_0_, bf16[768,384]{1,0:T(8,128)(2,1)} %fusion.1.refs_1_, bf16[768,128]{1,0:T(8,128)(2,1)} %fusion.2.refs_2_, ...), custom_call_target="tpu_custom_call" | custom-call | tf_op jit(solution)/shard_map/context_sum/pallas_call | solution.py:495
  586.6 5.4 convert_bitcast_fusion.1
  594.4 3.3 fusion
  597.7 3.2 convert_bitcast_fusion
  (168 shorter events, 71.9 us)
Async XLA Ops:
  0.6 10.8 %copy-start = (bf16[2240,768]{1,0:T(8,128)(2,1)S(1)}, bf16[2240,768]{1,0:T(8,128)(2,1)}, u32[]{:S(2)}) copy-start(bf16[2240,768]{1,0:T(8,128)(2,1)} %param.29) | copy-start | bytes 10321924
  4.7 13.1 %collective-permute-start = (bf16[1,1984]{1,0:T(2,128)(2,1)S(1)}, bf16[1,1984]{1,0:T(2,128)(2,1)S(1)}, u32[]{:S(2)}, u32[]{:S(2)}) collective-permute-start(bf16[1,1984]{1,0:T(2,128)(2,1)S(1)} %concatenate.103), channel_id=1, source_target_pairs={{0,16},{16,0},{1,17},{17,1},{2,18},{18,2},{3,19},{19,3},{4,20},{20... | collective-permute-start | bytes 11912 | tf_op jit(solution)/shard_map/ppermute | solution.py:829
  11.4 19.3 %collective-permute-start.1 = (bf16[768,512]{1,0:T(8,128)(2,1)}, bf16[768,512]{1,0:T(8,128)(2,1)}, u32[]{:S(2)}, u32[]{:S(2)}) collective-permute-start(bf16[768,512]{1,0:T(8,128)(2,1)} %pad_maximum_fusion.4.refs_0_), channel_id=1, source_target_pairs={{0,16},{16,0},{1,17},{17,1},{2,18},{18,2},{3,19},{19,3},{4,20},{20... | collective-permute-start | bytes 2359304 | tf_op jit(solution)/shard_map/ppermute | solution.py:829
  17.8 24.3 %copy-start.28 = (s32[1,8]{1,0:T(1,128)S(1)}, s32[1,8]{1,0:T(1,128)}, u32[]{:S(2)}) copy-start(s32[1,8]{1,0:T(1,128)} %param.17) | copy-start | bytes 100
  30.7 196.5 %collective-permute-start.8 = (bf16[3360,768]{1,0:T(8,128)(2,1)}, bf16[3360,768]{1,0:T(8,128)(2,1)}, u32[]{:S(2)}, u32[]{:S(2)}) collective-permute-start(bf16[3360,768]{1,0:T(8,128)(2,1)} %pad_maximum_fusion.refs_0_.refs_2_.refs_4_), channel_id=1, source_target_pairs={{0,16},{16,0},{1,17},{17,1},{2,18},{18,2},{3,19},{19,3},{4,20},{20... | collective-permute-start | bytes 15482888 | tf_op jit(solution)/shard_map/ppermute | solution.py:829
  32.9 40.2 %copy-start.2 = (bf16[128,1536]{1,0:T(8,128)(2,1)}, bf16[128,1536]{1,0:T(8,128)(2,1)S(1)}, u32[]{:S(2)}) copy-start(bf16[128,1536]{1,0:T(8,128)(2,1)S(1)} %get-tuple-element.115.dy_ref) | copy-start | bytes 1179652
  35.7 36.2 %collective-permute-start.5 = (bf16[256,1536]{1,0:T(8,128)(2,1)}, bf16[256,1536]{1,0:T(8,128)(2,1)S(1)}, u32[]{:S(2)}, u32[]{:S(2)}) collective-permute-start(bf16[256,1536]{1,0:T(8,128)(2,1)} %pad_maximum_fusion.5), channel_id=1, source_target_pairs={{0,8},{4,12},{8,0},{12,4},{1,9},{5,13},{9,1},{13,5},{2,10},{6,14},... | collective-permute-start | bytes 2359304 | tf_op jit(solution)/shard_map/ppermute | solution.py:829
  38.5 34.6 %collective-permute-start.3 = (bf16[256,1536]{1,0:T(8,128)(2,1)}, bf16[256,1536]{1,0:T(8,128)(2,1)S(1)}, u32[]{:S(2)}, u32[]{:S(2)}) collective-permute-start(bf16[256,1536]{1,0:T(8,128)(2,1)} %pad_maximum_fusion.5), channel_id=1, source_target_pairs={{0,4},{4,0},{8,12},{12,8},{1,5},{5,1},{9,13},{13,9},{2,6},{6,2},{1... | collective-permute-start | bytes 2359304 | tf_op jit(solution)/shard_map/ppermute | solution.py:829
  40.1 115.4 %collective-permute-start.2 = (bf16[384,768]{1,0:T(8,128)(2,1)}, bf16[384,768]{1,0:T(8,128)(2,1)}, u32[]{:S(2)}, u32[]{:S(2)}) collective-permute-start(bf16[384,768]{1,0:T(8,128)(2,1)} %param.25), channel_id=1, source_target_pairs={{0,16},{16,0},{1,17},{17,1},{2,18},{18,2},{3,19},{19,3},{4,20},{20... | collective-permute-start | bytes 1769480 | tf_op jit(solution)/shard_map/ppermute | solution.py:829
  71.9 18.4 %collective-permute-start.6 = (bf16[256,1536]{1,0:T(8,128)(2,1)S(1)}, bf16[256,1536]{1,0:T(8,128)(2,1)S(1)}, u32[]{:S(2)}, u32[]{:S(2)}) collective-permute-start(bf16[256,1536]{1,0:T(8,128)(2,1)S(1)} %collective-permute-done.5), channel_id=1, source_target_pairs={{0,4},{4,0},{8,12},{12,8},{1,5},{5,1},{9,13},{13,9},{2,6},{6,2},{1... | collective-permute-start | bytes 2359304 | tf_op jit(solution)/shard_map/ppermute | solution.py:829
  74.3 145.7 %collective-permute-start.4 = (bf16[512,1536]{1,0:T(8,128)(2,1)}, bf16[512,1536]{1,0:T(8,128)(2,1)}, u32[]{:S(2)}, u32[]{:S(2)}) collective-permute-start(bf16[512,1536]{1,0:T(8,128)(2,1)} %pad_maximum_fusion.1), channel_id=1, source_target_pairs={{0,1},{1,0},{2,3},{3,2},{4,5},{5,4},{6,7},{7,6},{8,9},{9,8},{10,11... | collective-permute-start | bytes 4718600 | tf_op jit(solution)/shard_map/ppermute | solution.py:829
  91.6 132.9 %collective-permute-start.7 = (bf16[512,1536]{1,0:T(8,128)(2,1)}, bf16[512,1536]{1,0:T(8,128)(2,1)}, u32[]{:S(2)}, u32[]{:S(2)}) collective-permute-start(bf16[512,1536]{1,0:T(8,128)(2,1)} %pad_maximum_fusion.2), channel_id=1, source_target_pairs={{0,1},{1,0},{2,3},{3,2},{4,5},{5,4},{6,7},{7,6},{8,9},{9,8},{10,11... | collective-permute-start | bytes 4718600 | tf_op jit(solution)/shard_map/ppermute | solution.py:829
  129.6 29.7 %copy-start.19 = (bf16[128,384]{1,0:T(8,128)(2,1)}, bf16[128,384]{1,0:T(8,128)(2,1)S(1)}, u32[]{:S(2)}) copy-start(bf16[128,384]{1,0:T(8,128)(2,1)S(1)} %get-tuple-element.139) | copy-start | bytes 294916
  129.6 29.7 %copy-start.21 = (bf16[128,384]{1,0:T(8,128)(2,1)}, bf16[128,384]{1,0:T(8,128)(2,1)S(1)}, u32[]{:S(2)}) copy-start(bf16[128,384]{1,0:T(8,128)(2,1)S(1)} %get-tuple-element.140) | copy-start | bytes 294916
  129.6 29.7 %copy-start.23 = (bf16[128,384]{1,0:T(8,128)(2,1)}, bf16[128,384]{1,0:T(8,128)(2,1)S(1)}, u32[]{:S(2)}) copy-start(bf16[128,384]{1,0:T(8,128)(2,1)S(1)} %get-tuple-element.141) | copy-start | bytes 294916
  301.3 76.2 %collective-permute-start.9 = (bf16[1120,768]{1,0:T(8,128)(2,1)}, bf16[1120,768]{1,0:T(8,128)(2,1)S(1)}, u32[]{:S(2)}, u32[]{:S(2)}) collective-permute-start(bf16[1120,768]{1,0:T(8,128)(2,1)} %get-tuple-element.75), channel_id=1, source_target_pairs={{0,16},{16,0},{1,17},{17,1},{2,18},{18,2},{3,19},{19,3},{4,20},{20... | collective-permute-start | bytes 5160968 | tf_op jit(solution)/shard_map/ppermute | solution.py:829
  303.5 138.7 %collective-permute-start.14 = (bf16[2240,768]{1,0:T(8,128)(2,1)}, bf16[2240,768]{1,0:T(8,128)(2,1)}, u32[]{:S(2)}, u32[]{:S(2)}) collective-permute-start(bf16[2240,768]{1,0:T(8,128)(2,1)} %get-tuple-element.76), channel_id=1, source_target_pairs={{0,16},{16,0},{1,17},{17,1},{2,18},{18,2},{3,19},{19,3},{4,20},{20... | collective-permute-start | bytes 10321928 | tf_op jit(solution)/shard_map/ppermute | solution.py:829
  377.5 5.0 copy-start.26
  380.7 205.9 %collective-permute-start.13 = (bf16[1120,768]{1,0:T(8,128)(2,1)}, bf16[1120,768]{1,0:T(8,128)(2,1)}, u32[]{:S(2)}, u32[]{:S(2)}) collective-permute-start(bf16[1120,768]{1,0:T(8,128)(2,1)} %add_convert_fusion.1), channel_id=1, source_target_pairs={{0,4},{4,0},{8,12},{12,8},{1,5},{5,1},{9,13},{13,9},{2,6},{6,2},{1... | collective-permute-start | bytes 5160968 | tf_op jit(solution)/shard_map/ppermute | solution.py:829
  401.4 30.0 %copy-start.7 = (f32[512,64]{1,0:T(8,128)S(1)}, f32[512,64]{1,0:T(8,128)}, u32[]{:S(2)}) copy-start(f32[512,64]{1,0:T(8,128)} %copy-done.6) | copy-start | bytes 393220
  401.4 31.3 %copy-start.12 = (bf16[512,384]{1,0:T(8,128)(2,1)S(1)}, bf16[512,384]{1,0:T(8,128)(2,1)}, u32[]{:S(2)}) copy-start(bf16[512,384]{1,0:T(8,128)(2,1)} %get-tuple-element.96) | copy-start | bytes 1179652
  401.4 31.5 %copy-start.10 = (bf16[512,1536]{1,0:T(8,128)(2,1)S(1)}, bf16[512,1536]{1,0:T(8,128)(2,1)}, u32[]{:S(2)}) copy-start(bf16[512,1536]{1,0:T(8,128)(2,1)} %get-tuple-element.103) | copy-start | bytes 4718596
  431.5 5.4 copy-start.20
  432.7 6.3 %copy-start.4 = (bf16[512,128]{1,0:T(8,128)(2,1)}, bf16[512,128]{1,0:T(8,128)(2,1)S(1)}, u32[]{:S(2)}) copy-start(bf16[512,128]{1,0:T(8,128)(2,1)S(1)} %fusion.13) | copy-start | bytes 393220
  433.4 42.5 %collective-permute-start.12 = (bf16[768,128]{1,0:T(8,128)(2,1)S(1)}, bf16[768,128]{1,0:T(8,128)(2,1)S(1)}, u32[]{:S(2)}, u32[]{:S(2)}) collective-permute-start(bf16[768,128]{1,0:T(8,128)(2,1)S(1)} %convolution_convert_fusion.6), channel_id=1, source_target_pairs={{0,16},{16,0},{1,17},{17,1},{2,18},{18,2},{3,19},{19,3},{4,20},{20... | collective-permute-start | bytes 589832 | tf_op jit(solution)/shard_map/ppermute | solution.py:829
  435.6 45.4 %collective-permute-start.11 = (bf16[768,384]{1,0:T(8,128)(2,1)}, bf16[768,384]{1,0:T(8,128)(2,1)}, u32[]{:S(2)}, u32[]{:S(2)}) collective-permute-start(bf16[768,384]{1,0:T(8,128)(2,1)} %convolution_convert_fusion.3), channel_id=1, source_target_pairs={{0,16},{16,0},{1,17},{17,1},{2,18},{18,2},{3,19},{19,3},{4,20},{20... | collective-permute-start | bytes 1769480 | tf_op jit(solution)/shard_map/ppermute | solution.py:829
  438.2 40.0 %collective-permute-start.10 = (bf16[384,768]{1,0:T(8,128)(2,1)}, bf16[384,768]{1,0:T(8,128)(2,1)}, u32[]{:S(2)}, u32[]{:S(2)}) collective-permute-start(bf16[384,768]{1,0:T(8,128)(2,1)} %convolution_convert_fusion.4), channel_id=1, source_target_pairs={{0,16},{16,0},{1,17},{17,1},{2,18},{18,2},{3,19},{19,3},{4,20},{20... | collective-permute-start | bytes 1769480 | tf_op jit(solution)/shard_map/ppermute | solution.py:829
  445.3 146.9 %collective-permute-start.15 = (bf16[2240,768]{1,0:T(8,128)(2,1)S(1)}, bf16[2240,768]{1,0:T(8,128)(2,1)}, u32[]{:S(2)}, u32[]{:S(2)}) collective-permute-start(bf16[2240,768]{1,0:T(8,128)(2,1)S(1)} %add_convert_fusion), channel_id=1, source_target_pairs={{0,4},{4,0},{8,12},{12,8},{1,5},{5,1},{9,13},{13,9},{2,6},{6,2},{1... | collective-permute-start | bytes 10321928 | tf_op jit(solution)/shard_map/ppermute | solution.py:829
  447.1 28.8 %copy-start.5 = (bf16[512,128]{1,0:T(8,128)(2,1)S(1)}, bf16[512,128]{1,0:T(8,128)(2,1)}, u32[]{:S(2)}) copy-start(bf16[512,128]{1,0:T(8,128)(2,1)} %copy-done.4) | copy-start | bytes 393220
  475.8 5.2 copy-start.11
  475.8 5.2 copy-start.13
  576.8 5.1 copy-start.17
  (13 other events, 37.6 us)

commit v5 on v4

--- a/solution.py
+++ b/solution.py
@@ -175,25 +175,23 @@
 
 
 def qkv_kernel(pieces, meta_ref, x_ref, gain_ref, bias_ref, cos_ref, sin_ref, *refs):
-    weights, (xn_ref, factor_ref, q_ref, kv_ref) = refs[:pieces], refs[pieces:]
+    weights, (xn_ref, factor_ref, q_ref, kv_ref) = refs[: 2 * pieces], refs[2 * pieces :]
     values = x_ref[...].astype(f32)
     factor = lax.rsqrt(jnp.mean(values * values, axis=-1, keepdims=True) + EPSILON)
     factor_ref[...] = factor
     xn_ref[...] = (values * factor * gain_ref[...]).astype(bf16)
-    total = bias_ref[...]
-    for j, weight in enumerate(weights):
-        depth = weight.shape[0]
-        total = total + dot(xn_ref[:, columns_of(meta_ref, j, depth, pieces)], weight[...])
+    depth = weights[0].shape[0]
+    normed = [xn_ref[:, columns_of(meta_ref, j, depth, pieces)] for j in range(pieces)]
     cosine, sine = cos_ref[...], sin_ref[...]
     sign = jnp.where(lax.broadcasted_iota(jnp.int32, cosine.shape, 1) < HD // 2, -1.0, 1.0)
-    heads = q_ref.shape[1] // HD
-    for h in range(heads + 1):
-        own = total[:, h * HD : (h + 1) * HD]
-        turned = own * cosine + pltpu.roll(own, HD // 2, 1) * sign * sine
-        if h < heads:
-            q_ref[:, h * HD : (h + 1) * HD] = turned.astype(bf16)
-        else:
-            kv_ref[...] = jnp.where(meta_ref[2] == 0, turned, own).astype(bf16)
+    sine = sine * sign
+    width = q_ref.shape[1]
+    total = bias_ref[:, :width] + sum(dot(x, w[...]) for x, w in zip(normed, weights[:pieces]))
+    turn = lambda own: own * cosine + pltpu.roll(own, HD // 2, 1) * sine
+    for h in range(width // HD):
+        q_ref[:, h * HD : (h + 1) * HD] = turn(total[:, h * HD : (h + 1) * HD]).astype(bf16)
+    own = bias_ref[:, width:] + sum(dot(x, w[...]) for x, w in zip(normed, weights[pieces:]))
+    kv_ref[...] = jnp.where(meta_ref[2] == 0, turn(own), own).astype(bf16)
 
 
 def columns_of(meta_ref, j, depth, pieces):
@@ -202,136 +200,144 @@
     return pl.ds(pl.multiple_of(meta_ref[j] * depth, LANES), depth)
 
 
-def qkv(meta, inputs, gain, bias, cosine, sine, weights):
+def qkv(meta, inputs, gain, bias, cosine, sine, w_q, w_kv):
     rows, width = inputs.shape
-    out = weights[0].shape[1]
+    out = w_q[0].shape[1]
     tile = 256
     row = lambda n: pl.BlockSpec((tile, n), lambda i, m: (i, 0))
     fixed = lambda w: pl.BlockSpec(w.shape, lambda i, m: (0, 0))
     return pl.pallas_call(
-        functools.partial(qkv_kernel, len(weights)),
+        functools.partial(qkv_kernel, len(w_q)),
         name="qkv",
         grid_spec=pltpu.PrefetchScalarGridSpec(
             num_scalar_prefetch=1,
             grid=(rows // tile,),
             in_specs=[row(width), fixed(gain), fixed(bias), row(HD), row(HD)]
-            + [fixed(w) for w in weights],
-            out_specs=[row(width), row(1), row(out - HD), row(HD)],
+            + [fixed(w) for w in (*w_q, *w_kv)],
+            out_specs=[row(width), row(1), row(out), row(HD)],
         ),
         out_shape=[
             jax.ShapeDtypeStruct((rows, width), bf16),
             jax.ShapeDtypeStruct((rows, 1), f32),
-            jax.ShapeDtypeStruct((rows, out - HD), bf16),
+            jax.ShapeDtypeStruct((rows, out), bf16),
             jax.ShapeDtypeStruct((rows, HD), bf16),
         ],
         compiler_params=pltpu.CompilerParams(vmem_limit_bytes=VMEM_LIMIT),
-    )(meta, inputs, gain, bias, cosine, sine, *weights)
-
-
-def ffn_kernel(with_dx, pieces, meta_ref, x_ref, dy_ref, *refs):
+    )(meta, inputs, gain, bias, cosine, sine, *w_q, *w_kv)
+
+
+def qkv_back_kernel(pieces, meta_ref, dq_ref, dkv_ref, *refs):
+    w_q, w_kv, out_ref = refs[:pieces], refs[pieces : 2 * pieces], refs[-1]
+    for j in range(pieces):
+        out_ref[:, columns_of(meta_ref, j, w_q[j].shape[0], pieces)] = (
+            dot_cols(dq_ref[...], w_q[j][...]) + dot_cols(dkv_ref[...], w_kv[j][...])
+        ).astype(bf16)
+
+
+def qkv_back(meta, grad_q, grad_kv, w_q, w_kv):
+    rows, width = grad_q.shape[0], sum(w.shape[0] for w in w_q)
+    tile = 256
+    row = lambda n: pl.BlockSpec((tile, n), lambda i, m: (i, 0))
+    fixed = lambda w: pl.BlockSpec(w.shape, lambda i, m: (0, 0))
+    return pl.pallas_call(
+        functools.partial(qkv_back_kernel, len(w_q)),
+        name="qkv_back",
+        grid_spec=pltpu.PrefetchScalarGridSpec(
+            num_scalar_prefetch=1,
+            grid=(rows // tile,),
+            in_specs=[row(grad_q.shape[1]), row(HD)] + [fixed(w) for w in (*w_q, *w_kv)],
+            out_specs=row(width),
+        ),
+        out_shape=jax.ShapeDtypeStruct((rows, width), bf16),
+        compiler_params=pltpu.CompilerParams(vmem_limit_bytes=VMEM_LIMIT),
+    )(meta, grad_q, grad_kv, *w_q, *w_kv)
+
+
+def ffn_kernel(pieces, meta_ref, x_ref, dy_ref, *refs):
     wg, wu, wd = (refs[m * pieces : (m + 1) * pieces] for m in range(3))
-    outs = refs[-5:] if with_dx else refs[-3:]
-    hid_ref, dg_ref, du_ref = outs[:3]
+    hid_ref, dg_ref, du_ref, dx_ref, out_ref = refs[-5:]
     columns = [columns_of(meta_ref, j, wg[j].shape[1], pieces) for j in range(pieces)]
     gate = sum(dot_cols(x_ref[:, at], w[...]) for at, w in zip(columns, wg))
     up = sum(dot_cols(x_ref[:, at], w[...]) for at, w in zip(columns, wu))
     grad_hidden = sum(dot_cols(dy_ref[:, at], w[...]) for at, w in zip(columns, wd))
     sigma = 1.0 / (1.0 + jnp.exp(-gate))
     gated = gate * sigma
-    hidden = (gated * up).astype(bf16)
-    hid_ref[...] = hidden
-    grad_gate = (grad_hidden * up * (sigma + gated * (1.0 - sigma))).astype(bf16)
-    grad_up = (grad_hidden * gated).astype(bf16)
-    dg_ref[...] = grad_gate
-    du_ref[...] = grad_up
-    if with_dx:
-        for at, g, u in zip(columns, wg, wu):
-            outs[3][:, at] = (dot(grad_gate, g[...]) + dot(grad_up, u[...])).astype(bf16)
-        for at, d in zip(columns, wd):
-            outs[4][:, at] = dot(hidden, d[...]).astype(bf16)
-
-
-def ffn(meta, normed, grad_out, weights, with_dx):
+    hid_ref[...] = (gated * up).astype(bf16)
+    dg_ref[...] = (grad_hidden * up * (sigma + gated * (1.0 - sigma))).astype(bf16)
+    du_ref[...] = (grad_hidden * gated).astype(bf16)
+
+    @pl.when(pl.program_id(0) < pl.num_programs(0) // 2)
+    def _():
+        for at, g, u, d in zip(columns, wg, wu, wd):
+            dx_ref[:, at] = (dot(dg_ref[...], g[...]) + dot(du_ref[...], u[...])).astype(bf16)
+            out_ref[:, at] = dot(hid_ref[...], d[...]).astype(bf16)
+
+
+def ffn(meta, normed, grad_out, weights):
     width = normed.shape[-1]
-    half = 0 if with_dx else 1
-    rows = normed.shape[1] * normed.shape[2]
+    rows = normed.shape[0] * normed.shape[1]
     units = weights[0].shape[0] // 3
     tile = 512
     steps = rows // tile
     flat = lambda x: x.reshape(-1, width)
-    row = lambda n: pl.BlockSpec((tile, n), lambda i, m: (i, 0))
-    read = pl.BlockSpec((tile, width), lambda i, m: (i + half * steps, 0))
+    read = pl.BlockSpec((tile, width), lambda i, m: (i, 0))
     weight = lambda w, k: pl.BlockSpec(
         (units, w.shape[1]), lambda i, m: (k, 0), pipeline_mode=pl.Buffered(1)
     )
-    widths = [units] * 3 + [width] * (2 * with_dx)
+    placed = pl.BlockSpec(
+        (tile, units), lambda i, m: (lax.rem(i + m[3] * (steps // 2), steps), 0)
+    )
+    near = pl.BlockSpec((tile, width), lambda i, m: (jnp.minimum(i, steps // 2 - 1), 0))
     return pl.pallas_call(
-        functools.partial(ffn_kernel, with_dx, len(weights)),
-        name="ffn_pair" if with_dx else "ffn_far",
+        functools.partial(ffn_kernel, len(weights)),
+        name="ffn",
         grid_spec=pltpu.PrefetchScalarGridSpec(
             num_scalar_prefetch=1,
             grid=(steps,),
             in_specs=[read, read] + [weight(w, k) for k in range(3) for w in weights],
-            out_specs=[row(n) for n in widths],
+            out_specs=[placed] * 3 + [near] * 2,
         ),
-        out_shape=[jax.ShapeDtypeStruct((rows, n), bf16) for n in widths],
+        out_shape=[jax.ShapeDtypeStruct((rows, units), bf16)] * 3
+        + [jax.ShapeDtypeStruct((rows // 2, width), bf16)] * 2,
         compiler_params=pltpu.CompilerParams(vmem_limit_bytes=VMEM_LIMIT),
     )(meta, flat(normed), flat(grad_out), *(list(weights) * 3))
 
 
-def unit_grads_kernel(meta_ref, x, y, hp, hf, gp, gf, up, uf, og, oud, ag, au, ad):
-    step = pl.program_id(0)
-
-    @pl.when(step == 0)
-    def _():
-        for acc in (ag, au, ad):
-            acc[...] = jnp.zeros_like(acc)
-
-    for use, h, g, u in ((True, hp, gp, up), (False, hf, gf, uf)):
-
-        @pl.when((step // (pl.num_programs(0) // 2) == meta_ref[3]) == use)
-        def _():
-            ag[...] += dot_rows(g[...], x[...])
-            au[...] += dot_rows(u[...], x[...])
-            ad[...] += dot_rows(h[...], y[...])
-
-    @pl.when(step == pl.num_programs(0) - 1)
-    def _():
-        units = og.shape[0]
-        og[...] = ag[...].astype(bf16)
-        oud[:units] = au[...].astype(bf16)
-        oud[units:] = ad[...].astype(bf16)
-
-
-def unit_grads(meta, which, pieces, x, y, hid, dg, du):
+def unit_grads_kernel(count, meta_ref, near_ref, far_ref, *refs):
+    units, out_ref, x_ref = refs[:count], refs[-2], refs[-1]
+    half = near_ref.shape[0]
+    x_ref[pl.ds(pl.multiple_of(meta_ref[3] * half, half), half)] = near_ref[...]
+    x_ref[pl.ds(pl.multiple_of((1 - meta_ref[3]) * half, half), half)] = far_ref[...]
+    for k, unit in enumerate(units):
+        depth = unit.shape[1]
+        out_ref[k * depth : (k + 1) * depth] = dot_rows(unit[...], x_ref[...]).astype(bf16)
+
+
+def unit_grads(meta, which, pieces, x, units_of):
     width = x.shape[-1]
-    rows, units = dg[0].shape
+    count, (rows, units) = len(units_of), units_of[0].shape
     depth = width // pieces
-    tile = 512
-    steps = rows // tile
+    tile = 256
+    steps = depth // tile
     shard = (lambda m: m[which]) if pieces > 1 else (lambda m: 0)
-    near = lambda i, m: jnp.clip(i - steps * m[3], 0, steps - 1)
-    far = lambda i, m: jnp.clip(i - steps * (1 - m[3]), 0, steps - 1)
-    feature = pl.BlockSpec(
-        (tile, depth), lambda i, m: (lax.rem(i + steps * m[3], 2 * steps), shard(m))
+    feature = lambda half: pl.BlockSpec(
+        (rows // 2, tile), lambda i, m: (half, shard(m) * steps + i)
     )
-    unit = lambda at: pl.BlockSpec((tile, units), lambda i, m: (at(i, m), 0))
+    unit = pl.BlockSpec((rows, units), lambda i, m: (0, 0), pipeline_mode=pl.Buffered(1))
+    x = x.reshape(-1, width)
     return pl.pallas_call(
-        unit_grads_kernel,
-        name=f"unit_grads_{which}",
+        functools.partial(unit_grads_kernel, count),
+        name=f"unit_grads_{which}_{count}",
         grid_spec=pltpu.PrefetchScalarGridSpec(
             num_scalar_prefetch=1,
-            grid=(2 * steps,),
-            in_specs=[feature] * 2 + [unit(near), unit(far)] * 3,
-            out_specs=[
-                pl.BlockSpec((k * units, depth), lambda i, m: (0, 0), pipeline_mode=pl.Buffered(1))
-                for k in (1, 2)
-            ],
-            scratch_shapes=[pltpu.VMEM((units, depth), f32)] * 3,
+            grid=(steps,),
+            in_specs=[feature(0), feature(1)] + [unit] * count,
+            out_specs=pl.BlockSpec((count * units, tile), lambda i, m: (0, i)),
+            scratch_shapes=[pltpu.VMEM((rows, tile), bf16)],
         ),
-        out_shape=[jax.ShapeDtypeStruct((k * units, depth), bf16) for k in (1, 2)],
+        out_shape=jax.ShapeDtypeStruct((count * units, depth), bf16),
         compiler_params=pltpu.CompilerParams(vmem_limit_bytes=VMEM_LIMIT),
-    )(meta, x.reshape(-1, width), y.reshape(-1, width), *hid, *dg, *du)
+    )(meta, x, x, *units_of)
 
 
 class Wires:
@@ -340,10 +346,10 @@
         self.used = self.used_local = 0
         self.started = []
 
-    def copy(self, source, target, device):
+    def plan(self, source, target, device):
         k = self.used
         self.used += 1
-        one = pltpu.make_async_remote_copy(
+        return pltpu.make_async_remote_copy(
             source,
             target,
             self.sends.at[k],
@@ -351,6 +357,9 @@
             device_id=device,
             device_id_type=pl.DeviceIdType.MESH,
         )
+
+    def copy(self, source, target, device):
+        one = self.plan(source, target, device)
         one.start()
         self.started.append(one)
         return one
@@ -390,22 +399,32 @@
     return x.astype(f32)
 
 
+def ranks():
+    t = lax.axis_index("tensor")
+    flip = lambda x, bit: x + bit * (1 - 2 * lax.rem(x // bit, 2))
+    return (t, flip(t, 1), flip(t, 2), flip(flip(t, 1), 2))
+
+
 def scatter_rank(wires, to, part, own, got_core, sent, got_y):
     size = part.shape[1] // 2
     halves = [pl.ds(0, size), pl.ds(size, size)]
+    rank = ranks()
     from_core = {}
     for block in (1, 0):
         for k, at in enumerate(halves):
             from_core[block, k] = wires.copy(
-                part.at[2 + block, at], got_core.at[block, at], to["core"]
+                part.at[rank[1 + 2 * block], at], got_core.at[block, at], to["core"]
             )
-    mine = wires.here(part.at[pl.ds(0, 2)], own)
-    mine.wait()
+    mine = [wires.here(part.at[rank[2 * block]], own.at[block]) for block in (0, 1)]
+    yield
+    for one in mine:
+        one.wait()
     from_y = []
     for k, at in enumerate(halves):
         from_core[1, k].wait_recv()
         sent[at] = (wide(own[1, at]) + wide(got_core[1, at])).astype(bf16)
         from_y.append(wires.copy(sent.at[at], got_y.at[at], to["y"]))
+    yield
     for k in range(2):
         from_core[0, k].wait_recv()
     total = wide(own[0]) + wide(got_core[0])
@@ -455,16 +474,17 @@
             return done.value
 
 
-def gather_rank(wires, to, block, out, at):
+def gather_rank(wires, to, block, out):
     size = block.shape[0] // 2
     halves = [pl.ds(0, size), pl.ds(size, size)]
-    mine = wires.here(block, out.at[at(0, 0)])
-    from_y = [wires.copy(block.at[h], out.at[at(0, 2), h], to["y"]) for h in halves]
-    from_core = [wires.copy(block, out.at[at(0, 1)], to["core"])]
+    rank = ranks()
+    mine = wires.here(block, out.at[rank[0]])
+    from_y = [wires.copy(block.at[h], out.at[rank[0], h], to["y"]) for h in halves]
+    from_core = [wires.copy(block, out.at[rank[0]], to["core"])]
     yield
     for h, one in zip(halves, from_y):
         one.wait_recv()
-        from_core.append(wires.copy(out.at[at(2, 0), h], out.at[at(2, 1), h], to["core"]))
+        from_core.append(wires.copy(out.at[rank[2], h], out.at[rank[2], h], to["core"]))
     for one in from_core:
         one.wait_recv()
     mine.wait()
@@ -474,15 +494,18 @@
     size = block.shape[0] // 2
     low, high = pl.ds(0, size), pl.ds(size, size)
     at = lambda j: out.at[base + j]
+    from_z = wires.copy(block, at(2), to["z"])
+    yield
     from_y = wires.copy(block, at(1), to["y"])
-    from_z = wires.copy(block, at(2), to["z"])
     from_core = [wires.copy(block, at(4), to["core"])]
+    yield
     from_y.wait_recv()
     via_z = wires.copy(out.at[base + 1, low], out.at[base + 3, low], to["z"])
     from_core.append(wires.copy(at(1), at(5), to["core"]))
     from_z.wait_recv()
     via_y = wires.copy(out.at[base + 2, high], out.at[base + 3, high], to["y"])
     from_core.append(wires.copy(at(2), at(6), to["core"]))
+    yield
     via_z.wait_recv()
     via_y.wait_recv()
     from_core.append(wires.copy(at(3), at(7), to["core"]))
@@ -502,7 +525,7 @@
         + [
             pltpu.SemaphoreType.DMA((copies,)),
             pltpu.SemaphoreType.DMA((copies,)),
-            pltpu.SemaphoreType.DMA((4,)),
+            pltpu.SemaphoreType.DMA((6,)),
         ],
         compiler_params=pltpu.CompilerParams(
             collective_id=key, has_side_effects=True, vmem_limit_bytes=VMEM_LIMIT
@@ -543,79 +566,118 @@
     )[0]
 
 
-def kv_scatter_kernel(part_ref, out_ref, own, got_core, sent, got, *sems):
-    wires, to = Wires(*sems), partners()
+def kv_scatter_kernel(
+    part_ref, out_part, mid_ref, dkv_ref, outputs, own, got_core, sent, got, low, *rest
+):
+    first, wires, to = rest[:7], Wires(*rest[7:]), partners()
     kind = lax.rem(lax.axis_index("tensor"), 2)
-    rows = out_ref.shape[0]
+    rows = dkv_ref.shape[0]
     block = lambda j: pl.ds(j * rows, rows)
-    meet([to[k] for k in ("core", "z", "far", "last")])
+    meet([to[k] for k in ("core", "y", "z", "far", "last")])
     steps = ((3, "last"), (2, "far"), (1, "z"), (0, None))
     from_core = {
         j: wires.copy(part_ref.at[1 - kind, block(j)], got_core.at[block(j)], to["core"])
         for j, _ in steps
     }
     mine = wires.here(part_ref.at[kind], own)
+    ahead = scatter_pair(wires, to, out_part, *first)
+    next(ahead)
     mine.wait()
     arrive = []
     for j, k in steps[:3]:
         from_core[j].wait_recv()
         sent[block(j)] = (wide(own[block(j)]) + wide(got_core[block(j)])).astype(bf16)
         arrive.append(wires.copy(sent.at[block(j)], got.at[block(j)], to[k]))
+    next(ahead)
     from_core[0].wait_recv()
     total = wide(own[block(0)]) + wide(got_core[block(0)])
     for one in arrive:
         one.wait_recv()
     for j in (1, 2, 3):
         total = total + wide(got[block(j)])
-    out_ref[...] = total
+    dkv_ref[...] = total
+    low[...] = (mid_ref[...] + result_of(ahead)).astype(bf16)
+    result_of(gather_rank(wires, to, low, outputs))
     wires.finish()
 
 
-def kv_scatter(part):
+def kv_scatter(part, out_part, middle):
     _, rows, width = part.shape
     n_c = lax.axis_size("context")
+    out_rows, out_width = middle.shape
     return remote_call(
         kv_scatter_kernel,
         "kv_scatter",
         1,
-        [part],
-        [jax.ShapeDtypeStruct((rows // n_c, width), f32)],
-        [pltpu.VMEM((rows, width), bf16)] * 4,
-        7,
-        ([False], [True]),
-    )[0]
-
-
-def middle_kernel(part, x_ref, gain_ref, mid_ref, factor_ref, out, own, core, sent, got, xn, *sems):
+        [part, out_part.reshape(8, out_rows, out_width), middle],
+        [
+            jax.ShapeDtypeStruct((rows // n_c, width), f32),
+            jax.ShapeDtypeStruct((4, out_rows, out_width), bf16),
+        ],
+        [pltpu.VMEM((rows, width), bf16)] * 4
+        + [pltpu.VMEM((out_rows, out_width), bf16)]
+        + pair_scratch(out_rows, out_width),
+        24,
+        ([False, False, True], [True, False]),
+    )
+
+
+def middle_kernel(
+    part, x_ref, gain_ref, dy_ref, mid_ref, factor_ref, out, dys, own, core, sent, got, xn, *sems
+):
     wires, to = Wires(*sems), partners()
+    blocks = out.shape[0] // 2
     meet([to[k] for k in ("core", "y", "z", "far")])
-    middle = wide(x_ref[...]) + scatter_rank(wires, to, part, own, core, sent, got)
+    summed = scatter_rank(wires, to, part, own, core, sent, got)
+    next(summed)
+    dy_far = wires.copy(dy_ref, dys.at[blocks], to["far"])
+    mine = [wires.here(dy_ref, dys.at[0])]
+    dy_near = gather_pair(wires, to, dy_ref, dys, 0)
+    next(dy_near)
+    next(summed)
+    next(dy_near)
+    middle = wide(x_ref[...]) + result_of(summed)
     mid_ref[...] = middle
     factor = lax.rsqrt(jnp.mean(middle * middle, axis=-1, keepdims=True) + EPSILON)
     factor_ref[...] = factor
     xn[...] = (middle * factor * gain_ref[...]).astype(bf16)
-    blocks = out.shape[0] // 2
-    mine = wires.here(xn, out.at[0])
-    from_far = wires.copy(xn, out.at[blocks], to["far"])
-    last = gather_pair(wires, to, xn, out, 0)
-    from_far.wait_recv()
-    last += gather_pair(wires, to, out.at[blocks], out, blocks)
-    for one in last:
+    mine.append(wires.here(xn, out.at[0]))
+    xn_far = wires.copy(xn, out.at[blocks], to["far"])
+    xn_near = gather_pair(wires, to, xn, out, 0)
+    next(xn_near)
+    next(xn_near)
+    next(dy_near)
+    next(xn_near)
+    dy_far.wait_recv()
+    dy_last = gather_pair(wires, to, dys.at[blocks], dys, blocks)
+    next(dy_last)
+    next(dy_last)
+    xn_far.wait_recv()
+    xn_last = gather_pair(wires, to, out.at[blocks], out, blocks)
+    next(xn_last)
+    next(xn_last)
+    ends = result_of(dy_near) + result_of(xn_near)
+    next(dy_last)
+    next(xn_last)
+    ends += result_of(dy_last) + result_of(xn_last)
+    for one in ends:
         one.wait_recv()
-    mine.wait()
+    for one in mine:
+        one.wait()
     wires.finish()
 
 
-def middle_norm(part, inputs_part, gain):
+def middle_norm(part, inputs_part, gain, dy_part):
     rows, width = inputs_part.shape
     return remote_call(
         middle_kernel,
         "middle_norm",
         2,
-        [part.reshape(4, rows, width), inputs_part, gain],
+        [part.reshape(4, rows, width), inputs_part, gain, dy_part],
         [
             jax.ShapeDtypeStruct((rows, width), f32),
             jax.ShapeDtypeStruct((rows, 1), f32),
+            jax.ShapeDtypeStruct((16, rows, width), bf16),
             jax.ShapeDtypeStruct((16, rows, width), bf16),
         ],
         [
@@ -625,8 +687,8 @@
             pltpu.VMEM((rows, width), bf16),
             pltpu.VMEM((rows, width), bf16),
         ],
-        32,
-        ([False, True, True], [True, True, False]),
+        48,
+        ([False, True, True, True], [True, True, False, False]),
     )
 
 
@@ -637,42 +699,20 @@
     return grad_values, jnp.sum(grad_normed * values * factor, axis=0, keepdims=True)
 
 
-MIXED = (0, 2, 1, 3)
-
-
-def natural_place(t):
-    flip = lambda x, bit: x + bit * (1 - 2 * lax.rem(x // bit, 2))
-    return lambda j, _: t if j == 0 else flip(t, j)
-
-
 def middle_back_kernel(
-    part, out_part, mid_ref, factor_ref, gain_ref, dy_ref, dmid_ref, dgain_ref, out, outputs, *rest
+    part, mid_ref, factor_ref, gain_ref, dy_ref, dmid_ref, dgain_ref, out, low, *rest
 ):
-    low, out_low, first, second, wires = rest[0], rest[1], rest[2:9], rest[9:16], Wires(*rest[16:])
-    to = partners()
+    first, wires, to = rest[:7], Wires(*rest[7:]), partners()
     meet([to[k] for k in ("core", "y", "z")])
-    back = scatter_pair(wires, to, part, *first)
-    ahead = scatter_pair(wires, to, out_part, *second)
-    next(back)
-    next(ahead)
-    next(back)
-    next(back)
-    next(ahead)
-    grad_normed = result_of(back)
+    grad_normed = result_of(scatter_pair(wires, to, part, *first))
     du, dgain = norm_back_rows(mid_ref[...], factor_ref[...], gain_ref[...], grad_normed)
     dgain_ref[...] = dgain
     dmid = wide(dy_ref[...]) + du
+    low[...] = dmid.astype(bf16)
+    share = gather_rank(wires, to, low, out)
+    next(share)
     dmid_ref[...] = dmid
-    low[...] = dmid.astype(bf16)
-    share = gather_rank(wires, to, low, out, lambda j, flip: MIXED.index(j ^ flip))
-    next(share)
-    next(ahead)
-    out_low[...] = (mid_ref[...] + result_of(ahead)).astype(bf16)
-    place = natural_place(lax.axis_index("tensor"))
-    out_share = gather_rank(wires, to, out_low, outputs, place)
-    next(out_share)
     result_of(share)
-    result_of(out_share)
     wires.finish()
 
 
@@ -688,23 +728,21 @@
     ]
 
 
-def middle_back(part, out_part, middle, factor, gain, dy_part):
+def middle_back(part, middle, factor, gain, dy_part):
     rows, width = middle.shape
     return remote_call(
         middle_back_kernel,
         "middle_back",
         3,
-        [part.reshape(8, rows, width), out_part.reshape(8, rows, width)]
-        + [middle, factor, gain, dy_part],
+        [part.reshape(8, rows, width), middle, factor, gain, dy_part],
         [
             jax.ShapeDtypeStruct((rows, width), f32),
             jax.ShapeDtypeStruct((1, width), f32),
             jax.ShapeDtypeStruct((4, rows, width), bf16),
-            jax.ShapeDtypeStruct((4, rows, width), bf16),
         ],
-        [pltpu.VMEM((rows, width), bf16)] * 2 + pair_scratch(rows, width) * 2,
-        32,
-        ([False, False, True, True, True, True], [True, True, False, False]),
+        [pltpu.VMEM((rows, width), bf16)] + pair_scratch(rows, width),
+        16,
+        ([False, True, True, True, True], [True, True, False]),
     )
 
 
@@ -722,10 +760,10 @@
     low, own, core, sent, got, slots = rest[:-3]
     wires, to = Wires(*rest[-3:]), partners()
     meet([to[k] for k in ("core", "y")])
-    grad_normed = scatter_rank(wires, to, part, own, core, sent, got)
+    grad_normed = result_of(scatter_rank(wires, to, part, own, core, sent, got))
     du, dgain = norm_back_rows(wide(x_ref[...]), factor_ref[...], gain_ref[...], grad_normed)
     low[...] = (dmid_ref[...] + du).astype(bf16)
-    share = gather_rank(wires, to, low, out, natural_place(lax.axis_index("tensor")))
+    share = gather_rank(wires, to, low, out)
     next(share)
     width = dgain.shape[1]
     sum_ref[:, width:] = small_ref[:, width:]
@@ -760,66 +798,87 @@
 
 
 def context_sum_kernel(over_f, *refs):
-    (parts, refs), (small_ref, refs) = (refs[:3], refs[3:]), (refs[3], refs[4:])
-    (outs, refs), (sum_ref, shared, refs) = (refs[:3], refs[3:]), (refs[3], refs[4], refs[5:])
-    gots, slots, wires = refs[:3], refs[3], Wires(*refs[4:])
-    to, c = partners(), lax.axis_index("context")
-    ways = ((1, "z"), (2, "far"), (3, "last"))
+    parts, small_ref, outs, sum_ref, shared = refs[:3], refs[3], refs[4:6], refs[6], refs[7]
+    lows, from_end, from_middle, slots = refs[8:11], refs[11:14], refs[14:17], refs[17]
+    wires, to, c = Wires(*refs[18:]), partners(), lax.axis_index("context")
+    last = lax.axis_size("context") - 1
+    end = (c == 0) | (c == last)
     greet = ["core", "y", "z", "far", "last"]
-    flip = lambda x, bit: x + bit * (1 - 2 * lax.rem(x // bit, 2))
     if over_f:
         to["f"] = {"fsdp": 1 - lax.axis_index("fsdp")}
         greet.append("f")
     meet([to[k] for k in greet])
-    rank = {1: flip(c, 1), 2: flip(c, 2), 3: flip(flip(c, 1), 2)}
-    arrive = []
-    order = (2, 0, 1)
-    quarter = lambda ref, k: pl.ds(
-        pl.multiple_of(k * (ref.shape[0] // 4), ref.shape[0] // 4), ref.shape[0] // 4
-    )
-    for i in order:
-        part, got = parts[i], gots[i]
-        arrive.append(
-            [
-                wires.copy(part.at[quarter(part, rank[j])], got.at[j - 1], to[way])
-                for j, way in ways
-            ]
-        )
+    chunks = []
+    for i, cuts in ((2, 1), (0, 2), (1, 2)):
+        size = parts[i].shape[0] // cuts
+        chunks += [(i, pl.ds(k * size, size)) for k in range(cuts)]
+    inward = [wires.plan(parts[i].at[at], from_end[i].at[at], to["z"]) for i, at in chunks]
+    across = [wires.plan(lows[i].at[at], from_middle[i].at[at], to["last"]) for i, at in chunks]
+    outward = [wires.plan(lows[i].at[at], lows[i].at[at], to["z"]) for i, at in chunks]
+
+    @pl.when(end)
+    def _():
+        for one in inward:
+            one.start()
+
+    @pl.when(jnp.logical_not(end))
+    def _():
+        for k, (i, at) in enumerate(chunks):
+            inward[k].wait_recv()
+            lows[i][at] = (wide(parts[i][at]) + wide(from_end[i][at])).astype(bf16)
+            across[k].start()
+
     sum_ref[...] = small_ref[...]
-    sent = []
-    for i, copies in zip(order, arrive):
-        part, got, out = parts[i], gots[i], outs[i]
-        for one in copies:
-            one.wait_recv()
-        at = quarter(part, c)
-        out[at] = (
-            wide(part[at]) + wide(got[0]) + wide(got[1]) + wide(got[2])
-        ).astype(bf16)
-        sent.append([wires.copy(out.at[at], out.at[at], to[way]) for _, way in ways])
     add_all(wires, [to[k] for k in (("f",) if over_f else ()) + ("z", "far")], sum_ref, slots)
-    for one in sent[0]:
-        one.wait_recv()
-    share = gather_rank(wires, to, outs[2], shared, natural_place(lax.axis_index("tensor")))
+
+    @pl.when(jnp.logical_not(end))
+    def _():
+        for k, (i, at) in enumerate(chunks):
+            across[k].wait_recv()
+            across[k].wait_send()
+            lows[i][at] = (wide(lows[i][at]) + wide(from_middle[i][at])).astype(bf16)
+            outward[k].start()
+
+    def arrived(k):
+        @pl.when(end)
+        def _():
+            outward[k].wait_recv()
+
+    arrived(0)
+    share = gather_rank(wires, to, lows[2], shared)
     next(share)
-    for one in sent[1] + sent[2]:
-        one.wait_recv()
+    for k in range(1, len(chunks)):
+        arrived(k)
+    for i in (0, 1):
+        outs[i][...] = wide(lows[i][...])
     result_of(share)
+
+    @pl.when(end)
+    def _():
+        for one in inward:
+            one.wait_send()
+
+    @pl.when(jnp.logical_not(end))
+    def _():
+        for one in outward:
+            one.wait_send()
+
     wires.finish()
 
 
 def context_sum(over_f, parts, small):
-    shape = lambda x: jax.ShapeDtypeStruct(x.shape, x.dtype)
+    like = lambda x: pltpu.VMEM(x.shape, bf16)
     return remote_call(
         functools.partial(context_sum_kernel, over_f),
         "context_sum",
         6,
         [*parts, small],
-        [shape(x) for x in parts]
-        + [shape(small), jax.ShapeDtypeStruct((4,) + parts[2].shape, bf16)],
-        [pltpu.VMEM((3, x.shape[0] // 4, x.shape[1]), bf16) for x in parts]
-        + [pltpu.VMEM((3,) + small.shape, f32)],
+        [jax.ShapeDtypeStruct(x.shape, f32) for x in parts[:2]]
+        + [jax.ShapeDtypeStruct(small.shape, f32)]
+        + [jax.ShapeDtypeStruct((4,) + parts[2].shape, bf16)],
+        [like(x) for x in parts] * 3 + [pltpu.VMEM((3,) + small.shape, f32)],
         32,
-        ([True] * 4, [True] * 4 + [False]),
+        ([True] * 4, [True] * 3 + [False]),
     )
 
 
@@ -871,41 +930,24 @@
                 return by_bit(f, x, flip(x, "fsdp", 1), axis)
             return lax.all_gather(x, "fsdp", axis=axis, tiled=True)
 
-        def columns_f(parts):
-            parts = [x.astype(bf16) for x in parts]
-            return by_bit(f, parts[0], parts[1], 1) if n_f == 2 else parts[0]
-
-        def grad_f(left, right, side):
-            if n_f == 2:
-                half = width // 2
-                source = (left, right)[side]
-                own = lax.dynamic_slice_in_dim(source, f * half, half, 1)
-                far = lax.dynamic_slice_in_dim(source, (1 - f) * half, half, 1)
-                pick = lambda x: dot_rows(x, right) if side == 0 else dot_rows(left, x)
-                got = flip(pick(far).astype(bf16), "fsdp", 1)
-                return pick(own) + got.astype(f32)
-            return lax.psum_scatter(
-                dot_rows(left, right).astype(bf16), "fsdp", scatter_dimension=side, tiled=True
-            ).astype(f32)
-
-        order = MIXED
-
-        def mixed(x):
-            return jnp.concatenate(
-                [lax.dynamic_slice_in_dim(x, (t ^ j) * part, part, 0) for j in order], axis=0
-            )
-
-        def natural(x):
-            blocks_of = [x[i * part : (i + 1) * part] for i in range(n_t)]
-            place = [blocks_of[order.index(j)] for j in range(n_t)]
-            out = jnp.stack(place)
-            return jnp.concatenate(
-                [lax.dynamic_index_in_dim(out, n ^ t, 0, keepdims=False) for n in range(n_t)],
-                axis=0,
-            )
-
-        def grow(x, axis, bit):
-            return jnp.concatenate([x, flip(x, axis, bit)], axis=0)
+        def grad_far(left, right, side):
+            if n_f > 2:
+                return None
+            source = (left, right)[side]
+            half = width // 2
+            far = lax.dynamic_slice_in_dim(source, (1 - f) * half, half, 1)
+            return (dot_rows(far, right) if side == 0 else dot_rows(left, far)).astype(bf16)
+
+        def grad_sum(left, right, side, far):
+            if n_f > 2:
+                return lax.psum_scatter(
+                    dot_rows(left, right).astype(bf16), "fsdp", scatter_dimension=side, tiled=True
+                )
+            source = (left, right)[side]
+            half = width // 2
+            own = lax.dynamic_slice_in_dim(source, f * half, half, 1)
+            own = dot_rows(own, right) if side == 0 else dot_rows(left, own)
+            return (own + flip(far, "fsdp", 1).astype(f32)).astype(bf16)
 
         small = jnp.concatenate(
             [v.reshape(1, -1) for v in (attn_gain, ffn_gain, b_query, b_key, b_value)], axis=1
@@ -918,7 +960,8 @@
             else [lax.all_gather(x, "fsdp", axis=axis, tiled=True)]
         )
         meta = jnp.stack([f, 1 - f, core, pair]).astype(jnp.int32)
-        w_qkv = pieces_f(jnp.concatenate([w_query, w_kv_own], axis=1), 0)
+        w_q = pieces_f(w_query, 0)
+        w_kv = pieces_f(w_kv_own, 0)
         small = gather_f(small, 0)
         w_out_all = gather_f(w_out, 1)
         piece = attn_gain.shape[0]
@@ -939,13 +982,9 @@
 
         unit_slice = lambda w: lax.dynamic_slice_in_dim(w, parity * units, units, 0)
         own_units = jnp.concatenate([unit_slice(w) for w in (w_gate.T, w_up.T, w_down)], axis=0)
-        w_units = pieces_f(after(own_units, w_qkv, small), 1)
-
-        dy_own = mixed(cotangent)[: 2 * part]
-        dy_near = jnp.concatenate([dy_own, flip(dy_own, "context", 1)], axis=0)
-        dy_pair = grow(dy_near, "tensor", 1)
-        dy_far = grow(grow(flip(dy_own, "context", 2), "context", 1), "tensor", 1)
-        dy_all = jnp.concatenate([dy_pair, dy_far], axis=0).reshape(2, -1, part, width)
+        w_units = pieces_f(after(own_units, w_q, w_kv, small, w_out_all), 1)
+
+        dy_part = lax.dynamic_slice_in_dim(cotangent, t * part, part, 0)
 
         seq_blocks = blocks[0].reshape(n_c, -1)
         own_blocks = seq_blocks.shape[1]
@@ -958,56 +997,63 @@
         cosine, sine = rope_tables(positions)
         bias = jnp.concatenate([bq.reshape(1, -1), b_kv], axis=1)
         normed, factor_first, queries, kv_own = qkv(
-            meta, inputs, gain_first, bias, cosine, sine, w_qkv
+            meta, inputs, gain_first, bias, cosine, sine, w_q, w_kv
         )
         kv = kv_gather(kv_own)
         attended, lse = attention(key_blocks, queries, kv)
-        attended_mixed = mixed(attended)
         inputs_part = lax.dynamic_slice_in_dim(inputs, t * part, part, 0)
-        middle, factor_second, normed2 = middle_norm(
-            dot(attended_mixed, w_out_all).astype(bf16), inputs_part, gain_second
-        )
-
-        normed2 = normed2.reshape(2, -1, part, width)
-        hid_pair, dg_pair, du_pair, dx_part, out_part = ffn(meta, normed2, dy_all, w_units, True)
-        hid_far, dg_far, du_far = ffn(meta, after(normed2, dx_part), dy_all, w_units, False)
-        grad_args = (normed2, dy_all, (hid_pair, hid_far), (dg_pair, dg_far), (du_pair, du_far))
+        middle, factor_second, normed2, dy_all = middle_norm(
+            dot(attended, w_out_all).astype(bf16), inputs_part, gain_second, dy_part
+        )
+
+        hidden, grad_gate, grad_up, dx_part, out_part = ffn(meta, normed2, dy_all, w_units)
+        down, gate_up = [hidden], [grad_gate, grad_up]
         if n_f == 2:
-            unit_sent = unit_grads(meta, 1, 2, *grad_args)
-            unit_got = [flip(x, "fsdp", 1) for x in unit_sent]
-            unit_own = unit_grads(meta, 0, 2, *after(grad_args, unit_sent))
-            dx_part = after(dx_part, unit_own)
+            down_sent = unit_grads(meta, 1, 2, dy_all, down)
+            down_got = flip(down_sent, "fsdp", 1)
+            gate_up_sent = unit_grads(meta, 1, 2, *after((normed2, gate_up), down_sent))
+            gate_up_got = flip(gate_up_sent, "fsdp", 1)
+            dx_part = after(dx_part, gate_up_sent)
         else:
-            unit_own = [
-                lax.psum_scatter(x, "fsdp", scatter_dimension=1, tiled=True)
-                for x in unit_grads(meta, 0, 1, *grad_args)
-            ]
-            unit_got = [jnp.zeros_like(x) for x in unit_own]
-
-        unit_sum = lambda own, got: (own.astype(f32) + got.astype(f32)).astype(bf16)
+            over_f = lambda x: lax.psum_scatter(x, "fsdp", scatter_dimension=1, tiled=True)
+            down_own = over_f(unit_grads(meta, 0, 1, dy_all, down))
+            gate_up_own = over_f(unit_grads(meta, 0, 1, normed2, gate_up))
+            down_got, gate_up_got = jnp.zeros_like(down_own), jnp.zeros_like(gate_up_own)
+
+        def unit_done(own, got):
+            low = (own.astype(f32) + got.astype(f32)).astype(bf16)
+            return low, flip(low, "context", 1)
+
         unit_whole = lambda low, other: by_bit(parity, low, other, 0).astype(f32)
 
-        dy_part = lax.dynamic_slice_in_dim(cotangent, t * part, part, 0)
-        grad_middle, ffn_gain_grad, grad_middle_low, outputs = middle_back(
-            dx_part, out_part, middle, factor_second, gain_second, dy_part
-        )
+        grad_middle, ffn_gain_grad, grad_middle_low = middle_back(
+            dx_part, middle, factor_second, gain_second, dy_part
+        )
+        grad_middle_low = grad_middle_low.reshape(rows, width)
+        if n_f == 2:
+            down_own = unit_grads(meta, 0, 2, *after((dy_all, down), grad_middle_low))
+        down_done = unit_done(down_own, after(down_got, grad_middle_low))
+        grad_attended = dot_cols(after(grad_middle_low, down_done[0]), w_out_all).astype(bf16)
+
+        dq_low, dkv = attention_back(key_blocks, queries, grad_attended, lse, cosine, sine, kv)
+        if n_f == 2:
+            gate_up_own = unit_grads(meta, 0, 2, *after((normed2, gate_up), dkv))
+            dkv = after(dkv, gate_up_own)
+        dkv, outputs = kv_scatter(after(dkv, down_done), out_part, middle)
         outputs = outputs.reshape(rows, width)
-        grad_middle_low = grad_middle_low.reshape(rows, width)
-        unit_low = [unit_sum(unit_own[0], after(unit_got[0], grad_middle_low))]
-        unit_other = [flip(unit_low[0], "context", 1)]
-        grad_attended = natural(
-            dot_cols(after(grad_middle_low, unit_low), w_out_all).astype(bf16)
-        )
-
-        dq_low, dkv = attention_back(key_blocks, queries, grad_attended, lse, cosine, sine, kv)
-        dkv = kv_scatter(dkv)
-        unit_low.append(unit_sum(unit_own[1], after(unit_got[1], dkv)))
-        unit_other.append(flip(unit_low[1], "context", 1))
-        wo_part = grad_f(attended_mixed, after(grad_middle_low, dkv), 1).astype(bf16)
+        gate_up_got = after(gate_up_got, dkv)
+        gate_done, up_done = (
+            unit_done(gate_up_own[k : k + units], gate_up_got[k : k + units]) for k in (0, units)
+        )
+        dkv = after(dkv, gate_done[0], up_done[0])
         dkv_low = jnp.where(core == 0, rotate_back(dkv, cosine, sine), dkv).astype(bf16)
-        wq_part = grad_f(normed, dq_low, 0).astype(bf16)
-        wkv_part = grad_f(normed, dkv_low, 0).astype(bf16)
-        d_qkv = mixed(jnp.concatenate([dq_low, dkv_low], axis=1))
+        attention_args = (
+            (attended, after(grad_middle_low, dkv), 1),
+            (normed, after(dq_low, dkv), 0),
+            (normed, dkv_low, 0),
+        )
+        fars = [grad_far(*args) for args in attention_args]
+        dkv_low = after(dkv_low, fars)
         factor_part = lax.dynamic_slice_in_dim(factor_first, t * part, part, 0)
         own_biases = jnp.sum(
             jnp.concatenate([dq_low, dkv_low], axis=1).astype(f32), axis=0, keepdims=True
@@ -1019,7 +1065,7 @@
             [jnp.zeros((1, width), f32), ffn_gain_grad, slots.reshape(1, -1)], axis=1
         )
         small_grads, input_grad = input_back(
-            columns_f([dot_cols(d_qkv, w) for w in w_qkv]),
+            qkv_back(meta, dq_low, dkv_low, w_q, w_kv),
             inputs_part,
             factor_part,
             gain_first,
@@ -1029,10 +1075,15 @@
         input_grad = input_grad.reshape(rows, width)
         if n_f > 2:
             small_grads = lax.psum(small_grads, "fsdp")
-        wo_grad, wq_grad, _, packed, wkv_all = context_sum(
-            n_f == 2, (wo_part, wq_part, wkv_part), small_grads
-        )
-        wo_grad, wq_grad, wkv_all = (x.astype(f32) for x in (wo_grad, wq_grad, wkv_all))
+        attention_parts = [grad_sum(*args, far) for args, far in zip(attention_args, fars)]
+        wd_grad = unit_whole(*after(down_done, small_grads))
+        small_grads, gate_done, up_done = lax.optimization_barrier(
+            (small_grads, gate_done, up_done)
+        )
+        wo_grad, wq_grad, packed, wkv_all = context_sum(
+            n_f == 2, attention_parts, after(small_grads, wd_grad)
+        )
+        wkv_all = wkv_all.astype(f32)
         wk_grad = jnp.concatenate([wkv_all[0], wkv_all[2]], axis=1)
         wv_grad = jnp.concatenate([wkv_all[1], wkv_all[3]], axis=1)
         packed = packed[0]
@@ -1044,12 +1095,7 @@
         bk_out = slots[0::2, heads]
         bv_out = slots[1::2, heads]
 
-        shares = [
-            (low[k : k + units], other[k : k + units])
-            for low, other in zip(unit_low, unit_other)
-            for k in range(0, low.shape[0], units)
-        ]
-        wg_grad, wu_grad, wd_grad = (unit_whole(*share) for share in shares)
+        wg_grad, wu_grad = unit_whole(*gate_done), unit_whole(*up_done)
         wg_grad, wu_grad = wg_grad.T, wu_grad.T
 
         return (

time: 612 us -> 556 us (0.908)
  waiting for transfers between devices: 79.5 us -> 54.5 us
  local copies, waits for them, and re-layouts: 36 us -> 26.2 us
  Pallas kernels: 406 us -> 398 us
    ppermute x16 -> x13, waiting for transfers between devices: 79.5 us -> 54.5 us  [flip(): return lax.ppermute(x, axis, [(i, i ^ bit) for i in range(size)])]
    pallas_call x6, Pallas kernels: 281 us -> 269 us  [remote_call(): pl.pallas_call(kernel, name=name, out_shape=outs, in_specs=[spec(x) for x...]
    concatenate x6 -> x0, other arithmetic: 6.27 us -> none  [the longest x1 2.01 us: local(): w_qkv = pieces_f(jnp.concatenate([w_query, w_kv_own], axis=1), 0)]
    unnamed x71 -> x61, local copies, waits for them, and re-layouts: 16.7 us -> 11.4 us
    pallas_call x5 -> x7, Pallas kernels: 99.7 us -> 104 us  [the longest x1 47.2 us: ffn(): pl.pallas_call(functools.partial(ffn_kernel, len(weights)), name='ffn', g...]
    ppermute x16 -> x13, starting transfers between devices: 18.3 us -> 14.6 us  [flip(): return lax.ppermute(x, axis, [(i, i ^ bit) for i in range(size)])]
  transfers between devices with their start and end apart: 16 -> 13, of which waited for: 4 -> 4; matrix products, arithmetic and copies ran while one was open for 13% -> 8% of each run, Pallas kernels for 55% -> 49%
where the time goes in v5:
time: 556 us; the launch traced here: 549 us
  Pallas kernels  398 us (72%)
  waiting for transfers between devices  54.5 us (10%)
  other arithmetic  37.9 us (7%)
  local copies, waits for them, and re-layouts  26.2 us (5%)
  matrix products  17.1 us (3%)
  starting transfers between devices  14.6 us (3%)
    pallas_call x6, Pallas kernels, remote_call(): pl.pallas_call(kernel, name=name, out_shape=outs, in_specs=[spec(x) for x...  269 us
    ppermute x13, waiting for transfers between devices, flip(): return lax.ppermute(x, axis, [(i, i ^ bit) for i in range(size)])  54.5 us
    pallas_call x1, Pallas kernels, ffn(): pl.pallas_call(functools.partial(ffn_kernel, len(weights)), name='ffn', g...  47.2 us
    pallas_call x4, Pallas kernels, unit_grads(): pl.pallas_call(functools.partial(unit_grads_kernel, count), name=f'unit_g...  46 us
    pallas_call x1, Pallas kernels, attention_back(): pl.pallas_call(functools.partial(attention_back_kernel, kv.shape[1] // BL...  15 us
    ppermute x13, starting transfers between devices, flip(): return lax.ppermute(x, axis, [(i, i ^ bit) for i in range(size)])  14.6 us
    unnamed x61, local copies, waits for them, and re-layouts  11.4 us
  transfers between devices with their start and end apart: 13, of which 4 were waited for; matrix products, arithmetic and copies ran while one was open for 8% of the time, Pallas kernels for 49%

profile of v5, /device:TPU:0, one launch (start us, length us, event | category | flops | bytes accessed | tf_op | source)
XLA Modules:
  0.0 549.4 jit_solution(11276013097765020506)
XLA Ops:
  4.7 3.0 collective-permute-start
  9.4 2.0 collective-permute-start.3
  15.1 2.6 pad_maximum_fusion.refs_0_.refs_2_.refs_4_
  17.8 12.4 %collective-permute-done.3 = bf16[384,768]{1,0:T(8,128)(2,1)} collective-permute-done((bf16[384,768]{1,0:T(8,128)(2,1)}, bf16[384,768]{1,0:T(8,128)(2,1)}, u32[]{:S(2)}, u32[]{:S(2)}) %collective-permute-start.3) | collective-permute-done | bytes 589856 | tf_op jit(solution)/shard_map/ppermute | solution.py:888
  32.1 9.2 %collective-permute-done.1.refs_1_ = bf16[768,384]{1,0:T(8,128)(2,1)} collective-permute-done((bf16[768,384]{1,0:T(8,128)(2,1)}, bf16[768,384]{1,0:T(8,128)(2,1)}, u32[]{:S(2)}, u32[]{:S(2)}) %collective-permute-start.1) | collective-permute-done | bytes 589856 | tf_op jit(solution)/shard_map/ppermute | solution.py:888
  52.1 5.8 %qkv.1 = (bf16[512,1536]{1,0:T(8,128)(2,1)}, f32[512,1]{1,0:T(8,128)}, bf16[512,384]{1,0:T(8,128)(2,1)}, bf16[512,128]{1,0:T(8,128)(2,1)}) custom-call(s32[4]{0:T(128)} %pad_add_fusion.1.meta_ref, bf16[512,1536]{1,0:T(8,128)(2,1)} %x_ref.1, f32[1,1536]{1,0:T(1,128)} %bitcast.95, f32[1,512]{1,0:T(1,128)} %pad_maximum_fusion.6.bias_ref, ...), custom_call_target="tpu_custom_call" | custom-call | tf_op jit(solution)/shard_map/qkv/pallas_call | solution.py:209
  57.9 17.4 %kv_gather.1.k_ref.v_ref = bf16[2,2048,128]{2,1,0:T(8,128)(2,1)} custom-call(bf16[512,128]{1,0:T(8,128)(2,1)} %get-tuple-element.70.own_ref), custom_call_target="tpu_custom_call" | custom-call | tf_op jit(solution)/shard_map/kv_gather/pallas_call | solution.py:518
  75.3 10.2 %attention.1 = (bf16[512,384]{1,0:T(8,128)(2,1)}, f32[3,512,1]{2,1,0:T(8,128)}) custom-call(s32[8]{0:T(128)} %pad_add_fusion.kb_ref, bf16[512,384]{1,0:T(8,128)(2,1)} %get-tuple-element.69.q_ref, bf16[2,2048,128]{2,1,0:T(8,128)(2,1)} %kv_gather.1.k_ref.v_ref, bf16[2,2048,128]{2,1,0:T(8,128)(2,1)} %kv_gather.1.k_ref.v_ref), custom_call_target="tpu_custom_call" | custom-call | tf_op jit(solution)/shard_map/attention/pallas_call | solution.py:85
  85.5 3.1 convolution_convert_fusion
  88.6 76.0 %middle_norm.1 = (f32[128,1536]{1,0:T(8,128)}, f32[128,1]{1,0:T(8,128)}, bf16[16,128,1536]{2,1,0:T(8,128)(2,1)}, bf16[16,128,1536]{2,1,0:T(8,128)(2,1)}) custom-call(bf16[4,128,1536]{2,1,0:T(8,128)(2,1)} %bitcast.87, bf16[128,1536]{1,0:T(8,128)(2,1)} %constant_dynamic-slice_fusion.7.x_ref, f32[1,1536]{1,0:T(1,128)} %bitcast.93, ...), custom_call_target="tpu_custom_call" | custom-call | tf_op jit(solution)/shard_map/middle_norm/pallas_call | solution.py:518
  164.7 47.2 %ffn.1 = (bf16[2048,1120]{1,0:T(8,128)(2,1)}, bf16[2048,1120]{1,0:T(8,128)(2,1)}, bf16[2048,1120]{1,0:T(8,128)(2,1)}, bf16[1024,1536]{1,0:T(8,128)(2,1)}, bf16[1024,1536]{1,0:T(8,128)(2,1)}) custom-call(s32[4]{0:T(128)} %pad_add_fusion.1.meta_ref, bf16[2048,1536]{1,0:T(8,128)(2,1)} %bitcast.76, bf16[2048,1536]{1,0:T(8,128)(2,1)} %bitcast.81, ...), custom_call_target="tpu_custom_call" | custom-call | tf_op jit(solution)/shard_map/ffn/pallas_call | solution.py:291
  211.9 8.7 %unit_grads_1_1.1 = bf16[1120,768]{1,0:T(8,128)(2,1)} custom-call(s32[4]{0:T(128)} %pad_add_fusion.1.meta_ref, bf16[2048,1536]{1,0:T(8,128)(2,1)} %bitcast.82, bf16[2048,1536]{1,0:T(8,128)(2,1)} %bitcast.83, bf16[2048,1120]{1,0:T(8,128)(2,1)} %get-tuple-element.87.refs_0_), custom_call_target="tpu_custom_call" | custom-call | tf_op jit(solution)/shard_map/unit_grads_1_1/pallas_call | solution.py:328
  222.4 14.4 %unit_grads_1_2.1 = bf16[2240,768]{1,0:T(8,128)(2,1)} custom-call(s32[4]{0:T(128)} %pad_add_fusion.1.meta_ref, bf16[2048,1536]{1,0:T(8,128)(2,1)} %bitcast.77, bf16[2048,1536]{1,0:T(8,128)(2,1)} %bitcast.78, bf16[2048,1120]{1,0:T(8,128)(2,1)} %get-tuple-element.93.refs_0_, bf16[2048,1120]{1,0:T(8,128)(2,1)} %get-tuple-element.94.refs_1_), custom_call_target="tpu_custom_call" | custom-call | tf_op jit(solution)/shard_map/unit_grads_1_2/pallas_call | solution.py:328
  236.9 32.2 %middle_back.1 = (f32[128,1536]{1,0:T(8,128)}, f32[1,1536]{1,0:T(1,128)}, bf16[4,128,1536]{2,1,0:T(8,128)(2,1)}) custom-call(bf16[8,128,1536]{2,1,0:T(8,128)(2,1)} %bitcast.89, f32[128,1536]{1,0:T(8,128)} %get-tuple-element.83.mid_ref, f32[128,1]{1,0:T(8,128)} %get-tuple-element.84.factor_ref, f32[1,1536]{1,0:T(1,128)} %bitcast.94, ...), custom_call_target="tpu_custom_call" | custom-call | tf_op jit(solution)/shard_map/middle_back/pallas_call | solution.py:518
  269.2 8.7 %unit_grads_0_1.1 = bf16[1120,768]{1,0:T(8,128)(2,1)} custom-call(s32[4]{0:T(128)} %pad_add_fusion.1.meta_ref, bf16[2048,1536]{1,0:T(8,128)(2,1)} %bitcast.84, bf16[2048,1536]{1,0:T(8,128)(2,1)} %bitcast.85, bf16[2048,1120]{1,0:T(8,128)(2,1)} %get-tuple-element.87.refs_0_), custom_call_target="tpu_custom_call" | custom-call | tf_op jit(solution)/shard_map/unit_grads_0_1/pallas_call | solution.py:328
  277.9 2.4 add_convert_fusion.2
  283.2 3.2 convolution_convert_fusion.3.do_ref
  286.4 15.0 %attention_back.1 = (bf16[512,384]{1,0:T(8,128)(2,1)}, bf16[2,2048,128]{2,1,0:T(8,128)(2,1)}) custom-call(s32[8]{0:T(128)} %pad_add_fusion.kb_ref, bf16[512,384]{1,0:T(8,128)(2,1)} %get-tuple-element.69.q_ref, bf16[512,384]{1,0:T(8,128)(2,1)} %convolution_convert_fusion.3.do_ref, f32[3,512,1]{2,1,0:T(8,128)} %get-tuple-element.90.lse_ref, ...), custom_call_target="tpu_custom_call" | custom-call | tf_op jit(solution)/shard_map/attention_back/pallas_call | solution.py:151
  301.3 14.3 %unit_grads_0_2.1 = bf16[2240,768]{1,0:T(8,128)(2,1)} custom-call(s32[4]{0:T(128)} %pad_add_fusion.1.meta_ref, bf16[2048,1536]{1,0:T(8,128)(2,1)} %bitcast.79, bf16[2048,1536]{1,0:T(8,128)(2,1)} %bitcast.80, bf16[2048,1120]{1,0:T(8,128)(2,1)} %get-tuple-element.93.refs_0_, bf16[2048,1120]{1,0:T(8,128)(2,1)} %get-tuple-element.94.refs_1_), custom_call_target="tpu_custom_call" | custom-call | tf_op jit(solution)/shard_map/unit_grads_0_2/pallas_call | solution.py:328
  315.6 4.8 collective-permute-done.6
  320.4 40.5 %kv_scatter.1 = (f32[512,128]{1,0:T(8,128)}, bf16[4,128,1536]{2,1,0:T(8,128)(2,1)}) custom-call(bf16[2,2048,128]{2,1,0:T(8,128)(2,1)} %get-tuple-element.96.part_ref, bf16[8,128,1536]{2,1,0:T(8,128)(2,1)} %bitcast.88, f32[128,1536]{1,0:T(8,128)} %get-tuple-element.83.mid_ref), custom_call_target="tpu_custom_call" | custom-call | tf_op jit(solution)/shard_map/kv_scatter/pallas_call | solution.py:518
  361.0 4.6 add_convert_fusion
  377.6 4.7 qkv_back.1
  382.3 28.7 %input_back.1 = (f32[1,5120]{1,0:T(1,128)}, bf16[4,128,1536]{2,1,0:T(8,128)(2,1)}) custom-call(bf16[4,128,1536]{2,1,0:T(8,128)(2,1)} %bitcast.86, bf16[128,1536]{1,0:T(8,128)(2,1)} %constant_dynamic-slice_fusion.7.x_ref, f32[128,1]{1,0:T(8,128)} %constant_dynamic-slice_fusion.4.factor_ref, f32[1,1536]{1,0:T(1,128)} %bitcast.96, ...), custom_call_target="tpu_custom_call" | custom-call | tf_op jit(solution)/shard_map/input_back/pallas_call | solution.py:518
  411.0 4.8 fusion
  415.9 2.1 fusion.3.refs_2_
  418.0 2.4 fusion.1.refs_0_
  420.4 2.5 fusion.2.refs_1_
  422.9 28.1 %collective-permute-done.11 = bf16[1120,768]{1,0:T(8,128)(2,1)} collective-permute-done((bf16[1120,768]{1,0:T(8,128)(2,1)}, bf16[1120,768]{1,0:T(8,128)(2,1)}, u32[]{:S(2)}, u32[]{:S(2)}) %collective-permute-start.11) | collective-permute-done | bytes 1720352 | tf_op jit(solution)/shard_map/ppermute | solution.py:888
  451.0 73.9 %context_sum.1 = (f32[384,768]{1,0:T(8,128)}, f32[768,384]{1,0:T(8,128)}, f32[1,5120]{1,0:T(1,128)}, bf16[4,768,128]{2,1,0:T(8,128)(2,1)}) custom-call(bf16[384,768]{1,0:T(8,128)(2,1)} %fusion.1.refs_0_, bf16[768,384]{1,0:T(8,128)(2,1)} %fusion.2.refs_1_, bf16[768,128]{1,0:T(8,128)(2,1)} %fusion.3.refs_2_, f32[1,5120]{1,0:T(1,128)} %get-tuple-element.115.refs_3_), custom_call_target="tpu_custom_call" | custom-call | tf_op jit(solution)/shard_map/context_sum/pallas_call | solution.py:518
  531.4 5.4 convert_bitcast_fusion.1
  536.8 5.4 convert_bitcast_fusion
  (138 shorter events, 52.5 us)
Async XLA Ops:
  0.6 10.8 %copy-start = (bf16[2240,768]{1,0:T(8,128)(2,1)S(1)}, bf16[2240,768]{1,0:T(8,128)(2,1)}, u32[]{:S(2)}) copy-start(bf16[2240,768]{1,0:T(8,128)(2,1)} %param.29) | copy-start | bytes 10321924
  4.7 13.1 %collective-permute-start = (bf16[1,1984]{1,0:T(2,128)(2,1)S(1)}, bf16[1,1984]{1,0:T(2,128)(2,1)S(1)}, u32[]{:S(2)}, u32[]{:S(2)}) collective-permute-start(bf16[1,1984]{1,0:T(2,128)(2,1)S(1)} %concatenate.64), channel_id=1, source_target_pairs={{0,16},{16,0},{1,17},{17,1},{2,18},{18,2},{3,19},{19,3},{4,20},{20... | collective-permute-start | bytes 11912 | tf_op jit(solution)/shard_map/ppermute | solution.py:888
  9.4 22.7 %collective-permute-start.2 = (bf16[768,128]{1,0:T(8,128)(2,1)}, bf16[768,128]{1,0:T(8,128)(2,1)}, u32[]{:S(2)}, u32[]{:S(2)}) collective-permute-start(bf16[768,128]{1,0:T(8,128)(2,1)} %dynamic-slice_select_fusion.refs_2_), channel_id=1, source_target_pairs={{0,16},{16,0},{1,17},{17,1},{2,18},{18,2},{3,19},{19,3},{4,20},{20... | collective-permute-start | bytes 589832 | tf_op jit(solution)/shard_map/ppermute | solution.py:888
  9.4 20.7 %collective-permute-start.3 = (bf16[384,768]{1,0:T(8,128)(2,1)}, bf16[384,768]{1,0:T(8,128)(2,1)}, u32[]{:S(2)}, u32[]{:S(2)}) collective-permute-start(bf16[384,768]{1,0:T(8,128)(2,1)} %param.25), channel_id=1, source_target_pairs={{0,16},{16,0},{1,17},{17,1},{2,18},{18,2},{3,19},{19,3},{4,20},{20... | collective-permute-start | bytes 1769480 | tf_op jit(solution)/shard_map/ppermute | solution.py:888
  11.4 29.9 %collective-permute-start.1 = (bf16[768,384]{1,0:T(8,128)(2,1)}, bf16[768,384]{1,0:T(8,128)(2,1)}, u32[]{:S(2)}, u32[]{:S(2)}) collective-permute-start(bf16[768,384]{1,0:T(8,128)(2,1)} %refs_0_.3), channel_id=1, source_target_pairs={{0,16},{16,0},{1,17},{17,1},{2,18},{18,2},{3,19},{19,3},{4,20},{20... | collective-permute-start | bytes 1769480 | tf_op jit(solution)/shard_map/ppermute | solution.py:888
  17.8 24.4 %copy-start.25 = (s32[1,8]{1,0:T(1,128)S(1)}, s32[1,8]{1,0:T(1,128)}, u32[]{:S(2)}) copy-start(s32[1,8]{1,0:T(1,128)} %param.17) | copy-start | bytes 100
  41.3 123.3 %collective-permute-start.4 = (bf16[3360,768]{1,0:T(8,128)(2,1)}, bf16[3360,768]{1,0:T(8,128)(2,1)}, u32[]{:S(2)}, u32[]{:S(2)}) collective-permute-start(bf16[3360,768]{1,0:T(8,128)(2,1)} %pad_maximum_fusion.refs_0_.refs_2_.refs_4_), channel_id=1, source_target_pairs={{0,16},{16,0},{1,17},{17,1},{2,18},{18,2},{3,19},{19,3},{4,20},{20... | collective-permute-start | bytes 15482888 | tf_op jit(solution)/shard_map/ppermute | solution.py:888
  45.2 12.6 %copy-start.7 = (f32[512,64]{1,0:T(8,128)}, f32[512,64]{1,0:T(8,128)S(1)}, u32[]{:S(2)}) copy-start(f32[512,64]{1,0:T(8,128)S(1)} %get-tuple-element.140) | copy-start | bytes 393220
  45.3 12.6 %copy-start.9 = (f32[512,64]{1,0:T(8,128)}, f32[512,64]{1,0:T(8,128)S(1)}, u32[]{:S(2)}) copy-start(f32[512,64]{1,0:T(8,128)S(1)} %get-tuple-element.141) | copy-start | bytes 393220
  220.5 57.4 %collective-permute-start.5 = (bf16[1120,768]{1,0:T(8,128)(2,1)}, bf16[1120,768]{1,0:T(8,128)(2,1)}, u32[]{:S(2)}, u32[]{:S(2)}) collective-permute-start(bf16[1120,768]{1,0:T(8,128)(2,1)} %unit_grads_1_1.1), channel_id=1, source_target_pairs={{0,16},{16,0},{1,17},{17,1},{2,18},{18,2},{3,19},{19,3},{4,20},{20... | collective-permute-start | bytes 5160968 | tf_op jit(solution)/shard_map/ppermute | solution.py:888
  236.7 124.2 %collective-permute-start.7 = (bf16[2240,768]{1,0:T(8,128)(2,1)}, bf16[2240,768]{1,0:T(8,128)(2,1)}, u32[]{:S(2)}, u32[]{:S(2)}) collective-permute-start(bf16[2240,768]{1,0:T(8,128)(2,1)} %unit_grads_1_2.1), channel_id=1, source_target_pairs={{0,16},{16,0},{1,17},{17,1},{2,18},{18,2},{3,19},{19,3},{4,20},{20... | collective-permute-start | bytes 10321928 | tf_op jit(solution)/shard_map/ppermute | solution.py:888
  280.3 6.0 %copy-start.3 = (bf16[1120,768]{1,0:T(8,128)(2,1)}, bf16[1120,768]{1,0:T(8,128)(2,1)S(1)}, u32[]{:S(2)}) copy-start(bf16[1120,768]{1,0:T(8,128)(2,1)S(1)} %add_convert_fusion.2) | copy-start | bytes 5160964
  280.3 40.1 %collective-permute-start.6 = (bf16[1120,768]{1,0:T(8,128)(2,1)S(1)}, bf16[1120,768]{1,0:T(8,128)(2,1)}, u32[]{:S(2)}, u32[]{:S(2)}) collective-permute-start(bf16[1120,768]{1,0:T(8,128)(2,1)S(1)} %add_convert_fusion.2), channel_id=1, source_target_pairs={{0,4},{4,0},{8,12},{12,8},{1,5},{5,1},{9,13},{13,9},{2,6},{6,2},{1... | collective-permute-start | bytes 5160968 | tf_op jit(solution)/shard_map/ppermute | solution.py:888
  320.4 40.6 %copy-start.2 = (bf16[2240,768]{1,0:T(8,128)(2,1)S(1)}, bf16[2240,768]{1,0:T(8,128)(2,1)}, u32[]{:S(2)}) copy-start(bf16[2240,768]{1,0:T(8,128)(2,1)} %unit_grads_0_2.1) | copy-start | bytes 10321924
  360.9 4.6 copy-start.8
  361.0 4.6 copy-start.18
  365.7 4.2 copy-start.14
  366.8 10.0 %copy-start.5 = (bf16[512,128]{1,0:T(8,128)(2,1)}, bf16[512,128]{1,0:T(8,128)(2,1)S(1)}, u32[]{:S(2)}) copy-start(bf16[512,128]{1,0:T(8,128)(2,1)S(1)} %fusion.11.dkv_ref) | copy-start | bytes 393220
  366.8 4.6 copy-start.20
  366.8 4.6 copy-start.23
  368.2 8.8 %copy-start.22 = (f32[1,1536]{1,0:T(1,128)S(1)}, f32[1,1536]{1,0:T(1,128)}, u32[]{:S(2)}) copy-start(f32[1,1536]{1,0:T(1,128)} %get-tuple-element.109) | copy-start | bytes 18436
  368.2 47.7 %collective-permute-start.10 = (bf16[768,128]{1,0:T(8,128)(2,1)}, bf16[768,128]{1,0:T(8,128)(2,1)}, u32[]{:S(2)}, u32[]{:S(2)}) collective-permute-start(bf16[768,128]{1,0:T(8,128)(2,1)} %convolution_convert_fusion.4), channel_id=1, source_target_pairs={{0,16},{16,0},{1,17},{17,1},{2,18},{18,2},{3,19},{19,3},{4,20},{20... | collective-permute-start | bytes 589832 | tf_op jit(solution)/shard_map/ppermute | solution.py:888
  372.7 45.2 %collective-permute-start.8 = (bf16[384,768]{1,0:T(8,128)(2,1)}, bf16[384,768]{1,0:T(8,128)(2,1)}, u32[]{:S(2)}, u32[]{:S(2)}) collective-permute-start(bf16[384,768]{1,0:T(8,128)(2,1)} %convolution_convert_fusion.2), channel_id=1, source_target_pairs={{0,16},{16,0},{1,17},{17,1},{2,18},{18,2},{3,19},{19,3},{4,20},{20... | collective-permute-start | bytes 1769480 | tf_op jit(solution)/shard_map/ppermute | solution.py:888
  373.0 47.4 %collective-permute-start.9 = (bf16[768,384]{1,0:T(8,128)(2,1)}, bf16[768,384]{1,0:T(8,128)(2,1)}, u32[]{:S(2)}, u32[]{:S(2)}) collective-permute-start(bf16[768,384]{1,0:T(8,128)(2,1)} %convolution_convert_fusion.1), channel_id=1, source_target_pairs={{0,16},{16,0},{1,17},{17,1},{2,18},{18,2},{3,19},{19,3},{4,20},{20... | collective-permute-start | bytes 1769480 | tf_op jit(solution)/shard_map/ppermute | solution.py:888
  374.8 48.1 %collective-permute-start.12 = (bf16[1120,768]{1,0:T(8,128)(2,1)}, bf16[1120,768]{1,0:T(8,128)(2,1)}, u32[]{:S(2)}, u32[]{:S(2)}) collective-permute-start(bf16[1120,768]{1,0:T(8,128)(2,1)} %get-tuple-element.122), channel_id=1, source_target_pairs={{0,4},{4,0},{8,12},{12,8},{1,5},{5,1},{9,13},{13,9},{2,6},{6,2},{1... | collective-permute-start | bytes 5160968 | tf_op jit(solution)/shard_map/ppermute | solution.py:888
  376.0 75.0 %collective-permute-start.11 = (bf16[1120,768]{1,0:T(8,128)(2,1)}, bf16[1120,768]{1,0:T(8,128)(2,1)}, u32[]{:S(2)}, u32[]{:S(2)}) collective-permute-start(bf16[1120,768]{1,0:T(8,128)(2,1)} %get-tuple-element.120), channel_id=1, source_target_pairs={{0,4},{4,0},{8,12},{12,8},{1,5},{5,1},{9,13},{13,9},{2,6},{6,2},{1... | collective-permute-start | bytes 5160968 | tf_op jit(solution)/shard_map/ppermute | solution.py:888
  382.3 28.7 %copy-start.4 = (bf16[1120,768]{1,0:T(8,128)(2,1)S(1)}, bf16[1120,768]{1,0:T(8,128)(2,1)}, u32[]{:S(2)}) copy-start(bf16[1120,768]{1,0:T(8,128)(2,1)} %copy-done.3) | copy-start | bytes 5160964
  411.0 4.9 copy-start.6
  411.0 6.9 %copy-start.21 = (bf16[512,384]{1,0:T(8,128)(2,1)S(1)}, bf16[512,384]{1,0:T(8,128)(2,1)}, u32[]{:S(2)}) copy-start(bf16[512,384]{1,0:T(8,128)(2,1)} %get-tuple-element.71) | copy-start | bytes 1179652
  411.0 6.9 %copy-start.24 = (bf16[4,128,1536]{2,1,0:T(8,128)(2,1)S(1)}, bf16[4,128,1536]{2,1,0:T(8,128)(2,1)}, u32[]{:S(2)}) copy-start(bf16[4,128,1536]{2,1,0:T(8,128)(2,1)} %get-tuple-element.85) | copy-start | bytes 4718596
  415.9 4.5 copy-start.15
  536.8 5.4 copy-start.11
  (7 other events, 13.0 us)

commit v6 on v5

--- a/solution.py
+++ b/solution.py
@@ -18,6 +18,7 @@
 SCALING = HD ** (-0.5)
 LANES = 128
 VMEM_LIMIT = 60 << 20
+FFN_VMEM_LIMIT = 63 << 20
 
 f32 = jnp.float32
 bf16 = jnp.bfloat16
@@ -255,7 +256,8 @@
 
 def ffn_kernel(pieces, meta_ref, x_ref, dy_ref, *refs):
     wg, wu, wd = (refs[m * pieces : (m + 1) * pieces] for m in range(3))
-    hid_ref, dg_ref, du_ref, dx_ref, out_ref = refs[-5:]
+    refs = refs[3 * pieces :]
+    hid_ref, dg_ref, du_ref, dx_ref, out_ref = refs[:5]
     columns = [columns_of(meta_ref, j, wg[j].shape[1], pieces) for j in range(pieces)]
     gate = sum(dot_cols(x_ref[:, at], w[...]) for at, w in zip(columns, wg))
     up = sum(dot_cols(x_ref[:, at], w[...]) for at, w in zip(columns, wu))
@@ -265,41 +267,61 @@
     hid_ref[...] = (gated * up).astype(bf16)
     dg_ref[...] = (grad_hidden * up * (sigma + gated * (1.0 - sigma))).astype(bf16)
     du_ref[...] = (grad_hidden * gated).astype(bf16)
-
-    @pl.when(pl.program_id(0) < pl.num_programs(0) // 2)
+    step, steps = pl.program_id(0), pl.num_programs(0)
+
+    @pl.when(step // (steps // 2) == meta_ref[3])
     def _():
         for at, g, u, d in zip(columns, wg, wu, wd):
             dx_ref[:, at] = (dot(dg_ref[...], g[...]) + dot(du_ref[...], u[...])).astype(bf16)
             out_ref[:, at] = dot(hid_ref[...], d[...]).astype(bf16)
 
+    if pieces == 2:
+        outs, totals = refs[5:8], refs[8:11]
+        sources = ((hid_ref, dy_ref), (dg_ref, x_ref), (du_ref, x_ref))
+
+        @pl.when(step == 0)
+        def _():
+            for total in totals:
+                total[...] = jnp.zeros_like(total)
+
+        for total, (unit, row) in zip(totals, sources):
+            total[...] += dot_rows(unit[...], row[:, columns[1]])
+
+        @pl.when(step == steps - 1)
+        def _():
+            for out, total in zip(outs, totals):
+                out[...] = total[...].astype(bf16)
+
 
 def ffn(meta, normed, grad_out, weights):
     width = normed.shape[-1]
     rows = normed.shape[0] * normed.shape[1]
-    units = weights[0].shape[0] // 3
+    pieces = len(weights)
+    units, depth = weights[0].shape[0] // 3, weights[0].shape[1]
     tile = 512
     steps = rows // tile
+    half = steps // 2
     flat = lambda x: x.reshape(-1, width)
-    read = pl.BlockSpec((tile, width), lambda i, m: (i, 0))
-    weight = lambda w, k: pl.BlockSpec(
-        (units, w.shape[1]), lambda i, m: (k, 0), pipeline_mode=pl.Buffered(1)
-    )
-    placed = pl.BlockSpec(
-        (tile, units), lambda i, m: (lax.rem(i + m[3] * (steps // 2), steps), 0)
-    )
-    near = pl.BlockSpec((tile, width), lambda i, m: (jnp.minimum(i, steps // 2 - 1), 0))
+    read = pl.BlockSpec((tile, width), lambda i, m: (lax.rem(i + m[3] * half, steps), 0))
+    once = pl.Buffered(1)
+    weight = lambda w, k: pl.BlockSpec((units, depth), lambda i, m: (k, 0), pipeline_mode=once)
+    placed = pl.BlockSpec((tile, units), lambda i, m: (i, 0))
+    near = pl.BlockSpec((tile, width), lambda i, m: (jnp.clip(i - m[3] * half, 0, half - 1), 0))
+    grads = [pl.BlockSpec((units, depth), lambda i, m: (0, 0), pipeline_mode=once)] * 3
+    grads = grads if pieces == 2 else []
+    shapes = [(rows, units)] * 3 + [(rows // 2, width)] * 2 + [(units, depth)] * len(grads)
     return pl.pallas_call(
-        functools.partial(ffn_kernel, len(weights)),
+        functools.partial(ffn_kernel, pieces),
         name="ffn",
         grid_spec=pltpu.PrefetchScalarGridSpec(
             num_scalar_prefetch=1,
             grid=(steps,),
             in_specs=[read, read] + [weight(w, k) for k in range(3) for w in weights],
-            out_specs=[placed] * 3 + [near] * 2,
+            out_specs=[placed] * 3 + [near] * 2 + grads,
+            scratch_shapes=[pltpu.VMEM((units, depth), f32)] * len(grads),
         ),
-        out_shape=[jax.ShapeDtypeStruct((rows, units), bf16)] * 3
-        + [jax.ShapeDtypeStruct((rows // 2, width), bf16)] * 2,
-        compiler_params=pltpu.CompilerParams(vmem_limit_bytes=VMEM_LIMIT),
+        out_shape=[jax.ShapeDtypeStruct(shape, bf16) for shape in shapes],
+        compiler_params=pltpu.CompilerParams(vmem_limit_bytes=FFN_VMEM_LIMIT),
     )(meta, flat(normed), flat(grad_out), *(list(weights) * 3))
 
 
@@ -566,29 +588,24 @@
     )[0]
 
 
-def kv_scatter_kernel(
-    part_ref, out_part, mid_ref, dkv_ref, outputs, own, got_core, sent, got, low, *rest
-):
-    first, wires, to = rest[:7], Wires(*rest[7:]), partners()
+def kv_scatter_kernel(part_ref, dkv_ref, own, got_core, sent, got, *sems):
+    wires, to = Wires(*sems), partners()
     kind = lax.rem(lax.axis_index("tensor"), 2)
     rows = dkv_ref.shape[0]
     block = lambda j: pl.ds(j * rows, rows)
-    meet([to[k] for k in ("core", "y", "z", "far", "last")])
+    meet([to[k] for k in ("core", "z", "far", "last")])
     steps = ((3, "last"), (2, "far"), (1, "z"), (0, None))
     from_core = {
         j: wires.copy(part_ref.at[1 - kind, block(j)], got_core.at[block(j)], to["core"])
         for j, _ in steps
     }
     mine = wires.here(part_ref.at[kind], own)
-    ahead = scatter_pair(wires, to, out_part, *first)
-    next(ahead)
     mine.wait()
     arrive = []
     for j, k in steps[:3]:
         from_core[j].wait_recv()
         sent[block(j)] = (wide(own[block(j)]) + wide(got_core[block(j)])).astype(bf16)
         arrive.append(wires.copy(sent.at[block(j)], got.at[block(j)], to[k]))
-    next(ahead)
     from_core[0].wait_recv()
     total = wide(own[block(0)]) + wide(got_core[block(0)])
     for one in arrive:
@@ -596,30 +613,22 @@
     for j in (1, 2, 3):
         total = total + wide(got[block(j)])
     dkv_ref[...] = total
-    low[...] = (mid_ref[...] + result_of(ahead)).astype(bf16)
-    result_of(gather_rank(wires, to, low, outputs))
     wires.finish()
 
 
-def kv_scatter(part, out_part, middle):
+def kv_scatter(part):
     _, rows, width = part.shape
     n_c = lax.axis_size("context")
-    out_rows, out_width = middle.shape
     return remote_call(
         kv_scatter_kernel,
         "kv_scatter",
         1,
-        [part, out_part.reshape(8, out_rows, out_width), middle],
-        [
-            jax.ShapeDtypeStruct((rows // n_c, width), f32),
-            jax.ShapeDtypeStruct((4, out_rows, out_width), bf16),
-        ],
-        [pltpu.VMEM((rows, width), bf16)] * 4
-        + [pltpu.VMEM((out_rows, out_width), bf16)]
-        + pair_scratch(out_rows, out_width),
-        24,
-        ([False, False, True], [True, False]),
-    )
+        [part],
+        [jax.ShapeDtypeStruct((rows // n_c, width), f32)],
+        [pltpu.VMEM((rows, width), bf16)] * 4,
+        7,
+        ([False], [True]),
+    )[0]
 
 
 def middle_kernel(
@@ -798,46 +807,67 @@
 
 
 def context_sum_kernel(over_f, *refs):
-    parts, small_ref, outs, sum_ref, shared = refs[:3], refs[3], refs[4:6], refs[6], refs[7]
-    lows, from_end, from_middle, slots = refs[8:11], refs[11:14], refs[14:17], refs[17]
-    wires, to, c = Wires(*refs[18:]), partners(), lax.axis_index("context")
-    last = lax.axis_size("context") - 1
-    end = (c == 0) | (c == last)
-    greet = ["core", "y", "z", "far", "last"]
+    parts, small_ref, out_part, mid_ref = refs[:3], refs[3], refs[4], refs[5]
+    outs, sum_ref, shared, outputs = refs[6:8], refs[8], refs[9], refs[10]
+    lows, from_end, from_middle = refs[11:15], refs[15:19], refs[19:23]
+    out_low, slot, scratch = refs[23], refs[24], refs[25:32]
+    wires, to, c = Wires(*refs[32:]), partners(), lax.axis_index("context")
+    end = (c == 0) | (c == lax.axis_size("context") - 1)
+    inner = jnp.logical_not(end)
+    greet = ["core", "y", "z", "last"]
     if over_f:
         to["f"] = {"fsdp": 1 - lax.axis_index("fsdp")}
         greet.append("f")
     meet([to[k] for k in greet])
+    ahead = scatter_pair(wires, to, out_part, *scratch)
+    next(ahead)
+    sum_ref[...] = small_ref[...]
+    from_f = wires.copy(small_ref, slot, to["f"]) if over_f else None
+    next(ahead)
+    sources = [*parts, sum_ref]
     chunks = []
-    for i, cuts in ((2, 1), (0, 2), (1, 2)):
-        size = parts[i].shape[0] // cuts
+    for i, cuts in ((2, 1), (0, 2), (1, 2), (3, 1)):
+        size = sources[i].shape[0] // cuts
         chunks += [(i, pl.ds(k * size, size)) for k in range(cuts)]
-    inward = [wires.plan(parts[i].at[at], from_end[i].at[at], to["z"]) for i, at in chunks]
+    inward = [wires.plan(sources[i].at[at], from_end[i].at[at], to["z"]) for i, at in chunks]
     across = [wires.plan(lows[i].at[at], from_middle[i].at[at], to["last"]) for i, at in chunks]
     outward = [wires.plan(lows[i].at[at], lows[i].at[at], to["z"]) for i, at in chunks]
-
-    @pl.when(end)
+    small = len(chunks) - 1
+
+    def send_in(k):
+        @pl.when(end)
+        def _():
+            inward[k].start()
+
+    for k in range(small):
+        send_in(k)
+    next(ahead)
+    if over_f:
+        from_f.wait_recv()
+        sum_ref[...] = sum_ref[...] + slot[...]
+    send_in(small)
+    out_low[...] = (mid_ref[...] + result_of(ahead)).astype(bf16)
+    out_share = gather_rank(wires, to, out_low, outputs)
+    next(out_share)
+
+    @pl.when(inner)
     def _():
-        for one in inward:
-            one.start()
-
-    @pl.when(jnp.logical_not(end))
-    def _():
+        def send_out(k):
+            i, at = chunks[k]
+            across[k].wait()
+            lows[i][at] = (wide(lows[i][at]) + wide(from_middle[i][at])).astype(lows[i].dtype)
+            outward[k].start()
+
         for k, (i, at) in enumerate(chunks):
             inward[k].wait_recv()
-            lows[i][at] = (wide(parts[i][at]) + wide(from_end[i][at])).astype(bf16)
+            total = wide(sources[i][at]) + wide(from_end[i][at])
+            lows[i][at] = total.astype(lows[i].dtype)
             across[k].start()
-
-    sum_ref[...] = small_ref[...]
-    add_all(wires, [to[k] for k in (("f",) if over_f else ()) + ("z", "far")], sum_ref, slots)
-
-    @pl.when(jnp.logical_not(end))
-    def _():
-        for k, (i, at) in enumerate(chunks):
-            across[k].wait_recv()
-            across[k].wait_send()
-            lows[i][at] = (wide(lows[i][at]) + wide(from_middle[i][at])).astype(bf16)
-            outward[k].start()
+            if k:
+                send_out(k - 1)
+        send_out(small)
+
+    result_of(out_share)
 
     def arrived(k):
         @pl.when(end)
@@ -849,16 +879,18 @@
     next(share)
     for k in range(1, len(chunks)):
         arrived(k)
-    for i in (0, 1):
-        outs[i][...] = wide(lows[i][...])
-    result_of(share)
 
     @pl.when(end)
     def _():
         for one in inward:
             one.wait_send()
 
-    @pl.when(jnp.logical_not(end))
+    for i in (0, 1):
+        outs[i][...] = wide(lows[i][...])
+    sum_ref[...] = lows[3][...]
+    result_of(share)
+
+    @pl.when(inner)
     def _():
         for one in outward:
             one.wait_send()
@@ -866,19 +898,23 @@
     wires.finish()
 
 
-def context_sum(over_f, parts, small):
-    like = lambda x: pltpu.VMEM(x.shape, bf16)
+def context_sum(over_f, parts, small, out_part, middle):
+    rows, width = middle.shape
+    lines = [pltpu.VMEM(x.shape, x.dtype) for x in (*parts, small)]
     return remote_call(
         functools.partial(context_sum_kernel, over_f),
         "context_sum",
         6,
-        [*parts, small],
+        [*parts, small, out_part.reshape(8, rows, width), middle],
         [jax.ShapeDtypeStruct(x.shape, f32) for x in parts[:2]]
         + [jax.ShapeDtypeStruct(small.shape, f32)]
-        + [jax.ShapeDtypeStruct((4,) + parts[2].shape, bf16)],
-        [like(x) for x in parts] * 3 + [pltpu.VMEM((3,) + small.shape, f32)],
-        32,
-        ([True] * 4, [True] * 3 + [False]),
+        + [jax.ShapeDtypeStruct((4,) + parts[2].shape, bf16)]
+        + [jax.ShapeDtypeStruct((4, rows, width), bf16)],
+        lines * 3
+        + [pltpu.VMEM((rows, width), bf16), pltpu.VMEM(small.shape, f32)]
+        + pair_scratch(rows, width),
+        48,
+        ([True] * 4 + [False, True], [True] * 3 + [False] * 2),
     )
 
 
@@ -963,7 +999,7 @@
         w_q = pieces_f(w_query, 0)
         w_kv = pieces_f(w_kv_own, 0)
         small = gather_f(small, 0)
-        w_out_all = gather_f(w_out, 1)
+        w_out_all = gather_f(after(w_out, small), 1)
         piece = attn_gain.shape[0]
         gain_first = small[:, :piece].reshape(1, width).astype(f32)
         gain_second = small[:, piece : 2 * piece].reshape(1, width).astype(f32)
@@ -982,7 +1018,6 @@
 
         unit_slice = lambda w: lax.dynamic_slice_in_dim(w, parity * units, units, 0)
         own_units = jnp.concatenate([unit_slice(w) for w in (w_gate.T, w_up.T, w_down)], axis=0)
-        w_units = pieces_f(after(own_units, w_q, w_kv, small, w_out_all), 1)
 
         dy_part = lax.dynamic_slice_in_dim(cotangent, t * part, part, 0)
 
@@ -999,26 +1034,24 @@
         normed, factor_first, queries, kv_own = qkv(
             meta, inputs, gain_first, bias, cosine, sine, w_q, w_kv
         )
-        kv = kv_gather(kv_own)
+        w_units = pieces_f(after(own_units, kv_own, w_out_all), 1)
+        kv = kv_gather(after(kv_own, w_out_all))
         attended, lse = attention(key_blocks, queries, kv)
         inputs_part = lax.dynamic_slice_in_dim(inputs, t * part, part, 0)
         middle, factor_second, normed2, dy_all = middle_norm(
             dot(attended, w_out_all).astype(bf16), inputs_part, gain_second, dy_part
         )
 
-        hidden, grad_gate, grad_up, dx_part, out_part = ffn(meta, normed2, dy_all, w_units)
-        down, gate_up = [hidden], [grad_gate, grad_up]
+        hidden, grad_gate, grad_up, dx_part, out_part, *unit_far = ffn(
+            meta, normed2, dy_all, w_units
+        )
         if n_f == 2:
-            down_sent = unit_grads(meta, 1, 2, dy_all, down)
-            down_got = flip(down_sent, "fsdp", 1)
-            gate_up_sent = unit_grads(meta, 1, 2, *after((normed2, gate_up), down_sent))
-            gate_up_got = flip(gate_up_sent, "fsdp", 1)
-            dx_part = after(dx_part, gate_up_sent)
+            down_got, gate_got, up_got = (flip(x, "fsdp", 1) for x in unit_far)
         else:
             over_f = lambda x: lax.psum_scatter(x, "fsdp", scatter_dimension=1, tiled=True)
-            down_own = over_f(unit_grads(meta, 0, 1, dy_all, down))
-            gate_up_own = over_f(unit_grads(meta, 0, 1, normed2, gate_up))
-            down_got, gate_up_got = jnp.zeros_like(down_own), jnp.zeros_like(gate_up_own)
+            down_own = over_f(unit_grads(meta, 0, 1, dy_all, [hidden]))
+            gate_up_own = over_f(unit_grads(meta, 0, 1, normed2, [grad_gate, grad_up]))
+            down_got = gate_got = up_got = jnp.zeros_like(down_own)
 
         def unit_done(own, got):
             low = (own.astype(f32) + got.astype(f32)).astype(bf16)
@@ -1031,20 +1064,17 @@
         )
         grad_middle_low = grad_middle_low.reshape(rows, width)
         if n_f == 2:
-            down_own = unit_grads(meta, 0, 2, *after((dy_all, down), grad_middle_low))
+            down_own = unit_grads(meta, 0, 2, *after((dy_all, [hidden]), grad_middle_low))
         down_done = unit_done(down_own, after(down_got, grad_middle_low))
         grad_attended = dot_cols(after(grad_middle_low, down_done[0]), w_out_all).astype(bf16)
 
         dq_low, dkv = attention_back(key_blocks, queries, grad_attended, lse, cosine, sine, kv)
         if n_f == 2:
-            gate_up_own = unit_grads(meta, 0, 2, *after((normed2, gate_up), dkv))
+            gate_up_own = unit_grads(meta, 0, 2, *after((normed2, [grad_gate, grad_up]), dkv))
             dkv = after(dkv, gate_up_own)
-        dkv, outputs = kv_scatter(after(dkv, down_done), out_part, middle)
-        outputs = outputs.reshape(rows, width)
-        gate_up_got = after(gate_up_got, dkv)
-        gate_done, up_done = (
-            unit_done(gate_up_own[k : k + units], gate_up_got[k : k + units]) for k in (0, units)
-        )
+        dkv = kv_scatter(after(dkv, down_done))
+        gate_done = unit_done(gate_up_own[:units], after(gate_got, dkv))
+        up_done = unit_done(gate_up_own[units:], after(up_got, gate_done[0]))
         dkv = after(dkv, gate_done[0], up_done[0])
         dkv_low = jnp.where(core == 0, rotate_back(dkv, cosine, sine), dkv).astype(bf16)
         attention_args = (
@@ -1077,12 +1107,14 @@
             small_grads = lax.psum(small_grads, "fsdp")
         attention_parts = [grad_sum(*args, far) for args, far in zip(attention_args, fars)]
         wd_grad = unit_whole(*after(down_done, small_grads))
-        small_grads, gate_done, up_done = lax.optimization_barrier(
-            (small_grads, gate_done, up_done)
-        )
-        wo_grad, wq_grad, packed, wkv_all = context_sum(
-            n_f == 2, attention_parts, after(small_grads, wd_grad)
-        )
+        wg_grad = unit_whole(*after(gate_done, small_grads))
+        small_grads, up_done, wg_grad, wd_grad = lax.optimization_barrier(
+            (small_grads, up_done, wg_grad, wd_grad)
+        )
+        wo_grad, wq_grad, packed, wkv_all, outputs = context_sum(
+            n_f == 2, attention_parts, small_grads, out_part, middle
+        )
+        outputs = outputs.reshape(rows, width)
         wkv_all = wkv_all.astype(f32)
         wk_grad = jnp.concatenate([wkv_all[0], wkv_all[2]], axis=1)
         wv_grad = jnp.concatenate([wkv_all[1], wkv_all[3]], axis=1)
@@ -1095,7 +1127,7 @@
         bk_out = slots[0::2, heads]
         bv_out = slots[1::2, heads]
 
-        wg_grad, wu_grad = unit_whole(*gate_done), unit_whole(*up_done)
+        wu_grad = unit_whole(*up_done)
         wg_grad, wu_grad = wg_grad.T, wu_grad.T
 
         return (

time: 556 us -> 519 us (0.933)
  waiting for transfers between devices: 54.5 us -> 27.6 us
  Pallas kernels: 398 us -> 387 us
    ppermute x13 -> x14, waiting for transfers between devices: 54.5 us -> 27.6 us  [flip(): return lax.ppermute(x, axis, [(i, i ^ bit) for i in range(size)])]
    pallas_call x4 -> x2, Pallas kernels: 46 us -> 22.9 us  [unit_grads(): pl.pallas_call(functools.partial(unit_grads_kernel, count), name=f'unit_g...]
    pallas_call x1, Pallas kernels: 47.2 us -> 62 us  [ffn(): pl.pallas_call(functools.partial(ffn_kernel, pieces), name='ffn', grid_sp...]
    transpose x2 -> x1, other arithmetic: 10.8 us -> 4.78 us  [local(): wg_grad, wu_grad = (wg_grad.T, wu_grad.T)]
    unnamed x61 -> x65, local copies, waits for them, and re-layouts: 11.4 us -> 11.7 us
    ppermute x13 -> x14, starting transfers between devices: 14.6 us -> 14.5 us  [flip(): return lax.ppermute(x, axis, [(i, i ^ bit) for i in range(size)])]
  transfers between devices with their start and end apart: 13 -> 14, of which waited for: 4 -> 5; matrix products, arithmetic and copies ran while one was open for 8% -> 11% of each run, Pallas kernels for 49% -> 45%
where the time goes in v6:
time: 519 us; the launch traced here: 512 us
  Pallas kernels  387 us (75%)
  other arithmetic  36.7 us (7%)
  local copies, waits for them, and re-layouts  27.7 us (5%)
  waiting for transfers between devices  27.6 us (5%)
  matrix products  17.2 us (3%)
  starting transfers between devices  14.5 us (3%)
    pallas_call x6, Pallas kernels, remote_call(): pl.pallas_call(kernel, name=name, out_shape=outs, in_specs=[spec(x) for x...  266 us
    pallas_call x1, Pallas kernels, ffn(): pl.pallas_call(functools.partial(ffn_kernel, pieces), name='ffn', grid_sp...  62 us
    ppermute x14, waiting for transfers between devices, flip(): return lax.ppermute(x, axis, [(i, i ^ bit) for i in range(size)])  27.6 us
    pallas_call x2, Pallas kernels, unit_grads(): pl.pallas_call(functools.partial(unit_grads_kernel, count), name=f'unit_g...  22.9 us
    pallas_call x1, Pallas kernels, attention_back(): pl.pallas_call(functools.partial(attention_back_kernel, kv.shape[1] // BL...  15 us
    ppermute x14, starting transfers between devices, flip(): return lax.ppermute(x, axis, [(i, i ^ bit) for i in range(size)])  14.5 us
    unnamed x65, local copies, waits for them, and re-layouts  11.7 us
    dot_general x6, matrix products, dot_rows(): lax.dot_general(left, right, (((0,), (0,)), ((), ())), preferred_element_...  10.9 us
  transfers between devices with their start and end apart: 14, of which 5 were waited for; matrix products, arithmetic and copies ran while one was open for 11% of the time, Pallas kernels for 45%

profile of v6, /device:TPU:0, one launch (start us, length us, event | category | flops | bytes accessed | tf_op | source)
XLA Modules:
  0.0 511.8 jit_solution(18176583833864475271)
XLA Ops:
  4.4 3.0 collective-permute-start
  8.5 2.0 collective-permute-start.1
  19.5 2.6 pad_maximum_fusion.refs_0_.refs_2_.refs_4_
  24.5 4.4 collective-permute-done.1.refs_1_
  29.7 5.8 %qkv.1 = (bf16[512,1536]{1,0:T(8,128)(2,1)}, f32[512,1]{1,0:T(8,128)}, bf16[512,384]{1,0:T(8,128)(2,1)}, bf16[512,128]{1,0:T(8,128)(2,1)}) custom-call(s32[4]{0:T(128)} %pad_add_fusion.1.meta_ref, bf16[512,1536]{1,0:T(8,128)(2,1)} %x_ref.1, f32[1,1536]{1,0:T(1,128)} %bitcast.90, f32[1,512]{1,0:T(1,128)} %pad_maximum_fusion.6.bias_ref, ...), custom_call_target="tpu_custom_call" | custom-call | tf_op jit(solution)/shard_map/qkv/pallas_call | solution.py:210
  35.6 4.5 collective-permute-done.3
  41.4 1.8 constant_dynamic-slice_fusion.7.x_ref
  45.6 17.4 %kv_gather.1.k_ref.v_ref = bf16[2,2048,128]{2,1,0:T(8,128)(2,1)} custom-call(bf16[512,128]{1,0:T(8,128)(2,1)} %get-tuple-element.74.own_ref), custom_call_target="tpu_custom_call" | custom-call | tf_op jit(solution)/shard_map/kv_gather/pallas_call | solution.py:540
  63.0 10.1 %attention.1 = (bf16[512,384]{1,0:T(8,128)(2,1)}, f32[3,512,1]{2,1,0:T(8,128)}) custom-call(s32[8]{0:T(128)} %pad_add_fusion.kb_ref, bf16[512,384]{1,0:T(8,128)(2,1)} %get-tuple-element.71.q_ref, bf16[2,2048,128]{2,1,0:T(8,128)(2,1)} %kv_gather.1.k_ref.v_ref, bf16[2,2048,128]{2,1,0:T(8,128)(2,1)} %kv_gather.1.k_ref.v_ref), custom_call_target="tpu_custom_call" | custom-call | tf_op jit(solution)/shard_map/attention/pallas_call | solution.py:86
  73.1 3.1 convolution_convert_fusion
  76.2 76.1 %middle_norm.1 = (f32[128,1536]{1,0:T(8,128)}, f32[128,1]{1,0:T(8,128)}, bf16[16,128,1536]{2,1,0:T(8,128)(2,1)}, bf16[16,128,1536]{2,1,0:T(8,128)(2,1)}) custom-call(bf16[4,128,1536]{2,1,0:T(8,128)(2,1)} %bitcast.82, bf16[128,1536]{1,0:T(8,128)(2,1)} %constant_dynamic-slice_fusion.7.x_ref, f32[1,1536]{1,0:T(1,128)} %bitcast.88, ...), custom_call_target="tpu_custom_call" | custom-call | tf_op jit(solution)/shard_map/middle_norm/pallas_call | solution.py:540
  152.6 62.0 %ffn.1 = (bf16[2048,1120]{1,0:T(8,128)(2,1)}, bf16[2048,1120]{1,0:T(8,128)(2,1)}, bf16[2048,1120]{1,0:T(8,128)(2,1)}, bf16[1024,1536]{1,0:T(8,128)(2,1)}, bf16[1...) custom-call(s32[4]{0:T(128)} %pad_add_fusion.1.meta_ref, ...), custom_call_target="tpu_custom_call" | custom-call | tf_op jit(solution)/shard_map/ffn/pallas_call | solution.py:313
  215.9 32.4 %middle_back.1 = (f32[128,1536]{1,0:T(8,128)}, f32[1,1536]{1,0:T(1,128)}, bf16[4,128,1536]{2,1,0:T(8,128)(2,1)}) custom-call(bf16[8,128,1536]{2,1,0:T(8,128)(2,1)} %bitcast.84, f32[128,1536]{1,0:T(8,128)} %get-tuple-element.80.mid_ref.refs_5_, f32[128,1]{1,0:T(8,128)} %get-tuple-element.81.factor_ref, f32[1,1536]{1,0:T(1,128)} %bitcast.89, ...), custom_call_target="tpu_custom_call" | custom-call | tf_op jit(solution)/shard_map/middle_back/pallas_call | solution.py:540
  248.3 8.7 %unit_grads_0_1.1 = bf16[1120,768]{1,0:T(8,128)(2,1)} custom-call(s32[4]{0:T(128)} %pad_add_fusion.1.meta_ref, bf16[2048,1536]{1,0:T(8,128)(2,1)} %bitcast.78, bf16[2048,1536]{1,0:T(8,128)(2,1)} %bitcast.79, bf16[2048,1120]{1,0:T(8,128)(2,1)} %get-tuple-element.85.refs_0_), custom_call_target="tpu_custom_call" | custom-call | tf_op jit(solution)/shard_map/unit_grads_0_1/pallas_call | solution.py:350
  257.0 2.5 add_convert_fusion.2
  264.6 3.1 convolution_convert_fusion.3.do_ref
  267.8 15.0 %attention_back.1 = (bf16[512,384]{1,0:T(8,128)(2,1)}, bf16[2,2048,128]{2,1,0:T(8,128)(2,1)}) custom-call(s32[8]{0:T(128)} %pad_add_fusion.kb_ref, bf16[512,384]{1,0:T(8,128)(2,1)} %get-tuple-element.71.q_ref, bf16[512,384]{1,0:T(8,128)(2,1)} %convolution_convert_fusion.3.do_ref, f32[3,512,1]{2,1,0:T(8,128)} %get-tuple-element.89.lse_ref, ...), custom_call_target="tpu_custom_call" | custom-call | tf_op jit(solution)/shard_map/attention_back/pallas_call | solution.py:152
  282.8 14.3 %unit_grads_0_2.1 = bf16[2240,768]{1,0:T(8,128)(2,1)} custom-call(s32[4]{0:T(128)} %pad_add_fusion.1.meta_ref, bf16[2048,1536]{1,0:T(8,128)(2,1)} %bitcast.75, bf16[2048,1536]{1,0:T(8,128)(2,1)} %bitcast.76, bf16[2048,1120]{1,0:T(8,128)(2,1)} %get-tuple-element.94.refs_0_, bf16[2048,1120]{1,0:T(8,128)(2,1)} %get-tuple-element.95.refs_1_), custom_call_target="tpu_custom_call" | custom-call | tf_op jit(solution)/shard_map/unit_grads_0_2/pallas_call | solution.py:350
  297.0 2.5 collective-permute-done.6
  299.6 18.7 %kv_scatter.1 = f32[512,128]{1,0:T(8,128)} custom-call(bf16[2,2048,128]{2,1,0:T(8,128)(2,1)} %get-tuple-element.97.part_ref), custom_call_target="tpu_custom_call" | custom-call | tf_op jit(solution)/shard_map/kv_scatter/pallas_call | solution.py:540
  318.3 3.7 add_convert_fusion.1
  322.0 15.8 %collective-permute-done.8 = bf16[1120,768]{1,0:T(8,128)(2,1)} collective-permute-done((bf16[1120,768]{1,0:T(8,128)(2,1)}, bf16[1120,768]{1,0:T(8,128)(2,1)}, u32[]{:S(2)}, u32[]{:S(2)}) %collective-permute-start.8) | collective-permute-done | bytes 1720352 | tf_op jit(solution)/shard_map/ppermute | solution.py:924
  337.9 2.0 add_convert_fusion
  350.1 4.7 qkv_back.1
  354.8 28.7 %input_back.1 = (f32[1,5120]{1,0:T(1,128)}, bf16[4,128,1536]{2,1,0:T(8,128)(2,1)}) custom-call(bf16[4,128,1536]{2,1,0:T(8,128)(2,1)} %bitcast.81, bf16[128,1536]{1,0:T(8,128)(2,1)} %constant_dynamic-slice_fusion.7.x_ref, f32[128,1]{1,0:T(8,128)} %constant_dynamic-slice_fusion.4.factor_ref, f32[1,1536]{1,0:T(1,128)} %bitcast.91, ...), custom_call_target="tpu_custom_call" | custom-call | tf_op jit(solution)/shard_map/input_back/pallas_call | solution.py:540
  383.5 4.8 fusion.1
  388.3 2.2 fusion.4.refs_2_
  390.5 2.5 fusion.3.refs_1_
  393.0 2.4 fusion.2.refs_0_
  395.4 5.3 %fusion = f32[2240,768]{1,0:T(8,128)} fusion(bf16[1120,768]{1,0:T(8,128)(2,1)} %collective-permute-done.13, bf16[1120,768]{1,0:T(8,128)(2,1)} %add_convert_fusion.1, pred[]{:T(512)S(6)} %eq.19), kind=kLoop, calls=%fused_computation.3 | loop fusion | flops 17203200 | bytes 10321921 | tf_op jit(solution)/shard_map/convert_element_type | solution.py:1060
  400.6 92.9 %context_sum.1 = (f32[384,768]{1,0:T(8,128)}, f32[768,384]{1,0:T(8,128)}, f32[1,5120]{1,0:T(1,128)}, bf16[4,768,128]{2,1,0:T(8,128)(2,1)}, bf16[4,128,1536]{2,1,0:T(8,128)(2,1)}) custom-call(bf16[384,768]{1,0:T(8,128)(2,1)} %fusion.2.refs_0_, bf16[768,384]{1,0:T(8,128)(2,1)} %fusion.3.refs_1_, bf16[768,128]{1,0:T(8,128)(2,1)} %fusion.4.refs_2_, ...), custom_call_target="tpu_custom_call" | custom-call | tf_op jit(solution)/shard_map/context_sum/pallas_call | solution.py:540
  500.0 4.8 convert_bitcast_fusion
  (143 shorter events, 50.7 us)
Async XLA Ops:
  4.4 18.4 %collective-permute-start = (bf16[1,1984]{1,0:T(2,128)(2,1)S(1)}, bf16[1,1984]{1,0:T(2,128)(2,1)S(1)}, u32[]{:S(2)}, u32[]{:S(2)}) collective-permute-start(bf16[1,1984]{1,0:T(2,128)(2,1)S(1)} %concatenate.64), channel_id=1, source_target_pairs={{0,16},{16,0},{1,17},{17,1},{2,18},{18,2},{3,19},{19,3},{4,20},{20... | collective-permute-start | bytes 11912 | tf_op jit(solution)/shard_map/ppermute | solution.py:924
  8.4 8.6 %copy-start.11 = (bf16[768,128]{1,0:T(8,128)(2,1)}, bf16[768,128]{1,0:T(8,128)(2,1)S(1)}, u32[]{:S(2)}) copy-start(bf16[768,128]{1,0:T(8,128)(2,1)S(1)} %dynamic-slice_select_fusion.refs_2_) | copy-start | bytes 589828
  8.4 16.1 %collective-permute-start.2 = (bf16[768,128]{1,0:T(8,128)(2,1)S(1)}, bf16[768,128]{1,0:T(8,128)(2,1)S(1)}, u32[]{:S(2)}, u32[]{:S(2)}) collective-permute-start(bf16[768,128]{1,0:T(8,128)(2,1)S(1)} %dynamic-slice_select_fusion.refs_2_), channel_id=1, source_target_pairs={{0,16},{16,0},{1,17},{17,1},{2,18},{18,2},{3,19},{19,3},{4,20},{20... | collective-permute-start | bytes 589832 | tf_op jit(solution)/shard_map/ppermute | solution.py:924
  8.5 20.4 %collective-permute-start.1 = (bf16[768,384]{1,0:T(8,128)(2,1)}, bf16[768,384]{1,0:T(8,128)(2,1)S(1)}, u32[]{:S(2)}, u32[]{:S(2)}) collective-permute-start(bf16[768,384]{1,0:T(8,128)(2,1)} %refs_0_.3), channel_id=1, source_target_pairs={{0,16},{16,0},{1,17},{17,1},{2,18},{18,2},{3,19},{19,3},{4,20},{20... | collective-permute-start | bytes 1769480 | tf_op jit(solution)/shard_map/ppermute | solution.py:924
  23.1 17.0 %collective-permute-start.3 = (bf16[384,768]{1,0:T(8,128)(2,1)S(1)}, bf16[384,768]{1,0:T(8,128)(2,1)S(1)}, u32[]{:S(2)}, u32[]{:S(2)}) collective-permute-start(bf16[384,768]{1,0:T(8,128)(2,1)S(1)} %copy-done.22), channel_id=1, source_target_pairs={{0,16},{16,0},{1,17},{17,1},{2,18},{18,2},{3,19},{19,3},{4,20},{20... | collective-permute-start | bytes 1769480 | tf_op jit(solution)/shard_map/ppermute | solution.py:924
  24.5 4.4 copy-start.21
  40.4 32.7 %copy-start.1 = (bf16[384,1536]{1,0:T(8,128)(2,1)}, bf16[384,1536]{1,0:T(8,128)(2,1)S(1)}, u32[]{:S(2)}) copy-start(bf16[384,1536]{1,0:T(8,128)(2,1)S(1)} %maximum_select_fusion.3) | copy-start | bytes 3538948
  40.4 112.2 %collective-permute-start.4 = (bf16[3360,768]{1,0:T(8,128)(2,1)}, bf16[3360,768]{1,0:T(8,128)(2,1)}, u32[]{:S(2)}, u32[]{:S(2)}) collective-permute-start(bf16[3360,768]{1,0:T(8,128)(2,1)} %pad_maximum_fusion.refs_0_.refs_2_.refs_4_), channel_id=1, source_target_pairs={{0,16},{16,0},{1,17},{17,1},{2,18},{18,2},{3,19},{19,3},{4,20},{20... | collective-permute-start | bytes 15482888 | tf_op jit(solution)/shard_map/ppermute | solution.py:924
  214.7 42.3 %collective-permute-start.5 = (bf16[1120,768]{1,0:T(8,128)(2,1)}, bf16[1120,768]{1,0:T(8,128)(2,1)}, u32[]{:S(2)}, u32[]{:S(2)}) collective-permute-start(bf16[1120,768]{1,0:T(8,128)(2,1)} %get-tuple-element.86), channel_id=1, source_target_pairs={{0,16},{16,0},{1,17},{17,1},{2,18},{18,2},{3,19},{19,3},{4,20},{20... | collective-permute-start | bytes 5160968 | tf_op jit(solution)/shard_map/ppermute | solution.py:924
  257.0 7.6 %copy-start.2 = (bf16[384,1536]{1,0:T(8,128)(2,1)S(1)}, bf16[384,1536]{1,0:T(8,128)(2,1)}, u32[]{:S(2)}) copy-start(bf16[384,1536]{1,0:T(8,128)(2,1)} %copy-done.1) | copy-start | bytes 3538948
  259.5 40.1 %collective-permute-start.6 = (bf16[1120,768]{1,0:T(8,128)(2,1)S(1)}, bf16[1120,768]{1,0:T(8,128)(2,1)}, u32[]{:S(2)}, u32[]{:S(2)}) collective-permute-start(bf16[1120,768]{1,0:T(8,128)(2,1)S(1)} %add_convert_fusion.2), channel_id=1, source_target_pairs={{0,4},{4,0},{8,12},{12,8},{1,5},{5,1},{9,13},{13,9},{2,6},{6,2},{1... | collective-permute-start | bytes 5160968 | tf_op jit(solution)/shard_map/ppermute | solution.py:924
  261.1 57.2 %collective-permute-start.7 = (bf16[1120,768]{1,0:T(8,128)(2,1)}, bf16[1120,768]{1,0:T(8,128)(2,1)}, u32[]{:S(2)}, u32[]{:S(2)}) collective-permute-start(bf16[1120,768]{1,0:T(8,128)(2,1)} %get-tuple-element.98), channel_id=1, source_target_pairs={{0,16},{16,0},{1,17},{17,1},{2,18},{18,2},{3,19},{19,3},{4,20},{20... | collective-permute-start | bytes 5160968 | tf_op jit(solution)/shard_map/ppermute | solution.py:924
  262.6 75.2 %collective-permute-start.8 = (bf16[1120,768]{1,0:T(8,128)(2,1)}, bf16[1120,768]{1,0:T(8,128)(2,1)}, u32[]{:S(2)}, u32[]{:S(2)}) collective-permute-start(bf16[1120,768]{1,0:T(8,128)(2,1)} %get-tuple-element.100), channel_id=1, source_target_pairs={{0,16},{16,0},{1,17},{17,1},{2,18},{18,2},{3,19},{19,3},{4,20},{20... | collective-permute-start | bytes 5160968 | tf_op jit(solution)/shard_map/ppermute | solution.py:924
  318.3 19.6 %copy-start = (bf16[2240,768]{1,0:T(8,128)(2,1)S(1)}, bf16[2240,768]{1,0:T(8,128)(2,1)}, u32[]{:S(2)}) copy-start(bf16[2240,768]{1,0:T(8,128)(2,1)} %unit_grads_0_2.1) | copy-start | bytes 10321924
  322.0 17.8 %copy-start.6 = (f32[512,64]{1,0:T(8,128)S(1)}, f32[512,64]{1,0:T(8,128)}, u32[]{:S(2)}) copy-start(f32[512,64]{1,0:T(8,128)} %copy-done.5) | copy-start | bytes 393220
  322.0 17.8 %copy-start.7 = (f32[512,128]{1,0:T(8,128)S(1)}, f32[512,128]{1,0:T(8,128)}, u32[]{:S(2)}) copy-start(f32[512,128]{1,0:T(8,128)} %kv_scatter.1) | copy-start | bytes 786436
  322.0 73.3 %collective-permute-start.13 = (bf16[1120,768]{1,0:T(8,128)(2,1)}, bf16[1120,768]{1,0:T(8,128)(2,1)}, u32[]{:S(2)}, u32[]{:S(2)}) collective-permute-start(bf16[1120,768]{1,0:T(8,128)(2,1)} %add_convert_fusion.1), channel_id=1, source_target_pairs={{0,4},{4,0},{8,12},{12,8},{1,5},{5,1},{9,13},{13,9},{2,6},{6,2},{1... | collective-permute-start | bytes 5160968 | tf_op jit(solution)/shard_map/ppermute | solution.py:924
  340.0 4.0 copy-start.23
  340.0 4.0 copy-start.26
  341.0 8.2 %copy-start.3 = (bf16[512,128]{1,0:T(8,128)(2,1)}, bf16[512,128]{1,0:T(8,128)(2,1)S(1)}, u32[]{:S(2)}) copy-start(bf16[512,128]{1,0:T(8,128)(2,1)S(1)} %fusion.12.dkv_ref) | copy-start | bytes 393220
  341.0 4.3 copy-start.16
  342.5 45.8 %collective-permute-start.11 = (bf16[768,128]{1,0:T(8,128)(2,1)}, bf16[768,128]{1,0:T(8,128)(2,1)}, u32[]{:S(2)}, u32[]{:S(2)}) collective-permute-start(bf16[768,128]{1,0:T(8,128)(2,1)} %convolution_convert_fusion.4), channel_id=1, source_target_pairs={{0,16},{16,0},{1,17},{17,1},{2,18},{18,2},{3,19},{19,3},{4,20},{20... | collective-permute-start | bytes 589832 | tf_op jit(solution)/shard_map/ppermute | solution.py:924
  345.3 4.1 copy-start.25
  346.7 43.7 %collective-permute-start.10 = (bf16[768,384]{1,0:T(8,128)(2,1)}, bf16[768,384]{1,0:T(8,128)(2,1)}, u32[]{:S(2)}, u32[]{:S(2)}) collective-permute-start(bf16[768,384]{1,0:T(8,128)(2,1)} %convolution_convert_fusion.1), channel_id=1, source_target_pairs={{0,16},{16,0},{1,17},{17,1},{2,18},{18,2},{3,19},{19,3},{4,20},{20... | collective-permute-start | bytes 1769480 | tf_op jit(solution)/shard_map/ppermute | solution.py:924
  347.2 45.7 %collective-permute-start.9 = (bf16[384,768]{1,0:T(8,128)(2,1)}, bf16[384,768]{1,0:T(8,128)(2,1)}, u32[]{:S(2)}, u32[]{:S(2)}) collective-permute-start(bf16[384,768]{1,0:T(8,128)(2,1)} %convolution_convert_fusion.2), channel_id=1, source_target_pairs={{0,16},{16,0},{1,17},{17,1},{2,18},{18,2},{3,19},{19,3},{4,20},{20... | collective-permute-start | bytes 1769480 | tf_op jit(solution)/shard_map/ppermute | solution.py:924
  348.8 51.9 %collective-permute-start.12 = (bf16[1120,768]{1,0:T(8,128)(2,1)S(1)}, bf16[1120,768]{1,0:T(8,128)(2,1)}, u32[]{:S(2)}, u32[]{:S(2)}) collective-permute-start(bf16[1120,768]{1,0:T(8,128)(2,1)S(1)} %add_convert_fusion), channel_id=1, source_target_pairs={{0,4},{4,0},{8,12},{12,8},{1,5},{5,1},{9,13},{13,9},{2,6},{6,2},{1... | collective-permute-start | bytes 5160968 | tf_op jit(solution)/shard_map/ppermute | solution.py:924
  383.4 4.8 copy-start.4
  383.4 4.8 copy-start.15
  383.5 7.0 %copy-start.17 = (bf16[512,384]{1,0:T(8,128)(2,1)S(1)}, bf16[512,384]{1,0:T(8,128)(2,1)}, u32[]{:S(2)}) copy-start(bf16[512,384]{1,0:T(8,128)(2,1)} %get-tuple-element.106.dq_ref) | copy-start | bytes 1179652
  388.3 4.7 copy-start.24
  388.3 4.7 copy-start.27
  500.0 4.8 copy-start.13
  (10 other events, 16.4 us)

commit v7 on v6

--- a/solution.py
+++ b/solution.py
@@ -18,7 +18,6 @@
 SCALING = HD ** (-0.5)
 LANES = 128
 VMEM_LIMIT = 60 << 20
-FFN_VMEM_LIMIT = 63 << 20
 
 f32 = jnp.float32
 bf16 = jnp.bfloat16
@@ -254,75 +253,128 @@
     )(meta, grad_q, grad_kv, *w_q, *w_kv)
 
 
-def ffn_kernel(pieces, meta_ref, x_ref, dy_ref, *refs):
-    wg, wu, wd = (refs[m * pieces : (m + 1) * pieces] for m in range(3))
-    refs = refs[3 * pieces :]
-    hid_ref, dg_ref, du_ref, dx_ref, out_ref = refs[:5]
+def add_rows(unit_refs, row_refs, columns, totals, outs):
+    step = pl.program_id(0)
+
+    @pl.when(step == 0)
+    def _():
+        for total in totals:
+            total[...] = jnp.zeros_like(total)
+
+    for total, unit, row in zip(totals, unit_refs, row_refs):
+        total[...] += dot_rows(unit[...], row[:, columns])
+
+    @pl.when(step == pl.num_programs(0) - 1)
+    def _():
+        for out, total in zip(outs, totals):
+            out[...] = total[...].astype(bf16)
+
+
+def hidden_kernel(pieces, meta_ref, x_ref, dy_ref, *refs):
+    wg, wu, refs = refs[:pieces], refs[pieces : 2 * pieces], refs[2 * pieces :]
+    hid_ref, slope_ref, gated_ref = refs[:3]
     columns = [columns_of(meta_ref, j, wg[j].shape[1], pieces) for j in range(pieces)]
     gate = sum(dot_cols(x_ref[:, at], w[...]) for at, w in zip(columns, wg))
     up = sum(dot_cols(x_ref[:, at], w[...]) for at, w in zip(columns, wu))
-    grad_hidden = sum(dot_cols(dy_ref[:, at], w[...]) for at, w in zip(columns, wd))
     sigma = 1.0 / (1.0 + jnp.exp(-gate))
     gated = gate * sigma
     hid_ref[...] = (gated * up).astype(bf16)
-    dg_ref[...] = (grad_hidden * up * (sigma + gated * (1.0 - sigma))).astype(bf16)
-    du_ref[...] = (grad_hidden * gated).astype(bf16)
-    step, steps = pl.program_id(0), pl.num_programs(0)
-
-    @pl.when(step // (steps // 2) == meta_ref[3])
+    slope_ref[...] = (up * (sigma + gated * (1.0 - sigma))).astype(bf16)
+    gated_ref[...] = gated.astype(bf16)
+    if pieces == 2:
+        add_rows([hid_ref], [dy_ref], columns[1], refs[4:], refs[3:4])
+
+
+def hidden_back_kernel(pieces, meta_ref, x_ref, dy_ref, hid_ref, slope_ref, gated_ref, *refs):
+    wg, wu, wd = (refs[m * pieces : (m + 1) * pieces] for m in range(3))
+    refs = refs[3 * pieces :]
+    dg_ref, du_ref, dx_ref, out_ref = refs[:4]
+    columns = [columns_of(meta_ref, j, wg[j].shape[1], pieces) for j in range(pieces)]
+    grad_hidden = sum(dot_cols(dy_ref[:, at], w[...]) for at, w in zip(columns, wd))
+    dg_ref[...] = (grad_hidden * slope_ref[...].astype(f32)).astype(bf16)
+    du_ref[...] = (grad_hidden * gated_ref[...].astype(f32)).astype(bf16)
+
+    @pl.when(pl.program_id(0) // (pl.num_programs(0) // 2) == meta_ref[3])
     def _():
         for at, g, u, d in zip(columns, wg, wu, wd):
             dx_ref[:, at] = (dot(dg_ref[...], g[...]) + dot(du_ref[...], u[...])).astype(bf16)
             out_ref[:, at] = dot(hid_ref[...], d[...]).astype(bf16)
 
     if pieces == 2:
-        outs, totals = refs[5:8], refs[8:11]
-        sources = ((hid_ref, dy_ref), (dg_ref, x_ref), (du_ref, x_ref))
-
-        @pl.when(step == 0)
-        def _():
-            for total in totals:
-                total[...] = jnp.zeros_like(total)
-
-        for total, (unit, row) in zip(totals, sources):
-            total[...] += dot_rows(unit[...], row[:, columns[1]])
-
-        @pl.when(step == steps - 1)
-        def _():
-            for out, total in zip(outs, totals):
-                out[...] = total[...].astype(bf16)
-
-
-def ffn(meta, normed, grad_out, weights):
+        add_rows([dg_ref, du_ref], [x_ref, x_ref], columns[1], refs[6:], refs[4:6])
+
+
+def hidden_specs(meta, normed, weights):
     width = normed.shape[-1]
     rows = normed.shape[0] * normed.shape[1]
-    pieces = len(weights)
     units, depth = weights[0].shape[0] // 3, weights[0].shape[1]
     tile = 512
     steps = rows // tile
     half = steps // 2
-    flat = lambda x: x.reshape(-1, width)
-    read = pl.BlockSpec((tile, width), lambda i, m: (lax.rem(i + m[3] * half, steps), 0))
     once = pl.Buffered(1)
-    weight = lambda w, k: pl.BlockSpec((units, depth), lambda i, m: (k, 0), pipeline_mode=once)
-    placed = pl.BlockSpec((tile, units), lambda i, m: (i, 0))
-    near = pl.BlockSpec((tile, width), lambda i, m: (jnp.clip(i - m[3] * half, 0, half - 1), 0))
-    grads = [pl.BlockSpec((units, depth), lambda i, m: (0, 0), pipeline_mode=once)] * 3
-    grads = grads if pieces == 2 else []
-    shapes = [(rows, units)] * 3 + [(rows // 2, width)] * 2 + [(units, depth)] * len(grads)
+    inside = lambda i, m: jnp.clip(i - m[3] * half, 0, half - 1)
+    return {
+        "steps": steps,
+        "flat": lambda x: x.reshape(-1, width),
+        "row": pl.BlockSpec((tile, width), lambda i, m: (lax.rem(i + m[3] * half, steps), 0)),
+        "unit": pl.BlockSpec((tile, units), lambda i, m: (i, 0)),
+        "near_unit": pl.BlockSpec((tile, units), lambda i, m: (inside(i, m) + m[3] * half, 0)),
+        "near_row": pl.BlockSpec((tile, width), lambda i, m: (inside(i, m), 0)),
+        "weight": lambda k: pl.BlockSpec((units, depth), lambda i, m: (k, 0), pipeline_mode=once),
+        "grad": pl.BlockSpec((units, depth), lambda i, m: (0, 0), pipeline_mode=once),
+        "unit_shape": jax.ShapeDtypeStruct((rows, units), bf16),
+        "near_shape": jax.ShapeDtypeStruct((rows // 2, width), bf16),
+        "grad_shape": jax.ShapeDtypeStruct((units, depth), bf16),
+        "total": pltpu.VMEM((units, depth), f32),
+    }
+
+
+def hidden_call(kernel, name, meta, args, in_specs, outs, grads, specs):
     return pl.pallas_call(
-        functools.partial(ffn_kernel, pieces),
-        name="ffn",
+        kernel,
+        name=name,
         grid_spec=pltpu.PrefetchScalarGridSpec(
             num_scalar_prefetch=1,
-            grid=(steps,),
-            in_specs=[read, read] + [weight(w, k) for k in range(3) for w in weights],
-            out_specs=[placed] * 3 + [near] * 2 + grads,
-            scratch_shapes=[pltpu.VMEM((units, depth), f32)] * len(grads),
+            grid=(specs["steps"],),
+            in_specs=in_specs,
+            out_specs=[specs[x] for x in outs] + [specs["grad"]] * grads,
+            scratch_shapes=[specs["total"]] * grads,
         ),
-        out_shape=[jax.ShapeDtypeStruct(shape, bf16) for shape in shapes],
-        compiler_params=pltpu.CompilerParams(vmem_limit_bytes=FFN_VMEM_LIMIT),
-    )(meta, flat(normed), flat(grad_out), *(list(weights) * 3))
+        out_shape=[specs[x.split("_")[0] + "_shape"] for x in outs]
+        + [specs["grad_shape"]] * grads,
+        compiler_params=pltpu.CompilerParams(vmem_limit_bytes=VMEM_LIMIT),
+    )(meta, *args)
+
+
+def hidden_units(meta, normed, grad_out, weights):
+    specs, pieces = hidden_specs(meta, normed, weights), len(weights)
+    return hidden_call(
+        functools.partial(hidden_kernel, pieces),
+        "hidden_units",
+        meta,
+        [specs["flat"](normed), specs["flat"](grad_out)] + list(weights) * 2,
+        [specs["row"]] * 2 + [specs["weight"](k) for k in range(2) for _ in weights],
+        ["unit"] * 3,
+        pieces == 2,
+        specs,
+    )
+
+
+def hidden_back(meta, normed, grad_out, hidden, slope, gated, weights):
+    specs, pieces = hidden_specs(meta, normed, weights), len(weights)
+    return hidden_call(
+        functools.partial(hidden_back_kernel, pieces),
+        "hidden_back",
+        meta,
+        [specs["flat"](normed), specs["flat"](grad_out), hidden, slope, gated]
+        + list(weights) * 3,
+        [specs["row"]] * 2
+        + [specs["near_unit"], specs["unit"], specs["unit"]]
+        + [specs["weight"](k) for k in range(3) for _ in weights],
+        ["unit", "unit", "near_row", "near_row"],
+        2 * (pieces == 2),
+        specs,
+    )
 
 
 def unit_grads_kernel(count, meta_ref, near_ref, far_ref, *refs):
@@ -839,32 +891,40 @@
         def _():
             inward[k].start()
 
-    for k in range(small):
-        send_in(k)
+    def pass_on(first, past):
+        @pl.when(inner)
+        def _():
+            for k in range(first, past):
+                i, at = chunks[k]
+                inward[k].wait_recv()
+                total = wide(sources[i][at]) + wide(from_end[i][at])
+                lows[i][at] = total.astype(lows[i].dtype)
+                across[k].start()
+                if k:
+                    send_out(k - 1)
+
+    def send_out(k):
+        i, at = chunks[k]
+        across[k].wait()
+        lows[i][at] = (wide(lows[i][at]) + wide(from_middle[i][at])).astype(lows[i].dtype)
+        outward[k].start()
+
+    send_in(0)
+    send_in(1)
     next(ahead)
     if over_f:
         from_f.wait_recv()
         sum_ref[...] = sum_ref[...] + slot[...]
-    send_in(small)
+    for k in range(2, small + 1):
+        send_in(k)
+    pass_on(0, 2)
     out_low[...] = (mid_ref[...] + result_of(ahead)).astype(bf16)
     out_share = gather_rank(wires, to, out_low, outputs)
     next(out_share)
+    pass_on(2, small + 1)
 
     @pl.when(inner)
     def _():
-        def send_out(k):
-            i, at = chunks[k]
-            across[k].wait()
-            lows[i][at] = (wide(lows[i][at]) + wide(from_middle[i][at])).astype(lows[i].dtype)
-            outward[k].start()
-
-        for k, (i, at) in enumerate(chunks):
-            inward[k].wait_recv()
-            total = wide(sources[i][at]) + wide(from_end[i][at])
-            lows[i][at] = total.astype(lows[i].dtype)
-            across[k].start()
-            if k:
-                send_out(k - 1)
         send_out(small)
 
     result_of(out_share)
@@ -1042,20 +1102,29 @@
             dot(attended, w_out_all).astype(bf16), inputs_part, gain_second, dy_part
         )
 
-        hidden, grad_gate, grad_up, dx_part, out_part, *unit_far = ffn(
-            meta, normed2, dy_all, w_units
-        )
+        hidden, slope, gated, *down_far = hidden_units(meta, normed2, dy_all, w_units)
+        grad_gate, grad_up, dx_part, out_part, *unit_far = hidden_back(
+            meta, normed2, dy_all, hidden, slope, gated, w_units
+        )
+
+        def unit_done(own, got):
+            low = (own.astype(f32) + got.astype(f32)).astype(bf16)
+            return low, flip(low, "context", 1)
+
         if n_f == 2:
-            down_got, gate_got, up_got = (flip(x, "fsdp", 1) for x in unit_far)
+            down_got, gate_got, up_got = (flip(x, "fsdp", 1) for x in (*down_far, *unit_far))
+            down_own = unit_grads(meta, 0, 2, *after((dy_all, [hidden]), dx_part))
+            down_done = unit_done(down_own, after(down_got, down_own))
+            gate_up_own = unit_grads(
+                meta, 0, 2, *after((normed2, [grad_gate, grad_up]), down_done[0])
+            )
+            dx_part = after(dx_part, gate_up_own)
         else:
             over_f = lambda x: lax.psum_scatter(x, "fsdp", scatter_dimension=1, tiled=True)
             down_own = over_f(unit_grads(meta, 0, 1, dy_all, [hidden]))
             gate_up_own = over_f(unit_grads(meta, 0, 1, normed2, [grad_gate, grad_up]))
-            down_got = gate_got = up_got = jnp.zeros_like(down_own)
-
-        def unit_done(own, got):
-            low = (own.astype(f32) + got.astype(f32)).astype(bf16)
-            return low, flip(low, "context", 1)
+            gate_got = up_got = jnp.zeros_like(down_own)
+            down_done = unit_done(down_own, gate_got)
 
         unit_whole = lambda low, other: by_bit(parity, low, other, 0).astype(f32)
 
@@ -1063,19 +1132,15 @@
             dx_part, middle, factor_second, gain_second, dy_part
         )
         grad_middle_low = grad_middle_low.reshape(rows, width)
-        if n_f == 2:
-            down_own = unit_grads(meta, 0, 2, *after((dy_all, [hidden]), grad_middle_low))
-        down_done = unit_done(down_own, after(down_got, grad_middle_low))
-        grad_attended = dot_cols(after(grad_middle_low, down_done[0]), w_out_all).astype(bf16)
+        gate_done = unit_done(gate_up_own[:units], after(gate_got, grad_middle_low))
+        grad_attended = dot_cols(
+            after(grad_middle_low, gate_done[0], down_done), w_out_all
+        ).astype(bf16)
 
         dq_low, dkv = attention_back(key_blocks, queries, grad_attended, lse, cosine, sine, kv)
-        if n_f == 2:
-            gate_up_own = unit_grads(meta, 0, 2, *after((normed2, [grad_gate, grad_up]), dkv))
-            dkv = after(dkv, gate_up_own)
-        dkv = kv_scatter(after(dkv, down_done))
-        gate_done = unit_done(gate_up_own[:units], after(gate_got, dkv))
-        up_done = unit_done(gate_up_own[units:], after(up_got, gate_done[0]))
-        dkv = after(dkv, gate_done[0], up_done[0])
+        dkv = kv_scatter(after(dkv, gate_done))
+        up_done = unit_done(gate_up_own[units:], after(up_got, dkv))
+        dkv = after(dkv, up_done[0])
         dkv_low = jnp.where(core == 0, rotate_back(dkv, cosine, sine), dkv).astype(bf16)
         attention_args = (
             (attended, after(grad_middle_low, dkv), 1),

time: 519 us -> 527 us (1.015)
    pallas_call x1 -> x2, Pallas kernels: 62 us -> 71.7 us  [hidden_call(): pl.pallas_call(kernel, name=name, grid_spec=pltpu.PrefetchScalarGridSpec(...]
    pallas_call x6, Pallas kernels: 266 us -> 256 us  [remote_call(): pl.pallas_call(kernel, name=name, out_shape=outs, in_specs=[spec(x) for x...]
    unnamed x65 -> x61, local copies, waits for them, and re-layouts: 11.7 us -> 12.3 us
  transfers between devices with their start and end apart: 14 -> 14, of which waited for: 5 -> 4; matrix products, arithmetic and copies ran while one was open for 11% -> 10% of each run, Pallas kernels for 45% -> 56%
where the time goes in v7:
time: 527 us; the launch traced here: 517 us
  Pallas kernels  387 us (73%)
  other arithmetic  39.2 us (7%)
  waiting for transfers between devices  28.2 us (5%)
  local copies, waits for them, and re-layouts  27 us (5%)
  matrix products  17.5 us (3%)
  starting transfers between devices  16.5 us (3%)
    pallas_call x6, Pallas kernels, remote_call(): pl.pallas_call(kernel, name=name, out_shape=outs, in_specs=[spec(x) for x...  256 us
    pallas_call x2, Pallas kernels, hidden_call(): pl.pallas_call(kernel, name=name, grid_spec=pltpu.PrefetchScalarGridSpec(...  71.7 us
    ppermute x14, waiting for transfers between devices, flip(): return lax.ppermute(x, axis, [(i, i ^ bit) for i in range(size)])  28.2 us
    pallas_call x2, Pallas kernels, unit_grads(): pl.pallas_call(functools.partial(unit_grads_kernel, count), name=f'unit_g...  22.9 us
    ppermute x14, starting transfers between devices, flip(): return lax.ppermute(x, axis, [(i, i ^ bit) for i in range(size)])  16.5 us
    pallas_call x1, Pallas kernels, attention_back(): pl.pallas_call(functools.partial(attention_back_kernel, kv.shape[1] // BL...  15 us
    unnamed x61, local copies, waits for them, and re-layouts  12.3 us
    dot_general x6, matrix products, dot_rows(): lax.dot_general(left, right, (((0,), (0,)), ((), ())), preferred_element_...  10.9 us
  transfers between devices with their start and end apart: 14, of which 4 were waited for; matrix products, arithmetic and copies ran while one was open for 10% of the time, Pallas kernels for 56%

profile of v7, /device:TPU:0, one launch (start us, length us, event | category | flops | bytes accessed | tf_op | source)
XLA Modules:
  0.0 517.0 jit_solution(11254587192321817281)
XLA Ops:
  4.7 3.0 collective-permute-start
  19.9 2.6 pad_maximum_fusion.refs_0_.refs_2_.refs_4_
  24.9 5.2 %collective-permute-done.1.refs_1_ = bf16[768,384]{1,0:T(8,128)(2,1)} collective-permute-done((bf16[768,384]{1,0:T(8,128)(2,1)}, bf16[768,384]{1,0:T(8,128)(2,1)}, u32[]{:S(2)}, u32[]{:S(2)}) %collective-permute-start.1) | collective-permute-done | bytes 589856 | tf_op jit(solution)/shard_map/ppermute | solution.py:984
  30.2 5.9 %qkv.1 = (bf16[512,1536]{1,0:T(8,128)(2,1)}, f32[512,1]{1,0:T(8,128)}, bf16[512,384]{1,0:T(8,128)(2,1)}, bf16[512,128]{1,0:T(8,128)(2,1)}) custom-call(s32[4]{0:T(128)} %pad_add_fusion.1.meta_ref, bf16[512,1536]{1,0:T(8,128)(2,1)} %x_ref.1, f32[1,1536]{1,0:T(1,128)} %bitcast.92, f32[1,512]{1,0:T(1,128)} %pad_maximum_fusion.6.bias_ref, ...), custom_call_target="tpu_custom_call" | custom-call | tf_op jit(solution)/shard_map/qkv/pallas_call | solution.py:209
  36.1 5.1 collective-permute-done.3
  46.7 17.4 %kv_gather.1.k_ref.v_ref = bf16[2,2048,128]{2,1,0:T(8,128)(2,1)} custom-call(bf16[512,128]{1,0:T(8,128)(2,1)} %get-tuple-element.76.own_ref), custom_call_target="tpu_custom_call" | custom-call | tf_op jit(solution)/shard_map/kv_gather/pallas_call | solution.py:592
  64.1 10.2 %attention.1 = (bf16[512,384]{1,0:T(8,128)(2,1)}, f32[3,512,1]{2,1,0:T(8,128)}) custom-call(s32[8]{0:T(128)} %pad_add_fusion.kb_ref, bf16[512,384]{1,0:T(8,128)(2,1)} %get-tuple-element.73.q_ref, bf16[2,2048,128]{2,1,0:T(8,128)(2,1)} %kv_gather.1.k_ref.v_ref, bf16[2,2048,128]{2,1,0:T(8,128)(2,1)} %kv_gather.1.k_ref.v_ref), custom_call_target="tpu_custom_call" | custom-call | tf_op jit(solution)/shard_map/attention/pallas_call | solution.py:85
  74.2 3.1 convolution_convert_fusion
  77.3 76.1 %middle_norm.1 = (f32[128,1536]{1,0:T(8,128)}, f32[128,1]{1,0:T(8,128)}, bf16[16,128,1536]{2,1,0:T(8,128)(2,1)}, bf16[16,128,1536]{2,1,0:T(8,128)(2,1)}) custom-call(bf16[4,128,1536]{2,1,0:T(8,128)(2,1)} %bitcast.84, bf16[128,1536]{1,0:T(8,128)(2,1)} %constant_dynamic-slice_fusion.7.x_ref, f32[1,1536]{1,0:T(1,128)} %bitcast.90, ...), custom_call_target="tpu_custom_call" | custom-call | tf_op jit(solution)/shard_map/middle_norm/pallas_call | solution.py:592
  153.7 29.7 %hidden_units.1 = (bf16[2048,1120]{1,0:T(8,128)(2,1)}, bf16[2048,1120]{1,0:T(8,128)(2,1)}, bf16[2048,1120]{1,0:T(8,128)(2,1)}, bf16[1120,768]{1,0:T(8,128)(2,1)}) custom-call(s32[4]{0:T(128)} %pad_add_fusion.1.meta_ref, bf16[2048,1536]{1,0:T(8,128)(2,1)} %bitcast.74, bf16[2048,1536]{1,0:T(8,128)(2,1)} %bitcast.78, ...), custom_call_target="tpu_custom_call" | custom-call | tf_op jit(solution)/shard_map/hidden_units/pallas_call | solution.py:333
  184.9 42.0 %hidden_back.1 = (bf16[2048,1120]{1,0:T(8,128)(2,1)}, bf16[2048,1120]{1,0:T(8,128)(2,1)}, bf16[1024,1536]{1,0:T(8,128)(2,1)}, bf16[1024,1536]{1,0:T(8,128)(2,1)}...) custom-call(s32[4]{0:T(128)} %pad_add_fusion.1.meta_ref, bf16[2048,1536]{1,0:T(8,128)(2,1)} %bitcast.75, ...), custom_call_target="tpu_custom_call" | custom-call | tf_op jit(solution)/shard_map/hidden_back/pallas_call | solution.py:333
  227.5 8.7 %unit_grads_0_1.1 = bf16[1120,768]{1,0:T(8,128)(2,1)} custom-call(s32[4]{0:T(128)} %pad_add_fusion.1.meta_ref, bf16[2048,1536]{1,0:T(8,128)(2,1)} %bitcast.80, bf16[2048,1536]{1,0:T(8,128)(2,1)} %bitcast.81, bf16[2048,1120]{1,0:T(8,128)(2,1)} %get-tuple-element.88.hid_ref.refs_0_), custom_call_target="tpu_custom_call" | custom-call | tf_op jit(solution)/shard_map/unit_grads_0_1/pallas_call | solution.py:402
  236.2 3.1 add_convert_fusion.2
  240.8 14.2 %unit_grads_0_2.1 = bf16[2240,768]{1,0:T(8,128)(2,1)} custom-call(s32[4]{0:T(128)} %pad_add_fusion.1.meta_ref, bf16[2048,1536]{1,0:T(8,128)(2,1)} %bitcast.76, bf16[2048,1536]{1,0:T(8,128)(2,1)} %bitcast.77, bf16[2048,1120]{1,0:T(8,128)(2,1)} %get-tuple-element.92.refs_0_, bf16[2048,1120]{1,0:T(8,128)(2,1)} %get-tuple-element.93.refs_1_), custom_call_target="tpu_custom_call" | custom-call | tf_op jit(solution)/shard_map/unit_grads_0_2/pallas_call | solution.py:402
  255.1 47.2 %middle_back.1 = (f32[128,1536]{1,0:T(8,128)}, f32[1,1536]{1,0:T(1,128)}, bf16[4,128,1536]{2,1,0:T(8,128)(2,1)}) custom-call(bf16[8,128,1536]{2,1,0:T(8,128)(2,1)} %bitcast.86, f32[128,1536]{1,0:T(8,128)} %get-tuple-element.95.mid_ref.refs_5_, f32[128,1]{1,0:T(8,128)} %get-tuple-element.96.factor_ref, f32[1,1536]{1,0:T(1,128)} %bitcast.91, ...), custom_call_target="tpu_custom_call" | custom-call | tf_op jit(solution)/shard_map/middle_back/pallas_call | solution.py:592
  302.3 3.1 add_convert_fusion.1
  305.4 2.7 collective-permute-start.9
  309.6 3.5 convolution_convert_fusion.3.do_ref
  313.1 15.0 %attention_back.1 = (bf16[512,384]{1,0:T(8,128)(2,1)}, bf16[2,2048,128]{2,1,0:T(8,128)(2,1)}) custom-call(s32[8]{0:T(128)} %pad_add_fusion.kb_ref, bf16[512,384]{1,0:T(8,128)(2,1)} %get-tuple-element.73.q_ref, bf16[512,384]{1,0:T(8,128)(2,1)} %convolution_convert_fusion.3.do_ref, f32[3,512,1]{2,1,0:T(8,128)} %get-tuple-element.101.lse_ref, ...), custom_call_target="tpu_custom_call" | custom-call | tf_op jit(solution)/shard_map/attention_back/pallas_call | solution.py:151
  328.1 17.6 %collective-permute-done.8 = bf16[1120,768]{1,0:T(8,128)(2,1)} collective-permute-done((bf16[1120,768]{1,0:T(8,128)(2,1)}, bf16[1120,768]{1,0:T(8,128)(2,1)}, u32[]{:S(2)}, u32[]{:S(2)}) %collective-permute-start.8) | collective-permute-done | bytes 1720352 | tf_op jit(solution)/shard_map/ppermute | solution.py:984
  345.6 17.5 %kv_scatter.1 = f32[512,128]{1,0:T(8,128)} custom-call(bf16[2,2048,128]{2,1,0:T(8,128)(2,1)} %get-tuple-element.103.part_ref), custom_call_target="tpu_custom_call" | custom-call | tf_op jit(solution)/shard_map/kv_scatter/pallas_call | solution.py:592
  363.2 3.2 add_convert_fusion
  369.0 2.7 collective-permute-start.12
  377.3 4.9 qkv_back.1
  382.3 28.7 %input_back.1 = (f32[1,5120]{1,0:T(1,128)}, bf16[4,128,1536]{2,1,0:T(8,128)(2,1)}) custom-call(bf16[4,128,1536]{2,1,0:T(8,128)(2,1)} %bitcast.83, bf16[128,1536]{1,0:T(8,128)(2,1)} %constant_dynamic-slice_fusion.7.x_ref, f32[128,1]{1,0:T(8,128)} %constant_dynamic-slice_fusion.4.factor_ref, f32[1,1536]{1,0:T(1,128)} %bitcast.93, ...), custom_call_target="tpu_custom_call" | custom-call | tf_op jit(solution)/shard_map/input_back/pallas_call | solution.py:592
  411.0 5.4 %fusion = f32[2240,768]{1,0:T(8,128)} fusion(bf16[1120,768]{1,0:T(8,128)(2,1)} %collective-permute-done.8, bf16[1120,768]{1,0:T(8,128)(2,1)} %add_convert_fusion.1, pred[]{:T(512)S(6)} %eq.19), kind=kLoop, calls=%fused_computation.3 | loop fusion | flops 17203200 | bytes 10321921 | tf_op jit(solution)/shard_map/convert_element_type | solution.py:1129
  416.4 5.5 %fusion.1 = f32[2240,768]{1,0:T(8,128)} fusion(bf16[1120,768]{1,0:T(8,128)(2,1)} %collective-permute-done.7, bf16[1120,768]{1,0:T(8,128)(2,1)} %add_convert_fusion.2, pred[]{:T(512)S(6)} %eq.19), kind=kLoop, calls=%fused_computation.5 | loop fusion | flops 17203200 | bytes 10321921 | tf_op jit(solution)/shard_map/convert_element_type | solution.py:1129
  421.8 2.2 fusion.4.refs_2_
  424.0 2.5 fusion.3.refs_1_
  426.5 2.4 fusion.2.refs_0_
  428.9 69.5 %context_sum.1 = (f32[384,768]{1,0:T(8,128)}, f32[768,384]{1,0:T(8,128)}, f32[1,5120]{1,0:T(1,128)}, bf16[4,768,128]{2,1,0:T(8,128)(2,1)}, bf16[4,128,1536]{2,1,0:T(8,128)(2,1)}) custom-call(bf16[384,768]{1,0:T(8,128)(2,1)} %fusion.2.refs_0_, bf16[768,384]{1,0:T(8,128)(2,1)} %fusion.3.refs_1_, bf16[768,128]{1,0:T(8,128)(2,1)} %fusion.4.refs_2_, ...), custom_call_target="tpu_custom_call" | custom-call | tf_op jit(solution)/shard_map/context_sum/pallas_call | solution.py:592
  504.9 4.8 convert_bitcast_fusion
  (140 shorter events, 51.0 us)
Async XLA Ops:
  0.6 15.6 %copy-start = (bf16[2240,768]{1,0:T(8,128)(2,1)S(1)}, bf16[2240,768]{1,0:T(8,128)(2,1)}, u32[]{:S(2)}) copy-start(bf16[2240,768]{1,0:T(8,128)(2,1)} %param.29) | copy-start | bytes 10321924
  4.7 18.5 %collective-permute-start = (bf16[1,1984]{1,0:T(2,128)(2,1)S(1)}, bf16[1,1984]{1,0:T(2,128)(2,1)S(1)}, u32[]{:S(2)}, u32[]{:S(2)}) collective-permute-start(bf16[1,1984]{1,0:T(2,128)(2,1)S(1)} %concatenate.64), channel_id=1, source_target_pairs={{0,16},{16,0},{1,17},{17,1},{2,18},{18,2},{3,19},{19,3},{4,20},{20... | collective-permute-start | bytes 11912 | tf_op jit(solution)/shard_map/ppermute | solution.py:984
  9.4 15.5 %collective-permute-start.2 = (bf16[768,128]{1,0:T(8,128)(2,1)}, bf16[768,128]{1,0:T(8,128)(2,1)}, u32[]{:S(2)}, u32[]{:S(2)}) collective-permute-start(bf16[768,128]{1,0:T(8,128)(2,1)} %dynamic-slice_select_fusion.refs_2_), channel_id=1, source_target_pairs={{0,16},{16,0},{1,17},{17,1},{2,18},{18,2},{3,19},{19,3},{4,20},{20... | collective-permute-start | bytes 589832 | tf_op jit(solution)/shard_map/ppermute | solution.py:984
  9.4 20.7 %collective-permute-start.1 = (bf16[768,384]{1,0:T(8,128)(2,1)}, bf16[768,384]{1,0:T(8,128)(2,1)}, u32[]{:S(2)}, u32[]{:S(2)}) collective-permute-start(bf16[768,384]{1,0:T(8,128)(2,1)} %refs_0_.3), channel_id=1, source_target_pairs={{0,16},{16,0},{1,17},{17,1},{2,18},{18,2},{3,19},{19,3},{4,20},{20... | collective-permute-start | bytes 1769480 | tf_op jit(solution)/shard_map/ppermute | solution.py:984
  23.5 17.7 %collective-permute-start.3 = (bf16[384,768]{1,0:T(8,128)(2,1)}, bf16[384,768]{1,0:T(8,128)(2,1)S(1)}, u32[]{:S(2)}, u32[]{:S(2)}) collective-permute-start(bf16[384,768]{1,0:T(8,128)(2,1)} %param.25), channel_id=1, source_target_pairs={{0,16},{16,0},{1,17},{17,1},{2,18},{18,2},{3,19},{19,3},{4,20},{20... | collective-permute-start | bytes 1769480 | tf_op jit(solution)/shard_map/ppermute | solution.py:984
  30.2 11.1 %copy-start.20 = (bf16[384,768]{1,0:T(8,128)(2,1)S(1)}, bf16[384,768]{1,0:T(8,128)(2,1)}, u32[]{:S(2)}) copy-start(bf16[384,768]{1,0:T(8,128)(2,1)} %param.25) | copy-start | bytes 1769476
  41.5 32.7 %copy-start.3 = (bf16[384,1536]{1,0:T(8,128)(2,1)}, bf16[384,1536]{1,0:T(8,128)(2,1)S(1)}, u32[]{:S(2)}) copy-start(bf16[384,1536]{1,0:T(8,128)(2,1)S(1)} %maximum_select_fusion.3) | copy-start | bytes 3538948
  41.5 112.2 %collective-permute-start.4 = (bf16[3360,768]{1,0:T(8,128)(2,1)}, bf16[3360,768]{1,0:T(8,128)(2,1)}, u32[]{:S(2)}, u32[]{:S(2)}) collective-permute-start(bf16[3360,768]{1,0:T(8,128)(2,1)} %pad_maximum_fusion.refs_0_.refs_2_.refs_4_), channel_id=1, source_target_pairs={{0,16},{16,0},{1,17},{17,1},{2,18},{18,2},{3,19},{19,3},{4,20},{20... | collective-permute-start | bytes 15482888 | tf_op jit(solution)/shard_map/ppermute | solution.py:984
  183.5 52.7 %collective-permute-start.5 = (bf16[1120,768]{1,0:T(8,128)(2,1)}, bf16[1120,768]{1,0:T(8,128)(2,1)S(1)}, u32[]{:S(2)}, u32[]{:S(2)}) collective-permute-start(bf16[1120,768]{1,0:T(8,128)(2,1)} %get-tuple-element.89), channel_id=1, source_target_pairs={{0,16},{16,0},{1,17},{17,1},{2,18},{18,2},{3,19},{19,3},{4,20},{20... | collective-permute-start | bytes 5160968 | tf_op jit(solution)/shard_map/ppermute | solution.py:984
  226.9 75.4 %collective-permute-start.6 = (bf16[1120,768]{1,0:T(8,128)(2,1)}, bf16[1120,768]{1,0:T(8,128)(2,1)}, u32[]{:S(2)}, u32[]{:S(2)}) collective-permute-start(bf16[1120,768]{1,0:T(8,128)(2,1)} %get-tuple-element.98), channel_id=1, source_target_pairs={{0,16},{16,0},{1,17},{17,1},{2,18},{18,2},{3,19},{19,3},{4,20},{20... | collective-permute-start | bytes 5160968 | tf_op jit(solution)/shard_map/ppermute | solution.py:984
  239.3 70.3 %collective-permute-start.7 = (bf16[1120,768]{1,0:T(8,128)(2,1)}, bf16[1120,768]{1,0:T(8,128)(2,1)}, u32[]{:S(2)}, u32[]{:S(2)}) collective-permute-start(bf16[1120,768]{1,0:T(8,128)(2,1)} %add_convert_fusion.2), channel_id=1, source_target_pairs={{0,4},{4,0},{8,12},{12,8},{1,5},{5,1},{9,13},{13,9},{2,6},{6,2},{1... | collective-permute-start | bytes 5160968 | tf_op jit(solution)/shard_map/ppermute | solution.py:984
  255.1 47.3 %copy-start.2 = (bf16[2240,768]{1,0:T(8,128)(2,1)S(1)}, bf16[2240,768]{1,0:T(8,128)(2,1)}, u32[]{:S(2)}) copy-start(bf16[2240,768]{1,0:T(8,128)(2,1)} %unit_grads_0_2.1) | copy-start | bytes 10321924
  305.4 40.2 %collective-permute-start.8 = (bf16[1120,768]{1,0:T(8,128)(2,1)}, bf16[1120,768]{1,0:T(8,128)(2,1)}, u32[]{:S(2)}, u32[]{:S(2)}) collective-permute-start(bf16[1120,768]{1,0:T(8,128)(2,1)} %add_convert_fusion.1), channel_id=1, source_target_pairs={{0,4},{4,0},{8,12},{12,8},{1,5},{5,1},{9,13},{13,9},{2,6},{6,2},{1... | collective-permute-start | bytes 5160968 | tf_op jit(solution)/shard_map/ppermute | solution.py:984
  305.4 57.8 %collective-permute-start.9 = (bf16[1120,768]{1,0:T(8,128)(2,1)}, bf16[1120,768]{1,0:T(8,128)(2,1)}, u32[]{:S(2)}, u32[]{:S(2)}) collective-permute-start(bf16[1120,768]{1,0:T(8,128)(2,1)} %get-tuple-element.104), channel_id=1, source_target_pairs={{0,16},{16,0},{1,17},{17,1},{2,18},{18,2},{3,19},{19,3},{4,20},{20... | collective-permute-start | bytes 5160968 | tf_op jit(solution)/shard_map/ppermute | solution.py:984
  363.2 3.2 copy-start.7
  363.2 3.2 copy-start.8
  366.5 5.2 copy-start.21
  366.5 5.2 copy-start.24
  367.5 8.9 %copy-start.4 = (bf16[512,128]{1,0:T(8,128)(2,1)}, bf16[512,128]{1,0:T(8,128)(2,1)S(1)}, u32[]{:S(2)}) copy-start(bf16[512,128]{1,0:T(8,128)(2,1)S(1)} %fusion.12.dkv_ref) | copy-start | bytes 393220
  367.6 5.5 %copy-start.15 = (bf16[512,384]{1,0:T(8,128)(2,1)S(1)}, bf16[512,384]{1,0:T(8,128)(2,1)}, u32[]{:S(2)}) copy-start(bf16[512,384]{1,0:T(8,128)(2,1)} %get-tuple-element.110.dq_ref) | copy-start | bytes 1179652
  369.0 52.8 %collective-permute-start.12 = (bf16[768,128]{1,0:T(8,128)(2,1)}, bf16[768,128]{1,0:T(8,128)(2,1)}, u32[]{:S(2)}, u32[]{:S(2)}) collective-permute-start(bf16[768,128]{1,0:T(8,128)(2,1)} %convolution_convert_fusion.4), channel_id=1, source_target_pairs={{0,16},{16,0},{1,17},{17,1},{2,18},{18,2},{3,19},{19,3},{4,20},{20... | collective-permute-start | bytes 589832 | tf_op jit(solution)/shard_map/ppermute | solution.py:984
  373.0 3.7 copy-start.23
  374.5 49.6 %collective-permute-start.11 = (bf16[768,384]{1,0:T(8,128)(2,1)}, bf16[768,384]{1,0:T(8,128)(2,1)}, u32[]{:S(2)}, u32[]{:S(2)}) collective-permute-start(bf16[768,384]{1,0:T(8,128)(2,1)} %convolution_convert_fusion.1), channel_id=1, source_target_pairs={{0,16},{16,0},{1,17},{17,1},{2,18},{18,2},{3,19},{19,3},{4,20},{20... | collective-permute-start | bytes 1769480 | tf_op jit(solution)/shard_map/ppermute | solution.py:984
  374.5 52.1 %collective-permute-start.10 = (bf16[384,768]{1,0:T(8,128)(2,1)}, bf16[384,768]{1,0:T(8,128)(2,1)}, u32[]{:S(2)}, u32[]{:S(2)}) collective-permute-start(bf16[384,768]{1,0:T(8,128)(2,1)} %convolution_convert_fusion.2), channel_id=1, source_target_pairs={{0,16},{16,0},{1,17},{17,1},{2,18},{18,2},{3,19},{19,3},{4,20},{20... | collective-permute-start | bytes 1769480 | tf_op jit(solution)/shard_map/ppermute | solution.py:984
  376.5 52.4 %collective-permute-start.13 = (bf16[1120,768]{1,0:T(8,128)(2,1)}, bf16[1120,768]{1,0:T(8,128)(2,1)S(1)}, u32[]{:S(2)}, u32[]{:S(2)}) collective-permute-start(bf16[1120,768]{1,0:T(8,128)(2,1)} %add_convert_fusion), channel_id=1, source_target_pairs={{0,4},{4,0},{8,12},{12,8},{1,5},{5,1},{9,13},{13,9},{2,6},{6,2},{1... | collective-permute-start | bytes 5160968 | tf_op jit(solution)/shard_map/ppermute | solution.py:984
  416.3 5.5 %copy-start.5 = (bf16[512,128]{1,0:T(8,128)(2,1)S(1)}, bf16[512,128]{1,0:T(8,128)(2,1)}, u32[]{:S(2)}) copy-start(bf16[512,128]{1,0:T(8,128)(2,1)} %copy-done.4) | copy-start | bytes 393220
  416.3 5.5 %copy-start.14 = (bf16[512,1536]{1,0:T(8,128)(2,1)S(1)}, bf16[512,1536]{1,0:T(8,128)(2,1)}, u32[]{:S(2)}) copy-start(bf16[512,1536]{1,0:T(8,128)(2,1)} %get-tuple-element.108) | copy-start | bytes 4718596
  416.4 7.7 %copy-start.16 = (bf16[512,384]{1,0:T(8,128)(2,1)S(1)}, bf16[512,384]{1,0:T(8,128)(2,1)}, u32[]{:S(2)}) copy-start(bf16[512,384]{1,0:T(8,128)(2,1)} %get-tuple-element.110.dq_ref) | copy-start | bytes 1179652
  421.8 4.7 copy-start.22
  421.8 4.7 copy-start.25
  504.9 4.8 copy-start.12
  513.5 3.0 copy-start.1
  (8 other events, 11.5 us)

commit v8 on v6

--- a/solution.py
+++ b/solution.py
@@ -547,7 +547,7 @@
         + [
             pltpu.SemaphoreType.DMA((copies,)),
             pltpu.SemaphoreType.DMA((copies,)),
-            pltpu.SemaphoreType.DMA((6,)),
+            pltpu.SemaphoreType.DMA((8,)),
         ],
         compiler_params=pltpu.CompilerParams(
             collective_id=key, has_side_effects=True, vmem_limit_bytes=VMEM_LIMIT
@@ -632,19 +632,45 @@
 
 
 def middle_kernel(
-    part, x_ref, gain_ref, dy_ref, mid_ref, factor_ref, out, dys, own, core, sent, got, xn, *sems
+    part,
+    x_ref,
+    gain_ref,
+    dy_ref,
+    dy_y,
+    dy_z,
+    dy_far,
+    mid_ref,
+    factor_ref,
+    out,
+    dys,
+    own,
+    core,
+    sent,
+    got,
+    xn,
+    *sems,
 ):
     wires, to = Wires(*sems), partners()
     blocks = out.shape[0] // 2
+    size = xn.shape[0] // 2
+    low, high = pl.ds(0, size), pl.ds(size, size)
     meet([to[k] for k in ("core", "y", "z", "far")])
     summed = scatter_rank(wires, to, part, own, core, sent, got)
     next(summed)
-    dy_far = wires.copy(dy_ref, dys.at[blocks], to["far"])
-    mine = [wires.here(dy_ref, dys.at[0])]
-    dy_near = gather_pair(wires, to, dy_ref, dys, 0)
-    next(dy_near)
+    mine = [
+        wires.here(block, dys.at[k])
+        for block, k in ((dy_ref, 0), (dy_y, 1), (dy_z, 2), (dy_far, blocks))
+    ]
+    via_z = wires.copy(dy_y.at[low], dys.at[3, low], to["z"])
+    dy_last = gather_pair(wires, to, dy_far, dys, blocks)
+    next(dy_last)
     next(summed)
-    next(dy_near)
+    via_y = wires.copy(dy_z.at[high], dys.at[3, high], to["y"])
+    ends = [
+        wires.copy(block, dys.at[4 + k], to["core"])
+        for k, block in enumerate((dy_ref, dy_y, dy_z))
+    ]
+    next(dy_last)
     middle = wide(x_ref[...]) + result_of(summed)
     mid_ref[...] = middle
     factor = lax.rsqrt(jnp.mean(middle * middle, axis=-1, keepdims=True) + EPSILON)
@@ -655,20 +681,18 @@
     xn_near = gather_pair(wires, to, xn, out, 0)
     next(xn_near)
     next(xn_near)
-    next(dy_near)
+    via_z.wait_recv()
+    via_y.wait_recv()
+    ends.append(wires.copy(dys.at[3], dys.at[7], to["core"]))
+    next(dy_last)
     next(xn_near)
-    dy_far.wait_recv()
-    dy_last = gather_pair(wires, to, dys.at[blocks], dys, blocks)
-    next(dy_last)
-    next(dy_last)
     xn_far.wait_recv()
     xn_last = gather_pair(wires, to, out.at[blocks], out, blocks)
     next(xn_last)
     next(xn_last)
-    ends = result_of(dy_near) + result_of(xn_near)
-    next(dy_last)
+    ends += result_of(dy_last) + result_of(xn_near)
     next(xn_last)
-    ends += result_of(dy_last) + result_of(xn_last)
+    ends += result_of(xn_last)
     for one in ends:
         one.wait_recv()
     for one in mine:
@@ -676,13 +700,13 @@
     wires.finish()
 
 
-def middle_norm(part, inputs_part, gain, dy_part):
+def middle_norm(part, inputs_part, gain, dy_blocks):
     rows, width = inputs_part.shape
     return remote_call(
         middle_kernel,
         "middle_norm",
         2,
-        [part.reshape(4, rows, width), inputs_part, gain, dy_part],
+        [part.reshape(4, rows, width), inputs_part, gain, *dy_blocks],
         [
             jax.ShapeDtypeStruct((rows, width), f32),
             jax.ShapeDtypeStruct((rows, 1), f32),
@@ -697,7 +721,7 @@
             pltpu.VMEM((rows, width), bf16),
         ],
         48,
-        ([False, True, True, True], [True, True, False, False]),
+        ([False] + [True] * 6, [True, True, False, False]),
     )
 
 
@@ -839,32 +863,40 @@
         def _():
             inward[k].start()
 
-    for k in range(small):
-        send_in(k)
+    def pass_on(first, past):
+        @pl.when(inner)
+        def _():
+            for k in range(first, past):
+                i, at = chunks[k]
+                inward[k].wait_recv()
+                total = wide(sources[i][at]) + wide(from_end[i][at])
+                lows[i][at] = total.astype(lows[i].dtype)
+                across[k].start()
+                if k:
+                    send_out(k - 1)
+
+    def send_out(k):
+        i, at = chunks[k]
+        across[k].wait()
+        lows[i][at] = (wide(lows[i][at]) + wide(from_middle[i][at])).astype(lows[i].dtype)
+        outward[k].start()
+
+    send_in(0)
+    send_in(1)
     next(ahead)
     if over_f:
         from_f.wait_recv()
         sum_ref[...] = sum_ref[...] + slot[...]
-    send_in(small)
+    for k in range(2, small + 1):
+        send_in(k)
+    pass_on(0, 2)
     out_low[...] = (mid_ref[...] + result_of(ahead)).astype(bf16)
     out_share = gather_rank(wires, to, out_low, outputs)
     next(out_share)
+    pass_on(2, small + 1)
 
     @pl.when(inner)
     def _():
-        def send_out(k):
-            i, at = chunks[k]
-            across[k].wait()
-            lows[i][at] = (wide(lows[i][at]) + wide(from_middle[i][at])).astype(lows[i].dtype)
-            outward[k].start()
-
-        for k, (i, at) in enumerate(chunks):
-            inward[k].wait_recv()
-            total = wide(sources[i][at]) + wide(from_end[i][at])
-            lows[i][at] = total.astype(lows[i].dtype)
-            across[k].start()
-            if k:
-                send_out(k - 1)
         send_out(small)
 
     result_of(out_share)
@@ -999,7 +1031,7 @@
         w_q = pieces_f(w_query, 0)
         w_kv = pieces_f(w_kv_own, 0)
         small = gather_f(small, 0)
-        w_out_all = gather_f(after(w_out, small), 1)
+        w_out_all = gather_f(after(w_out, small, w_q, w_kv), 1)
         piece = attn_gain.shape[0]
         gain_first = small[:, :piece].reshape(1, width).astype(f32)
         gain_second = small[:, piece : 2 * piece].reshape(1, width).astype(f32)
@@ -1031,6 +1063,13 @@
         ).reshape(-1)
         cosine, sine = rope_tables(positions)
         bias = jnp.concatenate([bq.reshape(1, -1), b_kv], axis=1)
+        dy_blocks = [
+            dy_part,
+            flip(dy_part, "tensor", 2),
+            flip(dy_part, "context", 1),
+            flip(dy_part, "context", 2),
+        ]
+        bias = after(bias, dy_blocks)
         normed, factor_first, queries, kv_own = qkv(
             meta, inputs, gain_first, bias, cosine, sine, w_q, w_kv
         )
@@ -1039,7 +1078,7 @@
         attended, lse = attention(key_blocks, queries, kv)
         inputs_part = lax.dynamic_slice_in_dim(inputs, t * part, part, 0)
         middle, factor_second, normed2, dy_all = middle_norm(
-            dot(attended, w_out_all).astype(bf16), inputs_part, gain_second, dy_part
+            dot(attended, w_out_all).astype(bf16), inputs_part, gain_second, dy_blocks
         )
 
         hidden, grad_gate, grad_up, dx_part, out_part, *unit_far = ffn(
@@ -1072,7 +1111,7 @@
         if n_f == 2:
             gate_up_own = unit_grads(meta, 0, 2, *after((normed2, [grad_gate, grad_up]), dkv))
             dkv = after(dkv, gate_up_own)
-        dkv = kv_scatter(after(dkv, down_done))
+        dkv = kv_scatter(after(dkv, down_done, gate_got))
         gate_done = unit_done(gate_up_own[:units], after(gate_got, dkv))
         up_done = unit_done(gate_up_own[units:], after(up_got, gate_done[0]))
         dkv = after(dkv, gate_done[0], up_done[0])

time: 519 us -> 497 us (0.958)
  Pallas kernels: 387 us -> 345 us
  waiting for transfers between devices: 27.6 us -> 40.5 us
  starting transfers between devices: 14.5 us -> 23.2 us
    pallas_call x6, Pallas kernels: 266 us -> 225 us  [remote_call(): pl.pallas_call(kernel, name=name, out_shape=outs, in_specs=[spec(x) for x...]
    ppermute x14 -> x17, waiting for transfers between devices: 27.6 us -> 40.5 us  [flip(): return lax.ppermute(x, axis, [(i, i ^ bit) for i in range(size)])]
    ppermute x14 -> x17, starting transfers between devices: 14.5 us -> 23.2 us  [flip(): return lax.ppermute(x, axis, [(i, i ^ bit) for i in range(size)])]
    unnamed x65 -> x73, local copies, waits for them, and re-layouts: 11.7 us -> 10.9 us
  transfers between devices with their start and end apart: 14 -> 17, of which waited for: 5 -> 6; matrix products, arithmetic and copies ran while one was open for 11% -> 12% of each run, Pallas kernels for 45% -> 44%
where the time goes in v8:
time: 497 us; the launch traced here: 489 us
  Pallas kernels  345 us (69%)
  waiting for transfers between devices  40.5 us (8%)
  other arithmetic  35.7 us (7%)
  local copies, waits for them, and re-layouts  26.2 us (5%)
  starting transfers between devices  23.2 us (5%)
  matrix products  17.2 us (3%)
    pallas_call x6, Pallas kernels, remote_call(): pl.pallas_call(kernel, name=name, out_shape=outs, in_specs=[spec(x) for x...  225 us
    pallas_call x1, Pallas kernels, ffn(): pl.pallas_call(functools.partial(ffn_kernel, pieces), name='ffn', grid_sp...  62 us
    ppermute x17, waiting for transfers between devices, flip(): return lax.ppermute(x, axis, [(i, i ^ bit) for i in range(size)])  40.5 us
    ppermute x17, starting transfers between devices, flip(): return lax.ppermute(x, axis, [(i, i ^ bit) for i in range(size)])  23.2 us
    pallas_call x2, Pallas kernels, unit_grads(): pl.pallas_call(functools.partial(unit_grads_kernel, count), name=f'unit_g...  22.9 us
    pallas_call x1, Pallas kernels, attention_back(): pl.pallas_call(functools.partial(attention_back_kernel, kv.shape[1] // BL...  15 us
    dot_general x6, matrix products, dot_rows(): lax.dot_general(left, right, (((0,), (0,)), ((), ())), preferred_element_...  10.9 us
    unnamed x73, local copies, waits for them, and re-layouts  10.9 us
  transfers between devices with their start and end apart: 17, of which 6 were waited for; matrix products, arithmetic and copies ran while one was open for 12% of the time, Pallas kernels for 44%

profile of v8, /device:TPU:0, one launch (start us, length us, event | category | flops | bytes accessed | tf_op | source)
XLA Modules:
  0.0 489.4 jit_solution(13244587670933406350)
XLA Ops:
  1.7 4.1 collective-permute-start.3
  23.7 2.6 pad_maximum_fusion.refs_0_.refs_2_.refs_4_
  28.8 3.9 collective-permute-done.5.refs_3_
  35.7 5.8 %qkv.1 = (bf16[512,1536]{1,0:T(8,128)(2,1)}, f32[512,1]{1,0:T(8,128)}, bf16[512,384]{1,0:T(8,128)(2,1)}, bf16[512,128]{1,0:T(8,128)(2,1)}) custom-call(s32[4]{0:T(128)} %pad_add_fusion.1.meta_ref, bf16[512,1536]{1,0:T(8,128)(2,1)} %x_ref.1, f32[1,1536]{1,0:T(1,128)} %bitcast.88, f32[1,512]{1,0:T(1,128)} %pad_maximum_fusion.6.bias_ref, ...), custom_call_target="tpu_custom_call" | custom-call | tf_op jit(solution)/shard_map/qkv/pallas_call | solution.py:210
  41.5 4.2 collective-permute-done.6
  50.6 14.8 %kv_gather.1.k_ref.v_ref = bf16[2,2048,128]{2,1,0:T(8,128)(2,1)} custom-call(bf16[512,128]{1,0:T(8,128)(2,1)} %get-tuple-element.76.own_ref), custom_call_target="tpu_custom_call" | custom-call | tf_op jit(solution)/shard_map/kv_gather/pallas_call | solution.py:540
  65.4 10.2 %attention.1 = (bf16[512,384]{1,0:T(8,128)(2,1)}, f32[3,512,1]{2,1,0:T(8,128)}) custom-call(s32[8]{0:T(128)} %pad_add_fusion.kb_ref, bf16[512,384]{1,0:T(8,128)(2,1)} %get-tuple-element.73.q_ref, bf16[2,2048,128]{2,1,0:T(8,128)(2,1)} %kv_gather.1.k_ref.v_ref, bf16[2,2048,128]{2,1,0:T(8,128)(2,1)} %kv_gather.1.k_ref.v_ref), custom_call_target="tpu_custom_call" | custom-call | tf_op jit(solution)/shard_map/attention/pallas_call | solution.py:86
  75.6 3.1 convolution_convert_fusion
  78.7 62.7 %middle_norm.1 = (f32[128,1536]{1,0:T(8,128)}, f32[128,1]{1,0:T(8,128)}, bf16[16,128,1536]{2,1,0:T(8,128)(2,1)}, bf16[16,128,1536]{2,1,0:T(8,128)(2,1)}) custom-call(bf16[4,128,1536]{2,1,0:T(8,128)(2,1)} %bitcast.82, bf16[128,1536]{1,0:T(8,128)(2,1)} %constant_dynamic-slice_fusion.6.x_ref, f32[1,1536]{1,0:T(1,128)} %bitcast.90, bf16[128,1536]{1,0:T(8,128)(2,1)} %copy-done.3, ...), custom_call_target="tpu_custom_call" | custom-call | tf_op jit(solution)/shard_map/middle_norm/pallas_call | solution.py:540
  141.4 14.9 %collective-permute-done.7.refs_1_.refs_3_.refs_5_ = bf16[3360,768]{1,0:T(8,128)(2,1)} collective-permute-done((bf16[3360,768]{1,0:T(8,128)(2,1)}, bf16[3360,768]{1,0:T(8,128)(2,1)}, u32[]{:S(2)}, u32[]{:S(2)}) %collective-permute-start.7) | collective-permute-done | bytes 5160992 | tf_op jit(solution)/shard_map/ppermute | solution.py:956
  156.3 62.0 %ffn.1 = (bf16[2048,1120]{1,0:T(8,128)(2,1)}, bf16[2048,1120]{1,0:T(8,128)(2,1)}, bf16[2048,1120]{1,0:T(8,128)(2,1)}, bf16[1024,1536]{1,0:T(8,128)(2,1)}, bf16[1...) custom-call(s32[4]{0:T(128)} %pad_add_fusion.1.meta_ref, ...), custom_call_target="tpu_custom_call" | custom-call | tf_op jit(solution)/shard_map/ffn/pallas_call | solution.py:313
  219.6 32.0 %middle_back.1 = (f32[128,1536]{1,0:T(8,128)}, f32[1,1536]{1,0:T(1,128)}, bf16[4,128,1536]{2,1,0:T(8,128)(2,1)}) custom-call(bf16[8,128,1536]{2,1,0:T(8,128)(2,1)} %bitcast.84, f32[128,1536]{1,0:T(8,128)} %get-tuple-element.82.mid_ref.refs_5_, f32[128,1]{1,0:T(8,128)} %get-tuple-element.83.factor_ref, f32[1,1536]{1,0:T(1,128)} %bitcast.91, ...), custom_call_target="tpu_custom_call" | custom-call | tf_op jit(solution)/shard_map/middle_back/pallas_call | solution.py:540
  252.5 8.7 %unit_grads_0_1.1 = bf16[1120,768]{1,0:T(8,128)(2,1)} custom-call(s32[4]{0:T(128)} %pad_add_fusion.1.meta_ref, bf16[2048,1536]{1,0:T(8,128)(2,1)} %bitcast.78, bf16[2048,1536]{1,0:T(8,128)(2,1)} %bitcast.79, bf16[2048,1120]{1,0:T(8,128)(2,1)} %get-tuple-element.87.refs_0_), custom_call_target="tpu_custom_call" | custom-call | tf_op jit(solution)/shard_map/unit_grads_0_1/pallas_call | solution.py:350
  261.2 2.5 add_convert_fusion.2
  268.0 3.1 convolution_convert_fusion.3.do_ref
  271.1 15.0 %attention_back.1 = (bf16[512,384]{1,0:T(8,128)(2,1)}, bf16[2,2048,128]{2,1,0:T(8,128)(2,1)}) custom-call(s32[8]{0:T(128)} %pad_add_fusion.kb_ref, bf16[512,384]{1,0:T(8,128)(2,1)} %get-tuple-element.73.q_ref, bf16[512,384]{1,0:T(8,128)(2,1)} %convolution_convert_fusion.3.do_ref, f32[3,512,1]{2,1,0:T(8,128)} %get-tuple-element.91.lse_ref, ...), custom_call_target="tpu_custom_call" | custom-call | tf_op jit(solution)/shard_map/attention_back/pallas_call | solution.py:152
  286.1 14.3 %unit_grads_0_2.1 = bf16[2240,768]{1,0:T(8,128)(2,1)} custom-call(s32[4]{0:T(128)} %pad_add_fusion.1.meta_ref, bf16[2048,1536]{1,0:T(8,128)(2,1)} %bitcast.75, bf16[2048,1536]{1,0:T(8,128)(2,1)} %bitcast.76, bf16[2048,1120]{1,0:T(8,128)(2,1)} %get-tuple-element.96.refs_0_, bf16[2048,1120]{1,0:T(8,128)(2,1)} %get-tuple-element.97.refs_1_), custom_call_target="tpu_custom_call" | custom-call | tf_op jit(solution)/shard_map/unit_grads_0_2/pallas_call | solution.py:350
  300.4 3.1 collective-permute-done.9
  303.5 17.6 %kv_scatter.1 = f32[512,128]{1,0:T(8,128)} custom-call(bf16[2,2048,128]{2,1,0:T(8,128)(2,1)} %get-tuple-element.100.part_ref), custom_call_target="tpu_custom_call" | custom-call | tf_op jit(solution)/shard_map/kv_scatter/pallas_call | solution.py:540
  321.1 3.7 add_convert_fusion.1
  324.9 3.9 collective-permute-done.11
  328.8 2.0 add_convert_fusion
  341.3 4.7 qkv_back.1
  346.0 27.7 %input_back.1 = (f32[1,5120]{1,0:T(1,128)}, bf16[4,128,1536]{2,1,0:T(8,128)(2,1)}) custom-call(bf16[4,128,1536]{2,1,0:T(8,128)(2,1)} %bitcast.81, bf16[128,1536]{1,0:T(8,128)(2,1)} %constant_dynamic-slice_fusion.6.x_ref, f32[128,1]{1,0:T(8,128)} %constant_dynamic-slice_fusion.4.factor_ref, f32[1,1536]{1,0:T(1,128)} %bitcast.89, ...), custom_call_target="tpu_custom_call" | custom-call | tf_op jit(solution)/shard_map/input_back/pallas_call | solution.py:540
  373.7 4.8 fusion.1
  378.5 2.2 fusion.4.refs_2_
  380.7 2.5 fusion.3.refs_1_
  383.2 2.4 fusion.2.refs_0_
  385.6 5.3 %fusion = f32[2240,768]{1,0:T(8,128)} fusion(bf16[1120,768]{1,0:T(8,128)(2,1)} %collective-permute-done.16, bf16[1120,768]{1,0:T(8,128)(2,1)} %add_convert_fusion.1, pred[]{:T(512)S(6)} %eq.19), kind=kLoop, calls=%fused_computation.3 | loop fusion | flops 17203200 | bytes 10321921 | tf_op jit(solution)/shard_map/convert_element_type | solution.py:1099
  390.9 10.5 %collective-permute-done.15 = bf16[1120,768]{1,0:T(8,128)(2,1)} collective-permute-done((bf16[1120,768]{1,0:T(8,128)(2,1)S(1)}, bf16[1120,768]{1,0:T(8,128)(2,1)}, u32[]{:S(2)}, u32[]{:S(2)}) %collective-permute-start.15) | collective-permute-done | bytes 1720352 | tf_op jit(solution)/shard_map/ppermute | solution.py:956
  401.4 69.7 %context_sum.1 = (f32[384,768]{1,0:T(8,128)}, f32[768,384]{1,0:T(8,128)}, f32[1,5120]{1,0:T(1,128)}, bf16[4,768,128]{2,1,0:T(8,128)(2,1)}, bf16[4,128,1536]{2,1,0:T(8,128)(2,1)}) custom-call(bf16[384,768]{1,0:T(8,128)(2,1)} %fusion.2.refs_0_, bf16[768,384]{1,0:T(8,128)(2,1)} %fusion.3.refs_1_, bf16[768,128]{1,0:T(8,128)(2,1)} %fusion.4.refs_2_, ...), custom_call_target="tpu_custom_call" | custom-call | tf_op jit(solution)/shard_map/context_sum/pallas_call | solution.py:540
  477.7 4.8 convert_bitcast_fusion
  (157 shorter events, 59.1 us)
Async XLA Ops:
  1.7 19.5 %copy-start.3 = (bf16[128,1536]{1,0:T(8,128)(2,1)}, bf16[128,1536]{1,0:T(8,128)(2,1)S(1)}, u32[]{:S(2)}) copy-start(bf16[128,1536]{1,0:T(8,128)(2,1)S(1)} %constant_dynamic-slice_fusion.7.dy_ref) | copy-start | bytes 1179652
  1.7 34.0 %collective-permute-start.3 = (bf16[128,1536]{1,0:T(8,128)(2,1)S(1)}, bf16[128,1536]{1,0:T(8,128)(2,1)S(1)}, u32[]{:S(2)}, u32[]{:S(2)}) collective-permute-start(bf16[128,1536]{1,0:T(8,128)(2,1)S(1)} %constant_dynamic-slice_fusion.7.dy_ref), channel_id=1, source_target_pairs={{0,8},{4,12},{8,0},{12,4},{1,9},{5,13},{9,1},{13,5},{2,10},{6,14},... | collective-permute-start | bytes 1179656 | tf_op jit(solution)/shard_map/ppermute | solution.py:956
  5.8 29.9 %collective-permute-start.2 = (bf16[128,1536]{1,0:T(8,128)(2,1)S(1)}, bf16[128,1536]{1,0:T(8,128)(2,1)}, u32[]{:S(2)}, u32[]{:S(2)}) collective-permute-start(bf16[128,1536]{1,0:T(8,128)(2,1)S(1)} %constant_dynamic-slice_fusion.7.dy_ref), channel_id=1, source_target_pairs={{0,4},{4,0},{8,12},{12,8},{1,5},{5,1},{9,13},{13,9},{2,6},{6,2},{1... | collective-permute-start | bytes 1179656 | tf_op jit(solution)/shard_map/ppermute | solution.py:956
  7.4 28.3 %collective-permute-start.1 = (bf16[128,1536]{1,0:T(8,128)(2,1)S(1)}, bf16[128,1536]{1,0:T(8,128)(2,1)}, u32[]{:S(2)}, u32[]{:S(2)}) collective-permute-start(bf16[128,1536]{1,0:T(8,128)(2,1)S(1)} %constant_dynamic-slice_fusion.7.dy_ref), channel_id=1, source_target_pairs={{0,2},{1,3},{2,0},{3,1},{4,6},{5,7},{6,4},{7,5},{8,10},{9,11},{10,... | collective-permute-start | bytes 1179656 | tf_op jit(solution)/shard_map/ppermute | solution.py:956
  12.6 14.4 %collective-permute-start = (bf16[1,1984]{1,0:T(2,128)(2,1)S(1)}, bf16[1,1984]{1,0:T(2,128)(2,1)S(1)}, u32[]{:S(2)}, u32[]{:S(2)}) collective-permute-start(bf16[1,1984]{1,0:T(2,128)(2,1)S(1)} %concatenate.64), channel_id=1, source_target_pairs={{0,16},{16,0},{1,17},{17,1},{2,18},{18,2},{3,19},{19,3},{4,20},{20... | collective-permute-start | bytes 11912 | tf_op jit(solution)/shard_map/ppermute | solution.py:956
  14.1 18.6 %collective-permute-start.4 = (bf16[768,384]{1,0:T(8,128)(2,1)}, bf16[768,384]{1,0:T(8,128)(2,1)S(1)}, u32[]{:S(2)}, u32[]{:S(2)}) collective-permute-start(bf16[768,384]{1,0:T(8,128)(2,1)} %refs_0_.3), channel_id=1, source_target_pairs={{0,16},{16,0},{1,17},{17,1},{2,18},{18,2},{3,19},{19,3},{4,20},{20... | collective-permute-start | bytes 1769480 | tf_op jit(solution)/shard_map/ppermute | solution.py:956
  23.7 9.0 %copy-start.23 = (bf16[384,768]{1,0:T(8,128)(2,1)S(1)}, bf16[384,768]{1,0:T(8,128)(2,1)}, u32[]{:S(2)}) copy-start(bf16[384,768]{1,0:T(8,128)(2,1)} %param.25) | copy-start | bytes 1769476
  26.4 9.3 %copy-start.12 = (bf16[768,128]{1,0:T(8,128)(2,1)}, bf16[768,128]{1,0:T(8,128)(2,1)S(1)}, u32[]{:S(2)}) copy-start(bf16[768,128]{1,0:T(8,128)(2,1)S(1)} %dynamic-slice_select_fusion.refs_2_) | copy-start | bytes 589828
  27.0 5.7 %collective-permute-start.5 = (bf16[768,128]{1,0:T(8,128)(2,1)S(1)}, bf16[768,128]{1,0:T(8,128)(2,1)S(1)}, u32[]{:S(2)}, u32[]{:S(2)}) collective-permute-start(bf16[768,128]{1,0:T(8,128)(2,1)S(1)} %dynamic-slice_select_fusion.refs_2_), channel_id=1, source_target_pairs={{0,16},{16,0},{1,17},{17,1},{2,18},{18,2},{3,19},{19,3},{4,20},{20... | collective-permute-start | bytes 589832 | tf_op jit(solution)/shard_map/ppermute | solution.py:956
  32.7 13.0 %collective-permute-start.6 = (bf16[384,768]{1,0:T(8,128)(2,1)S(1)}, bf16[384,768]{1,0:T(8,128)(2,1)S(1)}, u32[]{:S(2)}, u32[]{:S(2)}) collective-permute-start(bf16[384,768]{1,0:T(8,128)(2,1)S(1)} %copy-done.23), channel_id=1, source_target_pairs={{0,16},{16,0},{1,17},{17,1},{2,18},{18,2},{3,19},{19,3},{4,20},{20... | collective-permute-start | bytes 1769480 | tf_op jit(solution)/shard_map/ppermute | solution.py:956
  35.6 5.9 %copy-start.26 = (bf16[128,1536]{1,0:T(8,128)(2,1)}, bf16[128,1536]{1,0:T(8,128)(2,1)S(1)}, u32[]{:S(2)}) copy-start(bf16[128,1536]{1,0:T(8,128)(2,1)S(1)} %collective-permute-done.3.dy_far) | copy-start | bytes 1179652
  46.0 29.6 %copy-start.1 = (bf16[384,1536]{1,0:T(8,128)(2,1)}, bf16[384,1536]{1,0:T(8,128)(2,1)S(1)}, u32[]{:S(2)}) copy-start(bf16[384,1536]{1,0:T(8,128)(2,1)S(1)} %maximum_select_fusion.3) | copy-start | bytes 3538948
  46.0 110.3 %collective-permute-start.7 = (bf16[3360,768]{1,0:T(8,128)(2,1)}, bf16[3360,768]{1,0:T(8,128)(2,1)}, u32[]{:S(2)}, u32[]{:S(2)}) collective-permute-start(bf16[3360,768]{1,0:T(8,128)(2,1)} %pad_maximum_fusion.refs_0_.refs_2_.refs_4_), channel_id=1, source_target_pairs={{0,16},{16,0},{1,17},{17,1},{2,18},{18,2},{3,19},{19,3},{4,20},{20... | collective-permute-start | bytes 15482888 | tf_op jit(solution)/shard_map/ppermute | solution.py:956
  218.3 42.9 %collective-permute-start.8 = (bf16[1120,768]{1,0:T(8,128)(2,1)}, bf16[1120,768]{1,0:T(8,128)(2,1)}, u32[]{:S(2)}, u32[]{:S(2)}) collective-permute-start(bf16[1120,768]{1,0:T(8,128)(2,1)} %get-tuple-element.88), channel_id=1, source_target_pairs={{0,16},{16,0},{1,17},{17,1},{2,18},{18,2},{3,19},{19,3},{4,20},{20... | collective-permute-start | bytes 5160968 | tf_op jit(solution)/shard_map/ppermute | solution.py:956
  251.7 48.7 %collective-permute-start.10 = (bf16[1120,768]{1,0:T(8,128)(2,1)}, bf16[1120,768]{1,0:T(8,128)(2,1)}, u32[]{:S(2)}, u32[]{:S(2)}) collective-permute-start(bf16[1120,768]{1,0:T(8,128)(2,1)} %get-tuple-element.99), channel_id=1, source_target_pairs={{0,16},{16,0},{1,17},{17,1},{2,18},{18,2},{3,19},{19,3},{4,20},{20... | collective-permute-start | bytes 5160968 | tf_op jit(solution)/shard_map/ppermute | solution.py:956
  261.2 6.8 %copy-start.2 = (bf16[384,1536]{1,0:T(8,128)(2,1)S(1)}, bf16[384,1536]{1,0:T(8,128)(2,1)}, u32[]{:S(2)}) copy-start(bf16[384,1536]{1,0:T(8,128)(2,1)} %copy-done.1) | copy-start | bytes 3538948
  263.7 39.8 %collective-permute-start.9 = (bf16[1120,768]{1,0:T(8,128)(2,1)S(1)}, bf16[1120,768]{1,0:T(8,128)(2,1)}, u32[]{:S(2)}, u32[]{:S(2)}) collective-permute-start(bf16[1120,768]{1,0:T(8,128)(2,1)S(1)} %add_convert_fusion.2), channel_id=1, source_target_pairs={{0,4},{4,0},{8,12},{12,8},{1,5},{5,1},{9,13},{13,9},{2,6},{6,2},{1... | collective-permute-start | bytes 5160968 | tf_op jit(solution)/shard_map/ppermute | solution.py:956
  265.3 63.5 %collective-permute-start.11 = (bf16[1120,768]{1,0:T(8,128)(2,1)}, bf16[1120,768]{1,0:T(8,128)(2,1)}, u32[]{:S(2)}, u32[]{:S(2)}) collective-permute-start(bf16[1120,768]{1,0:T(8,128)(2,1)} %get-tuple-element.102), channel_id=1, source_target_pairs={{0,16},{16,0},{1,17},{17,1},{2,18},{18,2},{3,19},{19,3},{4,20},{20... | collective-permute-start | bytes 5160968 | tf_op jit(solution)/shard_map/ppermute | solution.py:956
  321.1 7.7 %copy-start = (bf16[2240,768]{1,0:T(8,128)(2,1)S(1)}, bf16[2240,768]{1,0:T(8,128)(2,1)}, u32[]{:S(2)}) copy-start(bf16[2240,768]{1,0:T(8,128)(2,1)} %unit_grads_0_2.1) | copy-start | bytes 10321924
  324.9 5.9 %copy-start.7 = (f32[512,64]{1,0:T(8,128)S(1)}, f32[512,64]{1,0:T(8,128)}, u32[]{:S(2)}) copy-start(f32[512,64]{1,0:T(8,128)} %copy-done.6) | copy-start | bytes 393220
  324.9 5.9 %copy-start.8 = (f32[512,128]{1,0:T(8,128)S(1)}, f32[512,128]{1,0:T(8,128)}, u32[]{:S(2)}) copy-start(f32[512,128]{1,0:T(8,128)} %kv_scatter.1) | copy-start | bytes 786436
  324.9 60.8 %collective-permute-start.16 = (bf16[1120,768]{1,0:T(8,128)(2,1)}, bf16[1120,768]{1,0:T(8,128)(2,1)}, u32[]{:S(2)}, u32[]{:S(2)}) collective-permute-start(bf16[1120,768]{1,0:T(8,128)(2,1)} %add_convert_fusion.1), channel_id=1, source_target_pairs={{0,4},{4,0},{8,12},{12,8},{1,5},{5,1},{9,13},{13,9},{2,6},{6,2},{1... | collective-permute-start | bytes 5160968 | tf_op jit(solution)/shard_map/ppermute | solution.py:956
  332.0 8.5 %copy-start.4 = (bf16[512,128]{1,0:T(8,128)(2,1)}, bf16[512,128]{1,0:T(8,128)(2,1)S(1)}, u32[]{:S(2)}) copy-start(bf16[512,128]{1,0:T(8,128)(2,1)S(1)} %fusion.12.dkv_ref) | copy-start | bytes 393220
  333.4 45.1 %collective-permute-start.14 = (bf16[768,128]{1,0:T(8,128)(2,1)}, bf16[768,128]{1,0:T(8,128)(2,1)}, u32[]{:S(2)}, u32[]{:S(2)}) collective-permute-start(bf16[768,128]{1,0:T(8,128)(2,1)} %convolution_convert_fusion.4), channel_id=1, source_target_pairs={{0,16},{16,0},{1,17},{17,1},{2,18},{18,2},{3,19},{19,3},{4,20},{20... | collective-permute-start | bytes 589832 | tf_op jit(solution)/shard_map/ppermute | solution.py:956
  335.5 5.2 %copy-start.29 = (f32[1,1536]{1,0:T(1,128)S(1)}, f32[1,1536]{1,0:T(1,128)}, u32[]{:S(2)}) copy-start(f32[1,1536]{1,0:T(1,128)} %get-tuple-element.112) | copy-start | bytes 18436
  337.0 43.8 %collective-permute-start.13 = (bf16[768,384]{1,0:T(8,128)(2,1)}, bf16[768,384]{1,0:T(8,128)(2,1)}, u32[]{:S(2)}, u32[]{:S(2)}) collective-permute-start(bf16[768,384]{1,0:T(8,128)(2,1)} %convolution_convert_fusion.1), channel_id=1, source_target_pairs={{0,16},{16,0},{1,17},{17,1},{2,18},{18,2},{3,19},{19,3},{4,20},{20... | collective-permute-start | bytes 1769480 | tf_op jit(solution)/shard_map/ppermute | solution.py:956
  338.2 45.1 %collective-permute-start.12 = (bf16[384,768]{1,0:T(8,128)(2,1)}, bf16[384,768]{1,0:T(8,128)(2,1)}, u32[]{:S(2)}, u32[]{:S(2)}) collective-permute-start(bf16[384,768]{1,0:T(8,128)(2,1)} %convolution_convert_fusion.2), channel_id=1, source_target_pairs={{0,16},{16,0},{1,17},{17,1},{2,18},{18,2},{3,19},{19,3},{4,20},{20... | collective-permute-start | bytes 1769480 | tf_op jit(solution)/shard_map/ppermute | solution.py:956
  339.0 62.5 %collective-permute-start.15 = (bf16[1120,768]{1,0:T(8,128)(2,1)S(1)}, bf16[1120,768]{1,0:T(8,128)(2,1)}, u32[]{:S(2)}, u32[]{:S(2)}) collective-permute-start(bf16[1120,768]{1,0:T(8,128)(2,1)S(1)} %add_convert_fusion), channel_id=1, source_target_pairs={{0,4},{4,0},{8,12},{12,8},{1,5},{5,1},{9,13},{13,9},{2,6},{6,2},{1... | collective-permute-start | bytes 5160968 | tf_op jit(solution)/shard_map/ppermute | solution.py:956
  373.7 4.9 copy-start.5
  373.7 4.8 copy-start.16
  373.7 7.0 %copy-start.18 = (bf16[512,384]{1,0:T(8,128)(2,1)S(1)}, bf16[512,384]{1,0:T(8,128)(2,1)}, u32[]{:S(2)}) copy-start(bf16[512,384]{1,0:T(8,128)(2,1)} %get-tuple-element.108.dq_ref) | copy-start | bytes 1179652
  477.7 4.8 copy-start.14
  (17 other events, 42.7 us)

commit v9 on v8

--- a/solution.py
+++ b/solution.py
@@ -297,14 +297,14 @@
     width = normed.shape[-1]
     rows = normed.shape[0] * normed.shape[1]
     pieces = len(weights)
-    units, depth = weights[0].shape[0] // 3, weights[0].shape[1]
+    units, depth = weights[0][1].shape
     tile = 512
     steps = rows // tile
     half = steps // 2
     flat = lambda x: x.reshape(-1, width)
     read = pl.BlockSpec((tile, width), lambda i, m: (lax.rem(i + m[3] * half, steps), 0))
     once = pl.Buffered(1)
-    weight = lambda w, k: pl.BlockSpec((units, depth), lambda i, m: (k, 0), pipeline_mode=once)
+    weight = lambda k: pl.BlockSpec((units, depth), lambda i, m: (k, 0), pipeline_mode=once)
     placed = pl.BlockSpec((tile, units), lambda i, m: (i, 0))
     near = pl.BlockSpec((tile, width), lambda i, m: (jnp.clip(i - m[3] * half, 0, half - 1), 0))
     grads = [pl.BlockSpec((units, depth), lambda i, m: (0, 0), pipeline_mode=once)] * 3
@@ -316,13 +316,13 @@
         grid_spec=pltpu.PrefetchScalarGridSpec(
             num_scalar_prefetch=1,
             grid=(steps,),
-            in_specs=[read, read] + [weight(w, k) for k in range(3) for w in weights],
+            in_specs=[read, read] + [weight(k) for k in (0, 1, 0) for _ in weights],
             out_specs=[placed] * 3 + [near] * 2 + grads,
             scratch_shapes=[pltpu.VMEM((units, depth), f32)] * len(grads),
         ),
         out_shape=[jax.ShapeDtypeStruct(shape, bf16) for shape in shapes],
         compiler_params=pltpu.CompilerParams(vmem_limit_bytes=FFN_VMEM_LIMIT),
-    )(meta, flat(normed), flat(grad_out), *(list(weights) * 3))
+    )(meta, flat(normed), flat(grad_out), *[w[k] for k in (0, 0, 1) for w in weights])
 
 
 def unit_grads_kernel(count, meta_ref, near_ref, far_ref, *refs):
@@ -638,7 +638,6 @@
     dy_ref,
     dy_y,
     dy_z,
-    dy_far,
     mid_ref,
     factor_ref,
     out,
@@ -659,18 +658,16 @@
     next(summed)
     mine = [
         wires.here(block, dys.at[k])
-        for block, k in ((dy_ref, 0), (dy_y, 1), (dy_z, 2), (dy_far, blocks))
+        for block, k in ((dy_ref, 0), (dy_y, 1), (dy_z, 2))
     ]
+    dy_far = wires.copy(dy_ref, dys.at[blocks], to["far"])
     via_z = wires.copy(dy_y.at[low], dys.at[3, low], to["z"])
-    dy_last = gather_pair(wires, to, dy_far, dys, blocks)
-    next(dy_last)
     next(summed)
     via_y = wires.copy(dy_z.at[high], dys.at[3, high], to["y"])
     ends = [
         wires.copy(block, dys.at[4 + k], to["core"])
         for k, block in enumerate((dy_ref, dy_y, dy_z))
     ]
-    next(dy_last)
     middle = wide(x_ref[...]) + result_of(summed)
     mid_ref[...] = middle
     factor = lax.rsqrt(jnp.mean(middle * middle, axis=-1, keepdims=True) + EPSILON)
@@ -684,15 +681,19 @@
     via_z.wait_recv()
     via_y.wait_recv()
     ends.append(wires.copy(dys.at[3], dys.at[7], to["core"]))
+    next(xn_near)
+    dy_far.wait_recv()
+    dy_last = gather_pair(wires, to, dys.at[blocks], dys, blocks)
     next(dy_last)
-    next(xn_near)
+    next(dy_last)
     xn_far.wait_recv()
     xn_last = gather_pair(wires, to, out.at[blocks], out, blocks)
     next(xn_last)
     next(xn_last)
-    ends += result_of(dy_last) + result_of(xn_near)
+    ends += result_of(xn_near)
+    next(dy_last)
     next(xn_last)
-    ends += result_of(xn_last)
+    ends += result_of(dy_last) + result_of(xn_last)
     for one in ends:
         one.wait_recv()
     for one in mine:
@@ -721,7 +722,7 @@
             pltpu.VMEM((rows, width), bf16),
         ],
         48,
-        ([False] + [True] * 6, [True, True, False, False]),
+        ([False] + [True] * 5, [True, True, False, False]),
     )
 
 
@@ -1049,9 +1050,10 @@
         b_kv = lax.dynamic_index_in_dim(jnp.where(core == 0, bk, bv), group, 0)
 
         unit_slice = lambda w: lax.dynamic_slice_in_dim(w, parity * units, units, 0)
-        own_units = jnp.concatenate([unit_slice(w) for w in (w_gate.T, w_up.T, w_down)], axis=0)
-
-        dy_part = lax.dynamic_slice_in_dim(cotangent, t * part, part, 0)
+        own_gate_up = jnp.concatenate([unit_slice(w) for w in (w_gate.T, w_up.T)], axis=0)
+        own_down = unit_slice(w_down)
+
+        dy_part = after(lax.dynamic_slice_in_dim(cotangent, t * part, part, 0), small)
 
         seq_blocks = blocks[0].reshape(n_c, -1)
         own_blocks = seq_blocks.shape[1]
@@ -1067,14 +1069,22 @@
             dy_part,
             flip(dy_part, "tensor", 2),
             flip(dy_part, "context", 1),
-            flip(dy_part, "context", 2),
         ]
         bias = after(bias, dy_blocks)
         normed, factor_first, queries, kv_own = qkv(
             meta, inputs, gain_first, bias, cosine, sine, w_q, w_kv
         )
-        w_units = pieces_f(after(own_units, kv_own, w_out_all), 1)
+        if n_f == 2:
+            half_down = lax.dynamic_slice_in_dim(own_down, pair * (units // 2), units // 2, 0)
+            got_half = flip(after(half_down, w_q, w_kv, small), "fsdp", 1)
+        else:
+            w_units = [tuple(pieces_f(w, 1)[0] for w in (own_gate_up, own_down))]
         kv = kv_gather(after(kv_own, w_out_all))
+        if n_f == 2:
+            far_half = flip(after(got_half, kv), "context", 2)
+            got_gate_up = flip(after(own_gate_up, kv, got_half), "fsdp", 1)
+            got_down = by_bit(pair, got_half, far_half, 0)
+            w_units = [(own_gate_up, own_down), (got_gate_up, got_down)]
         attended, lse = attention(key_blocks, queries, kv)
         inputs_part = lax.dynamic_slice_in_dim(inputs, t * part, part, 0)
         middle, factor_second, normed2, dy_all = middle_norm(

time: 497 us -> 518 us (1.042)
  Pallas kernels: 345 us -> 374 us
  waiting for transfers between devices: 40.5 us -> 28.1 us
  other arithmetic: 35.7 us -> 41.6 us
    pallas_call x6, Pallas kernels: 225 us -> 253 us  [remote_call(): pl.pallas_call(kernel, name=name, out_shape=outs, in_specs=[spec(x) for x...]
    ppermute x17 -> x18, waiting for transfers between devices: 40.5 us -> 28.1 us  [flip(): return lax.ppermute(x, axis, [(i, i ^ bit) for i in range(size)])]
    select_n x2 -> x3, other arithmetic: 0.33 us -> 6.59 us  [by_bit(): jnp.where(bit == 0, jnp.concatenate([x, other], axis=axis), jnp.concatena...]
    ppermute x17 -> x18, starting transfers between devices: 23.2 us -> 19 us  [flip(): return lax.ppermute(x, axis, [(i, i ^ bit) for i in range(size)])]
    unnamed x73 -> x57, local copies, waits for them, and re-layouts: 10.9 us -> 9.29 us
  transfers between devices with their start and end apart: 17 -> 18, of which waited for: 6 -> 7; matrix products, arithmetic and copies ran while one was open for 12% -> 13% of each run, Pallas kernels for 44% -> 47%
where the time goes in v9:
time: 518 us; the launch traced here: 510 us
  Pallas kernels  374 us (72%)
  other arithmetic  41.6 us (8%)
  local copies, waits for them, and re-layouts  28.8 us (6%)
  waiting for transfers between devices  28.1 us (5%)
  starting transfers between devices  19 us (4%)
  matrix products  17.6 us (3%)
    pallas_call x6, Pallas kernels, remote_call(): pl.pallas_call(kernel, name=name, out_shape=outs, in_specs=[spec(x) for x...  253 us
    pallas_call x1, Pallas kernels, ffn(): pl.pallas_call(functools.partial(ffn_kernel, pieces), name='ffn', grid_sp...  62 us
    ppermute x18, waiting for transfers between devices, flip(): return lax.ppermute(x, axis, [(i, i ^ bit) for i in range(size)])  28.1 us
    pallas_call x2, Pallas kernels, unit_grads(): pl.pallas_call(functools.partial(unit_grads_kernel, count), name=f'unit_g...  22.9 us
    ppermute x18, starting transfers between devices, flip(): return lax.ppermute(x, axis, [(i, i ^ bit) for i in range(size)])  19 us
    pallas_call x1, Pallas kernels, attention_back(): pl.pallas_call(functools.partial(attention_back_kernel, kv.shape[1] // BL...  15 us
    dot_general x6, matrix products, dot_rows(): lax.dot_general(left, right, (((0,), (0,)), ((), ())), preferred_element_...  10.9 us
  transfers between devices with their start and end apart: 18, of which 7 were waited for; matrix products, arithmetic and copies ran while one was open for 13% of the time, Pallas kernels for 47%

profile of v9, /device:TPU:0, one launch (start us, length us, event | category | flops | bytes accessed | tf_op | source)
XLA Modules:
  0.0 510.1 jit_solution(8175953668426878028)
XLA Ops:
  4.3 3.0 collective-permute-start
  16.0 2.5 constant_dynamic-slice_fusion.6
  25.7 2.8 collective-permute-done.3.refs_1_
  34.0 5.8 %qkv.1 = (bf16[512,1536]{1,0:T(8,128)(2,1)}, f32[512,1]{1,0:T(8,128)}, bf16[512,384]{1,0:T(8,128)(2,1)}, bf16[512,128]{1,0:T(8,128)(2,1)}) custom-call(s32[4]{0:T(128)} %pad_add_fusion.1.meta_ref, bf16[512,1536]{1,0:T(8,128)(2,1)} %x_ref.1, f32[1,1536]{1,0:T(1,128)} %bitcast.90, f32[1,512]{1,0:T(1,128)} %pad_maximum_fusion.6.bias_ref, ...), custom_call_target="tpu_custom_call" | custom-call | tf_op jit(solution)/shard_map/qkv/pallas_call | solution.py:210
  39.8 5.3 %collective-permute-done.5 = bf16[384,768]{1,0:T(8,128)(2,1)} collective-permute-done((bf16[384,768]{1,0:T(8,128)(2,1)}, bf16[384,768]{1,0:T(8,128)(2,1)}, u32[]{:S(2)}, u32[]{:S(2)}) %collective-permute-start.5) | collective-permute-done | bytes 589856 | tf_op jit(solution)/shard_map/ppermute | solution.py:957
  45.1 2.9 maximum_select_fusion.4
  48.0 17.2 %kv_gather.1.k_ref.v_ref = bf16[2,2048,128]{2,1,0:T(8,128)(2,1)} custom-call(bf16[512,128]{1,0:T(8,128)(2,1)} %get-tuple-element.80.own_ref), custom_call_target="tpu_custom_call" | custom-call | tf_op jit(solution)/shard_map/kv_gather/pallas_call | solution.py:540
  68.3 2.8 constant_dynamic-slice_fusion.5.refs_4_
  71.7 10.2 %attention.1 = (bf16[512,384]{1,0:T(8,128)(2,1)}, f32[3,512,1]{2,1,0:T(8,128)}) custom-call(s32[8]{0:T(128)} %pad_add_fusion.kb_ref, bf16[512,384]{1,0:T(8,128)(2,1)} %get-tuple-element.77.q_ref, bf16[2,2048,128]{2,1,0:T(8,128)(2,1)} %kv_gather.1.k_ref.v_ref, bf16[2,2048,128]{2,1,0:T(8,128)(2,1)} %kv_gather.1.k_ref.v_ref), custom_call_target="tpu_custom_call" | custom-call | tf_op jit(solution)/shard_map/attention/pallas_call | solution.py:86
  81.8 3.5 convolution_convert_fusion
  85.4 86.5 %middle_norm.1 = (f32[128,1536]{1,0:T(8,128)}, f32[128,1]{1,0:T(8,128)}, bf16[16,128,1536]{2,1,0:T(8,128)(2,1)}, bf16[16,128,1536]{2,1,0:T(8,128)(2,1)}) custom-call(bf16[4,128,1536]{2,1,0:T(8,128)(2,1)} %bitcast.82, bf16[128,1536]{1,0:T(8,128)(2,1)} %constant_dynamic-slice_fusion.7.x_ref, f32[1,1536]{1,0:T(1,128)} %bitcast.88, ...), custom_call_target="tpu_custom_call" | custom-call | tf_op jit(solution)/shard_map/middle_norm/pallas_call | solution.py:540
  171.9 3.6 maximum_select_fusion.3.refs_5_
  175.5 62.0 %ffn.1 = (bf16[2048,1120]{1,0:T(8,128)(2,1)}, bf16[2048,1120]{1,0:T(8,128)(2,1)}, bf16[2048,1120]{1,0:T(8,128)(2,1)}, bf16[1024,1536]{1,0:T(8,128)(2,1)}, bf16[1...) custom-call(s32[4]{0:T(128)} %pad_add_fusion.1.meta_ref, ...), custom_call_target="tpu_custom_call" | custom-call | tf_op jit(solution)/shard_map/ffn/pallas_call | solution.py:313
  239.3 33.0 %middle_back.1 = (f32[128,1536]{1,0:T(8,128)}, f32[1,1536]{1,0:T(1,128)}, bf16[4,128,1536]{2,1,0:T(8,128)(2,1)}) custom-call(bf16[8,128,1536]{2,1,0:T(8,128)(2,1)} %bitcast.84, f32[128,1536]{1,0:T(8,128)} %get-tuple-element.88.mid_ref.refs_5_, f32[128,1]{1,0:T(8,128)} %get-tuple-element.89.factor_ref, f32[1,1536]{1,0:T(1,128)} %bitcast.89, ...), custom_call_target="tpu_custom_call" | custom-call | tf_op jit(solution)/shard_map/middle_back/pallas_call | solution.py:540
  272.9 8.7 %unit_grads_0_1.1 = bf16[1120,768]{1,0:T(8,128)(2,1)} custom-call(s32[4]{0:T(128)} %pad_add_fusion.1.meta_ref, bf16[2048,1536]{1,0:T(8,128)(2,1)} %bitcast.78, bf16[2048,1536]{1,0:T(8,128)(2,1)} %bitcast.79, bf16[2048,1120]{1,0:T(8,128)(2,1)} %get-tuple-element.93.refs_0_), custom_call_target="tpu_custom_call" | custom-call | tf_op jit(solution)/shard_map/unit_grads_0_1/pallas_call | solution.py:350
  281.6 2.5 add_convert_fusion.2
  287.7 3.1 convolution_convert_fusion.3.do_ref
  290.8 15.0 %attention_back.1 = (bf16[512,384]{1,0:T(8,128)(2,1)}, bf16[2,2048,128]{2,1,0:T(8,128)(2,1)}) custom-call(s32[8]{0:T(128)} %pad_add_fusion.kb_ref, bf16[512,384]{1,0:T(8,128)(2,1)} %get-tuple-element.77.q_ref, bf16[512,384]{1,0:T(8,128)(2,1)} %convolution_convert_fusion.3.do_ref, f32[3,512,1]{2,1,0:T(8,128)} %get-tuple-element.97.lse_ref, ...), custom_call_target="tpu_custom_call" | custom-call | tf_op jit(solution)/shard_map/attention_back/pallas_call | solution.py:152
  305.8 14.3 %unit_grads_0_2.1 = bf16[2240,768]{1,0:T(8,128)(2,1)} custom-call(s32[4]{0:T(128)} %pad_add_fusion.1.meta_ref, bf16[2048,1536]{1,0:T(8,128)(2,1)} %bitcast.75, bf16[2048,1536]{1,0:T(8,128)(2,1)} %bitcast.76, bf16[2048,1120]{1,0:T(8,128)(2,1)} %get-tuple-element.102.refs_0_, bf16[2048,1120]{1,0:T(8,128)(2,1)} %get-tuple-element.103.refs_1_), custom_call_target="tpu_custom_call" | custom-call | tf_op jit(solution)/shard_map/unit_grads_0_2/pallas_call | solution.py:350
  320.0 3.8 collective-permute-done.10
  323.9 17.8 %kv_scatter.1 = f32[512,128]{1,0:T(8,128)} custom-call(bf16[2,2048,128]{2,1,0:T(8,128)(2,1)} %get-tuple-element.106.part_ref), custom_call_target="tpu_custom_call" | custom-call | tf_op jit(solution)/shard_map/kv_scatter/pallas_call | solution.py:540
  341.7 3.7 add_convert_fusion.1
  345.4 6.1 %collective-permute-done.12 = bf16[1120,768]{1,0:T(8,128)(2,1)} collective-permute-done((bf16[1120,768]{1,0:T(8,128)(2,1)}, bf16[1120,768]{1,0:T(8,128)(2,1)}, u32[]{:S(2)}, u32[]{:S(2)}) %collective-permute-start.12) | collective-permute-done | bytes 1720352 | tf_op jit(solution)/shard_map/ppermute | solution.py:957
  363.4 4.7 qkv_back.1
  368.1 28.6 %input_back.1 = (f32[1,5120]{1,0:T(1,128)}, bf16[4,128,1536]{2,1,0:T(8,128)(2,1)}) custom-call(bf16[4,128,1536]{2,1,0:T(8,128)(2,1)} %bitcast.81, bf16[128,1536]{1,0:T(8,128)(2,1)} %constant_dynamic-slice_fusion.7.x_ref, f32[128,1]{1,0:T(8,128)} %constant_dynamic-slice_fusion.4.factor_ref, f32[1,1536]{1,0:T(1,128)} %bitcast.91, ...), custom_call_target="tpu_custom_call" | custom-call | tf_op jit(solution)/shard_map/input_back/pallas_call | solution.py:540
  396.8 4.8 fusion.1
  403.8 2.5 fusion.3.refs_1_
  406.3 2.4 fusion.2.refs_0_
  408.7 5.3 %fusion = f32[2240,768]{1,0:T(8,128)} fusion(bf16[1120,768]{1,0:T(8,128)(2,1)} %collective-permute-done.17, bf16[1120,768]{1,0:T(8,128)(2,1)} %add_convert_fusion.1, pred[]{:T(512)S(6)} %eq.23), kind=kLoop, calls=%fused_computation.3 | loop fusion | flops 17203200 | bytes 10321921 | tf_op jit(solution)/shard_map/convert_element_type | solution.py:1109
  414.0 8.0 %collective-permute-done.16 = bf16[1120,768]{1,0:T(8,128)(2,1)} collective-permute-done((bf16[1120,768]{1,0:T(8,128)(2,1)S(1)}, bf16[1120,768]{1,0:T(8,128)(2,1)}, u32[]{:S(2)}, u32[]{:S(2)}) %collective-permute-start.16) | collective-permute-done | bytes 1720352 | tf_op jit(solution)/shard_map/ppermute | solution.py:957
  422.0 69.8 %context_sum.1 = (f32[384,768]{1,0:T(8,128)}, f32[768,384]{1,0:T(8,128)}, f32[1,5120]{1,0:T(1,128)}, bf16[4,768,128]{2,1,0:T(8,128)(2,1)}, bf16[4,128,1536]{2,1,0:T(8,128)(2,1)}) custom-call(bf16[384,768]{1,0:T(8,128)(2,1)} %fusion.2.refs_0_, bf16[768,384]{1,0:T(8,128)(2,1)} %fusion.3.refs_1_, bf16[768,128]{1,0:T(8,128)(2,1)} %fusion.4.refs_2_, ...), custom_call_target="tpu_custom_call" | custom-call | tf_op jit(solution)/shard_map/context_sum/pallas_call | solution.py:540
  498.3 4.8 convert_bitcast_fusion
  (145 shorter events, 61.6 us)
Async XLA Ops:
  4.3 17.9 %collective-permute-start = (bf16[1,1984]{1,0:T(2,128)(2,1)S(1)}, bf16[1,1984]{1,0:T(2,128)(2,1)S(1)}, u32[]{:S(2)}, u32[]{:S(2)}) collective-permute-start(bf16[1,1984]{1,0:T(2,128)(2,1)S(1)} %concatenate.70), channel_id=1, source_target_pairs={{0,16},{16,0},{1,17},{17,1},{2,18},{18,2},{3,19},{19,3},{4,20},{20... | collective-permute-start | bytes 11912 | tf_op jit(solution)/shard_map/ppermute | solution.py:957
  7.3 11.2 %copy-start.18 = (bf16[768,2240]{0,1:T(8,128)(2,1)S(1)}, bf16[768,2240]{0,1:T(8,128)(2,1)}, u32[]{:S(2)}) copy-start(bf16[768,2240]{0,1:T(8,128)(2,1)} %param.28) | copy-start | bytes 10321924
  9.2 16.5 %collective-permute-start.4 = (bf16[768,128]{1,0:T(8,128)(2,1)}, bf16[768,128]{1,0:T(8,128)(2,1)}, u32[]{:S(2)}, u32[]{:S(2)}) collective-permute-start(bf16[768,128]{1,0:T(8,128)(2,1)} %dynamic-slice_select_fusion.refs_2_), channel_id=1, source_target_pairs={{0,16},{16,0},{1,17},{17,1},{2,18},{18,2},{3,19},{19,3},{4,20},{20... | collective-permute-start | bytes 589832 | tf_op jit(solution)/shard_map/ppermute | solution.py:957
  9.3 19.2 %collective-permute-start.3 = (bf16[768,384]{1,0:T(8,128)(2,1)}, bf16[768,384]{1,0:T(8,128)(2,1)}, u32[]{:S(2)}, u32[]{:S(2)}) collective-permute-start(bf16[768,384]{1,0:T(8,128)(2,1)} %refs_0_.3), channel_id=1, source_target_pairs={{0,16},{16,0},{1,17},{17,1},{2,18},{18,2},{3,19},{19,3},{4,20},{20... | collective-permute-start | bytes 1769480 | tf_op jit(solution)/shard_map/ppermute | solution.py:957
  20.4 44.9 %copy-start = (bf16[2240,768]{1,0:T(8,128)(2,1)}, bf16[2240,768]{1,0:T(8,128)(2,1)S(1)}, u32[]{:S(2)}) copy-start(bf16[2240,768]{1,0:T(8,128)(2,1)S(1)} %pad_maximum_fusion.refs_0_.refs_2_) | copy-start | bytes 10321924
  22.3 10.4 %collective-permute-start.2 = (bf16[128,1536]{1,0:T(8,128)(2,1)}, bf16[128,1536]{1,0:T(8,128)(2,1)}, u32[]{:S(2)}, u32[]{:S(2)}) collective-permute-start(bf16[128,1536]{1,0:T(8,128)(2,1)} %constant_dynamic-slice_fusion.8.dy_ref), channel_id=1, source_target_pairs={{0,4},{4,0},{8,12},{12,8},{1,5},{5,1},{9,13},{13,9},{2,6},{6,2},{1... | collective-permute-start | bytes 1179656 | tf_op jit(solution)/shard_map/ppermute | solution.py:957
  23.9 10.1 %collective-permute-start.1 = (bf16[128,1536]{1,0:T(8,128)(2,1)}, bf16[128,1536]{1,0:T(8,128)(2,1)}, u32[]{:S(2)}, u32[]{:S(2)}) collective-permute-start(bf16[128,1536]{1,0:T(8,128)(2,1)} %constant_dynamic-slice_fusion.8.dy_ref), channel_id=1, source_target_pairs={{0,2},{1,3},{2,0},{3,1},{4,6},{5,7},{6,4},{7,5},{8,10},{9,11},{10,... | collective-permute-start | bytes 1179656 | tf_op jit(solution)/shard_map/ppermute | solution.py:957
  28.5 16.6 %collective-permute-start.5 = (bf16[384,768]{1,0:T(8,128)(2,1)}, bf16[384,768]{1,0:T(8,128)(2,1)}, u32[]{:S(2)}, u32[]{:S(2)}) collective-permute-start(bf16[384,768]{1,0:T(8,128)(2,1)} %param.25), channel_id=1, source_target_pairs={{0,16},{16,0},{1,17},{17,1},{2,18},{18,2},{3,19},{19,3},{4,20},{20... | collective-permute-start | bytes 1769480 | tf_op jit(solution)/shard_map/ppermute | solution.py:957
  28.9 36.4 %collective-permute-start.6 = (bf16[560,768]{1,0:T(8,128)(2,1)}, bf16[560,768]{1,0:T(8,128)(2,1)}, u32[]{:S(2)}, u32[]{:S(2)}) collective-permute-start(bf16[560,768]{1,0:T(8,128)(2,1)} %constant_dynamic-slice_fusion.6), channel_id=1, source_target_pairs={{0,16},{16,0},{1,17},{17,1},{2,18},{18,2},{3,19},{19,3},{4,20},{20... | collective-permute-start | bytes 2580488 | tf_op jit(solution)/shard_map/ppermute | solution.py:957
  65.3 110.3 %collective-permute-start.7 = (bf16[2240,768]{1,0:T(8,128)(2,1)S(1)}, bf16[2240,768]{1,0:T(8,128)(2,1)}, u32[]{:S(2)}, u32[]{:S(2)}) collective-permute-start(bf16[2240,768]{1,0:T(8,128)(2,1)S(1)} %pad_maximum_fusion.refs_0_.refs_2_), channel_id=1, source_target_pairs={{0,16},{16,0},{1,17},{17,1},{2,18},{18,2},{3,19},{19,3},{4,20},{20... | collective-permute-start | bytes 10321928 | tf_op jit(solution)/shard_map/ppermute | solution.py:957
  65.9 106.0 %collective-permute-start.8 = (bf16[560,768]{1,0:T(8,128)(2,1)}, bf16[560,768]{1,0:T(8,128)(2,1)}, u32[]{:S(2)}, u32[]{:S(2)}) collective-permute-start(bf16[560,768]{1,0:T(8,128)(2,1)} %collective-permute-done.6), channel_id=1, source_target_pairs={{0,8},{4,12},{8,0},{12,4},{1,9},{5,13},{9,1},{13,5},{2,10},{6,14},... | collective-permute-start | bytes 2580488 | tf_op jit(solution)/shard_map/ppermute | solution.py:957
  237.5 44.1 %collective-permute-start.9 = (bf16[1120,768]{1,0:T(8,128)(2,1)}, bf16[1120,768]{1,0:T(8,128)(2,1)}, u32[]{:S(2)}, u32[]{:S(2)}) collective-permute-start(bf16[1120,768]{1,0:T(8,128)(2,1)} %get-tuple-element.94), channel_id=1, source_target_pairs={{0,16},{16,0},{1,17},{17,1},{2,18},{18,2},{3,19},{19,3},{4,20},{20... | collective-permute-start | bytes 5160968 | tf_op jit(solution)/shard_map/ppermute | solution.py:957
  272.3 47.8 %collective-permute-start.11 = (bf16[1120,768]{1,0:T(8,128)(2,1)}, bf16[1120,768]{1,0:T(8,128)(2,1)}, u32[]{:S(2)}, u32[]{:S(2)}) collective-permute-start(bf16[1120,768]{1,0:T(8,128)(2,1)} %get-tuple-element.105), channel_id=1, source_target_pairs={{0,16},{16,0},{1,17},{17,1},{2,18},{18,2},{3,19},{19,3},{4,20},{20... | collective-permute-start | bytes 5160968 | tf_op jit(solution)/shard_map/ppermute | solution.py:957
  281.6 6.1 %copy-start.2 = (bf16[384,1536]{1,0:T(8,128)(2,1)S(1)}, bf16[384,1536]{1,0:T(8,128)(2,1)}, u32[]{:S(2)}) copy-start(bf16[384,1536]{1,0:T(8,128)(2,1)} %maximum_select_fusion.4) | copy-start | bytes 3538948
  284.1 39.8 %collective-permute-start.10 = (bf16[1120,768]{1,0:T(8,128)(2,1)S(1)}, bf16[1120,768]{1,0:T(8,128)(2,1)}, u32[]{:S(2)}, u32[]{:S(2)}) collective-permute-start(bf16[1120,768]{1,0:T(8,128)(2,1)S(1)} %add_convert_fusion.2), channel_id=1, source_target_pairs={{0,4},{4,0},{8,12},{12,8},{1,5},{5,1},{9,13},{13,9},{2,6},{6,2},{1... | collective-permute-start | bytes 5160968 | tf_op jit(solution)/shard_map/ppermute | solution.py:957
  284.5 67.0 %collective-permute-start.12 = (bf16[1120,768]{1,0:T(8,128)(2,1)}, bf16[1120,768]{1,0:T(8,128)(2,1)}, u32[]{:S(2)}, u32[]{:S(2)}) collective-permute-start(bf16[1120,768]{1,0:T(8,128)(2,1)} %get-tuple-element.108), channel_id=1, source_target_pairs={{0,16},{16,0},{1,17},{17,1},{2,18},{18,2},{3,19},{19,3},{4,20},{20... | collective-permute-start | bytes 5160968 | tf_op jit(solution)/shard_map/ppermute | solution.py:957
  341.7 9.9 %copy-start.1 = (bf16[2240,768]{1,0:T(8,128)(2,1)S(1)}, bf16[2240,768]{1,0:T(8,128)(2,1)}, u32[]{:S(2)}) copy-start(bf16[2240,768]{1,0:T(8,128)(2,1)} %unit_grads_0_2.1) | copy-start | bytes 10321924
  345.4 8.1 %copy-start.6 = (f32[512,64]{1,0:T(8,128)S(1)}, f32[512,64]{1,0:T(8,128)}, u32[]{:S(2)}) copy-start(f32[512,64]{1,0:T(8,128)} %copy-done.5) | copy-start | bytes 393220
  345.4 8.1 %copy-start.7 = (f32[512,128]{1,0:T(8,128)S(1)}, f32[512,128]{1,0:T(8,128)}, u32[]{:S(2)}) copy-start(f32[512,128]{1,0:T(8,128)} %kv_scatter.1) | copy-start | bytes 786436
  345.4 63.3 %collective-permute-start.17 = (bf16[1120,768]{1,0:T(8,128)(2,1)}, bf16[1120,768]{1,0:T(8,128)(2,1)}, u32[]{:S(2)}, u32[]{:S(2)}) collective-permute-start(bf16[1120,768]{1,0:T(8,128)(2,1)} %add_convert_fusion.1), channel_id=1, source_target_pairs={{0,4},{4,0},{8,12},{12,8},{1,5},{5,1},{9,13},{13,9},{2,6},{6,2},{1... | collective-permute-start | bytes 5160968 | tf_op jit(solution)/shard_map/ppermute | solution.py:957
  354.7 7.9 %copy-start.3 = (bf16[512,128]{1,0:T(8,128)(2,1)}, bf16[512,128]{1,0:T(8,128)(2,1)S(1)}, u32[]{:S(2)}) copy-start(bf16[512,128]{1,0:T(8,128)(2,1)S(1)} %fusion.12.dkv_ref) | copy-start | bytes 393220
  354.7 4.4 copy-start.14
  356.1 45.5 %collective-permute-start.15 = (bf16[768,128]{1,0:T(8,128)(2,1)}, bf16[768,128]{1,0:T(8,128)(2,1)}, u32[]{:S(2)}, u32[]{:S(2)}) collective-permute-start(bf16[768,128]{1,0:T(8,128)(2,1)} %convolution_convert_fusion.4), channel_id=1, source_target_pairs={{0,16},{16,0},{1,17},{17,1},{2,18},{18,2},{3,19},{19,3},{4,20},{20... | collective-permute-start | bytes 589832 | tf_op jit(solution)/shard_map/ppermute | solution.py:957
  360.6 43.3 %collective-permute-start.14 = (bf16[768,384]{1,0:T(8,128)(2,1)}, bf16[768,384]{1,0:T(8,128)(2,1)}, u32[]{:S(2)}, u32[]{:S(2)}) collective-permute-start(bf16[768,384]{1,0:T(8,128)(2,1)} %convolution_convert_fusion.1), channel_id=1, source_target_pairs={{0,16},{16,0},{1,17},{17,1},{2,18},{18,2},{3,19},{19,3},{4,20},{20... | collective-permute-start | bytes 1769480 | tf_op jit(solution)/shard_map/ppermute | solution.py:957
  360.9 45.4 %collective-permute-start.13 = (bf16[384,768]{1,0:T(8,128)(2,1)}, bf16[384,768]{1,0:T(8,128)(2,1)}, u32[]{:S(2)}, u32[]{:S(2)}) collective-permute-start(bf16[384,768]{1,0:T(8,128)(2,1)} %convolution_convert_fusion.2), channel_id=1, source_target_pairs={{0,16},{16,0},{1,17},{17,1},{2,18},{18,2},{3,19},{19,3},{4,20},{20... | collective-permute-start | bytes 1769480 | tf_op jit(solution)/shard_map/ppermute | solution.py:957
  362.6 59.4 %collective-permute-start.16 = (bf16[1120,768]{1,0:T(8,128)(2,1)S(1)}, bf16[1120,768]{1,0:T(8,128)(2,1)}, u32[]{:S(2)}, u32[]{:S(2)}) collective-permute-start(bf16[1120,768]{1,0:T(8,128)(2,1)S(1)} %add_convert_fusion), channel_id=1, source_target_pairs={{0,4},{4,0},{8,12},{12,8},{1,5},{5,1},{9,13},{13,9},{2,6},{6,2},{1... | collective-permute-start | bytes 5160968 | tf_op jit(solution)/shard_map/ppermute | solution.py:957
  396.8 4.9 copy-start.4
  396.8 4.9 copy-start.13
  396.8 7.0 %copy-start.15 = (bf16[512,384]{1,0:T(8,128)(2,1)S(1)}, bf16[512,384]{1,0:T(8,128)(2,1)}, u32[]{:S(2)}) copy-start(bf16[512,384]{1,0:T(8,128)(2,1)} %get-tuple-element.114.dq_ref) | copy-start | bytes 1179652
  401.6 4.7 copy-start.20
  401.6 4.7 copy-start.23
  498.3 4.8 copy-start.11
  (10 other events, 28.6 us)

commit v10 on v7

--- a/solution.py
+++ b/solution.py
@@ -307,7 +307,7 @@
 def hidden_specs(meta, normed, weights):
     width = normed.shape[-1]
     rows = normed.shape[0] * normed.shape[1]
-    units, depth = weights[0].shape[0] // 3, weights[0].shape[1]
+    units, depth = weights[0].shape[0] // 2, weights[0].shape[1]
     tile = 512
     steps = rows // tile
     half = steps // 2
@@ -360,17 +360,18 @@
     )
 
 
-def hidden_back(meta, normed, grad_out, hidden, slope, gated, weights):
+def hidden_back(meta, normed, grad_out, hidden, slope, gated, weights, down_weights):
     specs, pieces = hidden_specs(meta, normed, weights), len(weights)
     return hidden_call(
         functools.partial(hidden_back_kernel, pieces),
         "hidden_back",
         meta,
         [specs["flat"](normed), specs["flat"](grad_out), hidden, slope, gated]
-        + list(weights) * 3,
+        + list(weights) * 2
+        + list(down_weights),
         [specs["row"]] * 2
         + [specs["near_unit"], specs["unit"], specs["unit"]]
-        + [specs["weight"](k) for k in range(3) for _ in weights],
+        + [specs["weight"](k) for k in (0, 1, 0) for _ in weights],
         ["unit", "unit", "near_row", "near_row"],
         2 * (pieces == 2),
         specs,
@@ -599,7 +600,7 @@
         + [
             pltpu.SemaphoreType.DMA((copies,)),
             pltpu.SemaphoreType.DMA((copies,)),
-            pltpu.SemaphoreType.DMA((6,)),
+            pltpu.SemaphoreType.DMA((8,)),
         ],
         compiler_params=pltpu.CompilerParams(
             collective_id=key, has_side_effects=True, vmem_limit_bytes=VMEM_LIMIT
@@ -684,19 +685,45 @@
 
 
 def middle_kernel(
-    part, x_ref, gain_ref, dy_ref, mid_ref, factor_ref, out, dys, own, core, sent, got, xn, *sems
+    part,
+    x_ref,
+    gain_ref,
+    dy_ref,
+    dy_y,
+    dy_z,
+    dy_far,
+    mid_ref,
+    factor_ref,
+    out,
+    dys,
+    own,
+    core,
+    sent,
+    got,
+    xn,
+    *sems,
 ):
     wires, to = Wires(*sems), partners()
     blocks = out.shape[0] // 2
+    size = xn.shape[0] // 2
+    low, high = pl.ds(0, size), pl.ds(size, size)
     meet([to[k] for k in ("core", "y", "z", "far")])
     summed = scatter_rank(wires, to, part, own, core, sent, got)
     next(summed)
-    dy_far = wires.copy(dy_ref, dys.at[blocks], to["far"])
-    mine = [wires.here(dy_ref, dys.at[0])]
-    dy_near = gather_pair(wires, to, dy_ref, dys, 0)
-    next(dy_near)
+    mine = [
+        wires.here(block, dys.at[k])
+        for block, k in ((dy_ref, 0), (dy_y, 1), (dy_z, 2), (dy_far, blocks))
+    ]
+    via_z = wires.copy(dy_y.at[low], dys.at[3, low], to["z"])
+    dy_last = gather_pair(wires, to, dy_far, dys, blocks)
+    next(dy_last)
     next(summed)
-    next(dy_near)
+    via_y = wires.copy(dy_z.at[high], dys.at[3, high], to["y"])
+    ends = [
+        wires.copy(block, dys.at[4 + k], to["core"])
+        for k, block in enumerate((dy_ref, dy_y, dy_z))
+    ]
+    next(dy_last)
     middle = wide(x_ref[...]) + result_of(summed)
     mid_ref[...] = middle
     factor = lax.rsqrt(jnp.mean(middle * middle, axis=-1, keepdims=True) + EPSILON)
@@ -707,20 +734,18 @@
     xn_near = gather_pair(wires, to, xn, out, 0)
     next(xn_near)
     next(xn_near)
-    next(dy_near)
+    via_z.wait_recv()
+    via_y.wait_recv()
+    ends.append(wires.copy(dys.at[3], dys.at[7], to["core"]))
+    next(dy_last)
     next(xn_near)
-    dy_far.wait_recv()
-    dy_last = gather_pair(wires, to, dys.at[blocks], dys, blocks)
-    next(dy_last)
-    next(dy_last)
     xn_far.wait_recv()
     xn_last = gather_pair(wires, to, out.at[blocks], out, blocks)
     next(xn_last)
     next(xn_last)
-    ends = result_of(dy_near) + result_of(xn_near)
-    next(dy_last)
+    ends += result_of(dy_last) + result_of(xn_near)
     next(xn_last)
-    ends += result_of(dy_last) + result_of(xn_last)
+    ends += result_of(xn_last)
     for one in ends:
         one.wait_recv()
     for one in mine:
@@ -728,13 +753,13 @@
     wires.finish()
 
 
-def middle_norm(part, inputs_part, gain, dy_part):
+def middle_norm(part, inputs_part, gain, dy_blocks):
     rows, width = inputs_part.shape
     return remote_call(
         middle_kernel,
         "middle_norm",
         2,
-        [part.reshape(4, rows, width), inputs_part, gain, dy_part],
+        [part.reshape(4, rows, width), inputs_part, gain, *dy_blocks],
         [
             jax.ShapeDtypeStruct((rows, width), f32),
             jax.ShapeDtypeStruct((rows, 1), f32),
@@ -749,7 +774,7 @@
             pltpu.VMEM((rows, width), bf16),
         ],
         48,
-        ([False, True, True, True], [True, True, False, False]),
+        ([False] + [True] * 6, [True, True, False, False]),
     )
 
 
@@ -1034,7 +1059,7 @@
             far = lax.dynamic_slice_in_dim(source, (1 - f) * half, half, 1)
             return (dot_rows(far, right) if side == 0 else dot_rows(left, far)).astype(bf16)
 
-        def grad_sum(left, right, side, far):
+        def grad_sum(left, right, side, far, late):
             if n_f > 2:
                 return lax.psum_scatter(
                     dot_rows(left, right).astype(bf16), "fsdp", scatter_dimension=side, tiled=True
@@ -1043,7 +1068,7 @@
             half = width // 2
             own = lax.dynamic_slice_in_dim(source, f * half, half, 1)
             own = dot_rows(own, right) if side == 0 else dot_rows(left, own)
-            return (own + flip(far, "fsdp", 1).astype(f32)).astype(bf16)
+            return (own + after(flip(far, "fsdp", 1), late).astype(f32)).astype(bf16)
 
         small = jnp.concatenate(
             [v.reshape(1, -1) for v in (attn_gain, ffn_gain, b_query, b_key, b_value)], axis=1
@@ -1059,7 +1084,7 @@
         w_q = pieces_f(w_query, 0)
         w_kv = pieces_f(w_kv_own, 0)
         small = gather_f(small, 0)
-        w_out_all = gather_f(after(w_out, small), 1)
+        w_out_all = gather_f(after(w_out, small, w_q, w_kv), 1)
         piece = attn_gain.shape[0]
         gain_first = small[:, :piece].reshape(1, width).astype(f32)
         gain_second = small[:, piece : 2 * piece].reshape(1, width).astype(f32)
@@ -1077,7 +1102,8 @@
         b_kv = lax.dynamic_index_in_dim(jnp.where(core == 0, bk, bv), group, 0)
 
         unit_slice = lambda w: lax.dynamic_slice_in_dim(w, parity * units, units, 0)
-        own_units = jnp.concatenate([unit_slice(w) for w in (w_gate.T, w_up.T, w_down)], axis=0)
+        own_gate_up = jnp.concatenate([unit_slice(w) for w in (w_gate.T, w_up.T)], axis=0)
+        own_down = unit_slice(w_down)
 
         dy_part = lax.dynamic_slice_in_dim(cotangent, t * part, part, 0)
 
@@ -1091,40 +1117,43 @@
         ).reshape(-1)
         cosine, sine = rope_tables(positions)
         bias = jnp.concatenate([bq.reshape(1, -1), b_kv], axis=1)
+        dy_blocks = [
+            dy_part,
+            flip(dy_part, "tensor", 2),
+            flip(dy_part, "context", 1),
+            flip(dy_part, "context", 2),
+        ]
+        bias = after(bias, dy_blocks)
         normed, factor_first, queries, kv_own = qkv(
             meta, inputs, gain_first, bias, cosine, sine, w_q, w_kv
         )
-        w_units = pieces_f(after(own_units, kv_own, w_out_all), 1)
+        far_gate_up = pieces_f(after(own_gate_up, kv_own, w_out_all), 1)[-1]
+        w_gate_up = [own_gate_up, far_gate_up] if n_f == 2 else [far_gate_up]
         kv = kv_gather(after(kv_own, w_out_all))
+        far_down = pieces_f(after(own_down, kv), 1)[-1]
+        w_downs = [own_down, far_down] if n_f == 2 else [far_down]
         attended, lse = attention(key_blocks, queries, kv)
         inputs_part = lax.dynamic_slice_in_dim(inputs, t * part, part, 0)
         middle, factor_second, normed2, dy_all = middle_norm(
-            dot(attended, w_out_all).astype(bf16), inputs_part, gain_second, dy_part
-        )
-
-        hidden, slope, gated, *down_far = hidden_units(meta, normed2, dy_all, w_units)
+            dot(attended, w_out_all).astype(bf16), inputs_part, gain_second, dy_blocks
+        )
+
+        hidden, slope, gated, *down_far = hidden_units(meta, normed2, dy_all, w_gate_up)
         grad_gate, grad_up, dx_part, out_part, *unit_far = hidden_back(
-            meta, normed2, dy_all, hidden, slope, gated, w_units
-        )
-
-        def unit_done(own, got):
-            low = (own.astype(f32) + got.astype(f32)).astype(bf16)
-            return low, flip(low, "context", 1)
-
+            meta, normed2, dy_all, hidden, slope, gated, w_gate_up, w_downs
+        )
+        unit_far = [*down_far, *unit_far]
         if n_f == 2:
-            down_got, gate_got, up_got = (flip(x, "fsdp", 1) for x in (*down_far, *unit_far))
-            down_own = unit_grads(meta, 0, 2, *after((dy_all, [hidden]), dx_part))
-            down_done = unit_done(down_own, after(down_got, down_own))
-            gate_up_own = unit_grads(
-                meta, 0, 2, *after((normed2, [grad_gate, grad_up]), down_done[0])
-            )
-            dx_part = after(dx_part, gate_up_own)
+            down_got, gate_got, up_got = (flip(x, "fsdp", 1) for x in unit_far)
         else:
             over_f = lambda x: lax.psum_scatter(x, "fsdp", scatter_dimension=1, tiled=True)
             down_own = over_f(unit_grads(meta, 0, 1, dy_all, [hidden]))
             gate_up_own = over_f(unit_grads(meta, 0, 1, normed2, [grad_gate, grad_up]))
-            gate_got = up_got = jnp.zeros_like(down_own)
-            down_done = unit_done(down_own, gate_got)
+            down_got = gate_got = up_got = jnp.zeros_like(down_own)
+
+        def unit_done(own, got):
+            low = (own.astype(f32) + got.astype(f32)).astype(bf16)
+            return low, flip(low, "context", 1)
 
         unit_whole = lambda low, other: by_bit(parity, low, other, 0).astype(f32)
 
@@ -1132,22 +1161,23 @@
             dx_part, middle, factor_second, gain_second, dy_part
         )
         grad_middle_low = grad_middle_low.reshape(rows, width)
-        gate_done = unit_done(gate_up_own[:units], after(gate_got, grad_middle_low))
-        grad_attended = dot_cols(
-            after(grad_middle_low, gate_done[0], down_done), w_out_all
-        ).astype(bf16)
+        if n_f == 2:
+            down_own = unit_grads(meta, 0, 2, *after((dy_all, [hidden]), grad_middle_low))
+        down_done = unit_done(down_own, after(down_got, grad_middle_low))
+        grad_attended = dot_cols(after(grad_middle_low, down_done[0]), w_out_all).astype(bf16)
 
         dq_low, dkv = attention_back(key_blocks, queries, grad_attended, lse, cosine, sine, kv)
-        dkv = kv_scatter(after(dkv, gate_done))
-        up_done = unit_done(gate_up_own[units:], after(up_got, dkv))
-        dkv = after(dkv, up_done[0])
+        if n_f == 2:
+            gate_up_own = unit_grads(meta, 0, 2, *after((normed2, [grad_gate, grad_up]), dkv))
+            dkv = after(dkv, gate_up_own)
+        attention_args = [(attended, grad_middle_low, 1), (normed, dq_low, 0)]
+        fars = [grad_far(*args) for args in attention_args]
+        dkv = kv_scatter(after(dkv, down_done, gate_got, fars))
+        gate_done = unit_done(gate_up_own[:units], after(gate_got, dkv))
+        dkv = after(dkv, gate_done[0])
         dkv_low = jnp.where(core == 0, rotate_back(dkv, cosine, sine), dkv).astype(bf16)
-        attention_args = (
-            (attended, after(grad_middle_low, dkv), 1),
-            (normed, after(dq_low, dkv), 0),
-            (normed, dkv_low, 0),
-        )
-        fars = [grad_far(*args) for args in attention_args]
+        attention_args.append((normed, dkv_low, 0))
+        fars.append(grad_far(*attention_args[-1]))
         dkv_low = after(dkv_low, fars)
         factor_part = lax.dynamic_slice_in_dim(factor_first, t * part, part, 0)
         own_biases = jnp.sum(
@@ -1159,8 +1189,10 @@
         small_grads = jnp.concatenate(
             [jnp.zeros((1, width), f32), ffn_gain_grad, slots.reshape(1, -1)], axis=1
         )
+        grad_qkv = qkv_back(meta, dq_low, dkv_low, w_q, w_kv)
+        up_done = unit_done(gate_up_own[units:], after(up_got, grad_qkv))
         small_grads, input_grad = input_back(
-            qkv_back(meta, dq_low, dkv_low, w_q, w_kv),
+            after(grad_qkv, up_done[0]),
             inputs_part,
             factor_part,
             gain_first,
@@ -1170,7 +1202,9 @@
         input_grad = input_grad.reshape(rows, width)
         if n_f > 2:
             small_grads = lax.psum(small_grads, "fsdp")
-        attention_parts = [grad_sum(*args, far) for args, far in zip(attention_args, fars)]
+        attention_parts = [
+            grad_sum(*args, far, small_grads) for args, far in zip(attention_args, fars)
+        ]
         wd_grad = unit_whole(*after(down_done, small_grads))
         wg_grad = unit_whole(*after(gate_done, small_grads))
         small_grads, up_done, wg_grad, wd_grad = lax.optimization_barrier(

time: 527 us -> 500 us (0.949); the launches traced: 517 us -> 496 us
  Pallas kernels: 387 us -> 358 us
    pallas_call x6, Pallas kernels: 256 us -> 227 us  [remote_call(): pl.pallas_call(kernel, name=name, out_shape=outs, in_specs=[spec(x) for x...]
    ppermute x14 -> x18, starting transfers between devices: 16.5 us -> 20.4 us  [flip(): return lax.ppermute(x, axis, [(i, i ^ bit) for i in range(size)])]
    ppermute x14 -> x18, waiting for transfers between devices: 28.2 us -> 31.5 us  [flip(): return lax.ppermute(x, axis, [(i, i ^ bit) for i in range(size)])]
    unnamed x61 -> x69, local copies, waits for them, and re-layouts: 12.3 us -> 11.7 us
  transfers between devices with their start and end apart: 14 -> 18, of which waited for: 4 -> 4; matrix products, arithmetic and copies ran while one was open for 10% -> 12% of each run, Pallas kernels for 56% -> 58%
where the time goes in v10:
time: 500 us; the launch traced here: 496 us
  Pallas kernels  358 us (72%)
  other arithmetic  38.9 us (8%)
  waiting for transfers between devices  31.5 us (6%)
  local copies, waits for them, and re-layouts  28.1 us (6%)
  starting transfers between devices  20.4 us (4%)
  matrix products  18.5 us (4%)
    pallas_call x6, Pallas kernels, remote_call(): pl.pallas_call(kernel, name=name, out_shape=outs, in_specs=[spec(x) for x...  227 us
    pallas_call x2, Pallas kernels, hidden_call(): pl.pallas_call(kernel, name=name, grid_spec=pltpu.PrefetchScalarGridSpec(...  71.8 us
    ppermute x18, waiting for transfers between devices, flip(): return lax.ppermute(x, axis, [(i, i ^ bit) for i in range(size)])  31.5 us
    pallas_call x2, Pallas kernels, unit_grads(): pl.pallas_call(functools.partial(unit_grads_kernel, count), name=f'unit_g...  22.9 us
    ppermute x18, starting transfers between devices, flip(): return lax.ppermute(x, axis, [(i, i ^ bit) for i in range(size)])  20.4 us
    pallas_call x1, Pallas kernels, attention_back(): pl.pallas_call(functools.partial(attention_back_kernel, kv.shape[1] // BL...  15 us
    dot_general x6, matrix products, dot_rows(): lax.dot_general(left, right, (((0,), (0,)), ((), ())), preferred_element_...  13.6 us
    unnamed x69, local copies, waits for them, and re-layouts  11.7 us
  transfers between devices with their start and end apart: 18, of which 4 were waited for; matrix products, arithmetic and copies ran while one was open for 12% of the time, Pallas kernels for 58%

profile of v10, /device:TPU:0, one launch (start us, length us, event | category | flops | bytes accessed | tf_op | source)
XLA Modules:
  0.0 496.5 jit_solution(15019551138900311482)
XLA Ops:
  2.6 4.0 collective-permute-start.3
  20.3 2.2 dynamic-slice_bitcast_fusion
  27.7 5.8 %collective-permute-done.5.refs_3_ = bf16[768,128]{1,0:T(8,128)(2,1)} collective-permute-done((bf16[768,128]{1,0:T(8,128)(2,1)}, bf16[768,128]{1,0:T(8,128)(2,1)}, u32[]{:S(2)}, u32[]{:S(2)}) %collective-permute-start.5) | collective-permute-done | bytes 196640 | tf_op jit(solution)/shard_map/ppermute | solution.py:1009
  35.4 6.5 %qkv.1 = (bf16[512,1536]{1,0:T(8,128)(2,1)}, f32[512,1]{1,0:T(8,128)}, bf16[512,384]{1,0:T(8,128)(2,1)}, bf16[512,128]{1,0:T(8,128)(2,1)}) custom-call(s32[4]{0:T(128)} %pad_add_fusion.1.meta_ref, bf16[512,1536]{1,0:T(8,128)(2,1)} %x_ref.1, f32[1,1536]{1,0:T(1,128)} %bitcast.90, f32[1,512]{1,0:T(1,128)} %pad_maximum_fusion.6.bias_ref, ...), custom_call_target="tpu_custom_call" | custom-call | tf_op jit(solution)/shard_map/qkv/pallas_call | solution.py:209
  41.9 5.2 %collective-permute-done.6 = bf16[384,768]{1,0:T(8,128)(2,1)} collective-permute-done((bf16[384,768]{1,0:T(8,128)(2,1)}, bf16[384,768]{1,0:T(8,128)(2,1)}, u32[]{:S(2)}, u32[]{:S(2)}) %collective-permute-start.6) | collective-permute-done | bytes 589856 | tf_op jit(solution)/shard_map/ppermute | solution.py:1009
  47.2 2.5 maximum_select_fusion.3
  55.0 15.0 %kv_gather.1.k_ref.v_ref = bf16[2,2048,128]{2,1,0:T(8,128)(2,1)} custom-call(bf16[512,128]{1,0:T(8,128)(2,1)} %get-tuple-element.81.own_ref), custom_call_target="tpu_custom_call" | custom-call | tf_op jit(solution)/shard_map/kv_gather/pallas_call | solution.py:593
  71.0 10.2 %attention.1 = (bf16[512,384]{1,0:T(8,128)(2,1)}, f32[3,512,1]{2,1,0:T(8,128)}) custom-call(s32[8]{0:T(128)} %pad_add_fusion.kb_ref, bf16[512,384]{1,0:T(8,128)(2,1)} %get-tuple-element.78.q_ref, bf16[2,2048,128]{2,1,0:T(8,128)(2,1)} %kv_gather.1.k_ref.v_ref, bf16[2,2048,128]{2,1,0:T(8,128)(2,1)} %kv_gather.1.k_ref.v_ref), custom_call_target="tpu_custom_call" | custom-call | tf_op jit(solution)/shard_map/attention/pallas_call | solution.py:85
  81.1 3.1 convolution_convert_fusion
  84.2 62.5 %middle_norm.1 = (f32[128,1536]{1,0:T(8,128)}, f32[128,1]{1,0:T(8,128)}, bf16[16,128,1536]{2,1,0:T(8,128)(2,1)}, bf16[16,128,1536]{2,1,0:T(8,128)(2,1)}) custom-call(bf16[4,128,1536]{2,1,0:T(8,128)(2,1)} %bitcast.84, bf16[128,1536]{1,0:T(8,128)(2,1)} %constant_dynamic-slice_fusion.6.x_ref, f32[1,1536]{1,0:T(1,128)} %bitcast.92, ...), custom_call_target="tpu_custom_call" | custom-call | tf_op jit(solution)/shard_map/middle_norm/pallas_call | solution.py:593
  146.8 29.8 %hidden_units.1 = (bf16[2048,1120]{1,0:T(8,128)(2,1)}, bf16[2048,1120]{1,0:T(8,128)(2,1)}, bf16[2048,1120]{1,0:T(8,128)(2,1)}, bf16[1120,768]{1,0:T(8,128)(2,1)}) custom-call(s32[4]{0:T(128)} %pad_add_fusion.1.meta_ref, bf16[2048,1536]{1,0:T(8,128)(2,1)} %bitcast.74, bf16[2048,1536]{1,0:T(8,128)(2,1)} %bitcast.78, ...), custom_call_target="tpu_custom_call" | custom-call | tf_op jit(solution)/shard_map/hidden_units/pallas_call | solution.py:333
  179.0 42.0 %hidden_back.1 = (bf16[2048,1120]{1,0:T(8,128)(2,1)}, bf16[2048,1120]{1,0:T(8,128)(2,1)}, bf16[1024,1536]{1,0:T(8,128)(2,1)}, bf16[1024,1536]{1,0:T(8,128)(2,1)}...) custom-call(s32[4]{0:T(128)} %pad_add_fusion.1.meta_ref, bf16[2048,1536]{1,0:T(8,128)(2,1)} %bitcast.75, ...), custom_call_target="tpu_custom_call" | custom-call | tf_op jit(solution)/shard_map/hidden_back/pallas_call | solution.py:333
  221.0 33.0 %middle_back.1 = (f32[128,1536]{1,0:T(8,128)}, f32[1,1536]{1,0:T(1,128)}, bf16[4,128,1536]{2,1,0:T(8,128)(2,1)}) custom-call(bf16[8,128,1536]{2,1,0:T(8,128)(2,1)} %bitcast.86, f32[128,1536]{1,0:T(8,128)} %get-tuple-element.91.mid_ref.refs_5_, f32[128,1]{1,0:T(8,128)} %get-tuple-element.92.factor_ref, f32[1,1536]{1,0:T(1,128)} %bitcast.93, ...), custom_call_target="tpu_custom_call" | custom-call | tf_op jit(solution)/shard_map/middle_back/pallas_call | solution.py:593
  254.8 8.8 %unit_grads_0_1.1 = bf16[1120,768]{1,0:T(8,128)(2,1)} custom-call(s32[4]{0:T(128)} %pad_add_fusion.1.meta_ref, bf16[2048,1536]{1,0:T(8,128)(2,1)} %bitcast.80, bf16[2048,1536]{1,0:T(8,128)(2,1)} %bitcast.81, bf16[2048,1120]{1,0:T(8,128)(2,1)} %get-tuple-element.95.hid_ref.refs_0_), custom_call_target="tpu_custom_call" | custom-call | tf_op jit(solution)/shard_map/unit_grads_0_1/pallas_call | solution.py:403
  263.7 2.4 add_convert_fusion.2
  268.3 2.4 convolution_convert_fusion.2
  274.5 15.0 %attention_back.1 = (bf16[512,384]{1,0:T(8,128)(2,1)}, bf16[2,2048,128]{2,1,0:T(8,128)(2,1)}) custom-call(s32[8]{0:T(128)} %pad_add_fusion.kb_ref, bf16[512,384]{1,0:T(8,128)(2,1)} %get-tuple-element.78.q_ref, bf16[512,384]{1,0:T(8,128)(2,1)} %convolution_convert_fusion.3.do_ref, f32[3,512,1]{2,1,0:T(8,128)} %get-tuple-element.99.lse_ref, ...), custom_call_target="tpu_custom_call" | custom-call | tf_op jit(solution)/shard_map/attention_back/pallas_call | solution.py:151
  289.5 2.6 convolution_convert_fusion.1
  292.1 14.0 %unit_grads_0_2.1 = bf16[2240,768]{1,0:T(8,128)(2,1)} custom-call(s32[4]{0:T(128)} %pad_add_fusion.1.meta_ref, bf16[2048,1536]{1,0:T(8,128)(2,1)} %bitcast.76, bf16[2048,1536]{1,0:T(8,128)(2,1)} %bitcast.77, bf16[2048,1120]{1,0:T(8,128)(2,1)} %get-tuple-element.105.refs_0_, bf16[2048,1120]{1,0:T(8,128)(2,1)} %get-tuple-element.106.refs_1_), custom_call_target="tpu_custom_call" | custom-call | tf_op jit(solution)/shard_map/unit_grads_0_2/pallas_call | solution.py:403
  307.5 17.6 %kv_scatter.1 = f32[512,128]{1,0:T(8,128)} custom-call(bf16[2,2048,128]{2,1,0:T(8,128)(2,1)} %get-tuple-element.110.part_ref), custom_call_target="tpu_custom_call" | custom-call | tf_op jit(solution)/shard_map/kv_scatter/pallas_call | solution.py:593
  325.2 3.6 add_convert_fusion.1
  332.4 5.1 %qkv_back.1 = bf16[512,1536]{1,0:T(8,128)(2,1)} custom-call(s32[4]{0:T(128)} %pad_add_fusion.1.meta_ref, bf16[512,384]{1,0:T(8,128)(2,1)} %get-tuple-element.100.dq_ref, bf16[512,128]{1,0:T(8,128)(2,1)} %copy-done.6, bf16[768,384]{1,0:T(8,128)(2,1)} %refs_0_.3, bf16[768,384]{1,0:T(8,128)(2,1)} %collective-permute-done.4.refs_1_, ...), custom_call_target="tpu_custom_call" | custom-call | tf_op jit(solution)/shard_map/qkv_back/pallas_call | solution.py:242
  337.4 6.8 %collective-permute-done.13 = bf16[1120,768]{1,0:T(8,128)(2,1)} collective-permute-done((bf16[1120,768]{1,0:T(8,128)(2,1)}, bf16[1120,768]{1,0:T(8,128)(2,1)}, u32[]{:S(2)}, u32[]{:S(2)}) %collective-permute-start.13) | collective-permute-done | bytes 1720352 | tf_op jit(solution)/shard_map/ppermute | solution.py:1009
  344.3 3.1 add_convert_fusion
  348.5 28.7 %input_back.1 = (f32[1,5120]{1,0:T(1,128)}, bf16[4,128,1536]{2,1,0:T(8,128)(2,1)}) custom-call(bf16[4,128,1536]{2,1,0:T(8,128)(2,1)} %bitcast.83, bf16[128,1536]{1,0:T(8,128)(2,1)} %constant_dynamic-slice_fusion.6.x_ref, f32[128,1]{1,0:T(8,128)} %constant_dynamic-slice_fusion.4.factor_ref, f32[1,1536]{1,0:T(1,128)} %bitcast.91, ...), custom_call_target="tpu_custom_call" | custom-call | tf_op jit(solution)/shard_map/input_back/pallas_call | solution.py:593
  377.2 2.9 fusion.3.refs_1_
  380.1 4.8 fusion.1
  384.9 2.5 fusion.2.refs_0_
  389.5 5.3 %fusion = f32[2240,768]{1,0:T(8,128)} fusion(bf16[1120,768]{1,0:T(8,128)(2,1)} %collective-permute-done.17, bf16[1120,768]{1,0:T(8,128)(2,1)} %add_convert_fusion.1, pred[]{:T(512)S(6)} %eq.19), kind=kLoop, calls=%fused_computation.3 | loop fusion | flops 17203200 | bytes 10321921 | tf_op jit(solution)/shard_map/convert_element_type | solution.py:1158
  394.7 13.6 %collective-permute-done.16 = bf16[1120,768]{1,0:T(8,128)(2,1)S(1)} collective-permute-done((bf16[1120,768]{1,0:T(8,128)(2,1)}, bf16[1120,768]{1,0:T(8,128)(2,1)S(1)}, u32[]{:S(2)}, u32[]{:S(2)}) %collective-permute-start.16) | collective-permute-done | bytes 1720352 | tf_op jit(solution)/shard_map/ppermute | solution.py:1009
  408.3 69.7 %context_sum.1 = (f32[384,768]{1,0:T(8,128)}, f32[768,384]{1,0:T(8,128)}, f32[1,5120]{1,0:T(1,128)}, bf16[4,768,128]{2,1,0:T(8,128)(2,1)}, bf16[4,128,1536]{2,1,0:T(8,128)(2,1)}) custom-call(bf16[384,768]{1,0:T(8,128)(2,1)} %fusion.2.refs_0_, bf16[768,384]{1,0:T(8,128)(2,1)} %fusion.3.refs_1_, bf16[768,128]{1,0:T(8,128)(2,1)} %fusion.4.refs_2_, ...), custom_call_target="tpu_custom_call" | custom-call | tf_op jit(solution)/shard_map/context_sum/pallas_call | solution.py:593
  484.6 4.8 convert_bitcast_fusion
  (156 shorter events, 59.5 us)
Async XLA Ops:
  0.6 52.5 %copy-start = (bf16[2240,768]{1,0:T(8,128)(2,1)S(1)}, bf16[2240,768]{1,0:T(8,128)(2,1)}, u32[]{:S(2)}) copy-start(bf16[2240,768]{1,0:T(8,128)(2,1)} %param.29) | copy-start | bytes 10321924
  2.6 32.8 %collective-permute-start.3 = (bf16[128,1536]{1,0:T(8,128)(2,1)}, bf16[128,1536]{1,0:T(8,128)(2,1)}, u32[]{:S(2)}, u32[]{:S(2)}) collective-permute-start(bf16[128,1536]{1,0:T(8,128)(2,1)} %constant_dynamic-slice_fusion.7.dy_ref), channel_id=1, source_target_pairs={{0,8},{4,12},{8,0},{12,4},{1,9},{5,13},{9,1},{13,5},{2,10},{6,14},... | collective-permute-start | bytes 1179656 | tf_op jit(solution)/shard_map/ppermute | solution.py:1009
  6.6 28.8 %collective-permute-start.2 = (bf16[128,1536]{1,0:T(8,128)(2,1)}, bf16[128,1536]{1,0:T(8,128)(2,1)}, u32[]{:S(2)}, u32[]{:S(2)}) collective-permute-start(bf16[128,1536]{1,0:T(8,128)(2,1)} %constant_dynamic-slice_fusion.7.dy_ref), channel_id=1, source_target_pairs={{0,4},{4,0},{8,12},{12,8},{1,5},{5,1},{9,13},{13,9},{2,6},{6,2},{1... | collective-permute-start | bytes 1179656 | tf_op jit(solution)/shard_map/ppermute | solution.py:1009
  8.2 27.2 %collective-permute-start.1 = (bf16[128,1536]{1,0:T(8,128)(2,1)}, bf16[128,1536]{1,0:T(8,128)(2,1)}, u32[]{:S(2)}, u32[]{:S(2)}) collective-permute-start(bf16[128,1536]{1,0:T(8,128)(2,1)} %constant_dynamic-slice_fusion.7.dy_ref), channel_id=1, source_target_pairs={{0,2},{1,3},{2,0},{3,1},{4,6},{5,7},{6,4},{7,5},{8,10},{9,11},{10,... | collective-permute-start | bytes 1179656 | tf_op jit(solution)/shard_map/ppermute | solution.py:1009
  13.4 12.5 %collective-permute-start = (bf16[1,1984]{1,0:T(2,128)(2,1)S(1)}, bf16[1,1984]{1,0:T(2,128)(2,1)S(1)}, u32[]{:S(2)}, u32[]{:S(2)}) collective-permute-start(bf16[1,1984]{1,0:T(2,128)(2,1)S(1)} %concatenate.64), channel_id=1, source_target_pairs={{0,16},{16,0},{1,17},{17,1},{2,18},{18,2},{3,19},{19,3},{4,20},{20... | collective-permute-start | bytes 11912 | tf_op jit(solution)/shard_map/ppermute | solution.py:1009
  14.9 18.6 %collective-permute-start.4 = (bf16[768,384]{1,0:T(8,128)(2,1)}, bf16[768,384]{1,0:T(8,128)(2,1)}, u32[]{:S(2)}, u32[]{:S(2)}) collective-permute-start(bf16[768,384]{1,0:T(8,128)(2,1)} %refs_0_.3), channel_id=1, source_target_pairs={{0,16},{16,0},{1,17},{17,1},{2,18},{18,2},{3,19},{19,3},{4,20},{20... | collective-permute-start | bytes 1769480 | tf_op jit(solution)/shard_map/ppermute | solution.py:1009
  25.9 7.6 %collective-permute-start.5 = (bf16[768,128]{1,0:T(8,128)(2,1)}, bf16[768,128]{1,0:T(8,128)(2,1)}, u32[]{:S(2)}, u32[]{:S(2)}) collective-permute-start(bf16[768,128]{1,0:T(8,128)(2,1)} %dynamic-slice_select_fusion.refs_2_), channel_id=1, source_target_pairs={{0,16},{16,0},{1,17},{17,1},{2,18},{18,2},{3,19},{19,3},{4,20},{20... | collective-permute-start | bytes 589832 | tf_op jit(solution)/shard_map/ppermute | solution.py:1009
  33.5 13.7 %collective-permute-start.6 = (bf16[384,768]{1,0:T(8,128)(2,1)}, bf16[384,768]{1,0:T(8,128)(2,1)}, u32[]{:S(2)}, u32[]{:S(2)}) collective-permute-start(bf16[384,768]{1,0:T(8,128)(2,1)} %param.25), channel_id=1, source_target_pairs={{0,16},{16,0},{1,17},{17,1},{2,18},{18,2},{3,19},{19,3},{4,20},{20... | collective-permute-start | bytes 1769480 | tf_op jit(solution)/shard_map/ppermute | solution.py:1009
  35.4 11.7 %copy-start.22 = (bf16[384,768]{1,0:T(8,128)(2,1)S(1)}, bf16[384,768]{1,0:T(8,128)(2,1)}, u32[]{:S(2)}) copy-start(bf16[384,768]{1,0:T(8,128)(2,1)} %param.25) | copy-start | bytes 1769476
  49.7 97.1 %collective-permute-start.7 = (bf16[2240,768]{1,0:T(8,128)(2,1)}, bf16[2240,768]{1,0:T(8,128)(2,1)}, u32[]{:S(2)}, u32[]{:S(2)}) collective-permute-start(bf16[2240,768]{1,0:T(8,128)(2,1)} %pad_maximum_fusion.refs_0_.refs_2_), channel_id=1, source_target_pairs={{0,16},{16,0},{1,17},{17,1},{2,18},{18,2},{3,19},{19,3},{4,20},{20... | collective-permute-start | bytes 10321928 | tf_op jit(solution)/shard_map/ppermute | solution.py:1009
  55.0 26.1 %copy-start.5 = (bf16[384,1536]{1,0:T(8,128)(2,1)S(1)}, bf16[384,1536]{1,0:T(8,128)(2,1)}, u32[]{:S(2)}) copy-start(bf16[384,1536]{1,0:T(8,128)(2,1)} %maximum_select_fusion.3) | copy-start | bytes 3538948
  70.0 107.8 %collective-permute-start.8 = (bf16[1120,768]{1,0:T(8,128)(2,1)}, bf16[1120,768]{1,0:T(8,128)(2,1)S(1)}, u32[]{:S(2)}, u32[]{:S(2)}) collective-permute-start(bf16[1120,768]{1,0:T(8,128)(2,1)} %constant_dynamic-slice_fusion.5.refs_4_), channel_id=1, source_target_pairs={{0,16},{16,0},{1,17},{17,1},{2,18},{18,2},{3,19},{19,3},{4,20},{20... | collective-permute-start | bytes 5160968 | tf_op jit(solution)/shard_map/ppermute | solution.py:1009
  176.6 87.1 %collective-permute-start.10 = (bf16[1120,768]{1,0:T(8,128)(2,1)}, bf16[1120,768]{1,0:T(8,128)(2,1)}, u32[]{:S(2)}, u32[]{:S(2)}) collective-permute-start(bf16[1120,768]{1,0:T(8,128)(2,1)} %get-tuple-element.96), channel_id=1, source_target_pairs={{0,16},{16,0},{1,17},{17,1},{2,18},{18,2},{3,19},{19,3},{4,20},{20... | collective-permute-start | bytes 5160968 | tf_op jit(solution)/shard_map/ppermute | solution.py:1009
  254.0 53.5 %collective-permute-start.12 = (bf16[1120,768]{1,0:T(8,128)(2,1)}, bf16[1120,768]{1,0:T(8,128)(2,1)}, u32[]{:S(2)}, u32[]{:S(2)}) collective-permute-start(bf16[1120,768]{1,0:T(8,128)(2,1)} %get-tuple-element.108), channel_id=1, source_target_pairs={{0,16},{16,0},{1,17},{17,1},{2,18},{18,2},{3,19},{19,3},{4,20},{20... | collective-permute-start | bytes 5160968 | tf_op jit(solution)/shard_map/ppermute | solution.py:1009
  263.6 4.6 copy-start.23
  266.1 8.4 %copy-start.3 = (bf16[1120,768]{1,0:T(8,128)(2,1)}, bf16[1120,768]{1,0:T(8,128)(2,1)S(1)}, u32[]{:S(2)}) copy-start(bf16[1120,768]{1,0:T(8,128)(2,1)S(1)} %add_convert_fusion.2) | copy-start | bytes 5160964
  266.1 41.4 %collective-permute-start.11 = (bf16[1120,768]{1,0:T(8,128)(2,1)S(1)}, bf16[1120,768]{1,0:T(8,128)(2,1)}, u32[]{:S(2)}, u32[]{:S(2)}) collective-permute-start(bf16[1120,768]{1,0:T(8,128)(2,1)S(1)} %add_convert_fusion.2), channel_id=1, source_target_pairs={{0,4},{4,0},{8,12},{12,8},{1,5},{5,1},{9,13},{13,9},{2,6},{6,2},{1... | collective-permute-start | bytes 5160968 | tf_op jit(solution)/shard_map/ppermute | solution.py:1009
  266.7 6.1 %copy-start.28 = (bf16[4,128,1536]{2,1,0:T(8,128)(2,1)S(1)}, bf16[4,128,1536]{2,1,0:T(8,128)(2,1)}, u32[]{:S(2)}) copy-start(bf16[4,128,1536]{2,1,0:T(8,128)(2,1)} %get-tuple-element.93) | copy-start | bytes 4718596
  270.7 109.4 %collective-permute-start.9 = (bf16[384,768]{1,0:T(8,128)(2,1)}, bf16[384,768]{1,0:T(8,128)(2,1)}, u32[]{:S(2)}, u32[]{:S(2)}) collective-permute-start(bf16[384,768]{1,0:T(8,128)(2,1)} %convolution_convert_fusion.2), channel_id=1, source_target_pairs={{0,16},{16,0},{1,17},{17,1},{2,18},{18,2},{3,19},{19,3},{4,20},{20... | collective-permute-start | bytes 1769480 | tf_op jit(solution)/shard_map/ppermute | solution.py:1009
  272.0 72.2 %collective-permute-start.13 = (bf16[1120,768]{1,0:T(8,128)(2,1)}, bf16[1120,768]{1,0:T(8,128)(2,1)}, u32[]{:S(2)}, u32[]{:S(2)}) collective-permute-start(bf16[1120,768]{1,0:T(8,128)(2,1)} %get-tuple-element.114), channel_id=1, source_target_pairs={{0,16},{16,0},{1,17},{17,1},{2,18},{18,2},{3,19},{19,3},{4,20},{20... | collective-permute-start | bytes 5160968 | tf_op jit(solution)/shard_map/ppermute | solution.py:1009
  306.2 71.1 %collective-permute-start.14 = (bf16[768,384]{1,0:T(8,128)(2,1)}, bf16[768,384]{1,0:T(8,128)(2,1)}, u32[]{:S(2)}, u32[]{:S(2)}) collective-permute-start(bf16[768,384]{1,0:T(8,128)(2,1)} %convolution_convert_fusion.1), channel_id=1, source_target_pairs={{0,16},{16,0},{1,17},{17,1},{2,18},{18,2},{3,19},{19,3},{4,20},{20... | collective-permute-start | bytes 1769480 | tf_op jit(solution)/shard_map/ppermute | solution.py:1009
  325.1 3.7 copy-start.9
  325.2 3.7 copy-start.10
  331.4 56.0 %collective-permute-start.15 = (bf16[768,128]{1,0:T(8,128)(2,1)}, bf16[768,128]{1,0:T(8,128)(2,1)}, u32[]{:S(2)}, u32[]{:S(2)}) collective-permute-start(bf16[768,128]{1,0:T(8,128)(2,1)} %convolution_convert_fusion.4), channel_id=1, source_target_pairs={{0,16},{16,0},{1,17},{17,1},{2,18},{18,2},{3,19},{19,3},{4,20},{20... | collective-permute-start | bytes 589832 | tf_op jit(solution)/shard_map/ppermute | solution.py:1009
  332.1 57.3 %collective-permute-start.17 = (bf16[1120,768]{1,0:T(8,128)(2,1)}, bf16[1120,768]{1,0:T(8,128)(2,1)}, u32[]{:S(2)}, u32[]{:S(2)}) collective-permute-start(bf16[1120,768]{1,0:T(8,128)(2,1)} %add_convert_fusion.1), channel_id=1, source_target_pairs={{0,4},{4,0},{8,12},{12,8},{1,5},{5,1},{9,13},{13,9},{2,6},{6,2},{1... | collective-permute-start | bytes 5160968 | tf_op jit(solution)/shard_map/ppermute | solution.py:1009
  332.4 11.9 %copy-start.2 = (bf16[2240,768]{1,0:T(8,128)(2,1)S(1)}, bf16[2240,768]{1,0:T(8,128)(2,1)}, u32[]{:S(2)}) copy-start(bf16[2240,768]{1,0:T(8,128)(2,1)} %unit_grads_0_2.1) | copy-start | bytes 10321924
  337.4 10.4 %copy-start.27 = (f32[1,1536]{1,0:T(1,128)S(1)}, f32[1,1536]{1,0:T(1,128)}, u32[]{:S(2)}) copy-start(f32[1,1536]{1,0:T(1,128)} %get-tuple-element.119) | copy-start | bytes 18436
  347.4 29.8 %copy-start.19 = (bf16[512,384]{1,0:T(8,128)(2,1)S(1)}, bf16[512,384]{1,0:T(8,128)(2,1)}, u32[]{:S(2)}) copy-start(bf16[512,384]{1,0:T(8,128)(2,1)} %get-tuple-element.100.dq_ref) | copy-start | bytes 1179652
  347.4 60.9 %collective-permute-start.16 = (bf16[1120,768]{1,0:T(8,128)(2,1)}, bf16[1120,768]{1,0:T(8,128)(2,1)S(1)}, u32[]{:S(2)}, u32[]{:S(2)}) collective-permute-start(bf16[1120,768]{1,0:T(8,128)(2,1)} %add_convert_fusion), channel_id=1, source_target_pairs={{0,4},{4,0},{8,12},{12,8},{1,5},{5,1},{9,13},{13,9},{2,6},{6,2},{1... | collective-permute-start | bytes 5160968 | tf_op jit(solution)/shard_map/ppermute | solution.py:1009
  380.1 4.8 copy-start.24
  380.1 4.8 copy-start.29
  484.6 4.8 copy-start.15
  (16 other events, 30.9 us)

commit v11 on v8

--- a/solution.py
+++ b/solution.py
@@ -396,6 +396,55 @@
     def finish(self):
         for one in self.started:
             one.wait_send()
+
+
+class OwnGrad:
+    TILE = 256
+
+    def __init__(self, units, rows, out, units_here, rows_here):
+        self.units, self.rows, self.out = units, rows, out
+        self.units_here, self.rows_here = units_here, rows_here
+        self.tiles = out.shape[1] // self.TILE
+        self.copies = None
+
+    def fetch(self, wires):
+        half, depth = self.rows.shape[0] // 2, self.out.shape[1]
+        column = pl.multiple_of(lax.axis_index("fsdp") * depth, LANES)
+        pair = lax.axis_index("context") // 2
+        self.copies = [wires.here(self.units, self.units_here)]
+        for k, place in ((0, pair), (1, 1 - pair)):
+            self.copies.append(
+                wires.here(
+                    self.rows.at[pl.ds(k * half, half), pl.ds(column, depth)],
+                    self.rows_here.at[pl.ds(pl.multiple_of(place * half, half), half)],
+                )
+            )
+
+    def make(self, first, past):
+        for one in self.copies:
+            one.wait()
+        self.copies = []
+
+        @pl.loop(first, past)
+        def _(k):
+            at = pl.ds(pl.multiple_of(k * self.TILE, self.TILE), self.TILE)
+            self.out[:, at] = dot_rows(self.units_here[...], self.rows_here[:, at]).astype(bf16)
+
+
+def own_grad_call(fill, width):
+    args = [x for pair in fill for x in pair]
+    outs = [jax.ShapeDtypeStruct((units.shape[1], width), bf16) for units, _ in fill]
+    scratch = []
+    for units, rows in fill:
+        scratch += [pltpu.VMEM(units.shape, bf16), pltpu.VMEM((rows.shape[0], width), bf16)]
+    return args, outs, scratch
+
+
+def own_grads(count, args, outs, scratch):
+    return [
+        OwnGrad(args[2 * k], args[2 * k + 1], outs[k], scratch[2 * k], scratch[2 * k + 1])
+        for k in range(count)
+    ]
 
 
 def meet(devices):
@@ -588,8 +637,11 @@
     )[0]
 
 
-def kv_scatter_kernel(part_ref, dkv_ref, own, got_core, sent, got, *sems):
-    wires, to = Wires(*sems), partners()
+def kv_scatter_kernel(count, part_ref, *refs):
+    args, dkv_ref, outs = refs[: 2 * count], refs[2 * count], refs[2 * count + 1 : 3 * count + 1]
+    own, got_core, sent, got = refs[3 * count + 1 : 3 * count + 5]
+    wires, to = Wires(*refs[-3:]), partners()
+    fill = own_grads(count, args, outs, refs[3 * count + 5 : -3])
     kind = lax.rem(lax.axis_index("tensor"), 2)
     rows = dkv_ref.shape[0]
     block = lambda j: pl.ds(j * rows, rows)
@@ -600,12 +652,16 @@
         for j, _ in steps
     }
     mine = wires.here(part_ref.at[kind], own)
+    for one in fill:
+        one.fetch(wires)
     mine.wait()
     arrive = []
     for j, k in steps[:3]:
         from_core[j].wait_recv()
         sent[block(j)] = (wide(own[block(j)]) + wide(got_core[block(j)])).astype(bf16)
         arrive.append(wires.copy(sent.at[block(j)], got.at[block(j)], to[k]))
+    for one in fill:
+        one.make(0, one.tiles)
     from_core[0].wait_recv()
     total = wide(own[block(0)]) + wide(got_core[block(0)])
     for one in arrive:
@@ -616,19 +672,20 @@
     wires.finish()
 
 
-def kv_scatter(part):
-    _, rows, width = part.shape
+def kv_scatter(part, fill, width):
+    _, rows, depth = part.shape
     n_c = lax.axis_size("context")
+    args, outs, scratch = own_grad_call(fill, width)
     return remote_call(
-        kv_scatter_kernel,
+        functools.partial(kv_scatter_kernel, len(fill)),
         "kv_scatter",
         1,
-        [part],
-        [jax.ShapeDtypeStruct((rows // n_c, width), f32)],
-        [pltpu.VMEM((rows, width), bf16)] * 4,
+        [part, *args],
+        [jax.ShapeDtypeStruct((rows // n_c, depth), f32), *outs],
+        [pltpu.VMEM((rows, depth), bf16)] * 4 + scratch,
         7,
-        ([False], [True]),
-    )[0]
+        ([False] * (1 + len(args)), [True] * (1 + len(outs))),
+    )
 
 
 def middle_kernel(
@@ -732,12 +789,23 @@
     return grad_values, jnp.sum(grad_normed * values * factor, axis=0, keepdims=True)
 
 
-def middle_back_kernel(
-    part, mid_ref, factor_ref, gain_ref, dy_ref, dmid_ref, dgain_ref, out, low, *rest
-):
-    first, wires, to = rest[:7], Wires(*rest[7:]), partners()
+def middle_back_kernel(count, part, mid_ref, factor_ref, gain_ref, dy_ref, *refs):
+    args, (dmid_ref, dgain_ref, out) = refs[: 2 * count], refs[2 * count : 2 * count + 3]
+    outs, refs = refs[2 * count + 3 : 3 * count + 3], refs[3 * count + 3 :]
+    low, first, wires, to = refs[0], refs[1:8], Wires(*refs[-3:]), partners()
+    fill = own_grads(count, args, outs, refs[8:-3])
     meet([to[k] for k in ("core", "y", "z")])
-    grad_normed = result_of(scatter_pair(wires, to, part, *first))
+    back = scatter_pair(wires, to, part, *first)
+    next(back)
+    for one in fill:
+        one.fetch(wires)
+    next(back)
+    if fill:
+        fill[0].make(0, 1)
+    next(back)
+    if fill:
+        fill[0].make(1, fill[0].tiles)
+    grad_normed = result_of(back)
     du, dgain = norm_back_rows(mid_ref[...], factor_ref[...], gain_ref[...], grad_normed)
     dgain_ref[...] = dgain
     dmid = wide(dy_ref[...]) + du
@@ -745,6 +813,8 @@
     share = gather_rank(wires, to, low, out)
     next(share)
     dmid_ref[...] = dmid
+    for one in fill[1:]:
+        one.make(0, one.tiles)
     result_of(share)
     wires.finish()
 
@@ -761,21 +831,26 @@
     ]
 
 
-def middle_back(part, middle, factor, gain, dy_part):
+def middle_back(part, middle, factor, gain, dy_part, fill, shard):
     rows, width = middle.shape
+    args, outs, scratch = own_grad_call(fill, shard)
     return remote_call(
-        middle_back_kernel,
+        functools.partial(middle_back_kernel, len(fill)),
         "middle_back",
         3,
-        [part.reshape(8, rows, width), middle, factor, gain, dy_part],
+        [part.reshape(8, rows, width), middle, factor, gain, dy_part, *args],
         [
             jax.ShapeDtypeStruct((rows, width), f32),
             jax.ShapeDtypeStruct((1, width), f32),
             jax.ShapeDtypeStruct((4, rows, width), bf16),
+            *outs,
         ],
-        [pltpu.VMEM((rows, width), bf16)] + pair_scratch(rows, width),
+        [pltpu.VMEM((rows, width), bf16)] + pair_scratch(rows, width) + scratch,
         16,
-        ([False, True, True, True, True], [True, True, False]),
+        (
+            [False, True, True, True, True] + [False] * len(args),
+            [True, True, False] + [True] * len(outs),
+        ),
     )
 
 
@@ -1006,7 +1081,7 @@
             far = lax.dynamic_slice_in_dim(source, (1 - f) * half, half, 1)
             return (dot_rows(far, right) if side == 0 else dot_rows(left, far)).astype(bf16)
 
-        def grad_sum(left, right, side, far):
+        def grad_sum(left, right, side, far, late):
             if n_f > 2:
                 return lax.psum_scatter(
                     dot_rows(left, right).astype(bf16), "fsdp", scatter_dimension=side, tiled=True
@@ -1015,7 +1090,7 @@
             half = width // 2
             own = lax.dynamic_slice_in_dim(source, f * half, half, 1)
             own = dot_rows(own, right) if side == 0 else dot_rows(left, own)
-            return (own + flip(far, "fsdp", 1).astype(f32)).astype(bf16)
+            return (own + after(flip(far, "fsdp", 1), late).astype(f32)).astype(bf16)
 
         small = jnp.concatenate(
             [v.reshape(1, -1) for v in (attn_gain, ffn_gain, b_query, b_key, b_value)], axis=1
@@ -1084,13 +1159,19 @@
         hidden, grad_gate, grad_up, dx_part, out_part, *unit_far = ffn(
             meta, normed2, dy_all, w_units
         )
+        flat = lambda x: x.reshape(-1, width)
         if n_f == 2:
             down_got, gate_got, up_got = (flip(x, "fsdp", 1) for x in unit_far)
+            early = [(hidden, flat(dy_all)), (grad_gate, flat(normed2))]
+            later = [(grad_up, flat(normed2))]
         else:
             over_f = lambda x: lax.psum_scatter(x, "fsdp", scatter_dimension=1, tiled=True)
-            down_own = over_f(unit_grads(meta, 0, 1, dy_all, [hidden]))
-            gate_up_own = over_f(unit_grads(meta, 0, 1, normed2, [grad_gate, grad_up]))
-            down_got = gate_got = up_got = jnp.zeros_like(down_own)
+            owns = [
+                over_f(unit_grads(meta, 0, 1, x, [unit]))
+                for x, unit in ((dy_all, hidden), (normed2, grad_gate), (normed2, grad_up))
+            ]
+            down_got = gate_got = up_got = jnp.zeros_like(owns[0])
+            early = later = []
 
         def unit_done(own, got):
             low = (own.astype(f32) + got.astype(f32)).astype(bf16)
@@ -1098,30 +1179,26 @@
 
         unit_whole = lambda low, other: by_bit(parity, low, other, 0).astype(f32)
 
-        grad_middle, ffn_gain_grad, grad_middle_low = middle_back(
-            dx_part, middle, factor_second, gain_second, dy_part
+        grad_middle, ffn_gain_grad, grad_middle_low, *first_owns = middle_back(
+            dx_part, middle, factor_second, gain_second, dy_part, early, width // n_f
         )
         grad_middle_low = grad_middle_low.reshape(rows, width)
-        if n_f == 2:
-            down_own = unit_grads(meta, 0, 2, *after((dy_all, [hidden]), grad_middle_low))
+        down_own, gate_own = first_owns or owns[:2]
         down_done = unit_done(down_own, after(down_got, grad_middle_low))
         grad_attended = dot_cols(after(grad_middle_low, down_done[0]), w_out_all).astype(bf16)
 
         dq_low, dkv = attention_back(key_blocks, queries, grad_attended, lse, cosine, sine, kv)
-        if n_f == 2:
-            gate_up_own = unit_grads(meta, 0, 2, *after((normed2, [grad_gate, grad_up]), dkv))
-            dkv = after(dkv, gate_up_own)
-        dkv = kv_scatter(after(dkv, down_done, gate_got))
-        gate_done = unit_done(gate_up_own[:units], after(gate_got, dkv))
-        up_done = unit_done(gate_up_own[units:], after(up_got, gate_done[0]))
-        dkv = after(dkv, gate_done[0], up_done[0])
+        attention_args = [(attended, after(grad_middle_low, dq_low), 1), (normed, dq_low, 0)]
+        fars = [grad_far(*args) for args in attention_args]
+        dkv, *last_owns = kv_scatter(
+            after(dkv, gate_got, fars), later, width // n_f
+        )
+        (up_own,) = last_owns or owns[2:]
+        gate_done = unit_done(gate_own, after(gate_got, dkv, down_done))
+        dkv = after(dkv, gate_done[0])
         dkv_low = jnp.where(core == 0, rotate_back(dkv, cosine, sine), dkv).astype(bf16)
-        attention_args = (
-            (attended, after(grad_middle_low, dkv), 1),
-            (normed, after(dq_low, dkv), 0),
-            (normed, dkv_low, 0),
-        )
-        fars = [grad_far(*args) for args in attention_args]
+        attention_args.append((normed, dkv_low, 0))
+        fars.append(grad_far(*attention_args[-1]))
         dkv_low = after(dkv_low, fars)
         factor_part = lax.dynamic_slice_in_dim(factor_first, t * part, part, 0)
         own_biases = jnp.sum(
@@ -1133,8 +1210,10 @@
         small_grads = jnp.concatenate(
             [jnp.zeros((1, width), f32), ffn_gain_grad, slots.reshape(1, -1)], axis=1
         )
+        grad_qkv = qkv_back(meta, dq_low, dkv_low, w_q, w_kv)
+        up_done = unit_done(up_own, after(up_got, grad_qkv))
         small_grads, input_grad = input_back(
-            qkv_back(meta, dq_low, dkv_low, w_q, w_kv),
+            after(grad_qkv, up_done[0]),
             inputs_part,
             factor_part,
             gain_first,
@@ -1144,7 +1223,9 @@
         input_grad = input_grad.reshape(rows, width)
         if n_f > 2:
             small_grads = lax.psum(small_grads, "fsdp")
-        attention_parts = [grad_sum(*args, far) for args, far in zip(attention_args, fars)]
+        attention_parts = [
+            grad_sum(*args, far, small_grads) for args, far in zip(attention_args, fars)
+        ]
         wd_grad = unit_whole(*after(down_done, small_grads))
         wg_grad = unit_whole(*after(gate_done, small_grads))
         small_grads, up_done, wg_grad, wd_grad = lax.optimization_barrier(

time: 497 us -> 494 us (level)
  waiting for transfers between devices: 40.5 us -> 62.4 us
  Pallas kernels: 345 us -> 324 us
  starting transfers between devices: 23.2 us -> 17.7 us
    pallas_call x2 -> x0, Pallas kernels: 22.9 us -> none  [unit_grads(): pl.pallas_call(functools.partial(unit_grads_kernel, count), name=f'unit_g...]
    ppermute x17, waiting for transfers between devices: 40.5 us -> 62.4 us  [flip(): return lax.ppermute(x, axis, [(i, i ^ bit) for i in range(size)])]
    ppermute x17, starting transfers between devices: 23.2 us -> 17.7 us  [flip(): return lax.ppermute(x, axis, [(i, i ^ bit) for i in range(size)])]
    unnamed x73 -> x61, local copies, waits for them, and re-layouts: 10.9 us -> 10 us
  transfers between devices with their start and end apart: 17 -> 17, of which waited for: 6 -> 7; matrix products, arithmetic and copies ran while one was open for 12% -> 12% of each run, Pallas kernels for 44% -> 40%
where the time goes in v11:
time: 494 us; the launch traced here: 487 us
  Pallas kernels  324 us (66%)
  waiting for transfers between devices  62.4 us (13%)
  other arithmetic  36.1 us (7%)
  local copies, waits for them, and re-layouts  25.3 us (5%)
  matrix products  19.6 us (4%)
  starting transfers between devices  17.7 us (4%)
    pallas_call x6, Pallas kernels, remote_call(): pl.pallas_call(kernel, name=name, out_shape=outs, in_specs=[spec(x) for x...  226 us
    ppermute x17, waiting for transfers between devices, flip(): return lax.ppermute(x, axis, [(i, i ^ bit) for i in range(size)])  62.4 us
    pallas_call x1, Pallas kernels, ffn(): pl.pallas_call(functools.partial(ffn_kernel, pieces), name='ffn', grid_sp...  62 us
    ppermute x17, starting transfers between devices, flip(): return lax.ppermute(x, axis, [(i, i ^ bit) for i in range(size)])  17.7 us
    pallas_call x1, Pallas kernels, attention_back(): pl.pallas_call(functools.partial(attention_back_kernel, kv.shape[1] // BL...  15.1 us
    dot_general x6, matrix products, dot_rows(): lax.dot_general(left, right, (((0,), (0,)), ((), ())), preferred_element_...  13.4 us
    convert_element_type x2, other arithmetic, local(): unit_whole = lambda low, other: by_bit(parity, low, other, 0).astype(f32)  10.2 us
    pallas_call x1, Pallas kernels, attention(): pl.pallas_call(functools.partial(attention_kernel, kv.shape[1] // BLOCK),...  10.2 us
  transfers between devices with their start and end apart: 17, of which 7 were waited for; matrix products, arithmetic and copies ran while one was open for 12% of the time, Pallas kernels for 40%

profile of v11, /device:TPU:0, one launch (start us, length us, event | category | flops | bytes accessed | tf_op | source)
XLA Modules:
  0.0 486.7 jit_solution(5905952506441555809)
XLA Ops:
  1.7 4.1 collective-permute-start.3
  22.9 2.6 pad_maximum_fusion.refs_0_.refs_2_.refs_4_
  28.1 4.5 collective-permute-done.5.refs_3_
  34.9 5.8 %qkv.1 = (bf16[512,1536]{1,0:T(8,128)(2,1)}, f32[512,1]{1,0:T(8,128)}, bf16[512,384]{1,0:T(8,128)(2,1)}, bf16[512,128]{1,0:T(8,128)(2,1)}) custom-call(s32[4]{0:T(128)} %pad_add_fusion.1.meta_ref, bf16[512,1536]{1,0:T(8,128)(2,1)} %x_ref.1, f32[1,1536]{1,0:T(1,128)} %bitcast.85, f32[1,512]{1,0:T(1,128)} %pad_maximum_fusion.6.bias_ref, ...), custom_call_target="tpu_custom_call" | custom-call | tf_op jit(solution)/shard_map/qkv/pallas_call | solution.py:210
  40.8 5.7 %collective-permute-done.6 = bf16[384,768]{1,0:T(8,128)(2,1)S(1)} collective-permute-done((bf16[384,768]{1,0:T(8,128)(2,1)S(1)}, bf16[384,768]{1,0:T(8,128)(2,1)S(1)}, u32[]{:S(2)}, u32[]{:S(2)}) %collective-permute-start.6) | collective-permute-done | bytes 589856 | tf_op jit(solution)/shard_map/ppermute | solution.py:1031
  50.1 15.0 %kv_gather.1.k_ref.v_ref = bf16[2,2048,128]{2,1,0:T(8,128)(2,1)} custom-call(bf16[512,128]{1,0:T(8,128)(2,1)} %get-tuple-element.77.own_ref), custom_call_target="tpu_custom_call" | custom-call | tf_op jit(solution)/shard_map/kv_gather/pallas_call | solution.py:589
  65.1 10.2 %attention.1 = (bf16[512,384]{1,0:T(8,128)(2,1)}, f32[3,512,1]{2,1,0:T(8,128)}) custom-call(s32[8]{0:T(128)} %pad_add_fusion.kb_ref, bf16[512,384]{1,0:T(8,128)(2,1)} %get-tuple-element.74.q_ref, bf16[2,2048,128]{2,1,0:T(8,128)(2,1)} %kv_gather.1.k_ref.v_ref, bf16[2,2048,128]{2,1,0:T(8,128)(2,1)} %kv_gather.1.k_ref.v_ref), custom_call_target="tpu_custom_call" | custom-call | tf_op jit(solution)/shard_map/attention/pallas_call | solution.py:86
  75.2 3.1 convolution_convert_fusion
  78.3 62.5 %middle_norm.1 = (f32[128,1536]{1,0:T(8,128)}, f32[128,1]{1,0:T(8,128)}, bf16[16,128,1536]{2,1,0:T(8,128)(2,1)}, bf16[16,128,1536]{2,1,0:T(8,128)(2,1)}) custom-call(bf16[4,128,1536]{2,1,0:T(8,128)(2,1)} %bitcast.79, bf16[128,1536]{1,0:T(8,128)(2,1)} %constant_dynamic-slice_fusion.6.x_ref, f32[1,1536]{1,0:T(1,128)} %bitcast.87, bf16[128,1536]{1,0:T(8,128)(2,1)} %copy-done.2, ...), custom_call_target="tpu_custom_call" | custom-call | tf_op jit(solution)/shard_map/middle_norm/pallas_call | solution.py:589
  140.9 17.1 %collective-permute-done.7.refs_1_.refs_3_.refs_5_ = bf16[3360,768]{1,0:T(8,128)(2,1)} collective-permute-done((bf16[3360,768]{1,0:T(8,128)(2,1)}, bf16[3360,768]{1,0:T(8,128)(2,1)}, u32[]{:S(2)}, u32[]{:S(2)}) %collective-permute-start.7) | collective-permute-done | bytes 5160992 | tf_op jit(solution)/shard_map/ppermute | solution.py:1031
  158.0 62.0 %ffn.1 = (bf16[2048,1120]{1,0:T(8,128)(2,1)}, bf16[2048,1120]{1,0:T(8,128)(2,1)}, bf16[2048,1120]{1,0:T(8,128)(2,1)}, bf16[1024,1536]{1,0:T(8,128)(2,1)}, bf16[1...) custom-call(s32[4]{0:T(128)} %pad_add_fusion.1.meta_ref, ...), custom_call_target="tpu_custom_call" | custom-call | tf_op jit(solution)/shard_map/ffn/pallas_call | solution.py:313
  222.1 33.1 %middle_back.1 = (f32[128,1536]{1,0:T(8,128)}, f32[1,1536]{1,0:T(1,128)}, bf16[4,128,1536]{2,1,0:T(8,128)(2,1)}, bf16[1120,768]{1,0:T(8,128)(2,1)}, bf16[1120,768]{1,0:T(8,128)(2,1)}) custom-call(bf16[8,128,1536]{2,1,0:T(8,128)(2,1)} %bitcast.81, f32[128,1536]{1,0:T(8,128)} %get-tuple-element.83.mid_ref.refs_5_, f32[128,1]{1,0:T(8,128)} %get-tuple-element.84.factor_ref, ...), custom_call_target="tpu_custom_call" | custom-call | tf_op jit(solution)/shard_map/middle_back/pallas_call | solution.py:589
  255.2 5.6 %collective-permute-done.8 = bf16[1120,768]{1,0:T(8,128)(2,1)} collective-permute-done((bf16[1120,768]{1,0:T(8,128)(2,1)}, bf16[1120,768]{1,0:T(8,128)(2,1)}, u32[]{:S(2)}, u32[]{:S(2)}) %collective-permute-start.8) | collective-permute-done | bytes 1720352 | tf_op jit(solution)/shard_map/ppermute | solution.py:1031
  260.9 2.5 add_convert_fusion.2
  265.7 3.1 convolution_convert_fusion.3.do_ref
  268.8 15.1 %attention_back.1 = (bf16[512,384]{1,0:T(8,128)(2,1)}, bf16[2,2048,128]{2,1,0:T(8,128)(2,1)}) custom-call(s32[8]{0:T(128)} %pad_add_fusion.kb_ref, bf16[512,384]{1,0:T(8,128)(2,1)} %get-tuple-element.74.q_ref, bf16[512,384]{1,0:T(8,128)(2,1)} %convolution_convert_fusion.3.do_ref, f32[3,512,1]{2,1,0:T(8,128)} %get-tuple-element.92.lse_ref, ...), custom_call_target="tpu_custom_call" | custom-call | tf_op jit(solution)/shard_map/attention_back/pallas_call | solution.py:152
  283.9 2.6 convolution_convert_fusion.2
  286.5 2.4 convolution_convert_fusion.1
  290.9 6.8 %collective-permute-done.10 = bf16[1120,768]{1,0:T(8,128)(2,1)} collective-permute-done((bf16[1120,768]{1,0:T(8,128)(2,1)}, bf16[1120,768]{1,0:T(8,128)(2,1)}, u32[]{:S(2)}, u32[]{:S(2)}) %collective-permute-start.10) | collective-permute-done | bytes 1720352 | tf_op jit(solution)/shard_map/ppermute | solution.py:1031
  297.7 18.2 %kv_scatter.1 = (f32[512,128]{1,0:T(8,128)}, bf16[1120,768]{1,0:T(8,128)(2,1)}) custom-call(bf16[2,2048,128]{2,1,0:T(8,128)(2,1)} %get-tuple-element.98.part_ref, bf16[2048,1120]{1,0:T(8,128)(2,1)} %get-tuple-element.99.refs_0_, bf16[2048,1536]{1,0:T(8,128)(2,1)} %bitcast.74), custom_call_target="tpu_custom_call" | custom-call | tf_op jit(solution)/shard_map/kv_scatter/pallas_call | solution.py:589
  316.0 3.6 add_convert_fusion.1
  322.6 4.7 qkv_back.1
  327.3 7.3 %collective-permute-done.12 = bf16[1120,768]{1,0:T(8,128)(2,1)} collective-permute-done((bf16[1120,768]{1,0:T(8,128)(2,1)}, bf16[1120,768]{1,0:T(8,128)(2,1)}, u32[]{:S(2)}, u32[]{:S(2)}) %collective-permute-start.12) | collective-permute-done | bytes 1720352 | tf_op jit(solution)/shard_map/ppermute | solution.py:1031
  334.6 2.4 add_convert_fusion
  338.2 27.6 %input_back.1 = (f32[1,5120]{1,0:T(1,128)}, bf16[4,128,1536]{2,1,0:T(8,128)(2,1)}) custom-call(bf16[4,128,1536]{2,1,0:T(8,128)(2,1)} %bitcast.78, bf16[128,1536]{1,0:T(8,128)(2,1)} %constant_dynamic-slice_fusion.6.x_ref, f32[128,1]{1,0:T(8,128)} %constant_dynamic-slice_fusion.4.factor_ref, f32[1,1536]{1,0:T(1,128)} %bitcast.86, ...), custom_call_target="tpu_custom_call" | custom-call | tf_op jit(solution)/shard_map/input_back/pallas_call | solution.py:589
  365.9 2.7 fusion.3.refs_1_
  368.6 4.9 %fusion.1 = f32[2240,768]{1,0:T(8,128)} fusion(bf16[1120,768]{1,0:T(8,128)(2,1)} %collective-permute-done.11, bf16[1120,768]{1,0:T(8,128)(2,1)S(1)} %add_convert_fusion.2, pred[]{:T(512)S(6)} %eq.19), kind=kLoop, calls=%fused_computation.5 | loop fusion | flops 17203200 | bytes 10321921 | tf_op jit(solution)/shard_map/convert_element_type | solution.py:1180
  373.5 2.5 fusion.2.refs_0_
  378.1 5.3 %fusion = f32[2240,768]{1,0:T(8,128)} fusion(bf16[1120,768]{1,0:T(8,128)(2,1)} %collective-permute-done.16, bf16[1120,768]{1,0:T(8,128)(2,1)} %add_convert_fusion.1, pred[]{:T(512)S(6)} %eq.19), kind=kLoop, calls=%fused_computation.3 | loop fusion | flops 17203200 | bytes 10321921 | tf_op jit(solution)/shard_map/convert_element_type | solution.py:1180
  383.3 15.4 %collective-permute-done.15 = bf16[1120,768]{1,0:T(8,128)(2,1)} collective-permute-done((bf16[1120,768]{1,0:T(8,128)(2,1)S(1)}, bf16[1120,768]{1,0:T(8,128)(2,1)}, u32[]{:S(2)}, u32[]{:S(2)}) %collective-permute-start.15) | collective-permute-done | bytes 1720352 | tf_op jit(solution)/shard_map/ppermute | solution.py:1031
  398.7 69.7 %context_sum.1 = (f32[384,768]{1,0:T(8,128)}, f32[768,384]{1,0:T(8,128)}, f32[1,5120]{1,0:T(1,128)}, bf16[4,768,128]{2,1,0:T(8,128)(2,1)}, bf16[4,128,1536]{2,1,0:T(8,128)(2,1)}) custom-call(bf16[384,768]{1,0:T(8,128)(2,1)} %fusion.2.refs_0_, bf16[768,384]{1,0:T(8,128)(2,1)} %fusion.3.refs_1_, bf16[768,128]{1,0:T(8,128)(2,1)} %fusion.4.refs_2_, ...), custom_call_target="tpu_custom_call" | custom-call | tf_op jit(solution)/shard_map/context_sum/pallas_call | solution.py:589
  475.0 4.8 convert_bitcast_fusion
  (143 shorter events, 52.1 us)
Async XLA Ops:
  1.7 18.7 %copy-start.2 = (bf16[128,1536]{1,0:T(8,128)(2,1)}, bf16[128,1536]{1,0:T(8,128)(2,1)S(1)}, u32[]{:S(2)}) copy-start(bf16[128,1536]{1,0:T(8,128)(2,1)S(1)} %constant_dynamic-slice_fusion.7.dy_ref) | copy-start | bytes 1179652
  1.7 33.2 %collective-permute-start.3 = (bf16[128,1536]{1,0:T(8,128)(2,1)S(1)}, bf16[128,1536]{1,0:T(8,128)(2,1)}, u32[]{:S(2)}, u32[]{:S(2)}) collective-permute-start(bf16[128,1536]{1,0:T(8,128)(2,1)S(1)} %constant_dynamic-slice_fusion.7.dy_ref), channel_id=1, source_target_pairs={{0,8},{4,12},{8,0},{12,4},{1,9},{5,13},{9,1},{13,5},{2,10},{6,14},... | collective-permute-start | bytes 1179656 | tf_op jit(solution)/shard_map/ppermute | solution.py:1031
  5.8 29.1 %collective-permute-start.2 = (bf16[128,1536]{1,0:T(8,128)(2,1)S(1)}, bf16[128,1536]{1,0:T(8,128)(2,1)}, u32[]{:S(2)}, u32[]{:S(2)}) collective-permute-start(bf16[128,1536]{1,0:T(8,128)(2,1)S(1)} %constant_dynamic-slice_fusion.7.dy_ref), channel_id=1, source_target_pairs={{0,4},{4,0},{8,12},{12,8},{1,5},{5,1},{9,13},{13,9},{2,6},{6,2},{1... | collective-permute-start | bytes 1179656 | tf_op jit(solution)/shard_map/ppermute | solution.py:1031
  7.4 27.5 %collective-permute-start.1 = (bf16[128,1536]{1,0:T(8,128)(2,1)S(1)}, bf16[128,1536]{1,0:T(8,128)(2,1)}, u32[]{:S(2)}, u32[]{:S(2)}) collective-permute-start(bf16[128,1536]{1,0:T(8,128)(2,1)S(1)} %constant_dynamic-slice_fusion.7.dy_ref), channel_id=1, source_target_pairs={{0,2},{1,3},{2,0},{3,1},{4,6},{5,7},{6,4},{7,5},{8,10},{9,11},{10,... | collective-permute-start | bytes 1179656 | tf_op jit(solution)/shard_map/ppermute | solution.py:1031
  12.6 13.7 %collective-permute-start = (bf16[1,1984]{1,0:T(2,128)(2,1)S(1)}, bf16[1,1984]{1,0:T(2,128)(2,1)S(1)}, u32[]{:S(2)}, u32[]{:S(2)}) collective-permute-start(bf16[1,1984]{1,0:T(2,128)(2,1)S(1)} %concatenate.64), channel_id=1, source_target_pairs={{0,16},{16,0},{1,17},{17,1},{2,18},{18,2},{3,19},{19,3},{4,20},{20... | collective-permute-start | bytes 11912 | tf_op jit(solution)/shard_map/ppermute | solution.py:1031
  14.1 18.5 %collective-permute-start.4 = (bf16[768,384]{1,0:T(8,128)(2,1)}, bf16[768,384]{1,0:T(8,128)(2,1)S(1)}, u32[]{:S(2)}, u32[]{:S(2)}) collective-permute-start(bf16[768,384]{1,0:T(8,128)(2,1)} %refs_0_.3), channel_id=1, source_target_pairs={{0,16},{16,0},{1,17},{17,1},{2,18},{18,2},{3,19},{19,3},{4,20},{20... | collective-permute-start | bytes 1769480 | tf_op jit(solution)/shard_map/ppermute | solution.py:1031
  22.9 2.7 copy-start.22
  22.9 2.7 copy-start.23
  22.9 9.7 %copy-start.19 = (bf16[384,768]{1,0:T(8,128)(2,1)S(1)}, bf16[384,768]{1,0:T(8,128)(2,1)}, u32[]{:S(2)}) copy-start(bf16[384,768]{1,0:T(8,128)(2,1)} %param.25) | copy-start | bytes 1769476
  25.6 9.3 %copy-start.6 = (bf16[768,128]{1,0:T(8,128)(2,1)}, bf16[768,128]{1,0:T(8,128)(2,1)S(1)}, u32[]{:S(2)}) copy-start(bf16[768,128]{1,0:T(8,128)(2,1)S(1)} %dynamic-slice_select_fusion.refs_2_) | copy-start | bytes 589828
  26.3 6.3 %collective-permute-start.5 = (bf16[768,128]{1,0:T(8,128)(2,1)S(1)}, bf16[768,128]{1,0:T(8,128)(2,1)S(1)}, u32[]{:S(2)}, u32[]{:S(2)}) collective-permute-start(bf16[768,128]{1,0:T(8,128)(2,1)S(1)} %dynamic-slice_select_fusion.refs_2_), channel_id=1, source_target_pairs={{0,16},{16,0},{1,17},{17,1},{2,18},{18,2},{3,19},{19,3},{4,20},{20... | collective-permute-start | bytes 589832 | tf_op jit(solution)/shard_map/ppermute | solution.py:1031
  32.6 13.9 %collective-permute-start.6 = (bf16[384,768]{1,0:T(8,128)(2,1)S(1)}, bf16[384,768]{1,0:T(8,128)(2,1)S(1)}, u32[]{:S(2)}, u32[]{:S(2)}) collective-permute-start(bf16[384,768]{1,0:T(8,128)(2,1)S(1)} %copy-done.19), channel_id=1, source_target_pairs={{0,16},{16,0},{1,17},{17,1},{2,18},{18,2},{3,19},{19,3},{4,20},{20... | collective-permute-start | bytes 1769480 | tf_op jit(solution)/shard_map/ppermute | solution.py:1031
  46.7 28.5 %copy-start = (bf16[384,1536]{1,0:T(8,128)(2,1)}, bf16[384,1536]{1,0:T(8,128)(2,1)S(1)}, u32[]{:S(2)}) copy-start(bf16[384,1536]{1,0:T(8,128)(2,1)S(1)} %maximum_select_fusion.3) | copy-start | bytes 3538948
  46.7 111.2 %collective-permute-start.7 = (bf16[3360,768]{1,0:T(8,128)(2,1)}, bf16[3360,768]{1,0:T(8,128)(2,1)}, u32[]{:S(2)}, u32[]{:S(2)}) collective-permute-start(bf16[3360,768]{1,0:T(8,128)(2,1)} %pad_maximum_fusion.refs_0_.refs_2_.refs_4_), channel_id=1, source_target_pairs={{0,16},{16,0},{1,17},{17,1},{2,18},{18,2},{3,19},{19,3},{4,20},{20... | collective-permute-start | bytes 15482888 | tf_op jit(solution)/shard_map/ppermute | solution.py:1031
  220.0 40.9 %collective-permute-start.8 = (bf16[1120,768]{1,0:T(8,128)(2,1)}, bf16[1120,768]{1,0:T(8,128)(2,1)}, u32[]{:S(2)}, u32[]{:S(2)}) collective-permute-start(bf16[1120,768]{1,0:T(8,128)(2,1)} %get-tuple-element.89), channel_id=1, source_target_pairs={{0,16},{16,0},{1,17},{17,1},{2,18},{18,2},{3,19},{19,3},{4,20},{20... | collective-permute-start | bytes 5160968 | tf_op jit(solution)/shard_map/ppermute | solution.py:1031
  220.3 77.4 %collective-permute-start.10 = (bf16[1120,768]{1,0:T(8,128)(2,1)}, bf16[1120,768]{1,0:T(8,128)(2,1)}, u32[]{:S(2)}, u32[]{:S(2)}) collective-permute-start(bf16[1120,768]{1,0:T(8,128)(2,1)} %get-tuple-element.96), channel_id=1, source_target_pairs={{0,16},{16,0},{1,17},{17,1},{2,18},{18,2},{3,19},{19,3},{4,20},{20... | collective-permute-start | bytes 5160968 | tf_op jit(solution)/shard_map/ppermute | solution.py:1031
  260.9 4.8 copy-start.1
  263.4 52.6 %collective-permute-start.11 = (bf16[1120,768]{1,0:T(8,128)(2,1)S(1)}, bf16[1120,768]{1,0:T(8,128)(2,1)}, u32[]{:S(2)}, u32[]{:S(2)}) collective-permute-start(bf16[1120,768]{1,0:T(8,128)(2,1)S(1)} %add_convert_fusion.2), channel_id=1, source_target_pairs={{0,4},{4,0},{8,12},{12,8},{1,5},{5,1},{9,13},{13,9},{2,6},{6,2},{1... | collective-permute-start | bytes 5160968 | tf_op jit(solution)/shard_map/ppermute | solution.py:1031
  265.4 69.2 %collective-permute-start.12 = (bf16[1120,768]{1,0:T(8,128)(2,1)}, bf16[1120,768]{1,0:T(8,128)(2,1)}, u32[]{:S(2)}, u32[]{:S(2)}) collective-permute-start(bf16[1120,768]{1,0:T(8,128)(2,1)} %get-tuple-element.106), channel_id=1, source_target_pairs={{0,16},{16,0},{1,17},{17,1},{2,18},{18,2},{3,19},{19,3},{4,20},{20... | collective-permute-start | bytes 5160968 | tf_op jit(solution)/shard_map/ppermute | solution.py:1031
  268.8 15.1 %copy-start.20 = (bf16[512,384]{1,0:T(8,128)(2,1)S(1)}, bf16[512,384]{1,0:T(8,128)(2,1)}, u32[]{:S(2)}) copy-start(bf16[512,384]{1,0:T(8,128)(2,1)} %get-tuple-element.78) | copy-start | bytes 1179652
  288.9 76.9 %collective-permute-start.13 = (bf16[768,384]{1,0:T(8,128)(2,1)}, bf16[768,384]{1,0:T(8,128)(2,1)}, u32[]{:S(2)}, u32[]{:S(2)}) collective-permute-start(bf16[768,384]{1,0:T(8,128)(2,1)} %convolution_convert_fusion.1), channel_id=1, source_target_pairs={{0,16},{16,0},{1,17},{17,1},{2,18},{18,2},{3,19},{19,3},{4,20},{20... | collective-permute-start | bytes 1769480 | tf_op jit(solution)/shard_map/ppermute | solution.py:1031
  290.7 77.9 %collective-permute-start.9 = (bf16[384,768]{1,0:T(8,128)(2,1)}, bf16[384,768]{1,0:T(8,128)(2,1)}, u32[]{:S(2)}, u32[]{:S(2)}) collective-permute-start(bf16[384,768]{1,0:T(8,128)(2,1)} %convolution_convert_fusion.2), channel_id=1, source_target_pairs={{0,16},{16,0},{1,17},{17,1},{2,18},{18,2},{3,19},{19,3},{4,20},{20... | collective-permute-start | bytes 1769480 | tf_op jit(solution)/shard_map/ppermute | solution.py:1031
  316.0 3.6 copy-start.16
  319.8 2.6 copy-start.12
  322.1 53.9 %collective-permute-start.14 = (bf16[768,128]{1,0:T(8,128)(2,1)}, bf16[768,128]{1,0:T(8,128)(2,1)}, u32[]{:S(2)}, u32[]{:S(2)}) collective-permute-start(bf16[768,128]{1,0:T(8,128)(2,1)} %convolution_convert_fusion.4), channel_id=1, source_target_pairs={{0,16},{16,0},{1,17},{17,1},{2,18},{18,2},{3,19},{19,3},{4,20},{20... | collective-permute-start | bytes 589832 | tf_op jit(solution)/shard_map/ppermute | solution.py:1031
  322.4 55.6 %collective-permute-start.16 = (bf16[1120,768]{1,0:T(8,128)(2,1)}, bf16[1120,768]{1,0:T(8,128)(2,1)}, u32[]{:S(2)}, u32[]{:S(2)}) collective-permute-start(bf16[1120,768]{1,0:T(8,128)(2,1)} %add_convert_fusion.1), channel_id=1, source_target_pairs={{0,4},{4,0},{8,12},{12,8},{1,5},{5,1},{9,13},{13,9},{2,6},{6,2},{1... | collective-permute-start | bytes 5160968 | tf_op jit(solution)/shard_map/ppermute | solution.py:1031
  334.6 2.9 copy-start.24
  337.0 28.8 %copy-start.13 = (bf16[512,384]{1,0:T(8,128)(2,1)S(1)}, bf16[512,384]{1,0:T(8,128)(2,1)}, u32[]{:S(2)}) copy-start(bf16[512,384]{1,0:T(8,128)(2,1)} %get-tuple-element.93.dq_ref) | copy-start | bytes 1179652
  337.0 61.7 %collective-permute-start.15 = (bf16[1120,768]{1,0:T(8,128)(2,1)S(1)}, bf16[1120,768]{1,0:T(8,128)(2,1)}, u32[]{:S(2)}, u32[]{:S(2)}) collective-permute-start(bf16[1120,768]{1,0:T(8,128)(2,1)S(1)} %add_convert_fusion), channel_id=1, source_target_pairs={{0,4},{4,0},{8,12},{12,8},{1,5},{5,1},{9,13},{13,9},{2,6},{6,2},{1... | collective-permute-start | bytes 5160968 | tf_op jit(solution)/shard_map/ppermute | solution.py:1031
  368.6 4.9 %copy-start.21 = (bf16[512,384]{1,0:T(8,128)(2,1)S(1)}, bf16[512,384]{1,0:T(8,128)(2,1)}, u32[]{:S(2)}) copy-start(bf16[512,384]{1,0:T(8,128)(2,1)} %get-tuple-element.78) | copy-start | bytes 1179652
  368.6 4.9 %copy-start.25 = (bf16[4,128,1536]{2,1,0:T(8,128)(2,1)S(1)}, bf16[4,128,1536]{2,1,0:T(8,128)(2,1)}, u32[]{:S(2)}) copy-start(bf16[4,128,1536]{2,1,0:T(8,128)(2,1)} %get-tuple-element.87) | copy-start | bytes 4718596
  475.0 4.8 copy-start.8
  (11 other events, 23.4 us)

commit v12 on v10

--- a/solution.py
+++ b/solution.py
@@ -449,6 +449,55 @@
     def finish(self):
         for one in self.started:
             one.wait_send()
+
+
+class OwnGrad:
+    TILE = 256
+
+    def __init__(self, units, rows, out, units_here, rows_here):
+        self.units, self.rows, self.out = units, rows, out
+        self.units_here, self.rows_here = units_here, rows_here
+        self.tiles = out.shape[1] // self.TILE
+        self.copies = None
+
+    def fetch(self, wires):
+        half, depth = self.rows.shape[0] // 2, self.out.shape[1]
+        column = pl.multiple_of(lax.axis_index("fsdp") * depth, LANES)
+        pair = lax.axis_index("context") // 2
+        self.copies = [wires.here(self.units, self.units_here)]
+        for k, place in ((0, pair), (1, 1 - pair)):
+            self.copies.append(
+                wires.here(
+                    self.rows.at[pl.ds(k * half, half), pl.ds(column, depth)],
+                    self.rows_here.at[pl.ds(pl.multiple_of(place * half, half), half)],
+                )
+            )
+
+    def make(self, first, past):
+        for one in self.copies:
+            one.wait()
+        self.copies = []
+
+        @pl.loop(first, past)
+        def _(k):
+            at = pl.ds(pl.multiple_of(k * self.TILE, self.TILE), self.TILE)
+            self.out[:, at] = dot_rows(self.units_here[...], self.rows_here[:, at]).astype(bf16)
+
+
+def own_grad_call(fill, width):
+    args = [x for pair in fill for x in pair]
+    outs = [jax.ShapeDtypeStruct((units.shape[1], width), bf16) for units, _ in fill]
+    scratch = []
+    for units, rows in fill:
+        scratch += [pltpu.VMEM(units.shape, bf16), pltpu.VMEM((rows.shape[0], width), bf16)]
+    return args, outs, scratch
+
+
+def own_grads(count, args, outs, scratch):
+    return [
+        OwnGrad(args[2 * k], args[2 * k + 1], outs[k], scratch[2 * k], scratch[2 * k + 1])
+        for k in range(count)
+    ]
 
 
 def meet(devices):
@@ -641,8 +690,11 @@
     )[0]
 
 
-def kv_scatter_kernel(part_ref, dkv_ref, own, got_core, sent, got, *sems):
-    wires, to = Wires(*sems), partners()
+def kv_scatter_kernel(count, part_ref, *refs):
+    args, dkv_ref, outs = refs[: 2 * count], refs[2 * count], refs[2 * count + 1 : 3 * count + 1]
+    own, got_core, sent, got = refs[3 * count + 1 : 3 * count + 5]
+    wires, to = Wires(*refs[-3:]), partners()
+    fill = own_grads(count, args, outs, refs[3 * count + 5 : -3])
     kind = lax.rem(lax.axis_index("tensor"), 2)
     rows = dkv_ref.shape[0]
     block = lambda j: pl.ds(j * rows, rows)
@@ -653,12 +705,16 @@
         for j, _ in steps
     }
     mine = wires.here(part_ref.at[kind], own)
+    for one in fill:
+        one.fetch(wires)
     mine.wait()
     arrive = []
     for j, k in steps[:3]:
         from_core[j].wait_recv()
         sent[block(j)] = (wide(own[block(j)]) + wide(got_core[block(j)])).astype(bf16)
         arrive.append(wires.copy(sent.at[block(j)], got.at[block(j)], to[k]))
+    for one in fill:
+        one.make(0, one.tiles)
     from_core[0].wait_recv()
     total = wide(own[block(0)]) + wide(got_core[block(0)])
     for one in arrive:
@@ -669,19 +725,20 @@
     wires.finish()
 
 
-def kv_scatter(part):
-    _, rows, width = part.shape
+def kv_scatter(part, fill, width):
+    _, rows, depth = part.shape
     n_c = lax.axis_size("context")
+    args, outs, scratch = own_grad_call(fill, width)
     return remote_call(
-        kv_scatter_kernel,
+        functools.partial(kv_scatter_kernel, len(fill)),
         "kv_scatter",
         1,
-        [part],
-        [jax.ShapeDtypeStruct((rows // n_c, width), f32)],
-        [pltpu.VMEM((rows, width), bf16)] * 4,
+        [part, *args],
+        [jax.ShapeDtypeStruct((rows // n_c, depth), f32), *outs],
+        [pltpu.VMEM((rows, depth), bf16)] * 4 + scratch,
         7,
-        ([False], [True]),
-    )[0]
+        ([False] * (1 + len(args)), [True] * (1 + len(outs))),
+    )
 
 
 def middle_kernel(
@@ -785,12 +842,23 @@
     return grad_values, jnp.sum(grad_normed * values * factor, axis=0, keepdims=True)
 
 
-def middle_back_kernel(
-    part, mid_ref, factor_ref, gain_ref, dy_ref, dmid_ref, dgain_ref, out, low, *rest
-):
-    first, wires, to = rest[:7], Wires(*rest[7:]), partners()
+def middle_back_kernel(count, part, mid_ref, factor_ref, gain_ref, dy_ref, *refs):
+    args, (dmid_ref, dgain_ref, out) = refs[: 2 * count], refs[2 * count : 2 * count + 3]
+    outs, refs = refs[2 * count + 3 : 3 * count + 3], refs[3 * count + 3 :]
+    low, first, wires, to = refs[0], refs[1:8], Wires(*refs[-3:]), partners()
+    fill = own_grads(count, args, outs, refs[8:-3])
     meet([to[k] for k in ("core", "y", "z")])
-    grad_normed = result_of(scatter_pair(wires, to, part, *first))
+    back = scatter_pair(wires, to, part, *first)
+    next(back)
+    for one in fill:
+        one.fetch(wires)
+    next(back)
+    if fill:
+        fill[0].make(0, 1)
+    next(back)
+    if fill:
+        fill[0].make(1, fill[0].tiles)
+    grad_normed = result_of(back)
     du, dgain = norm_back_rows(mid_ref[...], factor_ref[...], gain_ref[...], grad_normed)
     dgain_ref[...] = dgain
     dmid = wide(dy_ref[...]) + du
@@ -798,6 +866,8 @@
     share = gather_rank(wires, to, low, out)
     next(share)
     dmid_ref[...] = dmid
+    for one in fill[1:]:
+        one.make(0, one.tiles)
     result_of(share)
     wires.finish()
 
@@ -814,21 +884,26 @@
     ]
 
 
-def middle_back(part, middle, factor, gain, dy_part):
+def middle_back(part, middle, factor, gain, dy_part, fill, shard):
     rows, width = middle.shape
+    args, outs, scratch = own_grad_call(fill, shard)
     return remote_call(
-        middle_back_kernel,
+        functools.partial(middle_back_kernel, len(fill)),
         "middle_back",
         3,
-        [part.reshape(8, rows, width), middle, factor, gain, dy_part],
+        [part.reshape(8, rows, width), middle, factor, gain, dy_part, *args],
         [
             jax.ShapeDtypeStruct((rows, width), f32),
             jax.ShapeDtypeStruct((1, width), f32),
             jax.ShapeDtypeStruct((4, rows, width), bf16),
+            *outs,
         ],
-        [pltpu.VMEM((rows, width), bf16)] + pair_scratch(rows, width),
+        [pltpu.VMEM((rows, width), bf16)] + pair_scratch(rows, width) + scratch,
         16,
-        ([False, True, True, True, True], [True, True, False]),
+        (
+            [False, True, True, True, True] + [False] * len(args),
+            [True, True, False] + [True] * len(outs),
+        ),
     )
 
 
@@ -1102,7 +1177,9 @@
         b_kv = lax.dynamic_index_in_dim(jnp.where(core == 0, bk, bv), group, 0)
 
         unit_slice = lambda w: lax.dynamic_slice_in_dim(w, parity * units, units, 0)
-        own_gate_up = jnp.concatenate([unit_slice(w) for w in (w_gate.T, w_up.T)], axis=0)
+        own_gate_up = jnp.concatenate(
+            [unit_slice(after(w, w_kv_own)) for w in (w_gate.T, w_up.T)], axis=0
+        )
         own_down = unit_slice(w_down)
 
         dy_part = lax.dynamic_slice_in_dim(cotangent, t * part, part, 0)
@@ -1123,7 +1200,8 @@
             flip(dy_part, "context", 1),
             flip(dy_part, "context", 2),
         ]
-        bias = after(bias, dy_blocks)
+        inputs_part = lax.dynamic_slice_in_dim(inputs, t * part, part, 0)
+        bias = after(bias, dy_blocks[2:], own_gate_up, own_down, inputs_part)
         normed, factor_first, queries, kv_own = qkv(
             meta, inputs, gain_first, bias, cosine, sine, w_q, w_kv
         )
@@ -1133,7 +1211,6 @@
         far_down = pieces_f(after(own_down, kv), 1)[-1]
         w_downs = [own_down, far_down] if n_f == 2 else [far_down]
         attended, lse = attention(key_blocks, queries, kv)
-        inputs_part = lax.dynamic_slice_in_dim(inputs, t * part, part, 0)
         middle, factor_second, normed2, dy_all = middle_norm(
             dot(attended, w_out_all).astype(bf16), inputs_part, gain_second, dy_blocks
         )
@@ -1143,13 +1220,19 @@
             meta, normed2, dy_all, hidden, slope, gated, w_gate_up, w_downs
         )
         unit_far = [*down_far, *unit_far]
+        flat = lambda x: x.reshape(-1, width)
         if n_f == 2:
             down_got, gate_got, up_got = (flip(x, "fsdp", 1) for x in unit_far)
+            early = [(hidden, flat(dy_all)), (grad_gate, flat(normed2))]
+            later = [(grad_up, flat(normed2))]
         else:
             over_f = lambda x: lax.psum_scatter(x, "fsdp", scatter_dimension=1, tiled=True)
-            down_own = over_f(unit_grads(meta, 0, 1, dy_all, [hidden]))
-            gate_up_own = over_f(unit_grads(meta, 0, 1, normed2, [grad_gate, grad_up]))
-            down_got = gate_got = up_got = jnp.zeros_like(down_own)
+            owns = [
+                over_f(unit_grads(meta, 0, 1, x, [unit]))
+                for x, unit in ((dy_all, hidden), (normed2, grad_gate), (normed2, grad_up))
+            ]
+            down_got = gate_got = up_got = jnp.zeros_like(owns[0])
+            early = later = []
 
         def unit_done(own, got):
             low = (own.astype(f32) + got.astype(f32)).astype(bf16)
@@ -1157,23 +1240,22 @@
 
         unit_whole = lambda low, other: by_bit(parity, low, other, 0).astype(f32)
 
-        grad_middle, ffn_gain_grad, grad_middle_low = middle_back(
-            dx_part, middle, factor_second, gain_second, dy_part
+        grad_middle, ffn_gain_grad, grad_middle_low, *first_owns = middle_back(
+            dx_part, middle, factor_second, gain_second, dy_part, early, width // n_f
         )
         grad_middle_low = grad_middle_low.reshape(rows, width)
-        if n_f == 2:
-            down_own = unit_grads(meta, 0, 2, *after((dy_all, [hidden]), grad_middle_low))
+        down_own, gate_own = first_owns or owns[:2]
         down_done = unit_done(down_own, after(down_got, grad_middle_low))
         grad_attended = dot_cols(after(grad_middle_low, down_done[0]), w_out_all).astype(bf16)
 
         dq_low, dkv = attention_back(key_blocks, queries, grad_attended, lse, cosine, sine, kv)
-        if n_f == 2:
-            gate_up_own = unit_grads(meta, 0, 2, *after((normed2, [grad_gate, grad_up]), dkv))
-            dkv = after(dkv, gate_up_own)
-        attention_args = [(attended, grad_middle_low, 1), (normed, dq_low, 0)]
+        attention_args = [(attended, after(grad_middle_low, dq_low), 1), (normed, dq_low, 0)]
         fars = [grad_far(*args) for args in attention_args]
-        dkv = kv_scatter(after(dkv, down_done, gate_got, fars))
-        gate_done = unit_done(gate_up_own[:units], after(gate_got, dkv))
+        dkv, *last_owns = kv_scatter(
+            after(dkv, gate_got, fars), later, width // n_f
+        )
+        (up_own,) = last_owns or owns[2:]
+        gate_done = unit_done(gate_own, after(gate_got, dkv, down_done))
         dkv = after(dkv, gate_done[0])
         dkv_low = jnp.where(core == 0, rotate_back(dkv, cosine, sine), dkv).astype(bf16)
         attention_args.append((normed, dkv_low, 0))
@@ -1190,7 +1272,7 @@
             [jnp.zeros((1, width), f32), ffn_gain_grad, slots.reshape(1, -1)], axis=1
         )
         grad_qkv = qkv_back(meta, dq_low, dkv_low, w_q, w_kv)
-        up_done = unit_done(gate_up_own[units:], after(up_got, grad_qkv))
+        up_done = unit_done(up_own, after(up_got, grad_qkv))
         small_grads, input_grad = input_back(
             after(grad_qkv, up_done[0]),
             inputs_part,

time: 500 us -> 483 us (0.966)
  Pallas kernels: 358 us -> 339 us
    pallas_call x2 -> x0, Pallas kernels: 22.9 us -> none  [unit_grads(): pl.pallas_call(functools.partial(unit_grads_kernel, count), name=f'unit_g...]
    unnamed x69 -> x63, local copies, waits for them, and re-layouts: 11.7 us -> 12.3 us
  transfers between devices with their start and end apart: 18 -> 18, of which waited for: 4 -> 3; matrix products, arithmetic and copies ran while one was open for 12% -> 12% of each run, Pallas kernels for 58% -> 56%
where the time goes in v12:
time: 483 us; the launch traced here: 479 us
  Pallas kernels  339 us (70%)
  other arithmetic  37.7 us (8%)
  waiting for transfers between devices  31.1 us (6%)
  local copies, waits for them, and re-layouts  28.1 us (6%)
  starting transfers between devices  21.7 us (4%)
  matrix products  20 us (4%)
    pallas_call x6, Pallas kernels, remote_call(): pl.pallas_call(kernel, name=name, out_shape=outs, in_specs=[spec(x) for x...  231 us
    pallas_call x2, Pallas kernels, hidden_call(): pl.pallas_call(kernel, name=name, grid_spec=pltpu.PrefetchScalarGridSpec(...  71.7 us
    ppermute x18, waiting for transfers between devices, flip(): return lax.ppermute(x, axis, [(i, i ^ bit) for i in range(size)])  31.1 us
    ppermute x18, starting transfers between devices, flip(): return lax.ppermute(x, axis, [(i, i ^ bit) for i in range(size)])  21.7 us
    pallas_call x1, Pallas kernels, attention_back(): pl.pallas_call(functools.partial(attention_back_kernel, kv.shape[1] // BL...  15.1 us
    dot_general x6, matrix products, dot_rows(): lax.dot_general(left, right, (((0,), (0,)), ((), ())), preferred_element_...  13.4 us
    unnamed x63, local copies, waits for them, and re-layouts  12.3 us
    pallas_call x1, Pallas kernels, attention(): pl.pallas_call(functools.partial(attention_kernel, kv.shape[1] // BLOCK),...  10.2 us
  transfers between devices with their start and end apart: 18, of which 3 were waited for; matrix products, arithmetic and copies ran while one was open for 12% of the time, Pallas kernels for 56%

profile of v12, /device:TPU:0, one launch (start us, length us, event | category | flops | bytes accessed | tf_op | source)
XLA Modules:
  0.0 479.1 jit_solution(7486692389967682448)
XLA Ops:
  0.7 1.9 constant_dynamic-slice_fusion.9.dy_ref
  2.6 4.0 collective-permute-start.2
  19.2 1.8 constant_dynamic-slice_fusion.5.x_ref
  28.9 5.1 %collective-permute-done.3.refs_1_ = bf16[768,384]{1,0:T(8,128)(2,1)} collective-permute-done((bf16[768,384]{1,0:T(8,128)(2,1)}, bf16[768,384]{1,0:T(8,128)(2,1)}, u32[]{:S(2)}, u32[]{:S(2)}) %collective-permute-start.3) | collective-permute-done | bytes 589856 | tf_op jit(solution)/shard_map/ppermute | solution.py:1084
  35.9 6.5 %qkv.1 = (bf16[512,1536]{1,0:T(8,128)(2,1)}, f32[512,1]{1,0:T(8,128)}, bf16[512,384]{1,0:T(8,128)(2,1)}, bf16[512,128]{1,0:T(8,128)(2,1)}) custom-call(s32[4]{0:T(128)} %pad_add_fusion.1.meta_ref, bf16[512,1536]{1,0:T(8,128)(2,1)} %x_ref.1, f32[1,1536]{1,0:T(1,128)} %bitcast.87, f32[1,512]{1,0:T(1,128)} %pad_maximum_fusion.6.bias_ref, ...), custom_call_target="tpu_custom_call" | custom-call | tf_op jit(solution)/shard_map/qkv/pallas_call | solution.py:209
  42.3 5.2 %collective-permute-done.5 = bf16[384,768]{1,0:T(8,128)(2,1)} collective-permute-done((bf16[384,768]{1,0:T(8,128)(2,1)}, bf16[384,768]{1,0:T(8,128)(2,1)}, u32[]{:S(2)}, u32[]{:S(2)}) %collective-permute-start.5) | collective-permute-done | bytes 589856 | tf_op jit(solution)/shard_map/ppermute | solution.py:1084
  47.6 2.5 maximum_select_fusion.3
  53.3 14.8 %kv_gather.1.k_ref.v_ref = bf16[2,2048,128]{2,1,0:T(8,128)(2,1)} custom-call(bf16[512,128]{1,0:T(8,128)(2,1)} %get-tuple-element.84.own_ref), custom_call_target="tpu_custom_call" | custom-call | tf_op jit(solution)/shard_map/kv_gather/pallas_call | solution.py:642
  69.8 10.2 %attention.1 = (bf16[512,384]{1,0:T(8,128)(2,1)}, f32[3,512,1]{2,1,0:T(8,128)}) custom-call(s32[8]{0:T(128)} %pad_add_fusion.kb_ref, bf16[512,384]{1,0:T(8,128)(2,1)} %get-tuple-element.81.q_ref, bf16[2,2048,128]{2,1,0:T(8,128)(2,1)} %kv_gather.1.k_ref.v_ref, bf16[2,2048,128]{2,1,0:T(8,128)(2,1)} %kv_gather.1.k_ref.v_ref), custom_call_target="tpu_custom_call" | custom-call | tf_op jit(solution)/shard_map/attention/pallas_call | solution.py:85
  79.9 3.5 convolution_convert_fusion
  83.4 62.6 %middle_norm.1 = (f32[128,1536]{1,0:T(8,128)}, f32[128,1]{1,0:T(8,128)}, bf16[16,128,1536]{2,1,0:T(8,128)(2,1)}, bf16[16,128,1536]{2,1,0:T(8,128)(2,1)}) custom-call(bf16[4,128,1536]{2,1,0:T(8,128)(2,1)} %bitcast.79, bf16[128,1536]{1,0:T(8,128)(2,1)} %constant_dynamic-slice_fusion.5.x_ref, f32[1,1536]{1,0:T(1,128)} %bitcast.89, ...), custom_call_target="tpu_custom_call" | custom-call | tf_op jit(solution)/shard_map/middle_norm/pallas_call | solution.py:642
  146.0 29.8 %hidden_units.1 = (bf16[2048,1120]{1,0:T(8,128)(2,1)}, bf16[2048,1120]{1,0:T(8,128)(2,1)}, bf16[2048,1120]{1,0:T(8,128)(2,1)}, bf16[1120,768]{1,0:T(8,128)(2,1)}) custom-call(s32[4]{0:T(128)} %pad_add_fusion.1.meta_ref, bf16[2048,1536]{1,0:T(8,128)(2,1)} %bitcast.70, bf16[2048,1536]{1,0:T(8,128)(2,1)} %bitcast.74, bf16[2240,768]{1,0:T(8,128)(2,1)} %copy-done.2, ...), custom_call_target="tpu_custom_call" | custom-call | tf_op jit(solution)/shard_map/hidden_units/pallas_call | solution.py:333
  176.6 42.0 %hidden_back.1 = (bf16[2048,1120]{1,0:T(8,128)(2,1)}, bf16[2048,1120]{1,0:T(8,128)(2,1)}, bf16[1024,1536]{1,0:T(8,128)(2,1)}, bf16[1024,1536]{1,0:T(8,128)(2,1)}...) custom-call(s32[4]{0:T(128)} %pad_add_fusion.1.meta_ref, bf16[2048,1536]{1,0:T(8,128)(2,1)} %bitcast.71, ...), custom_call_target="tpu_custom_call" | custom-call | tf_op jit(solution)/shard_map/hidden_back/pallas_call | solution.py:333
  219.9 34.2 %middle_back.1 = (f32[128,1536]{1,0:T(8,128)}, f32[1,1536]{1,0:T(1,128)}, bf16[4,128,1536]{2,1,0:T(8,128)(2,1)}, bf16[1120,768]{1,0:T(8,128)(2,1)}, bf16[1120,768]{1,0:T(8,128)(2,1)}) custom-call(bf16[8,128,1536]{2,1,0:T(8,128)(2,1)} %bitcast.81, f32[128,1536]{1,0:T(8,128)} %get-tuple-element.94.mid_ref.refs_5_, f32[128,1]{1,0:T(8,128)} %get-tuple-element.95.factor_ref, ...), custom_call_target="tpu_custom_call" | custom-call | tf_op jit(solution)/shard_map/middle_back/pallas_call | solution.py:642
  255.2 2.5 add_convert_fusion.2
  260.6 3.1 convolution_convert_fusion.3.do_ref
  263.7 15.1 %attention_back.1 = (bf16[512,384]{1,0:T(8,128)(2,1)}, bf16[2,2048,128]{2,1,0:T(8,128)(2,1)}) custom-call(s32[8]{0:T(128)} %pad_add_fusion.kb_ref, bf16[512,384]{1,0:T(8,128)(2,1)} %get-tuple-element.81.q_ref, bf16[512,384]{1,0:T(8,128)(2,1)} %convolution_convert_fusion.3.do_ref, f32[3,512,1]{2,1,0:T(8,128)} %get-tuple-element.102.lse_ref, ...), custom_call_target="tpu_custom_call" | custom-call | tf_op jit(solution)/shard_map/attention_back/pallas_call | solution.py:151
  278.8 2.6 convolution_convert_fusion.2
  281.4 2.4 convolution_convert_fusion.1
  285.9 21.8 %kv_scatter.1 = (f32[512,128]{1,0:T(8,128)}, bf16[1120,768]{1,0:T(8,128)(2,1)}) custom-call(bf16[2,2048,128]{2,1,0:T(8,128)(2,1)} %get-tuple-element.108.part_ref, bf16[2048,1120]{1,0:T(8,128)(2,1)} %get-tuple-element.109.refs_0_, bf16[2048,1536]{1,0:T(8,128)(2,1)} %bitcast.73), custom_call_target="tpu_custom_call" | custom-call | tf_op jit(solution)/shard_map/kv_scatter/pallas_call | solution.py:642
  307.7 3.6 add_convert_fusion.1
  315.5 4.9 %qkv_back.1 = bf16[512,1536]{1,0:T(8,128)(2,1)} custom-call(s32[4]{0:T(128)} %pad_add_fusion.1.meta_ref, bf16[512,384]{1,0:T(8,128)(2,1)} %get-tuple-element.103.dq_ref, bf16[512,128]{1,0:T(8,128)(2,1)} %copy-done.4, bf16[768,384]{1,0:T(8,128)(2,1)} %refs_0_.3, bf16[768,384]{1,0:T(8,128)(2,1)} %collective-permute-done.3.refs_1_, ...), custom_call_target="tpu_custom_call" | custom-call | tf_op jit(solution)/shard_map/qkv_back/pallas_call | solution.py:242
  320.5 2.4 add_convert_fusion
  325.1 27.6 %input_back.1 = (f32[1,5120]{1,0:T(1,128)}, bf16[4,128,1536]{2,1,0:T(8,128)(2,1)}) custom-call(bf16[4,128,1536]{2,1,0:T(8,128)(2,1)} %bitcast.78, bf16[128,1536]{1,0:T(8,128)(2,1)} %constant_dynamic-slice_fusion.5.x_ref, f32[128,1]{1,0:T(8,128)} %constant_dynamic-slice_fusion.4.factor_ref, f32[1,1536]{1,0:T(1,128)} %bitcast.88, ...), custom_call_target="tpu_custom_call" | custom-call | tf_op jit(solution)/shard_map/input_back/pallas_call | solution.py:642
  352.7 2.7 fusion.3.refs_1_
  355.5 4.8 %fusion.1 = f32[2240,768]{1,0:T(8,128)} fusion(bf16[1120,768]{1,0:T(8,128)(2,1)} %collective-permute-done.12, bf16[1120,768]{1,0:T(8,128)(2,1)S(1)} %add_convert_fusion.2, pred[]{:T(512)S(6)} %eq.19), kind=kLoop, calls=%fused_computation.5 | loop fusion | flops 17203200 | bytes 10321921 | tf_op jit(solution)/shard_map/convert_element_type | solution.py:1241
  360.3 2.5 fusion.2.refs_0_
  362.8 2.0 fusion.4.refs_2_
  364.9 5.3 %fusion = f32[2240,768]{1,0:T(8,128)} fusion(bf16[1120,768]{1,0:T(8,128)(2,1)} %collective-permute-done.17, bf16[1120,768]{1,0:T(8,128)(2,1)} %add_convert_fusion.1, pred[]{:T(512)S(6)} %eq.19), kind=kLoop, calls=%fused_computation.3 | loop fusion | flops 17203200 | bytes 10321921 | tf_op jit(solution)/shard_map/convert_element_type | solution.py:1241
  370.1 20.8 %collective-permute-done.16 = bf16[1120,768]{1,0:T(8,128)(2,1)} collective-permute-done((bf16[1120,768]{1,0:T(8,128)(2,1)S(1)}, bf16[1120,768]{1,0:T(8,128)(2,1)}, u32[]{:S(2)}, u32[]{:S(2)}) %collective-permute-start.16) | collective-permute-done | bytes 1720352 | tf_op jit(solution)/shard_map/ppermute | solution.py:1084
  390.9 69.8 %context_sum.1 = (f32[384,768]{1,0:T(8,128)}, f32[768,384]{1,0:T(8,128)}, f32[1,5120]{1,0:T(1,128)}, bf16[4,768,128]{2,1,0:T(8,128)(2,1)}, bf16[4,128,1536]{2,1,0:T(8,128)(2,1)}) custom-call(bf16[384,768]{1,0:T(8,128)(2,1)} %fusion.2.refs_0_, bf16[768,384]{1,0:T(8,128)(2,1)} %fusion.3.refs_1_, bf16[768,128]{1,0:T(8,128)(2,1)} %fusion.4.refs_2_, ...), custom_call_target="tpu_custom_call" | custom-call | tf_op jit(solution)/shard_map/context_sum/pallas_call | solution.py:642
  467.2 4.8 convert_bitcast_fusion
  (148 shorter events, 54.9 us)
Async XLA Ops:
  0.6 21.4 %copy-start = (bf16[2240,768]{1,0:T(8,128)(2,1)S(1)}, bf16[2240,768]{1,0:T(8,128)(2,1)}, u32[]{:S(2)}) copy-start(bf16[2240,768]{1,0:T(8,128)(2,1)} %param.29) | copy-start | bytes 10321924
  2.6 33.2 %collective-permute-start.2 = (bf16[128,1536]{1,0:T(8,128)(2,1)}, bf16[128,1536]{1,0:T(8,128)(2,1)}, u32[]{:S(2)}, u32[]{:S(2)}) collective-permute-start(bf16[128,1536]{1,0:T(8,128)(2,1)} %constant_dynamic-slice_fusion.9.dy_ref), channel_id=1, source_target_pairs={{0,8},{4,12},{8,0},{12,4},{1,9},{5,13},{9,1},{13,5},{2,10},{6,14},... | collective-permute-start | bytes 1179656 | tf_op jit(solution)/shard_map/ppermute | solution.py:1084
  6.6 29.2 %collective-permute-start.1 = (bf16[128,1536]{1,0:T(8,128)(2,1)}, bf16[128,1536]{1,0:T(8,128)(2,1)}, u32[]{:S(2)}, u32[]{:S(2)}) collective-permute-start(bf16[128,1536]{1,0:T(8,128)(2,1)} %constant_dynamic-slice_fusion.9.dy_ref), channel_id=1, source_target_pairs={{0,4},{4,0},{8,12},{12,8},{1,5},{5,1},{9,13},{13,9},{2,6},{6,2},{1... | collective-permute-start | bytes 1179656 | tf_op jit(solution)/shard_map/ppermute | solution.py:1084
  11.9 16.7 %collective-permute-start = (bf16[1,1984]{1,0:T(2,128)(2,1)S(1)}, bf16[1,1984]{1,0:T(2,128)(2,1)S(1)}, u32[]{:S(2)}, u32[]{:S(2)}) collective-permute-start(bf16[1,1984]{1,0:T(2,128)(2,1)S(1)} %concatenate.64), channel_id=1, source_target_pairs={{0,16},{16,0},{1,17},{17,1},{2,18},{18,2},{3,19},{19,3},{4,20},{20... | collective-permute-start | bytes 11912 | tf_op jit(solution)/shard_map/ppermute | solution.py:1084
  15.2 13.7 %collective-permute-start.4 = (bf16[768,128]{1,0:T(8,128)(2,1)}, bf16[768,128]{1,0:T(8,128)(2,1)}, u32[]{:S(2)}, u32[]{:S(2)}) collective-permute-start(bf16[768,128]{1,0:T(8,128)(2,1)} %dynamic-slice_select_fusion.refs_2_), channel_id=1, source_target_pairs={{0,16},{16,0},{1,17},{17,1},{2,18},{18,2},{3,19},{19,3},{4,20},{20... | collective-permute-start | bytes 589832 | tf_op jit(solution)/shard_map/ppermute | solution.py:1084
  15.7 18.2 %collective-permute-start.3 = (bf16[768,384]{1,0:T(8,128)(2,1)}, bf16[768,384]{1,0:T(8,128)(2,1)}, u32[]{:S(2)}, u32[]{:S(2)}) collective-permute-start(bf16[768,384]{1,0:T(8,128)(2,1)} %refs_0_.3), channel_id=1, source_target_pairs={{0,16},{16,0},{1,17},{17,1},{2,18},{18,2},{3,19},{19,3},{4,20},{20... | collective-permute-start | bytes 1769480 | tf_op jit(solution)/shard_map/ppermute | solution.py:1084
  22.0 4.7 copy-start.6
  22.0 4.7 copy-start.8
  26.7 23.4 %copy-start.2 = (bf16[2240,768]{1,0:T(8,128)(2,1)}, bf16[2240,768]{1,0:T(8,128)(2,1)S(1)}, u32[]{:S(2)}) copy-start(bf16[2240,768]{1,0:T(8,128)(2,1)S(1)} %pad_maximum_fusion.refs_0_.refs_2_) | copy-start | bytes 10321924
  33.9 13.6 %collective-permute-start.5 = (bf16[384,768]{1,0:T(8,128)(2,1)}, bf16[384,768]{1,0:T(8,128)(2,1)}, u32[]{:S(2)}, u32[]{:S(2)}) collective-permute-start(bf16[384,768]{1,0:T(8,128)(2,1)} %param.25), channel_id=1, source_target_pairs={{0,16},{16,0},{1,17},{17,1},{2,18},{18,2},{3,19},{19,3},{4,20},{20... | collective-permute-start | bytes 1769480 | tf_op jit(solution)/shard_map/ppermute | solution.py:1084
  35.9 11.7 %copy-start.22 = (bf16[384,768]{1,0:T(8,128)(2,1)S(1)}, bf16[384,768]{1,0:T(8,128)(2,1)}, u32[]{:S(2)}) copy-start(bf16[384,768]{1,0:T(8,128)(2,1)} %param.25) | copy-start | bytes 1769476
  50.1 95.9 %collective-permute-start.7 = (bf16[2240,768]{1,0:T(8,128)(2,1)S(1)}, bf16[2240,768]{1,0:T(8,128)(2,1)}, u32[]{:S(2)}, u32[]{:S(2)}) collective-permute-start(bf16[2240,768]{1,0:T(8,128)(2,1)S(1)} %pad_maximum_fusion.refs_0_.refs_2_), channel_id=1, source_target_pairs={{0,16},{16,0},{1,17},{17,1},{2,18},{18,2},{3,19},{19,3},{4,20},{20... | collective-permute-start | bytes 10321928 | tf_op jit(solution)/shard_map/ppermute | solution.py:1084
  50.6 32.8 %collective-permute-start.6 = (bf16[128,1536]{1,0:T(8,128)(2,1)}, bf16[128,1536]{1,0:T(8,128)(2,1)}, u32[]{:S(2)}, u32[]{:S(2)}) collective-permute-start(bf16[128,1536]{1,0:T(8,128)(2,1)} %constant_dynamic-slice_fusion.9.dy_ref), channel_id=1, source_target_pairs={{0,2},{1,3},{2,0},{3,1},{4,6},{5,7},{6,4},{7,5},{8,10},{9,11},{10,... | collective-permute-start | bytes 1179656 | tf_op jit(solution)/shard_map/ppermute | solution.py:1084
  68.2 108.4 %collective-permute-start.8 = (bf16[1120,768]{1,0:T(8,128)(2,1)}, bf16[1120,768]{1,0:T(8,128)(2,1)}, u32[]{:S(2)}, u32[]{:S(2)}) collective-permute-start(bf16[1120,768]{1,0:T(8,128)(2,1)} %constant_dynamic-slice_fusion.6.refs_4_), channel_id=1, source_target_pairs={{0,16},{16,0},{1,17},{17,1},{2,18},{18,2},{3,19},{19,3},{4,20},{20... | collective-permute-start | bytes 5160968 | tf_op jit(solution)/shard_map/ppermute | solution.py:1084
  175.8 78.2 %collective-permute-start.9 = (bf16[1120,768]{1,0:T(8,128)(2,1)}, bf16[1120,768]{1,0:T(8,128)(2,1)S(1)}, u32[]{:S(2)}, u32[]{:S(2)}) collective-permute-start(bf16[1120,768]{1,0:T(8,128)(2,1)} %get-tuple-element.99), channel_id=1, source_target_pairs={{0,16},{16,0},{1,17},{17,1},{2,18},{18,2},{3,19},{19,3},{4,20},{20... | collective-permute-start | bytes 5160968 | tf_op jit(solution)/shard_map/ppermute | solution.py:1084
  218.6 67.3 %collective-permute-start.11 = (bf16[1120,768]{1,0:T(8,128)(2,1)}, bf16[1120,768]{1,0:T(8,128)(2,1)}, u32[]{:S(2)}, u32[]{:S(2)}) collective-permute-start(bf16[1120,768]{1,0:T(8,128)(2,1)} %get-tuple-element.106), channel_id=1, source_target_pairs={{0,16},{16,0},{1,17},{17,1},{2,18},{18,2},{3,19},{19,3},{4,20},{20... | collective-permute-start | bytes 5160968 | tf_op jit(solution)/shard_map/ppermute | solution.py:1084
  255.2 5.3 %copy-start.3 = (bf16[384,1536]{1,0:T(8,128)(2,1)S(1)}, bf16[384,1536]{1,0:T(8,128)(2,1)}, u32[]{:S(2)}) copy-start(bf16[384,1536]{1,0:T(8,128)(2,1)} %maximum_select_fusion.3) | copy-start | bytes 3538948
  257.7 50.0 %collective-permute-start.12 = (bf16[1120,768]{1,0:T(8,128)(2,1)S(1)}, bf16[1120,768]{1,0:T(8,128)(2,1)}, u32[]{:S(2)}, u32[]{:S(2)}) collective-permute-start(bf16[1120,768]{1,0:T(8,128)(2,1)S(1)} %add_convert_fusion.2), channel_id=1, source_target_pairs={{0,4},{4,0},{8,12},{12,8},{1,5},{5,1},{9,13},{13,9},{2,6},{6,2},{1... | collective-permute-start | bytes 5160968 | tf_op jit(solution)/shard_map/ppermute | solution.py:1084
  259.8 60.7 %collective-permute-start.13 = (bf16[1120,768]{1,0:T(8,128)(2,1)}, bf16[1120,768]{1,0:T(8,128)(2,1)}, u32[]{:S(2)}, u32[]{:S(2)}) collective-permute-start(bf16[1120,768]{1,0:T(8,128)(2,1)} %get-tuple-element.116), channel_id=1, source_target_pairs={{0,16},{16,0},{1,17},{17,1},{2,18},{18,2},{3,19},{19,3},{4,20},{20... | collective-permute-start | bytes 5160968 | tf_op jit(solution)/shard_map/ppermute | solution.py:1084
  263.7 15.1 %copy-start.23 = (bf16[512,384]{1,0:T(8,128)(2,1)S(1)}, bf16[512,384]{1,0:T(8,128)(2,1)}, u32[]{:S(2)}) copy-start(bf16[512,384]{1,0:T(8,128)(2,1)} %get-tuple-element.85) | copy-start | bytes 1179652
  283.9 68.9 %collective-permute-start.14 = (bf16[768,384]{1,0:T(8,128)(2,1)}, bf16[768,384]{1,0:T(8,128)(2,1)}, u32[]{:S(2)}, u32[]{:S(2)}) collective-permute-start(bf16[768,384]{1,0:T(8,128)(2,1)} %convolution_convert_fusion.1), channel_id=1, source_target_pairs={{0,16},{16,0},{1,17},{17,1},{2,18},{18,2},{3,19},{19,3},{4,20},{20... | collective-permute-start | bytes 1769480 | tf_op jit(solution)/shard_map/ppermute | solution.py:1084
  285.1 70.4 %collective-permute-start.10 = (bf16[384,768]{1,0:T(8,128)(2,1)}, bf16[384,768]{1,0:T(8,128)(2,1)}, u32[]{:S(2)}, u32[]{:S(2)}) collective-permute-start(bf16[384,768]{1,0:T(8,128)(2,1)} %convolution_convert_fusion.2), channel_id=1, source_target_pairs={{0,16},{16,0},{1,17},{17,1},{2,18},{18,2},{3,19},{19,3},{4,20},{20... | collective-permute-start | bytes 1769480 | tf_op jit(solution)/shard_map/ppermute | solution.py:1084
  307.7 3.7 copy-start.7
  311.5 3.8 copy-start.16
  314.0 48.8 %collective-permute-start.15 = (bf16[768,128]{1,0:T(8,128)(2,1)}, bf16[768,128]{1,0:T(8,128)(2,1)}, u32[]{:S(2)}, u32[]{:S(2)}) collective-permute-start(bf16[768,128]{1,0:T(8,128)(2,1)} %convolution_convert_fusion.4), channel_id=1, source_target_pairs={{0,16},{16,0},{1,17},{17,1},{2,18},{18,2},{3,19},{19,3},{4,20},{20... | collective-permute-start | bytes 589832 | tf_op jit(solution)/shard_map/ppermute | solution.py:1084
  314.8 50.1 %collective-permute-start.17 = (bf16[1120,768]{1,0:T(8,128)(2,1)}, bf16[1120,768]{1,0:T(8,128)(2,1)}, u32[]{:S(2)}, u32[]{:S(2)}) collective-permute-start(bf16[1120,768]{1,0:T(8,128)(2,1)} %add_convert_fusion.1), channel_id=1, source_target_pairs={{0,4},{4,0},{8,12},{12,8},{1,5},{5,1},{9,13},{13,9},{2,6},{6,2},{1... | collective-permute-start | bytes 5160968 | tf_op jit(solution)/shard_map/ppermute | solution.py:1084
  320.4 4.0 copy-start.25
  322.9 29.9 %copy-start.17 = (bf16[512,384]{1,0:T(8,128)(2,1)S(1)}, bf16[512,384]{1,0:T(8,128)(2,1)}, u32[]{:S(2)}) copy-start(bf16[512,384]{1,0:T(8,128)(2,1)} %get-tuple-element.103.dq_ref) | copy-start | bytes 1179652
  322.9 68.0 %collective-permute-start.16 = (bf16[1120,768]{1,0:T(8,128)(2,1)S(1)}, bf16[1120,768]{1,0:T(8,128)(2,1)}, u32[]{:S(2)}, u32[]{:S(2)}) collective-permute-start(bf16[1120,768]{1,0:T(8,128)(2,1)S(1)} %add_convert_fusion), channel_id=1, source_target_pairs={{0,4},{4,0},{8,12},{12,8},{1,5},{5,1},{9,13},{13,9},{2,6},{6,2},{1... | collective-permute-start | bytes 5160968 | tf_op jit(solution)/shard_map/ppermute | solution.py:1084
  355.5 4.8 %copy-start.24 = (bf16[512,384]{1,0:T(8,128)(2,1)S(1)}, bf16[512,384]{1,0:T(8,128)(2,1)}, u32[]{:S(2)}) copy-start(bf16[512,384]{1,0:T(8,128)(2,1)} %get-tuple-element.85) | copy-start | bytes 1179652
  355.5 4.8 %copy-start.26 = (bf16[4,128,1536]{2,1,0:T(8,128)(2,1)S(1)}, bf16[4,128,1536]{2,1,0:T(8,128)(2,1)}, u32[]{:S(2)}) copy-start(bf16[4,128,1536]{2,1,0:T(8,128)(2,1)} %get-tuple-element.97) | copy-start | bytes 4718596
  467.2 4.8 %copy-start.12 = (bf16[4,128,1536]{2,1,0:T(8,128)(2,1)S(1)}, bf16[4,128,1536]{2,1,0:T(8,128)(2,1)}, u32[]{:S(2)}) copy-start(bf16[4,128,1536]{2,1,0:T(8,128)(2,1)} %get-tuple-element.132) | copy-start | bytes 4718596
  (13 other events, 28.9 us)

commit v13 on v12

--- a/solution.py
+++ b/solution.py
@@ -843,8 +843,11 @@
 
 
 def middle_back_kernel(count, part, mid_ref, factor_ref, gain_ref, dy_ref, *refs):
-    args, (dmid_ref, dgain_ref, out) = refs[: 2 * count], refs[2 * count : 2 * count + 3]
-    outs, refs = refs[2 * count + 3 : 3 * count + 3], refs[3 * count + 3 :]
+    args, refs = refs[: 2 * count], refs[2 * count :]
+    got_ref, refs = (refs[0], refs[1:]) if count else (None, refs)
+    (dmid_ref, dgain_ref, out), refs = refs[:3], refs[3:]
+    outs, refs = refs[:count], refs[count:]
+    (low_ref, half_ref), refs = (refs[:2], refs[2:]) if count else ((None, None), refs)
     low, first, wires, to = refs[0], refs[1:8], Wires(*refs[-3:]), partners()
     fill = own_grads(count, args, outs, refs[8:-3])
     meet([to[k] for k in ("core", "y", "z")])
@@ -858,6 +861,8 @@
     next(back)
     if fill:
         fill[0].make(1, fill[0].tiles)
+        low_ref[...] = (wide(outs[0][...]) + wide(got_ref[...])).astype(bf16)
+        near_half = wires.copy(low_ref.at[pl.ds(0, half_ref.shape[0])], half_ref, to["z"])
     grad_normed = result_of(back)
     du, dgain = norm_back_rows(mid_ref[...], factor_ref[...], gain_ref[...], grad_normed)
     dgain_ref[...] = dgain
@@ -869,6 +874,8 @@
     for one in fill[1:]:
         one.make(0, one.tiles)
     result_of(share)
+    if fill:
+        near_half.wait_recv()
     wires.finish()
 
 
@@ -884,9 +891,13 @@
     ]
 
 
-def middle_back(part, middle, factor, gain, dy_part, fill, shard):
+def middle_back(part, middle, factor, gain, dy_part, fill, got, shard):
     rows, width = middle.shape
     args, outs, scratch = own_grad_call(fill, shard)
+    if fill:
+        args = [*args, got]
+        units = got.shape[0]
+        outs = [*outs, *(jax.ShapeDtypeStruct((n, shard), bf16) for n in (units, units // 2))]
     return remote_call(
         functools.partial(middle_back_kernel, len(fill)),
         "middle_back",
@@ -901,8 +912,8 @@
         [pltpu.VMEM((rows, width), bf16)] + pair_scratch(rows, width) + scratch,
         16,
         (
-            [False, True, True, True, True] + [False] * len(args),
-            [True, True, False] + [True] * len(outs),
+            [False] + [True] * 4 + ([False] * (len(args) - 1) + [True] if fill else []),
+            [True, True, False] + ([True] * (len(outs) - 1) + [False] if fill else []),
         ),
     )
 
@@ -1234,29 +1245,37 @@
             down_got = gate_got = up_got = jnp.zeros_like(owns[0])
             early = later = []
 
-        def unit_done(own, got):
-            low = (own.astype(f32) + got.astype(f32)).astype(bf16)
-            return low, flip(low, "context", 1)
-
-        unit_whole = lambda low, other: by_bit(parity, low, other, 0).astype(f32)
+        unit_whole = lambda low, *other: by_bit(
+            parity, low, jnp.concatenate(other, axis=0), 0
+        ).astype(f32)
 
         grad_middle, ffn_gain_grad, grad_middle_low, *first_owns = middle_back(
-            dx_part, middle, factor_second, gain_second, dy_part, early, width // n_f
+            dx_part, middle, factor_second, gain_second, dy_part, early, down_got, width // n_f
         )
         grad_middle_low = grad_middle_low.reshape(rows, width)
-        down_own, gate_own = first_owns or owns[:2]
-        down_done = unit_done(down_own, after(down_got, grad_middle_low))
-        grad_attended = dot_cols(after(grad_middle_low, down_done[0]), w_out_all).astype(bf16)
+        add = lambda own, got: (own.astype(f32) + got.astype(f32)).astype(bf16)
+        upper = units // 2
+        if n_f == 2:
+            _, gate_own, down_low, down_upper = first_owns
+        else:
+            down_low, gate_own = owns[:2]
+            down_upper = flip(down_low[:upper], "context", 1)
+        gate_low = add(gate_own, after(gate_got, grad_middle_low))
+        down_lower = flip(down_low[upper:], "context", 1)
+        gate_upper = flip(after(gate_low[:upper], down_low), "context", 1)
+        grad_middle_low = after(grad_middle_low, gate_low)
+        grad_attended = dot_cols(grad_middle_low, w_out_all).astype(bf16)
 
         dq_low, dkv = attention_back(key_blocks, queries, grad_attended, lse, cosine, sine, kv)
         attention_args = [(attended, after(grad_middle_low, dq_low), 1), (normed, dq_low, 0)]
         fars = [grad_far(*args) for args in attention_args]
         dkv, *last_owns = kv_scatter(
-            after(dkv, gate_got, fars), later, width // n_f
+            after(dkv, fars, down_lower, gate_upper), later, width // n_f
         )
         (up_own,) = last_owns or owns[2:]
-        gate_done = unit_done(gate_own, after(gate_got, dkv, down_done))
-        dkv = after(dkv, gate_done[0])
+        gate_lower = flip(after(gate_low[upper:], dkv, gate_upper), "context", 1)
+        up_low = add(up_own, after(up_got, dkv))
+        dkv = after(dkv, up_low, gate_upper)
         dkv_low = jnp.where(core == 0, rotate_back(dkv, cosine, sine), dkv).astype(bf16)
         attention_args.append((normed, dkv_low, 0))
         fars.append(grad_far(*attention_args[-1]))
@@ -1272,9 +1291,10 @@
             [jnp.zeros((1, width), f32), ffn_gain_grad, slots.reshape(1, -1)], axis=1
         )
         grad_qkv = qkv_back(meta, dq_low, dkv_low, w_q, w_kv)
-        up_done = unit_done(up_own, after(up_got, grad_qkv))
+        up_upper = flip(after(up_low[:upper], dkv_low), "context", 1)
+        up_lower = flip(after(up_low[upper:], grad_qkv), "context", 1)
         small_grads, input_grad = input_back(
-            after(grad_qkv, up_done[0]),
+            grad_qkv,
             inputs_part,
             factor_part,
             gain_first,
@@ -1284,13 +1304,14 @@
         input_grad = input_grad.reshape(rows, width)
         if n_f > 2:
             small_grads = lax.psum(small_grads, "fsdp")
+        small_grads = after(small_grads, gate_lower, up_upper)
         attention_parts = [
             grad_sum(*args, far, small_grads) for args, far in zip(attention_args, fars)
         ]
-        wd_grad = unit_whole(*after(down_done, small_grads))
-        wg_grad = unit_whole(*after(gate_done, small_grads))
-        small_grads, up_done, wg_grad, wd_grad = lax.optimization_barrier(
-            (small_grads, up_done, wg_grad, wd_grad)
+        wd_grad = unit_whole(*after((down_low, down_upper, down_lower), small_grads))
+        wg_grad = unit_whole(*after((gate_low, gate_upper, gate_lower), small_grads))
+        small_grads, up_lower, wg_grad, wd_grad = lax.optimization_barrier(
+            (small_grads, up_lower, wg_grad, wd_grad)
         )
         wo_grad, wq_grad, packed, wkv_all, outputs = context_sum(
             n_f == 2, attention_parts, small_grads, out_part, middle
@@ -1308,7 +1329,7 @@
         bk_out = slots[0::2, heads]
         bv_out = slots[1::2, heads]
 
-        wu_grad = unit_whole(*up_done)
+        wu_grad = unit_whole(up_low, up_upper, up_lower)
         wg_grad, wu_grad = wg_grad.T, wu_grad.T
 
         return (

time: 483 us -> 481 us (level)
  other arithmetic: 37.7 us -> 32.7 us
    slice x0 -> x3, local copies, waits for them, and re-layouts: none -> 5.38 us  [the longest x1 2.78 us: local(): down_lower = flip(down_low[upper:], 'context', 1)]
    convert_element_type x5 -> x4, other arithmetic: 18.6 us -> 13.5 us  [the longest x2 9.17 us: local(): unit_whole = lambda low, *other: by_bit(parity, low, jnp.concatenate(othe...]
    ppermute x18 -> x20, waiting for transfers between devices: 31.1 us -> 26.3 us  [flip(): return lax.ppermute(x, axis, [(i, i ^ bit) for i in range(size)])]
    unnamed x63 -> x73, local copies, waits for them, and re-layouts: 12.3 us -> 9.75 us
    ppermute x18 -> x20, starting transfers between devices: 21.7 us -> 23.6 us  [flip(): return lax.ppermute(x, axis, [(i, i ^ bit) for i in range(size)])]
  transfers between devices with their start and end apart: 18 -> 20, of which waited for: 3 -> 5; matrix products, arithmetic and copies ran while one was open for 12% -> 12% of each run, Pallas kernels for 56% -> 57%
where the time goes in v13:
time: 481 us; the launch traced here: 477 us
  Pallas kernels  343 us (71%)
  other arithmetic  32.7 us (7%)
  local copies, waits for them, and re-layouts  30.9 us (6%)
  waiting for transfers between devices  26.3 us (5%)
  starting transfers between devices  23.6 us (5%)
  matrix products  18.4 us (4%)
    pallas_call x6, Pallas kernels, remote_call(): pl.pallas_call(kernel, name=name, out_shape=outs, in_specs=[spec(x) for x...  235 us
    pallas_call x2, Pallas kernels, hidden_call(): pl.pallas_call(kernel, name=name, grid_spec=pltpu.PrefetchScalarGridSpec(...  71.8 us
    ppermute x20, waiting for transfers between devices, flip(): return lax.ppermute(x, axis, [(i, i ^ bit) for i in range(size)])  26.3 us
    ppermute x20, starting transfers between devices, flip(): return lax.ppermute(x, axis, [(i, i ^ bit) for i in range(size)])  23.6 us
    pallas_call x1, Pallas kernels, attention_back(): pl.pallas_call(functools.partial(attention_back_kernel, kv.shape[1] // BL...  15.1 us
    dot_general x6, matrix products, dot_rows(): lax.dot_general(left, right, (((0,), (0,)), ((), ())), preferred_element_...  13.1 us
    pallas_call x1, Pallas kernels, attention(): pl.pallas_call(functools.partial(attention_kernel, kv.shape[1] // BLOCK),...  10.2 us
    unnamed x73, local copies, waits for them, and re-layouts  9.75 us
  transfers between devices with their start and end apart: 20, of which 5 were waited for; matrix products, arithmetic and copies ran while one was open for 12% of the time, Pallas kernels for 57%

profile of v13, /device:TPU:0, one launch (start us, length us, event | category | flops | bytes accessed | tf_op | source)
XLA Modules:
  0.0 476.6 jit_solution(8486767205670427887)
XLA Ops:
  0.7 1.9 constant_dynamic-slice_fusion.9.dy_ref
  2.6 4.0 collective-permute-start.2
  27.5 6.4 %collective-permute-done.3.refs_1_ = bf16[768,384]{1,0:T(8,128)(2,1)} collective-permute-done((bf16[768,384]{1,0:T(8,128)(2,1)}, bf16[768,384]{1,0:T(8,128)(2,1)}, u32[]{:S(2)}, u32[]{:S(2)}) %collective-permute-start.3) | collective-permute-done | bytes 589856 | tf_op jit(solution)/shard_map/ppermute | solution.py:1095
  35.8 6.3 %qkv.1 = (bf16[512,1536]{1,0:T(8,128)(2,1)}, f32[512,1]{1,0:T(8,128)}, bf16[512,384]{1,0:T(8,128)(2,1)}, bf16[512,128]{1,0:T(8,128)(2,1)}) custom-call(s32[4]{0:T(128)} %pad_add_fusion.1.meta_ref, bf16[512,1536]{1,0:T(8,128)(2,1)} %x_ref.1, f32[1,1536]{1,0:T(1,128)} %bitcast.87, f32[1,512]{1,0:T(1,128)} %pad_maximum_fusion.6.bias_ref, ...), custom_call_target="tpu_custom_call" | custom-call | tf_op jit(solution)/shard_map/qkv/pallas_call | solution.py:209
  42.2 5.4 %collective-permute-done.5 = bf16[384,768]{1,0:T(8,128)(2,1)} collective-permute-done((bf16[384,768]{1,0:T(8,128)(2,1)}, bf16[384,768]{1,0:T(8,128)(2,1)}, u32[]{:S(2)}, u32[]{:S(2)}) %collective-permute-start.5) | collective-permute-done | bytes 589856 | tf_op jit(solution)/shard_map/ppermute | solution.py:1095
  47.5 2.5 maximum_select_fusion.3
  50.6 15.0 %kv_gather.1.k_ref.v_ref = bf16[2,2048,128]{2,1,0:T(8,128)(2,1)} custom-call(bf16[512,128]{1,0:T(8,128)(2,1)} %get-tuple-element.89.own_ref), custom_call_target="tpu_custom_call" | custom-call | tf_op jit(solution)/shard_map/kv_gather/pallas_call | solution.py:642
  69.8 10.2 %attention.1 = (bf16[512,384]{1,0:T(8,128)(2,1)}, f32[3,512,1]{2,1,0:T(8,128)}) custom-call(s32[8]{0:T(128)} %pad_add_fusion.kb_ref, bf16[512,384]{1,0:T(8,128)(2,1)} %get-tuple-element.86.q_ref, bf16[2,2048,128]{2,1,0:T(8,128)(2,1)} %kv_gather.1.k_ref.v_ref, bf16[2,2048,128]{2,1,0:T(8,128)(2,1)} %kv_gather.1.k_ref.v_ref), custom_call_target="tpu_custom_call" | custom-call | tf_op jit(solution)/shard_map/attention/pallas_call | solution.py:85
  79.9 3.5 convolution_convert_fusion
  83.4 62.5 %middle_norm.1 = (f32[128,1536]{1,0:T(8,128)}, f32[128,1]{1,0:T(8,128)}, bf16[16,128,1536]{2,1,0:T(8,128)(2,1)}, bf16[16,128,1536]{2,1,0:T(8,128)(2,1)}) custom-call(bf16[4,128,1536]{2,1,0:T(8,128)(2,1)} %bitcast.79, bf16[128,1536]{1,0:T(8,128)(2,1)} %constant_dynamic-slice_fusion.5.x_ref, f32[1,1536]{1,0:T(1,128)} %bitcast.89, ...), custom_call_target="tpu_custom_call" | custom-call | tf_op jit(solution)/shard_map/middle_norm/pallas_call | solution.py:642
  146.0 29.7 %hidden_units.1 = (bf16[2048,1120]{1,0:T(8,128)(2,1)}, bf16[2048,1120]{1,0:T(8,128)(2,1)}, bf16[2048,1120]{1,0:T(8,128)(2,1)}, bf16[1120,768]{1,0:T(8,128)(2,1)}) custom-call(s32[4]{0:T(128)} %pad_add_fusion.1.meta_ref, bf16[2048,1536]{1,0:T(8,128)(2,1)} %bitcast.70, bf16[2048,1536]{1,0:T(8,128)(2,1)} %bitcast.74, bf16[2240,768]{1,0:T(8,128)(2,1)} %copy-done.2, ...), custom_call_target="tpu_custom_call" | custom-call | tf_op jit(solution)/shard_map/hidden_units/pallas_call | solution.py:333
  176.5 42.0 %hidden_back.1 = (bf16[2048,1120]{1,0:T(8,128)(2,1)}, bf16[2048,1120]{1,0:T(8,128)(2,1)}, bf16[1024,1536]{1,0:T(8,128)(2,1)}, bf16[1024,1536]{1,0:T(8,128)(2,1)}...) custom-call(s32[4]{0:T(128)} %pad_add_fusion.1.meta_ref, bf16[2048,1536]{1,0:T(8,128)(2,1)} %bitcast.71, ...), custom_call_target="tpu_custom_call" | custom-call | tf_op jit(solution)/shard_map/hidden_back/pallas_call | solution.py:333
  221.8 40.9 %middle_back.1 = (f32[128,1536]{1,0:T(8,128)}, f32[1,1536]{1,0:T(1,128)}, bf16[4,128,1536]{2,1,0:T(8,128)(2,1)}, bf16[1120,768]{1,0:T(8,128)(2,1)}, bf16[1120,76...) custom-call(bf16[8,128,1536]{2,1,0:T(8,128)(2,1)} %bitcast.80, ...), custom_call_target="tpu_custom_call" | custom-call | tf_op jit(solution)/shard_map/middle_back/pallas_call | solution.py:642
  262.7 2.8 slice.69
  274.0 15.1 %attention_back.1 = (bf16[512,384]{1,0:T(8,128)(2,1)}, bf16[2,2048,128]{2,1,0:T(8,128)(2,1)}) custom-call(s32[8]{0:T(128)} %pad_add_fusion.kb_ref, bf16[512,384]{1,0:T(8,128)(2,1)} %get-tuple-element.86.q_ref, bf16[512,384]{1,0:T(8,128)(2,1)} %convolution_convert_fusion.3.do_ref, f32[3,512,1]{2,1,0:T(8,128)} %get-tuple-element.108.lse_ref, ...), custom_call_target="tpu_custom_call" | custom-call | tf_op jit(solution)/shard_map/attention_back/pallas_call | solution.py:151
  289.1 2.4 convolution_convert_fusion.1
  292.7 2.4 convolution_convert_fusion.2
  296.0 9.2 %collective-permute-done.13 = bf16[560,768]{1,0:T(8,128)(2,1)} collective-permute-done((bf16[560,768]{1,0:T(8,128)(2,1)}, bf16[560,768]{1,0:T(8,128)(2,1)}, u32[]{:S(2)}, u32[]{:S(2)}) %collective-permute-start.13) | collective-permute-done | bytes 860192 | tf_op jit(solution)/shard_map/ppermute | solution.py:1095
  305.2 18.2 %kv_scatter.1 = (f32[512,128]{1,0:T(8,128)}, bf16[1120,768]{1,0:T(8,128)(2,1)}) custom-call(bf16[2,2048,128]{2,1,0:T(8,128)(2,1)} %get-tuple-element.115.part_ref, bf16[2048,1120]{1,0:T(8,128)(2,1)} %get-tuple-element.116.refs_0_, bf16[2048,1536]{1,0:T(8,128)(2,1)} %bitcast.73), custom_call_target="tpu_custom_call" | custom-call | tf_op jit(solution)/shard_map/kv_scatter/pallas_call | solution.py:642
  323.5 2.5 add_convert_fusion
  331.3 2.0 collective-permute-start.16
  333.9 5.1 %qkv_back.1 = bf16[512,1536]{1,0:T(8,128)(2,1)} custom-call(s32[4]{0:T(128)} %pad_add_fusion.1.meta_ref, bf16[512,384]{1,0:T(8,128)(2,1)} %get-tuple-element.109.dq_ref, bf16[512,128]{1,0:T(8,128)(2,1)} %copy-done.5, bf16[768,384]{1,0:T(8,128)(2,1)} %refs_0_.3, bf16[768,384]{1,0:T(8,128)(2,1)} %collective-permute-done.3.refs_1_, ...), custom_call_target="tpu_custom_call" | custom-call | tf_op jit(solution)/shard_map/qkv_back/pallas_call | solution.py:242
  339.0 28.6 %input_back.1 = (f32[1,5120]{1,0:T(1,128)}, bf16[4,128,1536]{2,1,0:T(8,128)(2,1)}) custom-call(bf16[4,128,1536]{2,1,0:T(8,128)(2,1)} %bitcast.78, bf16[128,1536]{1,0:T(8,128)(2,1)} %constant_dynamic-slice_fusion.5.x_ref, f32[128,1]{1,0:T(8,128)} %constant_dynamic-slice_fusion.4.factor_ref, f32[1,1536]{1,0:T(1,128)} %bitcast.88, ...), custom_call_target="tpu_custom_call" | custom-call | tf_op jit(solution)/shard_map/input_back/pallas_call | solution.py:642
  367.8 2.9 collective-permute-done.16
  370.7 2.7 fusion.3.refs_1_
  373.5 2.4 fusion.2.refs_0_
  375.9 4.8 %fusion = f32[2240,768]{1,0:T(8,128)} fusion(bf16[560,768]{1,0:T(8,128)(2,1)} %collective-permute-done.15, bf16[560,768]{1,0:T(8,128)(2,1)} %collective-permute-done.13, bf16[1120,768]{1,0:T(8,128)(2,1)S(1)} %add_convert_fusion.1, pred[]{:T(512)S(6)} %eq.19), kind=kLoop, calls=%fused_computation.3 | loop fusion | flops 24084480 | bytes 10321921 | tf_op jit(solution)/shard_map/convert_element_type | solution.py:1250
  380.7 2.0 fusion.4.refs_2_
  382.7 4.4 fusion.1
  387.1 2.4 collective-permute-done.19
  389.4 69.8 %context_sum.1 = (f32[384,768]{1,0:T(8,128)}, f32[768,384]{1,0:T(8,128)}, f32[1,5120]{1,0:T(1,128)}, bf16[4,768,128]{2,1,0:T(8,128)(2,1)}, bf16[4,128,1536]{2,1,0:T(8,128)(2,1)}) custom-call(bf16[384,768]{1,0:T(8,128)(2,1)} %fusion.2.refs_0_, bf16[768,384]{1,0:T(8,128)(2,1)} %fusion.3.refs_1_, bf16[768,128]{1,0:T(8,128)(2,1)} %fusion.4.refs_2_, ...), custom_call_target="tpu_custom_call" | custom-call | tf_op jit(solution)/shard_map/context_sum/pallas_call | solution.py:642
  465.8 4.7 convert_bitcast_fusion
  (164 shorter events, 60.4 us)
Async XLA Ops:
  0.6 21.3 %copy-start = (bf16[2240,768]{1,0:T(8,128)(2,1)S(1)}, bf16[2240,768]{1,0:T(8,128)(2,1)}, u32[]{:S(2)}) copy-start(bf16[2240,768]{1,0:T(8,128)(2,1)} %param.29) | copy-start | bytes 10321924
  2.6 33.2 %collective-permute-start.2 = (bf16[128,1536]{1,0:T(8,128)(2,1)}, bf16[128,1536]{1,0:T(8,128)(2,1)}, u32[]{:S(2)}, u32[]{:S(2)}) collective-permute-start(bf16[128,1536]{1,0:T(8,128)(2,1)} %constant_dynamic-slice_fusion.9.dy_ref), channel_id=1, source_target_pairs={{0,8},{4,12},{8,0},{12,4},{1,9},{5,13},{9,1},{13,5},{2,10},{6,14},... | collective-permute-start | bytes 1179656 | tf_op jit(solution)/shard_map/ppermute | solution.py:1095
  6.6 29.2 %collective-permute-start.1 = (bf16[128,1536]{1,0:T(8,128)(2,1)}, bf16[128,1536]{1,0:T(8,128)(2,1)}, u32[]{:S(2)}, u32[]{:S(2)}) collective-permute-start(bf16[128,1536]{1,0:T(8,128)(2,1)} %constant_dynamic-slice_fusion.9.dy_ref), channel_id=1, source_target_pairs={{0,4},{4,0},{8,12},{12,8},{1,5},{5,1},{9,13},{13,9},{2,6},{6,2},{1... | collective-permute-start | bytes 1179656 | tf_op jit(solution)/shard_map/ppermute | solution.py:1095
  11.9 15.3 %collective-permute-start = (bf16[1,1984]{1,0:T(2,128)(2,1)S(1)}, bf16[1,1984]{1,0:T(2,128)(2,1)S(1)}, u32[]{:S(2)}, u32[]{:S(2)}) collective-permute-start(bf16[1,1984]{1,0:T(2,128)(2,1)S(1)} %concatenate.73), channel_id=1, source_target_pairs={{0,16},{16,0},{1,17},{17,1},{2,18},{18,2},{3,19},{19,3},{4,20},{20... | collective-permute-start | bytes 11912 | tf_op jit(solution)/shard_map/ppermute | solution.py:1095
  15.2 12.3 %collective-permute-start.4 = (bf16[768,128]{1,0:T(8,128)(2,1)}, bf16[768,128]{1,0:T(8,128)(2,1)}, u32[]{:S(2)}, u32[]{:S(2)}) collective-permute-start(bf16[768,128]{1,0:T(8,128)(2,1)} %dynamic-slice_select_fusion.refs_2_), channel_id=1, source_target_pairs={{0,16},{16,0},{1,17},{17,1},{2,18},{18,2},{3,19},{19,3},{4,20},{20... | collective-permute-start | bytes 589832 | tf_op jit(solution)/shard_map/ppermute | solution.py:1095
  15.7 18.2 %collective-permute-start.3 = (bf16[768,384]{1,0:T(8,128)(2,1)}, bf16[768,384]{1,0:T(8,128)(2,1)}, u32[]{:S(2)}, u32[]{:S(2)}) collective-permute-start(bf16[768,384]{1,0:T(8,128)(2,1)} %refs_0_.3), channel_id=1, source_target_pairs={{0,16},{16,0},{1,17},{17,1},{2,18},{18,2},{3,19},{19,3},{4,20},{20... | collective-permute-start | bytes 1769480 | tf_op jit(solution)/shard_map/ppermute | solution.py:1095
  25.3 24.8 %copy-start.2 = (bf16[2240,768]{1,0:T(8,128)(2,1)}, bf16[2240,768]{1,0:T(8,128)(2,1)S(1)}, u32[]{:S(2)}) copy-start(bf16[2240,768]{1,0:T(8,128)(2,1)S(1)} %pad_maximum_fusion.refs_0_.refs_2_) | copy-start | bytes 10321924
  33.9 13.6 %collective-permute-start.5 = (bf16[384,768]{1,0:T(8,128)(2,1)}, bf16[384,768]{1,0:T(8,128)(2,1)}, u32[]{:S(2)}, u32[]{:S(2)}) collective-permute-start(bf16[384,768]{1,0:T(8,128)(2,1)} %param.25), channel_id=1, source_target_pairs={{0,16},{16,0},{1,17},{17,1},{2,18},{18,2},{3,19},{19,3},{4,20},{20... | collective-permute-start | bytes 1769480 | tf_op jit(solution)/shard_map/ppermute | solution.py:1095
  34.6 12.9 %copy-start.26 = (bf16[384,768]{1,0:T(8,128)(2,1)S(1)}, bf16[384,768]{1,0:T(8,128)(2,1)}, u32[]{:S(2)}) copy-start(bf16[384,768]{1,0:T(8,128)(2,1)} %param.25) | copy-start | bytes 1769476
  50.1 95.9 %collective-permute-start.7 = (bf16[2240,768]{1,0:T(8,128)(2,1)S(1)}, bf16[2240,768]{1,0:T(8,128)(2,1)}, u32[]{:S(2)}, u32[]{:S(2)}) collective-permute-start(bf16[2240,768]{1,0:T(8,128)(2,1)S(1)} %pad_maximum_fusion.refs_0_.refs_2_), channel_id=1, source_target_pairs={{0,16},{16,0},{1,17},{17,1},{2,18},{18,2},{3,19},{19,3},{4,20},{20... | collective-permute-start | bytes 10321928 | tf_op jit(solution)/shard_map/ppermute | solution.py:1095
  65.6 110.9 %collective-permute-start.8 = (bf16[1120,768]{1,0:T(8,128)(2,1)}, bf16[1120,768]{1,0:T(8,128)(2,1)}, u32[]{:S(2)}, u32[]{:S(2)}) collective-permute-start(bf16[1120,768]{1,0:T(8,128)(2,1)} %constant_dynamic-slice_fusion.6.refs_4_), channel_id=1, source_target_pairs={{0,16},{16,0},{1,17},{17,1},{2,18},{18,2},{3,19},{19,3},{4,20},{20... | collective-permute-start | bytes 5160968 | tf_op jit(solution)/shard_map/ppermute | solution.py:1095
  67.0 16.4 %collective-permute-start.6 = (bf16[128,1536]{1,0:T(8,128)(2,1)}, bf16[128,1536]{1,0:T(8,128)(2,1)}, u32[]{:S(2)}, u32[]{:S(2)}) collective-permute-start(bf16[128,1536]{1,0:T(8,128)(2,1)} %constant_dynamic-slice_fusion.9.dy_ref), channel_id=1, source_target_pairs={{0,2},{1,3},{2,0},{3,1},{4,6},{5,7},{6,4},{7,5},{8,10},{9,11},{10,... | collective-permute-start | bytes 1179656 | tf_op jit(solution)/shard_map/ppermute | solution.py:1095
  175.7 44.9 %collective-permute-start.9 = (bf16[1120,768]{1,0:T(8,128)(2,1)}, bf16[1120,768]{1,0:T(8,128)(2,1)S(1)}, u32[]{:S(2)}, u32[]{:S(2)}) collective-permute-start(bf16[1120,768]{1,0:T(8,128)(2,1)} %get-tuple-element.102), channel_id=1, source_target_pairs={{0,16},{16,0},{1,17},{17,1},{2,18},{18,2},{3,19},{19,3},{4,20},{20... | collective-permute-start | bytes 5160968 | tf_op jit(solution)/shard_map/ppermute | solution.py:1095
  218.5 44.2 %collective-permute-start.10 = (bf16[1120,768]{1,0:T(8,128)(2,1)}, bf16[1120,768]{1,0:T(8,128)(2,1)S(1)}, u32[]{:S(2)}, u32[]{:S(2)}) collective-permute-start(bf16[1120,768]{1,0:T(8,128)(2,1)} %get-tuple-element.105), channel_id=1, source_target_pairs={{0,16},{16,0},{1,17},{17,1},{2,18},{18,2},{3,19},{19,3},{4,20},{20... | collective-permute-start | bytes 5160968 | tf_op jit(solution)/shard_map/ppermute | solution.py:1095
  219.8 103.6 %collective-permute-start.14 = (bf16[1120,768]{1,0:T(8,128)(2,1)}, bf16[1120,768]{1,0:T(8,128)(2,1)}, u32[]{:S(2)}, u32[]{:S(2)}) collective-permute-start(bf16[1120,768]{1,0:T(8,128)(2,1)} %get-tuple-element.119), channel_id=1, source_target_pairs={{0,16},{16,0},{1,17},{17,1},{2,18},{18,2},{3,19},{19,3},{4,20},{20... | collective-permute-start | bytes 5160968 | tf_op jit(solution)/shard_map/ppermute | solution.py:1095
  265.5 30.5 %collective-permute-start.12 = (bf16[560,768]{1,0:T(8,128)(2,1)}, bf16[560,768]{1,0:T(8,128)(2,1)}, u32[]{:S(2)}, u32[]{:S(2)}) collective-permute-start(bf16[560,768]{1,0:T(8,128)(2,1)} %slice.69), channel_id=1, source_target_pairs={{0,4},{4,0},{8,12},{12,8},{1,5},{5,1},{9,13},{13,9},{2,6},{6,2},{1... | collective-permute-start | bytes 2580488 | tf_op jit(solution)/shard_map/ppermute | solution.py:1095
  270.2 35.0 %collective-permute-start.13 = (bf16[560,768]{1,0:T(8,128)(2,1)}, bf16[560,768]{1,0:T(8,128)(2,1)}, u32[]{:S(2)}, u32[]{:S(2)}) collective-permute-start(bf16[560,768]{1,0:T(8,128)(2,1)} %get-tuple-element.114), channel_id=1, source_target_pairs={{0,4},{4,0},{8,12},{12,8},{1,5},{5,1},{9,13},{13,9},{2,6},{6,2},{1... | collective-permute-start | bytes 2580488 | tf_op jit(solution)/shard_map/ppermute | solution.py:1095
  274.0 15.1 %copy-start.16 = (bf16[512,1536]{1,0:T(8,128)(2,1)S(1)}, bf16[512,1536]{1,0:T(8,128)(2,1)}, u32[]{:S(2)}) copy-start(bf16[512,1536]{1,0:T(8,128)(2,1)} %get-tuple-element.112) | copy-start | bytes 4718596
  274.0 18.7 %copy-start.27 = (bf16[512,384]{1,0:T(8,128)(2,1)S(1)}, bf16[512,384]{1,0:T(8,128)(2,1)}, u32[]{:S(2)}) copy-start(bf16[512,384]{1,0:T(8,128)(2,1)} %get-tuple-element.90) | copy-start | bytes 1179652
  291.5 79.2 %collective-permute-start.17 = (bf16[768,384]{1,0:T(8,128)(2,1)}, bf16[768,384]{1,0:T(8,128)(2,1)}, u32[]{:S(2)}, u32[]{:S(2)}) collective-permute-start(bf16[768,384]{1,0:T(8,128)(2,1)} %convolution_convert_fusion.1), channel_id=1, source_target_pairs={{0,16},{16,0},{1,17},{17,1},{2,18},{18,2},{3,19},{19,3},{4,20},{20... | collective-permute-start | bytes 1769480 | tf_op jit(solution)/shard_map/ppermute | solution.py:1095
  295.2 75.5 %collective-permute-start.11 = (bf16[384,768]{1,0:T(8,128)(2,1)}, bf16[384,768]{1,0:T(8,128)(2,1)}, u32[]{:S(2)}, u32[]{:S(2)}) collective-permute-start(bf16[384,768]{1,0:T(8,128)(2,1)} %convolution_convert_fusion.2), channel_id=1, source_target_pairs={{0,16},{16,0},{1,17},{17,1},{2,18},{18,2},{3,19},{19,3},{4,20},{20... | collective-permute-start | bytes 1769480 | tf_op jit(solution)/shard_map/ppermute | solution.py:1095
  327.4 5.9 %copy-start.29 = (f32[1,1536]{1,0:T(1,128)S(1)}, f32[1,1536]{1,0:T(1,128)}, u32[]{:S(2)}) copy-start(f32[1,1536]{1,0:T(1,128)} %get-tuple-element.125) | copy-start | bytes 18436
  328.5 42.2 %collective-permute-start.18 = (bf16[768,128]{1,0:T(8,128)(2,1)}, bf16[768,128]{1,0:T(8,128)(2,1)}, u32[]{:S(2)}, u32[]{:S(2)}) collective-permute-start(bf16[768,128]{1,0:T(8,128)(2,1)} %convolution_convert_fusion.4), channel_id=1, source_target_pairs={{0,16},{16,0},{1,17},{17,1},{2,18},{18,2},{3,19},{19,3},{4,20},{20... | collective-permute-start | bytes 589832 | tf_op jit(solution)/shard_map/ppermute | solution.py:1095
  331.2 36.4 %collective-permute-start.15 = (bf16[560,768]{1,0:T(8,128)(2,1)}, bf16[560,768]{1,0:T(8,128)(2,1)}, u32[]{:S(2)}, u32[]{:S(2)}) collective-permute-start(bf16[560,768]{1,0:T(8,128)(2,1)} %get-tuple-element.127), channel_id=1, source_target_pairs={{0,4},{4,0},{8,12},{12,8},{1,5},{5,1},{9,13},{13,9},{2,6},{6,2},{1... | collective-permute-start | bytes 2580488 | tf_op jit(solution)/shard_map/ppermute | solution.py:1095
  331.3 39.4 %collective-permute-start.16 = (bf16[560,768]{1,0:T(8,128)(2,1)}, bf16[560,768]{1,0:T(8,128)(2,1)}, u32[]{:S(2)}, u32[]{:S(2)}) collective-permute-start(bf16[560,768]{1,0:T(8,128)(2,1)} %get-tuple-element.128), channel_id=1, source_target_pairs={{0,4},{4,0},{8,12},{12,8},{1,5},{5,1},{9,13},{13,9},{2,6},{6,2},{1... | collective-permute-start | bytes 2580488 | tf_op jit(solution)/shard_map/ppermute | solution.py:1095
  333.9 36.8 %copy-start.20 = (bf16[512,384]{1,0:T(8,128)(2,1)S(1)}, bf16[512,384]{1,0:T(8,128)(2,1)}, u32[]{:S(2)}) copy-start(bf16[512,384]{1,0:T(8,128)(2,1)} %get-tuple-element.109.dq_ref) | copy-start | bytes 1179652
  367.6 5.9 %copy-start.28 = (bf16[512,384]{1,0:T(8,128)(2,1)S(1)}, bf16[512,384]{1,0:T(8,128)(2,1)}, u32[]{:S(2)}) copy-start(bf16[512,384]{1,0:T(8,128)(2,1)} %get-tuple-element.90) | copy-start | bytes 1179652
  367.6 5.8 %copy-start.31 = (bf16[4,128,1536]{2,1,0:T(8,128)(2,1)S(1)}, bf16[4,128,1536]{2,1,0:T(8,128)(2,1)}, u32[]{:S(2)}) copy-start(bf16[4,128,1536]{2,1,0:T(8,128)(2,1)} %get-tuple-element.103) | copy-start | bytes 4718596
  367.6 21.8 %collective-permute-start.19 = (bf16[560,768]{1,0:T(8,128)(2,1)}, bf16[560,768]{1,0:T(8,128)(2,1)}, u32[]{:S(2)}, u32[]{:S(2)}) collective-permute-start(bf16[560,768]{1,0:T(8,128)(2,1)} %get-tuple-element.133), channel_id=1, source_target_pairs={{0,4},{4,0},{8,12},{12,8},{1,5},{5,1},{9,13},{13,9},{2,6},{6,2},{1... | collective-permute-start | bytes 2580488 | tf_op jit(solution)/shard_map/ppermute | solution.py:1095
  375.8 4.8 %copy-start.18 = (bf16[512,1536]{1,0:T(8,128)(2,1)S(1)}, bf16[512,1536]{1,0:T(8,128)(2,1)}, u32[]{:S(2)}) copy-start(bf16[512,1536]{1,0:T(8,128)(2,1)} %get-tuple-element.112) | copy-start | bytes 4718596
  375.8 6.8 %copy-start.4 = (bf16[1120,768]{1,0:T(8,128)(2,1)S(1)}, bf16[1120,768]{1,0:T(8,128)(2,1)}, u32[]{:S(2)}) copy-start(bf16[1120,768]{1,0:T(8,128)(2,1)} %get-tuple-element.138) | copy-start | bytes 5160964
  375.8 6.8 %copy-start.25 = (bf16[560,768]{1,0:T(8,128)(2,1)S(1)}, bf16[560,768]{1,0:T(8,128)(2,1)}, u32[]{:S(2)}) copy-start(bf16[560,768]{1,0:T(8,128)(2,1)} %get-tuple-element.139) | copy-start | bytes 2580484
  (20 other events, 62.0 us)

commit v14 on v13

--- a/solution.py
+++ b/solution.py
@@ -847,7 +847,9 @@
     got_ref, refs = (refs[0], refs[1:]) if count else (None, refs)
     (dmid_ref, dgain_ref, out), refs = refs[:3], refs[3:]
     outs, refs = refs[:count], refs[count:]
-    (low_ref, half_ref), refs = (refs[:2], refs[2:]) if count else ((None, None), refs)
+    (upper_ref, lower_ref, far_ref), refs = (
+        (refs[:3], refs[3:]) if count else ((None, None, None), refs)
+    )
     low, first, wires, to = refs[0], refs[1:8], Wires(*refs[-3:]), partners()
     fill = own_grads(count, args, outs, refs[8:-3])
     meet([to[k] for k in ("core", "y", "z")])
@@ -861,8 +863,10 @@
     next(back)
     if fill:
         fill[0].make(1, fill[0].tiles)
-        low_ref[...] = (wide(outs[0][...]) + wide(got_ref[...])).astype(bf16)
-        near_half = wires.copy(low_ref.at[pl.ds(0, half_ref.shape[0])], half_ref, to["z"])
+        cut = upper_ref.shape[0]
+        upper_ref[...] = (wide(outs[0][:cut]) + wide(got_ref[:cut])).astype(bf16)
+        near_half = wires.copy(upper_ref, far_ref, to["z"])
+        lower_ref[...] = (wide(outs[0][cut:]) + wide(got_ref[cut:])).astype(bf16)
     grad_normed = result_of(back)
     du, dgain = norm_back_rows(mid_ref[...], factor_ref[...], gain_ref[...], grad_normed)
     dgain_ref[...] = dgain
@@ -897,7 +901,8 @@
     if fill:
         args = [*args, got]
         units = got.shape[0]
-        outs = [*outs, *(jax.ShapeDtypeStruct((n, shard), bf16) for n in (units, units // 2))]
+        cut = units // 64 * 16
+        outs = [*outs, *(jax.ShapeDtypeStruct((n, shard), bf16) for n in (cut, units - cut, cut))]
     return remote_call(
         functools.partial(middle_back_kernel, len(fill)),
         "middle_back",
@@ -1245,9 +1250,9 @@
             down_got = gate_got = up_got = jnp.zeros_like(owns[0])
             early = later = []
 
-        unit_whole = lambda low, *other: by_bit(
-            parity, low, jnp.concatenate(other, axis=0), 0
-        ).astype(f32)
+        def unit_whole(own, other):
+            own, other = (jnp.concatenate(x, axis=0) for x in (own, other))
+            return by_bit(parity, own, other, 0).astype(f32)
 
         grad_middle, ffn_gain_grad, grad_middle_low, *first_owns = middle_back(
             dx_part, middle, factor_second, gain_second, dy_part, early, down_got, width // n_f
@@ -1256,13 +1261,14 @@
         add = lambda own, got: (own.astype(f32) + got.astype(f32)).astype(bf16)
         upper = units // 2
         if n_f == 2:
-            _, gate_own, down_low, down_upper = first_owns
+            _, gate_own, down_upper, down_lower, far_upper = first_owns
         else:
             down_low, gate_own = owns[:2]
-            down_upper = flip(down_low[:upper], "context", 1)
-        gate_low = add(gate_own, after(gate_got, grad_middle_low))
-        down_lower = flip(down_low[upper:], "context", 1)
-        gate_upper = flip(after(gate_low[:upper], down_low), "context", 1)
+            down_upper, down_lower = down_low[:upper], down_low[upper:]
+            far_upper = flip(down_upper, "context", 1)
+        gate_got = after(gate_got, grad_middle_low)
+        gate_low = add(gate_own, gate_got)
+        far_lower = flip(down_lower, "context", 1)
         grad_middle_low = after(grad_middle_low, gate_low)
         grad_attended = dot_cols(grad_middle_low, w_out_all).astype(bf16)
 
@@ -1270,12 +1276,13 @@
         attention_args = [(attended, after(grad_middle_low, dq_low), 1), (normed, dq_low, 0)]
         fars = [grad_far(*args) for args in attention_args]
         dkv, *last_owns = kv_scatter(
-            after(dkv, fars, down_lower, gate_upper), later, width // n_f
+            after(dkv, fars), later, width // n_f
         )
         (up_own,) = last_owns or owns[2:]
-        gate_lower = flip(after(gate_low[upper:], dkv, gate_upper), "context", 1)
-        up_low = add(up_own, after(up_got, dkv))
-        dkv = after(dkv, up_low, gate_upper)
+        far_gate = flip(after(gate_low, dkv, far_lower), "context", 1)
+        up_got = after(up_got, dkv)
+        up_low = add(up_own, up_got)
+        dkv = after(dkv, up_low, far_lower)
         dkv_low = jnp.where(core == 0, rotate_back(dkv, cosine, sine), dkv).astype(bf16)
         attention_args.append((normed, dkv_low, 0))
         fars.append(grad_far(*attention_args[-1]))
@@ -1291,8 +1298,7 @@
             [jnp.zeros((1, width), f32), ffn_gain_grad, slots.reshape(1, -1)], axis=1
         )
         grad_qkv = qkv_back(meta, dq_low, dkv_low, w_q, w_kv)
-        up_upper = flip(after(up_low[:upper], dkv_low), "context", 1)
-        up_lower = flip(after(up_low[upper:], grad_qkv), "context", 1)
+        far_up = flip(after(up_low, dkv_low), "context", 1)
         small_grads, input_grad = input_back(
             grad_qkv,
             inputs_part,
@@ -1304,17 +1310,24 @@
         input_grad = input_grad.reshape(rows, width)
         if n_f > 2:
             small_grads = lax.psum(small_grads, "fsdp")
-        small_grads = after(small_grads, gate_lower, up_upper)
+        zero = jnp.minimum(t, 0).astype(bf16)
+        input_grad = input_grad + zero
+        small_grads = after(small_grads, far_gate)
         attention_parts = [
             grad_sum(*args, far, small_grads) for args, far in zip(attention_args, fars)
         ]
-        wd_grad = unit_whole(*after((down_low, down_upper, down_lower), small_grads))
-        wg_grad = unit_whole(*after((gate_low, gate_upper, gate_lower), small_grads))
-        small_grads, up_lower, wg_grad, wd_grad = lax.optimization_barrier(
-            (small_grads, up_lower, wg_grad, wd_grad)
+        wd_grad = unit_whole(
+            *after(((down_upper, down_lower), (far_upper, far_lower)), small_grads)
+        )
+        wg_grad = unit_whole(*after(((gate_low,), (far_gate,)), small_grads))
+        small_grads, wd_grad, wg_grad, input_grad = lax.optimization_barrier(
+            (small_grads, wd_grad, wg_grad, input_grad)
         )
         wo_grad, wq_grad, packed, wkv_all, outputs = context_sum(
             n_f == 2, attention_parts, small_grads, out_part, middle
+        )
+        wo_grad, wq_grad, packed, wkv_all, outputs, far_up = lax.optimization_barrier(
+            (wo_grad, wq_grad, packed, wkv_all, outputs, far_up)
         )
         outputs = outputs.reshape(rows, width)
         wkv_all = wkv_all.astype(f32)
@@ -1329,7 +1342,7 @@
         bk_out = slots[0::2, heads]
         bv_out = slots[1::2, heads]
 
-        wu_grad = unit_whole(up_low, up_upper, up_lower)
+        wu_grad = unit_whole((up_low,), (far_up,))
         wg_grad, wu_grad = wg_grad.T, wu_grad.T
 
         return (

time: 481 us -> 465 us (0.967)
  waiting for transfers between devices: 26.3 us -> 11 us
    ppermute x20 -> x18, waiting for transfers between devices: 26.3 us -> 11 us  [flip(): return lax.ppermute(x, axis, [(i, i ^ bit) for i in range(size)])]
    slice x3 -> x0, local copies, waits for them, and re-layouts: 5.38 us -> none  [the longest x1 2.78 us: local(): down_lower = flip(down_low[upper:], 'context', 1)]
    unnamed x73 -> x70, local copies, waits for them, and re-layouts: 9.75 us -> 11.4 us
    ppermute x20 -> x18, starting transfers between devices: 23.6 us -> 22.2 us  [flip(): return lax.ppermute(x, axis, [(i, i ^ bit) for i in range(size)])]
  transfers between devices with their start and end apart: 20 -> 18, of which waited for: 5 -> 3; matrix products, arithmetic and copies ran while one was open for 12% -> 12% of each run, Pallas kernels for 57% -> 75%
where the time goes in v14:
time: 465 us; the launch traced here: 461 us
  Pallas kernels  345 us (74%)
  other arithmetic  36.7 us (8%)
  local copies, waits for them, and re-layouts  27.3 us (6%)
  starting transfers between devices  22.2 us (5%)
  matrix products  17.3 us (4%)
  waiting for transfers between devices  11 us (2%)
    pallas_call x6, Pallas kernels, remote_call(): pl.pallas_call(kernel, name=name, out_shape=outs, in_specs=[spec(x) for x...  237 us
    pallas_call x2, Pallas kernels, hidden_call(): pl.pallas_call(kernel, name=name, grid_spec=pltpu.PrefetchScalarGridSpec(...  71.8 us
    ppermute x18, starting transfers between devices, flip(): return lax.ppermute(x, axis, [(i, i ^ bit) for i in range(size)])  22.2 us
    pallas_call x1, Pallas kernels, attention_back(): pl.pallas_call(functools.partial(attention_back_kernel, kv.shape[1] // BL...  15.1 us
    dot_general x6, matrix products, dot_rows(): lax.dot_general(left, right, (((0,), (0,)), ((), ())), preferred_element_...  12 us
    unnamed x70, local copies, waits for them, and re-layouts  11.4 us
    ppermute x18, waiting for transfers between devices, flip(): return lax.ppermute(x, axis, [(i, i ^ bit) for i in range(size)])  11 us
    pallas_call x1, Pallas kernels, attention(): pl.pallas_call(functools.partial(attention_kernel, kv.shape[1] // BLOCK),...  10.2 us
  transfers between devices with their start and end apart: 18, of which 3 were waited for; matrix products, arithmetic and copies ran while one was open for 12% of the time, Pallas kernels for 75%

profile of v14, /device:TPU:0, one launch (start us, length us, event | category | flops | bytes accessed | tf_op | source)
XLA Modules:
  0.0 461.2 jit_solution(12673993587273834568)
XLA Ops:
  0.7 1.9 constant_dynamic-slice_fusion.9.dy_ref
  2.6 4.0 collective-permute-start.2
  13.4 1.8 dynamic-slice_select_fusion.refs_2_
  19.2 1.8 constant_dynamic-slice_fusion.5.x_ref
  24.8 1.7 constant_dynamic-slice_fusion.7
  28.9 5.0 %collective-permute-done.3.refs_1_ = bf16[768,384]{1,0:T(8,128)(2,1)} collective-permute-done((bf16[768,384]{1,0:T(8,128)(2,1)}, bf16[768,384]{1,0:T(8,128)(2,1)}, u32[]{:S(2)}, u32[]{:S(2)}) %collective-permute-start.3) | collective-permute-done | bytes 589856 | tf_op jit(solution)/shard_map/ppermute | solution.py:1100
  35.9 6.5 %qkv.1 = (bf16[512,1536]{1,0:T(8,128)(2,1)}, f32[512,1]{1,0:T(8,128)}, bf16[512,384]{1,0:T(8,128)(2,1)}, bf16[512,128]{1,0:T(8,128)(2,1)}) custom-call(s32[4]{0:T(128)} %pad_add_fusion.1.meta_ref, bf16[512,1536]{1,0:T(8,128)(2,1)} %x_ref.1, f32[1,1536]{1,0:T(1,128)} %bitcast.87, f32[1,512]{1,0:T(1,128)} %pad_maximum_fusion.6.bias_ref, ...), custom_call_target="tpu_custom_call" | custom-call | tf_op jit(solution)/shard_map/qkv/pallas_call | solution.py:209
  42.3 5.2 %collective-permute-done.5 = bf16[384,768]{1,0:T(8,128)(2,1)} collective-permute-done((bf16[384,768]{1,0:T(8,128)(2,1)}, bf16[384,768]{1,0:T(8,128)(2,1)}, u32[]{:S(2)}, u32[]{:S(2)}) %collective-permute-start.5) | collective-permute-done | bytes 589856 | tf_op jit(solution)/shard_map/ppermute | solution.py:1100
  47.6 2.5 maximum_select_fusion.3
  50.6 15.0 %kv_gather.1.k_ref.v_ref = bf16[2,2048,128]{2,1,0:T(8,128)(2,1)} custom-call(bf16[512,128]{1,0:T(8,128)(2,1)} %get-tuple-element.94.own_ref), custom_call_target="tpu_custom_call" | custom-call | tf_op jit(solution)/shard_map/kv_gather/pallas_call | solution.py:642
  69.8 10.2 %attention.1 = (bf16[512,384]{1,0:T(8,128)(2,1)}, f32[3,512,1]{2,1,0:T(8,128)}) custom-call(s32[8]{0:T(128)} %pad_add_fusion.kb_ref, bf16[512,384]{1,0:T(8,128)(2,1)} %get-tuple-element.91.q_ref, bf16[2,2048,128]{2,1,0:T(8,128)(2,1)} %kv_gather.1.k_ref.v_ref, bf16[2,2048,128]{2,1,0:T(8,128)(2,1)} %kv_gather.1.k_ref.v_ref), custom_call_target="tpu_custom_call" | custom-call | tf_op jit(solution)/shard_map/attention/pallas_call | solution.py:85
  79.9 3.5 convolution_convert_fusion
  83.5 62.5 %middle_norm.1 = (f32[128,1536]{1,0:T(8,128)}, f32[128,1]{1,0:T(8,128)}, bf16[16,128,1536]{2,1,0:T(8,128)(2,1)}, bf16[16,128,1536]{2,1,0:T(8,128)(2,1)}) custom-call(bf16[4,128,1536]{2,1,0:T(8,128)(2,1)} %bitcast.79, bf16[128,1536]{1,0:T(8,128)(2,1)} %constant_dynamic-slice_fusion.5.x_ref, f32[1,1536]{1,0:T(1,128)} %bitcast.89, ...), custom_call_target="tpu_custom_call" | custom-call | tf_op jit(solution)/shard_map/middle_norm/pallas_call | solution.py:642
  146.0 29.8 %hidden_units.1 = (bf16[2048,1120]{1,0:T(8,128)(2,1)}, bf16[2048,1120]{1,0:T(8,128)(2,1)}, bf16[2048,1120]{1,0:T(8,128)(2,1)}, bf16[1120,768]{1,0:T(8,128)(2,1)}) custom-call(s32[4]{0:T(128)} %pad_add_fusion.1.meta_ref, bf16[2048,1536]{1,0:T(8,128)(2,1)} %bitcast.70, bf16[2048,1536]{1,0:T(8,128)(2,1)} %bitcast.74, bf16[2240,768]{1,0:T(8,128)(2,1)} %copy-done.2, ...), custom_call_target="tpu_custom_call" | custom-call | tf_op jit(solution)/shard_map/hidden_units/pallas_call | solution.py:333
  176.6 42.0 %hidden_back.1 = (bf16[2048,1120]{1,0:T(8,128)(2,1)}, bf16[2048,1120]{1,0:T(8,128)(2,1)}, bf16[1024,1536]{1,0:T(8,128)(2,1)}, bf16[1024,1536]{1,0:T(8,128)(2,1)}...) custom-call(s32[4]{0:T(128)} %pad_add_fusion.1.meta_ref, bf16[2048,1536]{1,0:T(8,128)(2,1)} %bitcast.71, ...), custom_call_target="tpu_custom_call" | custom-call | tf_op jit(solution)/shard_map/hidden_back/pallas_call | solution.py:333
  223.3 35.2 %middle_back.1 = (f32[128,1536]{1,0:T(8,128)}, f32[1,1536]{1,0:T(1,128)}, bf16[4,128,1536]{2,1,0:T(8,128)(2,1)}, bf16[1120,768]{1,0:T(8,128)(2,1)}, bf16[1120,76...) custom-call(bf16[8,128,1536]{2,1,0:T(8,128)(2,1)} %bitcast.80, ...), custom_call_target="tpu_custom_call" | custom-call | tf_op jit(solution)/shard_map/middle_back/pallas_call | solution.py:642
  260.4 2.5 add_convert_fusion.1
  264.6 1.8 convolution_convert_fusion.3.do_ref
  266.3 15.1 %attention_back.1 = (bf16[512,384]{1,0:T(8,128)(2,1)}, bf16[2,2048,128]{2,1,0:T(8,128)(2,1)}) custom-call(s32[8]{0:T(128)} %pad_add_fusion.kb_ref, bf16[512,384]{1,0:T(8,128)(2,1)} %get-tuple-element.91.q_ref, bf16[512,384]{1,0:T(8,128)(2,1)} %convolution_convert_fusion.3.do_ref, f32[3,512,1]{2,1,0:T(8,128)} %get-tuple-element.113.lse_ref, ...), custom_call_target="tpu_custom_call" | custom-call | tf_op jit(solution)/shard_map/attention_back/pallas_call | solution.py:151
  281.5 2.6 convolution_convert_fusion.1
  287.4 18.1 %kv_scatter.1 = (f32[512,128]{1,0:T(8,128)}, bf16[1120,768]{1,0:T(8,128)(2,1)}) custom-call(bf16[2,2048,128]{2,1,0:T(8,128)(2,1)} %get-tuple-element.118.part_ref, bf16[2048,1120]{1,0:T(8,128)(2,1)} %get-tuple-element.119.refs_0_, bf16[2048,1536]{1,0:T(8,128)(2,1)} %bitcast.73), custom_call_target="tpu_custom_call" | custom-call | tf_op jit(solution)/shard_map/kv_scatter/pallas_call | solution.py:642
  305.5 2.5 add_convert_fusion
  313.2 4.9 %qkv_back.1 = bf16[512,1536]{1,0:T(8,128)(2,1)} custom-call(s32[4]{0:T(128)} %pad_add_fusion.1.meta_ref, bf16[512,384]{1,0:T(8,128)(2,1)} %get-tuple-element.114.dq_ref, bf16[512,128]{1,0:T(8,128)(2,1)} %copy-done.4, bf16[768,384]{1,0:T(8,128)(2,1)} %refs_0_.3, bf16[768,384]{1,0:T(8,128)(2,1)} %collective-permute-done.3.refs_1_, ...), custom_call_target="tpu_custom_call" | custom-call | tf_op jit(solution)/shard_map/qkv_back/pallas_call | solution.py:242
  318.8 27.7 %input_back.1 = (f32[1,5120]{1,0:T(1,128)}, bf16[4,128,1536]{2,1,0:T(8,128)(2,1)}) custom-call(bf16[4,128,1536]{2,1,0:T(8,128)(2,1)} %bitcast.78, bf16[128,1536]{1,0:T(8,128)(2,1)} %constant_dynamic-slice_fusion.5.x_ref, f32[128,1]{1,0:T(8,128)} %constant_dynamic-slice_fusion.4.factor_ref, f32[1,1536]{1,0:T(1,128)} %bitcast.88, ...), custom_call_target="tpu_custom_call" | custom-call | tf_op jit(solution)/shard_map/input_back/pallas_call | solution.py:642
  346.5 2.7 broadcast_add_fusion
  349.2 4.7 %fusion.1 = f32[2240,768]{1,0:T(8,128)} fusion(bf16[1120,768]{1,0:T(8,128)(2,1)} %collective-permute-done.14, bf16[1120,768]{1,0:T(8,128)(2,1)S(1)} %add_convert_fusion.1, pred[]{:T(512)S(6)} %eq.19), kind=kLoop, calls=%fused_computation.5 | loop fusion | flops 17203200 | bytes 10321921 | tf_op jit(solution)/shard_map/convert_element_type | solution.py:1255
  354.0 5.1 %fusion = f32[2240,768]{1,0:T(8,128)} fusion(bf16[848,768]{1,0:T(8,128)(2,1)} %collective-permute-done.13, bf16[272,768]{1,0:T(8,128)(2,1)S(1)} %copy-done.24, bf16[848,768]{1,0:T(8,128)(2,1)} %get-tuple-element.139, bf16[272,768]{1,0:T(8,128)(2,1)S(1)} %copy-done.23, pred[]{:T(512)S(6)} %eq.19), kind=kLoop, calls=%fused_computation.3 | loop fusion | flops 30965760 | bytes 10321921 | tf_op jit(solution)/shard_map/convert_element_type | solution.py:1255
  359.1 2.2 fusion.4.refs_2_
  361.3 2.5 fusion.3.refs_1_
  363.8 2.4 fusion.2.refs_0_
  366.1 78.5 %context_sum.1 = (f32[384,768]{1,0:T(8,128)}, f32[768,384]{1,0:T(8,128)}, f32[1,5120]{1,0:T(1,128)}, bf16[4,768,128]{2,1,0:T(8,128)(2,1)}, bf16[4,128,1536]{2,1,0:T(8,128)(2,1)}) custom-call(bf16[384,768]{1,0:T(8,128)(2,1)} %fusion.2.refs_0_, bf16[768,384]{1,0:T(8,128)(2,1)} %fusion.3.refs_1_, bf16[768,128]{1,0:T(8,128)(2,1)} %fusion.4.refs_2_, ...), custom_call_target="tpu_custom_call" | custom-call | tf_op jit(solution)/shard_map/context_sum/pallas_call | solution.py:642
  448.0 4.8 %convert_bitcast_fusion = f32[768,2240]{0,1:T(8,128)} fusion(bf16[1120,768]{1,0:T(8,128)(2,1)} %collective-permute-done.17, bf16[1120,768]{1,0:T(8,128)(2,1)S(1)} %add_convert_fusion, pred[]{:T(512)S(6)} %eq.19), kind=kLoop, calls=%fused_computation | loop fusion | flops 17203200 | bytes 10321921 | tf_op jit(solution)/shard_map/transpose | solution.py:1346
  (155 shorter events, 53.4 us)
Async XLA Ops:
  0.6 21.4 %copy-start = (bf16[2240,768]{1,0:T(8,128)(2,1)S(1)}, bf16[2240,768]{1,0:T(8,128)(2,1)}, u32[]{:S(2)}) copy-start(bf16[2240,768]{1,0:T(8,128)(2,1)} %param.29) | copy-start | bytes 10321924
  2.6 33.3 %collective-permute-start.2 = (bf16[128,1536]{1,0:T(8,128)(2,1)}, bf16[128,1536]{1,0:T(8,128)(2,1)}, u32[]{:S(2)}, u32[]{:S(2)}) collective-permute-start(bf16[128,1536]{1,0:T(8,128)(2,1)} %constant_dynamic-slice_fusion.9.dy_ref), channel_id=1, source_target_pairs={{0,8},{4,12},{8,0},{12,4},{1,9},{5,13},{9,1},{13,5},{2,10},{6,14},... | collective-permute-start | bytes 1179656 | tf_op jit(solution)/shard_map/ppermute | solution.py:1100
  6.6 29.2 %collective-permute-start.1 = (bf16[128,1536]{1,0:T(8,128)(2,1)}, bf16[128,1536]{1,0:T(8,128)(2,1)}, u32[]{:S(2)}, u32[]{:S(2)}) collective-permute-start(bf16[128,1536]{1,0:T(8,128)(2,1)} %constant_dynamic-slice_fusion.9.dy_ref), channel_id=1, source_target_pairs={{0,4},{4,0},{8,12},{12,8},{1,5},{5,1},{9,13},{13,9},{2,6},{6,2},{1... | collective-permute-start | bytes 1179656 | tf_op jit(solution)/shard_map/ppermute | solution.py:1100
  11.9 16.7 %collective-permute-start = (bf16[1,1984]{1,0:T(2,128)(2,1)S(1)}, bf16[1,1984]{1,0:T(2,128)(2,1)S(1)}, u32[]{:S(2)}, u32[]{:S(2)}) collective-permute-start(bf16[1,1984]{1,0:T(2,128)(2,1)S(1)} %concatenate.68), channel_id=1, source_target_pairs={{0,16},{16,0},{1,17},{17,1},{2,18},{18,2},{3,19},{19,3},{4,20},{20... | collective-permute-start | bytes 11912 | tf_op jit(solution)/shard_map/ppermute | solution.py:1100
  15.2 13.7 %collective-permute-start.4 = (bf16[768,128]{1,0:T(8,128)(2,1)}, bf16[768,128]{1,0:T(8,128)(2,1)}, u32[]{:S(2)}, u32[]{:S(2)}) collective-permute-start(bf16[768,128]{1,0:T(8,128)(2,1)} %dynamic-slice_select_fusion.refs_2_), channel_id=1, source_target_pairs={{0,16},{16,0},{1,17},{17,1},{2,18},{18,2},{3,19},{19,3},{4,20},{20... | collective-permute-start | bytes 589832 | tf_op jit(solution)/shard_map/ppermute | solution.py:1100
  15.7 18.2 %collective-permute-start.3 = (bf16[768,384]{1,0:T(8,128)(2,1)}, bf16[768,384]{1,0:T(8,128)(2,1)}, u32[]{:S(2)}, u32[]{:S(2)}) collective-permute-start(bf16[768,384]{1,0:T(8,128)(2,1)} %refs_0_.3), channel_id=1, source_target_pairs={{0,16},{16,0},{1,17},{17,1},{2,18},{18,2},{3,19},{19,3},{4,20},{20... | collective-permute-start | bytes 1769480 | tf_op jit(solution)/shard_map/ppermute | solution.py:1100
  22.0 4.7 %copy-start.6 = (f32[512,64]{1,0:T(8,128)}, f32[512,64]{1,0:T(8,128)S(1)}, u32[]{:S(2)}) copy-start(f32[512,64]{1,0:T(8,128)S(1)} %get-tuple-element.176) | copy-start | bytes 393220
  22.0 4.7 %copy-start.8 = (f32[512,64]{1,0:T(8,128)}, f32[512,64]{1,0:T(8,128)S(1)}, u32[]{:S(2)}) copy-start(f32[512,64]{1,0:T(8,128)S(1)} %get-tuple-element.177) | copy-start | bytes 393220
  26.7 23.4 %copy-start.2 = (bf16[2240,768]{1,0:T(8,128)(2,1)}, bf16[2240,768]{1,0:T(8,128)(2,1)S(1)}, u32[]{:S(2)}) copy-start(bf16[2240,768]{1,0:T(8,128)(2,1)S(1)} %pad_maximum_fusion.refs_0_.refs_2_) | copy-start | bytes 10321924
  33.9 13.6 %collective-permute-start.5 = (bf16[384,768]{1,0:T(8,128)(2,1)}, bf16[384,768]{1,0:T(8,128)(2,1)}, u32[]{:S(2)}, u32[]{:S(2)}) collective-permute-start(bf16[384,768]{1,0:T(8,128)(2,1)} %param.25), channel_id=1, source_target_pairs={{0,16},{16,0},{1,17},{17,1},{2,18},{18,2},{3,19},{19,3},{4,20},{20... | collective-permute-start | bytes 1769480 | tf_op jit(solution)/shard_map/ppermute | solution.py:1100
  35.9 11.7 %copy-start.22 = (bf16[384,768]{1,0:T(8,128)(2,1)S(1)}, bf16[384,768]{1,0:T(8,128)(2,1)}, u32[]{:S(2)}) copy-start(bf16[384,768]{1,0:T(8,128)(2,1)} %param.25) | copy-start | bytes 1769476
  50.1 95.9 %collective-permute-start.7 = (bf16[2240,768]{1,0:T(8,128)(2,1)S(1)}, bf16[2240,768]{1,0:T(8,128)(2,1)}, u32[]{:S(2)}, u32[]{:S(2)}) collective-permute-start(bf16[2240,768]{1,0:T(8,128)(2,1)S(1)} %pad_maximum_fusion.refs_0_.refs_2_), channel_id=1, source_target_pairs={{0,16},{16,0},{1,17},{17,1},{2,18},{18,2},{3,19},{19,3},{4,20},{20... | collective-permute-start | bytes 10321928 | tf_op jit(solution)/shard_map/ppermute | solution.py:1100
  65.6 111.0 %collective-permute-start.8 = (bf16[1120,768]{1,0:T(8,128)(2,1)}, bf16[1120,768]{1,0:T(8,128)(2,1)}, u32[]{:S(2)}, u32[]{:S(2)}) collective-permute-start(bf16[1120,768]{1,0:T(8,128)(2,1)} %constant_dynamic-slice_fusion.6.refs_4_), channel_id=1, source_target_pairs={{0,16},{16,0},{1,17},{17,1},{2,18},{18,2},{3,19},{19,3},{4,20},{20... | collective-permute-start | bytes 5160968 | tf_op jit(solution)/shard_map/ppermute | solution.py:1100
  67.1 16.4 %collective-permute-start.6 = (bf16[128,1536]{1,0:T(8,128)(2,1)}, bf16[128,1536]{1,0:T(8,128)(2,1)}, u32[]{:S(2)}, u32[]{:S(2)}) collective-permute-start(bf16[128,1536]{1,0:T(8,128)(2,1)} %constant_dynamic-slice_fusion.9.dy_ref), channel_id=1, source_target_pairs={{0,2},{1,3},{2,0},{3,1},{4,6},{5,7},{6,4},{7,5},{8,10},{9,11},{10,... | collective-permute-start | bytes 1179656 | tf_op jit(solution)/shard_map/ppermute | solution.py:1100
  175.8 46.3 %collective-permute-start.9 = (bf16[1120,768]{1,0:T(8,128)(2,1)}, bf16[1120,768]{1,0:T(8,128)(2,1)S(1)}, u32[]{:S(2)}, u32[]{:S(2)}) collective-permute-start(bf16[1120,768]{1,0:T(8,128)(2,1)} %get-tuple-element.107), channel_id=1, source_target_pairs={{0,16},{16,0},{1,17},{17,1},{2,18},{18,2},{3,19},{19,3},{4,20},{20... | collective-permute-start | bytes 5160968 | tf_op jit(solution)/shard_map/ppermute | solution.py:1100
  218.6 40.7 %collective-permute-start.10 = (bf16[1120,768]{1,0:T(8,128)(2,1)}, bf16[1120,768]{1,0:T(8,128)(2,1)S(1)}, u32[]{:S(2)}, u32[]{:S(2)}) collective-permute-start(bf16[1120,768]{1,0:T(8,128)(2,1)} %get-tuple-element.110), channel_id=1, source_target_pairs={{0,16},{16,0},{1,17},{17,1},{2,18},{18,2},{3,19},{19,3},{4,20},{20... | collective-permute-start | bytes 5160968 | tf_op jit(solution)/shard_map/ppermute | solution.py:1100
  219.9 85.6 %collective-permute-start.12 = (bf16[1120,768]{1,0:T(8,128)(2,1)}, bf16[1120,768]{1,0:T(8,128)(2,1)}, u32[]{:S(2)}, u32[]{:S(2)}) collective-permute-start(bf16[1120,768]{1,0:T(8,128)(2,1)} %get-tuple-element.122), channel_id=1, source_target_pairs={{0,16},{16,0},{1,17},{17,1},{2,18},{18,2},{3,19},{19,3},{4,20},{20... | collective-permute-start | bytes 5160968 | tf_op jit(solution)/shard_map/ppermute | solution.py:1100
  263.0 45.0 %collective-permute-start.13 = (bf16[848,768]{1,0:T(8,128)(2,1)}, bf16[848,768]{1,0:T(8,128)(2,1)}, u32[]{:S(2)}, u32[]{:S(2)}) collective-permute-start(bf16[848,768]{1,0:T(8,128)(2,1)} %get-tuple-element.139), channel_id=1, source_target_pairs={{0,4},{4,0},{8,12},{12,8},{1,5},{5,1},{9,13},{13,9},{2,6},{6,2},{1... | collective-permute-start | bytes 3907592 | tf_op jit(solution)/shard_map/ppermute | solution.py:1100
  266.3 15.1 %copy-start.13 = (bf16[512,1536]{1,0:T(8,128)(2,1)S(1)}, bf16[512,1536]{1,0:T(8,128)(2,1)}, u32[]{:S(2)}) copy-start(bf16[512,1536]{1,0:T(8,128)(2,1)} %get-tuple-element.117) | copy-start | bytes 4718596
  284.0 69.9 %collective-permute-start.15 = (bf16[768,384]{1,0:T(8,128)(2,1)}, bf16[768,384]{1,0:T(8,128)(2,1)}, u32[]{:S(2)}, u32[]{:S(2)}) collective-permute-start(bf16[768,384]{1,0:T(8,128)(2,1)} %convolution_convert_fusion.1), channel_id=1, source_target_pairs={{0,16},{16,0},{1,17},{17,1},{2,18},{18,2},{3,19},{19,3},{4,20},{20... | collective-permute-start | bytes 1769480 | tf_op jit(solution)/shard_map/ppermute | solution.py:1100
  286.6 67.4 %collective-permute-start.11 = (bf16[384,768]{1,0:T(8,128)(2,1)}, bf16[384,768]{1,0:T(8,128)(2,1)}, u32[]{:S(2)}, u32[]{:S(2)}) collective-permute-start(bf16[384,768]{1,0:T(8,128)(2,1)} %convolution_convert_fusion.2), channel_id=1, source_target_pairs={{0,16},{16,0},{1,17},{17,1},{2,18},{18,2},{3,19},{19,3},{4,20},{20... | collective-permute-start | bytes 1769480 | tf_op jit(solution)/shard_map/ppermute | solution.py:1100
  308.3 40.9 %collective-permute-start.14 = (bf16[1120,768]{1,0:T(8,128)(2,1)S(1)}, bf16[1120,768]{1,0:T(8,128)(2,1)}, u32[]{:S(2)}, u32[]{:S(2)}) collective-permute-start(bf16[1120,768]{1,0:T(8,128)(2,1)S(1)} %add_convert_fusion.1), channel_id=1, source_target_pairs={{0,4},{4,0},{8,12},{12,8},{1,5},{5,1},{9,13},{13,9},{2,6},{6,2},{1... | collective-permute-start | bytes 5160968 | tf_op jit(solution)/shard_map/ppermute | solution.py:1100
  310.6 43.3 %collective-permute-start.16 = (bf16[768,128]{1,0:T(8,128)(2,1)}, bf16[768,128]{1,0:T(8,128)(2,1)}, u32[]{:S(2)}, u32[]{:S(2)}) collective-permute-start(bf16[768,128]{1,0:T(8,128)(2,1)} %convolution_convert_fusion.4), channel_id=1, source_target_pairs={{0,16},{16,0},{1,17},{17,1},{2,18},{18,2},{3,19},{19,3},{4,20},{20... | collective-permute-start | bytes 589832 | tf_op jit(solution)/shard_map/ppermute | solution.py:1100
  312.0 6.2 %copy-start.27 = (f32[1,1536]{1,0:T(1,128)S(1)}, f32[1,1536]{1,0:T(1,128)}, u32[]{:S(2)}) copy-start(f32[1,1536]{1,0:T(1,128)} %get-tuple-element.129) | copy-start | bytes 18436
  312.0 132.6 %collective-permute-start.17 = (bf16[1120,768]{1,0:T(8,128)(2,1)S(1)}, bf16[1120,768]{1,0:T(8,128)(2,1)}, u32[]{:S(2)}, u32[]{:S(2)}) collective-permute-start(bf16[1120,768]{1,0:T(8,128)(2,1)S(1)} %add_convert_fusion), channel_id=1, source_target_pairs={{0,4},{4,0},{8,12},{12,8},{1,5},{5,1},{9,13},{13,9},{2,6},{6,2},{1... | collective-permute-start | bytes 5160968 | tf_op jit(solution)/shard_map/ppermute | solution.py:1100
  349.2 4.8 %copy-start.23 = (bf16[272,768]{1,0:T(8,128)(2,1)S(1)}, bf16[272,768]{1,0:T(8,128)(2,1)}, u32[]{:S(2)}) copy-start(bf16[272,768]{1,0:T(8,128)(2,1)} %get-tuple-element.138) | copy-start | bytes 1253380
  349.2 4.8 %copy-start.24 = (bf16[272,768]{1,0:T(8,128)(2,1)S(1)}, bf16[272,768]{1,0:T(8,128)(2,1)}, u32[]{:S(2)}) copy-start(bf16[272,768]{1,0:T(8,128)(2,1)} %get-tuple-element.140) | copy-start | bytes 1253380
  353.9 5.1 %copy-start.5 = (bf16[512,128]{1,0:T(8,128)(2,1)S(1)}, bf16[512,128]{1,0:T(8,128)(2,1)}, u32[]{:S(2)}) copy-start(bf16[512,128]{1,0:T(8,128)(2,1)} %copy-done.4) | copy-start | bytes 393220
  353.9 5.1 %copy-start.15 = (bf16[512,1536]{1,0:T(8,128)(2,1)S(1)}, bf16[512,1536]{1,0:T(8,128)(2,1)}, u32[]{:S(2)}) copy-start(bf16[512,1536]{1,0:T(8,128)(2,1)} %get-tuple-element.117) | copy-start | bytes 4718596
  353.9 7.3 %copy-start.17 = (bf16[512,384]{1,0:T(8,128)(2,1)S(1)}, bf16[512,384]{1,0:T(8,128)(2,1)}, u32[]{:S(2)}) copy-start(bf16[512,384]{1,0:T(8,128)(2,1)} %get-tuple-element.114.dq_ref) | copy-start | bytes 1179652
  359.1 4.7 %copy-start.26 = (bf16[512,384]{1,0:T(8,128)(2,1)S(1)}, bf16[512,384]{1,0:T(8,128)(2,1)}, u32[]{:S(2)}) copy-start(bf16[512,384]{1,0:T(8,128)(2,1)} %get-tuple-element.95) | copy-start | bytes 1179652
  359.1 4.7 %copy-start.30 = (bf16[4,128,1536]{2,1,0:T(8,128)(2,1)S(1)}, bf16[4,128,1536]{2,1,0:T(8,128)(2,1)}, u32[]{:S(2)}) copy-start(bf16[4,128,1536]{2,1,0:T(8,128)(2,1)} %get-tuple-element.108) | copy-start | bytes 4718596
  (17 other events, 44.3 us)

commit v15 on v14

--- a/solution.py
+++ b/solution.py
@@ -994,7 +994,7 @@
     next(ahead)
     sources = [*parts, sum_ref]
     chunks = []
-    for i, cuts in ((2, 1), (0, 2), (1, 2), (3, 1)):
+    for i, cuts in ((2, 1), (0, 2), (1, 4), (3, 1)):
         size = sources[i].shape[0] // cuts
         chunks += [(i, pl.ds(k * size, size)) for k in range(cuts)]
     inward = [wires.plan(sources[i].at[at], from_end[i].at[at], to["z"]) for i, at in chunks]
@@ -1221,9 +1221,9 @@
         normed, factor_first, queries, kv_own = qkv(
             meta, inputs, gain_first, bias, cosine, sine, w_q, w_kv
         )
-        far_gate_up = pieces_f(after(own_gate_up, kv_own, w_out_all), 1)[-1]
+        kv = after(kv_gather(kv_own), w_out_all)
+        far_gate_up = pieces_f(after(own_gate_up, kv), 1)[-1]
         w_gate_up = [own_gate_up, far_gate_up] if n_f == 2 else [far_gate_up]
-        kv = kv_gather(after(kv_own, w_out_all))
         far_down = pieces_f(after(own_down, kv), 1)[-1]
         w_downs = [own_down, far_down] if n_f == 2 else [far_down]
         attended, lse = attention(key_blocks, queries, kv)

time: 465 us -> 462 us (level)
  transfers between devices with their start and end apart: 18 -> 18, of which waited for: 3 -> 3; matrix products, arithmetic and copies ran while one was open for 12% -> 12% of each run, Pallas kernels for 75% -> 76%
where the time goes in v15:
time: 462 us; the launch traced here: 458 us
  Pallas kernels  347 us (75%)
  other arithmetic  36.7 us (8%)
  local copies, waits for them, and re-layouts  27.3 us (6%)
  starting transfers between devices  21.9 us (5%)
  matrix products  17.3 us (4%)
  waiting for transfers between devices  7.15 us (2%)
    pallas_call x6, Pallas kernels, remote_call(): pl.pallas_call(kernel, name=name, out_shape=outs, in_specs=[spec(x) for x...  238 us
    pallas_call x2, Pallas kernels, hidden_call(): pl.pallas_call(kernel, name=name, grid_spec=pltpu.PrefetchScalarGridSpec(...  71.8 us
    ppermute x18, starting transfers between devices, flip(): return lax.ppermute(x, axis, [(i, i ^ bit) for i in range(size)])  21.9 us
    pallas_call x1, Pallas kernels, attention_back(): pl.pallas_call(functools.partial(attention_back_kernel, kv.shape[1] // BL...  15.1 us
    dot_general x6, matrix products, dot_rows(): lax.dot_general(left, right, (((0,), (0,)), ((), ())), preferred_element_...  12 us
    unnamed x70, local copies, waits for them, and re-layouts  11.4 us
    pallas_call x1, Pallas kernels, attention(): pl.pallas_call(functools.partial(attention_kernel, kv.shape[1] // BLOCK),...  10.2 us
    convert_element_type x2, other arithmetic, unit_whole(): return by_bit(parity, own, other, 0).astype(f32)  9.81 us
  transfers between devices with their start and end apart: 18, of which 3 were waited for; matrix products, arithmetic and copies ran while one was open for 12% of the time, Pallas kernels for 76%

profile of v15, /device:TPU:0, one launch (start us, length us, event | category | flops | bytes accessed | tf_op | source)
XLA Modules:
  0.0 458.4 jit_solution(6118965256252242995)
XLA Ops:
  0.7 1.9 constant_dynamic-slice_fusion.9.dy_ref
  2.6 4.0 collective-permute-start.2
  13.4 1.8 dynamic-slice_select_fusion.refs_2_
  19.2 1.8 constant_dynamic-slice_fusion.5.x_ref
  24.8 1.7 constant_dynamic-slice_fusion.7
  28.9 5.0 %collective-permute-done.3.refs_1_ = bf16[768,384]{1,0:T(8,128)(2,1)} collective-permute-done((bf16[768,384]{1,0:T(8,128)(2,1)}, bf16[768,384]{1,0:T(8,128)(2,1)}, u32[]{:S(2)}, u32[]{:S(2)}) %collective-permute-start.3) | collective-permute-done | bytes 589856 | tf_op jit(solution)/shard_map/ppermute | solution.py:1100
  35.9 6.5 %qkv.1 = (bf16[512,1536]{1,0:T(8,128)(2,1)}, f32[512,1]{1,0:T(8,128)}, bf16[512,384]{1,0:T(8,128)(2,1)}, bf16[512,128]{1,0:T(8,128)(2,1)}) custom-call(s32[4]{0:T(128)} %pad_add_fusion.1.meta_ref, bf16[512,1536]{1,0:T(8,128)(2,1)} %x_ref.1, f32[1,1536]{1,0:T(1,128)} %bitcast.87, f32[1,512]{1,0:T(1,128)} %pad_maximum_fusion.6.bias_ref, ...), custom_call_target="tpu_custom_call" | custom-call | tf_op jit(solution)/shard_map/qkv/pallas_call | solution.py:209
  42.3 15.0 %kv_gather.1.k_ref.v_ref = bf16[2,2048,128]{2,1,0:T(8,128)(2,1)} custom-call(bf16[512,128]{1,0:T(8,128)(2,1)} %get-tuple-element.92.own_ref), custom_call_target="tpu_custom_call" | custom-call | tf_op jit(solution)/shard_map/kv_gather/pallas_call | solution.py:642
  57.4 2.5 maximum_select_fusion.3
  64.7 10.2 %attention.1 = (bf16[512,384]{1,0:T(8,128)(2,1)}, f32[3,512,1]{2,1,0:T(8,128)}) custom-call(s32[8]{0:T(128)} %pad_add_fusion.kb_ref, bf16[512,384]{1,0:T(8,128)(2,1)} %get-tuple-element.91.q_ref, bf16[2,2048,128]{2,1,0:T(8,128)(2,1)} %kv_gather.1.k_ref.v_ref, bf16[2,2048,128]{2,1,0:T(8,128)(2,1)} %kv_gather.1.k_ref.v_ref), custom_call_target="tpu_custom_call" | custom-call | tf_op jit(solution)/shard_map/attention/pallas_call | solution.py:85
  74.8 3.5 convolution_convert_fusion
  78.4 62.4 %middle_norm.1 = (f32[128,1536]{1,0:T(8,128)}, f32[128,1]{1,0:T(8,128)}, bf16[16,128,1536]{2,1,0:T(8,128)(2,1)}, bf16[16,128,1536]{2,1,0:T(8,128)(2,1)}) custom-call(bf16[4,128,1536]{2,1,0:T(8,128)(2,1)} %bitcast.79, bf16[128,1536]{1,0:T(8,128)(2,1)} %constant_dynamic-slice_fusion.5.x_ref, f32[1,1536]{1,0:T(1,128)} %bitcast.89, ...), custom_call_target="tpu_custom_call" | custom-call | tf_op jit(solution)/shard_map/middle_norm/pallas_call | solution.py:642
  140.8 29.8 %hidden_units.1 = (bf16[2048,1120]{1,0:T(8,128)(2,1)}, bf16[2048,1120]{1,0:T(8,128)(2,1)}, bf16[2048,1120]{1,0:T(8,128)(2,1)}, bf16[1120,768]{1,0:T(8,128)(2,1)}) custom-call(s32[4]{0:T(128)} %pad_add_fusion.1.meta_ref, bf16[2048,1536]{1,0:T(8,128)(2,1)} %bitcast.70, bf16[2048,1536]{1,0:T(8,128)(2,1)} %bitcast.74, bf16[2240,768]{1,0:T(8,128)(2,1)} %copy-done.2, ...), custom_call_target="tpu_custom_call" | custom-call | tf_op jit(solution)/shard_map/hidden_units/pallas_call | solution.py:333
  170.6 1.8 collective-permute-start.9
  173.6 42.0 %hidden_back.1 = (bf16[2048,1120]{1,0:T(8,128)(2,1)}, bf16[2048,1120]{1,0:T(8,128)(2,1)}, bf16[1024,1536]{1,0:T(8,128)(2,1)}, bf16[1024,1536]{1,0:T(8,128)(2,1)}...) custom-call(s32[4]{0:T(128)} %pad_add_fusion.1.meta_ref, bf16[2048,1536]{1,0:T(8,128)(2,1)} %bitcast.71, ...), custom_call_target="tpu_custom_call" | custom-call | tf_op jit(solution)/shard_map/hidden_back/pallas_call | solution.py:333
  220.4 35.1 %middle_back.1 = (f32[128,1536]{1,0:T(8,128)}, f32[1,1536]{1,0:T(1,128)}, bf16[4,128,1536]{2,1,0:T(8,128)(2,1)}, bf16[1120,768]{1,0:T(8,128)(2,1)}, bf16[1120,76...) custom-call(bf16[8,128,1536]{2,1,0:T(8,128)(2,1)} %bitcast.80, ...), custom_call_target="tpu_custom_call" | custom-call | tf_op jit(solution)/shard_map/middle_back/pallas_call | solution.py:642
  257.5 2.5 add_convert_fusion.1
  260.3 1.7 convolution_convert_fusion.3.do_ref
  262.1 15.1 %attention_back.1 = (bf16[512,384]{1,0:T(8,128)(2,1)}, bf16[2,2048,128]{2,1,0:T(8,128)(2,1)}) custom-call(s32[8]{0:T(128)} %pad_add_fusion.kb_ref, bf16[512,384]{1,0:T(8,128)(2,1)} %get-tuple-element.91.q_ref, bf16[512,384]{1,0:T(8,128)(2,1)} %convolution_convert_fusion.3.do_ref, f32[3,512,1]{2,1,0:T(8,128)} %get-tuple-element.113.lse_ref, ...), custom_call_target="tpu_custom_call" | custom-call | tf_op jit(solution)/shard_map/attention_back/pallas_call | solution.py:151
  277.2 2.6 convolution_convert_fusion.1
  283.1 18.8 %kv_scatter.1 = (f32[512,128]{1,0:T(8,128)}, bf16[1120,768]{1,0:T(8,128)(2,1)}) custom-call(bf16[2,2048,128]{2,1,0:T(8,128)(2,1)} %get-tuple-element.118.part_ref, bf16[2048,1120]{1,0:T(8,128)(2,1)} %get-tuple-element.119.refs_0_, bf16[2048,1536]{1,0:T(8,128)(2,1)} %bitcast.73), custom_call_target="tpu_custom_call" | custom-call | tf_op jit(solution)/shard_map/kv_scatter/pallas_call | solution.py:642
  302.0 2.5 add_convert_fusion
  309.7 4.9 %qkv_back.1 = bf16[512,1536]{1,0:T(8,128)(2,1)} custom-call(s32[4]{0:T(128)} %pad_add_fusion.1.meta_ref, bf16[512,384]{1,0:T(8,128)(2,1)} %get-tuple-element.114.dq_ref, bf16[512,128]{1,0:T(8,128)(2,1)} %copy-done.4, bf16[768,384]{1,0:T(8,128)(2,1)} %refs_0_.3, bf16[768,384]{1,0:T(8,128)(2,1)} %collective-permute-done.3.refs_1_, ...), custom_call_target="tpu_custom_call" | custom-call | tf_op jit(solution)/shard_map/qkv_back/pallas_call | solution.py:242
  315.3 28.7 %input_back.1 = (f32[1,5120]{1,0:T(1,128)}, bf16[4,128,1536]{2,1,0:T(8,128)(2,1)}) custom-call(bf16[4,128,1536]{2,1,0:T(8,128)(2,1)} %bitcast.78, bf16[128,1536]{1,0:T(8,128)(2,1)} %constant_dynamic-slice_fusion.5.x_ref, f32[128,1]{1,0:T(8,128)} %constant_dynamic-slice_fusion.4.factor_ref, f32[1,1536]{1,0:T(1,128)} %bitcast.88, ...), custom_call_target="tpu_custom_call" | custom-call | tf_op jit(solution)/shard_map/input_back/pallas_call | solution.py:642
  343.9 2.7 broadcast_add_fusion
  346.6 4.7 %fusion.1 = f32[2240,768]{1,0:T(8,128)} fusion(bf16[1120,768]{1,0:T(8,128)(2,1)} %collective-permute-done.14, bf16[1120,768]{1,0:T(8,128)(2,1)S(1)} %add_convert_fusion.1, pred[]{:T(512)S(6)} %eq.19), kind=kLoop, calls=%fused_computation.5 | loop fusion | flops 17203200 | bytes 10321921 | tf_op jit(solution)/shard_map/convert_element_type | solution.py:1255
  351.4 5.1 %fusion = f32[2240,768]{1,0:T(8,128)} fusion(bf16[848,768]{1,0:T(8,128)(2,1)} %collective-permute-done.13, bf16[272,768]{1,0:T(8,128)(2,1)S(1)} %copy-done.24, bf16[848,768]{1,0:T(8,128)(2,1)} %get-tuple-element.139, bf16[272,768]{1,0:T(8,128)(2,1)S(1)} %copy-done.23, pred[]{:T(512)S(6)} %eq.19), kind=kLoop, calls=%fused_computation.3 | loop fusion | flops 30965760 | bytes 10321921 | tf_op jit(solution)/shard_map/convert_element_type | solution.py:1255
  356.5 2.2 fusion.4.refs_2_
  358.7 2.5 fusion.3.refs_1_
  361.2 2.4 fusion.2.refs_0_
  363.5 78.3 %context_sum.1 = (f32[384,768]{1,0:T(8,128)}, f32[768,384]{1,0:T(8,128)}, f32[1,5120]{1,0:T(1,128)}, bf16[4,768,128]{2,1,0:T(8,128)(2,1)}, bf16[4,128,1536]{2,1,0:T(8,128)(2,1)}) custom-call(bf16[384,768]{1,0:T(8,128)(2,1)} %fusion.2.refs_0_, bf16[768,384]{1,0:T(8,128)(2,1)} %fusion.3.refs_1_, bf16[768,128]{1,0:T(8,128)(2,1)} %fusion.4.refs_2_, ...), custom_call_target="tpu_custom_call" | custom-call | tf_op jit(solution)/shard_map/context_sum/pallas_call | solution.py:642
  445.2 4.8 %convert_bitcast_fusion = f32[768,2240]{0,1:T(8,128)} fusion(bf16[1120,768]{1,0:T(8,128)(2,1)} %collective-permute-done.17, bf16[1120,768]{1,0:T(8,128)(2,1)S(1)} %add_convert_fusion, pred[]{:T(512)S(6)} %eq.19), kind=kLoop, calls=%fused_computation | loop fusion | flops 17203200 | bytes 10321921 | tf_op jit(solution)/shard_map/transpose | solution.py:1346
  (155 shorter events, 52.6 us)
Async XLA Ops:
  0.6 21.4 %copy-start = (bf16[2240,768]{1,0:T(8,128)(2,1)S(1)}, bf16[2240,768]{1,0:T(8,128)(2,1)}, u32[]{:S(2)}) copy-start(bf16[2240,768]{1,0:T(8,128)(2,1)} %param.29) | copy-start | bytes 10321924
  2.6 33.3 %collective-permute-start.2 = (bf16[128,1536]{1,0:T(8,128)(2,1)}, bf16[128,1536]{1,0:T(8,128)(2,1)}, u32[]{:S(2)}, u32[]{:S(2)}) collective-permute-start(bf16[128,1536]{1,0:T(8,128)(2,1)} %constant_dynamic-slice_fusion.9.dy_ref), channel_id=1, source_target_pairs={{0,8},{4,12},{8,0},{12,4},{1,9},{5,13},{9,1},{13,5},{2,10},{6,14},... | collective-permute-start | bytes 1179656 | tf_op jit(solution)/shard_map/ppermute | solution.py:1100
  6.6 29.2 %collective-permute-start.1 = (bf16[128,1536]{1,0:T(8,128)(2,1)}, bf16[128,1536]{1,0:T(8,128)(2,1)}, u32[]{:S(2)}, u32[]{:S(2)}) collective-permute-start(bf16[128,1536]{1,0:T(8,128)(2,1)} %constant_dynamic-slice_fusion.9.dy_ref), channel_id=1, source_target_pairs={{0,4},{4,0},{8,12},{12,8},{1,5},{5,1},{9,13},{13,9},{2,6},{6,2},{1... | collective-permute-start | bytes 1179656 | tf_op jit(solution)/shard_map/ppermute | solution.py:1100
  11.9 16.7 %collective-permute-start = (bf16[1,1984]{1,0:T(2,128)(2,1)S(1)}, bf16[1,1984]{1,0:T(2,128)(2,1)S(1)}, u32[]{:S(2)}, u32[]{:S(2)}) collective-permute-start(bf16[1,1984]{1,0:T(2,128)(2,1)S(1)} %concatenate.68), channel_id=1, source_target_pairs={{0,16},{16,0},{1,17},{17,1},{2,18},{18,2},{3,19},{19,3},{4,20},{20... | collective-permute-start | bytes 11912 | tf_op jit(solution)/shard_map/ppermute | solution.py:1100
  15.2 13.7 %collective-permute-start.4 = (bf16[768,128]{1,0:T(8,128)(2,1)}, bf16[768,128]{1,0:T(8,128)(2,1)}, u32[]{:S(2)}, u32[]{:S(2)}) collective-permute-start(bf16[768,128]{1,0:T(8,128)(2,1)} %dynamic-slice_select_fusion.refs_2_), channel_id=1, source_target_pairs={{0,16},{16,0},{1,17},{17,1},{2,18},{18,2},{3,19},{19,3},{4,20},{20... | collective-permute-start | bytes 589832 | tf_op jit(solution)/shard_map/ppermute | solution.py:1100
  15.7 18.2 %collective-permute-start.3 = (bf16[768,384]{1,0:T(8,128)(2,1)}, bf16[768,384]{1,0:T(8,128)(2,1)}, u32[]{:S(2)}, u32[]{:S(2)}) collective-permute-start(bf16[768,384]{1,0:T(8,128)(2,1)} %refs_0_.3), channel_id=1, source_target_pairs={{0,16},{16,0},{1,17},{17,1},{2,18},{18,2},{3,19},{19,3},{4,20},{20... | collective-permute-start | bytes 1769480 | tf_op jit(solution)/shard_map/ppermute | solution.py:1100
  22.0 4.7 %copy-start.6 = (f32[512,64]{1,0:T(8,128)}, f32[512,64]{1,0:T(8,128)S(1)}, u32[]{:S(2)}) copy-start(f32[512,64]{1,0:T(8,128)S(1)} %get-tuple-element.176) | copy-start | bytes 393220
  22.0 4.7 %copy-start.8 = (f32[512,64]{1,0:T(8,128)}, f32[512,64]{1,0:T(8,128)S(1)}, u32[]{:S(2)}) copy-start(f32[512,64]{1,0:T(8,128)S(1)} %get-tuple-element.177) | copy-start | bytes 393220
  26.7 33.2 %copy-start.2 = (bf16[2240,768]{1,0:T(8,128)(2,1)}, bf16[2240,768]{1,0:T(8,128)(2,1)S(1)}, u32[]{:S(2)}) copy-start(bf16[2240,768]{1,0:T(8,128)(2,1)S(1)} %pad_maximum_fusion.refs_0_.refs_2_) | copy-start | bytes 10321924
  33.9 23.4 %collective-permute-start.5 = (bf16[384,768]{1,0:T(8,128)(2,1)}, bf16[384,768]{1,0:T(8,128)(2,1)}, u32[]{:S(2)}, u32[]{:S(2)}) collective-permute-start(bf16[384,768]{1,0:T(8,128)(2,1)} %param.25), channel_id=1, source_target_pairs={{0,16},{16,0},{1,17},{17,1},{2,18},{18,2},{3,19},{19,3},{4,20},{20... | collective-permute-start | bytes 1769480 | tf_op jit(solution)/shard_map/ppermute | solution.py:1100
  35.9 21.5 %copy-start.22 = (bf16[384,768]{1,0:T(8,128)(2,1)S(1)}, bf16[384,768]{1,0:T(8,128)(2,1)}, u32[]{:S(2)}) copy-start(bf16[384,768]{1,0:T(8,128)(2,1)} %param.25) | copy-start | bytes 1769476
  59.9 80.9 %collective-permute-start.7 = (bf16[2240,768]{1,0:T(8,128)(2,1)S(1)}, bf16[2240,768]{1,0:T(8,128)(2,1)}, u32[]{:S(2)}, u32[]{:S(2)}) collective-permute-start(bf16[2240,768]{1,0:T(8,128)(2,1)S(1)} %pad_maximum_fusion.refs_0_.refs_2_), channel_id=1, source_target_pairs={{0,16},{16,0},{1,17},{17,1},{2,18},{18,2},{3,19},{19,3},{4,20},{20... | collective-permute-start | bytes 10321928 | tf_op jit(solution)/shard_map/ppermute | solution.py:1100
  61.4 112.1 %collective-permute-start.8 = (bf16[1120,768]{1,0:T(8,128)(2,1)}, bf16[1120,768]{1,0:T(8,128)(2,1)}, u32[]{:S(2)}, u32[]{:S(2)}) collective-permute-start(bf16[1120,768]{1,0:T(8,128)(2,1)} %constant_dynamic-slice_fusion.6.refs_4_), channel_id=1, source_target_pairs={{0,16},{16,0},{1,17},{17,1},{2,18},{18,2},{3,19},{19,3},{4,20},{20... | collective-permute-start | bytes 5160968 | tf_op jit(solution)/shard_map/ppermute | solution.py:1100
  62.0 16.4 %collective-permute-start.6 = (bf16[128,1536]{1,0:T(8,128)(2,1)}, bf16[128,1536]{1,0:T(8,128)(2,1)}, u32[]{:S(2)}, u32[]{:S(2)}) collective-permute-start(bf16[128,1536]{1,0:T(8,128)(2,1)} %constant_dynamic-slice_fusion.9.dy_ref), channel_id=1, source_target_pairs={{0,2},{1,3},{2,0},{3,1},{4,6},{5,7},{6,4},{7,5},{8,10},{9,11},{10,... | collective-permute-start | bytes 1179656 | tf_op jit(solution)/shard_map/ppermute | solution.py:1100
  170.6 48.6 %collective-permute-start.9 = (bf16[1120,768]{1,0:T(8,128)(2,1)}, bf16[1120,768]{1,0:T(8,128)(2,1)S(1)}, u32[]{:S(2)}, u32[]{:S(2)}) collective-permute-start(bf16[1120,768]{1,0:T(8,128)(2,1)} %get-tuple-element.107), channel_id=1, source_target_pairs={{0,16},{16,0},{1,17},{17,1},{2,18},{18,2},{3,19},{19,3},{4,20},{20... | collective-permute-start | bytes 5160968 | tf_op jit(solution)/shard_map/ppermute | solution.py:1100
  215.6 40.8 %collective-permute-start.10 = (bf16[1120,768]{1,0:T(8,128)(2,1)}, bf16[1120,768]{1,0:T(8,128)(2,1)S(1)}, u32[]{:S(2)}, u32[]{:S(2)}) collective-permute-start(bf16[1120,768]{1,0:T(8,128)(2,1)} %get-tuple-element.110), channel_id=1, source_target_pairs={{0,16},{16,0},{1,17},{17,1},{2,18},{18,2},{3,19},{19,3},{4,20},{20... | collective-permute-start | bytes 5160968 | tf_op jit(solution)/shard_map/ppermute | solution.py:1100
  217.1 84.9 %collective-permute-start.12 = (bf16[1120,768]{1,0:T(8,128)(2,1)}, bf16[1120,768]{1,0:T(8,128)(2,1)}, u32[]{:S(2)}, u32[]{:S(2)}) collective-permute-start(bf16[1120,768]{1,0:T(8,128)(2,1)} %get-tuple-element.122), channel_id=1, source_target_pairs={{0,16},{16,0},{1,17},{17,1},{2,18},{18,2},{3,19},{19,3},{4,20},{20... | collective-permute-start | bytes 5160968 | tf_op jit(solution)/shard_map/ppermute | solution.py:1100
  260.1 44.4 %collective-permute-start.13 = (bf16[848,768]{1,0:T(8,128)(2,1)}, bf16[848,768]{1,0:T(8,128)(2,1)}, u32[]{:S(2)}, u32[]{:S(2)}) collective-permute-start(bf16[848,768]{1,0:T(8,128)(2,1)} %get-tuple-element.139), channel_id=1, source_target_pairs={{0,4},{4,0},{8,12},{12,8},{1,5},{5,1},{9,13},{13,9},{2,6},{6,2},{1... | collective-permute-start | bytes 3907592 | tf_op jit(solution)/shard_map/ppermute | solution.py:1100
  262.1 15.1 %copy-start.13 = (bf16[512,1536]{1,0:T(8,128)(2,1)S(1)}, bf16[512,1536]{1,0:T(8,128)(2,1)}, u32[]{:S(2)}) copy-start(bf16[512,1536]{1,0:T(8,128)(2,1)} %get-tuple-element.117) | copy-start | bytes 4718596
  279.8 71.6 %collective-permute-start.15 = (bf16[768,384]{1,0:T(8,128)(2,1)}, bf16[768,384]{1,0:T(8,128)(2,1)}, u32[]{:S(2)}, u32[]{:S(2)}) collective-permute-start(bf16[768,384]{1,0:T(8,128)(2,1)} %convolution_convert_fusion.1), channel_id=1, source_target_pairs={{0,16},{16,0},{1,17},{17,1},{2,18},{18,2},{3,19},{19,3},{4,20},{20... | collective-permute-start | bytes 1769480 | tf_op jit(solution)/shard_map/ppermute | solution.py:1100
  282.5 68.8 %collective-permute-start.11 = (bf16[384,768]{1,0:T(8,128)(2,1)}, bf16[384,768]{1,0:T(8,128)(2,1)}, u32[]{:S(2)}, u32[]{:S(2)}) collective-permute-start(bf16[384,768]{1,0:T(8,128)(2,1)} %convolution_convert_fusion.2), channel_id=1, source_target_pairs={{0,16},{16,0},{1,17},{17,1},{2,18},{18,2},{3,19},{19,3},{4,20},{20... | collective-permute-start | bytes 1769480 | tf_op jit(solution)/shard_map/ppermute | solution.py:1100
  304.8 41.8 %collective-permute-start.14 = (bf16[1120,768]{1,0:T(8,128)(2,1)S(1)}, bf16[1120,768]{1,0:T(8,128)(2,1)}, u32[]{:S(2)}, u32[]{:S(2)}) collective-permute-start(bf16[1120,768]{1,0:T(8,128)(2,1)S(1)} %add_convert_fusion.1), channel_id=1, source_target_pairs={{0,4},{4,0},{8,12},{12,8},{1,5},{5,1},{9,13},{13,9},{2,6},{6,2},{1... | collective-permute-start | bytes 5160968 | tf_op jit(solution)/shard_map/ppermute | solution.py:1100
  307.0 44.3 %collective-permute-start.16 = (bf16[768,128]{1,0:T(8,128)(2,1)}, bf16[768,128]{1,0:T(8,128)(2,1)}, u32[]{:S(2)}, u32[]{:S(2)}) collective-permute-start(bf16[768,128]{1,0:T(8,128)(2,1)} %convolution_convert_fusion.4), channel_id=1, source_target_pairs={{0,16},{16,0},{1,17},{17,1},{2,18},{18,2},{3,19},{19,3},{4,20},{20... | collective-permute-start | bytes 589832 | tf_op jit(solution)/shard_map/ppermute | solution.py:1100
  308.4 6.2 %copy-start.27 = (f32[1,1536]{1,0:T(1,128)S(1)}, f32[1,1536]{1,0:T(1,128)}, u32[]{:S(2)}) copy-start(f32[1,1536]{1,0:T(1,128)} %get-tuple-element.129) | copy-start | bytes 18436
  308.5 133.4 %collective-permute-start.17 = (bf16[1120,768]{1,0:T(8,128)(2,1)S(1)}, bf16[1120,768]{1,0:T(8,128)(2,1)}, u32[]{:S(2)}, u32[]{:S(2)}) collective-permute-start(bf16[1120,768]{1,0:T(8,128)(2,1)S(1)} %add_convert_fusion), channel_id=1, source_target_pairs={{0,4},{4,0},{8,12},{12,8},{1,5},{5,1},{9,13},{13,9},{2,6},{6,2},{1... | collective-permute-start | bytes 5160968 | tf_op jit(solution)/shard_map/ppermute | solution.py:1100
  346.6 4.8 %copy-start.23 = (bf16[272,768]{1,0:T(8,128)(2,1)S(1)}, bf16[272,768]{1,0:T(8,128)(2,1)}, u32[]{:S(2)}) copy-start(bf16[272,768]{1,0:T(8,128)(2,1)} %get-tuple-element.138) | copy-start | bytes 1253380
  346.6 4.8 %copy-start.24 = (bf16[272,768]{1,0:T(8,128)(2,1)S(1)}, bf16[272,768]{1,0:T(8,128)(2,1)}, u32[]{:S(2)}) copy-start(bf16[272,768]{1,0:T(8,128)(2,1)} %get-tuple-element.140) | copy-start | bytes 1253380
  351.3 5.1 %copy-start.5 = (bf16[512,128]{1,0:T(8,128)(2,1)S(1)}, bf16[512,128]{1,0:T(8,128)(2,1)}, u32[]{:S(2)}) copy-start(bf16[512,128]{1,0:T(8,128)(2,1)} %copy-done.4) | copy-start | bytes 393220
  351.3 5.1 %copy-start.15 = (bf16[512,1536]{1,0:T(8,128)(2,1)S(1)}, bf16[512,1536]{1,0:T(8,128)(2,1)}, u32[]{:S(2)}) copy-start(bf16[512,1536]{1,0:T(8,128)(2,1)} %get-tuple-element.117) | copy-start | bytes 4718596
  351.3 7.3 %copy-start.17 = (bf16[512,384]{1,0:T(8,128)(2,1)S(1)}, bf16[512,384]{1,0:T(8,128)(2,1)}, u32[]{:S(2)}) copy-start(bf16[512,384]{1,0:T(8,128)(2,1)} %get-tuple-element.114.dq_ref) | copy-start | bytes 1179652
  356.5 4.7 %copy-start.26 = (bf16[512,384]{1,0:T(8,128)(2,1)S(1)}, bf16[512,384]{1,0:T(8,128)(2,1)}, u32[]{:S(2)}) copy-start(bf16[512,384]{1,0:T(8,128)(2,1)} %get-tuple-element.95) | copy-start | bytes 1179652
  356.5 4.7 %copy-start.30 = (bf16[4,128,1536]{2,1,0:T(8,128)(2,1)S(1)}, bf16[4,128,1536]{2,1,0:T(8,128)(2,1)}, u32[]{:S(2)}) copy-start(bf16[4,128,1536]{2,1,0:T(8,128)(2,1)} %get-tuple-element.108) | copy-start | bytes 4718596
  (17 other events, 42.0 us)

commit v16 on v15

--- a/solution.py
+++ b/solution.py
@@ -175,10 +175,9 @@
 
 
 def qkv_kernel(pieces, meta_ref, x_ref, gain_ref, bias_ref, cos_ref, sin_ref, *refs):
-    weights, (xn_ref, factor_ref, q_ref, kv_ref) = refs[: 2 * pieces], refs[2 * pieces :]
+    weights, (xn_ref, q_ref, kv_ref) = refs[: 2 * pieces], refs[2 * pieces :]
     values = x_ref[...].astype(f32)
     factor = lax.rsqrt(jnp.mean(values * values, axis=-1, keepdims=True) + EPSILON)
-    factor_ref[...] = factor
     xn_ref[...] = (values * factor * gain_ref[...]).astype(bf16)
     depth = weights[0].shape[0]
     normed = [xn_ref[:, columns_of(meta_ref, j, depth, pieces)] for j in range(pieces)]
@@ -214,11 +213,10 @@
             grid=(rows // tile,),
             in_specs=[row(width), fixed(gain), fixed(bias), row(HD), row(HD)]
             + [fixed(w) for w in (*w_q, *w_kv)],
-            out_specs=[row(width), row(1), row(out), row(HD)],
+            out_specs=[row(width), row(out), row(HD)],
         ),
         out_shape=[
             jax.ShapeDtypeStruct((rows, width), bf16),
-            jax.ShapeDtypeStruct((rows, 1), f32),
             jax.ShapeDtypeStruct((rows, out), bf16),
             jax.ShapeDtypeStruct((rows, HD), bf16),
         ],
@@ -649,7 +647,7 @@
         + [
             pltpu.SemaphoreType.DMA((copies,)),
             pltpu.SemaphoreType.DMA((copies,)),
-            pltpu.SemaphoreType.DMA((8,)),
+            pltpu.SemaphoreType.DMA((10,)),
         ],
         compiler_params=pltpu.CompilerParams(
             collective_id=key, has_side_effects=True, vmem_limit_bytes=VMEM_LIMIT
@@ -844,25 +842,29 @@
 
 def middle_back_kernel(count, part, mid_ref, factor_ref, gain_ref, dy_ref, *refs):
     args, refs = refs[: 2 * count], refs[2 * count :]
-    got_ref, refs = (refs[0], refs[1:]) if count else (None, refs)
+    source_ref, refs = (refs[0], refs[1:]) if count else (None, refs)
     (dmid_ref, dgain_ref, out), refs = refs[:3], refs[3:]
     outs, refs = refs[:count], refs[count:]
     (upper_ref, lower_ref, far_ref), refs = (
         (refs[:3], refs[3:]) if count else ((None, None, None), refs)
     )
     low, first, wires, to = refs[0], refs[1:8], Wires(*refs[-3:]), partners()
-    fill = own_grads(count, args, outs, refs[8:-3])
+    fill = own_grads(count, args, outs, refs[8 : 8 + 2 * count])
     meet([to[k] for k in ("core", "y", "z")])
     back = scatter_pair(wires, to, part, *first)
     next(back)
     for one in fill:
         one.fetch(wires)
+    if fill:
+        got_ref = refs[8 + 2 * count]
+        fetched = wires.here(source_ref, got_ref)
     next(back)
     if fill:
         fill[0].make(0, 1)
     next(back)
     if fill:
         fill[0].make(1, fill[0].tiles)
+        fetched.wait()
         cut = upper_ref.shape[0]
         upper_ref[...] = (wide(outs[0][:cut]) + wide(got_ref[:cut])).astype(bf16)
         near_half = wires.copy(upper_ref, far_ref, to["z"])
@@ -900,6 +902,7 @@
     args, outs, scratch = own_grad_call(fill, shard)
     if fill:
         args = [*args, got]
+        scratch = [*scratch, pltpu.VMEM(got.shape, bf16)]
         units = got.shape[0]
         cut = units // 64 * 16
         outs = [*outs, *(jax.ShapeDtypeStruct((n, shard), bf16) for n in (cut, units - cut, cut))]
@@ -917,7 +920,7 @@
         [pltpu.VMEM((rows, width), bf16)] + pair_scratch(rows, width) + scratch,
         16,
         (
-            [False] + [True] * 4 + ([False] * (len(args) - 1) + [True] if fill else []),
+            [False] + [True] * 4 + [False] * len(args),
             [True, True, False] + ([True] * (len(outs) - 1) + [False] if fill else []),
         ),
     )
@@ -932,13 +935,15 @@
 
 
 def input_back_kernel(
-    part, x_ref, factor_ref, gain_ref, dmid_ref, small_ref, sum_ref, out, *rest
+    part, x_ref, gain_ref, dmid_ref, small_ref, sum_ref, out, *rest
 ):
     low, own, core, sent, got, slots = rest[:-3]
     wires, to = Wires(*rest[-3:]), partners()
     meet([to[k] for k in ("core", "y")])
     grad_normed = result_of(scatter_rank(wires, to, part, own, core, sent, got))
-    du, dgain = norm_back_rows(wide(x_ref[...]), factor_ref[...], gain_ref[...], grad_normed)
+    values = wide(x_ref[...])
+    factor = lax.rsqrt(jnp.mean(values * values, axis=-1, keepdims=True) + EPSILON)
+    du, dgain = norm_back_rows(values, factor, gain_ref[...], grad_normed)
     low[...] = (dmid_ref[...] + du).astype(bf16)
     share = gather_rank(wires, to, low, out)
     next(share)
@@ -950,13 +955,13 @@
     wires.finish()
 
 
-def input_back(part, inputs_part, factor, gain, grad_middle, small):
+def input_back(part, inputs_part, gain, grad_middle, small):
     rows, width = inputs_part.shape
     return remote_call(
         input_back_kernel,
         "input_back",
         5,
-        [part.reshape(4, rows, width), inputs_part, factor, gain, grad_middle, small],
+        [part.reshape(4, rows, width), inputs_part, gain, grad_middle, small],
         [
             jax.ShapeDtypeStruct(small.shape, f32),
             jax.ShapeDtypeStruct((4, rows, width), bf16),
@@ -970,7 +975,7 @@
             pltpu.VMEM((2,) + small.shape, f32),
         ],
         16,
-        ([False, True, True, True, True, True], [True, False]),
+        ([False, True, True, True, True], [True, False]),
     )
 
 
@@ -1218,7 +1223,7 @@
         ]
         inputs_part = lax.dynamic_slice_in_dim(inputs, t * part, part, 0)
         bias = after(bias, dy_blocks[2:], own_gate_up, own_down, inputs_part)
-        normed, factor_first, queries, kv_own = qkv(
+        normed, queries, kv_own = qkv(
             meta, inputs, gain_first, bias, cosine, sine, w_q, w_kv
         )
         kv = after(kv_gather(kv_own), w_out_all)
@@ -1280,14 +1285,8 @@
         )
         (up_own,) = last_owns or owns[2:]
         far_gate = flip(after(gate_low, dkv, far_lower), "context", 1)
-        up_got = after(up_got, dkv)
-        up_low = add(up_own, up_got)
-        dkv = after(dkv, up_low, far_lower)
+        dkv = after(dkv, far_lower)
         dkv_low = jnp.where(core == 0, rotate_back(dkv, cosine, sine), dkv).astype(bf16)
-        attention_args.append((normed, dkv_low, 0))
-        fars.append(grad_far(*attention_args[-1]))
-        dkv_low = after(dkv_low, fars)
-        factor_part = lax.dynamic_slice_in_dim(factor_first, t * part, part, 0)
         own_biases = jnp.sum(
             jnp.concatenate([dq_low, dkv_low], axis=1).astype(f32), axis=0, keepdims=True
         )
@@ -1298,11 +1297,13 @@
             [jnp.zeros((1, width), f32), ffn_gain_grad, slots.reshape(1, -1)], axis=1
         )
         grad_qkv = qkv_back(meta, dq_low, dkv_low, w_q, w_kv)
-        far_up = flip(after(up_low, dkv_low), "context", 1)
+        up_low = add(up_own, after(up_got, grad_qkv))
+        attention_args.append((after(normed, grad_qkv), dkv_low, 0))
+        fars.append(grad_far(*attention_args[-1]))
+        far_up = flip(up_low, "context", 1)
         small_grads, input_grad = input_back(
-            grad_qkv,
+            after(grad_qkv, up_low, fars),
             inputs_part,
-            factor_part,
             gain_first,
             grad_middle,
             small_grads,
@@ -1330,9 +1331,8 @@
             (wo_grad, wq_grad, packed, wkv_all, outputs, far_up)
         )
         outputs = outputs.reshape(rows, width)
-        wkv_all = wkv_all.astype(f32)
-        wk_grad = jnp.concatenate([wkv_all[0], wkv_all[2]], axis=1)
-        wv_grad = jnp.concatenate([wkv_all[1], wkv_all[3]], axis=1)
+        wk_grad = jnp.concatenate([wkv_all[0], wkv_all[2]], axis=1).astype(f32)
+        wv_grad = jnp.concatenate([wkv_all[1], wkv_all[3]], axis=1).astype(f32)
         packed = packed[0]
         attn_gain_grad = lax.dynamic_slice_in_dim(packed, f * piece, piece, 0)
         ffn_gain_grad = lax.dynamic_slice_in_dim(packed, width + f * piece, piece, 0)

time: 462 us -> 456 us (0.987)
  Pallas kernels: 347 us -> 342 us
    pallas_call x6, Pallas kernels: 238 us -> 233 us  [remote_call(): pl.pallas_call(kernel, name=name, out_shape=outs, in_specs=[spec(x) for x...]
    unnamed x70 -> x78, local copies, waits for them, and re-layouts: 11.4 us -> 10.7 us
where the time goes in v16:
time: 456 us; the launch traced here: 452 us
  Pallas kernels  342 us (75%)
  other arithmetic  35.9 us (8%)
  local copies, waits for them, and re-layouts  23.9 us (5%)
  starting transfers between devices  22.6 us (5%)
  matrix products  17.3 us (4%)
  waiting for transfers between devices  9.32 us (2%)
    pallas_call x6, Pallas kernels, remote_call(): pl.pallas_call(kernel, name=name, out_shape=outs, in_specs=[spec(x) for x...  233 us
    pallas_call x2, Pallas kernels, hidden_call(): pl.pallas_call(kernel, name=name, grid_spec=pltpu.PrefetchScalarGridSpec(...  71.8 us
    ppermute x18, starting transfers between devices, flip(): return lax.ppermute(x, axis, [(i, i ^ bit) for i in range(size)])  22.6 us
    pallas_call x1, Pallas kernels, attention_back(): pl.pallas_call(functools.partial(attention_back_kernel, kv.shape[1] // BL...  15.1 us
    dot_general x6, matrix products, dot_rows(): lax.dot_general(left, right, (((0,), (0,)), ((), ())), preferred_element_...  12 us
    unnamed x78, local copies, waits for them, and re-layouts  10.7 us
    pallas_call x1, Pallas kernels, attention(): pl.pallas_call(functools.partial(attention_kernel, kv.shape[1] // BLOCK),...  10.2 us
    convert_element_type x2, other arithmetic, unit_whole(): return by_bit(parity, own, other, 0).astype(f32)  9.41 us
  transfers between devices with their start and end apart: 18, of which 3 were waited for; matrix products, arithmetic and copies ran while one was open for 12% of the time, Pallas kernels for 76%

profile of v16, /device:TPU:0, one launch (start us, length us, event | category | flops | bytes accessed | tf_op | source)
XLA Modules:
  0.0 451.9 jit_solution(17424095672202106230)
XLA Ops:
  0.7 1.9 constant_dynamic-slice_fusion.8.dy_ref
  2.6 3.0 collective-permute-start.1
  5.6 2.6 collective-permute-start.2
  13.4 1.8 dynamic-slice_select_fusion.refs_2_
  17.2 1.8 constant_dynamic-slice_fusion.4.x_ref
  28.8 5.2 %collective-permute-done.3.refs_1_ = bf16[768,384]{1,0:T(8,128)(2,1)} collective-permute-done((bf16[768,384]{1,0:T(8,128)(2,1)}, bf16[768,384]{1,0:T(8,128)(2,1)}, u32[]{:S(2)}, u32[]{:S(2)}) %collective-permute-start.3) | collective-permute-done | bytes 589856 | tf_op jit(solution)/shard_map/ppermute | solution.py:1105
  35.9 6.5 %qkv.1 = (bf16[512,1536]{1,0:T(8,128)(2,1)}, bf16[512,384]{1,0:T(8,128)(2,1)}, bf16[512,128]{1,0:T(8,128)(2,1)}) custom-call(s32[4]{0:T(128)} %pad_add_fusion.1.meta_ref, bf16[512,1536]{1,0:T(8,128)(2,1)} %x_ref.1, f32[1,1536]{1,0:T(1,128)} %bitcast.87, f32[1,512]{1,0:T(1,128)} %pad_maximum_fusion.4.bias_ref, f32[512,128]{1,0:T(8,128)} %get-tuple-element.181.cos_ref, ...), custom_call_target="tpu_custom_call" | custom-call | tf_op jit(solution)/shard_map/qkv/pallas_call | solution.py:208
  42.4 15.0 %kv_gather.1.k_ref.v_ref = bf16[2,2048,128]{2,1,0:T(8,128)(2,1)} custom-call(bf16[512,128]{1,0:T(8,128)(2,1)} %get-tuple-element.91.own_ref), custom_call_target="tpu_custom_call" | custom-call | tf_op jit(solution)/shard_map/kv_gather/pallas_call | solution.py:640
  57.4 2.5 maximum_select_fusion.3
  64.7 10.2 %attention.1 = (bf16[512,384]{1,0:T(8,128)(2,1)}, f32[3,512,1]{2,1,0:T(8,128)}) custom-call(s32[8]{0:T(128)} %pad_add_fusion.kb_ref, bf16[512,384]{1,0:T(8,128)(2,1)} %get-tuple-element.90.q_ref, bf16[2,2048,128]{2,1,0:T(8,128)(2,1)} %kv_gather.1.k_ref.v_ref, bf16[2,2048,128]{2,1,0:T(8,128)(2,1)} %kv_gather.1.k_ref.v_ref), custom_call_target="tpu_custom_call" | custom-call | tf_op jit(solution)/shard_map/attention/pallas_call | solution.py:85
  74.8 3.5 convolution_convert_fusion
  78.4 62.4 %middle_norm.1 = (f32[128,1536]{1,0:T(8,128)}, f32[128,1]{1,0:T(8,128)}, bf16[16,128,1536]{2,1,0:T(8,128)(2,1)}, bf16[16,128,1536]{2,1,0:T(8,128)(2,1)}) custom-call(bf16[4,128,1536]{2,1,0:T(8,128)(2,1)} %bitcast.79, bf16[128,1536]{1,0:T(8,128)(2,1)} %constant_dynamic-slice_fusion.4.x_ref, f32[1,1536]{1,0:T(1,128)} %bitcast.89, ...), custom_call_target="tpu_custom_call" | custom-call | tf_op jit(solution)/shard_map/middle_norm/pallas_call | solution.py:640
  140.8 29.7 %hidden_units.1 = (bf16[2048,1120]{1,0:T(8,128)(2,1)}, bf16[2048,1120]{1,0:T(8,128)(2,1)}, bf16[2048,1120]{1,0:T(8,128)(2,1)}, bf16[1120,768]{1,0:T(8,128)(2,1)}) custom-call(s32[4]{0:T(128)} %pad_add_fusion.1.meta_ref, bf16[2048,1536]{1,0:T(8,128)(2,1)} %bitcast.70, bf16[2048,1536]{1,0:T(8,128)(2,1)} %bitcast.74, bf16[2240,768]{1,0:T(8,128)(2,1)} %copy-done.2, ...), custom_call_target="tpu_custom_call" | custom-call | tf_op jit(solution)/shard_map/hidden_units/pallas_call | solution.py:331
  173.6 42.0 %hidden_back.1 = (bf16[2048,1120]{1,0:T(8,128)(2,1)}, bf16[2048,1120]{1,0:T(8,128)(2,1)}, bf16[1024,1536]{1,0:T(8,128)(2,1)}, bf16[1024,1536]{1,0:T(8,128)(2,1)}...) custom-call(s32[4]{0:T(128)} %pad_add_fusion.1.meta_ref, bf16[2048,1536]{1,0:T(8,128)(2,1)} %bitcast.71, ...), custom_call_target="tpu_custom_call" | custom-call | tf_op jit(solution)/shard_map/hidden_back/pallas_call | solution.py:331
  218.9 34.6 %middle_back.1 = (f32[128,1536]{1,0:T(8,128)}, f32[1,1536]{1,0:T(1,128)}, bf16[4,128,1536]{2,1,0:T(8,128)(2,1)}, bf16[1120,768]{1,0:T(8,128)(2,1)}, bf16[1120,76...) custom-call(bf16[8,128,1536]{2,1,0:T(8,128)(2,1)} %bitcast.80, ...), custom_call_target="tpu_custom_call" | custom-call | tf_op jit(solution)/shard_map/middle_back/pallas_call | solution.py:640
  253.6 2.8 collective-permute-done.10
  257.6 2.5 add_convert_fusion.1
  262.2 15.1 %attention_back.1 = (bf16[512,384]{1,0:T(8,128)(2,1)}, bf16[2,2048,128]{2,1,0:T(8,128)(2,1)}) custom-call(s32[8]{0:T(128)} %pad_add_fusion.kb_ref, bf16[512,384]{1,0:T(8,128)(2,1)} %get-tuple-element.90.q_ref, bf16[512,384]{1,0:T(8,128)(2,1)} %convolution_convert_fusion.3.do_ref, f32[3,512,1]{2,1,0:T(8,128)} %get-tuple-element.112.lse_ref, ...), custom_call_target="tpu_custom_call" | custom-call | tf_op jit(solution)/shard_map/attention_back/pallas_call | solution.py:151
  277.3 2.6 convolution_convert_fusion.1
  283.2 18.8 %kv_scatter.1 = (f32[512,128]{1,0:T(8,128)}, bf16[1120,768]{1,0:T(8,128)(2,1)}) custom-call(bf16[2,2048,128]{2,1,0:T(8,128)(2,1)} %get-tuple-element.117.part_ref, bf16[2048,1120]{1,0:T(8,128)(2,1)} %get-tuple-element.118.refs_0_, bf16[2048,1536]{1,0:T(8,128)(2,1)} %bitcast.73), custom_call_target="tpu_custom_call" | custom-call | tf_op jit(solution)/shard_map/kv_scatter/pallas_call | solution.py:640
  304.3 4.8 %qkv_back.1 = bf16[512,1536]{1,0:T(8,128)(2,1)} custom-call(s32[4]{0:T(128)} %pad_add_fusion.1.meta_ref, bf16[512,384]{1,0:T(8,128)(2,1)} %get-tuple-element.113.dq_ref, bf16[512,128]{1,0:T(8,128)(2,1)} %fusion.18.dkv_ref, bf16[768,384]{1,0:T(8,128)(2,1)} %refs_0_.3, bf16[768,384]{1,0:T(8,128)(2,1)} %collective-permute-done.3.refs_1_, ...), custom_call_target="tpu_custom_call" | custom-call | tf_op jit(solution)/shard_map/qkv_back/pallas_call | solution.py:240
  311.5 2.5 add_convert_fusion
  313.9 2.0 collective-permute-start.17
  317.1 28.7 %input_back.1 = (f32[1,5120]{1,0:T(1,128)}, bf16[4,128,1536]{2,1,0:T(8,128)(2,1)}) custom-call(bf16[4,128,1536]{2,1,0:T(8,128)(2,1)} %bitcast.78, bf16[128,1536]{1,0:T(8,128)(2,1)} %constant_dynamic-slice_fusion.4.x_ref, f32[1,1536]{1,0:T(1,128)} %bitcast.88, f32[128,1536]{1,0:T(8,128)} %get-tuple-element.127.dmid_ref, f32[1,5120]{1,0:T(1,128)} %pad_maximum_fusion.3.small_ref), custom_call_target="tpu_custom_call" | custom-call | tf_op jit(solution)/shard_map/input_back/pallas_call | solution.py:640
  345.8 2.8 broadcast_add_fusion
  348.6 4.6 %fusion = f32[2240,768]{1,0:T(8,128)} fusion(bf16[848,768]{1,0:T(8,128)(2,1)} %collective-permute-done.12, bf16[272,768]{1,0:T(8,128)(2,1)S(1)} %copy-done.26, bf16[848,768]{1,0:T(8,128)(2,1)S(1)} %copy-done.18, bf16[272,768]{1,0:T(8,128)(2,1)S(1)} %copy-done.25, pred[]{:T(512)S(6)} %eq.19), kind=kLoop, calls=%fused_computation.3 | loop fusion | flops 30965760 | bytes 10321921 | tf_op jit(solution)/shard_map/convert_element_type | solution.py:1260
  353.2 4.8 %fusion.1 = f32[2240,768]{1,0:T(8,128)} fusion(bf16[1120,768]{1,0:T(8,128)(2,1)} %collective-permute-done.14, bf16[1120,768]{1,0:T(8,128)(2,1)S(1)} %add_convert_fusion.1, pred[]{:T(512)S(6)} %eq.19), kind=kLoop, calls=%fused_computation.5 | loop fusion | flops 17203200 | bytes 10321921 | tf_op jit(solution)/shard_map/convert_element_type | solution.py:1260
  358.1 2.2 fusion.9.refs_2_
  360.2 2.5 fusion.3.refs_1_
  362.7 2.4 fusion.2.refs_0_
  365.1 73.7 %context_sum.1 = (f32[384,768]{1,0:T(8,128)}, f32[768,384]{1,0:T(8,128)}, f32[1,5120]{1,0:T(1,128)}, bf16[4,768,128]{2,1,0:T(8,128)(2,1)}, bf16[4,128,1536]{2,1,0:T(8,128)(2,1)}) custom-call(bf16[384,768]{1,0:T(8,128)(2,1)} %fusion.2.refs_0_, bf16[768,384]{1,0:T(8,128)(2,1)} %fusion.3.refs_1_, bf16[768,128]{1,0:T(8,128)(2,1)} %fusion.9.refs_2_, ...), custom_call_target="tpu_custom_call" | custom-call | tf_op jit(solution)/shard_map/context_sum/pallas_call | solution.py:640
  438.8 4.8 %convert_bitcast_fusion = f32[768,2240]{0,1:T(8,128)} fusion(bf16[1120,768]{1,0:T(8,128)(2,1)} %collective-permute-done.17, bf16[1120,768]{1,0:T(8,128)(2,1)S(1)} %add_convert_fusion, pred[]{:T(512)S(6)} %eq.19), kind=kLoop, calls=%fused_computation | loop fusion | flops 17203200 | bytes 10321921 | tf_op jit(solution)/shard_map/transpose | solution.py:1346
  (161 shorter events, 50.2 us)
Async XLA Ops:
  0.6 19.8 %copy-start = (bf16[2240,768]{1,0:T(8,128)(2,1)S(1)}, bf16[2240,768]{1,0:T(8,128)(2,1)}, u32[]{:S(2)}) copy-start(bf16[2240,768]{1,0:T(8,128)(2,1)} %param.29) | copy-start | bytes 10321924
  0.7 18.9 %copy-start.34 = (s32[1,8]{1,0:T(1,128)S(1)}, s32[1,8]{1,0:T(1,128)}, u32[]{:S(2)}) copy-start(s32[1,8]{1,0:T(1,128)} %param.17) | copy-start | bytes 100
  2.6 33.3 %collective-permute-start.1 = (bf16[128,1536]{1,0:T(8,128)(2,1)}, bf16[128,1536]{1,0:T(8,128)(2,1)}, u32[]{:S(2)}, u32[]{:S(2)}) collective-permute-start(bf16[128,1536]{1,0:T(8,128)(2,1)} %constant_dynamic-slice_fusion.8.dy_ref), channel_id=1, source_target_pairs={{0,4},{4,0},{8,12},{12,8},{1,5},{5,1},{9,13},{13,9},{2,6},{6,2},{1... | collective-permute-start | bytes 1179656 | tf_op jit(solution)/shard_map/ppermute | solution.py:1105
  5.6 30.3 %collective-permute-start.2 = (bf16[128,1536]{1,0:T(8,128)(2,1)}, bf16[128,1536]{1,0:T(8,128)(2,1)}, u32[]{:S(2)}, u32[]{:S(2)}) collective-permute-start(bf16[128,1536]{1,0:T(8,128)(2,1)} %constant_dynamic-slice_fusion.8.dy_ref), channel_id=1, source_target_pairs={{0,8},{4,12},{8,0},{12,4},{1,9},{5,13},{9,1},{13,5},{2,10},{6,14},... | collective-permute-start | bytes 1179656 | tf_op jit(solution)/shard_map/ppermute | solution.py:1105
  11.9 16.6 %collective-permute-start = (bf16[1,1984]{1,0:T(2,128)(2,1)S(1)}, bf16[1,1984]{1,0:T(2,128)(2,1)S(1)}, u32[]{:S(2)}, u32[]{:S(2)}) collective-permute-start(bf16[1,1984]{1,0:T(2,128)(2,1)S(1)} %concatenate.68), channel_id=1, source_target_pairs={{0,16},{16,0},{1,17},{17,1},{2,18},{18,2},{3,19},{19,3},{4,20},{20... | collective-permute-start | bytes 11912 | tf_op jit(solution)/shard_map/ppermute | solution.py:1105
  15.2 13.6 %collective-permute-start.4 = (bf16[768,128]{1,0:T(8,128)(2,1)}, bf16[768,128]{1,0:T(8,128)(2,1)}, u32[]{:S(2)}, u32[]{:S(2)}) collective-permute-start(bf16[768,128]{1,0:T(8,128)(2,1)} %dynamic-slice_select_fusion.refs_2_), channel_id=1, source_target_pairs={{0,16},{16,0},{1,17},{17,1},{2,18},{18,2},{3,19},{19,3},{4,20},{20... | collective-permute-start | bytes 589832 | tf_op jit(solution)/shard_map/ppermute | solution.py:1105
  15.7 18.2 %collective-permute-start.3 = (bf16[768,384]{1,0:T(8,128)(2,1)}, bf16[768,384]{1,0:T(8,128)(2,1)}, u32[]{:S(2)}, u32[]{:S(2)}) collective-permute-start(bf16[768,384]{1,0:T(8,128)(2,1)} %refs_0_.3), channel_id=1, source_target_pairs={{0,16},{16,0},{1,17},{17,1},{2,18},{18,2},{3,19},{19,3},{4,20},{20... | collective-permute-start | bytes 1769480 | tf_op jit(solution)/shard_map/ppermute | solution.py:1105
  24.9 35.0 %copy-start.2 = (bf16[2240,768]{1,0:T(8,128)(2,1)}, bf16[2240,768]{1,0:T(8,128)(2,1)S(1)}, u32[]{:S(2)}) copy-start(bf16[2240,768]{1,0:T(8,128)(2,1)S(1)} %pad_maximum_fusion.refs_0_.refs_2_) | copy-start | bytes 10321924
  34.0 23.4 %collective-permute-start.5 = (bf16[384,768]{1,0:T(8,128)(2,1)}, bf16[384,768]{1,0:T(8,128)(2,1)}, u32[]{:S(2)}, u32[]{:S(2)}) collective-permute-start(bf16[384,768]{1,0:T(8,128)(2,1)} %param.25), channel_id=1, source_target_pairs={{0,16},{16,0},{1,17},{17,1},{2,18},{18,2},{3,19},{19,3},{4,20},{20... | collective-permute-start | bytes 1769480 | tf_op jit(solution)/shard_map/ppermute | solution.py:1105
  35.9 21.5 %copy-start.24 = (bf16[384,768]{1,0:T(8,128)(2,1)S(1)}, bf16[384,768]{1,0:T(8,128)(2,1)}, u32[]{:S(2)}) copy-start(bf16[384,768]{1,0:T(8,128)(2,1)} %param.25) | copy-start | bytes 1769476
  59.9 80.9 %collective-permute-start.7 = (bf16[2240,768]{1,0:T(8,128)(2,1)S(1)}, bf16[2240,768]{1,0:T(8,128)(2,1)}, u32[]{:S(2)}, u32[]{:S(2)}) collective-permute-start(bf16[2240,768]{1,0:T(8,128)(2,1)S(1)} %pad_maximum_fusion.refs_0_.refs_2_), channel_id=1, source_target_pairs={{0,16},{16,0},{1,17},{17,1},{2,18},{18,2},{3,19},{19,3},{4,20},{20... | collective-permute-start | bytes 10321928 | tf_op jit(solution)/shard_map/ppermute | solution.py:1105
  61.5 112.1 %collective-permute-start.8 = (bf16[1120,768]{1,0:T(8,128)(2,1)}, bf16[1120,768]{1,0:T(8,128)(2,1)}, u32[]{:S(2)}, u32[]{:S(2)}) collective-permute-start(bf16[1120,768]{1,0:T(8,128)(2,1)} %constant_dynamic-slice_fusion.5.refs_4_), channel_id=1, source_target_pairs={{0,16},{16,0},{1,17},{17,1},{2,18},{18,2},{3,19},{19,3},{4,20},{20... | collective-permute-start | bytes 5160968 | tf_op jit(solution)/shard_map/ppermute | solution.py:1105
  62.0 16.4 %collective-permute-start.6 = (bf16[128,1536]{1,0:T(8,128)(2,1)}, bf16[128,1536]{1,0:T(8,128)(2,1)}, u32[]{:S(2)}, u32[]{:S(2)}) collective-permute-start(bf16[128,1536]{1,0:T(8,128)(2,1)} %constant_dynamic-slice_fusion.8.dy_ref), channel_id=1, source_target_pairs={{0,2},{1,3},{2,0},{3,1},{4,6},{5,7},{6,4},{7,5},{8,10},{9,11},{10,... | collective-permute-start | bytes 1179656 | tf_op jit(solution)/shard_map/ppermute | solution.py:1105
  170.6 47.2 %collective-permute-start.9 = (bf16[1120,768]{1,0:T(8,128)(2,1)}, bf16[1120,768]{1,0:T(8,128)(2,1)S(1)}, u32[]{:S(2)}, u32[]{:S(2)}) collective-permute-start(bf16[1120,768]{1,0:T(8,128)(2,1)} %get-tuple-element.106), channel_id=1, source_target_pairs={{0,16},{16,0},{1,17},{17,1},{2,18},{18,2},{3,19},{19,3},{4,20},{20... | collective-permute-start | bytes 5160968 | tf_op jit(solution)/shard_map/ppermute | solution.py:1105
  215.6 40.8 %collective-permute-start.10 = (bf16[1120,768]{1,0:T(8,128)(2,1)}, bf16[1120,768]{1,0:T(8,128)(2,1)S(1)}, u32[]{:S(2)}, u32[]{:S(2)}) collective-permute-start(bf16[1120,768]{1,0:T(8,128)(2,1)} %get-tuple-element.109), channel_id=1, source_target_pairs={{0,16},{16,0},{1,17},{17,1},{2,18},{18,2},{3,19},{19,3},{4,20},{20... | collective-permute-start | bytes 5160968 | tf_op jit(solution)/shard_map/ppermute | solution.py:1105
  217.1 93.1 %collective-permute-start.13 = (bf16[1120,768]{1,0:T(8,128)(2,1)}, bf16[1120,768]{1,0:T(8,128)(2,1)}, u32[]{:S(2)}, u32[]{:S(2)}) collective-permute-start(bf16[1120,768]{1,0:T(8,128)(2,1)} %get-tuple-element.123), channel_id=1, source_target_pairs={{0,16},{16,0},{1,17},{17,1},{2,18},{18,2},{3,19},{19,3},{4,20},{20... | collective-permute-start | bytes 5160968 | tf_op jit(solution)/shard_map/ppermute | solution.py:1105
  256.4 45.7 %collective-permute-start.12 = (bf16[848,768]{1,0:T(8,128)(2,1)}, bf16[848,768]{1,0:T(8,128)(2,1)}, u32[]{:S(2)}, u32[]{:S(2)}) collective-permute-start(bf16[848,768]{1,0:T(8,128)(2,1)} %get-tuple-element.138), channel_id=1, source_target_pairs={{0,4},{4,0},{8,12},{12,8},{1,5},{5,1},{9,13},{13,9},{2,6},{6,2},{1... | collective-permute-start | bytes 3907592 | tf_op jit(solution)/shard_map/ppermute | solution.py:1105
  262.2 15.1 %copy-start.13 = (bf16[512,1536]{1,0:T(8,128)(2,1)S(1)}, bf16[512,1536]{1,0:T(8,128)(2,1)}, u32[]{:S(2)}) copy-start(bf16[512,1536]{1,0:T(8,128)(2,1)} %get-tuple-element.125) | copy-start | bytes 4718596
  279.8 78.2 %collective-permute-start.15 = (bf16[768,384]{1,0:T(8,128)(2,1)}, bf16[768,384]{1,0:T(8,128)(2,1)}, u32[]{:S(2)}, u32[]{:S(2)}) collective-permute-start(bf16[768,384]{1,0:T(8,128)(2,1)} %convolution_convert_fusion.1), channel_id=1, source_target_pairs={{0,16},{16,0},{1,17},{17,1},{2,18},{18,2},{3,19},{19,3},{4,20},{20... | collective-permute-start | bytes 1769480 | tf_op jit(solution)/shard_map/ppermute | solution.py:1105
  282.6 75.5 %collective-permute-start.11 = (bf16[384,768]{1,0:T(8,128)(2,1)}, bf16[384,768]{1,0:T(8,128)(2,1)}, u32[]{:S(2)}, u32[]{:S(2)}) collective-permute-start(bf16[384,768]{1,0:T(8,128)(2,1)} %convolution_convert_fusion.2), channel_id=1, source_target_pairs={{0,16},{16,0},{1,17},{17,1},{2,18},{18,2},{3,19},{19,3},{4,20},{20... | collective-permute-start | bytes 1769480 | tf_op jit(solution)/shard_map/ppermute | solution.py:1105
  283.2 19.0 %copy-start.7 = (f32[512,64]{1,0:T(8,128)S(1)}, f32[512,64]{1,0:T(8,128)}, u32[]{:S(2)}) copy-start(f32[512,64]{1,0:T(8,128)} %copy-done.6) | copy-start | bytes 393220
  302.1 46.5 %collective-permute-start.14 = (bf16[1120,768]{1,0:T(8,128)(2,1)S(1)}, bf16[1120,768]{1,0:T(8,128)(2,1)}, u32[]{:S(2)}, u32[]{:S(2)}) collective-permute-start(bf16[1120,768]{1,0:T(8,128)(2,1)S(1)} %add_convert_fusion.1), channel_id=1, source_target_pairs={{0,4},{4,0},{8,12},{12,8},{1,5},{5,1},{9,13},{13,9},{2,6},{6,2},{1... | collective-permute-start | bytes 5160968 | tf_op jit(solution)/shard_map/ppermute | solution.py:1105
  304.3 4.8 %copy-start.4 = (bf16[512,128]{1,0:T(8,128)(2,1)S(1)}, bf16[512,128]{1,0:T(8,128)(2,1)}, u32[]{:S(2)}) copy-start(bf16[512,128]{1,0:T(8,128)(2,1)} %fusion.18.dkv_ref) | copy-start | bytes 393220
  304.3 4.8 %copy-start.14 = (bf16[512,1536]{1,0:T(8,128)(2,1)S(1)}, bf16[512,1536]{1,0:T(8,128)(2,1)}, u32[]{:S(2)}) copy-start(bf16[512,1536]{1,0:T(8,128)(2,1)} %get-tuple-element.125) | copy-start | bytes 4718596
  310.3 47.8 %collective-permute-start.16 = (bf16[768,128]{1,0:T(8,128)(2,1)}, bf16[768,128]{1,0:T(8,128)(2,1)}, u32[]{:S(2)}, u32[]{:S(2)}) collective-permute-start(bf16[768,128]{1,0:T(8,128)(2,1)} %convolution_convert_fusion.4), channel_id=1, source_target_pairs={{0,16},{16,0},{1,17},{17,1},{2,18},{18,2},{3,19},{19,3},{4,20},{20... | collective-permute-start | bytes 589832 | tf_op jit(solution)/shard_map/ppermute | solution.py:1105
  311.5 4.9 %copy-start.30 = (f32[1,1536]{1,0:T(1,128)S(1)}, f32[1,1536]{1,0:T(1,128)}, u32[]{:S(2)}) copy-start(f32[1,1536]{1,0:T(1,128)} %get-tuple-element.128) | copy-start | bytes 18436
  313.9 124.9 %collective-permute-start.17 = (bf16[1120,768]{1,0:T(8,128)(2,1)S(1)}, bf16[1120,768]{1,0:T(8,128)(2,1)}, u32[]{:S(2)}, u32[]{:S(2)}) collective-permute-start(bf16[1120,768]{1,0:T(8,128)(2,1)S(1)} %add_convert_fusion), channel_id=1, source_target_pairs={{0,4},{4,0},{8,12},{12,8},{1,5},{5,1},{9,13},{13,9},{2,6},{6,2},{1... | collective-permute-start | bytes 5160968 | tf_op jit(solution)/shard_map/ppermute | solution.py:1105
  353.2 4.8 %copy-start.5 = (bf16[512,128]{1,0:T(8,128)(2,1)S(1)}, bf16[512,128]{1,0:T(8,128)(2,1)}, u32[]{:S(2)}) copy-start(bf16[512,128]{1,0:T(8,128)(2,1)} %fusion.18.dkv_ref) | copy-start | bytes 393220
  353.2 4.9 %copy-start.15 = (bf16[512,1536]{1,0:T(8,128)(2,1)S(1)}, bf16[512,1536]{1,0:T(8,128)(2,1)}, u32[]{:S(2)}) copy-start(bf16[512,1536]{1,0:T(8,128)(2,1)} %get-tuple-element.125) | copy-start | bytes 4718596
  353.2 7.0 %copy-start.17 = (bf16[512,384]{1,0:T(8,128)(2,1)S(1)}, bf16[512,384]{1,0:T(8,128)(2,1)}, u32[]{:S(2)}) copy-start(bf16[512,384]{1,0:T(8,128)(2,1)} %get-tuple-element.113.dq_ref) | copy-start | bytes 1179652
  438.8 4.8 %copy-start.23 = (bf16[4,768,128]{2,1,0:T(8,128)(2,1)S(1)}, bf16[4,768,128]{2,1,0:T(8,128)(2,1)}, u32[]{:S(2)}) copy-start(bf16[4,768,128]{2,1,0:T(8,128)(2,1)} %get-tuple-element.155) | copy-start | bytes 2359300
  438.8 4.8 %copy-start.29 = (f32[1,5120]{1,0:T(1,128)S(1)}, f32[1,5120]{1,0:T(1,128)}, u32[]{:S(2)}) copy-start(f32[1,5120]{1,0:T(1,128)} %get-tuple-element.153) | copy-start | bytes 61444
  (21 other events, 55.7 us)

commit v17 on v16

--- a/solution.py
+++ b/solution.py
@@ -636,7 +636,8 @@
 
 def remote_call(kernel, name, key, args, outs, scratch, copies, in_vmem):
     ins, out_in = in_vmem
-    spec = lambda inside: pl.BlockSpec(memory_space=pltpu.VMEM if inside else pl.ANY)
+    spaces = {True: pltpu.VMEM, False: pl.ANY, None: pltpu.HBM}
+    spec = lambda inside: pl.BlockSpec(memory_space=spaces[inside])
     return pl.pallas_call(
         kernel,
         name=name,
@@ -920,7 +921,7 @@
         [pltpu.VMEM((rows, width), bf16)] + pair_scratch(rows, width) + scratch,
         16,
         (
-            [False] + [True] * 4 + [False] * len(args),
+            [False] + [True] * 4 + [None] * len(args),
             [True, True, False] + ([True] * (len(outs) - 1) + [False] if fill else []),
         ),
     )
@@ -996,7 +997,6 @@
     next(ahead)
     sum_ref[...] = small_ref[...]
     from_f = wires.copy(small_ref, slot, to["f"]) if over_f else None
-    next(ahead)
     sources = [*parts, sum_ref]
     chunks = []
     for i, cuts in ((2, 1), (0, 2), (1, 4), (3, 1)):
@@ -1030,19 +1030,22 @@
         lows[i][at] = (wide(lows[i][at]) + wide(from_middle[i][at])).astype(lows[i].dtype)
         outward[k].start()
 
-    send_in(0)
-    send_in(1)
+    early = 3
+    for k in range(early):
+        send_in(k)
+    next(ahead)
+    for k in range(early, small):
+        send_in(k)
+    pass_on(0, early)
     next(ahead)
     if over_f:
         from_f.wait_recv()
         sum_ref[...] = sum_ref[...] + slot[...]
-    for k in range(2, small + 1):
-        send_in(k)
-    pass_on(0, 2)
+    send_in(small)
+    pass_on(early, small + 1)
     out_low[...] = (mid_ref[...] + result_of(ahead)).astype(bf16)
     out_share = gather_rank(wires, to, out_low, outputs)
     next(out_share)
-    pass_on(2, small + 1)
 
     @pl.when(inner)
     def _():
@@ -1271,17 +1274,15 @@
             down_low, gate_own = owns[:2]
             down_upper, down_lower = down_low[:upper], down_low[upper:]
             far_upper = flip(down_upper, "context", 1)
-        gate_got = after(gate_got, grad_middle_low)
-        gate_low = add(gate_own, gate_got)
         far_lower = flip(down_lower, "context", 1)
-        grad_middle_low = after(grad_middle_low, gate_low)
         grad_attended = dot_cols(grad_middle_low, w_out_all).astype(bf16)
 
         dq_low, dkv = attention_back(key_blocks, queries, grad_attended, lse, cosine, sine, kv)
         attention_args = [(attended, after(grad_middle_low, dq_low), 1), (normed, dq_low, 0)]
         fars = [grad_far(*args) for args in attention_args]
+        gate_low = add(gate_own, after(gate_got, dq_low))
         dkv, *last_owns = kv_scatter(
-            after(dkv, fars), later, width // n_f
+            after(dkv, fars, gate_low, far_lower), later, width // n_f
         )
         (up_own,) = last_owns or owns[2:]
         far_gate = flip(after(gate_low, dkv, far_lower), "context", 1)

time: 456 us -> 458 us (level)
  the two profiles are of different devices: /device:TPU:0 before, /device:TPU:9 now
where the time goes in v17:
time: 458 us; the launch traced here: 454 us
  Pallas kernels  350 us (76%)
  other arithmetic  35.3 us (8%)
  local copies, waits for them, and re-layouts  22.6 us (5%)
  matrix products  18.7 us (4%)
  starting transfers between devices  17.4 us (4%)
  waiting for transfers between devices  8.52 us (2%)
    pallas_call x6, Pallas kernels, remote_call(): pl.pallas_call(kernel, name=name, out_shape=outs, in_specs=[spec(x) for x...  242 us
    pallas_call x2, Pallas kernels, hidden_call(): pl.pallas_call(kernel, name=name, grid_spec=pltpu.PrefetchScalarGridSpec(...  71.8 us
    ppermute x18, starting transfers between devices, flip(): return lax.ppermute(x, axis, [(i, i ^ bit) for i in range(size)])  17.4 us
    pallas_call x1, Pallas kernels, attention_back(): pl.pallas_call(functools.partial(attention_back_kernel, kv.shape[1] // BL...  15.1 us
    dot_general x6, matrix products, dot_rows(): lax.dot_general(left, right, (((0,), (0,)), ((), ())), preferred_element_...  12 us
    pallas_call x1, Pallas kernels, attention(): pl.pallas_call(functools.partial(attention_kernel, kv.shape[1] // BLOCK),...  10.2 us
    unnamed x76, local copies, waits for them, and re-layouts  9.45 us
    convert_element_type x2, other arithmetic, unit_whole(): return by_bit(parity, own, other, 0).astype(f32)  9.37 us
  transfers between devices with their start and end apart: 18, of which 2 were waited for; matrix products, arithmetic and copies ran while one was open for 12% of the time, Pallas kernels for 77%

profile of v17, /device:TPU:9, one launch (start us, length us, event | category | flops | bytes accessed | tf_op | source)
XLA Modules:
  0.0 454.1 jit_solution(11224492756109077722)
XLA Ops:
  0.7 1.9 constant_dynamic-slice_fusion.8.dy_ref
  2.6 2.5 collective-permute-start.2
  10.0 1.8 dynamic-slice_select_fusion.refs_2_
  13.3 1.8 constant_dynamic-slice_fusion.4.x_ref
  24.8 4.8 %collective-permute-done.3.refs_1_ = bf16[768,384]{1,0:T(8,128)(2,1)} collective-permute-done((bf16[768,384]{1,0:T(8,128)(2,1)}, bf16[768,384]{1,0:T(8,128)(2,1)}, u32[]{:S(2)}, u32[]{:S(2)}) %collective-permute-start.3) | collective-permute-done | bytes 589856 | tf_op jit(solution)/shard_map/ppermute | solution.py:1108
  31.3 6.5 %qkv.1 = (bf16[512,1536]{1,0:T(8,128)(2,1)}, bf16[512,384]{1,0:T(8,128)(2,1)}, bf16[512,128]{1,0:T(8,128)(2,1)}) custom-call(s32[4]{0:T(128)} %pad_add_fusion.1.meta_ref, bf16[512,1536]{1,0:T(8,128)(2,1)} %x_ref.1, f32[1,1536]{1,0:T(1,128)} %bitcast.87, f32[1,512]{1,0:T(1,128)} %pad_maximum_fusion.4.bias_ref, f32[512,128]{1,0:T(8,128)} %get-tuple-element.179.cos_ref, ...), custom_call_target="tpu_custom_call" | custom-call | tf_op jit(solution)/shard_map/qkv/pallas_call | solution.py:208
  37.7 16.3 %kv_gather.1.k_ref.v_ref = bf16[2,2048,128]{2,1,0:T(8,128)(2,1)} custom-call(bf16[512,128]{1,0:T(8,128)(2,1)} %get-tuple-element.90.own_ref), custom_call_target="tpu_custom_call" | custom-call | tf_op jit(solution)/shard_map/kv_gather/pallas_call | solution.py:641
  54.0 2.5 maximum_select_fusion.3
  60.5 10.2 %attention.1 = (bf16[512,384]{1,0:T(8,128)(2,1)}, f32[3,512,1]{2,1,0:T(8,128)}) custom-call(s32[8]{0:T(128)} %pad_add_fusion.kb_ref, bf16[512,384]{1,0:T(8,128)(2,1)} %get-tuple-element.89.q_ref, bf16[2,2048,128]{2,1,0:T(8,128)(2,1)} %kv_gather.1.k_ref.v_ref, bf16[2,2048,128]{2,1,0:T(8,128)(2,1)} %kv_gather.1.k_ref.v_ref), custom_call_target="tpu_custom_call" | custom-call | tf_op jit(solution)/shard_map/attention/pallas_call | solution.py:85
  70.6 3.5 convolution_convert_fusion
  74.1 65.8 %middle_norm.1 = (f32[128,1536]{1,0:T(8,128)}, f32[128,1]{1,0:T(8,128)}, bf16[16,128,1536]{2,1,0:T(8,128)(2,1)}, bf16[16,128,1536]{2,1,0:T(8,128)(2,1)}) custom-call(bf16[4,128,1536]{2,1,0:T(8,128)(2,1)} %bitcast.79, bf16[128,1536]{1,0:T(8,128)(2,1)} %constant_dynamic-slice_fusion.4.x_ref, f32[1,1536]{1,0:T(1,128)} %bitcast.89, ...), custom_call_target="tpu_custom_call" | custom-call | tf_op jit(solution)/shard_map/middle_norm/pallas_call | solution.py:641
  139.9 29.8 %hidden_units.1 = (bf16[2048,1120]{1,0:T(8,128)(2,1)}, bf16[2048,1120]{1,0:T(8,128)(2,1)}, bf16[2048,1120]{1,0:T(8,128)(2,1)}, bf16[1120,768]{1,0:T(8,128)(2,1)}) custom-call(s32[4]{0:T(128)} %pad_add_fusion.1.meta_ref, bf16[2048,1536]{1,0:T(8,128)(2,1)} %bitcast.70, bf16[2048,1536]{1,0:T(8,128)(2,1)} %bitcast.74, bf16[2240,768]{1,0:T(8,128)(2,1)} %copy-done.2, ...), custom_call_target="tpu_custom_call" | custom-call | tf_op jit(solution)/shard_map/hidden_units/pallas_call | solution.py:331
  171.2 42.0 %hidden_back.1 = (bf16[2048,1120]{1,0:T(8,128)(2,1)}, bf16[2048,1120]{1,0:T(8,128)(2,1)}, bf16[1024,1536]{1,0:T(8,128)(2,1)}, bf16[1024,1536]{1,0:T(8,128)(2,1)}...) custom-call(s32[4]{0:T(128)} %pad_add_fusion.1.meta_ref, bf16[2048,1536]{1,0:T(8,128)(2,1)} %bitcast.71, ...), custom_call_target="tpu_custom_call" | custom-call | tf_op jit(solution)/shard_map/hidden_back/pallas_call | solution.py:331
  215.9 36.0 %middle_back.1 = (f32[128,1536]{1,0:T(8,128)}, f32[1,1536]{1,0:T(1,128)}, bf16[4,128,1536]{2,1,0:T(8,128)(2,1)}, bf16[1120,768]{1,0:T(8,128)(2,1)}, bf16[1120,76...) custom-call(bf16[8,128,1536]{2,1,0:T(8,128)(2,1)} %bitcast.80, ...), custom_call_target="tpu_custom_call" | custom-call | tf_op jit(solution)/shard_map/middle_back/pallas_call | solution.py:641
  253.2 3.2 convolution_convert_fusion.3.do_ref
  256.4 15.1 %attention_back.1 = (bf16[512,384]{1,0:T(8,128)(2,1)}, bf16[2,2048,128]{2,1,0:T(8,128)(2,1)}) custom-call(s32[8]{0:T(128)} %pad_add_fusion.kb_ref, bf16[512,384]{1,0:T(8,128)(2,1)} %get-tuple-element.89.q_ref, bf16[512,384]{1,0:T(8,128)(2,1)} %convolution_convert_fusion.3.do_ref, f32[3,512,1]{2,1,0:T(8,128)} %get-tuple-element.107.lse_ref, ...), custom_call_target="tpu_custom_call" | custom-call | tf_op jit(solution)/shard_map/attention_back/pallas_call | solution.py:151
  271.5 2.6 convolution_convert_fusion.1
  276.9 1.9 add_convert_fusion.1
  278.8 3.7 collective-permute-done.12
  282.5 18.1 %kv_scatter.1 = (f32[512,128]{1,0:T(8,128)}, bf16[1120,768]{1,0:T(8,128)(2,1)}) custom-call(bf16[2,2048,128]{2,1,0:T(8,128)(2,1)} %get-tuple-element.116.part_ref, bf16[2048,1120]{1,0:T(8,128)(2,1)} %get-tuple-element.117.refs_0_, bf16[2048,1536]{1,0:T(8,128)(2,1)} %bitcast.73), custom_call_target="tpu_custom_call" | custom-call | tf_op jit(solution)/shard_map/kv_scatter/pallas_call | solution.py:641
  300.6 2.3 collective-permute-start.14
  305.0 4.8 %qkv_back.1 = bf16[512,1536]{1,0:T(8,128)(2,1)} custom-call(s32[4]{0:T(128)} %pad_add_fusion.1.meta_ref, bf16[512,384]{1,0:T(8,128)(2,1)} %get-tuple-element.108.dq_ref, bf16[512,128]{1,0:T(8,128)(2,1)} %fusion.18.dkv_ref, bf16[768,384]{1,0:T(8,128)(2,1)} %refs_0_.3, bf16[768,384]{1,0:T(8,128)(2,1)} %collective-permute-done.3.refs_1_, ...), custom_call_target="tpu_custom_call" | custom-call | tf_op jit(solution)/shard_map/qkv_back/pallas_call | solution.py:240
  311.9 2.5 add_convert_fusion
  315.6 28.5 %input_back.1 = (f32[1,5120]{1,0:T(1,128)}, bf16[4,128,1536]{2,1,0:T(8,128)(2,1)}) custom-call(bf16[4,128,1536]{2,1,0:T(8,128)(2,1)} %bitcast.78, bf16[128,1536]{1,0:T(8,128)(2,1)} %constant_dynamic-slice_fusion.4.x_ref, f32[1,1536]{1,0:T(1,128)} %bitcast.88, f32[128,1536]{1,0:T(8,128)} %get-tuple-element.125.dmid_ref, f32[1,5120]{1,0:T(1,128)} %pad_maximum_fusion.3.small_ref), custom_call_target="tpu_custom_call" | custom-call | tf_op jit(solution)/shard_map/input_back/pallas_call | solution.py:641
  344.2 2.8 broadcast_add_fusion
  347.0 4.6 %fusion = f32[2240,768]{1,0:T(8,128)} fusion(bf16[848,768]{1,0:T(8,128)(2,1)} %collective-permute-done.12, bf16[272,768]{1,0:T(8,128)(2,1)S(1)} %copy-done.26, bf16[848,768]{1,0:T(8,128)(2,1)S(1)} %copy-done.18, bf16[272,768]{1,0:T(8,128)(2,1)S(1)} %copy-done.25, pred[]{:T(512)S(6)} %eq.19), kind=kLoop, calls=%fused_computation.3 | loop fusion | flops 30965760 | bytes 10321921 | tf_op jit(solution)/shard_map/convert_element_type | solution.py:1263
  351.6 4.8 %fusion.1 = f32[2240,768]{1,0:T(8,128)} fusion(bf16[1120,768]{1,0:T(8,128)(2,1)} %collective-permute-done.14, bf16[1120,768]{1,0:T(8,128)(2,1)S(1)} %add_convert_fusion.1, pred[]{:T(512)S(6)} %eq.19), kind=kLoop, calls=%fused_computation.5 | loop fusion | flops 17203200 | bytes 10321921 | tf_op jit(solution)/shard_map/convert_element_type | solution.py:1263
  356.4 2.2 fusion.9.refs_2_
  358.6 2.5 fusion.3.refs_1_
  361.1 2.4 fusion.2.refs_0_
  363.5 77.4 %context_sum.1 = (f32[384,768]{1,0:T(8,128)}, f32[768,384]{1,0:T(8,128)}, f32[1,5120]{1,0:T(1,128)}, bf16[4,768,128]{2,1,0:T(8,128)(2,1)}, bf16[4,128,1536]{2,1,0:T(8,128)(2,1)}) custom-call(bf16[384,768]{1,0:T(8,128)(2,1)} %fusion.2.refs_0_, bf16[768,384]{1,0:T(8,128)(2,1)} %fusion.3.refs_1_, bf16[768,128]{1,0:T(8,128)(2,1)} %fusion.9.refs_2_, ...), custom_call_target="tpu_custom_call" | custom-call | tf_op jit(solution)/shard_map/context_sum/pallas_call | solution.py:641
  440.9 4.9 %convert_bitcast_fusion = f32[768,2240]{0,1:T(8,128)} fusion(bf16[1120,768]{1,0:T(8,128)(2,1)} %collective-permute-done.17, bf16[1120,768]{1,0:T(8,128)(2,1)S(1)} %add_convert_fusion, pred[]{:T(512)S(6)} %eq.19), kind=kLoop, calls=%fused_computation | loop fusion | flops 17203200 | bytes 10321921 | tf_op jit(solution)/shard_map/transpose | solution.py:1347
  (159 shorter events, 43.4 us)
Async XLA Ops:
  0.6 15.8 %copy-start = (bf16[2240,768]{1,0:T(8,128)(2,1)S(1)}, bf16[2240,768]{1,0:T(8,128)(2,1)}, u32[]{:S(2)}) copy-start(bf16[2240,768]{1,0:T(8,128)(2,1)} %param.29) | copy-start | bytes 10321924
  0.7 14.9 %copy-start.33 = (s32[1,8]{1,0:T(1,128)S(1)}, s32[1,8]{1,0:T(1,128)}, u32[]{:S(2)}) copy-start(s32[1,8]{1,0:T(1,128)} %param.17) | copy-start | bytes 100
  2.6 28.6 %collective-permute-start.1 = (bf16[128,1536]{1,0:T(8,128)(2,1)}, bf16[128,1536]{1,0:T(8,128)(2,1)}, u32[]{:S(2)}, u32[]{:S(2)}) collective-permute-start(bf16[128,1536]{1,0:T(8,128)(2,1)} %constant_dynamic-slice_fusion.8.dy_ref), channel_id=1, source_target_pairs={{0,4},{4,0},{8,12},{12,8},{1,5},{5,1},{9,13},{13,9},{2,6},{6,2},{1... | collective-permute-start | bytes 1179656 | tf_op jit(solution)/shard_map/ppermute | solution.py:1108
  2.6 28.6 %collective-permute-start.2 = (bf16[128,1536]{1,0:T(8,128)(2,1)}, bf16[128,1536]{1,0:T(8,128)(2,1)}, u32[]{:S(2)}, u32[]{:S(2)}) collective-permute-start(bf16[128,1536]{1,0:T(8,128)(2,1)} %constant_dynamic-slice_fusion.8.dy_ref), channel_id=1, source_target_pairs={{0,8},{4,12},{8,0},{12,4},{1,9},{5,13},{9,1},{13,5},{2,10},{6,14},... | collective-permute-start | bytes 1179656 | tf_op jit(solution)/shard_map/ppermute | solution.py:1108
  8.8 15.7 %collective-permute-start = (bf16[1,1984]{1,0:T(2,128)(2,1)S(1)}, bf16[1,1984]{1,0:T(2,128)(2,1)S(1)}, u32[]{:S(2)}, u32[]{:S(2)}) collective-permute-start(bf16[1,1984]{1,0:T(2,128)(2,1)S(1)} %concatenate.68), channel_id=1, source_target_pairs={{0,16},{16,0},{1,17},{17,1},{2,18},{18,2},{3,19},{19,3},{4,20},{20... | collective-permute-start | bytes 11912 | tf_op jit(solution)/shard_map/ppermute | solution.py:1108
  11.8 13.0 %collective-permute-start.4 = (bf16[768,128]{1,0:T(8,128)(2,1)}, bf16[768,128]{1,0:T(8,128)(2,1)}, u32[]{:S(2)}, u32[]{:S(2)}) collective-permute-start(bf16[768,128]{1,0:T(8,128)(2,1)} %dynamic-slice_select_fusion.refs_2_), channel_id=1, source_target_pairs={{0,16},{16,0},{1,17},{17,1},{2,18},{18,2},{3,19},{19,3},{4,20},{20... | collective-permute-start | bytes 589832 | tf_op jit(solution)/shard_map/ppermute | solution.py:1108
  12.0 17.6 %collective-permute-start.3 = (bf16[768,384]{1,0:T(8,128)(2,1)}, bf16[768,384]{1,0:T(8,128)(2,1)}, u32[]{:S(2)}, u32[]{:S(2)}) collective-permute-start(bf16[768,384]{1,0:T(8,128)(2,1)} %refs_0_.3), channel_id=1, source_target_pairs={{0,16},{16,0},{1,17},{17,1},{2,18},{18,2},{3,19},{19,3},{4,20},{20... | collective-permute-start | bytes 1769480 | tf_op jit(solution)/shard_map/ppermute | solution.py:1108
  20.9 35.6 %copy-start.2 = (bf16[2240,768]{1,0:T(8,128)(2,1)}, bf16[2240,768]{1,0:T(8,128)(2,1)S(1)}, u32[]{:S(2)}) copy-start(bf16[2240,768]{1,0:T(8,128)(2,1)S(1)} %pad_maximum_fusion.refs_0_.refs_2_) | copy-start | bytes 10321924
  29.6 24.4 %collective-permute-start.5 = (bf16[384,768]{1,0:T(8,128)(2,1)}, bf16[384,768]{1,0:T(8,128)(2,1)}, u32[]{:S(2)}, u32[]{:S(2)}) collective-permute-start(bf16[384,768]{1,0:T(8,128)(2,1)} %param.25), channel_id=1, source_target_pairs={{0,16},{16,0},{1,17},{17,1},{2,18},{18,2},{3,19},{19,3},{4,20},{20... | collective-permute-start | bytes 1769480 | tf_op jit(solution)/shard_map/ppermute | solution.py:1108
  31.3 22.8 %copy-start.24 = (bf16[384,768]{1,0:T(8,128)(2,1)S(1)}, bf16[384,768]{1,0:T(8,128)(2,1)}, u32[]{:S(2)}) copy-start(bf16[384,768]{1,0:T(8,128)(2,1)} %param.25) | copy-start | bytes 1769476
  56.6 83.4 %collective-permute-start.7 = (bf16[2240,768]{1,0:T(8,128)(2,1)S(1)}, bf16[2240,768]{1,0:T(8,128)(2,1)}, u32[]{:S(2)}, u32[]{:S(2)}) collective-permute-start(bf16[2240,768]{1,0:T(8,128)(2,1)S(1)} %pad_maximum_fusion.refs_0_.refs_2_), channel_id=1, source_target_pairs={{0,16},{16,0},{1,17},{17,1},{2,18},{18,2},{3,19},{19,3},{4,20},{20... | collective-permute-start | bytes 10321928 | tf_op jit(solution)/shard_map/ppermute | solution.py:1108
  57.8 113.4 %collective-permute-start.8 = (bf16[1120,768]{1,0:T(8,128)(2,1)}, bf16[1120,768]{1,0:T(8,128)(2,1)}, u32[]{:S(2)}, u32[]{:S(2)}) collective-permute-start(bf16[1120,768]{1,0:T(8,128)(2,1)} %constant_dynamic-slice_fusion.5.refs_4_), channel_id=1, source_target_pairs={{0,16},{16,0},{1,17},{17,1},{2,18},{18,2},{3,19},{19,3},{4,20},{20... | collective-permute-start | bytes 5160968 | tf_op jit(solution)/shard_map/ppermute | solution.py:1108
  58.0 16.1 %collective-permute-start.6 = (bf16[128,1536]{1,0:T(8,128)(2,1)}, bf16[128,1536]{1,0:T(8,128)(2,1)}, u32[]{:S(2)}, u32[]{:S(2)}) collective-permute-start(bf16[128,1536]{1,0:T(8,128)(2,1)} %constant_dynamic-slice_fusion.8.dy_ref), channel_id=1, source_target_pairs={{0,2},{1,3},{2,0},{3,1},{4,6},{5,7},{6,4},{7,5},{8,10},{9,11},{10,... | collective-permute-start | bytes 1179656 | tf_op jit(solution)/shard_map/ppermute | solution.py:1108
  169.7 45.1 %collective-permute-start.9 = (bf16[1120,768]{1,0:T(8,128)(2,1)}, bf16[1120,768]{1,0:T(8,128)(2,1)S(1)}, u32[]{:S(2)}, u32[]{:S(2)}) collective-permute-start(bf16[1120,768]{1,0:T(8,128)(2,1)} %get-tuple-element.105), channel_id=1, source_target_pairs={{0,16},{16,0},{1,17},{17,1},{2,18},{18,2},{3,19},{19,3},{4,20},{20... | collective-permute-start | bytes 5160968 | tf_op jit(solution)/shard_map/ppermute | solution.py:1108
  213.2 62.2 %collective-permute-start.11 = (bf16[1120,768]{1,0:T(8,128)(2,1)}, bf16[1120,768]{1,0:T(8,128)(2,1)}, u32[]{:S(2)}, u32[]{:S(2)}) collective-permute-start(bf16[1120,768]{1,0:T(8,128)(2,1)} %get-tuple-element.113), channel_id=1, source_target_pairs={{0,16},{16,0},{1,17},{17,1},{2,18},{18,2},{3,19},{19,3},{4,20},{20... | collective-permute-start | bytes 5160968 | tf_op jit(solution)/shard_map/ppermute | solution.py:1108
  213.3 97.6 %collective-permute-start.13 = (bf16[1120,768]{1,0:T(8,128)(2,1)}, bf16[1120,768]{1,0:T(8,128)(2,1)}, u32[]{:S(2)}, u32[]{:S(2)}) collective-permute-start(bf16[1120,768]{1,0:T(8,128)(2,1)} %get-tuple-element.121), channel_id=1, source_target_pairs={{0,16},{16,0},{1,17},{17,1},{2,18},{18,2},{3,19},{19,3},{4,20},{20... | collective-permute-start | bytes 5160968 | tf_op jit(solution)/shard_map/ppermute | solution.py:1108
  215.9 37.3 %copy-start.3 = (bf16[384,1536]{1,0:T(8,128)(2,1)S(1)}, bf16[384,1536]{1,0:T(8,128)(2,1)}, u32[]{:S(2)}) copy-start(bf16[384,1536]{1,0:T(8,128)(2,1)} %maximum_select_fusion.3) | copy-start | bytes 3538948
  251.9 30.6 %collective-permute-start.12 = (bf16[848,768]{1,0:T(8,128)(2,1)}, bf16[848,768]{1,0:T(8,128)(2,1)}, u32[]{:S(2)}, u32[]{:S(2)}) collective-permute-start(bf16[848,768]{1,0:T(8,128)(2,1)} %get-tuple-element.136), channel_id=1, source_target_pairs={{0,4},{4,0},{8,12},{12,8},{1,5},{5,1},{9,13},{13,9},{2,6},{6,2},{1... | collective-permute-start | bytes 3907592 | tf_op jit(solution)/shard_map/ppermute | solution.py:1108
  256.4 15.1 %copy-start.13 = (bf16[512,1536]{1,0:T(8,128)(2,1)S(1)}, bf16[512,1536]{1,0:T(8,128)(2,1)}, u32[]{:S(2)}) copy-start(bf16[512,1536]{1,0:T(8,128)(2,1)} %get-tuple-element.123) | copy-start | bytes 4718596
  271.5 5.4 %copy-start.11 = (bf16[1120,768]{1,0:T(8,128)(2,1)S(1)}, bf16[1120,768]{1,0:T(8,128)(2,1)}, u32[]{:S(2)}) copy-start(bf16[1120,768]{1,0:T(8,128)(2,1)} %get-tuple-element.112) | copy-start | bytes 5160964
  275.4 81.0 %collective-permute-start.15 = (bf16[768,384]{1,0:T(8,128)(2,1)}, bf16[768,384]{1,0:T(8,128)(2,1)}, u32[]{:S(2)}, u32[]{:S(2)}) collective-permute-start(bf16[768,384]{1,0:T(8,128)(2,1)} %convolution_convert_fusion.1), channel_id=1, source_target_pairs={{0,16},{16,0},{1,17},{17,1},{2,18},{18,2},{3,19},{19,3},{4,20},{20... | collective-permute-start | bytes 1769480 | tf_op jit(solution)/shard_map/ppermute | solution.py:1108
  276.6 79.9 %collective-permute-start.10 = (bf16[384,768]{1,0:T(8,128)(2,1)}, bf16[384,768]{1,0:T(8,128)(2,1)}, u32[]{:S(2)}, u32[]{:S(2)}) collective-permute-start(bf16[384,768]{1,0:T(8,128)(2,1)} %convolution_convert_fusion.2), channel_id=1, source_target_pairs={{0,16},{16,0},{1,17},{17,1},{2,18},{18,2},{3,19},{19,3},{4,20},{20... | collective-permute-start | bytes 1769480 | tf_op jit(solution)/shard_map/ppermute | solution.py:1108
  282.5 20.5 %copy-start.7 = (f32[512,64]{1,0:T(8,128)S(1)}, f32[512,64]{1,0:T(8,128)}, u32[]{:S(2)}) copy-start(f32[512,64]{1,0:T(8,128)} %copy-done.6) | copy-start | bytes 393220
  300.6 46.4 %collective-permute-start.14 = (bf16[1120,768]{1,0:T(8,128)(2,1)S(1)}, bf16[1120,768]{1,0:T(8,128)(2,1)}, u32[]{:S(2)}, u32[]{:S(2)}) collective-permute-start(bf16[1120,768]{1,0:T(8,128)(2,1)S(1)} %add_convert_fusion.1), channel_id=1, source_target_pairs={{0,4},{4,0},{8,12},{12,8},{1,5},{5,1},{9,13},{13,9},{2,6},{6,2},{1... | collective-permute-start | bytes 5160968 | tf_op jit(solution)/shard_map/ppermute | solution.py:1108
  305.0 4.8 %copy-start.14 = (bf16[512,1536]{1,0:T(8,128)(2,1)S(1)}, bf16[512,1536]{1,0:T(8,128)(2,1)}, u32[]{:S(2)}) copy-start(bf16[512,1536]{1,0:T(8,128)(2,1)} %get-tuple-element.123) | copy-start | bytes 4718596
  310.9 45.5 %collective-permute-start.16 = (bf16[768,128]{1,0:T(8,128)(2,1)}, bf16[768,128]{1,0:T(8,128)(2,1)}, u32[]{:S(2)}, u32[]{:S(2)}) collective-permute-start(bf16[768,128]{1,0:T(8,128)(2,1)} %convolution_convert_fusion.4), channel_id=1, source_target_pairs={{0,16},{16,0},{1,17},{17,1},{2,18},{18,2},{3,19},{19,3},{4,20},{20... | collective-permute-start | bytes 589832 | tf_op jit(solution)/shard_map/ppermute | solution.py:1108
  314.4 126.5 %collective-permute-start.17 = (bf16[1120,768]{1,0:T(8,128)(2,1)S(1)}, bf16[1120,768]{1,0:T(8,128)(2,1)}, u32[]{:S(2)}, u32[]{:S(2)}) collective-permute-start(bf16[1120,768]{1,0:T(8,128)(2,1)S(1)} %add_convert_fusion), channel_id=1, source_target_pairs={{0,4},{4,0},{8,12},{12,8},{1,5},{5,1},{9,13},{13,9},{2,6},{6,2},{1... | collective-permute-start | bytes 5160968 | tf_op jit(solution)/shard_map/ppermute | solution.py:1108
  351.6 4.8 %copy-start.5 = (bf16[512,128]{1,0:T(8,128)(2,1)S(1)}, bf16[512,128]{1,0:T(8,128)(2,1)}, u32[]{:S(2)}) copy-start(bf16[512,128]{1,0:T(8,128)(2,1)} %fusion.18.dkv_ref) | copy-start | bytes 393220
  351.6 4.9 %copy-start.15 = (bf16[512,1536]{1,0:T(8,128)(2,1)S(1)}, bf16[512,1536]{1,0:T(8,128)(2,1)}, u32[]{:S(2)}) copy-start(bf16[512,1536]{1,0:T(8,128)(2,1)} %get-tuple-element.123) | copy-start | bytes 4718596
  351.6 7.0 %copy-start.17 = (bf16[512,384]{1,0:T(8,128)(2,1)S(1)}, bf16[512,384]{1,0:T(8,128)(2,1)}, u32[]{:S(2)}) copy-start(bf16[512,384]{1,0:T(8,128)(2,1)} %get-tuple-element.108.dq_ref) | copy-start | bytes 1179652
  440.9 4.9 %copy-start.23 = (bf16[4,768,128]{2,1,0:T(8,128)(2,1)S(1)}, bf16[4,768,128]{2,1,0:T(8,128)(2,1)}, u32[]{:S(2)}) copy-start(bf16[4,768,128]{2,1,0:T(8,128)(2,1)} %get-tuple-element.153) | copy-start | bytes 2359300
  440.9 5.0 %copy-start.29 = (f32[1,5120]{1,0:T(1,128)S(1)}, f32[1,5120]{1,0:T(1,128)}, u32[]{:S(2)}) copy-start(f32[1,5120]{1,0:T(1,128)} %get-tuple-element.151) | copy-start | bytes 61444
  (20 other events, 56.8 us)

commit v18 on v16

--- a/solution.py
+++ b/solution.py
@@ -996,7 +996,6 @@
     next(ahead)
     sum_ref[...] = small_ref[...]
     from_f = wires.copy(small_ref, slot, to["f"]) if over_f else None
-    next(ahead)
     sources = [*parts, sum_ref]
     chunks = []
     for i, cuts in ((2, 1), (0, 2), (1, 4), (3, 1)):
@@ -1030,19 +1029,24 @@
         lows[i][at] = (wide(lows[i][at]) + wide(from_middle[i][at])).astype(lows[i].dtype)
         outward[k].start()
 
-    send_in(0)
-    send_in(1)
+    early, late = 3, 5
+    for k in range(early):
+        send_in(k)
+    next(ahead)
+    for k in range(early, late):
+        send_in(k)
+    pass_on(0, early)
     next(ahead)
     if over_f:
         from_f.wait_recv()
         sum_ref[...] = sum_ref[...] + slot[...]
-    for k in range(2, small + 1):
+    for k in range(late, small + 1):
         send_in(k)
-    pass_on(0, 2)
+    pass_on(early, late)
     out_low[...] = (mid_ref[...] + result_of(ahead)).astype(bf16)
     out_share = gather_rank(wires, to, out_low, outputs)
     next(out_share)
-    pass_on(2, small + 1)
+    pass_on(late, small + 1)
 
     @pl.when(inner)
     def _():

time: 456 us -> 452 us (level)
  Pallas kernels: 342 us -> 337 us
    pallas_call x6, Pallas kernels: 233 us -> 228 us  [remote_call(): pl.pallas_call(kernel, name=name, out_shape=outs, in_specs=[spec(x) for x...]
  transfers between devices with their start and end apart: 18 -> 18, of which waited for: 3 -> 3; matrix products, arithmetic and copies ran while one was open for 12% -> 12% of each run, Pallas kernels for 76% -> 75%
where the time goes in v18:
time: 452 us; the launch traced here: 447 us
  Pallas kernels  337 us (75%)
  other arithmetic  35.9 us (8%)
  local copies, waits for them, and re-layouts  23.9 us (5%)
  starting transfers between devices  22.6 us (5%)
  matrix products  17.3 us (4%)
  waiting for transfers between devices  9.32 us (2%)
    pallas_call x6, Pallas kernels, remote_call(): pl.pallas_call(kernel, name=name, out_shape=outs, in_specs=[spec(x) for x...  228 us
    pallas_call x2, Pallas kernels, hidden_call(): pl.pallas_call(kernel, name=name, grid_spec=pltpu.PrefetchScalarGridSpec(...  71.8 us
    ppermute x18, starting transfers between devices, flip(): return lax.ppermute(x, axis, [(i, i ^ bit) for i in range(size)])  22.6 us
    pallas_call x1, Pallas kernels, attention_back(): pl.pallas_call(functools.partial(attention_back_kernel, kv.shape[1] // BL...  15.1 us
    dot_general x6, matrix products, dot_rows(): lax.dot_general(left, right, (((0,), (0,)), ((), ())), preferred_element_...  12 us
    unnamed x78, local copies, waits for them, and re-layouts  10.7 us
    pallas_call x1, Pallas kernels, attention(): pl.pallas_call(functools.partial(attention_kernel, kv.shape[1] // BLOCK),...  10.2 us
    convert_element_type x2, other arithmetic, unit_whole(): return by_bit(parity, own, other, 0).astype(f32)  9.41 us
  transfers between devices with their start and end apart: 18, of which 3 were waited for; matrix products, arithmetic and copies ran while one was open for 12% of the time, Pallas kernels for 75%

profile of v18, /device:TPU:0, one launch (start us, length us, event | category | flops | bytes accessed | tf_op | source)
XLA Modules:
  0.0 447.0 jit_solution(206654518707993091)
XLA Ops:
  0.7 1.9 constant_dynamic-slice_fusion.8.dy_ref
  2.6 3.0 collective-permute-start.1
  5.6 2.6 collective-permute-start.2
  13.4 1.8 dynamic-slice_select_fusion.refs_2_
  17.2 1.8 constant_dynamic-slice_fusion.4.x_ref
  28.8 5.2 %collective-permute-done.3.refs_1_ = bf16[768,384]{1,0:T(8,128)(2,1)} collective-permute-done((bf16[768,384]{1,0:T(8,128)(2,1)}, bf16[768,384]{1,0:T(8,128)(2,1)}, u32[]{:S(2)}, u32[]{:S(2)}) %collective-permute-start.3) | collective-permute-done | bytes 589856 | tf_op jit(solution)/shard_map/ppermute | solution.py:1109
  35.9 6.5 %qkv.1 = (bf16[512,1536]{1,0:T(8,128)(2,1)}, bf16[512,384]{1,0:T(8,128)(2,1)}, bf16[512,128]{1,0:T(8,128)(2,1)}) custom-call(s32[4]{0:T(128)} %pad_add_fusion.1.meta_ref, bf16[512,1536]{1,0:T(8,128)(2,1)} %x_ref.1, f32[1,1536]{1,0:T(1,128)} %bitcast.87, f32[1,512]{1,0:T(1,128)} %pad_maximum_fusion.4.bias_ref, f32[512,128]{1,0:T(8,128)} %get-tuple-element.181.cos_ref, ...), custom_call_target="tpu_custom_call" | custom-call | tf_op jit(solution)/shard_map/qkv/pallas_call | solution.py:208
  42.4 15.0 %kv_gather.1.k_ref.v_ref = bf16[2,2048,128]{2,1,0:T(8,128)(2,1)} custom-call(bf16[512,128]{1,0:T(8,128)(2,1)} %get-tuple-element.91.own_ref), custom_call_target="tpu_custom_call" | custom-call | tf_op jit(solution)/shard_map/kv_gather/pallas_call | solution.py:640
  57.4 2.5 maximum_select_fusion.3
  64.7 10.2 %attention.1 = (bf16[512,384]{1,0:T(8,128)(2,1)}, f32[3,512,1]{2,1,0:T(8,128)}) custom-call(s32[8]{0:T(128)} %pad_add_fusion.kb_ref, bf16[512,384]{1,0:T(8,128)(2,1)} %get-tuple-element.90.q_ref, bf16[2,2048,128]{2,1,0:T(8,128)(2,1)} %kv_gather.1.k_ref.v_ref, bf16[2,2048,128]{2,1,0:T(8,128)(2,1)} %kv_gather.1.k_ref.v_ref), custom_call_target="tpu_custom_call" | custom-call | tf_op jit(solution)/shard_map/attention/pallas_call | solution.py:85
  74.8 3.5 convolution_convert_fusion
  78.4 62.4 %middle_norm.1 = (f32[128,1536]{1,0:T(8,128)}, f32[128,1]{1,0:T(8,128)}, bf16[16,128,1536]{2,1,0:T(8,128)(2,1)}, bf16[16,128,1536]{2,1,0:T(8,128)(2,1)}) custom-call(bf16[4,128,1536]{2,1,0:T(8,128)(2,1)} %bitcast.79, bf16[128,1536]{1,0:T(8,128)(2,1)} %constant_dynamic-slice_fusion.4.x_ref, f32[1,1536]{1,0:T(1,128)} %bitcast.89, ...), custom_call_target="tpu_custom_call" | custom-call | tf_op jit(solution)/shard_map/middle_norm/pallas_call | solution.py:640
  140.8 29.7 %hidden_units.1 = (bf16[2048,1120]{1,0:T(8,128)(2,1)}, bf16[2048,1120]{1,0:T(8,128)(2,1)}, bf16[2048,1120]{1,0:T(8,128)(2,1)}, bf16[1120,768]{1,0:T(8,128)(2,1)}) custom-call(s32[4]{0:T(128)} %pad_add_fusion.1.meta_ref, bf16[2048,1536]{1,0:T(8,128)(2,1)} %bitcast.70, bf16[2048,1536]{1,0:T(8,128)(2,1)} %bitcast.74, bf16[2240,768]{1,0:T(8,128)(2,1)} %copy-done.2, ...), custom_call_target="tpu_custom_call" | custom-call | tf_op jit(solution)/shard_map/hidden_units/pallas_call | solution.py:331
  173.6 42.0 %hidden_back.1 = (bf16[2048,1120]{1,0:T(8,128)(2,1)}, bf16[2048,1120]{1,0:T(8,128)(2,1)}, bf16[1024,1536]{1,0:T(8,128)(2,1)}, bf16[1024,1536]{1,0:T(8,128)(2,1)}...) custom-call(s32[4]{0:T(128)} %pad_add_fusion.1.meta_ref, bf16[2048,1536]{1,0:T(8,128)(2,1)} %bitcast.71, ...), custom_call_target="tpu_custom_call" | custom-call | tf_op jit(solution)/shard_map/hidden_back/pallas_call | solution.py:331
  218.9 34.6 %middle_back.1 = (f32[128,1536]{1,0:T(8,128)}, f32[1,1536]{1,0:T(1,128)}, bf16[4,128,1536]{2,1,0:T(8,128)(2,1)}, bf16[1120,768]{1,0:T(8,128)(2,1)}, bf16[1120,76...) custom-call(bf16[8,128,1536]{2,1,0:T(8,128)(2,1)} %bitcast.80, ...), custom_call_target="tpu_custom_call" | custom-call | tf_op jit(solution)/shard_map/middle_back/pallas_call | solution.py:640
  253.6 2.8 collective-permute-done.10
  257.6 2.5 add_convert_fusion.1
  262.2 15.1 %attention_back.1 = (bf16[512,384]{1,0:T(8,128)(2,1)}, bf16[2,2048,128]{2,1,0:T(8,128)(2,1)}) custom-call(s32[8]{0:T(128)} %pad_add_fusion.kb_ref, bf16[512,384]{1,0:T(8,128)(2,1)} %get-tuple-element.90.q_ref, bf16[512,384]{1,0:T(8,128)(2,1)} %convolution_convert_fusion.3.do_ref, f32[3,512,1]{2,1,0:T(8,128)} %get-tuple-element.112.lse_ref, ...), custom_call_target="tpu_custom_call" | custom-call | tf_op jit(solution)/shard_map/attention_back/pallas_call | solution.py:151
  277.3 2.6 convolution_convert_fusion.1
  283.2 18.8 %kv_scatter.1 = (f32[512,128]{1,0:T(8,128)}, bf16[1120,768]{1,0:T(8,128)(2,1)}) custom-call(bf16[2,2048,128]{2,1,0:T(8,128)(2,1)} %get-tuple-element.117.part_ref, bf16[2048,1120]{1,0:T(8,128)(2,1)} %get-tuple-element.118.refs_0_, bf16[2048,1536]{1,0:T(8,128)(2,1)} %bitcast.73), custom_call_target="tpu_custom_call" | custom-call | tf_op jit(solution)/shard_map/kv_scatter/pallas_call | solution.py:640
  304.3 4.8 %qkv_back.1 = bf16[512,1536]{1,0:T(8,128)(2,1)} custom-call(s32[4]{0:T(128)} %pad_add_fusion.1.meta_ref, bf16[512,384]{1,0:T(8,128)(2,1)} %get-tuple-element.113.dq_ref, bf16[512,128]{1,0:T(8,128)(2,1)} %fusion.18.dkv_ref, bf16[768,384]{1,0:T(8,128)(2,1)} %refs_0_.3, bf16[768,384]{1,0:T(8,128)(2,1)} %collective-permute-done.3.refs_1_, ...), custom_call_target="tpu_custom_call" | custom-call | tf_op jit(solution)/shard_map/qkv_back/pallas_call | solution.py:240
  311.5 2.5 add_convert_fusion
  313.9 2.0 collective-permute-start.17
  317.1 28.7 %input_back.1 = (f32[1,5120]{1,0:T(1,128)}, bf16[4,128,1536]{2,1,0:T(8,128)(2,1)}) custom-call(bf16[4,128,1536]{2,1,0:T(8,128)(2,1)} %bitcast.78, bf16[128,1536]{1,0:T(8,128)(2,1)} %constant_dynamic-slice_fusion.4.x_ref, f32[1,1536]{1,0:T(1,128)} %bitcast.88, f32[128,1536]{1,0:T(8,128)} %get-tuple-element.127.dmid_ref, f32[1,5120]{1,0:T(1,128)} %pad_maximum_fusion.3.small_ref), custom_call_target="tpu_custom_call" | custom-call | tf_op jit(solution)/shard_map/input_back/pallas_call | solution.py:640
  345.8 2.8 broadcast_add_fusion
  348.6 4.6 %fusion = f32[2240,768]{1,0:T(8,128)} fusion(bf16[848,768]{1,0:T(8,128)(2,1)} %collective-permute-done.12, bf16[272,768]{1,0:T(8,128)(2,1)S(1)} %copy-done.26, bf16[848,768]{1,0:T(8,128)(2,1)S(1)} %copy-done.18, bf16[272,768]{1,0:T(8,128)(2,1)S(1)} %copy-done.25, pred[]{:T(512)S(6)} %eq.19), kind=kLoop, calls=%fused_computation.3 | loop fusion | flops 30965760 | bytes 10321921 | tf_op jit(solution)/shard_map/convert_element_type | solution.py:1264
  353.2 4.8 %fusion.1 = f32[2240,768]{1,0:T(8,128)} fusion(bf16[1120,768]{1,0:T(8,128)(2,1)} %collective-permute-done.14, bf16[1120,768]{1,0:T(8,128)(2,1)S(1)} %add_convert_fusion.1, pred[]{:T(512)S(6)} %eq.19), kind=kLoop, calls=%fused_computation.5 | loop fusion | flops 17203200 | bytes 10321921 | tf_op jit(solution)/shard_map/convert_element_type | solution.py:1264
  358.1 2.2 fusion.9.refs_2_
  360.2 2.5 fusion.3.refs_1_
  362.7 2.4 fusion.2.refs_0_
  365.1 68.8 %context_sum.1 = (f32[384,768]{1,0:T(8,128)}, f32[768,384]{1,0:T(8,128)}, f32[1,5120]{1,0:T(1,128)}, bf16[4,768,128]{2,1,0:T(8,128)(2,1)}, bf16[4,128,1536]{2,1,0:T(8,128)(2,1)}) custom-call(bf16[384,768]{1,0:T(8,128)(2,1)} %fusion.2.refs_0_, bf16[768,384]{1,0:T(8,128)(2,1)} %fusion.3.refs_1_, bf16[768,128]{1,0:T(8,128)(2,1)} %fusion.9.refs_2_, ...), custom_call_target="tpu_custom_call" | custom-call | tf_op jit(solution)/shard_map/context_sum/pallas_call | solution.py:640
  434.0 4.8 %convert_bitcast_fusion = f32[768,2240]{0,1:T(8,128)} fusion(bf16[1120,768]{1,0:T(8,128)(2,1)} %collective-permute-done.17, bf16[1120,768]{1,0:T(8,128)(2,1)S(1)} %add_convert_fusion, pred[]{:T(512)S(6)} %eq.19), kind=kLoop, calls=%fused_computation | loop fusion | flops 17203200 | bytes 10321921 | tf_op jit(solution)/shard_map/transpose | solution.py:1350
  (161 shorter events, 50.2 us)
Async XLA Ops:
  0.6 19.8 %copy-start = (bf16[2240,768]{1,0:T(8,128)(2,1)S(1)}, bf16[2240,768]{1,0:T(8,128)(2,1)}, u32[]{:S(2)}) copy-start(bf16[2240,768]{1,0:T(8,128)(2,1)} %param.29) | copy-start | bytes 10321924
  0.7 18.9 %copy-start.34 = (s32[1,8]{1,0:T(1,128)S(1)}, s32[1,8]{1,0:T(1,128)}, u32[]{:S(2)}) copy-start(s32[1,8]{1,0:T(1,128)} %param.17) | copy-start | bytes 100
  2.6 33.3 %collective-permute-start.1 = (bf16[128,1536]{1,0:T(8,128)(2,1)}, bf16[128,1536]{1,0:T(8,128)(2,1)}, u32[]{:S(2)}, u32[]{:S(2)}) collective-permute-start(bf16[128,1536]{1,0:T(8,128)(2,1)} %constant_dynamic-slice_fusion.8.dy_ref), channel_id=1, source_target_pairs={{0,4},{4,0},{8,12},{12,8},{1,5},{5,1},{9,13},{13,9},{2,6},{6,2},{1... | collective-permute-start | bytes 1179656 | tf_op jit(solution)/shard_map/ppermute | solution.py:1109
  5.6 30.3 %collective-permute-start.2 = (bf16[128,1536]{1,0:T(8,128)(2,1)}, bf16[128,1536]{1,0:T(8,128)(2,1)}, u32[]{:S(2)}, u32[]{:S(2)}) collective-permute-start(bf16[128,1536]{1,0:T(8,128)(2,1)} %constant_dynamic-slice_fusion.8.dy_ref), channel_id=1, source_target_pairs={{0,8},{4,12},{8,0},{12,4},{1,9},{5,13},{9,1},{13,5},{2,10},{6,14},... | collective-permute-start | bytes 1179656 | tf_op jit(solution)/shard_map/ppermute | solution.py:1109
  11.9 16.6 %collective-permute-start = (bf16[1,1984]{1,0:T(2,128)(2,1)S(1)}, bf16[1,1984]{1,0:T(2,128)(2,1)S(1)}, u32[]{:S(2)}, u32[]{:S(2)}) collective-permute-start(bf16[1,1984]{1,0:T(2,128)(2,1)S(1)} %concatenate.68), channel_id=1, source_target_pairs={{0,16},{16,0},{1,17},{17,1},{2,18},{18,2},{3,19},{19,3},{4,20},{20... | collective-permute-start | bytes 11912 | tf_op jit(solution)/shard_map/ppermute | solution.py:1109
  15.2 13.6 %collective-permute-start.4 = (bf16[768,128]{1,0:T(8,128)(2,1)}, bf16[768,128]{1,0:T(8,128)(2,1)}, u32[]{:S(2)}, u32[]{:S(2)}) collective-permute-start(bf16[768,128]{1,0:T(8,128)(2,1)} %dynamic-slice_select_fusion.refs_2_), channel_id=1, source_target_pairs={{0,16},{16,0},{1,17},{17,1},{2,18},{18,2},{3,19},{19,3},{4,20},{20... | collective-permute-start | bytes 589832 | tf_op jit(solution)/shard_map/ppermute | solution.py:1109
  15.7 18.2 %collective-permute-start.3 = (bf16[768,384]{1,0:T(8,128)(2,1)}, bf16[768,384]{1,0:T(8,128)(2,1)}, u32[]{:S(2)}, u32[]{:S(2)}) collective-permute-start(bf16[768,384]{1,0:T(8,128)(2,1)} %refs_0_.3), channel_id=1, source_target_pairs={{0,16},{16,0},{1,17},{17,1},{2,18},{18,2},{3,19},{19,3},{4,20},{20... | collective-permute-start | bytes 1769480 | tf_op jit(solution)/shard_map/ppermute | solution.py:1109
  24.9 35.0 %copy-start.2 = (bf16[2240,768]{1,0:T(8,128)(2,1)}, bf16[2240,768]{1,0:T(8,128)(2,1)S(1)}, u32[]{:S(2)}) copy-start(bf16[2240,768]{1,0:T(8,128)(2,1)S(1)} %pad_maximum_fusion.refs_0_.refs_2_) | copy-start | bytes 10321924
  34.0 23.4 %collective-permute-start.5 = (bf16[384,768]{1,0:T(8,128)(2,1)}, bf16[384,768]{1,0:T(8,128)(2,1)}, u32[]{:S(2)}, u32[]{:S(2)}) collective-permute-start(bf16[384,768]{1,0:T(8,128)(2,1)} %param.25), channel_id=1, source_target_pairs={{0,16},{16,0},{1,17},{17,1},{2,18},{18,2},{3,19},{19,3},{4,20},{20... | collective-permute-start | bytes 1769480 | tf_op jit(solution)/shard_map/ppermute | solution.py:1109
  35.9 21.5 %copy-start.24 = (bf16[384,768]{1,0:T(8,128)(2,1)S(1)}, bf16[384,768]{1,0:T(8,128)(2,1)}, u32[]{:S(2)}) copy-start(bf16[384,768]{1,0:T(8,128)(2,1)} %param.25) | copy-start | bytes 1769476
  59.9 80.9 %collective-permute-start.7 = (bf16[2240,768]{1,0:T(8,128)(2,1)S(1)}, bf16[2240,768]{1,0:T(8,128)(2,1)}, u32[]{:S(2)}, u32[]{:S(2)}) collective-permute-start(bf16[2240,768]{1,0:T(8,128)(2,1)S(1)} %pad_maximum_fusion.refs_0_.refs_2_), channel_id=1, source_target_pairs={{0,16},{16,0},{1,17},{17,1},{2,18},{18,2},{3,19},{19,3},{4,20},{20... | collective-permute-start | bytes 10321928 | tf_op jit(solution)/shard_map/ppermute | solution.py:1109
  61.5 112.1 %collective-permute-start.8 = (bf16[1120,768]{1,0:T(8,128)(2,1)}, bf16[1120,768]{1,0:T(8,128)(2,1)}, u32[]{:S(2)}, u32[]{:S(2)}) collective-permute-start(bf16[1120,768]{1,0:T(8,128)(2,1)} %constant_dynamic-slice_fusion.5.refs_4_), channel_id=1, source_target_pairs={{0,16},{16,0},{1,17},{17,1},{2,18},{18,2},{3,19},{19,3},{4,20},{20... | collective-permute-start | bytes 5160968 | tf_op jit(solution)/shard_map/ppermute | solution.py:1109
  62.0 16.4 %collective-permute-start.6 = (bf16[128,1536]{1,0:T(8,128)(2,1)}, bf16[128,1536]{1,0:T(8,128)(2,1)}, u32[]{:S(2)}, u32[]{:S(2)}) collective-permute-start(bf16[128,1536]{1,0:T(8,128)(2,1)} %constant_dynamic-slice_fusion.8.dy_ref), channel_id=1, source_target_pairs={{0,2},{1,3},{2,0},{3,1},{4,6},{5,7},{6,4},{7,5},{8,10},{9,11},{10,... | collective-permute-start | bytes 1179656 | tf_op jit(solution)/shard_map/ppermute | solution.py:1109
  170.6 47.2 %collective-permute-start.9 = (bf16[1120,768]{1,0:T(8,128)(2,1)}, bf16[1120,768]{1,0:T(8,128)(2,1)S(1)}, u32[]{:S(2)}, u32[]{:S(2)}) collective-permute-start(bf16[1120,768]{1,0:T(8,128)(2,1)} %get-tuple-element.106), channel_id=1, source_target_pairs={{0,16},{16,0},{1,17},{17,1},{2,18},{18,2},{3,19},{19,3},{4,20},{20... | collective-permute-start | bytes 5160968 | tf_op jit(solution)/shard_map/ppermute | solution.py:1109
  215.6 40.8 %collective-permute-start.10 = (bf16[1120,768]{1,0:T(8,128)(2,1)}, bf16[1120,768]{1,0:T(8,128)(2,1)S(1)}, u32[]{:S(2)}, u32[]{:S(2)}) collective-permute-start(bf16[1120,768]{1,0:T(8,128)(2,1)} %get-tuple-element.109), channel_id=1, source_target_pairs={{0,16},{16,0},{1,17},{17,1},{2,18},{18,2},{3,19},{19,3},{4,20},{20... | collective-permute-start | bytes 5160968 | tf_op jit(solution)/shard_map/ppermute | solution.py:1109
  217.1 93.1 %collective-permute-start.13 = (bf16[1120,768]{1,0:T(8,128)(2,1)}, bf16[1120,768]{1,0:T(8,128)(2,1)}, u32[]{:S(2)}, u32[]{:S(2)}) collective-permute-start(bf16[1120,768]{1,0:T(8,128)(2,1)} %get-tuple-element.123), channel_id=1, source_target_pairs={{0,16},{16,0},{1,17},{17,1},{2,18},{18,2},{3,19},{19,3},{4,20},{20... | collective-permute-start | bytes 5160968 | tf_op jit(solution)/shard_map/ppermute | solution.py:1109
  256.4 45.7 %collective-permute-start.12 = (bf16[848,768]{1,0:T(8,128)(2,1)}, bf16[848,768]{1,0:T(8,128)(2,1)}, u32[]{:S(2)}, u32[]{:S(2)}) collective-permute-start(bf16[848,768]{1,0:T(8,128)(2,1)} %get-tuple-element.138), channel_id=1, source_target_pairs={{0,4},{4,0},{8,12},{12,8},{1,5},{5,1},{9,13},{13,9},{2,6},{6,2},{1... | collective-permute-start | bytes 3907592 | tf_op jit(solution)/shard_map/ppermute | solution.py:1109
  262.2 15.1 %copy-start.13 = (bf16[512,1536]{1,0:T(8,128)(2,1)S(1)}, bf16[512,1536]{1,0:T(8,128)(2,1)}, u32[]{:S(2)}) copy-start(bf16[512,1536]{1,0:T(8,128)(2,1)} %get-tuple-element.125) | copy-start | bytes 4718596
  279.8 78.2 %collective-permute-start.15 = (bf16[768,384]{1,0:T(8,128)(2,1)}, bf16[768,384]{1,0:T(8,128)(2,1)}, u32[]{:S(2)}, u32[]{:S(2)}) collective-permute-start(bf16[768,384]{1,0:T(8,128)(2,1)} %convolution_convert_fusion.1), channel_id=1, source_target_pairs={{0,16},{16,0},{1,17},{17,1},{2,18},{18,2},{3,19},{19,3},{4,20},{20... | collective-permute-start | bytes 1769480 | tf_op jit(solution)/shard_map/ppermute | solution.py:1109
  282.6 75.5 %collective-permute-start.11 = (bf16[384,768]{1,0:T(8,128)(2,1)}, bf16[384,768]{1,0:T(8,128)(2,1)}, u32[]{:S(2)}, u32[]{:S(2)}) collective-permute-start(bf16[384,768]{1,0:T(8,128)(2,1)} %convolution_convert_fusion.2), channel_id=1, source_target_pairs={{0,16},{16,0},{1,17},{17,1},{2,18},{18,2},{3,19},{19,3},{4,20},{20... | collective-permute-start | bytes 1769480 | tf_op jit(solution)/shard_map/ppermute | solution.py:1109
  283.2 19.0 %copy-start.7 = (f32[512,64]{1,0:T(8,128)S(1)}, f32[512,64]{1,0:T(8,128)}, u32[]{:S(2)}) copy-start(f32[512,64]{1,0:T(8,128)} %copy-done.6) | copy-start | bytes 393220
  302.1 46.5 %collective-permute-start.14 = (bf16[1120,768]{1,0:T(8,128)(2,1)S(1)}, bf16[1120,768]{1,0:T(8,128)(2,1)}, u32[]{:S(2)}, u32[]{:S(2)}) collective-permute-start(bf16[1120,768]{1,0:T(8,128)(2,1)S(1)} %add_convert_fusion.1), channel_id=1, source_target_pairs={{0,4},{4,0},{8,12},{12,8},{1,5},{5,1},{9,13},{13,9},{2,6},{6,2},{1... | collective-permute-start | bytes 5160968 | tf_op jit(solution)/shard_map/ppermute | solution.py:1109
  304.3 4.8 %copy-start.4 = (bf16[512,128]{1,0:T(8,128)(2,1)S(1)}, bf16[512,128]{1,0:T(8,128)(2,1)}, u32[]{:S(2)}) copy-start(bf16[512,128]{1,0:T(8,128)(2,1)} %fusion.18.dkv_ref) | copy-start | bytes 393220
  304.3 4.8 %copy-start.14 = (bf16[512,1536]{1,0:T(8,128)(2,1)S(1)}, bf16[512,1536]{1,0:T(8,128)(2,1)}, u32[]{:S(2)}) copy-start(bf16[512,1536]{1,0:T(8,128)(2,1)} %get-tuple-element.125) | copy-start | bytes 4718596
  310.3 47.8 %collective-permute-start.16 = (bf16[768,128]{1,0:T(8,128)(2,1)}, bf16[768,128]{1,0:T(8,128)(2,1)}, u32[]{:S(2)}, u32[]{:S(2)}) collective-permute-start(bf16[768,128]{1,0:T(8,128)(2,1)} %convolution_convert_fusion.4), channel_id=1, source_target_pairs={{0,16},{16,0},{1,17},{17,1},{2,18},{18,2},{3,19},{19,3},{4,20},{20... | collective-permute-start | bytes 589832 | tf_op jit(solution)/shard_map/ppermute | solution.py:1109
  311.5 4.9 %copy-start.30 = (f32[1,1536]{1,0:T(1,128)S(1)}, f32[1,1536]{1,0:T(1,128)}, u32[]{:S(2)}) copy-start(f32[1,1536]{1,0:T(1,128)} %get-tuple-element.128) | copy-start | bytes 18436
  313.9 120.0 %collective-permute-start.17 = (bf16[1120,768]{1,0:T(8,128)(2,1)S(1)}, bf16[1120,768]{1,0:T(8,128)(2,1)}, u32[]{:S(2)}, u32[]{:S(2)}) collective-permute-start(bf16[1120,768]{1,0:T(8,128)(2,1)S(1)} %add_convert_fusion), channel_id=1, source_target_pairs={{0,4},{4,0},{8,12},{12,8},{1,5},{5,1},{9,13},{13,9},{2,6},{6,2},{1... | collective-permute-start | bytes 5160968 | tf_op jit(solution)/shard_map/ppermute | solution.py:1109
  353.2 4.8 %copy-start.5 = (bf16[512,128]{1,0:T(8,128)(2,1)S(1)}, bf16[512,128]{1,0:T(8,128)(2,1)}, u32[]{:S(2)}) copy-start(bf16[512,128]{1,0:T(8,128)(2,1)} %fusion.18.dkv_ref) | copy-start | bytes 393220
  353.2 4.9 %copy-start.15 = (bf16[512,1536]{1,0:T(8,128)(2,1)S(1)}, bf16[512,1536]{1,0:T(8,128)(2,1)}, u32[]{:S(2)}) copy-start(bf16[512,1536]{1,0:T(8,128)(2,1)} %get-tuple-element.125) | copy-start | bytes 4718596
  353.2 7.0 %copy-start.17 = (bf16[512,384]{1,0:T(8,128)(2,1)S(1)}, bf16[512,384]{1,0:T(8,128)(2,1)}, u32[]{:S(2)}) copy-start(bf16[512,384]{1,0:T(8,128)(2,1)} %get-tuple-element.113.dq_ref) | copy-start | bytes 1179652
  434.0 4.8 %copy-start.23 = (bf16[4,768,128]{2,1,0:T(8,128)(2,1)S(1)}, bf16[4,768,128]{2,1,0:T(8,128)(2,1)}, u32[]{:S(2)}) copy-start(bf16[4,768,128]{2,1,0:T(8,128)(2,1)} %get-tuple-element.155) | copy-start | bytes 2359300
  434.0 4.8 %copy-start.29 = (f32[1,5120]{1,0:T(1,128)S(1)}, f32[1,5120]{1,0:T(1,128)}, u32[]{:S(2)}) copy-start(f32[1,5120]{1,0:T(1,128)} %get-tuple-element.153) | copy-start | bytes 61444
  (21 other events, 55.7 us)

commit v19 on v18

--- a/solution.py
+++ b/solution.py
@@ -904,7 +904,7 @@
         args = [*args, got]
         scratch = [*scratch, pltpu.VMEM(got.shape, bf16)]
         units = got.shape[0]
-        cut = units // 64 * 16
+        cut = units * 3 // 128 * 16
         outs = [*outs, *(jax.ShapeDtypeStruct((n, shard), bf16) for n in (cut, units - cut, cut))]
     return remote_call(
         functools.partial(middle_back_kernel, len(fill)),
@@ -1275,17 +1275,15 @@
             down_low, gate_own = owns[:2]
             down_upper, down_lower = down_low[:upper], down_low[upper:]
             far_upper = flip(down_upper, "context", 1)
-        gate_got = after(gate_got, grad_middle_low)
-        gate_low = add(gate_own, gate_got)
         far_lower = flip(down_lower, "context", 1)
-        grad_middle_low = after(grad_middle_low, gate_low)
         grad_attended = dot_cols(grad_middle_low, w_out_all).astype(bf16)
 
         dq_low, dkv = attention_back(key_blocks, queries, grad_attended, lse, cosine, sine, kv)
         attention_args = [(attended, after(grad_middle_low, dq_low), 1), (normed, dq_low, 0)]
         fars = [grad_far(*args) for args in attention_args]
+        gate_low = add(gate_own, after(gate_got, dq_low))
         dkv, *last_owns = kv_scatter(
-            after(dkv, fars), later, width // n_f
+            after(dkv, fars, gate_low, far_lower), later, width // n_f
         )
         (up_own,) = last_owns or owns[2:]
         far_gate = flip(after(gate_low, dkv, far_lower), "context", 1)

time: 452 us -> 469 us (1.038)
  waiting for transfers between devices: 9.32 us -> 23.1 us
    ppermute x18, waiting for transfers between devices: 9.32 us -> 23.1 us  [flip(): return lax.ppermute(x, axis, [(i, i ^ bit) for i in range(size)])]
  transfers between devices with their start and end apart: 18 -> 18, of which waited for: 3 -> 3; matrix products, arithmetic and copies ran while one was open for 12% -> 12% of each run, Pallas kernels for 75% -> 73%
where the time goes in v19:
time: 469 us; the launch traced here: 464 us
  Pallas kernels  338 us (72%)
  other arithmetic  35.3 us (8%)
  starting transfers between devices  24 us (5%)
  local copies, waits for them, and re-layouts  23.6 us (5%)
  waiting for transfers between devices  23.1 us (5%)
  matrix products  18.7 us (4%)
    pallas_call x6, Pallas kernels, remote_call(): pl.pallas_call(kernel, name=name, out_shape=outs, in_specs=[spec(x) for x...  230 us
    pallas_call x2, Pallas kernels, hidden_call(): pl.pallas_call(kernel, name=name, grid_spec=pltpu.PrefetchScalarGridSpec(...  71.8 us
    ppermute x18, starting transfers between devices, flip(): return lax.ppermute(x, axis, [(i, i ^ bit) for i in range(size)])  24 us
    ppermute x18, waiting for transfers between devices, flip(): return lax.ppermute(x, axis, [(i, i ^ bit) for i in range(size)])  23.1 us
    pallas_call x1, Pallas kernels, attention_back(): pl.pallas_call(functools.partial(attention_back_kernel, kv.shape[1] // BL...  15.1 us
    dot_general x6, matrix products, dot_rows(): lax.dot_general(left, right, (((0,), (0,)), ((), ())), preferred_element_...  12 us
    unnamed x78, local copies, waits for them, and re-layouts  10.4 us
    pallas_call x1, Pallas kernels, attention(): pl.pallas_call(functools.partial(attention_kernel, kv.shape[1] // BLOCK),...  10.2 us
  transfers between devices with their start and end apart: 18, of which 3 were waited for; matrix products, arithmetic and copies ran while one was open for 12% of the time, Pallas kernels for 73%

profile of v19, /device:TPU:0, one launch (start us, length us, event | category | flops | bytes accessed | tf_op | source)
XLA Modules:
  0.0 463.8 jit_solution(2421461044205029217)
XLA Ops:
  0.7 1.9 constant_dynamic-slice_fusion.8.dy_ref
  2.6 3.0 collective-permute-start.1
  5.6 2.6 collective-permute-start.2
  17.2 1.8 constant_dynamic-slice_fusion.4.x_ref
  28.8 5.2 %collective-permute-done.3.refs_1_ = bf16[768,384]{1,0:T(8,128)(2,1)} collective-permute-done((bf16[768,384]{1,0:T(8,128)(2,1)}, bf16[768,384]{1,0:T(8,128)(2,1)}, u32[]{:S(2)}, u32[]{:S(2)}) %collective-permute-start.3) | collective-permute-done | bytes 589856 | tf_op jit(solution)/shard_map/ppermute | solution.py:1109
  35.9 6.5 %qkv.1 = (bf16[512,1536]{1,0:T(8,128)(2,1)}, bf16[512,384]{1,0:T(8,128)(2,1)}, bf16[512,128]{1,0:T(8,128)(2,1)}) custom-call(s32[4]{0:T(128)} %pad_add_fusion.1.meta_ref, bf16[512,1536]{1,0:T(8,128)(2,1)} %x_ref.1, f32[1,1536]{1,0:T(1,128)} %bitcast.87, f32[1,512]{1,0:T(1,128)} %pad_maximum_fusion.4.bias_ref, f32[512,128]{1,0:T(8,128)} %get-tuple-element.179.cos_ref, ...), custom_call_target="tpu_custom_call" | custom-call | tf_op jit(solution)/shard_map/qkv/pallas_call | solution.py:208
  42.3 15.0 %kv_gather.1.k_ref.v_ref = bf16[2,2048,128]{2,1,0:T(8,128)(2,1)} custom-call(bf16[512,128]{1,0:T(8,128)(2,1)} %get-tuple-element.90.own_ref), custom_call_target="tpu_custom_call" | custom-call | tf_op jit(solution)/shard_map/kv_gather/pallas_call | solution.py:640
  57.4 2.5 maximum_select_fusion.3
  64.7 10.2 %attention.1 = (bf16[512,384]{1,0:T(8,128)(2,1)}, f32[3,512,1]{2,1,0:T(8,128)}) custom-call(s32[8]{0:T(128)} %pad_add_fusion.kb_ref, bf16[512,384]{1,0:T(8,128)(2,1)} %get-tuple-element.89.q_ref, bf16[2,2048,128]{2,1,0:T(8,128)(2,1)} %kv_gather.1.k_ref.v_ref, bf16[2,2048,128]{2,1,0:T(8,128)(2,1)} %kv_gather.1.k_ref.v_ref), custom_call_target="tpu_custom_call" | custom-call | tf_op jit(solution)/shard_map/attention/pallas_call | solution.py:85
  74.8 3.5 convolution_convert_fusion
  78.4 62.4 %middle_norm.1 = (f32[128,1536]{1,0:T(8,128)}, f32[128,1]{1,0:T(8,128)}, bf16[16,128,1536]{2,1,0:T(8,128)(2,1)}, bf16[16,128,1536]{2,1,0:T(8,128)(2,1)}) custom-call(bf16[4,128,1536]{2,1,0:T(8,128)(2,1)} %bitcast.79, bf16[128,1536]{1,0:T(8,128)(2,1)} %constant_dynamic-slice_fusion.4.x_ref, f32[1,1536]{1,0:T(1,128)} %bitcast.89, ...), custom_call_target="tpu_custom_call" | custom-call | tf_op jit(solution)/shard_map/middle_norm/pallas_call | solution.py:640
  140.8 29.8 %hidden_units.1 = (bf16[2048,1120]{1,0:T(8,128)(2,1)}, bf16[2048,1120]{1,0:T(8,128)(2,1)}, bf16[2048,1120]{1,0:T(8,128)(2,1)}, bf16[1120,768]{1,0:T(8,128)(2,1)}) custom-call(s32[4]{0:T(128)} %pad_add_fusion.1.meta_ref, bf16[2048,1536]{1,0:T(8,128)(2,1)} %bitcast.70, bf16[2048,1536]{1,0:T(8,128)(2,1)} %bitcast.74, bf16[2240,768]{1,0:T(8,128)(2,1)} %copy-done.2, ...), custom_call_target="tpu_custom_call" | custom-call | tf_op jit(solution)/shard_map/hidden_units/pallas_call | solution.py:331
  173.6 42.0 %hidden_back.1 = (bf16[2048,1120]{1,0:T(8,128)(2,1)}, bf16[2048,1120]{1,0:T(8,128)(2,1)}, bf16[1024,1536]{1,0:T(8,128)(2,1)}, bf16[1024,1536]{1,0:T(8,128)(2,1)}...) custom-call(s32[4]{0:T(128)} %pad_add_fusion.1.meta_ref, bf16[2048,1536]{1,0:T(8,128)(2,1)} %bitcast.71, ...), custom_call_target="tpu_custom_call" | custom-call | tf_op jit(solution)/shard_map/hidden_back/pallas_call | solution.py:331
  218.9 35.7 %middle_back.1 = (f32[128,1536]{1,0:T(8,128)}, f32[1,1536]{1,0:T(1,128)}, bf16[4,128,1536]{2,1,0:T(8,128)(2,1)}, bf16[1120,768]{1,0:T(8,128)(2,1)}, bf16[1120,76...) custom-call(bf16[8,128,1536]{2,1,0:T(8,128)(2,1)} %bitcast.80, ...), custom_call_target="tpu_custom_call" | custom-call | tf_op jit(solution)/shard_map/middle_back/pallas_call | solution.py:640
  254.6 3.2 convolution_convert_fusion.3.do_ref
  257.8 15.1 %attention_back.1 = (bf16[512,384]{1,0:T(8,128)(2,1)}, bf16[2,2048,128]{2,1,0:T(8,128)(2,1)}) custom-call(s32[8]{0:T(128)} %pad_add_fusion.kb_ref, bf16[512,384]{1,0:T(8,128)(2,1)} %get-tuple-element.89.q_ref, bf16[512,384]{1,0:T(8,128)(2,1)} %convolution_convert_fusion.3.do_ref, f32[3,512,1]{2,1,0:T(8,128)} %get-tuple-element.107.lse_ref, ...), custom_call_target="tpu_custom_call" | custom-call | tf_op jit(solution)/shard_map/attention_back/pallas_call | solution.py:151
  274.5 2.6 convolution_convert_fusion.1
  280.4 1.9 add_convert_fusion.1
  282.3 16.6 %collective-permute-done.12 = bf16[704,768]{1,0:T(8,128)(2,1)S(1)} collective-permute-done((bf16[704,768]{1,0:T(8,128)(2,1)}, bf16[704,768]{1,0:T(8,128)(2,1)S(1)}, u32[]{:S(2)}, u32[]{:S(2)}) %collective-permute-start.12) | collective-permute-done | bytes 1081376 | tf_op jit(solution)/shard_map/ppermute | solution.py:1109
  299.9 18.8 %kv_scatter.1 = (f32[512,128]{1,0:T(8,128)}, bf16[1120,768]{1,0:T(8,128)(2,1)}) custom-call(bf16[2,2048,128]{2,1,0:T(8,128)(2,1)} %get-tuple-element.116.part_ref, bf16[2048,1120]{1,0:T(8,128)(2,1)} %get-tuple-element.117.refs_0_, bf16[2048,1536]{1,0:T(8,128)(2,1)} %bitcast.73), custom_call_target="tpu_custom_call" | custom-call | tf_op jit(solution)/shard_map/kv_scatter/pallas_call | solution.py:640
  321.0 4.8 %qkv_back.1 = bf16[512,1536]{1,0:T(8,128)(2,1)} custom-call(s32[4]{0:T(128)} %pad_add_fusion.1.meta_ref, bf16[512,384]{1,0:T(8,128)(2,1)} %get-tuple-element.108.dq_ref, bf16[512,128]{1,0:T(8,128)(2,1)} %fusion.18.dkv_ref, bf16[768,384]{1,0:T(8,128)(2,1)} %refs_0_.3, bf16[768,384]{1,0:T(8,128)(2,1)} %collective-permute-done.3.refs_1_, ...), custom_call_target="tpu_custom_call" | custom-call | tf_op jit(solution)/shard_map/qkv_back/pallas_call | solution.py:240
  328.1 2.5 add_convert_fusion
  330.6 2.0 collective-permute-start.17
  333.7 28.7 %input_back.1 = (f32[1,5120]{1,0:T(1,128)}, bf16[4,128,1536]{2,1,0:T(8,128)(2,1)}) custom-call(bf16[4,128,1536]{2,1,0:T(8,128)(2,1)} %bitcast.78, bf16[128,1536]{1,0:T(8,128)(2,1)} %constant_dynamic-slice_fusion.4.x_ref, f32[1,1536]{1,0:T(1,128)} %bitcast.88, f32[128,1536]{1,0:T(8,128)} %get-tuple-element.125.dmid_ref, f32[1,5120]{1,0:T(1,128)} %pad_maximum_fusion.3.small_ref), custom_call_target="tpu_custom_call" | custom-call | tf_op jit(solution)/shard_map/input_back/pallas_call | solution.py:640
  362.4 2.8 broadcast_add_fusion
  365.3 4.6 %fusion = f32[2240,768]{1,0:T(8,128)} fusion(bf16[704,768]{1,0:T(8,128)(2,1)S(1)} %copy-done.21, bf16[416,768]{1,0:T(8,128)(2,1)S(1)} %copy-done.26, bf16[704,768]{1,0:T(8,128)(2,1)} %get-tuple-element.136, bf16[416,768]{1,0:T(8,128)(2,1)S(1)} %copy-done.25, pred[]{:T(512)S(6)} %eq.19), kind=kLoop, calls=%fused_computation.3 | loop fusion | flops 30965760 | bytes 10321921 | tf_op jit(solution)/shard_map/convert_element_type | solution.py:1264
  369.9 4.8 %fusion.1 = f32[2240,768]{1,0:T(8,128)} fusion(bf16[1120,768]{1,0:T(8,128)(2,1)} %collective-permute-done.14, bf16[1120,768]{1,0:T(8,128)(2,1)S(1)} %add_convert_fusion.1, pred[]{:T(512)S(6)} %eq.19), kind=kLoop, calls=%fused_computation.5 | loop fusion | flops 17203200 | bytes 10321921 | tf_op jit(solution)/shard_map/convert_element_type | solution.py:1264
  374.8 2.2 fusion.9.refs_2_
  376.9 2.5 fusion.3.refs_1_
  379.4 2.4 fusion.2.refs_0_
  381.8 68.9 %context_sum.1 = (f32[384,768]{1,0:T(8,128)}, f32[768,384]{1,0:T(8,128)}, f32[1,5120]{1,0:T(1,128)}, bf16[4,768,128]{2,1,0:T(8,128)(2,1)}, bf16[4,128,1536]{2,1,0:T(8,128)(2,1)}) custom-call(bf16[384,768]{1,0:T(8,128)(2,1)} %fusion.2.refs_0_, bf16[768,384]{1,0:T(8,128)(2,1)} %fusion.3.refs_1_, bf16[768,128]{1,0:T(8,128)(2,1)} %fusion.9.refs_2_, ...), custom_call_target="tpu_custom_call" | custom-call | tf_op jit(solution)/shard_map/context_sum/pallas_call | solution.py:640
  450.7 4.8 %convert_bitcast_fusion = f32[768,2240]{0,1:T(8,128)} fusion(bf16[1120,768]{1,0:T(8,128)(2,1)} %collective-permute-done.17, bf16[1120,768]{1,0:T(8,128)(2,1)S(1)} %add_convert_fusion, pred[]{:T(512)S(6)} %eq.19), kind=kLoop, calls=%fused_computation | loop fusion | flops 17203200 | bytes 10321921 | tf_op jit(solution)/shard_map/transpose | solution.py:1348
  (161 shorter events, 51.3 us)
Async XLA Ops:
  0.6 19.7 %copy-start = (bf16[2240,768]{1,0:T(8,128)(2,1)S(1)}, bf16[2240,768]{1,0:T(8,128)(2,1)}, u32[]{:S(2)}) copy-start(bf16[2240,768]{1,0:T(8,128)(2,1)} %param.29) | copy-start | bytes 10321924
  0.7 18.9 %copy-start.34 = (s32[1,8]{1,0:T(1,128)S(1)}, s32[1,8]{1,0:T(1,128)}, u32[]{:S(2)}) copy-start(s32[1,8]{1,0:T(1,128)} %param.17) | copy-start | bytes 100
  2.6 33.3 %collective-permute-start.1 = (bf16[128,1536]{1,0:T(8,128)(2,1)}, bf16[128,1536]{1,0:T(8,128)(2,1)}, u32[]{:S(2)}, u32[]{:S(2)}) collective-permute-start(bf16[128,1536]{1,0:T(8,128)(2,1)} %constant_dynamic-slice_fusion.8.dy_ref), channel_id=1, source_target_pairs={{0,4},{4,0},{8,12},{12,8},{1,5},{5,1},{9,13},{13,9},{2,6},{6,2},{1... | collective-permute-start | bytes 1179656 | tf_op jit(solution)/shard_map/ppermute | solution.py:1109
  5.6 30.3 %collective-permute-start.2 = (bf16[128,1536]{1,0:T(8,128)(2,1)}, bf16[128,1536]{1,0:T(8,128)(2,1)}, u32[]{:S(2)}, u32[]{:S(2)}) collective-permute-start(bf16[128,1536]{1,0:T(8,128)(2,1)} %constant_dynamic-slice_fusion.8.dy_ref), channel_id=1, source_target_pairs={{0,8},{4,12},{8,0},{12,4},{1,9},{5,13},{9,1},{13,5},{2,10},{6,14},... | collective-permute-start | bytes 1179656 | tf_op jit(solution)/shard_map/ppermute | solution.py:1109
  11.9 16.6 %collective-permute-start = (bf16[1,1984]{1,0:T(2,128)(2,1)S(1)}, bf16[1,1984]{1,0:T(2,128)(2,1)S(1)}, u32[]{:S(2)}, u32[]{:S(2)}) collective-permute-start(bf16[1,1984]{1,0:T(2,128)(2,1)S(1)} %concatenate.68), channel_id=1, source_target_pairs={{0,16},{16,0},{1,17},{17,1},{2,18},{18,2},{3,19},{19,3},{4,20},{20... | collective-permute-start | bytes 11912 | tf_op jit(solution)/shard_map/ppermute | solution.py:1109
  15.2 13.6 %collective-permute-start.4 = (bf16[768,128]{1,0:T(8,128)(2,1)}, bf16[768,128]{1,0:T(8,128)(2,1)}, u32[]{:S(2)}, u32[]{:S(2)}) collective-permute-start(bf16[768,128]{1,0:T(8,128)(2,1)} %dynamic-slice_select_fusion.refs_2_), channel_id=1, source_target_pairs={{0,16},{16,0},{1,17},{17,1},{2,18},{18,2},{3,19},{19,3},{4,20},{20... | collective-permute-start | bytes 589832 | tf_op jit(solution)/shard_map/ppermute | solution.py:1109
  15.7 18.2 %collective-permute-start.3 = (bf16[768,384]{1,0:T(8,128)(2,1)}, bf16[768,384]{1,0:T(8,128)(2,1)}, u32[]{:S(2)}, u32[]{:S(2)}) collective-permute-start(bf16[768,384]{1,0:T(8,128)(2,1)} %refs_0_.3), channel_id=1, source_target_pairs={{0,16},{16,0},{1,17},{17,1},{2,18},{18,2},{3,19},{19,3},{4,20},{20... | collective-permute-start | bytes 1769480 | tf_op jit(solution)/shard_map/ppermute | solution.py:1109
  24.9 35.0 %copy-start.2 = (bf16[2240,768]{1,0:T(8,128)(2,1)}, bf16[2240,768]{1,0:T(8,128)(2,1)S(1)}, u32[]{:S(2)}) copy-start(bf16[2240,768]{1,0:T(8,128)(2,1)S(1)} %pad_maximum_fusion.refs_0_.refs_2_) | copy-start | bytes 10321924
  34.0 23.4 %collective-permute-start.5 = (bf16[384,768]{1,0:T(8,128)(2,1)}, bf16[384,768]{1,0:T(8,128)(2,1)}, u32[]{:S(2)}, u32[]{:S(2)}) collective-permute-start(bf16[384,768]{1,0:T(8,128)(2,1)} %param.25), channel_id=1, source_target_pairs={{0,16},{16,0},{1,17},{17,1},{2,18},{18,2},{3,19},{19,3},{4,20},{20... | collective-permute-start | bytes 1769480 | tf_op jit(solution)/shard_map/ppermute | solution.py:1109
  35.9 21.5 %copy-start.27 = (bf16[384,768]{1,0:T(8,128)(2,1)S(1)}, bf16[384,768]{1,0:T(8,128)(2,1)}, u32[]{:S(2)}) copy-start(bf16[384,768]{1,0:T(8,128)(2,1)} %param.25) | copy-start | bytes 1769476
  59.9 80.9 %collective-permute-start.7 = (bf16[2240,768]{1,0:T(8,128)(2,1)S(1)}, bf16[2240,768]{1,0:T(8,128)(2,1)}, u32[]{:S(2)}, u32[]{:S(2)}) collective-permute-start(bf16[2240,768]{1,0:T(8,128)(2,1)S(1)} %pad_maximum_fusion.refs_0_.refs_2_), channel_id=1, source_target_pairs={{0,16},{16,0},{1,17},{17,1},{2,18},{18,2},{3,19},{19,3},{4,20},{20... | collective-permute-start | bytes 10321928 | tf_op jit(solution)/shard_map/ppermute | solution.py:1109
  61.5 112.1 %collective-permute-start.8 = (bf16[1120,768]{1,0:T(8,128)(2,1)}, bf16[1120,768]{1,0:T(8,128)(2,1)}, u32[]{:S(2)}, u32[]{:S(2)}) collective-permute-start(bf16[1120,768]{1,0:T(8,128)(2,1)} %constant_dynamic-slice_fusion.5.refs_4_), channel_id=1, source_target_pairs={{0,16},{16,0},{1,17},{17,1},{2,18},{18,2},{3,19},{19,3},{4,20},{20... | collective-permute-start | bytes 5160968 | tf_op jit(solution)/shard_map/ppermute | solution.py:1109
  62.0 16.4 %collective-permute-start.6 = (bf16[128,1536]{1,0:T(8,128)(2,1)}, bf16[128,1536]{1,0:T(8,128)(2,1)}, u32[]{:S(2)}, u32[]{:S(2)}) collective-permute-start(bf16[128,1536]{1,0:T(8,128)(2,1)} %constant_dynamic-slice_fusion.8.dy_ref), channel_id=1, source_target_pairs={{0,2},{1,3},{2,0},{3,1},{4,6},{5,7},{6,4},{7,5},{8,10},{9,11},{10,... | collective-permute-start | bytes 1179656 | tf_op jit(solution)/shard_map/ppermute | solution.py:1109
  170.6 47.2 %collective-permute-start.9 = (bf16[1120,768]{1,0:T(8,128)(2,1)}, bf16[1120,768]{1,0:T(8,128)(2,1)S(1)}, u32[]{:S(2)}, u32[]{:S(2)}) collective-permute-start(bf16[1120,768]{1,0:T(8,128)(2,1)} %get-tuple-element.105), channel_id=1, source_target_pairs={{0,16},{16,0},{1,17},{17,1},{2,18},{18,2},{3,19},{19,3},{4,20},{20... | collective-permute-start | bytes 5160968 | tf_op jit(solution)/shard_map/ppermute | solution.py:1109
  215.6 62.7 %collective-permute-start.11 = (bf16[1120,768]{1,0:T(8,128)(2,1)}, bf16[1120,768]{1,0:T(8,128)(2,1)}, u32[]{:S(2)}, u32[]{:S(2)}) collective-permute-start(bf16[1120,768]{1,0:T(8,128)(2,1)} %get-tuple-element.113), channel_id=1, source_target_pairs={{0,16},{16,0},{1,17},{17,1},{2,18},{18,2},{3,19},{19,3},{4,20},{20... | collective-permute-start | bytes 5160968 | tf_op jit(solution)/shard_map/ppermute | solution.py:1109
  217.1 109.8 %collective-permute-start.13 = (bf16[1120,768]{1,0:T(8,128)(2,1)}, bf16[1120,768]{1,0:T(8,128)(2,1)}, u32[]{:S(2)}, u32[]{:S(2)}) collective-permute-start(bf16[1120,768]{1,0:T(8,128)(2,1)} %get-tuple-element.121), channel_id=1, source_target_pairs={{0,16},{16,0},{1,17},{17,1},{2,18},{18,2},{3,19},{19,3},{4,20},{20... | collective-permute-start | bytes 5160968 | tf_op jit(solution)/shard_map/ppermute | solution.py:1109
  218.9 35.7 %copy-start.3 = (bf16[384,1536]{1,0:T(8,128)(2,1)S(1)}, bf16[384,1536]{1,0:T(8,128)(2,1)}, u32[]{:S(2)}) copy-start(bf16[384,1536]{1,0:T(8,128)(2,1)} %maximum_select_fusion.3) | copy-start | bytes 3538948
  257.8 16.7 %copy-start.13 = (bf16[512,1536]{1,0:T(8,128)(2,1)S(1)}, bf16[512,1536]{1,0:T(8,128)(2,1)}, u32[]{:S(2)}) copy-start(bf16[512,1536]{1,0:T(8,128)(2,1)} %get-tuple-element.123) | copy-start | bytes 4718596
  272.9 26.0 %collective-permute-start.12 = (bf16[704,768]{1,0:T(8,128)(2,1)}, bf16[704,768]{1,0:T(8,128)(2,1)S(1)}, u32[]{:S(2)}, u32[]{:S(2)}) collective-permute-start(bf16[704,768]{1,0:T(8,128)(2,1)} %get-tuple-element.136), channel_id=1, source_target_pairs={{0,4},{4,0},{8,12},{12,8},{1,5},{5,1},{9,13},{13,9},{2,6},{6,2},{1... | collective-permute-start | bytes 3244040 | tf_op jit(solution)/shard_map/ppermute | solution.py:1109
  274.5 5.9 %copy-start.11 = (bf16[1120,768]{1,0:T(8,128)(2,1)S(1)}, bf16[1120,768]{1,0:T(8,128)(2,1)}, u32[]{:S(2)}) copy-start(bf16[1120,768]{1,0:T(8,128)(2,1)} %get-tuple-element.112) | copy-start | bytes 5160964
  278.4 96.4 %collective-permute-start.15 = (bf16[768,384]{1,0:T(8,128)(2,1)}, bf16[768,384]{1,0:T(8,128)(2,1)}, u32[]{:S(2)}, u32[]{:S(2)}) collective-permute-start(bf16[768,384]{1,0:T(8,128)(2,1)} %convolution_convert_fusion.1), channel_id=1, source_target_pairs={{0,16},{16,0},{1,17},{17,1},{2,18},{18,2},{3,19},{19,3},{4,20},{20... | collective-permute-start | bytes 1769480 | tf_op jit(solution)/shard_map/ppermute | solution.py:1109
  279.8 95.0 %collective-permute-start.10 = (bf16[384,768]{1,0:T(8,128)(2,1)}, bf16[384,768]{1,0:T(8,128)(2,1)}, u32[]{:S(2)}, u32[]{:S(2)}) collective-permute-start(bf16[384,768]{1,0:T(8,128)(2,1)} %convolution_convert_fusion.2), channel_id=1, source_target_pairs={{0,16},{16,0},{1,17},{17,1},{2,18},{18,2},{3,19},{19,3},{4,20},{20... | collective-permute-start | bytes 1769480 | tf_op jit(solution)/shard_map/ppermute | solution.py:1109
  299.9 19.0 %copy-start.7 = (f32[512,64]{1,0:T(8,128)S(1)}, f32[512,64]{1,0:T(8,128)}, u32[]{:S(2)}) copy-start(f32[512,64]{1,0:T(8,128)} %copy-done.6) | copy-start | bytes 393220
  318.7 46.5 %collective-permute-start.14 = (bf16[1120,768]{1,0:T(8,128)(2,1)S(1)}, bf16[1120,768]{1,0:T(8,128)(2,1)}, u32[]{:S(2)}, u32[]{:S(2)}) collective-permute-start(bf16[1120,768]{1,0:T(8,128)(2,1)S(1)} %add_convert_fusion.1), channel_id=1, source_target_pairs={{0,4},{4,0},{8,12},{12,8},{1,5},{5,1},{9,13},{13,9},{2,6},{6,2},{1... | collective-permute-start | bytes 5160968 | tf_op jit(solution)/shard_map/ppermute | solution.py:1109
  321.0 4.8 %copy-start.14 = (bf16[512,1536]{1,0:T(8,128)(2,1)S(1)}, bf16[512,1536]{1,0:T(8,128)(2,1)}, u32[]{:S(2)}) copy-start(bf16[512,1536]{1,0:T(8,128)(2,1)} %get-tuple-element.123) | copy-start | bytes 4718596
  326.9 47.8 %collective-permute-start.16 = (bf16[768,128]{1,0:T(8,128)(2,1)}, bf16[768,128]{1,0:T(8,128)(2,1)}, u32[]{:S(2)}, u32[]{:S(2)}) collective-permute-start(bf16[768,128]{1,0:T(8,128)(2,1)} %convolution_convert_fusion.4), channel_id=1, source_target_pairs={{0,16},{16,0},{1,17},{17,1},{2,18},{18,2},{3,19},{19,3},{4,20},{20... | collective-permute-start | bytes 589832 | tf_op jit(solution)/shard_map/ppermute | solution.py:1109
  328.1 4.9 %copy-start.31 = (f32[1,1536]{1,0:T(1,128)S(1)}, f32[1,1536]{1,0:T(1,128)}, u32[]{:S(2)}) copy-start(f32[1,1536]{1,0:T(1,128)} %get-tuple-element.126) | copy-start | bytes 18436
  330.6 120.1 %collective-permute-start.17 = (bf16[1120,768]{1,0:T(8,128)(2,1)S(1)}, bf16[1120,768]{1,0:T(8,128)(2,1)}, u32[]{:S(2)}, u32[]{:S(2)}) collective-permute-start(bf16[1120,768]{1,0:T(8,128)(2,1)S(1)} %add_convert_fusion), channel_id=1, source_target_pairs={{0,4},{4,0},{8,12},{12,8},{1,5},{5,1},{9,13},{13,9},{2,6},{6,2},{1... | collective-permute-start | bytes 5160968 | tf_op jit(solution)/shard_map/ppermute | solution.py:1109
  369.9 4.8 %copy-start.5 = (bf16[512,128]{1,0:T(8,128)(2,1)S(1)}, bf16[512,128]{1,0:T(8,128)(2,1)}, u32[]{:S(2)}) copy-start(bf16[512,128]{1,0:T(8,128)(2,1)} %fusion.18.dkv_ref) | copy-start | bytes 393220
  369.9 4.9 %copy-start.15 = (bf16[512,1536]{1,0:T(8,128)(2,1)S(1)}, bf16[512,1536]{1,0:T(8,128)(2,1)}, u32[]{:S(2)}) copy-start(bf16[512,1536]{1,0:T(8,128)(2,1)} %get-tuple-element.123) | copy-start | bytes 4718596
  369.9 7.0 %copy-start.17 = (bf16[512,384]{1,0:T(8,128)(2,1)S(1)}, bf16[512,384]{1,0:T(8,128)(2,1)}, u32[]{:S(2)}) copy-start(bf16[512,384]{1,0:T(8,128)(2,1)} %get-tuple-element.108.dq_ref) | copy-start | bytes 1179652
  450.7 4.8 %copy-start.30 = (f32[1,5120]{1,0:T(1,128)S(1)}, f32[1,5120]{1,0:T(1,128)}, u32[]{:S(2)}) copy-start(f32[1,5120]{1,0:T(1,128)} %get-tuple-element.151) | copy-start | bytes 61444
  (21 other events, 60.0 us)

commit v20 on v18

--- a/solution.py
+++ b/solution.py
@@ -1275,11 +1275,10 @@
             down_low, gate_own = owns[:2]
             down_upper, down_lower = down_low[:upper], down_low[upper:]
             far_upper = flip(down_upper, "context", 1)
-        gate_got = after(gate_got, grad_middle_low)
-        gate_low = add(gate_own, gate_got)
         far_lower = flip(down_lower, "context", 1)
-        grad_middle_low = after(grad_middle_low, gate_low)
         grad_attended = dot_cols(grad_middle_low, w_out_all).astype(bf16)
+        gate_low = add(gate_own, after(gate_got, grad_attended))
+        grad_attended = after(grad_attended, gate_low)
 
         dq_low, dkv = attention_back(key_blocks, queries, grad_attended, lse, cosine, sine, kv)
         attention_args = [(attended, after(grad_middle_low, dq_low), 1), (normed, dq_low, 0)]

time: 452 us -> 450 us (level)
    unnamed x78 -> x76, local copies, waits for them, and re-layouts: 10.7 us -> 9.46 us
  transfers between devices with their start and end apart: 18 -> 18, of which waited for: 3 -> 2; matrix products, arithmetic and copies ran while one was open for 12% -> 13% of each run, Pallas kernels for 75% -> 76%
where the time goes in v20:
time: 450 us; the launch traced here: 445 us
  Pallas kernels  337 us (75%)
  other arithmetic  35.4 us (8%)
  starting transfers between devices  23 us (5%)
  local copies, waits for them, and re-layouts  22.6 us (5%)
  matrix products  18.8 us (4%)
  waiting for transfers between devices  6.52 us (1%)
    pallas_call x6, Pallas kernels, remote_call(): pl.pallas_call(kernel, name=name, out_shape=outs, in_specs=[spec(x) for x...  229 us
    pallas_call x2, Pallas kernels, hidden_call(): pl.pallas_call(kernel, name=name, grid_spec=pltpu.PrefetchScalarGridSpec(...  71.8 us
    ppermute x18, starting transfers between devices, flip(): return lax.ppermute(x, axis, [(i, i ^ bit) for i in range(size)])  23 us
    pallas_call x1, Pallas kernels, attention_back(): pl.pallas_call(functools.partial(attention_back_kernel, kv.shape[1] // BL...  15.1 us
    dot_general x6, matrix products, dot_rows(): lax.dot_general(left, right, (((0,), (0,)), ((), ())), preferred_element_...  12 us
    pallas_call x1, Pallas kernels, attention(): pl.pallas_call(functools.partial(attention_kernel, kv.shape[1] // BLOCK),...  10.2 us
    unnamed x76, local copies, waits for them, and re-layouts  9.46 us
    convert_element_type x2, other arithmetic, unit_whole(): return by_bit(parity, own, other, 0).astype(f32)  9.36 us
  transfers between devices with their start and end apart: 18, of which 2 were waited for; matrix products, arithmetic and copies ran while one was open for 13% of the time, Pallas kernels for 76%

profile of v20, /device:TPU:0, one launch (start us, length us, event | category | flops | bytes accessed | tf_op | source)
XLA Modules:
  0.0 444.7 jit_solution(5347391785481345616)
XLA Ops:
  0.7 1.9 constant_dynamic-slice_fusion.8.dy_ref
  2.6 3.0 collective-permute-start.1
  5.6 2.6 collective-permute-start.2
  13.4 1.8 dynamic-slice_select_fusion.refs_2_
  17.2 1.8 constant_dynamic-slice_fusion.4.x_ref
  28.8 5.2 %collective-permute-done.3.refs_1_ = bf16[768,384]{1,0:T(8,128)(2,1)} collective-permute-done((bf16[768,384]{1,0:T(8,128)(2,1)}, bf16[768,384]{1,0:T(8,128)(2,1)}, u32[]{:S(2)}, u32[]{:S(2)}) %collective-permute-start.3) | collective-permute-done | bytes 589856 | tf_op jit(solution)/shard_map/ppermute | solution.py:1109
  35.9 6.5 %qkv.1 = (bf16[512,1536]{1,0:T(8,128)(2,1)}, bf16[512,384]{1,0:T(8,128)(2,1)}, bf16[512,128]{1,0:T(8,128)(2,1)}) custom-call(s32[4]{0:T(128)} %pad_add_fusion.1.meta_ref, bf16[512,1536]{1,0:T(8,128)(2,1)} %x_ref.1, f32[1,1536]{1,0:T(1,128)} %bitcast.87, f32[1,512]{1,0:T(1,128)} %pad_maximum_fusion.4.bias_ref, f32[512,128]{1,0:T(8,128)} %get-tuple-element.181.cos_ref, ...), custom_call_target="tpu_custom_call" | custom-call | tf_op jit(solution)/shard_map/qkv/pallas_call | solution.py:208
  42.3 15.0 %kv_gather.1.k_ref.v_ref = bf16[2,2048,128]{2,1,0:T(8,128)(2,1)} custom-call(bf16[512,128]{1,0:T(8,128)(2,1)} %get-tuple-element.91.own_ref), custom_call_target="tpu_custom_call" | custom-call | tf_op jit(solution)/shard_map/kv_gather/pallas_call | solution.py:640
  57.4 2.5 maximum_select_fusion.3
  64.7 10.2 %attention.1 = (bf16[512,384]{1,0:T(8,128)(2,1)}, f32[3,512,1]{2,1,0:T(8,128)}) custom-call(s32[8]{0:T(128)} %pad_add_fusion.kb_ref, bf16[512,384]{1,0:T(8,128)(2,1)} %get-tuple-element.90.q_ref, bf16[2,2048,128]{2,1,0:T(8,128)(2,1)} %kv_gather.1.k_ref.v_ref, bf16[2,2048,128]{2,1,0:T(8,128)(2,1)} %kv_gather.1.k_ref.v_ref), custom_call_target="tpu_custom_call" | custom-call | tf_op jit(solution)/shard_map/attention/pallas_call | solution.py:85
  74.8 3.5 convolution_convert_fusion
  78.4 62.4 %middle_norm.1 = (f32[128,1536]{1,0:T(8,128)}, f32[128,1]{1,0:T(8,128)}, bf16[16,128,1536]{2,1,0:T(8,128)(2,1)}, bf16[16,128,1536]{2,1,0:T(8,128)(2,1)}) custom-call(bf16[4,128,1536]{2,1,0:T(8,128)(2,1)} %bitcast.79, bf16[128,1536]{1,0:T(8,128)(2,1)} %constant_dynamic-slice_fusion.4.x_ref, f32[1,1536]{1,0:T(1,128)} %bitcast.89, ...), custom_call_target="tpu_custom_call" | custom-call | tf_op jit(solution)/shard_map/middle_norm/pallas_call | solution.py:640
  140.8 29.8 %hidden_units.1 = (bf16[2048,1120]{1,0:T(8,128)(2,1)}, bf16[2048,1120]{1,0:T(8,128)(2,1)}, bf16[2048,1120]{1,0:T(8,128)(2,1)}, bf16[1120,768]{1,0:T(8,128)(2,1)}) custom-call(s32[4]{0:T(128)} %pad_add_fusion.1.meta_ref, bf16[2048,1536]{1,0:T(8,128)(2,1)} %bitcast.70, bf16[2048,1536]{1,0:T(8,128)(2,1)} %bitcast.74, bf16[2240,768]{1,0:T(8,128)(2,1)} %copy-done.2, ...), custom_call_target="tpu_custom_call" | custom-call | tf_op jit(solution)/shard_map/hidden_units/pallas_call | solution.py:331
  173.6 42.0 %hidden_back.1 = (bf16[2048,1120]{1,0:T(8,128)(2,1)}, bf16[2048,1120]{1,0:T(8,128)(2,1)}, bf16[1024,1536]{1,0:T(8,128)(2,1)}, bf16[1024,1536]{1,0:T(8,128)(2,1)}...) custom-call(s32[4]{0:T(128)} %pad_add_fusion.1.meta_ref, bf16[2048,1536]{1,0:T(8,128)(2,1)} %bitcast.71, ...), custom_call_target="tpu_custom_call" | custom-call | tf_op jit(solution)/shard_map/hidden_back/pallas_call | solution.py:331
  218.9 34.8 %middle_back.1 = (f32[128,1536]{1,0:T(8,128)}, f32[1,1536]{1,0:T(1,128)}, bf16[4,128,1536]{2,1,0:T(8,128)(2,1)}, bf16[1120,768]{1,0:T(8,128)(2,1)}, bf16[1120,76...) custom-call(bf16[8,128,1536]{2,1,0:T(8,128)(2,1)} %bitcast.80, ...), custom_call_target="tpu_custom_call" | custom-call | tf_op jit(solution)/shard_map/middle_back/pallas_call | solution.py:640
  254.3 3.3 convolution_convert_fusion.3.do_ref
  257.6 2.0 add_convert_fusion.1
  259.6 15.1 %attention_back.1 = (bf16[512,384]{1,0:T(8,128)(2,1)}, bf16[2,2048,128]{2,1,0:T(8,128)(2,1)}) custom-call(s32[8]{0:T(128)} %pad_add_fusion.kb_ref, bf16[512,384]{1,0:T(8,128)(2,1)} %get-tuple-element.90.q_ref, bf16[512,384]{1,0:T(8,128)(2,1)} %convolution_convert_fusion.3.do_ref, f32[3,512,1]{2,1,0:T(8,128)} %get-tuple-element.112.lse_ref, ...), custom_call_target="tpu_custom_call" | custom-call | tf_op jit(solution)/shard_map/attention_back/pallas_call | solution.py:151
  274.7 2.6 convolution_convert_fusion.1
  280.7 18.8 %kv_scatter.1 = (f32[512,128]{1,0:T(8,128)}, bf16[1120,768]{1,0:T(8,128)(2,1)}) custom-call(bf16[2,2048,128]{2,1,0:T(8,128)(2,1)} %get-tuple-element.117.part_ref, bf16[2048,1120]{1,0:T(8,128)(2,1)} %get-tuple-element.118.refs_0_, bf16[2048,1536]{1,0:T(8,128)(2,1)} %bitcast.73), custom_call_target="tpu_custom_call" | custom-call | tf_op jit(solution)/shard_map/kv_scatter/pallas_call | solution.py:640
  301.7 4.8 %qkv_back.1 = bf16[512,1536]{1,0:T(8,128)(2,1)} custom-call(s32[4]{0:T(128)} %pad_add_fusion.1.meta_ref, bf16[512,384]{1,0:T(8,128)(2,1)} %get-tuple-element.113.dq_ref, bf16[512,128]{1,0:T(8,128)(2,1)} %fusion.18.dkv_ref, bf16[768,384]{1,0:T(8,128)(2,1)} %refs_0_.3, bf16[768,384]{1,0:T(8,128)(2,1)} %collective-permute-done.3.refs_1_, ...), custom_call_target="tpu_custom_call" | custom-call | tf_op jit(solution)/shard_map/qkv_back/pallas_call | solution.py:240
  308.9 2.5 add_convert_fusion
  311.4 2.0 collective-permute-start.17
  314.5 28.7 %input_back.1 = (f32[1,5120]{1,0:T(1,128)}, bf16[4,128,1536]{2,1,0:T(8,128)(2,1)}) custom-call(bf16[4,128,1536]{2,1,0:T(8,128)(2,1)} %bitcast.78, bf16[128,1536]{1,0:T(8,128)(2,1)} %constant_dynamic-slice_fusion.4.x_ref, f32[1,1536]{1,0:T(1,128)} %bitcast.88, f32[128,1536]{1,0:T(8,128)} %get-tuple-element.127.dmid_ref, f32[1,5120]{1,0:T(1,128)} %pad_maximum_fusion.3.small_ref), custom_call_target="tpu_custom_call" | custom-call | tf_op jit(solution)/shard_map/input_back/pallas_call | solution.py:640
  343.2 2.8 broadcast_add_fusion
  346.0 4.5 %fusion = f32[2240,768]{1,0:T(8,128)} fusion(bf16[848,768]{1,0:T(8,128)(2,1)} %collective-permute-done.12, bf16[272,768]{1,0:T(8,128)(2,1)S(1)} %copy-done.26, bf16[848,768]{1,0:T(8,128)(2,1)S(1)} %copy-done.18, bf16[272,768]{1,0:T(8,128)(2,1)S(1)} %copy-done.25, pred[]{:T(512)S(6)} %eq.19), kind=kLoop, calls=%fused_computation.3 | loop fusion | flops 30965760 | bytes 10321921 | tf_op jit(solution)/shard_map/convert_element_type | solution.py:1264
  350.6 4.8 %fusion.1 = f32[2240,768]{1,0:T(8,128)} fusion(bf16[1120,768]{1,0:T(8,128)(2,1)} %collective-permute-done.14, bf16[1120,768]{1,0:T(8,128)(2,1)S(1)} %add_convert_fusion.1, pred[]{:T(512)S(6)} %eq.19), kind=kLoop, calls=%fused_computation.5 | loop fusion | flops 17203200 | bytes 10321921 | tf_op jit(solution)/shard_map/convert_element_type | solution.py:1264
  355.5 2.2 fusion.9.refs_2_
  357.6 2.5 fusion.3.refs_1_
  360.1 2.4 fusion.2.refs_0_
  362.5 69.0 %context_sum.1 = (f32[384,768]{1,0:T(8,128)}, f32[768,384]{1,0:T(8,128)}, f32[1,5120]{1,0:T(1,128)}, bf16[4,768,128]{2,1,0:T(8,128)(2,1)}, bf16[4,128,1536]{2,1,0:T(8,128)(2,1)}) custom-call(bf16[384,768]{1,0:T(8,128)(2,1)} %fusion.2.refs_0_, bf16[768,384]{1,0:T(8,128)(2,1)} %fusion.3.refs_1_, bf16[768,128]{1,0:T(8,128)(2,1)} %fusion.9.refs_2_, ...), custom_call_target="tpu_custom_call" | custom-call | tf_op jit(solution)/shard_map/context_sum/pallas_call | solution.py:640
  431.5 4.9 %convert_bitcast_fusion = f32[768,2240]{0,1:T(8,128)} fusion(bf16[1120,768]{1,0:T(8,128)(2,1)} %collective-permute-done.17, bf16[1120,768]{1,0:T(8,128)(2,1)S(1)} %add_convert_fusion, pred[]{:T(512)S(6)} %eq.19), kind=kLoop, calls=%fused_computation | loop fusion | flops 17203200 | bytes 10321921 | tf_op jit(solution)/shard_map/transpose | solution.py:1349
  (159 shorter events, 47.6 us)
Async XLA Ops:
  0.6 19.7 %copy-start = (bf16[2240,768]{1,0:T(8,128)(2,1)S(1)}, bf16[2240,768]{1,0:T(8,128)(2,1)}, u32[]{:S(2)}) copy-start(bf16[2240,768]{1,0:T(8,128)(2,1)} %param.29) | copy-start | bytes 10321924
  0.7 18.9 %copy-start.33 = (s32[1,8]{1,0:T(1,128)S(1)}, s32[1,8]{1,0:T(1,128)}, u32[]{:S(2)}) copy-start(s32[1,8]{1,0:T(1,128)} %param.17) | copy-start | bytes 100
  2.6 33.3 %collective-permute-start.1 = (bf16[128,1536]{1,0:T(8,128)(2,1)}, bf16[128,1536]{1,0:T(8,128)(2,1)}, u32[]{:S(2)}, u32[]{:S(2)}) collective-permute-start(bf16[128,1536]{1,0:T(8,128)(2,1)} %constant_dynamic-slice_fusion.8.dy_ref), channel_id=1, source_target_pairs={{0,4},{4,0},{8,12},{12,8},{1,5},{5,1},{9,13},{13,9},{2,6},{6,2},{1... | collective-permute-start | bytes 1179656 | tf_op jit(solution)/shard_map/ppermute | solution.py:1109
  5.6 30.2 %collective-permute-start.2 = (bf16[128,1536]{1,0:T(8,128)(2,1)}, bf16[128,1536]{1,0:T(8,128)(2,1)}, u32[]{:S(2)}, u32[]{:S(2)}) collective-permute-start(bf16[128,1536]{1,0:T(8,128)(2,1)} %constant_dynamic-slice_fusion.8.dy_ref), channel_id=1, source_target_pairs={{0,8},{4,12},{8,0},{12,4},{1,9},{5,13},{9,1},{13,5},{2,10},{6,14},... | collective-permute-start | bytes 1179656 | tf_op jit(solution)/shard_map/ppermute | solution.py:1109
  11.9 16.5 %collective-permute-start = (bf16[1,1984]{1,0:T(2,128)(2,1)S(1)}, bf16[1,1984]{1,0:T(2,128)(2,1)S(1)}, u32[]{:S(2)}, u32[]{:S(2)}) collective-permute-start(bf16[1,1984]{1,0:T(2,128)(2,1)S(1)} %concatenate.68), channel_id=1, source_target_pairs={{0,16},{16,0},{1,17},{17,1},{2,18},{18,2},{3,19},{19,3},{4,20},{20... | collective-permute-start | bytes 11912 | tf_op jit(solution)/shard_map/ppermute | solution.py:1109
  15.2 13.6 %collective-permute-start.4 = (bf16[768,128]{1,0:T(8,128)(2,1)}, bf16[768,128]{1,0:T(8,128)(2,1)}, u32[]{:S(2)}, u32[]{:S(2)}) collective-permute-start(bf16[768,128]{1,0:T(8,128)(2,1)} %dynamic-slice_select_fusion.refs_2_), channel_id=1, source_target_pairs={{0,16},{16,0},{1,17},{17,1},{2,18},{18,2},{3,19},{19,3},{4,20},{20... | collective-permute-start | bytes 589832 | tf_op jit(solution)/shard_map/ppermute | solution.py:1109
  15.7 18.2 %collective-permute-start.3 = (bf16[768,384]{1,0:T(8,128)(2,1)}, bf16[768,384]{1,0:T(8,128)(2,1)}, u32[]{:S(2)}, u32[]{:S(2)}) collective-permute-start(bf16[768,384]{1,0:T(8,128)(2,1)} %refs_0_.3), channel_id=1, source_target_pairs={{0,16},{16,0},{1,17},{17,1},{2,18},{18,2},{3,19},{19,3},{4,20},{20... | collective-permute-start | bytes 1769480 | tf_op jit(solution)/shard_map/ppermute | solution.py:1109
  24.9 35.0 %copy-start.2 = (bf16[2240,768]{1,0:T(8,128)(2,1)}, bf16[2240,768]{1,0:T(8,128)(2,1)S(1)}, u32[]{:S(2)}) copy-start(bf16[2240,768]{1,0:T(8,128)(2,1)S(1)} %pad_maximum_fusion.refs_0_.refs_2_) | copy-start | bytes 10321924
  34.0 23.4 %collective-permute-start.5 = (bf16[384,768]{1,0:T(8,128)(2,1)}, bf16[384,768]{1,0:T(8,128)(2,1)}, u32[]{:S(2)}, u32[]{:S(2)}) collective-permute-start(bf16[384,768]{1,0:T(8,128)(2,1)} %param.25), channel_id=1, source_target_pairs={{0,16},{16,0},{1,17},{17,1},{2,18},{18,2},{3,19},{19,3},{4,20},{20... | collective-permute-start | bytes 1769480 | tf_op jit(solution)/shard_map/ppermute | solution.py:1109
  35.9 21.5 %copy-start.24 = (bf16[384,768]{1,0:T(8,128)(2,1)S(1)}, bf16[384,768]{1,0:T(8,128)(2,1)}, u32[]{:S(2)}) copy-start(bf16[384,768]{1,0:T(8,128)(2,1)} %param.25) | copy-start | bytes 1769476
  59.9 80.9 %collective-permute-start.7 = (bf16[2240,768]{1,0:T(8,128)(2,1)S(1)}, bf16[2240,768]{1,0:T(8,128)(2,1)}, u32[]{:S(2)}, u32[]{:S(2)}) collective-permute-start(bf16[2240,768]{1,0:T(8,128)(2,1)S(1)} %pad_maximum_fusion.refs_0_.refs_2_), channel_id=1, source_target_pairs={{0,16},{16,0},{1,17},{17,1},{2,18},{18,2},{3,19},{19,3},{4,20},{20... | collective-permute-start | bytes 10321928 | tf_op jit(solution)/shard_map/ppermute | solution.py:1109
  61.5 112.1 %collective-permute-start.8 = (bf16[1120,768]{1,0:T(8,128)(2,1)}, bf16[1120,768]{1,0:T(8,128)(2,1)}, u32[]{:S(2)}, u32[]{:S(2)}) collective-permute-start(bf16[1120,768]{1,0:T(8,128)(2,1)} %constant_dynamic-slice_fusion.5.refs_4_), channel_id=1, source_target_pairs={{0,16},{16,0},{1,17},{17,1},{2,18},{18,2},{3,19},{19,3},{4,20},{20... | collective-permute-start | bytes 5160968 | tf_op jit(solution)/shard_map/ppermute | solution.py:1109
  62.0 16.4 %collective-permute-start.6 = (bf16[128,1536]{1,0:T(8,128)(2,1)}, bf16[128,1536]{1,0:T(8,128)(2,1)}, u32[]{:S(2)}, u32[]{:S(2)}) collective-permute-start(bf16[128,1536]{1,0:T(8,128)(2,1)} %constant_dynamic-slice_fusion.8.dy_ref), channel_id=1, source_target_pairs={{0,2},{1,3},{2,0},{3,1},{4,6},{5,7},{6,4},{7,5},{8,10},{9,11},{10,... | collective-permute-start | bytes 1179656 | tf_op jit(solution)/shard_map/ppermute | solution.py:1109
  170.5 47.2 %collective-permute-start.9 = (bf16[1120,768]{1,0:T(8,128)(2,1)}, bf16[1120,768]{1,0:T(8,128)(2,1)S(1)}, u32[]{:S(2)}, u32[]{:S(2)}) collective-permute-start(bf16[1120,768]{1,0:T(8,128)(2,1)} %get-tuple-element.106), channel_id=1, source_target_pairs={{0,16},{16,0},{1,17},{17,1},{2,18},{18,2},{3,19},{19,3},{4,20},{20... | collective-permute-start | bytes 5160968 | tf_op jit(solution)/shard_map/ppermute | solution.py:1109
  215.6 42.0 %collective-permute-start.10 = (bf16[1120,768]{1,0:T(8,128)(2,1)}, bf16[1120,768]{1,0:T(8,128)(2,1)}, u32[]{:S(2)}, u32[]{:S(2)}) collective-permute-start(bf16[1120,768]{1,0:T(8,128)(2,1)} %get-tuple-element.109), channel_id=1, source_target_pairs={{0,16},{16,0},{1,17},{17,1},{2,18},{18,2},{3,19},{19,3},{4,20},{20... | collective-permute-start | bytes 5160968 | tf_op jit(solution)/shard_map/ppermute | solution.py:1109
  217.1 90.5 %collective-permute-start.13 = (bf16[1120,768]{1,0:T(8,128)(2,1)}, bf16[1120,768]{1,0:T(8,128)(2,1)}, u32[]{:S(2)}, u32[]{:S(2)}) collective-permute-start(bf16[1120,768]{1,0:T(8,128)(2,1)} %get-tuple-element.123), channel_id=1, source_target_pairs={{0,16},{16,0},{1,17},{17,1},{2,18},{18,2},{3,19},{19,3},{4,20},{20... | collective-permute-start | bytes 5160968 | tf_op jit(solution)/shard_map/ppermute | solution.py:1109
  218.9 35.4 %copy-start.3 = (bf16[384,1536]{1,0:T(8,128)(2,1)S(1)}, bf16[384,1536]{1,0:T(8,128)(2,1)}, u32[]{:S(2)}) copy-start(bf16[384,1536]{1,0:T(8,128)(2,1)} %maximum_select_fusion.3) | copy-start | bytes 3538948
  253.8 45.7 %collective-permute-start.12 = (bf16[848,768]{1,0:T(8,128)(2,1)}, bf16[848,768]{1,0:T(8,128)(2,1)}, u32[]{:S(2)}, u32[]{:S(2)}) collective-permute-start(bf16[848,768]{1,0:T(8,128)(2,1)} %get-tuple-element.138), channel_id=1, source_target_pairs={{0,4},{4,0},{8,12},{12,8},{1,5},{5,1},{9,13},{13,9},{2,6},{6,2},{1... | collective-permute-start | bytes 3907592 | tf_op jit(solution)/shard_map/ppermute | solution.py:1109
  259.6 15.1 %copy-start.13 = (bf16[512,1536]{1,0:T(8,128)(2,1)S(1)}, bf16[512,1536]{1,0:T(8,128)(2,1)}, u32[]{:S(2)}) copy-start(bf16[512,1536]{1,0:T(8,128)(2,1)} %get-tuple-element.125) | copy-start | bytes 4718596
  277.3 78.1 %collective-permute-start.15 = (bf16[768,384]{1,0:T(8,128)(2,1)}, bf16[768,384]{1,0:T(8,128)(2,1)}, u32[]{:S(2)}, u32[]{:S(2)}) collective-permute-start(bf16[768,384]{1,0:T(8,128)(2,1)} %convolution_convert_fusion.1), channel_id=1, source_target_pairs={{0,16},{16,0},{1,17},{17,1},{2,18},{18,2},{3,19},{19,3},{4,20},{20... | collective-permute-start | bytes 1769480 | tf_op jit(solution)/shard_map/ppermute | solution.py:1109
  280.0 75.4 %collective-permute-start.11 = (bf16[384,768]{1,0:T(8,128)(2,1)}, bf16[384,768]{1,0:T(8,128)(2,1)}, u32[]{:S(2)}, u32[]{:S(2)}) collective-permute-start(bf16[384,768]{1,0:T(8,128)(2,1)} %convolution_convert_fusion.2), channel_id=1, source_target_pairs={{0,16},{16,0},{1,17},{17,1},{2,18},{18,2},{3,19},{19,3},{4,20},{20... | collective-permute-start | bytes 1769480 | tf_op jit(solution)/shard_map/ppermute | solution.py:1109
  280.7 18.9 %copy-start.7 = (f32[512,64]{1,0:T(8,128)S(1)}, f32[512,64]{1,0:T(8,128)}, u32[]{:S(2)}) copy-start(f32[512,64]{1,0:T(8,128)} %copy-done.6) | copy-start | bytes 393220
  299.5 46.5 %collective-permute-start.14 = (bf16[1120,768]{1,0:T(8,128)(2,1)S(1)}, bf16[1120,768]{1,0:T(8,128)(2,1)}, u32[]{:S(2)}, u32[]{:S(2)}) collective-permute-start(bf16[1120,768]{1,0:T(8,128)(2,1)S(1)} %add_convert_fusion.1), channel_id=1, source_target_pairs={{0,4},{4,0},{8,12},{12,8},{1,5},{5,1},{9,13},{13,9},{2,6},{6,2},{1... | collective-permute-start | bytes 5160968 | tf_op jit(solution)/shard_map/ppermute | solution.py:1109
  301.7 4.8 %copy-start.14 = (bf16[512,1536]{1,0:T(8,128)(2,1)S(1)}, bf16[512,1536]{1,0:T(8,128)(2,1)}, u32[]{:S(2)}) copy-start(bf16[512,1536]{1,0:T(8,128)(2,1)} %get-tuple-element.125) | copy-start | bytes 4718596
  307.7 47.7 %collective-permute-start.16 = (bf16[768,128]{1,0:T(8,128)(2,1)}, bf16[768,128]{1,0:T(8,128)(2,1)}, u32[]{:S(2)}, u32[]{:S(2)}) collective-permute-start(bf16[768,128]{1,0:T(8,128)(2,1)} %convolution_convert_fusion.4), channel_id=1, source_target_pairs={{0,16},{16,0},{1,17},{17,1},{2,18},{18,2},{3,19},{19,3},{4,20},{20... | collective-permute-start | bytes 589832 | tf_op jit(solution)/shard_map/ppermute | solution.py:1109
  308.9 4.9 %copy-start.30 = (f32[1,1536]{1,0:T(1,128)S(1)}, f32[1,1536]{1,0:T(1,128)}, u32[]{:S(2)}) copy-start(f32[1,1536]{1,0:T(1,128)} %get-tuple-element.128) | copy-start | bytes 18436
  311.4 120.1 %collective-permute-start.17 = (bf16[1120,768]{1,0:T(8,128)(2,1)S(1)}, bf16[1120,768]{1,0:T(8,128)(2,1)}, u32[]{:S(2)}, u32[]{:S(2)}) collective-permute-start(bf16[1120,768]{1,0:T(8,128)(2,1)S(1)} %add_convert_fusion), channel_id=1, source_target_pairs={{0,4},{4,0},{8,12},{12,8},{1,5},{5,1},{9,13},{13,9},{2,6},{6,2},{1... | collective-permute-start | bytes 5160968 | tf_op jit(solution)/shard_map/ppermute | solution.py:1109
  350.6 4.8 %copy-start.5 = (bf16[512,128]{1,0:T(8,128)(2,1)S(1)}, bf16[512,128]{1,0:T(8,128)(2,1)}, u32[]{:S(2)}) copy-start(bf16[512,128]{1,0:T(8,128)(2,1)} %fusion.18.dkv_ref) | copy-start | bytes 393220
  350.6 4.9 %copy-start.15 = (bf16[512,1536]{1,0:T(8,128)(2,1)S(1)}, bf16[512,1536]{1,0:T(8,128)(2,1)}, u32[]{:S(2)}) copy-start(bf16[512,1536]{1,0:T(8,128)(2,1)} %get-tuple-element.125) | copy-start | bytes 4718596
  350.6 7.0 %copy-start.17 = (bf16[512,384]{1,0:T(8,128)(2,1)S(1)}, bf16[512,384]{1,0:T(8,128)(2,1)}, u32[]{:S(2)}) copy-start(bf16[512,384]{1,0:T(8,128)(2,1)} %get-tuple-element.113.dq_ref) | copy-start | bytes 1179652
  431.5 4.9 %copy-start.23 = (bf16[4,768,128]{2,1,0:T(8,128)(2,1)S(1)}, bf16[4,768,128]{2,1,0:T(8,128)(2,1)}, u32[]{:S(2)}) copy-start(bf16[4,768,128]{2,1,0:T(8,128)(2,1)} %get-tuple-element.155) | copy-start | bytes 2359300
  431.5 5.0 %copy-start.29 = (f32[1,5120]{1,0:T(1,128)S(1)}, f32[1,5120]{1,0:T(1,128)}, u32[]{:S(2)}) copy-start(f32[1,5120]{1,0:T(1,128)} %get-tuple-element.153) | copy-start | bytes 61444
  (20 other events, 57.3 us)
